TPU v7x, 32 devices: a whole 2x2x4 slice. The times are simulated.
32 devices in a mesh: dp: 8 (over y, x, core), tensor: 4 (over z).
Axes of the slice: x: 2, y: 2, z: 4, core: 2. Of those that a mesh axis runs over, the one named last changes fastest.
Arguments:
- hidden_in: bfloat16 [8, 256, 2048], P(None, 'dp'), may hold values from -6 to 6
- cotangent: bfloat16 [8, 256, 2048], P('dp'), may hold values from -6 to 6
- lengths: int32 [8], replicated, may hold values from 1 to 256, 1536 in all
- dealing: int32 [8], replicated, may hold values from 0 to 7, each once
- attn_routes: int32 [8, 256, 2], replicated, may hold values from 0 to 3, all different within a row; in each aligned block of 256 rows (0 to 255, 256 to 511, ..., all dimensions but the last counted through in order) at most 192 rows name the same one
- ffn_routes: int32 [8, 256, 2], replicated, may hold values from 0 to 3, all different within a row; in each aligned block of 256 rows (0 to 255, 256 to 511, ..., all dimensions but the last counted through in order) at most 192 rows name the same one
- attn_gain: float32 [2048], replicated, may hold values from 0.5 to 1.5
- attn_router: bfloat16 [2048, 4], replicated, may hold values from -0.0625 to 0.0625
- kv_weight: bfloat16 [2, 2048, 2048], P(None, 'dp', 'tensor'), may hold values from -0.125 to 0.125
- query_weight: bfloat16 [4, 2048, 2048], P(None, 'dp', 'tensor'), may hold values from -0.125 to 0.125
- proj_weight: bfloat16 [4, 2048, 2048], P(None, 'tensor', 'dp'), may hold values from -1 to 1
- ffn_gain: float32 [2048], replicated, may hold values from 0.5 to 1.5
- ffn_router: bfloat16 [2048, 4], replicated, may hold values from -0.0625 to 0.0625
- expert_in: bfloat16 [4, 2048, 2, 5632], P(None, 'dp', None, 'tensor'), may hold values from -0.125 to 0.125
- expert_out: bfloat16 [4, 5632, 2048], P(None, 'tensor', 'dp'), may hold values from -0.109375 to 0.109375
Outputs:
- layer_out: bfloat16 [8, 256, 2048], P(None, 'dp')
- input_grad: bfloat16 [8, 256, 2048], P(None, 'dp')
- attngain_grad: float32 [2048], replicated
- attnrouter_grad: float32 [2048, 4], replicated
- kv_grad: float32 [2, 2048, 2048], P(None, 'dp', 'tensor')
- query_grad: float32 [4, 2048, 2048], P(None, 'dp', 'tensor')
- proj_grad: float32 [4, 2048, 2048], P(None, 'tensor', 'dp')
- ffngain_grad: float32 [2048], replicated
- ffnrouter_grad: float32 [2048, 4], replicated
- expertin_grad: float32 [4, 2048, 2, 5632], P(None, 'dp', None, 'tensor')
- expertout_grad: float32 [4, 5632, 2048], P(None, 'tensor', 'dp')
Inputs may be any that keep to these rules, and one draw needn't show every extreme that they name: `attn_routes`: within each sequence's 256 rows no expert is named by more than 192 rows, a bound that some block reaches; a row names 2 different experts. `ffn_routes`: within each sequence's 256 rows no expert is named by more than 192 rows, a bound that some block reaches; a row names 2 different experts. `lengths`: the longest sequence has 256 positions. `dealing`: each sequence appears once.
All inputs are finite; a program needn't handle non-finite values.
Results may differ from a plain program's by a relative error of at most 0.02.
Values may be sent and summed in bfloat16 or wider, within the bound.
No kernel may reach another device: no remote copies, remote signals or barrier semaphores. Data moves between devices by JAX's collectives and lax.ppermute only.
A program may use at most 384 MiB of HBM per device.

v0:
```python
import jax
import jax.numpy as jnp
from jax import lax
from jax.sharding import PartitionSpec as P

HD = 128
TOP = 2
CAP = 192


EPSILON = 1e-06
ROPE_BASE = 10000.0
BEST = lax.Precision.HIGHEST


def rotate(values, positions, head_count, direction):
    head_width = values.shape[-1] // head_count
    half_width = head_width // 2
    frequency = ROPE_BASE ** (-2.0 * jnp.arange(half_width, dtype=jnp.float32) / head_width)
    angles = positions.astype(jnp.float32)[:, None] * frequency[None, :]
    cosine = jnp.cos(angles)[:, None, :]
    sine_part = direction * jnp.sin(angles)[:, None, :]
    shaped = values.reshape(values.shape[0], head_count, head_width)
    front_half = shaped[:, :, :half_width]
    back_half = shaped[:, :, half_width:]
    turned = jnp.concatenate(
        [front_half * cosine - back_half * sine_part, back_half * cosine + front_half * sine_part],
        axis=-1,
    )
    return turned.reshape(values.shape)


def dispatch_table(routes, experts, capacity):
    flat_routes = routes.reshape(-1)
    one_hot = (flat_routes[:, None] == jnp.arange(experts, dtype=jnp.int32)[None, :]).astype(
        jnp.int32
    )
    places = jnp.sum((jnp.cumsum(one_hot, axis=0) - 1) * one_hot, axis=1)
    targets = flat_routes * capacity + places
    sources = (
        jnp.zeros((experts * capacity,), jnp.int32)
        .at[targets]
        .set(jnp.arange(flat_routes.shape[0], dtype=jnp.int32))
    )
    filled = jnp.zeros((experts * capacity,), jnp.int32).at[targets].set(1)
    return (targets, sources, filled > 0)


def pick_gates(logits, routes):
    return jax.nn.softmax(jnp.take_along_axis(logits, routes, axis=1), axis=-1)


def router_back(gates, gate_grad, routes, experts):
    inner = jnp.sum(gates * gate_grad, axis=-1, keepdims=True)
    chosen_grad = gates * (gate_grad - inner)
    one_hot = (routes[..., None] == jnp.arange(experts, dtype=jnp.int32)).astype(jnp.float32)
    return jnp.sum(one_hot * chosen_grad[..., None], axis=1)


def norm_back(upstream, normed, scale_rms, gain):
    gain_grad = jnp.sum(upstream * normed, axis=0)
    scaled = upstream * gain
    inner = jnp.mean(scaled * normed, axis=-1, keepdims=True)
    return (scale_rms * (scaled - normed * inner), gain_grad)


def scores_of(queries, key_heads, allowed, score_scale):
    raw_scores = (
        jnp.einsum("sqkhd,suhd->skhqu", queries, key_heads, preferred_element_type=jnp.float32)
        * score_scale
    )
    return jnp.where(allowed[:, None, None], raw_scores, -jnp.inf)


def to_tokens(grouped, targets, row_count):
    flat_rows = grouped.reshape(-1, grouped.shape[-1])[targets]
    return flat_rows.reshape(row_count, TOP, grouped.shape[-1])


def local(
    hidden_in,
    cotangent,
    lengths,
    dealing,
    attn_routes,
    ffn_routes,
    attn_gain,
    attn_router,
    kv_weight,
    query_weight,
    proj_weight,
    ffn_gain,
    ffn_router,
    expert_in,
    expert_out,
):
    dp_index = lax.axis_index("dp")
    seq_count = cotangent.shape[0]
    seq_len = cotangent.shape[1]
    model_width = hidden_in.shape[2]
    rows_all = seq_count * seq_len
    head_local = query_weight.shape[2] // HD
    attn_experts = query_weight.shape[0]
    ffn_experts = expert_in.shape[0]
    capacity = seq_count * CAP
    score_scale = HD ** (-0.5)
    my_seqs = lax.dynamic_slice_in_dim(dealing, dp_index * seq_count, seq_count)
    dealt_rows = hidden_in[dealing]
    whole_seq = lax.all_to_all(dealt_rows, "dp", split_axis=0, concat_axis=1, tiled=True)
    seq_lens = lengths[my_seqs]
    attn_local = attn_routes[my_seqs].reshape(rows_all, TOP)
    ffn_local = ffn_routes[my_seqs].reshape(rows_all, TOP)
    inputs = whole_seq.reshape(rows_all, model_width).astype(jnp.float32)
    place_in_seq = jnp.arange(seq_len, dtype=jnp.int32)
    positions = jnp.tile(place_in_seq, seq_count)
    valid_rows = (
        (place_in_seq[None, :] < seq_lens[:, None]).reshape(rows_all).astype(jnp.float32)[:, None]
    )
    allowed = (place_in_seq[None, :] <= place_in_seq[:, None])[None] & (
        place_in_seq[None, None, :] < seq_lens[:, None, None]
    )
    kv_full, query_full, proj_full = (
        lax.all_gather(kv_weight, "dp", axis=1, tiled=True),
        lax.all_gather(query_weight, "dp", axis=1, tiled=True),
        lax.all_gather(proj_weight, "dp", axis=2, tiled=True),
    )
    rms_one = lax.rsqrt(jnp.mean(inputs * inputs, axis=-1, keepdims=True) + EPSILON)
    normed_one = inputs * rms_one
    attn_input = (normed_one * attn_gain).astype(jnp.bfloat16)
    attn_logits = jnp.dot(attn_input, attn_router, preferred_element_type=jnp.float32)
    attn_gates = pick_gates(attn_logits, attn_local)
    key_raw = jnp.dot(attn_input, kv_full[0], preferred_element_type=jnp.float32)
    keys_low = rotate(key_raw, positions, head_local, 1.0).astype(jnp.bfloat16)
    values_low = jnp.dot(attn_input, kv_full[1], preferred_element_type=jnp.float32).astype(
        jnp.bfloat16
    )
    key_heads = keys_low.reshape(seq_count, seq_len, head_local, HD)
    value_heads = values_low.reshape(seq_count, seq_len, head_local, HD)
    attn_targets, attn_sources, attn_filled = dispatch_table(attn_local, attn_experts, capacity)
    attn_tokens = attn_sources // TOP
    attn_grouped = attn_input[attn_tokens].reshape(attn_experts, capacity, model_width)
    query_raw = jnp.einsum(
        "ecd,edh->ech", attn_grouped, query_full, preferred_element_type=jnp.float32
    )
    slot_positions = positions[attn_tokens]
    query_group = rotate(
        query_raw.reshape(attn_experts * capacity, -1), slot_positions, head_local, 1.0
    ).astype(jnp.bfloat16)
    queries = query_group[attn_targets].reshape(seq_count, seq_len, TOP, head_local, HD)
    scores = scores_of(queries, key_heads, allowed, score_scale)
    top_score = jnp.max(scores, axis=-1, keepdims=True)
    raised = jnp.exp(scores - top_score)
    totals = jnp.sum(raised, axis=-1, keepdims=True)
    log_total = top_score + jnp.log(totals)
    attn_probs = (raised / totals).astype(jnp.bfloat16)
    mixed_heads = jnp.einsum(
        "skhqu,suhd->sqkhd", attn_probs, value_heads, preferred_element_type=jnp.float32
    )
    mixed_low = mixed_heads.reshape(rows_all * TOP, head_local * HD).astype(jnp.bfloat16)
    proj_group = mixed_low[attn_sources].reshape(attn_experts, capacity, head_local * HD)
    attn_group_out = jnp.einsum(
        "ech,ehd->ecd", proj_group, proj_full, preferred_element_type=jnp.float32
    )
    attn_slots = to_tokens(attn_group_out, attn_targets, rows_all)
    attn_part = jnp.sum(attn_gates[..., None] * attn_slots, axis=1)
    attn_total = lax.psum(attn_part, "tensor")
    after_attn = inputs + valid_rows * attn_total
    in_full, out_full = (
        lax.all_gather(expert_in, "dp", axis=1, tiled=True),
        lax.all_gather(expert_out, "dp", axis=2, tiled=True),
    )
    rms_two = lax.rsqrt(jnp.mean(after_attn * after_attn, axis=-1, keepdims=True) + EPSILON)
    normed_two = after_attn * rms_two
    ffn_input = (normed_two * ffn_gain).astype(jnp.bfloat16)
    ffn_logits = jnp.dot(ffn_input, ffn_router, preferred_element_type=jnp.float32)
    ffn_gates = pick_gates(ffn_logits, ffn_local)
    ffn_targets, ffn_sources, ffn_filled = dispatch_table(ffn_local, ffn_experts, capacity)
    ffn_grouped = ffn_input[ffn_sources // TOP].reshape(ffn_experts, capacity, model_width)
    gate_up = jnp.einsum("ecd,edjf->ecjf", ffn_grouped, in_full, preferred_element_type=jnp.float32)
    gate_pre = gate_up[:, :, 0]
    up_pre = gate_up[:, :, 1]
    hidden_low = (jax.nn.silu(gate_pre) * up_pre).astype(jnp.bfloat16)
    ffn_group_out = jnp.einsum(
        "ecf,efd->ecd", hidden_low, out_full, preferred_element_type=jnp.float32
    )
    ffn_slots = to_tokens(ffn_group_out, ffn_targets, rows_all)
    ffn_part = jnp.sum(ffn_gates[..., None] * ffn_slots, axis=1)
    ffn_total = lax.psum(ffn_part.astype(jnp.bfloat16), "tensor").astype(jnp.float32)
    result = after_attn + valid_rows * ffn_total
    dout = cotangent.reshape(rows_all, model_width).astype(jnp.float32)
    branch_grad = valid_rows * dout
    dgate_ffn_part = jnp.einsum("rkd,rd->rk", ffn_slots, branch_grad)
    dslot_ffn = (ffn_gates[..., None] * branch_grad[:, None, :]).astype(jnp.bfloat16)
    dslot_group = dslot_ffn.reshape(rows_all * TOP, model_width)[ffn_sources]
    dslot_group = jnp.where(ffn_filled[:, None], dslot_group, jnp.zeros_like(dslot_group)).reshape(
        ffn_experts, capacity, model_width
    )
    in_back, out_back = (
        lax.all_gather(expert_in, "dp", axis=1, tiled=True),
        lax.all_gather(expert_out, "dp", axis=2, tiled=True),
    )
    dhidden = jnp.einsum("ecd,efd->ecf", dslot_group, out_back, preferred_element_type=jnp.float32)
    sigma = jax.nn.sigmoid(gate_pre)
    dgate_pre = (dhidden * up_pre * sigma * (1.0 + gate_pre * (1.0 - sigma))).astype(jnp.bfloat16)
    dup_pre = (dhidden * gate_pre * sigma).astype(jnp.bfloat16)
    dgate_up = jnp.stack([dgate_pre, dup_pre], axis=2)
    dffn_group = jnp.einsum("ecjf,edjf->ecd", dgate_up, in_back, preferred_element_type=jnp.float32)
    dffn_part = jnp.sum(to_tokens(dffn_group, ffn_targets, rows_all), axis=1)
    in_shards = []
    out_shards = []
    for expert in range(ffn_experts):
        in_term = jnp.einsum(
            "cd,cjf->djf", ffn_grouped[expert], dgate_up[expert], preferred_element_type=jnp.float32
        )
        out_term = jnp.einsum(
            "cf,cd->fd", hidden_low[expert], dslot_group[expert], preferred_element_type=jnp.float32
        )
        in_piece, out_piece = (
            lax.psum_scatter(
                in_term.astype(jnp.bfloat16), "dp", scatter_dimension=0, tiled=True
            ).astype(jnp.float32),
            lax.psum_scatter(
                out_term.astype(jnp.bfloat16), "dp", scatter_dimension=1, tiled=True
            ).astype(jnp.float32),
        )
        in_shards.append(in_piece)
        out_shards.append(out_piece)
    expertin_grad = jnp.stack(in_shards, axis=0)
    expertout_grad = jnp.stack(out_shards, axis=0)
    dffn_sum, dgate_ffn = (
        lax.psum(dffn_part.astype(jnp.bfloat16), "tensor").astype(jnp.float32),
        lax.psum(dgate_ffn_part.astype(jnp.bfloat16), "tensor").astype(jnp.float32),
    )
    dlogit_ffn = router_back(ffn_gates, dgate_ffn, ffn_local, ffn_experts)
    ffnrouter_part = jnp.einsum(
        "rd,re->de", ffn_input.astype(jnp.float32), dlogit_ffn, precision=BEST
    )
    dffn_input = dffn_sum + jnp.dot(dlogit_ffn, ffn_router.astype(jnp.float32).T, precision=BEST)
    dafter_norm, ffngain_part = norm_back(dffn_input, normed_two, rms_two, ffn_gain)
    dafter = dout + dafter_norm
    attn_branch = valid_rows * dafter
    dgate_attn_part = jnp.einsum("rkd,rd->rk", attn_slots, attn_branch)
    dslot_attn = (attn_gates[..., None] * attn_branch[:, None, :]).astype(jnp.bfloat16)
    dslot_agroup = dslot_attn.reshape(rows_all * TOP, model_width)[attn_sources]
    dslot_agroup = jnp.where(
        attn_filled[:, None], dslot_agroup, jnp.zeros_like(dslot_agroup)
    ).reshape(attn_experts, capacity, model_width)
    kv_back, query_back, proj_back = (
        lax.all_gather(kv_weight, "dp", axis=1, tiled=True),
        lax.all_gather(query_weight, "dp", axis=1, tiled=True),
        lax.all_gather(proj_weight, "dp", axis=2, tiled=True),
    )
    proj_term = jnp.einsum(
        "ech,ecd->ehd", proj_group, dslot_agroup, preferred_element_type=jnp.float32
    )
    dmixed_group = jnp.einsum(
        "ecd,ehd->ech", dslot_agroup, proj_back, preferred_element_type=jnp.float32
    ).astype(jnp.bfloat16)
    dmixed = dmixed_group.reshape(attn_experts * capacity, -1)[attn_targets].reshape(
        seq_count, seq_len, TOP, head_local, HD
    )
    scores_again = scores_of(queries, key_heads, allowed, score_scale)
    probs_full = jnp.exp(scores_again - log_total)
    probs_low = probs_full.astype(jnp.bfloat16)
    dvalues = jnp.einsum("skhqu,sqkhd->suhd", probs_low, dmixed, preferred_element_type=jnp.float32)
    dvalues_low = dvalues.reshape(rows_all, head_local * HD).astype(jnp.bfloat16)
    dprob = jnp.einsum("sqkhd,suhd->skhqu", dmixed, value_heads, preferred_element_type=jnp.float32)
    delta_sum = jnp.sum(probs_full * dprob, axis=-1, keepdims=True)
    dscores = (probs_full * (dprob - delta_sum)).astype(jnp.bfloat16)
    dkeys = score_scale * jnp.einsum(
        "skhqu,sqkhd->suhd", dscores, queries, preferred_element_type=jnp.float32
    )
    dkeys_low = rotate(
        dkeys.reshape(rows_all, head_local * HD), positions, head_local, -1.0
    ).astype(jnp.bfloat16)
    dqueries = score_scale * jnp.einsum(
        "skhqu,suhd->sqkhd", dscores, key_heads, preferred_element_type=jnp.float32
    )
    dquery_rows = dqueries.reshape(rows_all * TOP, head_local * HD)[attn_sources]
    dquery_rows = jnp.where(attn_filled[:, None], dquery_rows, jnp.zeros_like(dquery_rows))
    dquery_group = (
        rotate(dquery_rows, slot_positions, head_local, -1.0)
        .astype(jnp.bfloat16)
        .reshape(attn_experts, capacity, head_local * HD)
    )
    query_term = jnp.einsum(
        "ecd,ech->edh", attn_grouped, dquery_group, preferred_element_type=jnp.float32
    )
    kv_term = jnp.stack(
        [
            jnp.einsum("rd,rh->dh", attn_input, dkeys_low, preferred_element_type=jnp.float32),
            jnp.einsum("rd,rh->dh", attn_input, dvalues_low, preferred_element_type=jnp.float32),
        ],
        axis=0,
    )
    kv_grad, query_grad, proj_grad = (
        lax.psum_scatter(
            kv_term.astype(jnp.bfloat16), "dp", scatter_dimension=1, tiled=True
        ).astype(jnp.float32),
        lax.psum_scatter(
            query_term.astype(jnp.bfloat16), "dp", scatter_dimension=1, tiled=True
        ).astype(jnp.float32),
        lax.psum_scatter(
            proj_term.astype(jnp.bfloat16), "dp", scatter_dimension=2, tiled=True
        ).astype(jnp.float32),
    )
    dquery_input = jnp.einsum(
        "ech,edh->ecd", dquery_group, query_back, preferred_element_type=jnp.float32
    )
    dattn_part = jnp.sum(to_tokens(dquery_input, attn_targets, rows_all), axis=1)
    dattn_part = dattn_part + jnp.einsum(
        "rh,dh->rd", dkeys_low, kv_back[0], preferred_element_type=jnp.float32
    )
    dattn_part = dattn_part + jnp.einsum(
        "rh,dh->rd", dvalues_low, kv_back[1], preferred_element_type=jnp.float32
    )
    dattn_sum, dgate_attn = (
        lax.psum(dattn_part.astype(jnp.bfloat16), "tensor").astype(jnp.float32),
        lax.psum(dgate_attn_part.astype(jnp.bfloat16), "tensor").astype(jnp.float32),
    )
    dlogit_attn = router_back(attn_gates, dgate_attn, attn_local, attn_experts)
    attnrouter_part = jnp.einsum(
        "rd,re->de", attn_input.astype(jnp.float32), dlogit_attn, precision=BEST
    )
    dattn_input = dattn_sum + jnp.dot(
        dlogit_attn, attn_router.astype(jnp.float32).T, precision=BEST
    )
    dinput_norm, attngain_part = norm_back(dattn_input, normed_one, rms_one, attn_gain)
    input_rows = dafter + dinput_norm
    attngain_grad, attnrouter_grad, ffngain_grad, ffnrouter_grad = (
        lax.psum(attngain_part.astype(jnp.bfloat16), "dp").astype(jnp.float32),
        lax.psum(attnrouter_part.astype(jnp.bfloat16), "dp").astype(jnp.float32),
        lax.psum(ffngain_part.astype(jnp.bfloat16), "dp").astype(jnp.float32),
        lax.psum(ffnrouter_part.astype(jnp.bfloat16), "dp").astype(jnp.float32),
    )
    out_seq = result.astype(jnp.bfloat16).reshape(seq_count, seq_len, model_width)
    grad_seq = input_rows.astype(jnp.bfloat16).reshape(seq_count, seq_len, model_width)
    out_dealt, grad_dealt = (
        lax.all_to_all(out_seq, "dp", split_axis=1, concat_axis=0, tiled=True),
        lax.all_to_all(grad_seq, "dp", split_axis=1, concat_axis=0, tiled=True),
    )
    inverse = jnp.zeros_like(dealing).at[dealing].set(jnp.arange(dealing.shape[0], dtype=jnp.int32))
    return (
        out_dealt[inverse],
        grad_dealt[inverse],
        attngain_grad,
        attnrouter_grad,
        kv_grad,
        query_grad,
        proj_grad,
        ffngain_grad,
        ffnrouter_grad,
        expertin_grad,
        expertout_grad,
    )


def solution(mesh):
    placed = (
        P(None, "dp", None),
        P("dp", None, None),
        P(),
        P(),
        P(),
        P(),
        P(),
        P(),
        P(None, "dp", "tensor"),
        P(None, "dp", "tensor"),
        P(None, "tensor", "dp"),
        P(),
        P(),
        P(None, "dp", None, "tensor"),
        P(None, "tensor", "dp"),
    )
    return jax.shard_map(
        local,
        mesh=mesh,
        in_specs=placed,
        out_specs=(
            P(None, "dp", None),
            P(None, "dp", None),
            P(),
            P(),
            P(None, "dp", "tensor"),
            P(None, "dp", "tensor"),
            P(None, "tensor", "dp"),
            P(),
            P(),
            P(None, "dp", None, "tensor"),
            P(None, "tensor", "dp"),
        ),
        check_vma=False,
    )
```

profile of v0, /device:TPU:0, one launch (start us, length us, event | category | flops | bytes accessed | tf_op | source)
XLA Modules:
  0.0 1806.4 jit_solution(6847102434269989911)
XLA Ops:
  11.5 5.2 all-to-all-start
  25.8 5.0 gather_fusion.2
  43.6 4.8 gather_fusion.16
  49.3 8.3 all-gather.6.cloned.1.call-done
  69.8 44.0 %all-gather.8.cloned.1.call-done = bf16[4,2048,512]{2,1,0:T(8,128)(2,1)} async-done(((bf16[4,256,512]{2,1,0:T(8,128)(2,1)}), bf16[4,2048,512]{2,1,0:T(8,128)(2,1)}) %all-gather.8.cloned.1.call-update) | async-done | bytes 8388624 | tf_op jit(solution)/shard_map/all_gather | solution.py:124
  113.7 7.3 fusion.121
  136.5 35.0 %all-gather.10.cloned.1.call-done = bf16[4,512,2048]{2,1,0:T(8,128)(2,1)} async-done(((bf16[4,512,256]{2,1,0:T(8,128)(2,1)}), bf16[4,512,2048]{2,1,0:T(8,128)(2,1)}) %all-gather.10.cloned.1.call-update) | async-done | bytes 8388624 | tf_op jit(solution)/shard_map/all_gather | solution.py:125
  171.5 8.1 fusion.122
  179.6 8.2 gather_fusion.5
  187.8 6.2 reshape.685
  194.0 10.1 multiply_reduce_fusion.1
  204.2 5.9 copy.192
  223.8 66.7 %all-reduce.6.cloned.1.call-done = f32[256,2048]{1,0:T(8,128)} async-done(((f32[256,2048]{1,0:T(8,128)}), f32[256,2048]{1,0:T(8,128)}) %all-reduce.6.cloned.1.call-update) | async-done | bytes 2097168 | tf_op jit(solution)/shard_map/psum | solution.py:166
  300.5 4.8 gather_fusion.17
  305.6 6.2 mul.619
  311.8 6.1 mul.620
  317.9 188.2 %all-gather.12.cloned.1.call-done = bf16[4,2048,2,1408]{3,1,2,0:T(8,128)(2,1)} async-done(((bf16[4,256,2,1408]{3,1,2,0:T(8,128)(2,1)}), bf16[4,2048,2,1408]{3,1,2,0:T(8,128)(2,1)}) %all-gather.12.cloned.1.call-update) | async-done | bytes 46137360 | tf_op jit(solution)/shard_map/all_gather | solution.py:169
  506.0 23.5 %fusion.124 = f32[4,192,2,1408]{3,1,2,0:T(8,128)} fusion(bf16[4,192,2048,1]{2,1,3,0:T(8,128)(2,1)} %bitcast.359, bf16[4,2048,2,1408]{3,1,2,0:T(8,128)(2,1)} %all-gather.12.cloned.1.call-done), kind=kOutput, calls=%fused_computation.307 | convolution fusion | flops 8858370048 | bytes 57933824 | tf_op jit(solution)/shard_map/ecd,edjf->ecjf/dot_general | solution.py:179
  529.5 4.8 multiply_convert_fusion.2
  534.3 94.4 %all-gather.14.cloned.1.call-done = bf16[4,1408,2048]{2,1,0:T(8,128)(2,1)} async-done(((bf16[4,1408,256]{2,1,0:T(8,128)(2,1)}), bf16[4,1408,2048]{2,1,0:T(8,128)(2,1)}) %all-gather.14.cloned.1.call-update) | async-done | bytes 23068688 | tf_op jit(solution)/shard_map/all_gather | solution.py:170
  628.7 11.8 fusion.125
  640.5 8.2 gather_fusion.7
  648.7 6.2 reshape.690
  654.9 6.7 fusion.31
  661.7 11.7 psum.73
  680.4 16.6 fusion.10
  697.0 23.6 %fusion = f32[4,192,2048,1]{2,1,0,3:T(8,128)} fusion(bf16[4,2048,2,1408]{3,1,2,0:T(8,128)(2,1)} %all-gather.12.cloned.1.call-done, bf16[4,192,1,1408]{3,1,0,2:T(8,128)(2,1)} %get-tuple-element.123, bf16[4,192,1,1408]{3,1,0,2:T(8,128)(2,1)S(1)} %get-tuple-element.122), kind=kOutput, calls=%fused_computation.23 | convolution fusion | flops 8860532736 | bytes 56754176 | tf_op jit(solution)/shard_map/ecjf,edjf->ecd/dot_general | solution.py:207
  720.6 8.2 gather_fusion.10
  728.8 5.8 reshape.693
  734.7 8.3 reduce_sum.195
  743.6 10.1 multiply_reduce_fusion
  753.7 38.7 %all-reduce.8.cloned.1.call-done = bf16[256,2048]{1,0:T(8,128)(2,1)} async-done(((bf16[256,2048]{1,0:T(8,128)(2,1)}), bf16[256,2048]{1,0:T(8,128)(2,1)}) %all-reduce.8.cloned.1.call-update) | async-done | bytes 1048592 | tf_op jit(solution)/shard_map/psum | solution.py:231
  803.2 6.4 mul.641
  816.4 7.3 fusion.40
  844.7 8.9 fusion.126
  853.7 8.2 gather_fusion.14
  861.8 6.0 reshape.699
  867.8 7.2 reduce_sum.200
  895.0 5.3 convolution_convert_fusion.5
  900.4 5.2 convolution_convert_fusion.6
  905.7 5.3 convolution_convert_fusion.7
  911.1 7.6 convolution_convert_fusion.9
  919.9 7.7 convolution_convert_fusion.8
  929.3 9.0 convolution_convert_fusion
  938.4 8.8 convolution_convert_fusion.1
  947.3 8.7 convolution_convert_fusion.2
  956.3 8.7 convolution_convert_fusion.3
  965.1 8.4 fusion.29
  973.6 10.5 psum.75
  993.3 6.8 reduce.11
  1007.9 7.8 reduce.12
  1018.5 8.8 all-to-all-done.1
  1033.3 31.9 %all-reduce = (bf16[2048]{0:T(1024)(128)(2,1)S(1)}, bf16[2048,4]{0,1:T(4,128)(2,1)S(1)}, bf16[2048]{0:T(1024)(128)(2,1)S(1)}, bf16[2048,4]{0,1:T(4,128)(2,1)S(1)}) all-reduce(bf16[2048]{0:T(1024)(128)(2,1)S(1)} %get-tuple-element.102, bf16[2048,4]{0,1:T(4,128)(2,1)S(1)} %convolution_convert_fusion.13, ...), channel_id=1, replica_groups=mesh['dp'=8,'tensor'=4] {'dp'}, use_global_device_ids=true, to_apply=%region_37.39 | all-reduce | flops 20480 | bytes 81920 | tf_op jit(solution)/shard_map/psum | solution.py:331
  1088.0 62.4 %reduce-scatter.30.cloned.1.call-done = bf16[1408,256]{1,0:T(8,128)(2,1)} async-done(((bf16[1408,2048]{1,0:T(8,128)(2,1)}), bf16[1408,256]{1,0:T(8,128)(2,1)}) %reduce-scatter.30.cloned.1.call-update) | async-done | bytes 720912 | tf_op jit(solution)/shard_map/reduce_scatter | solution.py:222
  1150.3 62.2 %reduce-scatter.28.cloned.1.call-done = bf16[1408,256]{1,0:T(8,128)(2,1)} async-done(((bf16[1408,2048]{1,0:T(8,128)(2,1)}), bf16[1408,256]{1,0:T(8,128)(2,1)}) %reduce-scatter.28.cloned.1.call-update) | async-done | bytes 720912 | tf_op jit(solution)/shard_map/reduce_scatter | solution.py:222
  1212.5 62.4 %reduce-scatter.26.cloned.1.call-done = bf16[1408,256]{1,0:T(8,128)(2,1)} async-done(((bf16[1408,2048]{1,0:T(8,128)(2,1)}), bf16[1408,256]{1,0:T(8,128)(2,1)}) %reduce-scatter.26.cloned.1.call-update) | async-done | bytes 720912 | tf_op jit(solution)/shard_map/reduce_scatter | solution.py:222
  1274.9 4.8 maximum_convert_fusion.1
  1279.7 70.1 %reduce-scatter.14.cloned.1.call-done = bf16[4,256,512]{2,1,0:T(8,128)(2,1)} async-done(((bf16[4,2048,512]{2,1,0:T(8,128)(2,1)}), bf16[4,256,512]{2,1,0:T(8,128)(2,1)}) %reduce-scatter.14.cloned.1.call-update) | async-done | bytes 1048592 | tf_op jit(solution)/shard_map/reduce_scatter | solution.py:300
  1352.6 71.8 %reduce-scatter.16.cloned.1.call-done = bf16[4,512,256]{2,1,0:T(8,128)(2,1)} async-done(((bf16[4,512,2048]{2,1,0:T(8,128)(2,1)}), bf16[4,512,256]{2,1,0:T(8,128)(2,1)}) %reduce-scatter.16.cloned.1.call-update) | async-done | bytes 1048592 | tf_op jit(solution)/shard_map/reduce_scatter | solution.py:303
  1427.1 88.2 %reduce-scatter.24.cloned.1.call-done = bf16[256,2,1408]{2,0,1:T(8,128)(2,1)} async-done(((bf16[2048,2,1408]{2,0,1:T(8,128)(2,1)}), bf16[256,2,1408]{2,0,1:T(8,128)(2,1)}) %reduce-scatter.24.cloned.1.call-update) | async-done | bytes 1441808 | tf_op jit(solution)/shard_map/reduce_scatter | solution.py:219
  1515.3 90.3 %reduce-scatter.22.cloned.1.call-done = bf16[256,2,1408]{2,0,1:T(8,128)(2,1)} async-done(((bf16[2048,2,1408]{2,0,1:T(8,128)(2,1)}), bf16[256,2,1408]{2,0,1:T(8,128)(2,1)}) %reduce-scatter.22.cloned.1.call-update) | async-done | bytes 1441808 | tf_op jit(solution)/shard_map/reduce_scatter | solution.py:219
  1605.6 90.3 %reduce-scatter.20.cloned.1.call-done = bf16[256,2,1408]{2,0,1:T(8,128)(2,1)} async-done(((bf16[2048,2,1408]{2,0,1:T(8,128)(2,1)}), bf16[256,2,1408]{2,0,1:T(8,128)(2,1)}) %reduce-scatter.20.cloned.1.call-update) | async-done | bytes 1441808 | tf_op jit(solution)/shard_map/reduce_scatter | solution.py:219
  1696.0 90.5 %reduce-scatter.18.cloned.1.call-done = bf16[256,2,1408]{2,0,1:T(8,128)(2,1)} async-done(((bf16[2048,2,1408]{2,0,1:T(8,128)(2,1)}), bf16[256,2,1408]{2,0,1:T(8,128)(2,1)}) %reduce-scatter.18.cloned.1.call-update) | async-done | bytes 1441808 | tf_op jit(solution)/shard_map/reduce_scatter | solution.py:219
  1790.2 9.3 copy.207
  (406 shorter events, 202.9 us)
Async XLA Ops:
  7.2 50.4 %all-gather.6.cloned.1.call-start = ((), (), s32[]{:S(2)}) async-start(), calls=%async_computation.14 | async-start | bytes 4718592 | tf_op jit(solution)/shard_map/all_gather | solution.py:123
  7.9 105.8 %all-gather.8.cloned.1.call-start = ((), (), s32[]{:S(2)}) async-start(), calls=%async_computation.15 | async-start | bytes 9437184 | tf_op jit(solution)/shard_map/all_gather | solution.py:124
  8.7 162.8 %all-gather.10.cloned.1.call-start = ((), (), s32[]{:S(2)}) async-start(), calls=%async_computation.16 | async-start | bytes 9437184 | tf_op jit(solution)/shard_map/all_gather | solution.py:125
  11.5 26.1 %all-to-all-start = ((bf16[8,32,2048]{2,1,0:T(8,128)(2,1)}), bf16[8,32,2048]{2,1,0:T(8,128)(2,1)S(1)}, u32[]{:S(2)}, u32[]{:S(2)}) async-start(bf16[8,32,2048]{2,1,0:T(8,128)(2,1)} %gather_fusion), calls=%async_computation | async-start | bytes 2097152 | tf_op jit(solution)/shard_map/all_to_all | solution.py:109
  16.7 273.7 %all-reduce.6.cloned.1.call-start = ((), (), s32[]{:S(2)}) async-start(), calls=%async_computation.17 | async-start | bytes 4194304 | tf_op jit(solution)/shard_map/psum | solution.py:166
  20.6 28.1 %copy-start.63 = (s32[1,256,2]{1,2,0:T(2,128)}, s32[1,256,2]{1,2,0:T(2,128)S(1)}, u32[]{:S(2)}) copy-start(s32[1,256,2]{1,2,0:T(2,128)S(1)} %get-tuple-element.152) | copy-start | bytes 6148
  21.4 9.5 copy-start.90
  23.1 8.7 copy-start.87
  33.1 100.7 %copy-start.61 = (s32[1024]{0:T(1024)}, s32[1024]{0:T(1024)S(1)}, u32[]{:S(2)}) copy-start(s32[1024]{0:T(1024)S(1)} %pad_clamp_fusion.4) | copy-start | bytes 12292
  37.2 86.6 %copy-start.36 = (f32[768,64]{1,0:T(8,128)}, f32[768,64]{1,0:T(8,128)S(1)}, u32[]{:S(2)}) copy-start(f32[768,64]{1,0:T(8,128)S(1)} %get-tuple-element.136) | copy-start | bytes 589828
  37.7 252.8 %copy-start.13 = (bf16[8,32,2048]{2,1,0:T(8,128)(2,1)}, bf16[8,32,2048]{2,1,0:T(8,128)(2,1)S(1)}, u32[]{:S(2)}) copy-start(bf16[8,32,2048]{2,1,0:T(8,128)(2,1)S(1)} %all-to-all-done) | copy-start | bytes 3145732
  48.7 11.9 copy-start.65
  48.7 11.9 copy-start.73
  48.8 11.8 copy-start.80
  48.9 145.1 %copy-start.43 = (f32[256,2]{1,0:T(8,128)}, f32[256,2]{1,0:T(8,128)S(1)}, u32[]{:S(2)}) copy-start(f32[256,2]{1,0:T(8,128)S(1)} %copy.176) | copy-start | bytes 6148
  49.3 17.7 copy-start.26
  67.0 64.9 %copy-start.45 = (bf16[256,4,128]{2,1,0:T(4,128)(2,1)}, bf16[256,4,128]{2,1,0:T(4,128)(2,1)S(1)}, u32[]{:S(2)}) copy-start(bf16[256,4,128]{2,1,0:T(4,128)(2,1)S(1)} %reshape.678) | copy-start | bytes 786436
  69.7 61.2 %copy-start.39 = (bf16[256,4,64]{0,2,1:T(8,128)(2,1)}, bf16[256,4,64]{0,2,1:T(8,128)(2,1)S(1)}, u32[]{:S(2)}) copy-start(bf16[256,4,64]{0,2,1:T(8,128)(2,1)S(1)} %get-tuple-element.132) | copy-start | bytes 393220
  69.8 61.2 %copy-start.41 = (bf16[256,4,64]{0,2,1:T(8,128)(2,1)}, bf16[256,4,64]{0,2,1:T(8,128)(2,1)S(1)}, u32[]{:S(2)}) copy-start(bf16[256,4,64]{0,2,1:T(8,128)(2,1)S(1)} %get-tuple-element.133) | copy-start | bytes 393220
  136.5 43.1 %copy-start.23 = (bf16[768,512]{1,0:T(8,128)(2,1)}, bf16[768,512]{1,0:T(8,128)(2,1)S(1)}, u32[]{:S(2)}) copy-start(bf16[768,512]{1,0:T(8,128)(2,1)S(1)} %gather_fusion.4) | copy-start | bytes 2359300
  204.2 301.9 %all-gather.12.cloned.1.call-start = ((), (), s32[]{:S(2)}) async-start(), calls=%async_computation.18 | async-start | bytes 51904512 | tf_op jit(solution)/shard_map/all_gather | solution.py:169
  210.2 11.2 copy-start.86
  210.2 12.4 copy-start.19
  210.2 418.5 %all-gather.14.cloned.1.call-start = ((), (), s32[]{:S(2)}) async-start(), calls=%async_computation.19 | async-start | bytes 25952256 | tf_op jit(solution)/shard_map/all_gather | solution.py:170
  210.8 581.5 %all-reduce.8.cloned.1.call-start = ((), (), s32[]{:S(2)}) async-start(), calls=%async_computation.20 | async-start | bytes 2097152 | tf_op jit(solution)/shard_map/psum | solution.py:231
  222.5 71.6 %copy-start.77 = (f32[256]{0:T(256)}, f32[256]{0:T(256)S(1)}, u32[]{:S(2)}) copy-start(f32[256]{0:T(256)S(1)} %fusion.111) | copy-start | bytes 3076
  223.7 71.6 %copy-start.53 = (f32[2048]{0:T(1024)S(1)}, f32[2048]{0:T(1024)}, u32[]{:S(2)}) copy-start(f32[2048]{0:T(1024)} %param.28) | copy-start | bytes 24580
  534.3 106.2 %copy-start.6 = (bf16[4,192,1408]{2,1,0:T(8,128)(2,1)}, bf16[4,192,1408]{2,1,0:T(8,128)(2,1)S(1)}, u32[]{:S(2)}) copy-start(bf16[4,192,1408]{2,1,0:T(8,128)(2,1)S(1)} %multiply_convert_fusion.2) | copy-start | bytes 6488068
  697.0 23.6 %copy-start.15 = (bf16[4,192,1,1408]{3,1,0,2:T(8,128)(2,1)}, bf16[4,192,1,1408]{3,1,0,2:T(8,128)(2,1)S(1)}, u32[]{:S(2)}) copy-start(bf16[4,192,1,1408]{3,1,0,2:T(8,128)(2,1)S(1)} %get-tuple-element.122) | copy-start | bytes 6488068
  734.7 8.8 copy-start.56
  734.7 8.8 copy-start.70
  743.0 241.2 %all-reduce.10.cloned.1.call-start = ((), (), s32[]{:S(2)}) async-start(), calls=%async_computation.32 | async-start | bytes 4194304 | tf_op jit(solution)/shard_map/psum | solution.py:188
  743.5 48.8 %copy-start.9 = (f32[256,2048]{1,0:T(8,128)S(1)}, f32[256,2048]{1,0:T(8,128)}, u32[]{:S(2)}) copy-start(f32[256,2048]{1,0:T(8,128)} %copy-done.8) | copy-start | bytes 6291460
  743.5 48.8 %copy-start.54 = (f32[2048]{0:T(1024)S(1)}, f32[2048]{0:T(1024)}, u32[]{:S(2)}) copy-start(f32[2048]{0:T(1024)} %param.28) | copy-start | bytes 24580
  743.5 48.8 %copy-start.60 = (bf16[2048,4]{0,1:T(4,128)(2,1)S(1)}, bf16[2048,4]{0,1:T(4,128)(2,1)}, u32[]{:S(2)}) copy-start(bf16[2048,4]{0,1:T(4,128)(2,1)} %param.29) | copy-start | bytes 49156
  743.5 48.8 %copy-start.72 = (f32[256]{0:T(256)S(1)}, f32[256]{0:T(256)}, u32[]{:S(2)}) copy-start(f32[256]{0:T(256)} %copy-done.71) | copy-start | bytes 3076
  753.7 43.0 %copy-start.20 = (bf16[1,256,2048]{2,1,0:T(8,128)(2,1)S(1)}, bf16[1,256,2048]{2,1,0:T(8,128)(2,1)}, u32[]{:S(2)}) copy-start(bf16[1,256,2048]{2,1,0:T(8,128)(2,1)} %param.18) | copy-start | bytes 3145732
  753.7 43.0 %copy-start.78 = (f32[256]{0:T(256)S(1)}, f32[256]{0:T(256)}, u32[]{:S(2)}) copy-start(f32[256]{0:T(256)} %copy-done.77) | copy-start | bytes 3076
  816.4 11.6 copy-start.46
  880.8 201.0 %reduce-scatter.12.cloned.1.call-start = ((), (), s32[]{:S(2)}) async-start(), calls=%async_computation.21 | async-start | bytes 4718592 | tf_op jit(solution)/shard_map/reduce_scatter | solution.py:297
  886.0 202.0 %reduce-scatter.32.cloned.1.call-start = ((), (), s32[]{:S(2)}) async-start(), calls=%async_computation.31 | async-start | bytes 6488064 | tf_op jit(solution)/shard_map/reduce_scatter | solution.py:222
  894.8 255.6 %reduce-scatter.30.cloned.1.call-start = ((), (), s32[]{:S(2)}) async-start(), calls=%async_computation.30 | async-start | bytes 6488064 | tf_op jit(solution)/shard_map/reduce_scatter | solution.py:222
  900.4 312.2 %reduce-scatter.28.cloned.1.call-start = ((), (), s32[]{:S(2)}) async-start(), calls=%async_computation.29 | async-start | bytes 6488064 | tf_op jit(solution)/shard_map/reduce_scatter | solution.py:222
  905.7 369.2 %reduce-scatter.26.cloned.1.call-start = ((), (), s32[]{:S(2)}) async-start(), calls=%async_computation.28 | async-start | bytes 6488064 | tf_op jit(solution)/shard_map/reduce_scatter | solution.py:222
  911.1 438.7 %reduce-scatter.14.cloned.1.call-start = ((), (), s32[]{:S(2)}) async-start(), calls=%async_computation.22 | async-start | bytes 9437184 | tf_op jit(solution)/shard_map/reduce_scatter | solution.py:300
  918.8 505.6 %reduce-scatter.16.cloned.1.call-start = ((), (), s32[]{:S(2)}) async-start(), calls=%async_computation.23 | async-start | bytes 9437184 | tf_op jit(solution)/shard_map/reduce_scatter | solution.py:303
  927.6 587.7 %reduce-scatter.24.cloned.1.call-start = ((), (), s32[]{:S(2)}) async-start(), calls=%async_computation.27 | async-start | bytes 12976128 | tf_op jit(solution)/shard_map/reduce_scatter | solution.py:219
  938.3 667.3 %reduce-scatter.22.cloned.1.call-start = ((), (), s32[]{:S(2)}) async-start(), calls=%async_computation.26 | async-start | bytes 12976128 | tf_op jit(solution)/shard_map/reduce_scatter | solution.py:219
  947.2 748.8 %reduce-scatter.20.cloned.1.call-start = ((), (), s32[]{:S(2)}) async-start(), calls=%async_computation.25 | async-start | bytes 12976128 | tf_op jit(solution)/shard_map/reduce_scatter | solution.py:219
  956.0 830.4 %reduce-scatter.18.cloned.1.call-start = ((), (), s32[]{:S(2)}) async-start(), calls=%async_computation.24 | async-start | bytes 12976128 | tf_op jit(solution)/shard_map/reduce_scatter | solution.py:219
  965.0 19.1 %copy-start.66 = (f32[256,2]{0,1:T(2,128)S(1)}, f32[256,2]{0,1:T(2,128)}, u32[]{:S(2)}) copy-start(f32[256,2]{0,1:T(2,128)} %copy-done.65) | copy-start | bytes 6148
  965.0 19.0 %copy-start.74 = (f32[256]{0:T(256)S(1)}, f32[256]{0:T(256)}, u32[]{:S(2)}) copy-start(f32[256]{0:T(256)} %copy-done.73) | copy-start | bytes 3076
  965.0 19.0 %copy-start.81 = (f32[256]{0:T(256)S(1)}, f32[256]{0:T(256)}, u32[]{:S(2)}) copy-start(f32[256]{0:T(256)} %copy-done.80) | copy-start | bytes 3076
  965.1 19.1 %copy-start.64 = (s32[1,256,2]{1,2,0:T(2,128)S(1)}, s32[1,256,2]{1,2,0:T(2,128)}, u32[]{:S(2)}) copy-start(s32[1,256,2]{1,2,0:T(2,128)} %copy-done.63) | copy-start | bytes 6148
  965.1 19.1 %copy-start.14 = (bf16[8,32,2048]{2,1,0:T(8,128)(2,1)S(1)}, bf16[8,32,2048]{2,1,0:T(8,128)(2,1)}, u32[]{:S(2)}) copy-start(bf16[8,32,2048]{2,1,0:T(8,128)(2,1)} %copy-done.13) | copy-start | bytes 3145732
  965.1 19.1 %copy-start.58 = (f32[2048]{0:T(1024)S(1)}, f32[2048]{0:T(1024)}, u32[]{:S(2)}) copy-start(f32[2048]{0:T(1024)} %param.23) | copy-start | bytes 24580
  965.1 19.1 %copy-start.76 = (bf16[2048,4]{0,1:T(4,128)(2,1)S(1)}, bf16[2048,4]{0,1:T(4,128)(2,1)}, u32[]{:S(2)}) copy-start(bf16[2048,4]{0,1:T(4,128)(2,1)} %param.24) | copy-start | bytes 49156
  965.1 19.1 %copy-start.83 = (f32[256]{0:T(256)S(1)}, f32[256]{0:T(256)}, u32[]{:S(2)}) copy-start(f32[256]{0:T(256)} %copy-done.82) | copy-start | bytes 3076
  965.1 22.3 %copy-start.21 = (bf16[1,256,2048]{2,1,0:T(8,128)(2,1)S(1)}, bf16[1,256,2048]{2,1,0:T(8,128)(2,1)}, u32[]{:S(2)}) copy-start(bf16[1,256,2048]{2,1,0:T(8,128)(2,1)} %param.18) | copy-start | bytes 3145732
  1001.7 25.6 %all-to-all-start.1 = ((bf16[8,2,32768]{2,1,0:T(2,128)(2,1)}), bf16[8,2,32768]{2,1,0:T(2,128)(2,1)}, u32[]{:S(2)}, u32[]{:S(2)}) async-start(bf16[8,2,32768]{2,1,0:T(2,128)(2,1)} %reshape.1008), calls=%async_computation.1 | async-start | bytes 2097152 | tf_op jit(solution)/shard_map/all_to_all | solution.py:339
  1015.7 16.6 copy-start.5
  1015.7 17.1 copy-start.3
  1027.3 45.4 %all-to-all-start.2 = ((bf16[8,2,32768]{2,1,0:T(2,128)(2,1)}), bf16[8,2,32768]{2,1,0:T(2,128)(2,1)}, u32[]{:S(2)}, u32[]{:S(2)}) async-start(bf16[8,2,32768]{2,1,0:T(2,128)(2,1)} %reshape.1010), calls=%async_computation.2 | async-start | bytes 2097152 | tf_op jit(solution)/shard_map/all_to_all | solution.py:340
  1790.2 9.4 copy-start.1
  (49 other events, 146.1 us)
Sparse Core Ops, SparseCore 0:
  9.9 47.5 all-gather.5
  59.5 54.2 all-gather.7
  115.6 55.8 all-gather.9
  204.3 86.1 all-reduce.5
  292.8 213.1 all-gather.11
  507.8 120.8 all-gather.13
  743.1 49.1 all-reduce.7
  880.9 85.4 all-reduce.9
  969.8 55.8 reduce-scatter.11
  1029.5 58.4 reduce-scatter.31
  1091.4 58.8 reduce-scatter.29
  1153.6 58.8 reduce-scatter.27
  1216.0 58.8 reduce-scatter.25
  1278.2 71.4 reduce-scatter.13
  1353.0 71.2 reduce-scatter.15
  1428.3 86.9 reduce-scatter.23
  1518.6 86.9 reduce-scatter.21
  1609.0 86.9 reduce-scatter.19
  1699.5 86.9 reduce-scatter.17
where the time goes:
time: 1810 us
  waiting for transfers between devices  1180 us (65%)
  matrix products  216 us (12%)
  local copies, waits for them, and re-layouts  207 us (11%)
  other arithmetic  116 us (6%)
  blocking collectives  54.1 us (3%)
    reduce_scatter x4, waiting for transfers between devices, local(): lax.psum_scatter(in_term.astype(jnp.bfloat16), 'dp', scatter_dimension=0,...  359 us
    reduce_scatter x4, waiting for transfers between devices, local(): lax.psum_scatter(out_term.astype(jnp.bfloat16), 'dp', scatter_dimension=1...  191 us
    all_gather x1, waiting for transfers between devices, local(): lax.all_gather(expert_in, 'dp', axis=1, tiled=True)  188 us
    all_gather x1, waiting for transfers between devices, local(): lax.all_gather(expert_out, 'dp', axis=2, tiled=True)  94.4 us
    reduce_scatter x1, waiting for transfers between devices, local(): lax.psum_scatter(proj_term.astype(jnp.bfloat16), 'dp', scatter_dimension=...  71.8 us
    reduce_scatter x1, waiting for transfers between devices, local(): lax.psum_scatter(query_term.astype(jnp.bfloat16), 'dp', scatter_dimension...  70.1 us
    psum x1, waiting for transfers between devices, local(): attn_total = lax.psum(attn_part, 'tensor')  66.7 us
    unnamed x194, local copies, waits for them, and re-layouts  45.1 us
  transfers between devices with their start and end apart: 22, of which 19 were waited for; matrix products, arithmetic and copies ran while one was open for 16% of the time, Pallas kernels for 0%

commit v1 on v0

v1 whole, which is shorter than its diff:
```python
import functools

import jax
import jax.numpy as jnp
from jax import lax
from jax.experimental import pallas as pl
from jax.experimental.pallas import tpu as pltpu
from jax.sharding import PartitionSpec as P

HD = 128
EPSILON = 1e-06
ROPE_BASE = 10000.0
BEST = lax.Precision.HIGHEST
F32 = jnp.float32
BF16 = jnp.bfloat16
VMEM_BYTES = 60 * 1024 * 1024


def nn(a, b):
    return lax.dot_general(a, b, (((1,), (0,)), ((), ())), preferred_element_type=F32)


def nt(a, b, precision=None):
    return lax.dot_general(
        a, b, (((1,), (1,)), ((), ())), preferred_element_type=F32, precision=precision
    )


def tn(a, b):
    return lax.dot_general(a, b, (((0,), (0,)), ((), ())), preferred_element_type=F32)


def lane_sums(values):
    ones = jnp.ones((8, values.shape[1]), F32)
    return nt(ones, values, BEST)


def run(body, name, grid, meta, ins, outs, scratch=(), flops=0):
    in_specs = []
    moved = 0
    for array, block, index in ins:
        if block is None:
            rank = array.ndim
            in_specs.append(pl.BlockSpec(array.shape, lambda *a, rank=rank: (0,) * rank))
        else:
            in_specs.append(pl.BlockSpec(block, index))
        moved += array.size * array.dtype.itemsize
    out_specs = []
    out_shape = []
    for shape, dtype, block, index in outs:
        if block is None:
            rank = len(shape)
            out_specs.append(pl.BlockSpec(shape, lambda *a, rank=rank: (0,) * rank))
        else:
            out_specs.append(pl.BlockSpec(block, index))
        out_shape.append(jax.ShapeDtypeStruct(shape, dtype))
        size = jnp.dtype(dtype).itemsize
        for extent in shape:
            size *= extent
        moved += size
    return pl.pallas_call(
        body,
        name=name,
        grid_spec=pltpu.PrefetchScalarGridSpec(
            num_scalar_prefetch=1,
            grid=grid,
            in_specs=in_specs,
            out_specs=out_specs,
            scratch_shapes=list(scratch),
        ),
        out_shape=out_shape,
        compiler_params=pltpu.CompilerParams(
            dimension_semantics=("arbitrary",) * len(grid), vmem_limit_bytes=VMEM_BYTES
        ),
        cost_estimate=pl.CostEstimate(flops=flops, bytes_accessed=moved, transcendentals=0),
    )(meta, *[array for array, _, _ in ins])


def pick(low_id, high_id, expert, low_value, high_value):
    zero = jnp.zeros_like(low_value)
    return jnp.where(
        low_id == expert, low_value, jnp.where(high_id == expert, high_value, zero)
    )


def two_slots(low_id, high_id, products):
    low_value = products[0]
    for expert in range(1, len(products) - 1):
        low_value = jnp.where(low_id == expert, products[expert], low_value)
    high_value = products[1]
    for expert in range(2, len(products)):
        high_value = jnp.where(high_id == expert, products[expert], high_value)
    return low_value, high_value


def turn(values, cosine, sine):
    return values * cosine + pltpu.roll(values, HD // 2, 1) * sine


def local(
    hidden_in,
    cotangent,
    lengths,
    dealing,
    attn_routes,
    ffn_routes,
    attn_gain,
    attn_router,
    kv_weight,
    query_weight,
    proj_weight,
    ffn_gain,
    ffn_router,
    expert_in,
    expert_out,
    *,
    dp,
    tp,
):
    seqs = dealing.shape[0]
    seq_len = cotangent.shape[1]
    held = cotangent.shape[0]
    per = hidden_in.shape[1]
    width = hidden_in.shape[2]
    heads = query_weight.shape[2] // HD
    groups = heads
    parts = dp // groups
    ds = width // dp
    hw = heads * HD
    rows_all = seqs * seq_len
    rows = rows_all * 3 // 4
    rp = rows // parts
    blk = rp // groups
    experts = query_weight.shape[0]
    ff = expert_out.shape[1]
    scale = HD ** (-0.5)
    pieces = range(parts)

    index = lax.axis_index("dp")
    z = lax.axis_index("tensor")
    g = index // parts
    c = index % parts
    meta = jnp.stack([g, c, g, g ^ 1, g ^ 2, g ^ 3]).astype(jnp.int32)

    def by_group(value, mask):
        pairs = [(a, ((a // parts) ^ mask) * parts + a % parts) for a in range(dp)]
        return lax.ppermute(value, "dp", pairs)

    def by_part(value, mask):
        pairs = [(a, (a // parts) * parts + ((a % parts) ^ mask)) for a in range(dp)]
        return lax.ppermute(value, "dp", pairs)

    def to_next(value):
        pairs = [(a, a + 1) for a in range(dp) if a % parts < parts - 1]
        return lax.ppermute(value, "dp", pairs)

    def to_previous(value):
        pairs = [(a, a - 1) for a in range(dp) if a % parts > 0]
        return lax.ppermute(value, "dp", pairs)

    def by_z(value, mask):
        return lax.ppermute(value, "tensor", [(a, a ^ mask) for a in range(tp)])

    def sum_groups(value):
        value = value + by_group(value, 1)
        return value + by_group(value, 2)

    def sum_z(value):
        value = value + by_z(value, 1)
        return value + by_z(value, 3)

    def wide_sum_z(value):
        inner = lax.ppermute(value, "tensor", [(0, 1), (3, 2)])
        value = (value.astype(F32) + inner.astype(F32)).astype(BF16)
        other = lax.ppermute(value, "tensor", [(1, 2), (2, 1)])
        value = (value.astype(F32) + other.astype(F32)).astype(BF16)
        outer = lax.ppermute(value, "tensor", [(1, 0), (2, 3)])
        return jnp.where((z == 1) | (z == 2), value, outer)

    def reduce_groups(first, second):
        ra = by_group(first[3], 1)
        rb = by_group(second[3], 2)
        ax = by_group(first[1], 1)
        by = by_group(second[2], 2)
        ay = by_group((first[2].astype(F32) + ra.astype(F32)).astype(BF16), 2)
        bx = by_group((second[1].astype(F32) + rb.astype(F32)).astype(BF16), 1)
        return (first[0], ax, ay), (second[0], bx, by)

    def gather_groups(first, second):
        ax, bx = by_group(first, 1), by_group(second, 1)
        ay, by = by_group(first, 2), by_group(second, 2)
        ad, bd = by_group(ax, 2), by_group(by, 1)
        return (first, ax, ay, ad), (second, bx, by, bd)

    def row_of(offset):
        return lambda *a: (a[-1][2 + offset], 0)

    ends = jnp.cumsum(lengths)
    starts = ends - lengths
    inverse = jnp.sum(
        (dealing[None, :] == jnp.arange(seqs, dtype=jnp.int32)[:, None])
        * jnp.arange(seqs, dtype=jnp.int32)[None, :],
        axis=1,
    )

    def places(part):
        packed = part * rp + jnp.arange(rp, dtype=jnp.int32)
        begun = starts[None, :] <= packed[:, None]
        first = jnp.max(jnp.where(begun, starts[None, :], 0), axis=1)
        seq = jnp.sum(begun.astype(jnp.int32), axis=1) - 1
        at = packed - first
        slot = jnp.sum(
            jnp.where(seq[:, None] == jnp.arange(seqs, dtype=jnp.int32)[None, :], inverse[None, :], 0),
            axis=1,
        )
        x_row = (at // per) * (seqs * per) + seq * per + at % per
        d_row = slot * seq_len + at
        return seq, at, first, x_row, d_row

    seq, at, first, x_row, d_row = places(c)

    x_send = hidden_in.reshape(seqs * per, dp, ds).transpose(1, 0, 2)
    x_all = lax.all_to_all(x_send, "dp", 0, 0, tiled=True).reshape(rows_all, ds)
    d_send = cotangent.reshape(held * seq_len, dp, ds).transpose(1, 0, 2)
    d_all = lax.all_to_all(d_send, "dp", 0, 0, tiled=True).reshape(rows_all, ds)
    x_pieces = [x_all[x_row]]
    d_pieces = [d_all[d_row]]
    for s in pieces[1:]:
        _, _, _, other_x, other_d = places(c ^ s)
        x_pieces.append(by_part(x_all[other_x], s))
        d_pieces.append(by_part(d_all[other_d], s))

    def spread(vector):
        tall = vector.reshape((groups, parts, ds) + vector.shape[1:])[g]
        return jnp.stack([tall[c ^ s] for s in pieces])

    gain_a = spread(attn_gain)[:, None, :]
    gain_f = spread(ffn_gain)[:, None, :]
    pad = ((0, 0), (0, 8 - experts), (0, 0))
    router_a = jnp.pad(spread(attn_router).transpose(0, 2, 1), pad)
    router_f = jnp.pad(spread(ffn_router).transpose(0, 2, 1), pad)

    in_own = expert_in.swapaxes(1, 2)
    wq = [query_weight] + [by_part(query_weight, s) for s in pieces[1:]]
    wkv = [kv_weight] + [by_part(kv_weight, s) for s in pieces[1:]]
    wp = [proj_weight] + [by_part(proj_weight, s) for s in pieces[1:]]
    wo = [expert_out] + [by_part(expert_out, s) for s in pieces[1:]]
    wi = [in_own] + [by_part(in_own, s) for s in pieces[1:]]

    routes = jnp.concatenate(
        [attn_routes.reshape(rows_all, 2), ffn_routes.reshape(rows_all, 2)], axis=1
    )
    here = (seq * seq_len + at)[:, None] == jnp.arange(rows_all, dtype=jnp.int32)[None, :]
    mine = jnp.dot(here.astype(BF16), routes.astype(BF16), preferred_element_type=F32)
    low_a, high_a = jnp.minimum(mine[:, 0], mine[:, 1]), jnp.maximum(mine[:, 0], mine[:, 1])
    low_f, high_f = jnp.minimum(mine[:, 2], mine[:, 3]), jnp.maximum(mine[:, 2], mine[:, 3])
    window = (first - c * rp + seq_len).astype(F32)
    nil = jnp.zeros_like(window)
    sel = jnp.stack([low_a, high_a, low_f, high_f, window, nil, nil, nil], axis=1)
    half = HD // 2
    frequency = ROPE_BASE ** (-2.0 * jnp.arange(half, dtype=F32) / HD)
    angles = at.astype(F32)[:, None] * frequency[None, :]
    cosine = jnp.concatenate([jnp.cos(angles)] * 2, axis=1)
    sine = jnp.sin(angles)
    sine = jnp.concatenate([-sine, sine], axis=1)

    def gate_columns(stats, low_id, high_id):
        rms = lax.rsqrt(stats[experts] / width + EPSILON)
        ids = jnp.arange(experts, dtype=F32)[:, None]
        logits = stats[:experts]
        low_logit = jnp.sum(jnp.where(low_id[None] == ids, logits, 0.0), axis=0) * rms
        high_logit = jnp.sum(jnp.where(high_id[None] == ids, logits, 0.0), axis=0) * rms
        gap = low_logit - high_logit
        low_gate, high_gate = jax.nn.sigmoid(gap), jax.nn.sigmoid(-gap)
        zero = jnp.zeros_like(rms)
        flat = jnp.stack([rms, low_gate, high_gate, gap, zero, zero, zero, zero])
        return flat, flat.T

    def dhidden_body(m, *refs):
        d_refs, w_refs = refs[:parts], refs[parts : 2 * parts]
        sel_ref, a_ref, b_ref = refs[2 * parts :]
        products = []
        for e in range(experts):
            products.append(sum(nt(d_refs[s][...], w_refs[s][e]) for s in pieces))
        low, high = two_slots(sel_ref[:, 2:3], sel_ref[:, 3:4], products)
        a_ref[...] = low.astype(BF16)
        b_ref[...] = high.astype(BF16)

    def dhidden(r):
        ins = [(d, (blk, ds), row_of(r)) for d in d_pieces]
        ins += [(w, None, None) for w in wo]
        ins += [(sel, (blk, 8), row_of(r))]
        outs = [((blk, ff), BF16, None, None)] * 2
        return run(
            dhidden_body, "dhidden", (1,), meta, ins, outs,
            flops=2 * blk * experts * parts * ds * ff,
        )

    dh = [dhidden(r) for r in range(4)]
    dh_a, dh_b = reduce_groups([v[0] for v in dh], [v[1] for v in dh])

    tile = 256

    def qkv_body(m, *refs):
        x_refs = refs[:parts]
        gain_ref, router_ref = refs[parts : parts + 2]
        q_refs = refs[parts + 2 : 2 * parts + 2]
        kv_refs = refs[2 * parts + 2 : 3 * parts + 2]
        sel_ref = refs[3 * parts + 2]
        outs = refs[3 * parts + 3 : 3 * parts + 11]
        stats_ref, scr = refs[3 * parts + 11 :]
        us = []
        logits = jnp.zeros((8, tile), F32)
        squares = jnp.zeros((8, tile), F32)
        for s in pieces:
            xf = x_refs[s][...].astype(F32)
            us.append((xf * gain_ref[s]).astype(BF16))
            logits += nt(router_ref[s], us[s])
            squares += lane_sums(xf * xf)
        line = lax.broadcasted_iota(jnp.int32, (8, tile), 0)
        stats_ref[...] = jnp.where(line < experts, logits, squares)
        products = []
        for e in range(experts):
            products.append(sum(nn(us[s], q_refs[s][e]) for s in pieces))
        low, high = two_slots(sel_ref[:, 0:1], sel_ref[:, 1:2], products)
        keys = sum(nn(us[s], kv_refs[s][0]) for s in pieces)
        values = sum(nn(us[s], kv_refs[s][1]) for s in pieces)
        for k, value in enumerate((low, high, keys, values)):
            value = value.astype(BF16)
            for h in range(heads):
                scr[h, :, k * HD : (k + 1) * HD] = value[:, h * HD : (h + 1) * HD]
        for r in range(4):
            block = scr[m[2 + r]]
            outs[2 * r][...] = block[:, : 2 * HD]
            outs[2 * r + 1][...] = block[:, 2 * HD :]

    ins = [(x, (tile, ds), lambda i, m: (i, 0)) for x in x_pieces]
    ins += [(gain_a, None, None), (router_a, None, None)]
    ins += [(w, None, None) for w in wq + wkv]
    ins += [(sel, (tile, 8), lambda i, m: (i, 0))]
    outs = [((rp, 2 * HD), BF16, (tile, 2 * HD), lambda i, m: (i, 0))] * 8
    outs += [((8, rp), F32, (8, tile), lambda i, m: (0, i))]
    qkv = run(
        qkv_body, "qkv", (rp // tile,), meta, ins, outs,
        [pltpu.VMEM((heads, tile, 4 * HD), BF16)],
        flops=2 * rp * (experts + 2) * parts * ds * hw,
    )
    q_sum, kv_sum = reduce_groups(qkv[0:8:2], qkv[1:8:2])
    stats_a = sum_groups(qkv[8])
    flat_a, cols_a = gate_columns(stats_a, low_a, high_a)

    def rope_body(m, a0, a1, a2, b0, b1, b2, cols, cos_ref, sin_ref, q_ref, kv_ref):
        rms = cols[:, 0:1]
        cos, sin = cos_ref[...], sin_ref[...]
        q = (a0[...].astype(F32) + a1[...].astype(F32) + a2[...].astype(F32)) * rms
        kv = (b0[...].astype(F32) + b1[...].astype(F32) + b2[...].astype(F32)) * rms
        q_ref[:, :HD] = turn(q[:, :HD], cos, sin).astype(BF16)
        q_ref[:, HD:] = turn(q[:, HD:], cos, sin).astype(BF16)
        kv_ref[:, :HD] = turn(kv[:, :HD], cos, sin).astype(BF16)
        kv_ref[:, HD:] = kv[:, HD:].astype(BF16)

    ins = [(v, (tile, 2 * HD), lambda i, m: (i, 0)) for v in q_sum + kv_sum]
    ins += [(cols_a, (tile, 8), lambda i, m: (i, 0))]
    ins += [(v, (tile, HD), lambda i, m: (i, 0)) for v in (cosine, sine)]
    outs = [((rp, 2 * HD), BF16, (tile, 2 * HD), lambda i, m: (i, 0))] * 2
    q_rot, kv_rot = run(rope_body, "rope", (rp // tile,), meta, ins, outs)
    halo = to_next(kv_rot[rp - seq_len :])

    qt = 128
    span = seq_len + qt

    def window_mask(i, low_key):
        u = i * qt + lax.broadcasted_iota(jnp.int32, (qt, span), 1)
        t = seq_len + i * qt + lax.broadcasted_iota(jnp.int32, (qt, span), 0)
        return (u >= low_key.astype(jnp.int32)) & (u <= t)

    def softmax_of(query, key, allowed):
        score = jnp.where(allowed, nt(query, key) * scale, -1e30)
        top = jnp.max(score, axis=1, keepdims=True)
        raised = jnp.exp(score - top)
        return raised / jnp.sum(raised, axis=1, keepdims=True)

    def attend_body(m, q_ref, kv_ref, halo_ref, sel_ref, cols, ga, gb, ma, mb, ext):
        i = pl.program_id(0)

        @pl.when(i == 0)
        def _():
            ext[:seq_len, :] = halo_ref[...]
            ext[seq_len:, :] = kv_ref[...]

        near = ext[pl.ds(pl.multiple_of(i * qt, qt), span), :]
        allowed = window_mask(i, sel_ref[:, 4:5])
        for k, (g_ref, m_ref) in enumerate(((ga, ma), (gb, mb))):
            probs = softmax_of(q_ref[:, k * HD : (k + 1) * HD], near[:, :HD], allowed)
            mixed = nn(probs.astype(BF16), near[:, HD:]).astype(BF16)
            m_ref[...] = mixed
            g_ref[...] = (mixed.astype(F32) * cols[:, 1 + k : 2 + k]).astype(BF16)

    def qrow(i, m):
        return (i, 0)

    ins = [(q_rot, (qt, 2 * HD), qrow), (kv_rot, None, None), (halo, None, None)]
    ins += [(sel, (qt, 8), qrow), (cols_a, (qt, 8), qrow)]
    outs = [((rp, HD), BF16, (qt, HD), qrow)] * 4
    gated_a, gated_b, mixed_a, mixed_b = run(
        attend_body, "attend", (rp // qt,), meta, ins, outs,
        [pltpu.VMEM((seq_len + rp, 2 * HD), BF16)],
        flops=8 * rp * span * HD,
    )
    gm_a, gm_b = gather_groups(gated_a, gated_b)

    chunks = 4
    zr = rp // chunks

    def proj_body(m, *refs):
        a_refs, b_refs = refs[:4], refs[4:8]
        sel_ref = refs[8]
        w_refs = refs[9 : 9 + parts]
        out_ref, lo, hi = refs[9 + parts :]
        for r in range(4):
            lanes = pl.ds(pl.multiple_of(m[2 + r] * HD, HD), HD)
            lo[:, lanes] = a_refs[r][...]
            hi[:, lanes] = b_refs[r][...]
        acc = [None] * parts
        for e in range(experts):
            x = pick(sel_ref[:, 0:1], sel_ref[:, 1:2], e, lo[...], hi[...])
            for s in pieces:
                term = nn(x, w_refs[s][e])
                acc[s] = term if e == 0 else acc[s] + term
        for s in pieces:
            out_ref[s] = acc[s].astype(BF16)

    def project(k):
        at_chunk = lambda i, m: (k, 0)
        ins = [(v, (zr, HD), at_chunk) for v in gm_a + gm_b]
        ins += [(sel, (zr, 8), at_chunk)]
        ins += [(w, None, None) for w in wp]
        return run(
            proj_body, "proj", (1,), meta, ins, [((parts, zr, ds), BF16, None, None)],
            [pltpu.VMEM((zr, hw), BF16)] * 2,
            flops=2 * zr * experts * hw * parts * ds,
        )[0]

    attn_totals = [wide_sum_z(project(k)) for k in range(chunks)]

    def norm_body(m, *refs):
        t_refs = refs[:chunks]
        x_refs = refs[chunks : chunks + parts]
        gain_ref, router_ref, after_ref, u_ref, stats_ref = refs[chunks + parts :]
        for k in range(chunks):
            span_k = slice(k * zr, (k + 1) * zr)
            for s in pieces:
                after_ref[s, span_k] = x_refs[s][span_k, :].astype(F32) + t_refs[k][s].astype(F32)
        logits = jnp.zeros((8, rp), F32)
        squares = jnp.zeros((8, rp), F32)
        for s in pieces:
            af = after_ref[s]
            u = (af * gain_ref[s]).astype(BF16)
            u_ref[s] = u
            logits += nt(router_ref[s], u)
            squares += lane_sums(af * af)
        line = lax.broadcasted_iota(jnp.int32, (8, rp), 0)
        stats_ref[...] = jnp.where(line < experts, logits, squares)

    ins = [(t, None, None) for t in attn_totals + x_pieces]
    ins += [(gain_f, None, None), (router_f, None, None)]
    outs = [
        ((parts, rp, ds), F32, None, None),
        ((parts, rp, ds), BF16, None, None),
        ((8, rp), F32, None, None),
    ]
    after, u_f, stats_part = run(norm_body, "norm", (1,), meta, ins, outs)
    stats_f = sum_groups(stats_part)
    flat_f, cols_f = gate_columns(stats_f, low_f, high_f)

    def up_body(m, *refs):
        u_ref = refs[0]
        w_refs = refs[1 : 1 + parts]
        sel_ref, a_ref, b_ref = refs[1 + parts :]
        products = []
        for e in range(experts):
            products.append(sum(nn(u_ref[s], w_refs[s][e, 0]) for s in pieces))
        low, high = two_slots(sel_ref[:, 2:3], sel_ref[:, 3:4], products)
        a_ref[0] = low.astype(BF16)
        b_ref[0] = high.astype(BF16)

    def up(r):
        ins = [(u_f, (parts, blk, ds), lambda j, m: (0, m[2 + r], 0))]
        ins += [(w, (experts, 1, ds, ff), lambda j, m: (0, j, 0, 0)) for w in wi]
        ins += [(sel, (blk, 8), row_of(r))]
        outs = [((2, blk, ff), BF16, (1, blk, ff), lambda j, m: (j, 0, 0))] * 2
        return run(
            up_body, "up", (2,), meta, ins, outs, flops=4 * blk * experts * parts * ds * ff
        )

    ups = [None] * 4
    for r in (3, 1, 2, 0):
        ups[r] = up(r)
    gu_a, gu_b = reduce_groups([v[0] for v in ups], [v[1] for v in ups])

    ft = HD

    def mid_body(m, *refs):
        gu = (refs[0:3], refs[3:6])
        dhr = (refs[6:9], refs[9:12])
        cols = refs[12]
        outs, dots = refs[13:15], refs[15]
        j = pl.program_id(0)

        @pl.when(j == 0)
        def _():
            dots[...] = jnp.zeros_like(dots)

        rms = cols[:, 0:1]
        line = lax.broadcasted_iota(jnp.int32, (8, blk), 0)
        inner = jnp.zeros((blk, ft), F32)
        found = []
        for k in range(2):
            gate = cols[:, 1 + k : 2 + k]
            gp = sum(v[0].astype(F32) for v in gu[k]) * rms
            up_pre = sum(v[1].astype(F32) for v in gu[k]) * rms
            raw = sum(v[...].astype(F32) for v in dhr[k])
            sg = jax.nn.sigmoid(gp)
            act = (gp * sg * up_pre).astype(BF16).astype(F32)
            grad = raw * gate
            dgp = (grad * up_pre * sg * (1.0 + gp * (1.0 - sg))).astype(BF16)
            dup = (grad * gp * sg).astype(BF16)
            outs[k][0] = (act * gate).astype(BF16)
            outs[k][1] = dgp
            outs[k][2] = dup
            found.append(act * raw)
            inner += dgp.astype(F32) * gp + dup.astype(F32) * up_pre
        sums = jnp.where(
            line == 0, lane_sums(found[0]), jnp.where(line == 1, lane_sums(found[1]), lane_sums(inner))
        )
        dots[...] += sums

    ins = [(v, (2, blk, ft), lambda j, m: (0, 0, j)) for v in gu_a + gu_b]
    ins += [(v, (blk, ft), lambda j, m: (0, j)) for v in dh_a + dh_b]
    ins += [(cols_f, (blk, 8), row_of(0))]
    outs = [((3, blk, ff), BF16, (3, blk, ft), lambda j, m: (0, 0, j))] * 2
    outs += [((8, blk), F32, None, None)]
    act_a, act_b, dots_f = run(mid_body, "mid", (ff // ft,), meta, ins, outs)
    ag_a, ag_b = gather_groups(act_a, act_b)

    dots_f = sum_z(dots_f)
    dots_f = jnp.stack([dots_f, by_group(dots_f, 1), by_group(dots_f, 2), by_group(dots_f, 3)])
    dots_f = jnp.take(dots_f, g ^ jnp.arange(4, dtype=jnp.int32), axis=0)
    dots_f = dots_f.transpose(1, 0, 2).reshape(8, rp)

    def back_columns(flat, dots, low_id, high_id):
        delta = flat[1] * flat[2] * (dots[0] - dots[1])
        inner = (dots[2] + delta * flat[3]) / width
        ids = jnp.arange(experts, dtype=F32)[:, None]
        dlogit = jnp.where(low_id[None] == ids, delta[None], 0.0) - jnp.where(
            high_id[None] == ids, delta[None], 0.0
        )
        zero = jnp.zeros((1, rp), F32)
        return jnp.concatenate(
            [dlogit, inner[None], flat[0:1]] + [zero] * (6 - experts), axis=0
        ).T

    back_f = back_columns(flat_f, dots_f, low_f, high_f)

    def dx_body(m, *refs):
        a_ref, b_ref = refs[:2]
        w_refs = refs[2 : 2 + parts]
        sel_ref, out_ref, acc = refs[2 + parts :]
        e = pl.program_id(0)
        expert = e.astype(F32)
        gate = pick(sel_ref[:, 2:3], sel_ref[:, 3:4], expert, a_ref[1], b_ref[1])
        upper = pick(sel_ref[:, 2:3], sel_ref[:, 3:4], expert, a_ref[2], b_ref[2])

        @pl.when(e == 0)
        def _():
            acc[...] = jnp.zeros_like(acc)

        for s in pieces:
            acc[s] += nt(gate, w_refs[s][0, 0]) + nt(upper, w_refs[s][0, 1])

        @pl.when(e == experts - 1)
        def _():
            out_ref[...] = acc[...].astype(BF16)

    def dx(r):
        ins = [(ag_a[r], None, None), (ag_b[r], None, None)]
        ins += [(w, (1, 2, ds, ff), lambda e, m: (e, 0, 0, 0)) for w in wi]
        ins += [(sel, (blk, 8), row_of(r))]
        return run(
            dx_body, "dx", (experts,), meta, ins, [((parts, blk, ds), BF16, None, None)],
            [pltpu.VMEM((parts, blk, ds), F32)], flops=4 * blk * experts * parts * ds * ff,
        )[0]

    dx_totals = [wide_sum_z(dx(r)) for r in range(4)]

    def down_body(m, *refs):
        a_ref, b_ref = refs[:2]
        w_refs = refs[2 : 2 + parts]
        sel_ref, out_ref, acc = refs[2 + parts :]
        e = pl.program_id(0)
        x = pick(sel_ref[:, 2:3], sel_ref[:, 3:4], e.astype(F32), a_ref[0], b_ref[0])

        @pl.when(e == 0)
        def _():
            acc[...] = jnp.zeros_like(acc)

        for s in pieces:
            acc[s] += nn(x, w_refs[s][0])

        @pl.when(e == experts - 1)
        def _():
            out_ref[...] = acc[...].astype(BF16)

    def down(r):
        whole = lambda e, m: (0, 0, 0)
        ins = [(ag_a[r], (1, blk, ff), whole), (ag_b[r], (1, blk, ff), whole)]
        ins += [(w, (1, ff, ds), lambda e, m: (e, 0, 0)) for w in wo]
        ins += [(sel, (blk, 8), row_of(r))]
        return run(
            down_body, "down", (experts,), meta, ins, [((parts, blk, ds), BF16, None, None)],
            [pltpu.VMEM((parts, blk, ds), F32)], flops=2 * blk * experts * parts * ds * ff,
        )[0]

    def norm_back_body(low_precision_out, m, *refs):
        t_refs = refs[:4]
        after_ref = refs[4]
        up_refs = refs[5 : 5 + parts]
        gain_ref, router_ref, back = refs[5 + parts : 8 + parts]
        outs = refs[8 + parts :]
        small = outs[-1]
        for s in pieces:
            gain = gain_ref[s]
            router = router_ref[s].astype(F32)
            gain_sum = jnp.zeros((1, ds), F32)
            router_sum = [jnp.zeros((1, ds), F32)] * experts
            for r in range(4):
                if low_precision_out:
                    span_r = pl.ds(pl.multiple_of(m[2 + r] * blk, blk), blk)
                else:
                    span_r = slice(r * blk, (r + 1) * blk)
                up_value = up_refs[s][span_r, :] if low_precision_out else up_refs[0][s, span_r, :]
                x = after_ref[s, span_r, :].astype(F32)
                cols = back[span_r, :]
                rms = cols[:, experts + 1 : experts + 2]
                grad = t_refs[r][s].astype(F32)
                for e in range(experts):
                    grad += cols[:, e : e + 1] * router[e : e + 1]
                normed = x * rms
                token = (normed * gain).astype(BF16).astype(F32)
                gain_sum += jnp.sum(grad * normed, axis=0, keepdims=True)
                for e in range(experts):
                    router_sum[e] = router_sum[e] + jnp.sum(
                        token * cols[:, e : e + 1], axis=0, keepdims=True
                    )
                dn = grad * gain
                total = up_value.astype(F32) + rms * (
                    dn - normed * cols[:, experts : experts + 1]
                )
                if low_precision_out:
                    outs[0][s, span_r, :] = total
                    outs[1][s, span_r, :] = total.astype(BF16)
                else:
                    outs[0][s, span_r, :] = total.astype(BF16)
            for e in range(experts):
                small[e, s] = router_sum[e][0]
            small[experts, s] = gain_sum[0]

    ins = [(t, None, None) for t in dx_totals]
    ins += [(after, None, None)] + [(d, None, None) for d in d_pieces]
    ins += [(gain_f, None, None), (router_f, None, None), (back_f, None, None)]
    outs = [
        ((parts, rp, ds), F32, None, None),
        ((parts, rp, ds), BF16, None, None),
        ((experts + 1, parts, ds), F32, None, None),
    ]
    dafter, dafter_low, small_f = run(
        functools.partial(norm_back_body, True), "norm_back", (1,), meta, ins, outs
    )

    def whole_vectors(small):
        full = jnp.zeros((experts + 1, dp, ds), F32)
        for s in pieces:
            full = lax.dynamic_update_slice_in_dim(
                full, small[:, s : s + 1], g * parts + (c ^ s), axis=1
            )
        mask = 1
        while mask < dp:
            full = full + lax.ppermute(full, "dp", [(a, a ^ mask) for a in range(dp)])
            mask *= 2
        full = full.reshape(experts + 1, width)
        return full[:experts].T, full[experts]

    ffnrouter_grad, ffngain_grad = whole_vectors(small_f)

    def dmix_body(m, *refs):
        d_ref = refs[0]
        w_refs = refs[1 : 1 + parts]
        sel_ref = refs[1 + parts]
        outs = refs[2 + parts : 10 + parts]
        scr = refs[10 + parts]
        products = []
        for e in range(experts):
            products.append(sum(nt(d_ref[s], w_refs[s][e]) for s in pieces))
        low, high = two_slots(sel_ref[:, 0:1], sel_ref[:, 1:2], products)
        for k, value in enumerate((low, high)):
            value = value.astype(BF16)
            for h in range(heads):
                scr[h, :, k * HD : (k + 1) * HD] = value[:, h * HD : (h + 1) * HD]
        for r in range(4):
            block = scr[m[2 + r]]
            outs[2 * r][...] = block[:, :HD]
            outs[2 * r + 1][...] = block[:, HD:]

    ins = [(dafter_low, (parts, tile, ds), lambda i, m: (0, i, 0))]
    ins += [(w, None, None) for w in wp]
    ins += [(sel, (tile, 8), lambda i, m: (i, 0))]
    outs = [((rp, HD), BF16, (tile, HD), lambda i, m: (i, 0))] * 8
    dm = run(
        dmix_body, "dmix", (rp // tile,), meta, ins, outs,
        [pltpu.VMEM((heads, tile, 2 * HD), BF16)],
        flops=2 * rp * experts * parts * ds * hw,
    )
    dm_a, dm_b = reduce_groups(dm[0:8:2], dm[1:8:2])

    def attend_back_body(m, *refs):
        q_ref, kv_ref, halo_ref, sel_ref, cols, cos_ref, sin_ref = refs[:7]
        d_refs = (refs[7:10], refs[10:13])
        mix_refs = refs[13:15]
        dq_ref, own_ref, far_ref, dots_ref, ext, acc = refs[15:]
        i = pl.program_id(0)

        @pl.when(i == 0)
        def _():
            ext[:seq_len, :] = halo_ref[...]
            ext[seq_len:, :] = kv_ref[...]
            acc[...] = jnp.zeros_like(acc)

        near_rows = pl.ds(pl.multiple_of(i * qt, qt), span)
        near = ext[near_rows, :]
        allowed = window_mask(i, sel_ref[:, 4:5])
        line = lax.broadcasted_iota(jnp.int32, (8, qt), 0)
        inner = jnp.zeros((qt, HD), F32)
        found = []
        dk = jnp.zeros((span, HD), F32)
        dv = jnp.zeros((span, HD), F32)
        for k in range(2):
            query = q_ref[:, k * HD : (k + 1) * HD]
            probs = softmax_of(query, near[:, :HD], allowed)
            raw = sum(v[...].astype(F32) for v in d_refs[k])
            dmixed = (raw * cols[:, 1 + k : 2 + k]).astype(BF16)
            found.append(raw * mix_refs[k][...].astype(F32))
            dv += tn(probs.astype(BF16), dmixed)
            dprob = nt(dmixed, near[:, HD:])
            rest = jnp.sum(probs * dprob, axis=1, keepdims=True)
            dscore = (probs * (dprob - rest)).astype(BF16)
            dk += tn(dscore, query) * scale
            dquery = nn(dscore, near[:, :HD]) * scale
            inner += dquery * query.astype(F32)
            dq_ref[:, k * HD : (k + 1) * HD] = turn(dquery, cos_ref[...], -sin_ref[...]).astype(BF16)
        acc[near_rows, :HD] += dk
        acc[near_rows, HD:] += dv
        dots_ref[...] = jnp.where(
            line == 0, lane_sums(found[0]), jnp.where(line == 1, lane_sums(found[1]), lane_sums(inner))
        )

        @pl.when(i == rp // qt - 1)
        def _():
            far_ref[...] = acc[:seq_len, :]
            own_ref[...] = acc[seq_len:, :]

    ins = [(q_rot, (qt, 2 * HD), qrow), (kv_rot, None, None), (halo, None, None)]
    ins += [(sel, (qt, 8), qrow), (cols_a, (qt, 8), qrow)]
    ins += [(cosine, (qt, HD), qrow), (sine, (qt, HD), qrow)]
    ins += [(v, (qt, HD), qrow) for v in dm_a + dm_b + (mixed_a, mixed_b)]
    outs = [
        ((rp, 2 * HD), BF16, (qt, 2 * HD), qrow),
        ((rp, 2 * HD), F32, None, None),
        ((seq_len, 2 * HD), F32, None, None),
        ((8, rp), F32, (8, qt), lambda i, m: (0, i)),
    ]
    dq, dkv_own, dkv_far, dots_q = run(
        attend_back_body, "attend_back", (rp // qt,), meta, ins, outs,
        [pltpu.VMEM((seq_len + rp, 2 * HD), BF16), pltpu.VMEM((seq_len + rp, 2 * HD), F32)],
        flops=20 * rp * span * HD,
    )
    dkv_in = to_previous(dkv_far)

    def dkv_body(m, own_ref, in_ref, kv_ref, cos_ref, sin_ref, out_ref, dots_ref):
        head = rp - seq_len
        for rows_here in (slice(0, head), slice(head, rp)):
            value = own_ref[rows_here, :]
            if rows_here.start == head:
                value = value + in_ref[...]
            out_ref[rows_here, :HD] = turn(
                value[:, :HD], cos_ref[rows_here, :], -sin_ref[rows_here, :]
            ).astype(BF16)
            out_ref[rows_here, HD:] = value[:, HD:].astype(BF16)
            dots_ref[:, rows_here] = lane_sums(value * kv_ref[rows_here, :].astype(F32))

    ins = [(v, None, None) for v in (dkv_own, dkv_in, kv_rot, cosine, sine)]
    outs = [((rp, 2 * HD), BF16, None, None), ((8, rp), F32, None, None)]
    dkv, dots_kv = run(dkv_body, "dkv", (1,), meta, ins, outs)
    third = jnp.arange(8)[:, None] == 2
    dots_a = sum_z(sum_groups(dots_q + jnp.where(third, dots_kv, 0.0)))
    back_a = back_columns(flat_a, dots_a, low_a, high_a)
    da_a, da_b = gather_groups(dq, dkv)

    def place_heads(m, refs, lo, hi):
        for r in range(4):
            lanes = pl.ds(pl.multiple_of(m[2 + r] * HD, HD), HD)
            lo[:, lanes] = refs[r][:, :HD]
            hi[:, lanes] = refs[r][:, HD:]

    def dattn_body(m, *refs):
        a_refs, b_refs = refs[:4], refs[4:8]
        sel_ref = refs[8]
        q_refs = refs[9 : 9 + parts]
        kv_refs = refs[9 + parts : 9 + 2 * parts]
        out_ref, lo, hi, dk, dv = refs[9 + 2 * parts :]
        place_heads(m, a_refs, lo, hi)
        place_heads(m, b_refs, dk, dv)
        acc = [nt(dk[...], kv_refs[s][0]) + nt(dv[...], kv_refs[s][1]) for s in pieces]
        for e in range(experts):
            x = pick(sel_ref[:, 0:1], sel_ref[:, 1:2], e, lo[...], hi[...])
            for s in pieces:
                acc[s] += nt(x, q_refs[s][e])
        for s in pieces:
            out_ref[s] = acc[s].astype(BF16)

    def dattn(k):
        at_chunk = lambda i, m: (k, 0)
        ins = [(v, (zr, 2 * HD), at_chunk) for v in da_a + da_b]
        ins += [(sel, (zr, 8), at_chunk)]
        ins += [(w, None, None) for w in wq + wkv]
        return run(
            dattn_body, "dattn", (1,), meta, ins, [((parts, zr, ds), BF16, None, None)],
            [pltpu.VMEM((zr, hw), BF16)] * 4,
            flops=2 * zr * (experts + 2) * hw * parts * ds,
        )[0]

    da_totals = [wide_sum_z(dattn(k)) for k in range(chunks)]
    x_stack = jnp.stack(x_pieces)
    ins = [(t, None, None) for t in da_totals]
    ins += [(x_stack, None, None)] + [(dafter, None, None)] * parts
    ins += [(gain_a, None, None), (router_a, None, None), (back_a, None, None)]
    outs = [((parts, rp, ds), BF16, None, None), ((experts + 1, parts, ds), F32, None, None)]
    dinput, small_a = run(
        functools.partial(norm_back_body, False), "norm_back_first", (1,), meta, ins, outs
    )
    attnrouter_grad, attngain_grad = whole_vectors(small_a)

    def exchange(grad_of):
        received = [by_part(grad_of(s, None), s) for s in pieces[1:]]
        return grad_of(0, received)

    ffn_input = (after * flat_f[0][None, :, None] * gain_f).astype(BF16)
    attn_input = (x_stack.astype(F32) * flat_a[0][None, :, None] * gain_a).astype(BF16)

    def dwin_body(count, m, *refs):
        a_refs, b_refs = refs[:4], refs[4:8]
        sel_ref, x_ref = refs[8:10]
        add_refs = refs[10 : 10 + count]
        out_ref, xs, ids, mt = refs[10 + count :]
        j, e = pl.program_id(0), pl.program_id(1)

        @pl.when((j == 0) & (e == 0))
        def _():
            for r in range(4):
                src = pl.ds(pl.multiple_of(m[2 + r] * blk, blk), blk)
                xs[r * blk : (r + 1) * blk, :] = x_ref[0, src, :]
                ids[r * blk : (r + 1) * blk, :] = sel_ref[src, :]

        expert = e.astype(F32)
        for r in range(4):
            here_r = slice(r * blk, (r + 1) * blk)
            mt[here_r, :] = pick(
                ids[here_r, 2:3], ids[here_r, 3:4], expert, a_refs[r][0], b_refs[r][0]
            )
        acc = tn(xs[...], mt[...])
        for ref in add_refs:
            acc = acc + ref[0, 0].astype(F32)
        out_ref[0, 0] = acc.astype(out_ref.dtype)

    def dwin(s, received):
        adds = received or []
        spot = lambda j, e, m: (e, j, 0, 0)
        ins = [(v, (1, blk, ff), lambda j, e, m: (1 + j, 0, 0)) for v in ag_a + ag_b]
        ins += [(sel, None, None), (ffn_input, (1, rp, ds), lambda j, e, m: (s, 0, 0))]
        ins += [(v, (1, 1, ds, ff), spot) for v in adds]
        dtype = BF16 if received is None else F32
        outs = [((experts, 2, ds, ff), dtype, (1, 1, ds, ff), spot)]
        return run(
            functools.partial(dwin_body, len(adds)), "dwin", (2, experts), meta, ins, outs,
            [pltpu.VMEM((rp, ds), BF16), pltpu.VMEM((rp, 8), F32), pltpu.VMEM((rp, ff), BF16)],
            flops=4 * rp * experts * ds * ff,
        )[0]

    def dwout_body(count, m, *refs):
        a_refs, b_refs = refs[:4], refs[4:8]
        sel_ref, d_ref = refs[8:10]
        add_refs = refs[10 : 10 + count]
        out_ref, xs, ids, mt = refs[10 + count :]
        e = pl.program_id(0)

        @pl.when(e == 0)
        def _():
            for r in range(4):
                src = pl.ds(pl.multiple_of(m[2 + r] * blk, blk), blk)
                xs[r * blk : (r + 1) * blk, :] = d_ref[src, :]
                ids[r * blk : (r + 1) * blk, :] = sel_ref[src, :]

        expert = e.astype(F32)
        for r in range(4):
            here_r = slice(r * blk, (r + 1) * blk)
            mt[here_r, :] = pick(
                ids[here_r, 2:3], ids[here_r, 3:4], expert, a_refs[r][0], b_refs[r][0]
            )
        acc = tn(mt[...], xs[...])
        for ref in add_refs:
            acc = acc + ref[0].astype(F32)
        out_ref[0] = acc.astype(out_ref.dtype)

    def dwout(s, received):
        adds = received or []
        spot = lambda e, m: (e, 0, 0)
        ins = [(v, (1, blk, ff), lambda e, m: (0, 0, 0)) for v in ag_a + ag_b]
        ins += [(sel, None, None), (d_pieces[s], None, None)]
        ins += [(v, (1, ff, ds), spot) for v in adds]
        dtype = BF16 if received is None else F32
        outs = [((experts, ff, ds), dtype, (1, ff, ds), spot)]
        return run(
            functools.partial(dwout_body, len(adds)), "dwout", (experts,), meta, ins, outs,
            [pltpu.VMEM((rp, ds), BF16), pltpu.VMEM((rp, 8), F32), pltpu.VMEM((rp, ff), BF16)],
            flops=2 * rp * experts * ds * ff,
        )[0]

    def dwproj_body(count, m, *refs):
        a_refs, b_refs = refs[:4], refs[4:8]
        sel_ref, d_ref = refs[8:10]
        add_refs = refs[10 : 10 + count]
        out_ref, lo, hi = refs[10 + count :]
        e = pl.program_id(0)

        @pl.when(e == 0)
        def _():
            for r in range(4):
                lanes = pl.ds(pl.multiple_of(m[2 + r] * HD, HD), HD)
                lo[:, lanes] = a_refs[r][...]
                hi[:, lanes] = b_refs[r][...]

        x = pick(sel_ref[:, 0:1], sel_ref[:, 1:2], e.astype(F32), lo[...], hi[...])
        acc = tn(x, d_ref[0])
        for ref in add_refs:
            acc = acc + ref[0].astype(F32)
        out_ref[0] = acc.astype(out_ref.dtype)

    def dwproj(s, received):
        adds = received or []
        spot = lambda e, m: (e, 0, 0)
        ins = [(v, None, None) for v in gm_a + gm_b]
        ins += [(sel, None, None), (dafter_low, (1, rp, ds), lambda e, m: (s, 0, 0))]
        ins += [(v, (1, hw, ds), spot) for v in adds]
        dtype = BF16 if received is None else F32
        return run(
            functools.partial(dwproj_body, len(adds)), "dwproj", (experts,), meta, ins,
            [((experts, hw, ds), dtype, (1, hw, ds), spot)],
            [pltpu.VMEM((rp, hw), BF16)] * 2,
            flops=2 * rp * experts * hw * ds,
        )[0]

    def dwqkv_body(count, m, *refs):
        a_refs, b_refs = refs[:4], refs[4:8]
        sel_ref, x_ref = refs[8:10]
        add_q, add_kv = refs[10 : 10 + count], refs[10 + count : 10 + 2 * count]
        q_ref, kv_ref, lo, hi, dk, dv = refs[10 + 2 * count :]
        e = pl.program_id(0)

        @pl.when(e == 0)
        def _():
            place_heads(m, a_refs, lo, hi)
            place_heads(m, b_refs, dk, dv)

        @pl.when(e < experts)
        def _():
            x = pick(sel_ref[:, 0:1], sel_ref[:, 1:2], e.astype(F32), lo[...], hi[...])
            acc = tn(x_ref[0], x)
            for ref in add_q:
                acc = acc + ref[0].astype(F32)
            q_ref[0] = acc.astype(q_ref.dtype)

        for k, grad in enumerate((dk, dv)):

            @pl.when(e == experts + k)
            def _():
                acc = tn(x_ref[0], grad[...])
                for ref in add_kv:
                    acc = acc + ref[0].astype(F32)
                kv_ref[0] = acc.astype(kv_ref.dtype)

    def dwqkv(s, received):
        adds_q = [v[0] for v in received or []]
        adds_kv = [v[1] for v in received or []]
        q_spot = lambda e, m: (jnp.minimum(e, experts - 1), 0, 0)
        kv_spot = lambda e, m: (jnp.maximum(e - experts, 0), 0, 0)
        ins = [(v, None, None) for v in da_a + da_b]
        ins += [(sel, None, None), (attn_input, (1, rp, ds), lambda e, m: (s, 0, 0))]
        ins += [(v, (1, ds, hw), q_spot) for v in adds_q]
        ins += [(v, (1, ds, hw), kv_spot) for v in adds_kv]
        dtype = BF16 if received is None else F32
        outs = [
            ((experts, ds, hw), dtype, (1, ds, hw), q_spot),
            ((2, ds, hw), dtype, (1, ds, hw), kv_spot),
        ]
        return run(
            functools.partial(dwqkv_body, len(adds_q)), "dwqkv", (experts + 2,), meta, ins, outs,
            [pltpu.VMEM((rp, hw), BF16)] * 4,
            flops=2 * rp * (experts + 2) * hw * ds,
        )

    expertout_grad = exchange(dwout)
    expertin_grad = exchange(dwin).swapaxes(1, 2)
    proj_grad = exchange(dwproj)
    sent = [tuple(by_part(v, s) for v in dwqkv(s, None)) for s in pieces[1:]]
    query_grad, kv_grad = dwqkv(0, sent)

    down_totals = [wide_sum_z(down(r)) for r in range(4)]

    def finish_body(m, *refs):
        t_refs, after_ref, out_ref = refs[:4], refs[4], refs[5]
        for r in range(4):
            span_r = pl.ds(pl.multiple_of(m[2 + r] * blk, blk), blk)
            for s in pieces:
                out_ref[s, span_r, :] = (
                    after_ref[s, span_r, :] + t_refs[r][s].astype(F32)
                ).astype(BF16)

    ins = [(t, None, None) for t in down_totals] + [(after, None, None)]
    out_rows = run(
        finish_body, "finish", (1,), meta, ins, [((parts, rp, ds), BF16, None, None)]
    )[0]

    place = jnp.arange(seq_len, dtype=jnp.int32).reshape(dp, 1, per)
    seq_ids = jnp.arange(seqs, dtype=jnp.int32).reshape(1, seqs, 1)
    valid = place < lengths.reshape(1, seqs, 1)
    packed = jnp.where(valid, starts.reshape(1, seqs, 1) + place, 0)
    from_row = (((packed // rp) ^ c) * rp + packed % rp).reshape(-1)
    cot_row = (inverse.reshape(1, seqs, 1) * seq_len + place).reshape(-1)
    valid = valid.reshape(-1)[:, None]

    def unpack(value, otherwise):
        mine_all = [value[0]] + [by_part(value[s], s) for s in pieces[1:]]
        spread_rows = jnp.concatenate(mine_all, axis=0)[from_row]
        spread_rows = jnp.where(valid, spread_rows, otherwise)
        landed = lax.all_to_all(
            spread_rows.reshape(dp, seqs * per, ds), "dp", 0, 0, tiled=True
        )
        return landed.transpose(1, 0, 2).reshape(seqs, per, width)

    layer_out = unpack(out_rows, x_all)
    input_grad = unpack(dinput, d_all[cot_row])
    return (
        layer_out,
        input_grad,
        attngain_grad,
        attnrouter_grad,
        kv_grad,
        query_grad,
        proj_grad,
        ffngain_grad,
        ffnrouter_grad,
        expertin_grad,
        expertout_grad,
    )


def solution(mesh):
    placed = (
        P(None, "dp", None),
        P("dp", None, None),
        P(),
        P(),
        P(),
        P(),
        P(),
        P(),
        P(None, "dp", "tensor"),
        P(None, "dp", "tensor"),
        P(None, "tensor", "dp"),
        P(),
        P(),
        P(None, "dp", None, "tensor"),
        P(None, "tensor", "dp"),
    )
    return jax.shard_map(
        functools.partial(local, dp=mesh.shape["dp"], tp=mesh.shape["tensor"]),
        mesh=mesh,
        in_specs=placed,
        out_specs=(
            P(None, "dp", None),
            P(None, "dp", None),
            P(),
            P(),
            P(None, "dp", "tensor"),
            P(None, "dp", "tensor"),
            P(None, "tensor", "dp"),
            P(),
            P(),
            P(None, "dp", None, "tensor"),
            P(None, "tensor", "dp"),
        ),
        check_vma=False,
    )
```

time: 1810 us -> 898 us (0.50)
  waiting for transfers between devices: 1180 us -> 236 us
  Pallas kernels: 0 us -> 316 us
  matrix products: 216 us -> 1.3 us
  starting transfers between devices: 15.8 us -> 170 us
  local copies, waits for them, and re-layouts: 207 us -> 107 us
  other arithmetic: 116 us -> 52 us
  blocking collectives: 54.1 us -> 0 us
    reduce_scatter x11 -> x0, waiting for transfers between devices: 692 us -> none  [the longest x4 359 us: local(): lax.psum_scatter(in_term.astype(jnp.bfloat16), 'dp', scatter_dimension=0,...]
    all_gather x5 -> x0, waiting for transfers between devices: 370 us -> none  [the longest x1 188 us: local(): lax.all_gather(expert_in, 'dp', axis=1, tiled=True)]
    pallas_call x0 -> x43, Pallas kernels: none -> 316 us  [run(): pl.pallas_call(body, name=name, grid_spec=pltpu.PrefetchScalarGridSpec(nu...]
    ppermute x0 -> x125, waiting for transfers between devices: none -> 236 us  [the longest x51 115 us: by_group(): return lax.ppermute(value, 'dp', pairs)]
    dot_general x38 -> x1, matrix products: 216 us -> 1.3 us  [local(): jnp.dot(here.astype(BF16), routes.astype(BF16), preferred_element_type=F32)]
    ppermute x0 -> x125, starting transfers between devices: none -> 153 us  [the longest x51 56.8 us: by_group(): return lax.ppermute(value, 'dp', pairs)]
    psum x3 -> x0, waiting for transfers between devices: 105 us -> none  [the longest x1 66.7 us: local(): attn_total = lax.psum(attn_part, 'tensor')]
    psum x3 -> x0, blocking collectives: 54.1 us -> none  [the longest x1 31.9 us: local(): lax.psum(attngain_part.astype(jnp.bfloat16), 'dp').astype(jnp.float32)]
  transfers between devices with their start and end apart: 22 -> 129, of which waited for: 19 -> 42; matrix products, arithmetic and copies ran while one was open for 16% -> 15% of each run, Pallas kernels for 0% -> 32%
where the time goes in v1:
time: 898 us; the launch traced here: 884 us
  Pallas kernels  316 us (35%)
  waiting for transfers between devices  236 us (26%)
  starting transfers between devices  170 us (19%)
  local copies, waits for them, and re-layouts  107 us (12%)
  other arithmetic  52 us (6%)
    pallas_call x43, Pallas kernels, run(): pl.pallas_call(body, name=name, grid_spec=pltpu.PrefetchScalarGridSpec(nu...  316 us
    ppermute x51, waiting for transfers between devices, by_group(): return lax.ppermute(value, 'dp', pairs)  115 us
    ppermute x16, waiting for transfers between devices, wide_sum_z(): outer = lax.ppermute(value, 'tensor', [(1, 0), (2, 3)])  91.4 us
    ppermute x51, starting transfers between devices, by_group(): return lax.ppermute(value, 'dp', pairs)  56.8 us
    unnamed x190, local copies, waits for them, and re-layouts  42.3 us
    ppermute x16, starting transfers between devices, wide_sum_z(): inner = lax.ppermute(value, 'tensor', [(0, 1), (3, 2)])  33.4 us
    ppermute x16, starting transfers between devices, wide_sum_z(): outer = lax.ppermute(value, 'tensor', [(1, 0), (2, 3)])  20.6 us
    gather x2, local copies, waits for them, and re-layouts, unpack(): spread_rows = jnp.concatenate(mine_all, axis=0)[from_row]  18.1 us
  transfers between devices with their start and end apart: 129, of which 42 were waited for; matrix products, arithmetic and copies ran while one was open for 15% of the time, Pallas kernels for 32%

profile of v1, /device:TPU:0, one launch (start us, length us, event | category | flops | bytes accessed | tf_op | source)
XLA Modules:
  0.0 883.8 jit_solution(13006222757185307678)
XLA Ops:
  3.9 5.0 all-to-all-start
  9.6 5.9 copy.198
  44.7 8.5 qkv.1
  60.2 7.1 collective-permute-done.10
  73.2 6.6 collective-permute-done.3.a1
  92.0 4.7 rope.1
  97.7 11.9 %collective-permute-start.11 = (bf16[256,256]{1,0:T(8,128)(2,1)S(1)}, bf16[256,256]{1,0:T(8,128)(2,1)S(1)}, u32[]{:S(2)}, u32[]{:S(2)}) collective-permute-start(bf16[256,256]{1,0:T(8,128)(2,1)S(1)} %slice.102), channel_id=1, source_target_pairs={{0,4},{8,12},{16,20},{24,28},{1,5},{9,13},{17,21},{25,29},{2,6},{1... | collective-permute-start | bytes 393224 | tf_op jit(solution)/shard_map/ppermute | solution.py:155
  111.8 7.9 attend.1
  123.3 4.5 collective-permute-done.13.refs_2_
  139.7 9.0 %gather_fusion.7 = bf16[2048,256]{1,0:T(8,128)(2,1)} fusion(bf16[2048,256]{1,0:T(8,128)(2,1)S(1)} %bitcast.99, s32[2048]{0:T(1024)S(1)} %broadcast_clamp_fusion), kind=kCustom, calls=%fused_computation.7 | custom fusion | bytes 2105344 | tf_op jit(solution)/shard_map/gather | solution.py:1060
  183.7 6.2 dhidden.7
  189.9 6.1 dhidden.6
  200.3 13.4 %collective-permute-done.21 = bf16[2,192,256]{2,1,0:T(8,128)(2,1)S(1)} collective-permute-done((bf16[2,192,256]{2,1,0:T(8,128)(2,1)S(1)}, bf16[2,192,256]{2,1,0:T(8,128)(2,1)S(1)}, u32[]{:S(2)}, u32[]{:S(2)}) %collective-permute-start.21) | collective-permute-done | bytes 196640 | tf_op jit(solution)/shard_map/ppermute | solution.py:177
  215.6 5.6 collective-permute-done.24
  223.2 5.6 collective-permute-done.27
  230.7 5.6 collective-permute-done.30
  237.0 4.3 norm.1
  242.7 6.1 dhidden.5
  249.6 6.2 dhidden.4
  256.9 8.0 up.7
  270.1 7.4 up.6
  277.5 7.4 up.5
  306.1 7.4 up.4
  313.5 39.4 %collective-permute-done.44.refs_10_ = bf16[192,1408]{1,0:T(8,128)(2,1)S(1)} collective-permute-done((bf16[192,1408]{1,0:T(8,128)(2,1)}, bf16[192,1408]{1,0:T(8,128)(2,1)S(1)}, u32[]{:S(2)}, u32[]{:S(2)}) %collective-permute-start.44) | collective-permute-done | bytes 540704 | tf_op jit(solution)/shard_map/ppermute | solution.py:147
  354.0 14.0 %mid.1 = (bf16[3,192,1408]{2,1,0:T(8,128)(2,1)}, bf16[3,192,1408]{2,1,0:T(8,128)(2,1)}, f32[8,192]{1,0:T(8,128)}) custom-call(s32[6]{0:T(128)} %stack.85.m, bf16[2,192,1408]{2,1,0:T(8,128)(2,1)} %get-tuple-element.85.refs_0_, bf16[2,192,1408]{2,1,0:T(8,128)(2,1)} %collective-permute-done.32.refs_1_, bf16[2,192,1408]{2,1,0:T(8,128)(2,1)} %collective-permute-done.34.refs_2_, ...), custom_call_target="tpu_custom_call" | custom-call | bytes 13006848 | tf_op jit(solution)/shard_map/mid/pallas_call | solution.py:61
  374.0 10.1 %dx.4 = bf16[2,192,256]{2,1,0:T(8,128)(2,1)} custom-call(s32[6]{0:T(128)} %stack.85.m, bf16[3,192,1408]{2,1,0:T(8,128)(2,1)} %get-tuple-element.102.refs_0_, bf16[3,192,1408]{2,1,0:T(8,128)(2,1)} %get-tuple-element.103.refs_1_.refs_4_, bf16[4,2,256,1408]{3,2,1,0:T(8,128)(2,1)} %bitcast.94.refs_1_.refs_2_, ...), custom_call_target="tpu_custom_call" | custom-call | flops 2214592512 | bytes 14999552 | tf_op jit(solution)/shard_map/dx/pallas_call | solution.py:61
  387.7 6.5 down.4
  394.2 11.6 %collective-permute-done.83 = f32[8,192]{1,0:T(8,128)S(1)} collective-permute-done((f32[8,192]{1,0:T(8,128)S(1)}, f32[8,192]{1,0:T(8,128)S(1)}, u32[]{:S(2)}, u32[]{:S(2)}) %collective-permute-start.83) | collective-permute-done | bytes 6176 | tf_op jit(solution)/shard_map/ppermute | solution.py:147
  415.5 4.3 collective-permute-start.67
  425.8 19.7 %collective-permute-done.50 = bf16[2,192,256]{2,1,0:T(8,128)(2,1)S(1)} collective-permute-done((bf16[2,192,256]{2,1,0:T(8,128)(2,1)S(1)}, bf16[2,192,256]{2,1,0:T(8,128)(2,1)S(1)}, u32[]{:S(2)}, u32[]{:S(2)}) %collective-permute-start.50) | collective-permute-done | bytes 196640 | tf_op jit(solution)/shard_map/ppermute | solution.py:177
  447.4 5.6 collective-permute-done.69
  453.7 6.5 down.6
  461.6 10.3 %dx.6 = bf16[2,192,256]{2,1,0:T(8,128)(2,1)} custom-call(s32[6]{0:T(128)} %stack.85.m, bf16[3,192,1408]{2,1,0:T(8,128)(2,1)} %collective-permute-done.56.refs_0_.refs_2_, bf16[3,192,1408]{2,1,0:T(8,128)(2,1)} %collective-permute-done.57.refs_1_.refs_6_, bf16[4,2,256,1408]{3,2,1,0:T(8,128)(2,1)} %bitcast.94.refs_1_.refs_2_, ...), custom_call_target="tpu_custom_call" | custom-call | flops 2214592512 | bytes 14999552 | tf_op jit(solution)/shard_map/dx/pallas_call | solution.py:61
  473.3 6.5 down.5
  481.2 10.1 %dx.5 = bf16[2,192,256]{2,1,0:T(8,128)(2,1)} custom-call(s32[6]{0:T(128)} %stack.85.m, bf16[3,192,1408]{2,1,0:T(8,128)(2,1)} %collective-permute-done.51.refs_0_.refs_1_, bf16[3,192,1408]{2,1,0:T(8,128)(2,1)} %collective-permute-done.52.refs_1_.refs_5_, bf16[4,2,256,1408]{3,2,1,0:T(8,128)(2,1)} %bitcast.94.refs_1_.refs_2_, ...), custom_call_target="tpu_custom_call" | custom-call | flops 2214592512 | bytes 14999552 | tf_op jit(solution)/shard_map/dx/pallas_call | solution.py:61
  500.5 15.2 %collective-permute-done.61.refs_0_.refs_3_ = bf16[3,192,1408]{2,1,0:T(8,128)(2,1)S(1)} collective-permute-done((bf16[3,192,1408]{2,1,0:T(8,128)(2,1)}, bf16[3,192,1408]{2,1,0:T(8,128)(2,1)S(1)}, u32[]{:S(2)}, u32[]{:S(2)}) %collective-permute-start.61) | collective-permute-done | bytes 1622048 | tf_op jit(solution)/shard_map/ppermute | solution.py:147
  517.0 10.1 %dx.7 = bf16[2,192,256]{2,1,0:T(8,128)(2,1)} custom-call(s32[6]{0:T(128)} %stack.85.m, bf16[3,192,1408]{2,1,0:T(8,128)(2,1)} %copy-done, bf16[3,192,1408]{2,1,0:T(8,128)(2,1)} %collective-permute-done.62.refs_1_.refs_7_, bf16[4,2,256,1408]{3,2,1,0:T(8,128)(2,1)} %bitcast.94.refs_1_.refs_2_, ...), custom_call_target="tpu_custom_call" | custom-call | flops 2214592512 | bytes 14999552 | tf_op jit(solution)/shard_map/dx/pallas_call | solution.py:61
  527.1 4.5 collective-permute-start.76
  540.5 10.5 %collective-permute-done.78 = bf16[2,192,256]{2,1,0:T(8,128)(2,1)S(1)} collective-permute-done((bf16[2,192,256]{2,1,0:T(8,128)(2,1)S(1)}, bf16[2,192,256]{2,1,0:T(8,128)(2,1)S(1)}, u32[]{:S(2)}, u32[]{:S(2)}) %collective-permute-start.78) | collective-permute-done | bytes 196640 | tf_op jit(solution)/shard_map/ppermute | solution.py:177
  551.7 6.5 norm_back.1
  558.3 5.9 dmix.1
  575.1 6.5 down.7
  584.0 14.4 %attend_back.1 = (bf16[768,256]{1,0:T(8,128)(2,1)}, f32[768,256]{1,0:T(8,128)}, f32[256,256]{1,0:T(8,128)}, f32[8,768]{1,0:T(8,128)}) custom-call(s32[6]{0:T(128)} %stack.85.m, bf16[768,256]{1,0:T(8,128)(2,1)} %get-tuple-element.80.q_ref.refs_0_, bf16[768,256]{1,0:T(8,128)(2,1)} %get-tuple-element.81.kv_ref.refs_1_, bf16[256,256]{1,0:T(8,128)(2,1)} %copy-done.44, ...), custom_call_target="tpu_custom_call" | custom-call | flops 754974720 | bytes 4792320 | tf_op jit(solution)/shard_map/attend_back/pallas_call | solution.py:61
  599.8 8.8 dwout.2
  620.4 14.9 %dwin.2 = bf16[4,2,256,1408]{3,2,1,0:T(8,128)(2,1)} custom-call(s32[6]{0:T(128)} %stack.85.m, bf16[3,192,1408]{2,1,0:T(8,128)(2,1)} %get-tuple-element.102.refs_0_, bf16[3,192,1408]{2,1,0:T(8,128)(2,1)} %collective-permute-done.51.refs_0_.refs_1_, bf16[3,192,1408]{2,1,0:T(8,128)(2,1)} %collective-permute-done.56.refs_0_.refs_2_, ...), custom_call_target="tpu_custom_call" | custom-call | flops 4429185024 | bytes 19554304 | tf_op jit(solution)/shard_map/dwin/pallas_call | solution.py:61
  655.7 6.8 collective-permute-done.91.refs_2_
  663.0 5.6 collective-permute-done.92.refs_3_
  669.3 4.7 dattn.4
  677.4 4.7 dattn.5
  683.4 4.7 dattn.7
  688.1 4.9 dattn.6
  705.3 18.5 %collective-permute-done.99 = bf16[2,192,256]{2,1,0:T(8,128)(2,1)S(1)} collective-permute-done((bf16[2,192,256]{2,1,0:T(8,128)(2,1)S(1)}, bf16[2,192,256]{2,1,0:T(8,128)(2,1)S(1)}, u32[]{:S(2)}, u32[]{:S(2)}) %collective-permute-start.99) | collective-permute-done | bytes 196640 | tf_op jit(solution)/shard_map/ppermute | solution.py:177
  736.3 6.3 norm_back_first.1
  746.5 9.1 %gather_fusion.4 = bf16[2048,256]{1,0:T(8,128)(2,1)} fusion(bf16[1536,256]{1,0:T(8,128)(2,1)S(1)} %pad_maximum_fusion, s32[2048]{0:T(1024)S(1)} %copy-done.54), kind=kCustom, calls=%fused_computation.4 | custom fusion | bytes 2105344 | tf_op jit(solution)/shard_map/gather | solution.py:1052
  757.4 9.1 %gather_fusion.6 = bf16[2048,256]{1,0:T(8,128)(2,1)} fusion(bf16[1536,256]{1,0:T(8,128)(2,1)S(1)} %pad_maximum_fusion.2, s32[2048]{0:T(1024)S(1)} %copy-done.54), kind=kCustom, calls=%fused_computation.6 | custom fusion | bytes 2105344 | tf_op jit(solution)/shard_map/gather | solution.py:1052
  769.1 4.4 all-to-all-start.3
  775.7 6.3 dwproj.2
  782.1 6.9 collective-permute-done.121
  793.0 7.8 dwqkv.2
  811.2 6.8 dwproj.3
  822.1 9.7 %dwout.3 = f32[4,1408,256]{2,1,0:T(8,128)} custom-call(s32[6]{0:T(128)} %stack.85.m, bf16[3,192,1408]{2,1,0:T(8,128)(2,1)} %get-tuple-element.102.refs_0_, bf16[3,192,1408]{2,1,0:T(8,128)(2,1)} %collective-permute-done.51.refs_0_.refs_1_, bf16[3,192,1408]{2,1,0:T(8,128)(2,1)} %collective-permute-done.56.refs_0_.refs_2_, bf16[3,192,1408]{2,1,0:T(8,128)(2,1)} %copy-done, ...), custom_call_target="tpu_custom_call" | custom-call | flops 2214592512 | bytes 22044672 | tf_op jit(solution)/shard_map/dwout/pallas_call | solution.py:61
  833.6 8.9 %dwqkv.3 = (f32[4,256,512]{2,1,0:T(8,128)}, f32[2,256,512]{2,1,0:T(8,128)}) custom-call(s32[6]{0:T(128)} %stack.85.m, bf16[768,256]{1,0:T(8,128)(2,1)} %get-tuple-element.117.refs_0_, bf16[768,256]{1,0:T(8,128)(2,1)} %copy-done.6, bf16[768,256]{1,0:T(8,128)(2,1)} %copy-done.8, bf16[768,256]{1,0:T(8,128)(2,1)} %copy-done.10, ...), custom_call_target="tpu_custom_call" | custom-call | flops 1207959552 | bytes 8675328 | tf_op jit(solution)/shard_map/dwqkv/pallas_call | solution.py:61
  846.3 17.0 %dwin.3 = f32[4,2,256,1408]{3,2,1,0:T(8,128)} custom-call(s32[6]{0:T(128)} %stack.85.m, bf16[3,192,1408]{2,1,0:T(8,128)(2,1)} %get-tuple-element.102.refs_0_, bf16[3,192,1408]{2,1,0:T(8,128)(2,1)} %collective-permute-done.51.refs_0_.refs_1_, bf16[3,192,1408]{2,1,0:T(8,128)(2,1)} %collective-permute-done.56.refs_0_.refs_2_, bf16[3,192,1408]{2,1,0:T(8,128)(2,1)} %copy-done, ...), custom_call_target="tpu_custom_call" | custom-call | flops 4429185024 | bytes 31088640 | tf_op jit(solution)/shard_map/dwin/pallas_call | solution.py:61
  863.3 20.2 %copy.188 = f32[4,256,2,1408]{3,2,1,0:T(2,128)} copy(f32[4,256,2,1408]{3,1,2,0:T(8,128)} %bitcast.102) | data formatting | bytes 23068672
  (621 shorter events, 316.4 us)
Async XLA Ops:
  0.6 43.3 %collective-permute-start.2 = (bf16[2,256,512]{2,1,0:T(8,128)(2,1)}, bf16[2,256,512]{2,1,0:T(8,128)(2,1)}, u32[]{:S(2)}, u32[]{:S(2)}) collective-permute-start(bf16[2,256,512]{2,1,0:T(8,128)(2,1)} %refs_11_.7), channel_id=1, source_target_pairs={{0,4},{4,0},{8,12},{12,8},{16,20},{20,16},{24,28},{28,24},{1,5},{5... | collective-permute-start | bytes 1572872 | tf_op jit(solution)/shard_map/ppermute | solution.py:151
  3.9 28.4 %all-to-all-start = ((bf16[8,256,256]{2,1,0:T(8,128)(2,1)}), bf16[8,256,256]{2,1,0:T(8,128)(2,1)S(1)}, u32[]{:S(2)}, u32[]{:S(2)}) async-start(bf16[8,256,256]{2,1,0:T(8,128)(2,1)} %bitcast.96), calls=%async_computation | async-start | bytes 2097152 | tf_op jit(solution)/shard_map/all_to_all | solution.py:223
  8.9 35.0 %collective-permute-start.1 = (bf16[4,256,512]{2,1,0:T(8,128)(2,1)}, bf16[4,256,512]{2,1,0:T(8,128)(2,1)}, u32[]{:S(2)}, u32[]{:S(2)}) collective-permute-start(bf16[4,256,512]{2,1,0:T(8,128)(2,1)} %refs_9_.15), channel_id=1, source_target_pairs={{0,4},{4,0},{8,12},{12,8},{16,20},{20,16},{24,28},{28,24},{1,5},{5... | collective-permute-start | bytes 3145736 | tf_op jit(solution)/shard_map/ppermute | solution.py:151
  9.5 112.3 %collective-permute-start.18 = (bf16[4,512,256]{2,1,0:T(8,128)(2,1)S(1)}, bf16[4,512,256]{2,1,0:T(8,128)(2,1)}, u32[]{:S(2)}, u32[]{:S(2)}) collective-permute-start(bf16[4,512,256]{2,1,0:T(8,128)(2,1)S(1)} %copy-done.1), channel_id=1, source_target_pairs={{0,4},{4,0},{8,12},{12,8},{16,20},{20,16},{24,28},{28,24},{1,5},{5... | collective-permute-start | bytes 3145736 | tf_op jit(solution)/shard_map/ppermute | solution.py:151
  15.5 241.4 %collective-permute-start.31 = (bf16[4,2,256,1408]{3,2,1,0:T(8,128)(2,1)}, bf16[4,2,256,1408]{3,2,1,0:T(8,128)(2,1)}, u32[]{:S(2)}, u32[]{:S(2)}) collective-permute-start(bf16[4,2,256,1408]{3,2,1,0:T(8,128)(2,1)} %bitcast.94.refs_1_.refs_2_), channel_id=1, source_target_pairs={{0,4},{4,0},{8,12},{12,8},{16,20},{20,16},{24,28},{28,24},{1,5},{5... | collective-permute-start | bytes 17301512 | tf_op jit(solution)/shard_map/ppermute | solution.py:151
  32.3 100.8 %all-to-all-start.1 = ((bf16[8,256,256]{2,1,0:T(8,128)(2,1)}), bf16[8,256,256]{2,1,0:T(8,128)(2,1)S(1)}, u32[]{:S(2)}, u32[]{:S(2)}) async-start(bf16[8,256,256]{2,1,0:T(8,128)(2,1)} %bitcast.108), calls=%async_computation.1 | async-start | bytes 2097152 | tf_op jit(solution)/shard_map/all_to_all | solution.py:225
  67.4 115.6 %collective-permute-start.39 = (bf16[4,1408,256]{2,1,0:T(8,128)(2,1)}, bf16[4,1408,256]{2,1,0:T(8,128)(2,1)}, u32[]{:S(2)}, u32[]{:S(2)}) collective-permute-start(bf16[4,1408,256]{2,1,0:T(8,128)(2,1)} %refs_2_.15), channel_id=1, source_target_pairs={{0,4},{4,0},{8,12},{12,8},{16,20},{20,16},{24,28},{28,24},{1,5},{5... | collective-permute-start | bytes 8650760 | tf_op jit(solution)/shard_map/ppermute | solution.py:151
  127.8 20.9 %collective-permute-start.15 = (bf16[768,128]{1,0:T(8,128)(2,1)}, bf16[768,128]{1,0:T(8,128)(2,1)S(1)}, u32[]{:S(2)}, u32[]{:S(2)}) collective-permute-start(bf16[768,128]{1,0:T(8,128)(2,1)} %get-tuple-element.83.refs_4_), channel_id=1, source_target_pairs={{0,8},{4,12},{8,0},{12,4},{16,24},{20,28},{24,16},{28,20},{1,9},{5... | collective-permute-start | bytes 589832 | tf_op jit(solution)/shard_map/ppermute | solution.py:147
  129.3 19.6 %collective-permute-start.14 = (bf16[768,128]{1,0:T(8,128)(2,1)}, bf16[768,128]{1,0:T(8,128)(2,1)S(1)}, u32[]{:S(2)}, u32[]{:S(2)}) collective-permute-start(bf16[768,128]{1,0:T(8,128)(2,1)} %collective-permute-done.12.refs_1_), channel_id=1, source_target_pairs={{0,16},{4,20},{8,24},{12,28},{16,0},{20,4},{24,8},{28,12},{1,17},{... | collective-permute-start | bytes 589832 | tf_op jit(solution)/shard_map/ppermute | solution.py:147
  131.6 17.2 %collective-permute-start.17 = (bf16[768,128]{1,0:T(8,128)(2,1)S(1)}, bf16[768,128]{1,0:T(8,128)(2,1)S(1)}, u32[]{:S(2)}, u32[]{:S(2)}) collective-permute-start(bf16[768,128]{1,0:T(8,128)(2,1)S(1)} %collective-permute-done.16.refs_6_), channel_id=1, source_target_pairs={{0,8},{4,12},{8,0},{12,4},{16,24},{20,28},{24,16},{28,20},{1,9},{5... | collective-permute-start | bytes 589832 | tf_op jit(solution)/shard_map/ppermute | solution.py:147
  148.7 33.6 %collective-permute-start.38 = (bf16[768,256]{1,0:T(8,128)(2,1)}, bf16[768,256]{1,0:T(8,128)(2,1)S(1)}, u32[]{:S(2)}, u32[]{:S(2)}) collective-permute-start(bf16[768,256]{1,0:T(8,128)(2,1)} %gather_fusion.3), channel_id=1, source_target_pairs={{0,4},{4,0},{8,12},{12,8},{16,20},{20,16},{24,28},{28,24},{1,5},{5... | collective-permute-start | bytes 1179656 | tf_op jit(solution)/shard_map/ppermute | solution.py:151
  153.9 17.2 %collective-permute-start.19 = (bf16[2,192,256]{2,1,0:T(8,128)(2,1)}, bf16[2,192,256]{2,1,0:T(8,128)(2,1)S(1)}, u32[]{:S(2)}, u32[]{:S(2)}) collective-permute-start(bf16[2,192,256]{2,1,0:T(8,128)(2,1)} %proj.4), channel_id=1, source_target_pairs={{0,1},{3,2},{4,5},{7,6},{8,9},{11,10},{12,13},{15,14},{16,17},{19,... | collective-permute-start | bytes 589832 | tf_op jit(solution)/shard_map/ppermute | solution.py:173
  178.0 18.1 %collective-permute-start.20 = (bf16[2,192,256]{2,1,0:T(8,128)(2,1)S(1)}, bf16[2,192,256]{2,1,0:T(8,128)(2,1)S(1)}, u32[]{:S(2)}, u32[]{:S(2)}) collective-permute-start(bf16[2,192,256]{2,1,0:T(8,128)(2,1)S(1)} %add_convert_fusion.39), channel_id=1, source_target_pairs={{1,2},{2,1},{5,6},{6,5},{9,10},{10,9},{13,14},{14,13},{17,18},{18,... | collective-permute-start | bytes 589832 | tf_op jit(solution)/shard_map/ppermute | solution.py:175
  181.6 15.0 %collective-permute-start.23 = (bf16[2,192,256]{2,1,0:T(8,128)(2,1)S(1)}, bf16[2,192,256]{2,1,0:T(8,128)(2,1)S(1)}, u32[]{:S(2)}, u32[]{:S(2)}) collective-permute-start(bf16[2,192,256]{2,1,0:T(8,128)(2,1)S(1)} %add_convert_fusion.37), channel_id=1, source_target_pairs={{1,2},{2,1},{5,6},{6,5},{9,10},{10,9},{13,14},{14,13},{17,18},{18,... | collective-permute-start | bytes 589832 | tf_op jit(solution)/shard_map/ppermute | solution.py:175
  182.3 15.6 %collective-permute-start.26 = (bf16[2,192,256]{2,1,0:T(8,128)(2,1)S(1)}, bf16[2,192,256]{2,1,0:T(8,128)(2,1)S(1)}, u32[]{:S(2)}, u32[]{:S(2)}) collective-permute-start(bf16[2,192,256]{2,1,0:T(8,128)(2,1)S(1)} %add_convert_fusion.35), channel_id=1, source_target_pairs={{1,2},{2,1},{5,6},{6,5},{9,10},{10,9},{13,14},{14,13},{17,18},{18,... | collective-permute-start | bytes 589832 | tf_op jit(solution)/shard_map/ppermute | solution.py:175
  183.0 15.9 %collective-permute-start.29 = (bf16[2,192,256]{2,1,0:T(8,128)(2,1)S(1)}, bf16[2,192,256]{2,1,0:T(8,128)(2,1)S(1)}, u32[]{:S(2)}, u32[]{:S(2)}) collective-permute-start(bf16[2,192,256]{2,1,0:T(8,128)(2,1)S(1)} %add_convert_fusion.33), channel_id=1, source_target_pairs={{1,2},{2,1},{5,6},{6,5},{9,10},{10,9},{13,14},{14,13},{17,18},{18,... | collective-permute-start | bytes 589832 | tf_op jit(solution)/shard_map/ppermute | solution.py:175
  196.0 69.8 %collective-permute-start.41 = (bf16[192,1408]{1,0:T(8,128)(2,1)}, bf16[192,1408]{1,0:T(8,128)(2,1)S(1)}, u32[]{:S(2)}, u32[]{:S(2)}) collective-permute-start(bf16[192,1408]{1,0:T(8,128)(2,1)} %get-tuple-element.96), channel_id=1, source_target_pairs={{0,8},{4,12},{8,0},{12,4},{16,24},{20,28},{24,16},{28,20},{1,9},{5... | collective-permute-start | bytes 1622024 | tf_op jit(solution)/shard_map/ppermute | solution.py:147
  196.6 100.0 %collective-permute-start.43 = (bf16[192,1408]{1,0:T(8,128)(2,1)}, bf16[192,1408]{1,0:T(8,128)(2,1)}, u32[]{:S(2)}, u32[]{:S(2)}) collective-permute-start(bf16[192,1408]{1,0:T(8,128)(2,1)} %get-tuple-element.99), channel_id=1, source_target_pairs={{0,16},{4,20},{8,24},{12,28},{16,0},{20,4},{24,8},{28,12},{1,17},{... | collective-permute-start | bytes 1622024 | tf_op jit(solution)/shard_map/ppermute | solution.py:147
  198.0 99.8 %collective-permute-start.45 = (bf16[192,1408]{1,0:T(8,128)(2,1)}, bf16[192,1408]{1,0:T(8,128)(2,1)}, u32[]{:S(2)}, u32[]{:S(2)}) collective-permute-start(bf16[192,1408]{1,0:T(8,128)(2,1)} %get-tuple-element.100), channel_id=1, source_target_pairs={{0,16},{4,20},{8,24},{12,28},{16,0},{20,4},{24,8},{28,12},{1,17},{... | collective-permute-start | bytes 1622024 | tf_op jit(solution)/shard_map/ppermute | solution.py:147
  198.9 14.7 %collective-permute-start.21 = (bf16[2,192,256]{2,1,0:T(8,128)(2,1)S(1)}, bf16[2,192,256]{2,1,0:T(8,128)(2,1)S(1)}, u32[]{:S(2)}, u32[]{:S(2)}) collective-permute-start(bf16[2,192,256]{2,1,0:T(8,128)(2,1)S(1)} %add_convert_fusion.38), channel_id=1, source_target_pairs={{1,0},{2,3},{5,4},{6,7},{9,8},{10,11},{13,12},{14,15},{17,16},{18,... | collective-permute-start | bytes 589832 | tf_op jit(solution)/shard_map/ppermute | solution.py:177
  255.7 42.8 %collective-permute-start.40 = (bf16[192,1408]{1,0:T(8,128)(2,1)}, bf16[192,1408]{1,0:T(8,128)(2,1)}, u32[]{:S(2)}, u32[]{:S(2)}) collective-permute-start(bf16[192,1408]{1,0:T(8,128)(2,1)} %get-tuple-element.94), channel_id=1, source_target_pairs={{0,8},{4,12},{8,0},{12,4},{16,24},{20,28},{24,16},{28,20},{1,9},{5... | collective-permute-start | bytes 1622024 | tf_op jit(solution)/shard_map/ppermute | solution.py:147
  264.9 23.6 %collective-permute-start.33 = (bf16[2,192,1408]{2,1,0:T(8,128)(2,1)}, bf16[2,192,1408]{2,1,0:T(8,128)(2,1)S(1)}, u32[]{:S(2)}, u32[]{:S(2)}) collective-permute-start(bf16[2,192,1408]{2,1,0:T(8,128)(2,1)} %get-tuple-element.88), channel_id=1, source_target_pairs={{0,8},{4,12},{8,0},{12,4},{16,24},{20,28},{24,16},{28,20},{1,9},{5... | collective-permute-start | bytes 3244040 | tf_op jit(solution)/shard_map/ppermute | solution.py:147
  266.7 25.8 %collective-permute-start.35 = (bf16[2,192,1408]{2,1,0:T(8,128)(2,1)}, bf16[2,192,1408]{2,1,0:T(8,128)(2,1)S(1)}, u32[]{:S(2)}, u32[]{:S(2)}) collective-permute-start(bf16[2,192,1408]{2,1,0:T(8,128)(2,1)} %get-tuple-element.91), channel_id=1, source_target_pairs={{0,16},{4,20},{8,24},{12,28},{16,0},{20,4},{24,8},{28,12},{1,17},{... | collective-permute-start | bytes 3244040 | tf_op jit(solution)/shard_map/ppermute | solution.py:147
  288.5 15.5 %collective-permute-start.42 = (bf16[192,1408]{1,0:T(8,128)(2,1)}, bf16[192,1408]{1,0:T(8,128)(2,1)}, u32[]{:S(2)}, u32[]{:S(2)}) collective-permute-start(bf16[192,1408]{1,0:T(8,128)(2,1)} %add_convert_fusion.3), channel_id=1, source_target_pairs={{0,16},{4,20},{8,24},{12,28},{16,0},{20,4},{24,8},{28,12},{1,17},{... | collective-permute-start | bytes 1622024 | tf_op jit(solution)/shard_map/ppermute | solution.py:147
  293.4 59.4 %collective-permute-start.37 = (bf16[2,192,1408]{2,1,0:T(8,128)(2,1)}, bf16[2,192,1408]{2,1,0:T(8,128)(2,1)S(1)}, u32[]{:S(2)}, u32[]{:S(2)}) collective-permute-start(bf16[2,192,1408]{2,1,0:T(8,128)(2,1)} %get-tuple-element.92), channel_id=1, source_target_pairs={{0,16},{4,20},{8,24},{12,28},{16,0},{20,4},{24,8},{28,12},{1,17},{... | collective-permute-start | bytes 3244040 | tf_op jit(solution)/shard_map/ppermute | solution.py:147
  296.6 56.2 %collective-permute-start.32 = (bf16[2,192,1408]{2,1,0:T(8,128)(2,1)}, bf16[2,192,1408]{2,1,0:T(8,128)(2,1)}, u32[]{:S(2)}, u32[]{:S(2)}) collective-permute-start(bf16[2,192,1408]{2,1,0:T(8,128)(2,1)} %get-tuple-element.86), channel_id=1, source_target_pairs={{0,8},{4,12},{8,0},{12,4},{16,24},{20,28},{24,16},{28,20},{1,9},{5... | collective-permute-start | bytes 3244040 | tf_op jit(solution)/shard_map/ppermute | solution.py:147
  297.7 55.1 %collective-permute-start.34 = (bf16[2,192,1408]{2,1,0:T(8,128)(2,1)}, bf16[2,192,1408]{2,1,0:T(8,128)(2,1)}, u32[]{:S(2)}, u32[]{:S(2)}) collective-permute-start(bf16[2,192,1408]{2,1,0:T(8,128)(2,1)} %add_convert_fusion.1), channel_id=1, source_target_pairs={{0,16},{4,20},{8,24},{12,28},{16,0},{20,4},{24,8},{28,12},{1,17},{... | collective-permute-start | bytes 3244040 | tf_op jit(solution)/shard_map/ppermute | solution.py:147
  298.6 54.3 %collective-permute-start.36 = (bf16[2,192,1408]{2,1,0:T(8,128)(2,1)}, bf16[2,192,1408]{2,1,0:T(8,128)(2,1)}, u32[]{:S(2)}, u32[]{:S(2)}) collective-permute-start(bf16[2,192,1408]{2,1,0:T(8,128)(2,1)} %add_convert_fusion), channel_id=1, source_target_pairs={{0,8},{4,12},{8,0},{12,4},{16,24},{20,28},{24,16},{28,20},{1,9},{5... | collective-permute-start | bytes 3244040 | tf_op jit(solution)/shard_map/ppermute | solution.py:147
  303.9 48.9 %collective-permute-start.44 = (bf16[192,1408]{1,0:T(8,128)(2,1)}, bf16[192,1408]{1,0:T(8,128)(2,1)S(1)}, u32[]{:S(2)}, u32[]{:S(2)}) collective-permute-start(bf16[192,1408]{1,0:T(8,128)(2,1)} %add_convert_fusion.2), channel_id=1, source_target_pairs={{0,8},{4,12},{8,0},{12,4},{16,24},{20,28},{24,16},{28,20},{1,9},{5... | collective-permute-start | bytes 1622024 | tf_op jit(solution)/shard_map/ppermute | solution.py:147
  369.3 84.4 %collective-permute-start.56 = (bf16[3,192,1408]{2,1,0:T(8,128)(2,1)}, bf16[3,192,1408]{2,1,0:T(8,128)(2,1)}, u32[]{:S(2)}, u32[]{:S(2)}) collective-permute-start(bf16[3,192,1408]{2,1,0:T(8,128)(2,1)} %get-tuple-element.102.refs_0_), channel_id=1, source_target_pairs={{0,16},{4,20},{8,24},{12,28},{16,0},{20,4},{24,8},{28,12},{1,17},{... | collective-permute-start | bytes 4866056 | tf_op jit(solution)/shard_map/ppermute | solution.py:147
  370.1 103.2 %collective-permute-start.51 = (bf16[3,192,1408]{2,1,0:T(8,128)(2,1)}, bf16[3,192,1408]{2,1,0:T(8,128)(2,1)}, u32[]{:S(2)}, u32[]{:S(2)}) collective-permute-start(bf16[3,192,1408]{2,1,0:T(8,128)(2,1)} %get-tuple-element.102.refs_0_), channel_id=1, source_target_pairs={{0,8},{4,12},{8,0},{12,4},{16,24},{20,28},{24,16},{28,20},{1,9},{5... | collective-permute-start | bytes 4866056 | tf_op jit(solution)/shard_map/ppermute | solution.py:147
  384.2 21.6 %collective-permute-start.83 = (f32[8,192]{1,0:T(8,128)S(1)}, f32[8,192]{1,0:T(8,128)S(1)}, u32[]{:S(2)}, u32[]{:S(2)}) collective-permute-start(f32[8,192]{1,0:T(8,128)S(1)} %add.737), channel_id=1, source_target_pairs={{0,24},{4,28},{8,16},{12,20},{16,8},{20,12},{24,0},{28,4},{1,25},{... | collective-permute-start | bytes 18440 | tf_op jit(solution)/shard_map/ppermute | solution.py:147
  386.0 20.4 %collective-permute-start.82 = (f32[8,192]{1,0:T(8,128)S(1)}, f32[8,192]{1,0:T(8,128)S(1)}, u32[]{:S(2)}, u32[]{:S(2)}) collective-permute-start(f32[8,192]{1,0:T(8,128)S(1)} %add.737), channel_id=1, source_target_pairs={{0,16},{4,20},{8,24},{12,28},{16,0},{20,4},{24,8},{28,12},{1,17},{... | collective-permute-start | bytes 18440 | tf_op jit(solution)/shard_map/ppermute | solution.py:147
  386.6 21.5 %collective-permute-start.81 = (f32[8,192]{1,0:T(8,128)S(1)}, f32[8,192]{1,0:T(8,128)S(1)}, u32[]{:S(2)}, u32[]{:S(2)}) collective-permute-start(f32[8,192]{1,0:T(8,128)S(1)} %add.737), channel_id=1, source_target_pairs={{0,8},{4,12},{8,0},{12,4},{16,24},{20,28},{24,16},{28,20},{1,9},{5... | collective-permute-start | bytes 18440 | tf_op jit(solution)/shard_map/ppermute | solution.py:147
  405.8 47.9 %collective-permute-start.57 = (bf16[3,192,1408]{2,1,0:T(8,128)(2,1)}, bf16[3,192,1408]{2,1,0:T(8,128)(2,1)}, u32[]{:S(2)}, u32[]{:S(2)}) collective-permute-start(bf16[3,192,1408]{2,1,0:T(8,128)(2,1)} %get-tuple-element.103.refs_1_.refs_4_), channel_id=1, source_target_pairs={{0,16},{4,20},{8,24},{12,28},{16,0},{20,4},{24,8},{28,12},{1,17},{... | collective-permute-start | bytes 4866056 | tf_op jit(solution)/shard_map/ppermute | solution.py:147
  406.4 66.9 %collective-permute-start.52 = (bf16[3,192,1408]{2,1,0:T(8,128)(2,1)}, bf16[3,192,1408]{2,1,0:T(8,128)(2,1)}, u32[]{:S(2)}, u32[]{:S(2)}) collective-permute-start(bf16[3,192,1408]{2,1,0:T(8,128)(2,1)} %get-tuple-element.103.refs_1_.refs_4_), channel_id=1, source_target_pairs={{0,8},{4,12},{8,0},{12,4},{16,24},{20,28},{24,16},{28,20},{1,9},{5... | collective-permute-start | bytes 4866056 | tf_op jit(solution)/shard_map/ppermute | solution.py:147
  424.4 21.0 %collective-permute-start.50 = (bf16[2,192,256]{2,1,0:T(8,128)(2,1)S(1)}, bf16[2,192,256]{2,1,0:T(8,128)(2,1)S(1)}, u32[]{:S(2)}, u32[]{:S(2)}) collective-permute-start(bf16[2,192,256]{2,1,0:T(8,128)(2,1)S(1)} %add_convert_fusion.30), channel_id=1, source_target_pairs={{1,0},{2,3},{5,4},{6,7},{9,8},{10,11},{13,12},{14,15},{17,16},{18,... | collective-permute-start | bytes 589832 | tf_op jit(solution)/shard_map/ppermute | solution.py:177
  460.2 33.0 %collective-permute-start.58 = (bf16[2,192,256]{2,1,0:T(8,128)(2,1)}, bf16[2,192,256]{2,1,0:T(8,128)(2,1)S(1)}, u32[]{:S(2)}, u32[]{:S(2)}) collective-permute-start(bf16[2,192,256]{2,1,0:T(8,128)(2,1)} %down.6), channel_id=1, source_target_pairs={{0,1},{3,2},{4,5},{7,6},{8,9},{11,10},{12,13},{15,14},{16,17},{19,... | collective-permute-start | bytes 589832 | tf_op jit(solution)/shard_map/ppermute | solution.py:173
  472.0 22.7 %collective-permute-start.73 = (bf16[2,192,256]{2,1,0:T(8,128)(2,1)}, bf16[2,192,256]{2,1,0:T(8,128)(2,1)S(1)}, u32[]{:S(2)}, u32[]{:S(2)}) collective-permute-start(bf16[2,192,256]{2,1,0:T(8,128)(2,1)} %dx.6), channel_id=1, source_target_pairs={{0,1},{3,2},{4,5},{7,6},{8,9},{11,10},{12,13},{15,14},{16,17},{19,... | collective-permute-start | bytes 589832 | tf_op jit(solution)/shard_map/ppermute | solution.py:173
  479.8 15.6 %collective-permute-start.53 = (bf16[2,192,256]{2,1,0:T(8,128)(2,1)}, bf16[2,192,256]{2,1,0:T(8,128)(2,1)S(1)}, u32[]{:S(2)}, u32[]{:S(2)}) collective-permute-start(bf16[2,192,256]{2,1,0:T(8,128)(2,1)} %down.5), channel_id=1, source_target_pairs={{0,1},{3,2},{4,5},{7,6},{8,9},{11,10},{12,13},{15,14},{16,17},{19,... | collective-permute-start | bytes 589832 | tf_op jit(solution)/shard_map/ppermute | solution.py:173
  492.8 22.9 %collective-permute-start.61 = (bf16[3,192,1408]{2,1,0:T(8,128)(2,1)}, bf16[3,192,1408]{2,1,0:T(8,128)(2,1)S(1)}, u32[]{:S(2)}, u32[]{:S(2)}) collective-permute-start(bf16[3,192,1408]{2,1,0:T(8,128)(2,1)} %collective-permute-done.51.refs_0_.refs_1_), channel_id=1, source_target_pairs={{0,16},{4,20},{8,24},{12,28},{16,0},{20,4},{24,8},{28,12},{1,17},{... | collective-permute-start | bytes 4866056 | tf_op jit(solution)/shard_map/ppermute | solution.py:147
  493.1 23.8 %collective-permute-start.62 = (bf16[3,192,1408]{2,1,0:T(8,128)(2,1)}, bf16[3,192,1408]{2,1,0:T(8,128)(2,1)}, u32[]{:S(2)}, u32[]{:S(2)}) collective-permute-start(bf16[3,192,1408]{2,1,0:T(8,128)(2,1)} %collective-permute-done.57.refs_1_.refs_6_), channel_id=1, source_target_pairs={{0,8},{4,12},{8,0},{12,4},{16,24},{20,28},{24,16},{28,20},{1,9},{5... | collective-permute-start | bytes 4866056 | tf_op jit(solution)/shard_map/ppermute | solution.py:147
  497.0 34.7 %collective-permute-start.71 = (bf16[2,192,256]{2,1,0:T(8,128)(2,1)S(1)}, bf16[2,192,256]{2,1,0:T(8,128)(2,1)S(1)}, u32[]{:S(2)}, u32[]{:S(2)}) collective-permute-start(bf16[2,192,256]{2,1,0:T(8,128)(2,1)S(1)} %add_convert_fusion.21), channel_id=1, source_target_pairs={{1,2},{2,1},{5,6},{6,5},{9,10},{10,9},{13,14},{14,13},{17,18},{18,... | collective-permute-start | bytes 589832 | tf_op jit(solution)/shard_map/ppermute | solution.py:175
  497.8 67.0 %collective-permute-start.60 = (bf16[2,192,256]{2,1,0:T(8,128)(2,1)S(1)}, bf16[2,192,256]{2,1,0:T(8,128)(2,1)S(1)}, u32[]{:S(2)}, u32[]{:S(2)}) collective-permute-start(bf16[2,192,256]{2,1,0:T(8,128)(2,1)S(1)} %add_convert_fusion.26), channel_id=1, source_target_pairs={{1,0},{2,3},{5,4},{6,7},{9,8},{10,11},{13,12},{14,15},{17,16},{18,... | collective-permute-start | bytes 589832 | tf_op jit(solution)/shard_map/ppermute | solution.py:177
  499.1 37.7 %collective-permute-start.75 = (bf16[2,192,256]{2,1,0:T(8,128)(2,1)S(1)}, bf16[2,192,256]{2,1,0:T(8,128)(2,1)}, u32[]{:S(2)}, u32[]{:S(2)}) collective-permute-start(bf16[2,192,256]{2,1,0:T(8,128)(2,1)S(1)} %add_convert_fusion.18), channel_id=1, source_target_pairs={{1,0},{2,3},{5,4},{6,7},{9,8},{10,11},{13,12},{14,15},{17,16},{18,... | collective-permute-start | bytes 589832 | tf_op jit(solution)/shard_map/ppermute | solution.py:177
  515.7 58.8 %collective-permute-start.55 = (bf16[2,192,256]{2,1,0:T(8,128)(2,1)S(1)}, bf16[2,192,256]{2,1,0:T(8,128)(2,1)S(1)}, u32[]{:S(2)}, u32[]{:S(2)}) collective-permute-start(bf16[2,192,256]{2,1,0:T(8,128)(2,1)S(1)} %add_convert_fusion.28), channel_id=1, source_target_pairs={{1,0},{2,3},{5,4},{6,7},{9,8},{10,11},{13,12},{14,15},{17,16},{18,... | collective-permute-start | bytes 589832 | tf_op jit(solution)/shard_map/ppermute | solution.py:177
  565.5 17.6 %collective-permute-start.84 = (bf16[768,128]{1,0:T(8,128)(2,1)}, bf16[768,128]{1,0:T(8,128)(2,1)S(1)}, u32[]{:S(2)}, u32[]{:S(2)}) collective-permute-start(bf16[768,128]{1,0:T(8,128)(2,1)} %get-tuple-element.108), channel_id=1, source_target_pairs={{0,8},{4,12},{8,0},{12,4},{16,24},{20,28},{24,16},{28,20},{1,9},{5... | collective-permute-start | bytes 589832 | tf_op jit(solution)/shard_map/ppermute | solution.py:147
  567.3 15.8 %collective-permute-start.89 = (bf16[768,128]{1,0:T(8,128)(2,1)}, bf16[768,128]{1,0:T(8,128)(2,1)S(1)}, u32[]{:S(2)}, u32[]{:S(2)}) collective-permute-start(bf16[768,128]{1,0:T(8,128)(2,1)} %get-tuple-element.114), channel_id=1, source_target_pairs={{0,16},{4,20},{8,24},{12,28},{16,0},{20,4},{24,8},{28,12},{1,17},{... | collective-permute-start | bytes 589832 | tf_op jit(solution)/shard_map/ppermute | solution.py:147
  581.6 28.1 %collective-permute-start.63 = (bf16[2,192,256]{2,1,0:T(8,128)(2,1)}, bf16[2,192,256]{2,1,0:T(8,128)(2,1)S(1)}, u32[]{:S(2)}, u32[]{:S(2)}) collective-permute-start(bf16[2,192,256]{2,1,0:T(8,128)(2,1)} %down.7), channel_id=1, source_target_pairs={{0,1},{3,2},{4,5},{7,6},{8,9},{11,10},{12,13},{15,14},{16,17},{19,... | collective-permute-start | bytes 589832 | tf_op jit(solution)/shard_map/ppermute | solution.py:173
  608.6 213.6 %collective-permute-start.124 = (bf16[4,1408,256]{2,1,0:T(8,128)(2,1)}, bf16[4,1408,256]{2,1,0:T(8,128)(2,1)}, u32[]{:S(2)}, u32[]{:S(2)}) collective-permute-start(bf16[4,1408,256]{2,1,0:T(8,128)(2,1)} %dwout.2), channel_id=1, source_target_pairs={{0,4},{4,0},{8,12},{12,8},{16,20},{20,16},{24,28},{28,24},{1,5},{5... | collective-permute-start | bytes 8650760 | tf_op jit(solution)/shard_map/ppermute | solution.py:151
  617.6 19.3 %collective-permute-start.65 = (bf16[2,192,256]{2,1,0:T(8,128)(2,1)S(1)}, bf16[2,192,256]{2,1,0:T(8,128)(2,1)S(1)}, u32[]{:S(2)}, u32[]{:S(2)}) collective-permute-start(bf16[2,192,256]{2,1,0:T(8,128)(2,1)S(1)} %add_convert_fusion.24), channel_id=1, source_target_pairs={{1,0},{2,3},{5,4},{6,7},{9,8},{10,11},{13,12},{14,15},{17,16},{18,... | collective-permute-start | bytes 589832 | tf_op jit(solution)/shard_map/ppermute | solution.py:177
  619.9 15.4 %collective-permute-start.110 = (f32[8,768]{1,0:T(8,128)S(1)}, f32[8,768]{1,0:T(8,128)S(1)}, u32[]{:S(2)}, u32[]{:S(2)}) collective-permute-start(f32[8,768]{1,0:T(8,128)S(1)} %add.751), channel_id=1, source_target_pairs={{0,16},{4,20},{8,24},{12,28},{16,0},{20,4},{24,8},{28,12},{1,17},{... | collective-permute-start | bytes 73736 | tf_op jit(solution)/shard_map/ppermute | solution.py:147
  653.3 15.2 %collective-permute-start.92 = (bf16[768,256]{1,0:T(8,128)(2,1)S(1)}, bf16[768,256]{1,0:T(8,128)(2,1)S(1)}, u32[]{:S(2)}, u32[]{:S(2)}) collective-permute-start(bf16[768,256]{1,0:T(8,128)(2,1)S(1)} %collective-permute-done.90.refs_1_), channel_id=1, source_target_pairs={{0,16},{4,20},{8,24},{12,28},{16,0},{20,4},{24,8},{28,12},{1,17},{... | collective-permute-start | bytes 1179656 | tf_op jit(solution)/shard_map/ppermute | solution.py:147
  662.5 183.9 %collective-permute-start.123 = (bf16[4,2,256,1408]{3,2,1,0:T(8,128)(2,1)}, bf16[4,2,256,1408]{3,2,1,0:T(8,128)(2,1)}, u32[]{:S(2)}, u32[]{:S(2)}) collective-permute-start(bf16[4,2,256,1408]{3,2,1,0:T(8,128)(2,1)} %dwin.2), channel_id=1, source_target_pairs={{0,4},{4,0},{8,12},{12,8},{16,20},{20,16},{24,28},{28,24},{1,5},{5... | collective-permute-start | bytes 17301512 | tf_op jit(solution)/shard_map/ppermute | solution.py:151
  662.5 82.9 %collective-permute-start.66 = (bf16[768,256]{1,0:T(8,128)(2,1)}, bf16[768,256]{1,0:T(8,128)(2,1)}, u32[]{:S(2)}, u32[]{:S(2)}) collective-permute-start(bf16[768,256]{1,0:T(8,128)(2,1)} %get-tuple-element.214), channel_id=1, source_target_pairs={{0,4},{4,0},{8,12},{12,8},{16,20},{20,16},{24,28},{28,24},{1,5},{5... | collective-permute-start | bytes 1179656 | tf_op jit(solution)/shard_map/ppermute | solution.py:151
  674.0 18.9 %collective-permute-start.97 = (bf16[2,192,256]{2,1,0:T(8,128)(2,1)}, bf16[2,192,256]{2,1,0:T(8,128)(2,1)S(1)}, u32[]{:S(2)}, u32[]{:S(2)}) collective-permute-start(bf16[2,192,256]{2,1,0:T(8,128)(2,1)} %dattn.4), channel_id=1, source_target_pairs={{0,1},{3,2},{4,5},{7,6},{8,9},{11,10},{12,13},{15,14},{16,17},{19,... | collective-permute-start | bytes 589832 | tf_op jit(solution)/shard_map/ppermute | solution.py:173
  702.5 21.2 %collective-permute-start.99 = (bf16[2,192,256]{2,1,0:T(8,128)(2,1)S(1)}, bf16[2,192,256]{2,1,0:T(8,128)(2,1)S(1)}, u32[]{:S(2)}, u32[]{:S(2)}) collective-permute-start(bf16[2,192,256]{2,1,0:T(8,128)(2,1)S(1)} %add_convert_fusion.12), channel_id=1, source_target_pairs={{1,0},{2,3},{5,4},{6,7},{9,8},{10,11},{13,12},{14,15},{17,16},{18,... | collective-permute-start | bytes 589832 | tf_op jit(solution)/shard_map/ppermute | solution.py:177
  703.9 24.1 %collective-permute-start.102 = (bf16[2,192,256]{2,1,0:T(8,128)(2,1)S(1)}, bf16[2,192,256]{2,1,0:T(8,128)(2,1)S(1)}, u32[]{:S(2)}, u32[]{:S(2)}) collective-permute-start(bf16[2,192,256]{2,1,0:T(8,128)(2,1)S(1)} %add_convert_fusion.10), channel_id=1, source_target_pairs={{1,0},{2,3},{5,4},{6,7},{9,8},{10,11},{13,12},{14,15},{17,16},{18,... | collective-permute-start | bytes 589832 | tf_op jit(solution)/shard_map/ppermute | solution.py:177
  744.8 28.7 %collective-permute-start.120 = (f32[5,8,256]{2,1,0:T(8,128)S(1)}, f32[5,8,256]{2,1,0:T(8,128)S(1)}, u32[]{:S(2)}, u32[]{:S(2)}) collective-permute-start(f32[5,8,256]{2,1,0:T(8,128)S(1)} %dynamic_update_slice.15), channel_id=1, source_target_pairs={{0,4},{4,0},{8,12},{12,8},{16,20},{20,16},{24,28},{28,24},{1,5},{5... | collective-permute-start | bytes 122888 | tf_op jit(solution)/shard_map/ppermute | solution.py:688
  769.1 35.0 %all-to-all-start.3 = ((bf16[8,256,256]{2,1,0:T(8,128)(2,1)}), bf16[8,256,256]{2,1,0:T(8,128)(2,1)S(1)}, u32[]{:S(2)}, u32[]{:S(2)}) async-start(bf16[8,256,256]{2,1,0:T(8,128)(2,1)} %get-tuple-element.248), calls=%async_computation.3 | async-start | bytes 2097152 | tf_op jit(solution)/shard_map/all_to_all | solution.py:1054
  773.6 15.3 %collective-permute-start.121 = (f32[5,8,256]{2,1,0:T(8,128)S(1)}, f32[5,8,256]{2,1,0:T(8,128)S(1)}, u32[]{:S(2)}, u32[]{:S(2)}) collective-permute-start(f32[5,8,256]{2,1,0:T(8,128)S(1)} %add.768), channel_id=1, source_target_pairs={{0,8},{4,12},{8,0},{12,4},{16,24},{20,28},{24,16},{28,20},{1,9},{5... | collective-permute-start | bytes 122888 | tf_op jit(solution)/shard_map/ppermute | solution.py:688
  782.1 29.2 %collective-permute-start.119 = (bf16[4,512,256]{2,1,0:T(8,128)(2,1)}, bf16[4,512,256]{2,1,0:T(8,128)(2,1)}, u32[]{:S(2)}, u32[]{:S(2)}) collective-permute-start(bf16[4,512,256]{2,1,0:T(8,128)(2,1)} %dwproj.2), channel_id=1, source_target_pairs={{0,4},{4,0},{8,12},{12,8},{16,20},{20,16},{24,28},{28,24},{1,5},{5... | collective-permute-start | bytes 3145736 | tf_op jit(solution)/shard_map/ppermute | solution.py:151
  800.8 31.1 %collective-permute-start.117 = (bf16[4,256,512]{2,1,0:T(8,128)(2,1)}, bf16[4,256,512]{2,1,0:T(8,128)(2,1)S(1)}, u32[]{:S(2)}, u32[]{:S(2)}) collective-permute-start(bf16[4,256,512]{2,1,0:T(8,128)(2,1)} %get-tuple-element.126), channel_id=1, source_target_pairs={{0,4},{4,0},{8,12},{12,8},{16,20},{20,16},{24,28},{28,24},{1,5},{5... | collective-permute-start | bytes 3145736 | tf_op jit(solution)/shard_map/ppermute | solution.py:151
  804.1 40.3 %all-to-all-start.2 = ((bf16[8,256,256]{2,1,0:T(8,128)(2,1)}), bf16[8,256,256]{2,1,0:T(8,128)(2,1)S(1)}, u32[]{:S(2)}, u32[]{:S(2)}) async-start(bf16[8,256,256]{2,1,0:T(8,128)(2,1)} %get-tuple-element.249), calls=%async_computation.2 | async-start | bytes 2097152 | tf_op jit(solution)/shard_map/all_to_all | solution.py:1054
  (154 other events, 1358.2 us)

commit v2 on v1

--- a/solution.py
+++ b/solution.py
@@ -140,7 +140,20 @@
     z = lax.axis_index("tensor")
     g = index // parts
     c = index % parts
-    meta = jnp.stack([g, c, g, g ^ 1, g ^ 2, g ^ 3]).astype(jnp.int32)
+    mine = ((z == 1) | (z == 2)).astype(jnp.int32)
+    theirs = 1 - mine
+    spots = [g, c, g, g ^ 1, g ^ 2, g ^ 3, mine, theirs]
+    spots += [g ^ mine, g ^ theirs, g ^ (2 + mine), g ^ (2 + theirs)]
+    spots += [g ^ (2 * mine), g ^ (2 * mine + 1), g ^ (2 * theirs), g ^ (2 * theirs + 1)]
+    spots += [mine, theirs, 2 + mine, 2 + theirs]
+    meta = jnp.stack(spots).astype(jnp.int32)
+    BY_CHUNK, BY_HALF, IN_ORDER = 8, 12, 16
+
+    def after(value, *others):
+        return lax.optimization_barrier((value,) + others)[0]
+
+    def both(a, b):
+        return (a.astype(F32) + b.astype(F32)).astype(BF16)
 
     def by_group(value, mask):
         pairs = [(a, ((a // parts) ^ mask) * parts + a % parts) for a in range(dp)]
@@ -169,21 +182,18 @@
         value = value + by_z(value, 1)
         return value + by_z(value, 3)
 
-    def wide_sum_z(value):
-        inner = lax.ppermute(value, "tensor", [(0, 1), (3, 2)])
-        value = (value.astype(F32) + inner.astype(F32)).astype(BF16)
-        other = lax.ppermute(value, "tensor", [(1, 2), (2, 1)])
-        value = (value.astype(F32) + other.astype(F32)).astype(BF16)
-        outer = lax.ppermute(value, "tensor", [(1, 0), (2, 3)])
-        return jnp.where((z == 1) | (z == 2), value, outer)
+    def wide_sum_z(keep, send):
+        half = both(keep, by_z(send, 1))
+        half = both(half, by_z(half, 3))
+        return half, by_z(half, 1)
 
     def reduce_groups(first, second):
         ra = by_group(first[3], 1)
         rb = by_group(second[3], 2)
         ax = by_group(first[1], 1)
         by = by_group(second[2], 2)
-        ay = by_group((first[2].astype(F32) + ra.astype(F32)).astype(BF16), 2)
-        bx = by_group((second[1].astype(F32) + rb.astype(F32)).astype(BF16), 1)
+        ay = by_group(both(first[2], ra), 2)
+        bx = by_group(both(second[1], rb), 1)
         return (first[0], ax, ay), (second[0], bx, by)
 
     def gather_groups(first, second):
@@ -194,6 +204,23 @@
 
     def row_of(offset):
         return lambda *a: (a[-1][2 + offset], 0)
+
+    def at_row(m, spot, count):
+        return pl.ds(pl.multiple_of(m[spot] * count, count), count)
+
+    wide = ds % 128 == 0
+
+    def nn_pieces(x, weights):
+        if not wide:
+            return [nn(x, w) for w in weights]
+        value = nn(x, jnp.concatenate(weights, axis=1))
+        return [value[:, s * ds : (s + 1) * ds] for s in pieces]
+
+    def nt_pieces(x, weights):
+        if not wide:
+            return [nt(x, w) for w in weights]
+        value = nt(x, jnp.concatenate(weights, axis=0))
+        return [value[:, s * ds : (s + 1) * ds] for s in pieces]
 
     ends = jnp.cumsum(lengths)
     starts = ends - lengths
@@ -276,28 +303,38 @@
         flat = jnp.stack([rms, low_gate, high_gate, gap, zero, zero, zero, zero])
         return flat, flat.T
 
+    def rows_pair(refs):
+        return jnp.concatenate([ref[...] for ref in refs], axis=0)
+
     def dhidden_body(m, *refs):
-        d_refs, w_refs = refs[:parts], refs[parts : 2 * parts]
-        sel_ref, a_ref, b_ref = refs[2 * parts :]
+        d_refs = refs[: 2 * parts]
+        w_refs, sel_refs = refs[2 * parts : 3 * parts], refs[3 * parts : 3 * parts + 2]
+        outs = refs[3 * parts + 2 :]
+        ids = rows_pair(sel_refs)
+        rows_of = [rows_pair(d_refs[2 * s : 2 * s + 2]) for s in pieces]
         products = []
         for e in range(experts):
-            products.append(sum(nt(d_refs[s][...], w_refs[s][e]) for s in pieces))
-        low, high = two_slots(sel_ref[:, 2:3], sel_ref[:, 3:4], products)
-        a_ref[...] = low.astype(BF16)
-        b_ref[...] = high.astype(BF16)
-
-    def dhidden(r):
-        ins = [(d, (blk, ds), row_of(r)) for d in d_pieces]
+            products.append(sum(nt(rows_of[s], w_refs[s][e]) for s in pieces))
+        low, high = two_slots(ids[:, 2:3], ids[:, 3:4], products)
+        low, high = low.astype(BF16), high.astype(BF16)
+        for step, pair in enumerate(((3, 1), (2, 0))):
+
+            @pl.when(pl.program_id(0) == step)
+            def _():
+                for k, r in enumerate(pair):
+                    outs[2 * r][...] = low[k * blk : (k + 1) * blk]
+                    outs[2 * r + 1][...] = high[k * blk : (k + 1) * blk]
+
+    def dhidden(meta):
+        spots = [lambda i, m: (m[5 - i], 0), lambda i, m: (m[3 - i], 0)]
+        ins = [(d, (blk, ds), spot) for d in d_pieces for spot in spots]
         ins += [(w, None, None) for w in wo]
-        ins += [(sel, (blk, 8), row_of(r))]
-        outs = [((blk, ff), BF16, None, None)] * 2
+        ins += [(sel, (blk, 8), spot) for spot in spots]
+        outs = [((blk, ff), BF16, None, None)] * 8
         return run(
-            dhidden_body, "dhidden", (1,), meta, ins, outs,
-            flops=2 * blk * experts * parts * ds * ff,
-        )
-
-    dh = [dhidden(r) for r in range(4)]
-    dh_a, dh_b = reduce_groups([v[0] for v in dh], [v[1] for v in dh])
+            dhidden_body, "dhidden", (2,), meta, ins, outs,
+            flops=2 * rp * experts * parts * ds * ff,
+        )
 
     tile = 256
 
@@ -345,7 +382,9 @@
         [pltpu.VMEM((heads, tile, 4 * HD), BF16)],
         flops=2 * rp * (experts + 2) * parts * ds * hw,
     )
+    dh = dhidden(after(meta, qkv[8]))
     q_sum, kv_sum = reduce_groups(qkv[0:8:2], qkv[1:8:2])
+    dh_a, dh_b = reduce_groups(dh[0:8:2], dh[1:8:2])
     stats_a = sum_groups(qkv[8])
     flat_a, cols_a = gate_columns(stats_a, low_a, high_a)
 
@@ -409,48 +448,58 @@
     )
     gm_a, gm_b = gather_groups(gated_a, gated_b)
 
-    chunks = 4
-    zr = rp // chunks
+    chunks = 2
+    zr = rp // chunks // 2
+    hold = [((parts, zr, ds), BF16, None, None)] * 2
+
+    def store_halves(i, refs, s, value):
+        @pl.when(i == 0)
+        def _():
+            refs[1][s] = value
+
+        @pl.when(i == 1)
+        def _():
+            refs[0][s] = value
 
     def proj_body(m, *refs):
         a_refs, b_refs = refs[:4], refs[4:8]
         sel_ref = refs[8]
         w_refs = refs[9 : 9 + parts]
-        out_ref, lo, hi = refs[9 + parts :]
+        outs, xs = refs[9 + parts : 11 + parts], refs[11 + parts]
         for r in range(4):
             lanes = pl.ds(pl.multiple_of(m[2 + r] * HD, HD), HD)
-            lo[:, lanes] = a_refs[r][...]
-            hi[:, lanes] = b_refs[r][...]
-        acc = [None] * parts
-        for e in range(experts):
-            x = pick(sel_ref[:, 0:1], sel_ref[:, 1:2], e, lo[...], hi[...])
-            for s in pieces:
-                term = nn(x, w_refs[s][e])
-                acc[s] = term if e == 0 else acc[s] + term
+            for e in range(experts):
+                xs[e, :, lanes] = pick(
+                    sel_ref[:, 0:1], sel_ref[:, 1:2], e, a_refs[r][...], b_refs[r][...]
+                )
+        acc = nn_pieces(xs[0], [w[0] for w in w_refs])
+        for e in range(1, experts):
+            for s, value in enumerate(nn_pieces(xs[e], [w[e] for w in w_refs])):
+                acc[s] += value
         for s in pieces:
-            out_ref[s] = acc[s].astype(BF16)
+            store_halves(pl.program_id(0), outs, s, acc[s].astype(BF16))
 
     def project(k):
-        at_chunk = lambda i, m: (k, 0)
-        ins = [(v, (zr, HD), at_chunk) for v in gm_a + gm_b]
-        ins += [(sel, (zr, 8), at_chunk)]
+        half = lambda i, m: (2 * k + m[7 - i], 0)
+        ins = [(v, (zr, HD), half) for v in gm_a + gm_b]
+        ins += [(sel, (zr, 8), half)]
         ins += [(w, None, None) for w in wp]
         return run(
-            proj_body, "proj", (1,), meta, ins, [((parts, zr, ds), BF16, None, None)],
-            [pltpu.VMEM((zr, hw), BF16)] * 2,
-            flops=2 * zr * experts * hw * parts * ds,
-        )[0]
-
-    attn_totals = [wide_sum_z(project(k)) for k in range(chunks)]
+            proj_body, "proj", (2,), meta, ins, hold,
+            [pltpu.VMEM((experts, zr, hw), BF16)],
+            flops=4 * zr * experts * hw * parts * ds,
+        )
+
+    attn_totals = [half for k in range(chunks) for half in wide_sum_z(*project(k))]
 
     def norm_body(m, *refs):
-        t_refs = refs[:chunks]
-        x_refs = refs[chunks : chunks + parts]
-        gain_ref, router_ref, after_ref, u_ref, stats_ref = refs[chunks + parts :]
-        for k in range(chunks):
-            span_k = slice(k * zr, (k + 1) * zr)
+        t_refs = refs[: 2 * chunks]
+        x_refs = refs[2 * chunks : 2 * chunks + parts]
+        gain_ref, router_ref, after_ref, u_ref, stats_ref = refs[2 * chunks + parts :]
+        for k in range(2 * chunks):
+            span_k = at_row(m, IN_ORDER + k, zr)
             for s in pieces:
-                after_ref[s, span_k] = x_refs[s][span_k, :].astype(F32) + t_refs[k][s].astype(F32)
+                after_ref[s, span_k, :] = x_refs[s][span_k, :].astype(F32) + t_refs[k][s].astype(F32)
         logits = jnp.zeros((8, rp), F32)
         squares = jnp.zeros((8, rp), F32)
         for s in pieces:
@@ -469,52 +518,55 @@
         ((parts, rp, ds), BF16, None, None),
         ((8, rp), F32, None, None),
     ]
-    after, u_f, stats_part = run(norm_body, "norm", (1,), meta, ins, outs)
+    after_rows, u_f, stats_part = run(norm_body, "norm", (1,), meta, ins, outs)
     stats_f = sum_groups(stats_part)
     flat_f, cols_f = gate_columns(stats_f, low_f, high_f)
 
     def up_body(m, *refs):
-        u_ref = refs[0]
-        w_refs = refs[1 : 1 + parts]
-        sel_ref, a_ref, b_ref = refs[1 + parts :]
+        u_refs, w_refs = refs[:2], refs[2 : 2 + parts]
+        sel_refs = refs[2 + parts : 4 + parts]
+        outs = refs[4 + parts :]
+        ids = rows_pair(sel_refs)
+        rows_of = [jnp.concatenate([u[s] for u in u_refs], axis=0) for s in pieces]
         products = []
         for e in range(experts):
-            products.append(sum(nn(u_ref[s], w_refs[s][e, 0]) for s in pieces))
-        low, high = two_slots(sel_ref[:, 2:3], sel_ref[:, 3:4], products)
-        a_ref[0] = low.astype(BF16)
-        b_ref[0] = high.astype(BF16)
-
-    def up(r):
-        ins = [(u_f, (parts, blk, ds), lambda j, m: (0, m[2 + r], 0))]
+            products.append(sum(nn(rows_of[s], w_refs[s][e, 0]) for s in pieces))
+        low, high = two_slots(ids[:, 2:3], ids[:, 3:4], products)
+        low, high = low.astype(BF16), high.astype(BF16)
+        for k in range(2):
+            outs[2 * k][0] = low[k * blk : (k + 1) * blk]
+            outs[2 * k + 1][0] = high[k * blk : (k + 1) * blk]
+
+    def up(pair, meta):
+        def block_of(r):
+            return lambda j, m: (0, m[2 + r], 0)
+
+        ins = [(u_f, (parts, blk, ds), block_of(r)) for r in pair]
         ins += [(w, (experts, 1, ds, ff), lambda j, m: (0, j, 0, 0)) for w in wi]
-        ins += [(sel, (blk, 8), row_of(r))]
-        outs = [((2, blk, ff), BF16, (1, blk, ff), lambda j, m: (j, 0, 0))] * 2
+        ins += [(sel, (blk, 8), row_of(r)) for r in pair]
+        outs = [((2, blk, ff), BF16, (1, blk, ff), lambda j, m: (j, 0, 0))] * 4
         return run(
-            up_body, "up", (2,), meta, ins, outs, flops=4 * blk * experts * parts * ds * ff
-        )
-
-    ups = [None] * 4
-    for r in (3, 1, 2, 0):
-        ups[r] = up(r)
-    gu_a, gu_b = reduce_groups([v[0] for v in ups], [v[1] for v in ups])
-
-    ft = HD
+            up_body, "up", (2,), meta, ins, outs, flops=8 * blk * experts * parts * ds * ff
+        )
+
+    up_far = up((3, 1), meta)
+    up_near = up((2, 0), after(meta, up_far[0]))
+    gu_a, gu_b = reduce_groups(
+        (up_near[2], up_far[2], up_near[0], up_far[0]),
+        (up_near[3], up_far[3], up_near[1], up_far[1]),
+    )
+
+    mt_rows = blk // 3
 
     def mid_body(m, *refs):
         gu = (refs[0:3], refs[3:6])
         dhr = (refs[6:9], refs[9:12])
         cols = refs[12]
-        outs, dots = refs[13:15], refs[15]
-        j = pl.program_id(0)
-
-        @pl.when(j == 0)
-        def _():
-            dots[...] = jnp.zeros_like(dots)
-
+        acts, grads, dots = refs[13:15], refs[15:17], refs[17]
         rms = cols[:, 0:1]
-        line = lax.broadcasted_iota(jnp.int32, (8, blk), 0)
-        inner = jnp.zeros((blk, ft), F32)
+        column = lax.broadcasted_iota(jnp.int32, (mt_rows, 8), 1)
         found = []
+        inner = jnp.zeros((mt_rows, 1), F32)
         for k in range(2):
             gate = cols[:, 1 + k : 2 + k]
             gp = sum(v[0].astype(F32) for v in gu[k]) * rms
@@ -525,23 +577,31 @@
             grad = raw * gate
             dgp = (grad * up_pre * sg * (1.0 + gp * (1.0 - sg))).astype(BF16)
             dup = (grad * gp * sg).astype(BF16)
-            outs[k][0] = (act * gate).astype(BF16)
-            outs[k][1] = dgp
-            outs[k][2] = dup
-            found.append(act * raw)
-            inner += dgp.astype(F32) * gp + dup.astype(F32) * up_pre
-        sums = jnp.where(
-            line == 0, lane_sums(found[0]), jnp.where(line == 1, lane_sums(found[1]), lane_sums(inner))
-        )
-        dots[...] += sums
-
-    ins = [(v, (2, blk, ft), lambda j, m: (0, 0, j)) for v in gu_a + gu_b]
-    ins += [(v, (blk, ft), lambda j, m: (0, j)) for v in dh_a + dh_b]
-    ins += [(cols_f, (blk, 8), row_of(0))]
-    outs = [((3, blk, ff), BF16, (3, blk, ft), lambda j, m: (0, 0, j))] * 2
-    outs += [((8, blk), F32, None, None)]
-    act_a, act_b, dots_f = run(mid_body, "mid", (ff // ft,), meta, ins, outs)
-    ag_a, ag_b = gather_groups(act_a, act_b)
+            acts[k][...] = (act * gate).astype(BF16)
+            grads[k][0] = dgp
+            grads[k][1] = dup
+            found.append(jnp.sum(act * raw, axis=1, keepdims=True))
+            inner += jnp.sum(
+                dgp.astype(F32) * gp + dup.astype(F32) * up_pre, axis=1, keepdims=True
+            )
+        zero = jnp.zeros((mt_rows, 8), F32)
+        for k, value in enumerate(found + [inner]):
+            zero = jnp.where(column == k, value, zero)
+        dots[...] = zero
+
+    rows_3 = lambda i, m: (0, i, 0)
+    rows_2 = lambda i, m: (i, 0)
+    ins = [(v, (2, mt_rows, ff), rows_3) for v in gu_a + gu_b]
+    ins += [(v, (mt_rows, ff), rows_2) for v in dh_a + dh_b]
+    ins += [(cols_f, (mt_rows, 8), lambda i, m: (3 * m[2] + i, 0))]
+    outs = [((blk, ff), BF16, (mt_rows, ff), rows_2)] * 2
+    outs += [((2, blk, ff), BF16, (2, mt_rows, ff), rows_3)] * 2
+    outs += [((blk, 8), F32, (mt_rows, 8), rows_2)]
+    act_a, act_b, grad_a, grad_b, dots_f = run(mid_body, "mid", (3,), meta, ins, outs)
+    gg_a, gg_b = gather_groups(grad_a, grad_b)
+    late = after(act_a, gg_a[1], gg_a[2]), after(act_b, gg_b[1], gg_b[2])
+    ag_a, ag_b = gather_groups(*late)
+    dots_f = dots_f.T
 
     dots_f = sum_z(dots_f)
     dots_f = jnp.stack([dots_f, by_group(dots_f, 1), by_group(dots_f, 2), by_group(dots_f, 3)])
@@ -563,70 +623,87 @@
     back_f = back_columns(flat_f, dots_f, low_f, high_f)
 
     def dx_body(m, *refs):
-        a_ref, b_ref = refs[:2]
-        w_refs = refs[2 : 2 + parts]
-        sel_ref, out_ref, acc = refs[2 + parts :]
+        a_refs, b_refs = refs[:2], refs[2:4]
+        w_refs = refs[4 : 4 + parts]
+        sel_refs = refs[4 + parts : 6 + parts]
+        keep_ref, send_ref, acc, xs = refs[6 + parts :]
         e = pl.program_id(0)
         expert = e.astype(F32)
-        gate = pick(sel_ref[:, 2:3], sel_ref[:, 3:4], expert, a_ref[1], b_ref[1])
-        upper = pick(sel_ref[:, 2:3], sel_ref[:, 3:4], expert, a_ref[2], b_ref[2])
 
         @pl.when(e == 0)
         def _():
             acc[...] = jnp.zeros_like(acc)
 
-        for s in pieces:
-            acc[s] += nt(gate, w_refs[s][0, 0]) + nt(upper, w_refs[s][0, 1])
+        for j in range(2):
+            for k in range(2):
+                ids = sel_refs[k]
+                xs[k * blk : (k + 1) * blk, :] = pick(
+                    ids[:, 2:3], ids[:, 3:4], expert, a_refs[k][j], b_refs[k][j]
+                )
+            for s, value in enumerate(nt_pieces(xs[...], [w[0, j] for w in w_refs])):
+                acc[s] += value
 
         @pl.when(e == experts - 1)
         def _():
-            out_ref[...] = acc[...].astype(BF16)
-
-    def dx(r):
-        ins = [(ag_a[r], None, None), (ag_b[r], None, None)]
+            keep_ref[...] = acc[:, at_row(m, 6, blk), :].astype(BF16)
+            send_ref[...] = acc[:, at_row(m, 7, blk), :].astype(BF16)
+
+    def dx(pair, meta):
+        ins = [(v[r], None, None) for v in (gg_a, gg_b) for r in pair]
         ins += [(w, (1, 2, ds, ff), lambda e, m: (e, 0, 0, 0)) for w in wi]
-        ins += [(sel, (blk, 8), row_of(r))]
+        ins += [(sel, (blk, 8), row_of(r)) for r in pair]
         return run(
-            dx_body, "dx", (experts,), meta, ins, [((parts, blk, ds), BF16, None, None)],
-            [pltpu.VMEM((parts, blk, ds), F32)], flops=4 * blk * experts * parts * ds * ff,
-        )[0]
-
-    dx_totals = [wide_sum_z(dx(r)) for r in range(4)]
+            dx_body, "dx", (experts,), meta, ins, [((parts, blk, ds), BF16, None, None)] * 2,
+            [pltpu.VMEM((parts, 2 * blk, ds), F32), pltpu.VMEM((2 * blk, ff), BF16)],
+            flops=8 * blk * experts * parts * ds * ff,
+        )
+
+    dx_near = dx((0, 1), meta)
+    dx_far = dx((2, 3), meta)
+    dx_totals = wide_sum_z(*dx_near) + wide_sum_z(*dx_far)
 
     def down_body(m, *refs):
-        a_ref, b_ref = refs[:2]
-        w_refs = refs[2 : 2 + parts]
-        sel_ref, out_ref, acc = refs[2 + parts :]
+        a_refs, b_refs = refs[:4], refs[4:8]
+        w_refs = refs[8 : 8 + parts]
+        sel_refs = refs[8 + parts : 12 + parts]
+        keep_ref, send_ref, acc, xs = refs[12 + parts :]
         e = pl.program_id(0)
-        x = pick(sel_ref[:, 2:3], sel_ref[:, 3:4], e.astype(F32), a_ref[0], b_ref[0])
 
         @pl.when(e == 0)
         def _():
             acc[...] = jnp.zeros_like(acc)
 
-        for s in pieces:
-            acc[s] += nn(x, w_refs[s][0])
+        for r in range(4):
+            ids = sel_refs[r]
+            xs[r * blk : (r + 1) * blk, :] = pick(
+                ids[:, 2:3], ids[:, 3:4], e.astype(F32), a_refs[r][...], b_refs[r][...]
+            )
+        for s, value in enumerate(nn_pieces(xs[...], [w[0] for w in w_refs])):
+            acc[s] += value
 
         @pl.when(e == experts - 1)
         def _():
-            out_ref[...] = acc[...].astype(BF16)
-
-    def down(r):
-        whole = lambda e, m: (0, 0, 0)
-        ins = [(ag_a[r], (1, blk, ff), whole), (ag_b[r], (1, blk, ff), whole)]
+            keep_ref[...] = acc[:, at_row(m, 6, 2 * blk), :].astype(BF16)
+            send_ref[...] = acc[:, at_row(m, 7, 2 * blk), :].astype(BF16)
+
+    def down(meta):
+        ins = [(v, None, None) for v in ag_a + ag_b]
         ins += [(w, (1, ff, ds), lambda e, m: (e, 0, 0)) for w in wo]
-        ins += [(sel, (blk, 8), row_of(r))]
+        ins += [(sel, (blk, 8), row_of(r)) for r in range(4)]
         return run(
-            down_body, "down", (experts,), meta, ins, [((parts, blk, ds), BF16, None, None)],
-            [pltpu.VMEM((parts, blk, ds), F32)], flops=2 * blk * experts * parts * ds * ff,
-        )[0]
+            down_body, "down", (experts,), meta, ins,
+            [((parts, 2 * blk, ds), BF16, None, None)] * 2,
+            [pltpu.VMEM((parts, rp, ds), F32), pltpu.VMEM((rp, ff), BF16)],
+            flops=2 * rp * experts * parts * ds * ff,
+        )
 
     def norm_back_body(low_precision_out, m, *refs):
         t_refs = refs[:4]
         after_ref = refs[4]
-        up_refs = refs[5 : 5 + parts]
-        gain_ref, router_ref, back = refs[5 + parts : 8 + parts]
-        outs = refs[8 + parts :]
+        ups = parts if low_precision_out else 1
+        up_refs = refs[5 : 5 + ups]
+        gain_ref, router_ref, back = refs[5 + ups : 8 + ups]
+        outs = refs[8 + ups :]
         small = outs[-1]
         for s in pieces:
             gain = gain_ref[s]
@@ -634,10 +711,7 @@
             gain_sum = jnp.zeros((1, ds), F32)
             router_sum = [jnp.zeros((1, ds), F32)] * experts
             for r in range(4):
-                if low_precision_out:
-                    span_r = pl.ds(pl.multiple_of(m[2 + r] * blk, blk), blk)
-                else:
-                    span_r = slice(r * blk, (r + 1) * blk)
+                span_r = at_row(m, (BY_CHUNK if low_precision_out else IN_ORDER) + r, blk)
                 up_value = up_refs[s][span_r, :] if low_precision_out else up_refs[0][s, span_r, :]
                 x = after_ref[s, span_r, :].astype(F32)
                 cols = back[span_r, :]
@@ -666,7 +740,7 @@
             small[experts, s] = gain_sum[0]
 
     ins = [(t, None, None) for t in dx_totals]
-    ins += [(after, None, None)] + [(d, None, None) for d in d_pieces]
+    ins += [(after_rows, None, None)] + [(d, None, None) for d in d_pieces]
     ins += [(gain_f, None, None), (router_f, None, None), (back_f, None, None)]
     outs = [
         ((parts, rp, ds), F32, None, None),
@@ -816,32 +890,35 @@
         sel_ref = refs[8]
         q_refs = refs[9 : 9 + parts]
         kv_refs = refs[9 + parts : 9 + 2 * parts]
-        out_ref, lo, hi, dk, dv = refs[9 + 2 * parts :]
+        outs = refs[9 + 2 * parts : 11 + 2 * parts]
+        lo, hi, dk, dv = refs[11 + 2 * parts :]
         place_heads(m, a_refs, lo, hi)
         place_heads(m, b_refs, dk, dv)
-        acc = [nt(dk[...], kv_refs[s][0]) + nt(dv[...], kv_refs[s][1]) for s in pieces]
+        acc = nt_pieces(dk[...], [w[0] for w in kv_refs])
+        for s, value in enumerate(nt_pieces(dv[...], [w[1] for w in kv_refs])):
+            acc[s] += value
         for e in range(experts):
             x = pick(sel_ref[:, 0:1], sel_ref[:, 1:2], e, lo[...], hi[...])
-            for s in pieces:
-                acc[s] += nt(x, q_refs[s][e])
+            for s, value in enumerate(nt_pieces(x, [w[e] for w in q_refs])):
+                acc[s] += value
         for s in pieces:
-            out_ref[s] = acc[s].astype(BF16)
+            store_halves(pl.program_id(0), outs, s, acc[s].astype(BF16))
 
     def dattn(k):
-        at_chunk = lambda i, m: (k, 0)
-        ins = [(v, (zr, 2 * HD), at_chunk) for v in da_a + da_b]
-        ins += [(sel, (zr, 8), at_chunk)]
+        half = lambda i, m: (2 * k + m[7 - i], 0)
+        ins = [(v, (zr, 2 * HD), half) for v in da_a + da_b]
+        ins += [(sel, (zr, 8), half)]
         ins += [(w, None, None) for w in wq + wkv]
         return run(
-            dattn_body, "dattn", (1,), meta, ins, [((parts, zr, ds), BF16, None, None)],
+            dattn_body, "dattn", (2,), meta, ins, hold,
             [pltpu.VMEM((zr, hw), BF16)] * 4,
-            flops=2 * zr * (experts + 2) * hw * parts * ds,
-        )[0]
-
-    da_totals = [wide_sum_z(dattn(k)) for k in range(chunks)]
+            flops=4 * zr * (experts + 2) * hw * parts * ds,
+        )
+
+    da_totals = [half for k in range(chunks) for half in wide_sum_z(*dattn(k))]
     x_stack = jnp.stack(x_pieces)
     ins = [(t, None, None) for t in da_totals]
-    ins += [(x_stack, None, None)] + [(dafter, None, None)] * parts
+    ins += [(x_stack, None, None), (dafter, None, None)]
     ins += [(gain_a, None, None), (router_a, None, None), (back_a, None, None)]
     outs = [((parts, rp, ds), BF16, None, None), ((experts + 1, parts, ds), F32, None, None)]
     dinput, small_a = run(
@@ -849,26 +926,44 @@
     )
     attnrouter_grad, attngain_grad = whole_vectors(small_a)
 
-    def exchange(grad_of):
-        received = [by_part(grad_of(s, None), s) for s in pieces[1:]]
-        return grad_of(0, received)
-
-    ffn_input = (after * flat_f[0][None, :, None] * gain_f).astype(BF16)
+    def exchange(sums):
+        total = sums[0].astype(F32)
+        for s in pieces[1:]:
+            total = total + by_part(sums[s], s).astype(F32)
+        return total
+
+    ffn_input = (after_rows * flat_f[0][None, :, None] * gain_f).astype(BF16)
     attn_input = (x_stack.astype(F32) * flat_a[0][None, :, None] * gain_a).astype(BF16)
 
-    def dwin_body(count, m, *refs):
+    def t_left(xs, value):
+        if not wide:
+            return [tn(x, value) for x in xs]
+        total = tn(jnp.concatenate(xs, axis=1), value)
+        return [total[s * ds : (s + 1) * ds] for s in pieces]
+
+    def t_right(value, xs):
+        if not wide:
+            return [tn(value, x) for x in xs]
+        total = tn(value, jnp.concatenate(xs, axis=1))
+        return [total[:, s * ds : (s + 1) * ds] for s in pieces]
+
+    def sort_rows(m, sel_ref, x_refs, xs, ids):
+        for r in range(4):
+            src, here_r = at_row(m, 2 + r, blk), slice(r * blk, (r + 1) * blk)
+            for s in pieces:
+                xs[s, here_r, :] = x_refs[s][src, :]
+            ids[here_r, :] = sel_ref[src, :]
+
+    def dwin_body(m, *refs):
         a_refs, b_refs = refs[:4], refs[4:8]
         sel_ref, x_ref = refs[8:10]
-        add_refs = refs[10 : 10 + count]
-        out_ref, xs, ids, mt = refs[10 + count :]
+        outs = refs[10 : 10 + parts]
+        xs, ids, mt = refs[10 + parts :]
         j, e = pl.program_id(0), pl.program_id(1)
 
         @pl.when((j == 0) & (e == 0))
         def _():
-            for r in range(4):
-                src = pl.ds(pl.multiple_of(m[2 + r] * blk, blk), blk)
-                xs[r * blk : (r + 1) * blk, :] = x_ref[0, src, :]
-                ids[r * blk : (r + 1) * blk, :] = sel_ref[src, :]
+            sort_rows(m, sel_ref, [x_ref.at[s] for s in pieces], xs, ids)
 
         expert = e.astype(F32)
         for r in range(4):
@@ -876,69 +971,56 @@
             mt[here_r, :] = pick(
                 ids[here_r, 2:3], ids[here_r, 3:4], expert, a_refs[r][0], b_refs[r][0]
             )
-        acc = tn(xs[...], mt[...])
-        for ref in add_refs:
-            acc = acc + ref[0, 0].astype(F32)
-        out_ref[0, 0] = acc.astype(out_ref.dtype)
-
-    def dwin(s, received):
-        adds = received or []
+        for s, value in enumerate(t_left([xs[s] for s in pieces], mt[...])):
+            outs[s][0, 0] = value.astype(BF16)
+
+    def dwin(meta):
         spot = lambda j, e, m: (e, j, 0, 0)
-        ins = [(v, (1, blk, ff), lambda j, e, m: (1 + j, 0, 0)) for v in ag_a + ag_b]
-        ins += [(sel, None, None), (ffn_input, (1, rp, ds), lambda j, e, m: (s, 0, 0))]
-        ins += [(v, (1, 1, ds, ff), spot) for v in adds]
-        dtype = BF16 if received is None else F32
-        outs = [((experts, 2, ds, ff), dtype, (1, 1, ds, ff), spot)]
+        ins = [(v, (1, blk, ff), lambda j, e, m: (j, 0, 0)) for v in gg_a + gg_b]
+        ins += [(sel, None, None), (ffn_input, None, None)]
+        outs = [((experts, 2, ds, ff), BF16, (1, 1, ds, ff), spot)] * parts
         return run(
-            functools.partial(dwin_body, len(adds)), "dwin", (2, experts), meta, ins, outs,
-            [pltpu.VMEM((rp, ds), BF16), pltpu.VMEM((rp, 8), F32), pltpu.VMEM((rp, ff), BF16)],
-            flops=4 * rp * experts * ds * ff,
-        )[0]
-
-    def dwout_body(count, m, *refs):
+            dwin_body, "dwin", (2, experts), meta, ins, outs,
+            [pltpu.VMEM((parts, rp, ds), BF16), pltpu.VMEM((rp, 8), F32), pltpu.VMEM((rp, ff), BF16)],
+            flops=4 * rp * experts * parts * ds * ff,
+        )
+
+    def dwout_body(m, *refs):
         a_refs, b_refs = refs[:4], refs[4:8]
-        sel_ref, d_ref = refs[8:10]
-        add_refs = refs[10 : 10 + count]
-        out_ref, xs, ids, mt = refs[10 + count :]
+        sel_ref, d_refs = refs[8], refs[9 : 9 + parts]
+        outs = refs[9 + parts : 9 + 2 * parts]
+        xs, ids, mt = refs[9 + 2 * parts :]
         e = pl.program_id(0)
 
         @pl.when(e == 0)
         def _():
-            for r in range(4):
-                src = pl.ds(pl.multiple_of(m[2 + r] * blk, blk), blk)
-                xs[r * blk : (r + 1) * blk, :] = d_ref[src, :]
-                ids[r * blk : (r + 1) * blk, :] = sel_ref[src, :]
+            sort_rows(m, sel_ref, d_refs, xs, ids)
 
         expert = e.astype(F32)
         for r in range(4):
             here_r = slice(r * blk, (r + 1) * blk)
             mt[here_r, :] = pick(
-                ids[here_r, 2:3], ids[here_r, 3:4], expert, a_refs[r][0], b_refs[r][0]
+                ids[here_r, 2:3], ids[here_r, 3:4], expert, a_refs[r][...], b_refs[r][...]
             )
-        acc = tn(mt[...], xs[...])
-        for ref in add_refs:
-            acc = acc + ref[0].astype(F32)
-        out_ref[0] = acc.astype(out_ref.dtype)
-
-    def dwout(s, received):
-        adds = received or []
+        for s, value in enumerate(t_right(mt[...], [xs[s] for s in pieces])):
+            outs[s][0] = value.astype(BF16)
+
+    def dwout(meta):
         spot = lambda e, m: (e, 0, 0)
-        ins = [(v, (1, blk, ff), lambda e, m: (0, 0, 0)) for v in ag_a + ag_b]
-        ins += [(sel, None, None), (d_pieces[s], None, None)]
-        ins += [(v, (1, ff, ds), spot) for v in adds]
-        dtype = BF16 if received is None else F32
-        outs = [((experts, ff, ds), dtype, (1, ff, ds), spot)]
+        ins = [(v, None, None) for v in ag_a + ag_b]
+        ins += [(sel, None, None)] + [(d, None, None) for d in d_pieces]
+        outs = [((experts, ff, ds), BF16, (1, ff, ds), spot)] * parts
         return run(
-            functools.partial(dwout_body, len(adds)), "dwout", (experts,), meta, ins, outs,
-            [pltpu.VMEM((rp, ds), BF16), pltpu.VMEM((rp, 8), F32), pltpu.VMEM((rp, ff), BF16)],
-            flops=2 * rp * experts * ds * ff,
-        )[0]
-
-    def dwproj_body(count, m, *refs):
+            dwout_body, "dwout", (experts,), meta, ins, outs,
+            [pltpu.VMEM((parts, rp, ds), BF16), pltpu.VMEM((rp, 8), F32), pltpu.VMEM((rp, ff), BF16)],
+            flops=2 * rp * experts * parts * ds * ff,
+        )
+
+    def dwproj_body(m, *refs):
         a_refs, b_refs = refs[:4], refs[4:8]
         sel_ref, d_ref = refs[8:10]
-        add_refs = refs[10 : 10 + count]
-        out_ref, lo, hi = refs[10 + count :]
+        outs = refs[10 : 10 + parts]
+        lo, hi = refs[10 + parts :]
         e = pl.program_id(0)
 
         @pl.when(e == 0)
@@ -949,31 +1031,26 @@
                 hi[:, lanes] = b_refs[r][...]
 
         x = pick(sel_ref[:, 0:1], sel_ref[:, 1:2], e.astype(F32), lo[...], hi[...])
-        acc = tn(x, d_ref[0])
-        for ref in add_refs:
-            acc = acc + ref[0].astype(F32)
-        out_ref[0] = acc.astype(out_ref.dtype)
-
-    def dwproj(s, received):
-        adds = received or []
-        spot = lambda e, m: (e, 0, 0)
+        for s, value in enumerate(t_right(x, [d_ref[s] for s in pieces])):
+            outs[s][0] = value.astype(BF16)
+
+    def dwproj(meta):
         ins = [(v, None, None) for v in gm_a + gm_b]
-        ins += [(sel, None, None), (dafter_low, (1, rp, ds), lambda e, m: (s, 0, 0))]
-        ins += [(v, (1, hw, ds), spot) for v in adds]
-        dtype = BF16 if received is None else F32
+        ins += [(sel, None, None), (dafter_low, None, None)]
         return run(
-            functools.partial(dwproj_body, len(adds)), "dwproj", (experts,), meta, ins,
-            [((experts, hw, ds), dtype, (1, hw, ds), spot)],
+            dwproj_body, "dwproj", (experts,), meta, ins,
+            [((experts, hw, ds), BF16, (1, hw, ds), lambda e, m: (e, 0, 0))] * parts,
             [pltpu.VMEM((rp, hw), BF16)] * 2,
-            flops=2 * rp * experts * hw * ds,
-        )[0]
-
-    def dwqkv_body(count, m, *refs):
+            flops=2 * rp * experts * hw * parts * ds,
+        )
+
+    def dwqkv_body(m, *refs):
         a_refs, b_refs = refs[:4], refs[4:8]
         sel_ref, x_ref = refs[8:10]
-        add_q, add_kv = refs[10 : 10 + count], refs[10 + count : 10 + 2 * count]
-        q_ref, kv_ref, lo, hi, dk, dv = refs[10 + 2 * count :]
+        q_outs, kv_outs = refs[10 : 10 + parts], refs[10 + parts : 10 + 2 * parts]
+        lo, hi, dk, dv = refs[10 + 2 * parts :]
         e = pl.program_id(0)
+        xs = [x_ref.at[s] for s in pieces]
 
         @pl.when(e == 0)
         def _():
@@ -983,58 +1060,48 @@
         @pl.when(e < experts)
         def _():
             x = pick(sel_ref[:, 0:1], sel_ref[:, 1:2], e.astype(F32), lo[...], hi[...])
-            acc = tn(x_ref[0], x)
-            for ref in add_q:
-                acc = acc + ref[0].astype(F32)
-            q_ref[0] = acc.astype(q_ref.dtype)
+            for s, value in enumerate(t_left([v[...] for v in xs], x)):
+                q_outs[s][0] = value.astype(BF16)
 
         for k, grad in enumerate((dk, dv)):
 
             @pl.when(e == experts + k)
             def _():
-                acc = tn(x_ref[0], grad[...])
-                for ref in add_kv:
-                    acc = acc + ref[0].astype(F32)
-                kv_ref[0] = acc.astype(kv_ref.dtype)
-
-    def dwqkv(s, received):
-        adds_q = [v[0] for v in received or []]
-        adds_kv = [v[1] for v in received or []]
+                for s, value in enumerate(t_left([v[...] for v in xs], grad[...])):
+                    kv_outs[s][0] = value.astype(BF16)
+
+    def dwqkv(meta):
         q_spot = lambda e, m: (jnp.minimum(e, experts - 1), 0, 0)
         kv_spot = lambda e, m: (jnp.maximum(e - experts, 0), 0, 0)
         ins = [(v, None, None) for v in da_a + da_b]
-        ins += [(sel, None, None), (attn_input, (1, rp, ds), lambda e, m: (s, 0, 0))]
-        ins += [(v, (1, ds, hw), q_spot) for v in adds_q]
-        ins += [(v, (1, ds, hw), kv_spot) for v in adds_kv]
-        dtype = BF16 if received is None else F32
-        outs = [
-            ((experts, ds, hw), dtype, (1, ds, hw), q_spot),
-            ((2, ds, hw), dtype, (1, ds, hw), kv_spot),
-        ]
+        ins += [(sel, None, None), (attn_input, None, None)]
+        outs = [((experts, ds, hw), BF16, (1, ds, hw), q_spot)] * parts
+        outs += [((2, ds, hw), BF16, (1, ds, hw), kv_spot)] * parts
         return run(
-            functools.partial(dwqkv_body, len(adds_q)), "dwqkv", (experts + 2,), meta, ins, outs,
+            dwqkv_body, "dwqkv", (experts + 2,), meta, ins, outs,
             [pltpu.VMEM((rp, hw), BF16)] * 4,
-            flops=2 * rp * (experts + 2) * hw * ds,
-        )
-
-    expertout_grad = exchange(dwout)
-    expertin_grad = exchange(dwin).swapaxes(1, 2)
-    proj_grad = exchange(dwproj)
-    sent = [tuple(by_part(v, s) for v in dwqkv(s, None)) for s in pieces[1:]]
-    query_grad, kv_grad = dwqkv(0, sent)
-
-    down_totals = [wide_sum_z(down(r)) for r in range(4)]
+            flops=2 * rp * (experts + 2) * hw * parts * ds,
+        )
+
+    expertin_grad = exchange(dwin(meta)).swapaxes(1, 2)
+    expertout_grad = exchange(dwout(meta))
+    proj_grad = exchange(dwproj(meta))
+    sums = dwqkv(meta)
+    query_grad, kv_grad = exchange(sums[:parts]), exchange(sums[parts:])
+
+    down_totals = wide_sum_z(*down(meta))
 
     def finish_body(m, *refs):
-        t_refs, after_ref, out_ref = refs[:4], refs[4], refs[5]
-        for r in range(4):
-            span_r = pl.ds(pl.multiple_of(m[2 + r] * blk, blk), blk)
+        t_refs, after_ref, out_ref = refs[:2], refs[2], refs[3]
+        for k in range(4):
+            span_k = at_row(m, BY_HALF + k, blk)
             for s in pieces:
-                out_ref[s, span_r, :] = (
-                    after_ref[s, span_r, :] + t_refs[r][s].astype(F32)
+                total = t_refs[k // 2][s, (k % 2) * blk : (k % 2 + 1) * blk, :]
+                out_ref[s, span_k, :] = (
+                    after_ref[s, span_k, :] + total.astype(F32)
                 ).astype(BF16)
 
-    ins = [(t, None, None) for t in down_totals] + [(after, None, None)]
+    ins = [(t, None, None) for t in down_totals] + [(after_rows, None, None)]
     out_rows = run(
         finish_body, "finish", (1,), meta, ins, [((parts, rp, ds), BF16, None, None)]
     )[0]
@@ -1047,10 +1114,29 @@
     cot_row = (inverse.reshape(1, seqs, 1) * seq_len + place).reshape(-1)
     valid = valid.reshape(-1)[:, None]
 
+    found_row = jnp.where(valid, from_row[:, None], -1)
+    ut = rows_all // dp
+
+    def unpack_body(m, at_ref, other_ref, *refs):
+        v_refs, out_ref = refs[:parts], refs[parts]
+        at = at_ref[...]
+        lane = lax.broadcasted_iota(jnp.int32, (ut, rp), 1)
+        total = jnp.zeros((ut, ds), F32)
+        for s in pieces:
+            hot = jnp.where(at - s * rp == lane, 1.0, 0.0).astype(BF16)
+            total += nn(hot, v_refs[s][...])
+        out_ref[...] = jnp.where(at >= 0, total, other_ref[...].astype(F32)).astype(BF16)
+
     def unpack(value, otherwise):
         mine_all = [value[0]] + [by_part(value[s], s) for s in pieces[1:]]
-        spread_rows = jnp.concatenate(mine_all, axis=0)[from_row]
-        spread_rows = jnp.where(valid, spread_rows, otherwise)
+        ins = [(found_row, (ut, 1), lambda i, m: (i, 0))]
+        ins += [(otherwise, (ut, ds), lambda i, m: (i, 0))]
+        ins += [(v, None, None) for v in mine_all]
+        spread_rows = run(
+            unpack_body, "unpack", (dp,), meta, ins,
+            [((rows_all, ds), BF16, (ut, ds), lambda i, m: (i, 0))],
+            flops=2 * rows_all * rp * parts * ds,
+        )[0]
         landed = lax.all_to_all(
             spread_rows.reshape(dp, seqs * per, ds), "dp", 0, 0, tiled=True
         )

time: 898 us -> 751 us (0.84)
  Pallas kernels: 316 us -> 230 us
  starting transfers between devices: 170 us -> 133 us
  local copies, waits for them, and re-layouts: 107 us -> 92.1 us
    ppermute x48 -> x0, waiting for transfers between devices: 106 us -> none  [the longest x16 91.4 us: wide_sum_z(): outer = lax.ppermute(value, 'tensor', [(1, 0), (2, 3)])]
    pallas_call x43 -> x27, Pallas kernels: 316 us -> 230 us  [run(): pl.pallas_call(body, name=name, grid_spec=pltpu.PrefetchScalarGridSpec(nu...]
    ppermute x51 -> x57, waiting for transfers between devices: 115 us -> 189 us  [by_group(): return lax.ppermute(value, 'dp', pairs)]
    ppermute x48 -> x0, starting transfers between devices: 65.1 us -> none  [the longest x16 33.4 us: wide_sum_z(): inner = lax.ppermute(value, 'tensor', [(0, 1), (3, 2)])]
    ppermute x4 -> x25, starting transfers between devices: 6.42 us -> 43.6 us  [by_z(): return lax.ppermute(value, 'tensor', [(a, a ^ mask) for a in range(tp)])]
    ppermute x4 -> x25, waiting for transfers between devices: 1.19 us -> 34.2 us  [by_z(): return lax.ppermute(value, 'tensor', [(a, a ^ mask) for a in range(tp)])]
    gather x2 -> x0, local copies, waits for them, and re-layouts: 18.1 us -> none  [unpack(): spread_rows = jnp.concatenate(mine_all, axis=0)[from_row]]
    add x0 -> x5, other arithmetic: none -> 13.3 us  [the longest x4 12.7 us: exchange(): total = total + by_part(sums[s], s).astype(F32)]
  transfers between devices with their start and end apart: 129 -> 108, of which waited for: 42 -> 40; matrix products, arithmetic and copies ran while one was open for 15% -> 13% of each run, Pallas kernels for 32% -> 30%
where the time goes in v2:
time: 751 us; the launch traced here: 744 us
  waiting for transfers between devices  233 us (31%)
  Pallas kernels  230 us (31%)
  starting transfers between devices  133 us (18%)
  local copies, waits for them, and re-layouts  92.1 us (12%)
  other arithmetic  52.2 us (7%)
    pallas_call x27, Pallas kernels, run(): pl.pallas_call(body, name=name, grid_spec=pltpu.PrefetchScalarGridSpec(nu...  230 us
    ppermute x57, waiting for transfers between devices, by_group(): return lax.ppermute(value, 'dp', pairs)  189 us
    ppermute x57, starting transfers between devices, by_group(): return lax.ppermute(value, 'dp', pairs)  60.9 us
    unnamed x208, local copies, waits for them, and re-layouts  45.1 us
    ppermute x25, starting transfers between devices, by_z(): return lax.ppermute(value, 'tensor', [(a, a ^ mask) for a in range(tp)])  43.6 us
    ppermute x25, waiting for transfers between devices, by_z(): return lax.ppermute(value, 'tensor', [(a, a ^ mask) for a in range(tp)])  34.2 us
  transfers between devices with their start and end apart: 108, of which 40 were waited for; matrix products, arithmetic and copies ran while one was open for 13% of the time, Pallas kernels for 30%

profile of v2, /device:TPU:0, one launch (start us, length us, event | category | flops | bytes accessed | tf_op | source)
XLA Modules:
  0.0 744.3 jit_solution(11230720120502486707)
XLA Ops:
  3.4 5.2 all-to-all-start
  9.7 5.9 copy.202
  30.8 4.7 all-to-all-start.1
  35.5 3.3 gather_fusion.1
  46.5 8.5 %qkv.1 = (bf16[768,256]{1,0:T(8,128)(2,1)}, bf16[768,256]{1,0:T(8,128)(2,1)}, bf16[768,256]{1,0:T(8,128)(2,1)}, bf16[768,256]{1,0:T(8,128)(2,1)}, bf16[768,256]{...) custom-call(s32[20]{0:T(128)} %stack.135.m, ...), custom_call_target="tpu_custom_call" | custom-call | flops 2415919104 | bytes 7137280 | tf_op jit(solution)/shard_map/qkv/pallas_call | solution.py:61
  62.6 7.5 %collective-permute-done.10 = f32[8,768]{1,0:T(8,128)S(1)} collective-permute-done((f32[8,768]{1,0:T(8,128)S(1)}, f32[8,768]{1,0:T(8,128)S(1)}, u32[]{:S(2)}, u32[]{:S(2)}) %collective-permute-start.10) | collective-permute-done | bytes 24608 | tf_op jit(solution)/shard_map/ppermute | solution.py:160
  74.2 8.2 %collective-permute-done.3.a1 = bf16[768,256]{1,0:T(8,128)(2,1)S(1)} collective-permute-done((bf16[768,256]{1,0:T(8,128)(2,1)S(1)}, bf16[768,256]{1,0:T(8,128)(2,1)S(1)}, u32[]{:S(2)}, u32[]{:S(2)}) %collective-permute-start.3) | collective-permute-done | bytes 393248 | tf_op jit(solution)/shard_map/ppermute | solution.py:160
  86.5 6.5 collective-permute-done.5.a2
  95.1 4.7 rope.1
  103.7 8.1 %attend.1 = (bf16[768,128]{1,0:T(8,128)(2,1)}, bf16[768,128]{1,0:T(8,128)(2,1)}, bf16[768,128]{1,0:T(8,128)(2,1)}, bf16[768,128]{1,0:T(8,128)(2,1)}) custom-call(s32[20]{0:T(128)} %stack.135.m, bf16[768,256]{1,0:T(8,128)(2,1)} %get-tuple-element.106.q_ref.refs_0_, bf16[768,256]{1,0:T(8,128)(2,1)} %get-tuple-element.107.kv_ref.refs_1_, ...), custom_call_target="tpu_custom_call" | custom-call | flops 301989888 | bytes 1753088 | tf_op jit(solution)/shard_map/attend/pallas_call | solution.py:61
  121.9 3.6 collective-permute-done.16.refs_6_
  131.9 6.7 proj.2
  141.4 3.3 gather_fusion.2
  147.4 6.7 proj.3
  154.7 3.7 collective-permute-start.20
  158.3 3.3 collective-permute-done.22
  162.6 6.8 collective-permute-start.23
  169.5 4.8 collective-permute-done.23
  177.8 12.0 %dhidden.1 = (bf16[192,1408]{1,0:T(8,128)(2,1)}, bf16[192,1408]{1,0:T(8,128)(2,1)}, bf16[192,1408]{1,0:T(8,128)(2,1)}, bf16[192,1408]{1,0:T(8,128)(2,1)}, bf16[1...) custom-call(s32[20]{0:T(128)} %stack.135.m, ...), custom_call_target="tpu_custom_call" | custom-call | flops 4429185024 | bytes 11714560 | tf_op jit(solution)/shard_map/dhidden/pallas_call | solution.py:61
  191.8 4.4 norm.1
  197.6 10.6 %up.2 = (bf16[2,192,1408]{2,1,0:T(8,128)(2,1)}, bf16[2,192,1408]{2,1,0:T(8,128)(2,1)}, bf16[2,192,1408]{2,1,0:T(8,128)(2,1)}, bf16[2,192,1408]{2,1,0:T(8,128)(2,1)}) custom-call(s32[20]{0:T(128)} %stack.135.m, bf16[2,768,256]{2,1,0:T(8,128)(2,1)} %get-tuple-element.114.refs_0_.refs_1_, bf16[2,768,256]{2,1,0:T(8,128)(2,1)} %get-tuple-element.114.refs_0_.refs_1_, ...), custom_call_target="tpu_custom_call" | custom-call | flops 4429185024 | bytes 17481728 | tf_op jit(solution)/shard_map/up/pallas_call | solution.py:61
  217.8 10.1 %up.3 = (bf16[2,192,1408]{2,1,0:T(8,128)(2,1)}, bf16[2,192,1408]{2,1,0:T(8,128)(2,1)}, bf16[2,192,1408]{2,1,0:T(8,128)(2,1)}, bf16[2,192,1408]{2,1,0:T(8,128)(2,1)}) custom-call(s32[20]{0:T(128)} %stack.135.m, bf16[2,768,256]{2,1,0:T(8,128)(2,1)} %get-tuple-element.114.refs_0_.refs_1_, bf16[2,768,256]{2,1,0:T(8,128)(2,1)} %get-tuple-element.114.refs_0_.refs_1_, ...), custom_call_target="tpu_custom_call" | custom-call | flops 4429185024 | bytes 17481728 | tf_op jit(solution)/shard_map/up/pallas_call | solution.py:61
  227.9 7.2 collective-permute-done.27
  238.3 22.7 %collective-permute-done.29 = bf16[2,192,1408]{2,1,0:T(8,128)(2,1)S(1)} collective-permute-done((bf16[2,192,1408]{2,1,0:T(8,128)(2,1)}, bf16[2,192,1408]{2,1,0:T(8,128)(2,1)S(1)}, u32[]{:S(2)}, u32[]{:S(2)}) %collective-permute-start.29) | collective-permute-done | bytes 1081376 | tf_op jit(solution)/shard_map/ppermute | solution.py:160
  268.4 4.3 collective-permute-done.36.refs_8_
  274.9 42.3 %collective-permute-done.38.refs_10_ = bf16[192,1408]{1,0:T(8,128)(2,1)} collective-permute-done((bf16[192,1408]{1,0:T(8,128)(2,1)}, bf16[192,1408]{1,0:T(8,128)(2,1)}, u32[]{:S(2)}, u32[]{:S(2)}) %collective-permute-start.38) | collective-permute-done | bytes 540704 | tf_op jit(solution)/shard_map/ppermute | solution.py:160
  318.6 8.2 %mid.1 = (bf16[192,1408]{1,0:T(8,128)(2,1)}, bf16[192,1408]{1,0:T(8,128)(2,1)}, bf16[2,192,1408]{2,1,0:T(8,128)(2,1)}, bf16[2,192,1408]{2,1,0:T(8,128)(2,1)}, f32[192,8]{1,0:T(8,128)}) custom-call(s32[20]{0:T(128)} %stack.135.m, bf16[2,192,1408]{2,1,0:T(8,128)(2,1)} %get-tuple-element.117.refs_0_, bf16[2,192,1408]{2,1,0:T(8,128)(2,1)} %copy-done.15, ...), custom_call_target="tpu_custom_call" | custom-call | bytes 13006848 | tf_op jit(solution)/shard_map/mid/pallas_call | solution.py:61
  327.6 9.0 %gather_fusion.4 = bf16[2048,256]{1,0:T(8,128)(2,1)} fusion(bf16[2048,256]{1,0:T(8,128)(2,1)S(1)} %bitcast.111, s32[2048]{0:T(1024)S(1)} %broadcast_clamp_fusion), kind=kCustom, calls=%fused_computation.4 | custom fusion | bytes 2105344 | tf_op jit(solution)/shard_map/gather | solution.py:1146
  347.8 16.7 %collective-permute-done.68 = f32[8,192]{0,1:T(8,128)S(1)} collective-permute-done((f32[8,192]{0,1:T(8,128)S(1)}, f32[8,192]{0,1:T(8,128)S(1)}, u32[]{:S(2)}, u32[]{:S(2)}) %collective-permute-start.68) | collective-permute-done | bytes 6176 | tf_op jit(solution)/shard_map/ppermute | solution.py:160
  365.0 5.2 collective-permute-done.67
  372.5 15.4 %collective-permute-done.66 = f32[8,192]{0,1:T(8,128)S(1)} collective-permute-done((f32[8,192]{0,1:T(8,128)S(1)}, f32[8,192]{0,1:T(8,128)S(1)}, u32[]{:S(2)}, u32[]{:S(2)}) %collective-permute-start.66) | collective-permute-done | bytes 6176 | tf_op jit(solution)/shard_map/ppermute | solution.py:160
  393.8 11.3 %dx.2 = (bf16[2,192,256]{2,1,0:T(8,128)(2,1)}, bf16[2,192,256]{2,1,0:T(8,128)(2,1)}) custom-call(s32[20]{0:T(128)} %stack.135.m, bf16[2,192,1408]{2,1,0:T(8,128)(2,1)} %get-tuple-element.135.refs_0_, bf16[2,192,1408]{2,1,0:T(8,128)(2,1)} %collective-permute-done.42.refs_1_, bf16[2,192,1408]{2,1,0:T(8,128)(2,1)} %get-tuple-element.138.refs_2_.refs_4_, ...), custom_call_target="tpu_custom_call" | custom-call | flops 4429185024 | bytes 16302080 | tf_op jit(solution)/shard_map/dx/pallas_call | solution.py:61
  413.4 12.6 %collective-permute-done.44.refs_1_ = bf16[192,1408]{1,0:T(8,128)(2,1)S(1)} collective-permute-done((bf16[192,1408]{1,0:T(8,128)(2,1)S(1)}, bf16[192,1408]{1,0:T(8,128)(2,1)S(1)}, u32[]{:S(2)}, u32[]{:S(2)}) %collective-permute-start.44) | collective-permute-done | bytes 540704 | tf_op jit(solution)/shard_map/ppermute | solution.py:160
  427.6 3.4 collective-permute-start.57
  433.1 11.0 %dx.3 = (bf16[2,192,256]{2,1,0:T(8,128)(2,1)}, bf16[2,192,256]{2,1,0:T(8,128)(2,1)}) custom-call(s32[20]{0:T(128)} %stack.135.m, bf16[2,192,1408]{2,1,0:T(8,128)(2,1)} %collective-permute-done.43.refs_0_.refs_2_, bf16[2,192,1408]{2,1,0:T(8,128)(2,1)} %collective-permute-done.59.refs_1_.refs_3_, ...), custom_call_target="tpu_custom_call" | custom-call | flops 4429185024 | bytes 16302080 | tf_op jit(solution)/shard_map/dx/pallas_call | solution.py:61
  444.3 5.8 collective-permute-done.61
  452.8 10.8 %down.1 = (bf16[2,384,256]{2,1,0:T(8,128)(2,1)}, bf16[2,384,256]{2,1,0:T(8,128)(2,1)}) custom-call(s32[20]{0:T(128)} %stack.135.m, bf16[192,1408]{1,0:T(8,128)(2,1)} %get-tuple-element.136.refs_0_, bf16[192,1408]{1,0:T(8,128)(2,1)} %copy-done.91, bf16[192,1408]{1,0:T(8,128)(2,1)} %copy-done.92, bf16[192,1408]{1,0:T(8,128)(2,1)} %collective-permute-done.46.refs_3_, ...), custom_call_target="tpu_custom_call" | custom-call | flops 4429185024 | bytes 10977280 | tf_op jit(solution)/shard_map/down/pallas_call | solution.py:61
  465.8 19.3 %dwin.1 = (bf16[4,2,256,1408]{3,2,1,0:T(8,128)(2,1)}, bf16[4,2,256,1408]{3,2,1,0:T(8,128)(2,1)}) custom-call(s32[20]{0:T(128)} %stack.135.m, bf16[2,192,1408]{2,1,0:T(8,128)(2,1)} %get-tuple-element.135.refs_0_, bf16[2,192,1408]{2,1,0:T(8,128)(2,1)} %collective-permute-done.42.refs_1_, bf16[2,192,1408]{2,1,0:T(8,128)(2,1)} %collective-permute-done.43.refs_0_.refs_2_, ...), custom_call_target="tpu_custom_call" | custom-call | flops 8858370048 | bytes 20996096 | tf_op jit(solution)/shard_map/dwin/pallas_call | solution.py:61
  486.0 6.5 norm_back.1
  492.5 6.1 dmix.1
  502.8 3.8 collective-permute-done.70
  518.2 14.4 %attend_back.1 = (bf16[768,256]{1,0:T(8,128)(2,1)}, f32[768,256]{1,0:T(8,128)}, f32[256,256]{1,0:T(8,128)}, f32[8,768]{1,0:T(8,128)}) custom-call(s32[20]{0:T(128)} %stack.135.m, bf16[768,256]{1,0:T(8,128)(2,1)} %get-tuple-element.106.q_ref.refs_0_, bf16[768,256]{1,0:T(8,128)(2,1)} %get-tuple-element.107.kv_ref.refs_1_, bf16[256,256]{1,0:T(8,128)(2,1)} %copy-done.37, ...), custom_call_target="tpu_custom_call" | custom-call | flops 754974720 | bytes 4792320 | tf_op jit(solution)/shard_map/attend_back/pallas_call | solution.py:61
  533.9 10.9 %dwout.1 = (bf16[4,1408,256]{2,1,0:T(8,128)(2,1)}, bf16[4,1408,256]{2,1,0:T(8,128)(2,1)}) custom-call(s32[20]{0:T(128)} %stack.135.m, bf16[192,1408]{1,0:T(8,128)(2,1)} %get-tuple-element.136.refs_0_, bf16[192,1408]{1,0:T(8,128)(2,1)} %copy-done.91, bf16[192,1408]{1,0:T(8,128)(2,1)} %copy-done.92, bf16[192,1408]{1,0:T(8,128)(2,1)} %collective-permute-done.46.refs_3_, ...), custom_call_target="tpu_custom_call" | custom-call | flops 4429185024 | bytes 10903552 | tf_op jit(solution)/shard_map/dwout/pallas_call | solution.py:61
  545.2 7.5 %dwproj.1 = (bf16[4,512,256]{2,1,0:T(8,128)(2,1)}, bf16[4,512,256]{2,1,0:T(8,128)(2,1)}) custom-call(s32[20]{0:T(128)} %stack.135.m, bf16[768,128]{1,0:T(8,128)(2,1)} %get-tuple-element.108.refs_0_, bf16[768,128]{1,0:T(8,128)(2,1)} %copy-done.21, bf16[768,128]{1,0:T(8,128)(2,1)} %copy-done.22, bf16[768,128]{1,0:T(8,128)(2,1)} %copy-done.25, ...), custom_call_target="tpu_custom_call" | custom-call | flops 1610612736 | bytes 4481024 | tf_op jit(solution)/shard_map/dwproj/pallas_call | solution.py:61
  553.5 3.8 dkv.1
  573.1 3.3 finish.1
  584.9 9.3 %collective-permute-done.80.refs_6_ = bf16[768,256]{1,0:T(8,128)(2,1)S(1)} collective-permute-done((bf16[768,256]{1,0:T(8,128)(2,1)S(1)}, bf16[768,256]{1,0:T(8,128)(2,1)S(1)}, u32[]{:S(2)}, u32[]{:S(2)}) %collective-permute-start.80) | collective-permute-done | bytes 393248 | tf_op jit(solution)/shard_map/ppermute | solution.py:160
  595.7 5.8 collective-permute-done.77.refs_3_
  604.0 6.4 dattn.2
  611.2 8.3 %unpack.2 = bf16[2048,256]{1,0:T(8,128)(2,1)} custom-call(s32[20]{0:T(128)} %stack.135.m, s32[2048,1]{1,0:T(8,128)} %fusion.5.at_ref, bf16[2048,256]{1,0:T(8,128)(2,1)} %bitcast.114, bf16[768,256]{1,0:T(8,128)(2,1)} %get-tuple-element.266.refs_0_, bf16[768,256]{1,0:T(8,128)(2,1)} %collective-permute-done.55.refs_1_), custom_call_target="tpu_custom_call" | custom-call | flops 1610612736 | bytes 2891776 | tf_op jit(solution)/shard_map/unpack/pallas_call | solution.py:61
  619.5 3.8 all-to-all-start.2
  623.3 6.5 dattn.3
  633.1 4.2 collective-permute-done.85
  639.7 3.3 collective-permute-done.83
  643.2 4.7 collective-permute-done.86
  648.0 3.8 collective-permute-start.87
  651.7 9.4 %dwqkv.1 = (bf16[4,256,512]{2,1,0:T(8,128)(2,1)}, bf16[4,256,512]{2,1,0:T(8,128)(2,1)}, bf16[2,256,512]{2,1,0:T(8,128)(2,1)}, bf16[2,256,512]{2,1,0:T(8,128)(2,1)}) custom-call(s32[20]{0:T(128)} %stack.135.m, bf16[768,256]{1,0:T(8,128)(2,1)} %get-tuple-element.159.refs_0_, bf16[768,256]{1,0:T(8,128)(2,1)} %copy-done.8, bf16[768,256]{1,0:T(8,128)(2,1)} %copy-done.9, ...), custom_call_target="tpu_custom_call" | custom-call | flops 2415919104 | bytes 7102464 | tf_op jit(solution)/shard_map/dwqkv/pallas_call | solution.py:61
  662.0 6.1 norm_back_first.1
  684.4 8.3 %unpack.3 = bf16[2048,256]{1,0:T(8,128)(2,1)} custom-call(s32[20]{0:T(128)} %stack.135.m, s32[2048,1]{1,0:T(8,128)} %fusion.5.at_ref, bf16[2048,256]{1,0:T(8,128)(2,1)} %gather_fusion.4, bf16[768,256]{1,0:T(8,128)(2,1)} %get-tuple-element.264.refs_0_, bf16[768,256]{1,0:T(8,128)(2,1)} %copy-done.96), custom_call_target="tpu_custom_call" | custom-call | flops 1610612736 | bytes 2891776 | tf_op jit(solution)/shard_map/unpack/pallas_call | solution.py:61
  692.7 4.1 all-to-all-start.3
  696.8 5.9 convert_add_fusion
  704.4 7.7 %all-to-all-done.3 = bf16[8,256,256]{2,1,0:T(8,128)(2,1)S(1)} async-done(((bf16[8,256,256]{2,1,0:T(8,128)(2,1)}), bf16[8,256,256]{2,1,0:T(8,128)(2,1)S(1)}, u32[]{:S(2)}, u32[]{:S(2)}) %all-to-all-start.3) | async-done | bytes 1048608 | tf_op jit(solution)/shard_map/all_to_all | solution.py:1140
  714.0 9.8 %add_bitcast_fusion = f32[4,256,2,1408]{3,1,2,0:T(8,128)} fusion(bf16[4,2,256,1408]{3,2,1,0:T(8,128)(2,1)} %collective-permute-done.102, bf16[4,2,256,1408]{3,2,1,0:T(8,128)(2,1)} %get-tuple-element.179), kind=kLoop, calls=%fused_computation.6 | loop fusion | flops 8650752 | bytes 23068672 | tf_op jit(solution)/shard_map/transpose | solution.py:1086
  723.8 20.2 %copy.192 = f32[4,256,2,1408]{3,2,1,0:T(2,128)} copy(f32[4,256,2,1408]{3,1,2,0:T(8,128)} %add_bitcast_fusion) | data formatting | bytes 23068672
  (544 shorter events, 213.9 us)
Async XLA Ops:
  3.4 27.4 %all-to-all-start = ((bf16[8,256,256]{2,1,0:T(8,128)(2,1)}), bf16[8,256,256]{2,1,0:T(8,128)(2,1)S(1)}, u32[]{:S(2)}, u32[]{:S(2)}) async-start(bf16[8,256,256]{2,1,0:T(8,128)(2,1)} %bitcast.108), calls=%async_computation | async-start | bytes 2097152 | tf_op jit(solution)/shard_map/all_to_all | solution.py:250
  8.6 37.1 %collective-permute-start.1 = (bf16[4,256,512]{2,1,0:T(8,128)(2,1)}, bf16[4,256,512]{2,1,0:T(8,128)(2,1)}, u32[]{:S(2)}, u32[]{:S(2)}) collective-permute-start(bf16[4,256,512]{2,1,0:T(8,128)(2,1)} %refs_9_.7), channel_id=1, source_target_pairs={{0,4},{4,0},{8,12},{12,8},{16,20},{20,16},{24,28},{28,24},{1,5},{5... | collective-permute-start | bytes 3145736 | tf_op jit(solution)/shard_map/ppermute | solution.py:164
  9.2 36.6 %collective-permute-start.2 = (bf16[2,256,512]{2,1,0:T(8,128)(2,1)}, bf16[2,256,512]{2,1,0:T(8,128)(2,1)}, u32[]{:S(2)}, u32[]{:S(2)}) collective-permute-start(bf16[2,256,512]{2,1,0:T(8,128)(2,1)} %refs_11_.3), channel_id=1, source_target_pairs={{0,4},{4,0},{8,12},{12,8},{16,20},{20,16},{24,28},{28,24},{1,5},{5... | collective-permute-start | bytes 1572872 | tf_op jit(solution)/shard_map/ppermute | solution.py:164
  9.3 104.7 %collective-permute-start.18 = (bf16[4,512,256]{2,1,0:T(8,128)(2,1)}, bf16[4,512,256]{2,1,0:T(8,128)(2,1)}, u32[]{:S(2)}, u32[]{:S(2)}) collective-permute-start(bf16[4,512,256]{2,1,0:T(8,128)(2,1)} %refs_1_.1), channel_id=1, source_target_pairs={{0,4},{4,0},{8,12},{12,8},{16,20},{20,16},{24,28},{28,24},{1,5},{5... | collective-permute-start | bytes 3145736 | tf_op jit(solution)/shard_map/ppermute | solution.py:164
  15.6 182.0 %collective-permute-start.25 = (bf16[4,2,256,1408]{3,2,1,0:T(8,128)(2,1)}, bf16[4,2,256,1408]{3,2,1,0:T(8,128)(2,1)}, u32[]{:S(2)}, u32[]{:S(2)}) collective-permute-start(bf16[4,2,256,1408]{3,2,1,0:T(8,128)(2,1)} %bitcast.106.refs_2_.refs_4_), channel_id=1, source_target_pairs={{0,4},{4,0},{8,12},{12,8},{16,20},{20,16},{24,28},{28,24},{1,5},{5... | collective-permute-start | bytes 17301512 | tf_op jit(solution)/shard_map/ppermute | solution.py:164
  30.8 110.6 %all-to-all-start.1 = ((bf16[8,256,256]{2,1,0:T(8,128)(2,1)}), bf16[8,256,256]{2,1,0:T(8,128)(2,1)S(1)}, u32[]{:S(2)}, u32[]{:S(2)}) async-start(bf16[8,256,256]{2,1,0:T(8,128)(2,1)} %bitcast.120), calls=%async_computation.1 | async-start | bytes 2097152 | tf_op jit(solution)/shard_map/all_to_all | solution.py:252
  58.1 12.7 %collective-permute-start.4 = (bf16[768,256]{1,0:T(8,128)(2,1)}, bf16[768,256]{1,0:T(8,128)(2,1)S(1)}, u32[]{:S(2)}, u32[]{:S(2)}) collective-permute-start(bf16[768,256]{1,0:T(8,128)(2,1)} %get-tuple-element.100), channel_id=1, source_target_pairs={{0,8},{4,12},{8,0},{12,4},{16,24},{20,28},{24,16},{28,20},{1,9},{5... | collective-permute-start | bytes 1179656 | tf_op jit(solution)/shard_map/ppermute | solution.py:160
  58.6 13.9 %collective-permute-start.6 = (bf16[768,256]{1,0:T(8,128)(2,1)}, bf16[768,256]{1,0:T(8,128)(2,1)S(1)}, u32[]{:S(2)}, u32[]{:S(2)}) collective-permute-start(bf16[768,256]{1,0:T(8,128)(2,1)} %get-tuple-element.103), channel_id=1, source_target_pairs={{0,16},{4,20},{8,24},{12,28},{16,0},{20,4},{24,8},{28,12},{1,17},{... | collective-permute-start | bytes 1179656 | tf_op jit(solution)/shard_map/ppermute | solution.py:160
  70.1 106.9 %collective-permute-start.33 = (bf16[4,1408,256]{2,1,0:T(8,128)(2,1)}, bf16[4,1408,256]{2,1,0:T(8,128)(2,1)}, u32[]{:S(2)}, u32[]{:S(2)}) collective-permute-start(bf16[4,1408,256]{2,1,0:T(8,128)(2,1)} %refs_8_.1), channel_id=1, source_target_pairs={{0,4},{4,0},{8,12},{12,8},{16,20},{20,16},{24,28},{28,24},{1,5},{5... | collective-permute-start | bytes 8650760 | tf_op jit(solution)/shard_map/ppermute | solution.py:164
  138.6 16.0 %collective-permute-start.19 = (bf16[2,192,256]{2,1,0:T(8,128)(2,1)}, bf16[2,192,256]{2,1,0:T(8,128)(2,1)S(1)}, u32[]{:S(2)}, u32[]{:S(2)}) collective-permute-start(bf16[2,192,256]{2,1,0:T(8,128)(2,1)} %get-tuple-element.111), channel_id=1, source_target_pairs={{0,1},{1,0},{2,3},{3,2},{4,5},{5,4},{6,7},{7,6},{8,9},{9,8},{10,11... | collective-permute-start | bytes 589832 | tf_op jit(solution)/shard_map/ppermute | solution.py:175
  147.4 29.6 %collective-permute-start.32 = (bf16[768,256]{1,0:T(8,128)(2,1)S(1)}, bf16[768,256]{1,0:T(8,128)(2,1)S(1)}, u32[]{:S(2)}, u32[]{:S(2)}) collective-permute-start(bf16[768,256]{1,0:T(8,128)(2,1)S(1)} %gather_fusion.3), channel_id=1, source_target_pairs={{0,4},{4,0},{8,12},{12,8},{16,20},{20,16},{24,28},{28,24},{1,5},{5... | collective-permute-start | bytes 1179656 | tf_op jit(solution)/shard_map/ppermute | solution.py:164
  154.7 14.7 %collective-permute-start.20 = (bf16[2,192,256]{2,1,0:T(8,128)(2,1)S(1)}, bf16[2,192,256]{2,1,0:T(8,128)(2,1)S(1)}, u32[]{:S(2)}, u32[]{:S(2)}) collective-permute-start(bf16[2,192,256]{2,1,0:T(8,128)(2,1)S(1)} %add_convert_fusion.21), channel_id=1, source_target_pairs={{0,3},{1,2},{2,1},{3,0},{4,7},{5,6},{6,5},{7,4},{8,11},{9,10},{10,... | collective-permute-start | bytes 589832 | tf_op jit(solution)/shard_map/ppermute | solution.py:175
  169.4 21.0 %collective-permute-start.21 = (bf16[2,192,256]{2,1,0:T(8,128)(2,1)S(1)}, bf16[2,192,256]{2,1,0:T(8,128)(2,1)S(1)}, u32[]{:S(2)}, u32[]{:S(2)}) collective-permute-start(bf16[2,192,256]{2,1,0:T(8,128)(2,1)S(1)} %add_convert_fusion.20.refs_0_), channel_id=1, source_target_pairs={{0,1},{1,0},{2,3},{3,2},{4,5},{5,4},{6,7},{7,6},{8,9},{9,8},{10,11... | collective-permute-start | bytes 589832 | tf_op jit(solution)/shard_map/ppermute | solution.py:175
  174.4 16.0 %collective-permute-start.24 = (bf16[2,192,256]{2,1,0:T(8,128)(2,1)S(1)}, bf16[2,192,256]{2,1,0:T(8,128)(2,1)S(1)}, u32[]{:S(2)}, u32[]{:S(2)}) collective-permute-start(bf16[2,192,256]{2,1,0:T(8,128)(2,1)S(1)} %add_convert_fusion.18.refs_2_), channel_id=1, source_target_pairs={{0,1},{1,0},{2,3},{3,2},{4,5},{5,4},{6,7},{7,6},{8,9},{9,8},{10,11... | collective-permute-start | bytes 589832 | tf_op jit(solution)/shard_map/ppermute | solution.py:175
  189.8 24.4 %collective-permute-start.35 = (bf16[192,1408]{1,0:T(8,128)(2,1)}, bf16[192,1408]{1,0:T(8,128)(2,1)S(1)}, u32[]{:S(2)}, u32[]{:S(2)}) collective-permute-start(bf16[192,1408]{1,0:T(8,128)(2,1)} %get-tuple-element.128), channel_id=1, source_target_pairs={{0,8},{4,12},{8,0},{12,4},{16,24},{20,28},{24,16},{28,20},{1,9},{5... | collective-permute-start | bytes 1622024 | tf_op jit(solution)/shard_map/ppermute | solution.py:160
  208.2 26.9 %collective-permute-start.27 = (bf16[2,192,1408]{2,1,0:T(8,128)(2,1)}, bf16[2,192,1408]{2,1,0:T(8,128)(2,1)S(1)}, u32[]{:S(2)}, u32[]{:S(2)}) collective-permute-start(bf16[2,192,1408]{2,1,0:T(8,128)(2,1)} %get-tuple-element.115), channel_id=1, source_target_pairs={{0,8},{4,12},{8,0},{12,4},{16,24},{20,28},{24,16},{28,20},{1,9},{5... | collective-permute-start | bytes 3244040 | tf_op jit(solution)/shard_map/ppermute | solution.py:160
  210.1 53.4 %collective-permute-start.34 = (bf16[192,1408]{1,0:T(8,128)(2,1)}, bf16[192,1408]{1,0:T(8,128)(2,1)}, u32[]{:S(2)}, u32[]{:S(2)}) collective-permute-start(bf16[192,1408]{1,0:T(8,128)(2,1)} %get-tuple-element.126), channel_id=1, source_target_pairs={{0,8},{4,12},{8,0},{12,4},{16,24},{20,28},{24,16},{28,20},{1,9},{5... | collective-permute-start | bytes 1622024 | tf_op jit(solution)/shard_map/ppermute | solution.py:160
  210.9 53.4 %collective-permute-start.37 = (bf16[192,1408]{1,0:T(8,128)(2,1)}, bf16[192,1408]{1,0:T(8,128)(2,1)}, u32[]{:S(2)}, u32[]{:S(2)}) collective-permute-start(bf16[192,1408]{1,0:T(8,128)(2,1)} %get-tuple-element.131), channel_id=1, source_target_pairs={{0,16},{4,20},{8,24},{12,28},{16,0},{20,4},{24,8},{28,12},{1,17},{... | collective-permute-start | bytes 1622024 | tf_op jit(solution)/shard_map/ppermute | solution.py:160
  213.0 52.6 %collective-permute-start.39 = (bf16[192,1408]{1,0:T(8,128)(2,1)}, bf16[192,1408]{1,0:T(8,128)(2,1)}, u32[]{:S(2)}, u32[]{:S(2)}) collective-permute-start(bf16[192,1408]{1,0:T(8,128)(2,1)} %get-tuple-element.132), channel_id=1, source_target_pairs={{0,16},{4,20},{8,24},{12,28},{16,0},{20,4},{24,8},{28,12},{1,17},{... | collective-permute-start | bytes 1622024 | tf_op jit(solution)/shard_map/ppermute | solution.py:160
  215.0 46.1 %collective-permute-start.29 = (bf16[2,192,1408]{2,1,0:T(8,128)(2,1)}, bf16[2,192,1408]{2,1,0:T(8,128)(2,1)S(1)}, u32[]{:S(2)}, u32[]{:S(2)}) collective-permute-start(bf16[2,192,1408]{2,1,0:T(8,128)(2,1)} %get-tuple-element.122), channel_id=1, source_target_pairs={{0,16},{4,20},{8,24},{12,28},{16,0},{20,4},{24,8},{28,12},{1,17},{... | collective-permute-start | bytes 3244040 | tf_op jit(solution)/shard_map/ppermute | solution.py:160
  235.2 37.6 %collective-permute-start.36 = (bf16[192,1408]{1,0:T(8,128)(2,1)}, bf16[192,1408]{1,0:T(8,128)(2,1)}, u32[]{:S(2)}, u32[]{:S(2)}) collective-permute-start(bf16[192,1408]{1,0:T(8,128)(2,1)} %add_convert_fusion.3), channel_id=1, source_target_pairs={{0,16},{4,20},{8,24},{12,28},{16,0},{20,4},{24,8},{28,12},{1,17},{... | collective-permute-start | bytes 1622024 | tf_op jit(solution)/shard_map/ppermute | solution.py:160
  261.0 56.2 %collective-permute-start.26 = (bf16[2,192,1408]{2,1,0:T(8,128)(2,1)}, bf16[2,192,1408]{2,1,0:T(8,128)(2,1)S(1)}, u32[]{:S(2)}, u32[]{:S(2)}) collective-permute-start(bf16[2,192,1408]{2,1,0:T(8,128)(2,1)} %get-tuple-element.118), channel_id=1, source_target_pairs={{0,8},{4,12},{8,0},{12,4},{16,24},{20,28},{24,16},{28,20},{1,9},{5... | collective-permute-start | bytes 3244040 | tf_op jit(solution)/shard_map/ppermute | solution.py:160
  263.5 53.8 %collective-permute-start.31 = (bf16[2,192,1408]{2,1,0:T(8,128)(2,1)}, bf16[2,192,1408]{2,1,0:T(8,128)(2,1)S(1)}, u32[]{:S(2)}, u32[]{:S(2)}) collective-permute-start(bf16[2,192,1408]{2,1,0:T(8,128)(2,1)} %get-tuple-element.123), channel_id=1, source_target_pairs={{0,16},{4,20},{8,24},{12,28},{16,0},{20,4},{24,8},{28,12},{1,17},{... | collective-permute-start | bytes 3244040 | tf_op jit(solution)/shard_map/ppermute | solution.py:160
  264.3 52.9 %collective-permute-start.28 = (bf16[2,192,1408]{2,1,0:T(8,128)(2,1)}, bf16[2,192,1408]{2,1,0:T(8,128)(2,1)}, u32[]{:S(2)}, u32[]{:S(2)}) collective-permute-start(bf16[2,192,1408]{2,1,0:T(8,128)(2,1)} %add_convert_fusion.1), channel_id=1, source_target_pairs={{0,16},{4,20},{8,24},{12,28},{16,0},{20,4},{24,8},{28,12},{1,17},{... | collective-permute-start | bytes 3244040 | tf_op jit(solution)/shard_map/ppermute | solution.py:160
  265.5 51.8 %collective-permute-start.30 = (bf16[2,192,1408]{2,1,0:T(8,128)(2,1)}, bf16[2,192,1408]{2,1,0:T(8,128)(2,1)}, u32[]{:S(2)}, u32[]{:S(2)}) collective-permute-start(bf16[2,192,1408]{2,1,0:T(8,128)(2,1)} %add_convert_fusion), channel_id=1, source_target_pairs={{0,8},{4,12},{8,0},{12,4},{16,24},{20,28},{24,16},{28,20},{1,9},{5... | collective-permute-start | bytes 3244040 | tf_op jit(solution)/shard_map/ppermute | solution.py:160
  272.7 44.5 %collective-permute-start.38 = (bf16[192,1408]{1,0:T(8,128)(2,1)}, bf16[192,1408]{1,0:T(8,128)(2,1)}, u32[]{:S(2)}, u32[]{:S(2)}) collective-permute-start(bf16[192,1408]{1,0:T(8,128)(2,1)} %add_convert_fusion.2), channel_id=1, source_target_pairs={{0,8},{4,12},{8,0},{12,4},{16,24},{20,28},{24,16},{28,20},{1,9},{5... | collective-permute-start | bytes 1622024 | tf_op jit(solution)/shard_map/ppermute | solution.py:160
  338.0 50.9 %collective-permute-start.42 = (bf16[2,192,1408]{2,1,0:T(8,128)(2,1)S(1)}, bf16[2,192,1408]{2,1,0:T(8,128)(2,1)}, u32[]{:S(2)}, u32[]{:S(2)}) collective-permute-start(bf16[2,192,1408]{2,1,0:T(8,128)(2,1)S(1)} %copy-done.14), channel_id=1, source_target_pairs={{0,8},{4,12},{8,0},{12,4},{16,24},{20,28},{24,16},{28,20},{1,9},{5... | collective-permute-start | bytes 3244040 | tf_op jit(solution)/shard_map/ppermute | solution.py:160
  339.1 51.8 %collective-permute-start.48 = (bf16[2,192,1408]{2,1,0:T(8,128)(2,1)}, bf16[2,192,1408]{2,1,0:T(8,128)(2,1)}, u32[]{:S(2)}, u32[]{:S(2)}) collective-permute-start(bf16[2,192,1408]{2,1,0:T(8,128)(2,1)} %get-tuple-element.138.refs_2_.refs_4_), channel_id=1, source_target_pairs={{0,16},{4,20},{8,24},{12,28},{16,0},{20,4},{24,8},{28,12},{1,17},{... | collective-permute-start | bytes 3244040 | tf_op jit(solution)/shard_map/ppermute | solution.py:160
  343.2 21.4 %collective-permute-start.68 = (f32[8,192]{0,1:T(8,128)S(1)}, f32[8,192]{0,1:T(8,128)S(1)}, u32[]{:S(2)}, u32[]{:S(2)}) collective-permute-start(f32[8,192]{0,1:T(8,128)S(1)} %add.699), channel_id=1, source_target_pairs={{0,24},{4,28},{8,16},{12,20},{16,8},{20,12},{24,0},{28,4},{1,25},{... | collective-permute-start | bytes 18440 | tf_op jit(solution)/shard_map/ppermute | solution.py:160
  344.7 25.6 %collective-permute-start.67 = (f32[8,192]{0,1:T(8,128)S(1)}, f32[8,192]{0,1:T(8,128)S(1)}, u32[]{:S(2)}, u32[]{:S(2)}) collective-permute-start(f32[8,192]{0,1:T(8,128)S(1)} %add.699), channel_id=1, source_target_pairs={{0,16},{4,20},{8,24},{12,28},{16,0},{20,4},{24,8},{28,12},{1,17},{... | collective-permute-start | bytes 18440 | tf_op jit(solution)/shard_map/ppermute | solution.py:160
  347.0 44.7 %collective-permute-start.43 = (bf16[2,192,1408]{2,1,0:T(8,128)(2,1)S(1)}, bf16[2,192,1408]{2,1,0:T(8,128)(2,1)}, u32[]{:S(2)}, u32[]{:S(2)}) collective-permute-start(bf16[2,192,1408]{2,1,0:T(8,128)(2,1)S(1)} %copy-done.14), channel_id=1, source_target_pairs={{0,16},{4,20},{8,24},{12,28},{16,0},{20,4},{24,8},{28,12},{1,17},{... | collective-permute-start | bytes 3244040 | tf_op jit(solution)/shard_map/ppermute | solution.py:160
  364.5 28.5 %collective-permute-start.47 = (bf16[2,192,1408]{2,1,0:T(8,128)(2,1)}, bf16[2,192,1408]{2,1,0:T(8,128)(2,1)}, u32[]{:S(2)}, u32[]{:S(2)}) collective-permute-start(bf16[2,192,1408]{2,1,0:T(8,128)(2,1)} %get-tuple-element.138.refs_2_.refs_4_), channel_id=1, source_target_pairs={{0,8},{4,12},{8,0},{12,4},{16,24},{20,28},{24,16},{28,20},{1,9},{5... | collective-permute-start | bytes 3244040 | tf_op jit(solution)/shard_map/ppermute | solution.py:160
  370.3 17.6 %collective-permute-start.66 = (f32[8,192]{0,1:T(8,128)S(1)}, f32[8,192]{0,1:T(8,128)S(1)}, u32[]{:S(2)}, u32[]{:S(2)}) collective-permute-start(f32[8,192]{0,1:T(8,128)S(1)} %add.699), channel_id=1, source_target_pairs={{0,8},{4,12},{8,0},{12,4},{16,24},{20,28},{24,16},{28,20},{1,9},{5... | collective-permute-start | bytes 18440 | tf_op jit(solution)/shard_map/ppermute | solution.py:160
  388.9 42.2 %collective-permute-start.59 = (bf16[2,192,1408]{2,1,0:T(8,128)(2,1)}, bf16[2,192,1408]{2,1,0:T(8,128)(2,1)}, u32[]{:S(2)}, u32[]{:S(2)}) collective-permute-start(bf16[2,192,1408]{2,1,0:T(8,128)(2,1)} %collective-permute-done.42.refs_1_), channel_id=1, source_target_pairs={{0,16},{4,20},{8,24},{12,28},{16,0},{20,4},{24,8},{28,12},{1,17},{... | collective-permute-start | bytes 3244040 | tf_op jit(solution)/shard_map/ppermute | solution.py:160
  390.9 42.1 %collective-permute-start.60 = (bf16[2,192,1408]{2,1,0:T(8,128)(2,1)}, bf16[2,192,1408]{2,1,0:T(8,128)(2,1)}, u32[]{:S(2)}, u32[]{:S(2)}) collective-permute-start(bf16[2,192,1408]{2,1,0:T(8,128)(2,1)} %collective-permute-done.48.refs_2_.refs_6_), channel_id=1, source_target_pairs={{0,8},{4,12},{8,0},{12,4},{16,24},{20,28},{24,16},{28,20},{1,9},{5... | collective-permute-start | bytes 3244040 | tf_op jit(solution)/shard_map/ppermute | solution.py:160
  391.7 34.3 %collective-permute-start.44 = (bf16[192,1408]{1,0:T(8,128)(2,1)S(1)}, bf16[192,1408]{1,0:T(8,128)(2,1)S(1)}, u32[]{:S(2)}, u32[]{:S(2)}) collective-permute-start(bf16[192,1408]{1,0:T(8,128)(2,1)S(1)} %copy-done.90), channel_id=1, source_target_pairs={{0,8},{4,12},{8,0},{12,4},{16,24},{20,28},{24,16},{28,20},{1,9},{5... | collective-permute-start | bytes 1622024 | tf_op jit(solution)/shard_map/ppermute | solution.py:160
  393.1 34.5 %collective-permute-start.50 = (bf16[192,1408]{1,0:T(8,128)(2,1)}, bf16[192,1408]{1,0:T(8,128)(2,1)}, u32[]{:S(2)}, u32[]{:S(2)}) collective-permute-start(bf16[192,1408]{1,0:T(8,128)(2,1)} %get-tuple-element.139.refs_4_), channel_id=1, source_target_pairs={{0,16},{4,20},{8,24},{12,28},{16,0},{20,4},{24,8},{28,12},{1,17},{... | collective-permute-start | bytes 1622024 | tf_op jit(solution)/shard_map/ppermute | solution.py:160
  411.1 39.9 %collective-permute-start.45 = (bf16[192,1408]{1,0:T(8,128)(2,1)S(1)}, bf16[192,1408]{1,0:T(8,128)(2,1)S(1)}, u32[]{:S(2)}, u32[]{:S(2)}) collective-permute-start(bf16[192,1408]{1,0:T(8,128)(2,1)S(1)} %copy-done.90), channel_id=1, source_target_pairs={{0,16},{4,20},{8,24},{12,28},{16,0},{20,4},{24,8},{28,12},{1,17},{... | collective-permute-start | bytes 1622024 | tf_op jit(solution)/shard_map/ppermute | solution.py:160
  426.0 26.0 %collective-permute-start.49 = (bf16[192,1408]{1,0:T(8,128)(2,1)}, bf16[192,1408]{1,0:T(8,128)(2,1)S(1)}, u32[]{:S(2)}, u32[]{:S(2)}) collective-permute-start(bf16[192,1408]{1,0:T(8,128)(2,1)} %get-tuple-element.139.refs_4_), channel_id=1, source_target_pairs={{0,8},{4,12},{8,0},{12,4},{16,24},{20,28},{24,16},{28,20},{1,9},{5... | collective-permute-start | bytes 1622024 | tf_op jit(solution)/shard_map/ppermute | solution.py:160
  427.6 16.5 %collective-permute-start.57 = (bf16[2,192,256]{2,1,0:T(8,128)(2,1)S(1)}, bf16[2,192,256]{2,1,0:T(8,128)(2,1)S(1)}, u32[]{:S(2)}, u32[]{:S(2)}) collective-permute-start(bf16[2,192,256]{2,1,0:T(8,128)(2,1)S(1)} %add_convert_fusion.17), channel_id=1, source_target_pairs={{0,3},{1,2},{2,1},{3,0},{4,7},{5,6},{6,5},{7,4},{8,11},{9,10},{10,... | collective-permute-start | bytes 589832 | tf_op jit(solution)/shard_map/ppermute | solution.py:175
  431.0 21.0 %collective-permute-start.46 = (bf16[192,1408]{1,0:T(8,128)(2,1)S(1)}, bf16[192,1408]{1,0:T(8,128)(2,1)}, u32[]{:S(2)}, u32[]{:S(2)}) collective-permute-start(bf16[192,1408]{1,0:T(8,128)(2,1)S(1)} %collective-permute-done.44.refs_1_), channel_id=1, source_target_pairs={{0,16},{4,20},{8,24},{12,28},{16,0},{20,4},{24,8},{28,12},{1,17},{... | collective-permute-start | bytes 1622024 | tf_op jit(solution)/shard_map/ppermute | solution.py:160
  433.0 19.0 %collective-permute-start.51 = (bf16[192,1408]{1,0:T(8,128)(2,1)}, bf16[192,1408]{1,0:T(8,128)(2,1)}, u32[]{:S(2)}, u32[]{:S(2)}) collective-permute-start(bf16[192,1408]{1,0:T(8,128)(2,1)} %collective-permute-done.50.refs_6_), channel_id=1, source_target_pairs={{0,8},{4,12},{8,0},{12,4},{16,24},{20,28},{24,16},{28,20},{1,9},{5... | collective-permute-start | bytes 1622024 | tf_op jit(solution)/shard_map/ppermute | solution.py:160
  450.1 35.1 %collective-permute-start.58 = (bf16[2,192,256]{2,1,0:T(8,128)(2,1)S(1)}, bf16[2,192,256]{2,1,0:T(8,128)(2,1)S(1)}, u32[]{:S(2)}, u32[]{:S(2)}) collective-permute-start(bf16[2,192,256]{2,1,0:T(8,128)(2,1)S(1)} %add_convert_fusion.16.refs_0_), channel_id=1, source_target_pairs={{0,1},{1,0},{2,3},{3,2},{4,5},{5,4},{6,7},{7,6},{8,9},{9,8},{10,11... | collective-permute-start | bytes 589832 | tf_op jit(solution)/shard_map/ppermute | solution.py:175
  451.1 13.9 %collective-permute-start.62 = (bf16[2,192,256]{2,1,0:T(8,128)(2,1)S(1)}, bf16[2,192,256]{2,1,0:T(8,128)(2,1)S(1)}, u32[]{:S(2)}, u32[]{:S(2)}) collective-permute-start(bf16[2,192,256]{2,1,0:T(8,128)(2,1)S(1)} %add_convert_fusion.15), channel_id=1, source_target_pairs={{0,3},{1,2},{2,1},{3,0},{4,7},{5,6},{6,5},{7,4},{8,11},{9,10},{10,... | collective-permute-start | bytes 589832 | tf_op jit(solution)/shard_map/ppermute | solution.py:175
  463.6 46.6 %collective-permute-start.52 = (bf16[2,384,256]{2,1,0:T(8,128)(2,1)}, bf16[2,384,256]{2,1,0:T(8,128)(2,1)S(1)}, u32[]{:S(2)}, u32[]{:S(2)}) collective-permute-start(bf16[2,384,256]{2,1,0:T(8,128)(2,1)} %get-tuple-element.141), channel_id=1, source_target_pairs={{0,1},{1,0},{2,3},{3,2},{4,5},{5,4},{6,7},{7,6},{8,9},{9,8},{10,11... | collective-permute-start | bytes 1179656 | tf_op jit(solution)/shard_map/ppermute | solution.py:175
  465.0 20.2 %collective-permute-start.63 = (bf16[2,192,256]{2,1,0:T(8,128)(2,1)S(1)}, bf16[2,192,256]{2,1,0:T(8,128)(2,1)S(1)}, u32[]{:S(2)}, u32[]{:S(2)}) collective-permute-start(bf16[2,192,256]{2,1,0:T(8,128)(2,1)S(1)} %add_convert_fusion.14.refs_2_), channel_id=1, source_target_pairs={{0,1},{1,0},{2,3},{3,2},{4,5},{5,4},{6,7},{7,6},{8,9},{9,8},{10,11... | collective-permute-start | bytes 589832 | tf_op jit(solution)/shard_map/ppermute | solution.py:175
  510.7 203.4 %collective-permute-start.102 = (bf16[4,2,256,1408]{3,2,1,0:T(8,128)(2,1)}, bf16[4,2,256,1408]{3,2,1,0:T(8,128)(2,1)}, u32[]{:S(2)}, u32[]{:S(2)}) collective-permute-start(bf16[4,2,256,1408]{3,2,1,0:T(8,128)(2,1)} %get-tuple-element.180), channel_id=1, source_target_pairs={{0,4},{4,0},{8,12},{12,8},{16,20},{20,16},{24,28},{28,24},{1,5},{5... | collective-permute-start | bytes 17301512 | tf_op jit(solution)/shard_map/ppermute | solution.py:164
  510.9 49.4 %collective-permute-start.53 = (bf16[2,384,256]{2,1,0:T(8,128)(2,1)S(1)}, bf16[2,384,256]{2,1,0:T(8,128)(2,1)S(1)}, u32[]{:S(2)}, u32[]{:S(2)}) collective-permute-start(bf16[2,384,256]{2,1,0:T(8,128)(2,1)S(1)} %add_convert_fusion.5), channel_id=1, source_target_pairs={{0,3},{1,2},{2,1},{3,0},{4,7},{5,6},{6,5},{7,4},{8,11},{9,10},{10,... | collective-permute-start | bytes 1179656 | tf_op jit(solution)/shard_map/ppermute | solution.py:175
  514.2 30.6 %collective-permute-start.100 = (f32[5,8,256]{2,1,0:T(8,128)S(1)}, f32[5,8,256]{2,1,0:T(8,128)S(1)}, u32[]{:S(2)}, u32[]{:S(2)}) collective-permute-start(f32[5,8,256]{2,1,0:T(8,128)S(1)} %add.724), channel_id=1, source_target_pairs={{0,8},{4,12},{8,0},{12,4},{16,24},{20,28},{24,16},{28,20},{1,9},{5... | collective-permute-start | bytes 122888 | tf_op jit(solution)/shard_map/ppermute | solution.py:762
  532.6 20.2 %collective-permute-start.78 = (f32[256,256]{1,0:T(8,128)}, f32[256,256]{1,0:T(8,128)S(1)}, u32[]{:S(2)}, u32[]{:S(2)}) collective-permute-start(f32[256,256]{1,0:T(8,128)} %get-tuple-element.161), channel_id=1, source_target_pairs={{4,0},{12,8},{20,16},{28,24},{5,1},{13,9},{21,17},{29,25},{6,2},{1... | collective-permute-start | bytes 786440 | tf_op jit(solution)/shard_map/ppermute | solution.py:172
  569.1 13.6 %collective-permute-start.75 = (bf16[768,256]{1,0:T(8,128)(2,1)S(1)}, bf16[768,256]{1,0:T(8,128)(2,1)S(1)}, u32[]{:S(2)}, u32[]{:S(2)}) collective-permute-start(bf16[768,256]{1,0:T(8,128)(2,1)S(1)} %copy-done.6), channel_id=1, source_target_pairs={{0,8},{4,12},{8,0},{12,4},{16,24},{20,28},{24,16},{28,20},{1,9},{5... | collective-permute-start | bytes 1179656 | tf_op jit(solution)/shard_map/ppermute | solution.py:160
  570.8 13.2 %collective-permute-start.76 = (bf16[768,256]{1,0:T(8,128)(2,1)S(1)}, bf16[768,256]{1,0:T(8,128)(2,1)S(1)}, u32[]{:S(2)}, u32[]{:S(2)}) collective-permute-start(bf16[768,256]{1,0:T(8,128)(2,1)S(1)} %copy-done.6), channel_id=1, source_target_pairs={{0,16},{4,20},{8,24},{12,28},{16,0},{20,4},{24,8},{28,12},{1,17},{... | collective-permute-start | bytes 1179656 | tf_op jit(solution)/shard_map/ppermute | solution.py:160
  581.6 29.6 %collective-permute-start.55 = (bf16[768,256]{1,0:T(8,128)(2,1)S(1)}, bf16[768,256]{1,0:T(8,128)(2,1)}, u32[]{:S(2)}, u32[]{:S(2)}) collective-permute-start(bf16[768,256]{1,0:T(8,128)(2,1)S(1)} %get-tuple-element.265), channel_id=1, source_target_pairs={{0,4},{4,0},{8,12},{12,8},{16,20},{20,16},{24,28},{28,24},{1,5},{5... | collective-permute-start | bytes 1179656 | tf_op jit(solution)/shard_map/ppermute | solution.py:164
  582.7 13.0 %collective-permute-start.79 = (bf16[768,256]{1,0:T(8,128)(2,1)S(1)}, bf16[768,256]{1,0:T(8,128)(2,1)S(1)}, u32[]{:S(2)}, u32[]{:S(2)}) collective-permute-start(bf16[768,256]{1,0:T(8,128)(2,1)S(1)} %copy-done.7), channel_id=1, source_target_pairs={{0,8},{4,12},{8,0},{12,4},{16,24},{20,28},{24,16},{28,20},{1,9},{5... | collective-permute-start | bytes 1179656 | tf_op jit(solution)/shard_map/ppermute | solution.py:160
  584.0 17.6 %collective-permute-start.77 = (bf16[768,256]{1,0:T(8,128)(2,1)S(1)}, bf16[768,256]{1,0:T(8,128)(2,1)S(1)}, u32[]{:S(2)}, u32[]{:S(2)}) collective-permute-start(bf16[768,256]{1,0:T(8,128)(2,1)S(1)} %collective-permute-done.75.refs_1_), channel_id=1, source_target_pairs={{0,16},{4,20},{8,24},{12,28},{16,0},{20,4},{24,8},{28,12},{1,17},{... | collective-permute-start | bytes 1179656 | tf_op jit(solution)/shard_map/ppermute | solution.py:160
  595.7 101.1 %collective-permute-start.103 = (bf16[4,1408,256]{2,1,0:T(8,128)(2,1)}, bf16[4,1408,256]{2,1,0:T(8,128)(2,1)}, u32[]{:S(2)}, u32[]{:S(2)}) collective-permute-start(bf16[4,1408,256]{2,1,0:T(8,128)(2,1)} %get-tuple-element.182), channel_id=1, source_target_pairs={{0,4},{4,0},{8,12},{12,8},{16,20},{20,16},{24,28},{28,24},{1,5},{5... | collective-permute-start | bytes 8650760 | tf_op jit(solution)/shard_map/ppermute | solution.py:164
  601.6 68.0 %collective-permute-start.98 = (bf16[4,512,256]{2,1,0:T(8,128)(2,1)}, bf16[4,512,256]{2,1,0:T(8,128)(2,1)}, u32[]{:S(2)}, u32[]{:S(2)}) collective-permute-start(bf16[4,512,256]{2,1,0:T(8,128)(2,1)} %get-tuple-element.177), channel_id=1, source_target_pairs={{0,4},{4,0},{8,12},{12,8},{16,20},{20,16},{24,28},{28,24},{1,5},{5... | collective-permute-start | bytes 3145736 | tf_op jit(solution)/shard_map/ppermute | solution.py:164
  610.5 20.7 %collective-permute-start.82 = (bf16[2,192,256]{2,1,0:T(8,128)(2,1)}, bf16[2,192,256]{2,1,0:T(8,128)(2,1)S(1)}, u32[]{:S(2)}, u32[]{:S(2)}) collective-permute-start(bf16[2,192,256]{2,1,0:T(8,128)(2,1)} %get-tuple-element.164), channel_id=1, source_target_pairs={{0,1},{1,0},{2,3},{3,2},{4,5},{5,4},{6,7},{7,6},{8,9},{9,8},{10,11... | collective-permute-start | bytes 589832 | tf_op jit(solution)/shard_map/ppermute | solution.py:175
  619.5 52.9 %all-to-all-start.2 = ((bf16[8,256,256]{2,1,0:T(8,128)(2,1)}), bf16[8,256,256]{2,1,0:T(8,128)(2,1)S(1)}, u32[]{:S(2)}, u32[]{:S(2)}) async-start(bf16[8,256,256]{2,1,0:T(8,128)(2,1)} %bitcast.132), calls=%async_computation.2 | async-start | bytes 2097152 | tf_op jit(solution)/shard_map/all_to_all | solution.py:1140
  643.1 18.1 %collective-permute-start.84 = (bf16[2,192,256]{2,1,0:T(8,128)(2,1)S(1)}, bf16[2,192,256]{2,1,0:T(8,128)(2,1)S(1)}, u32[]{:S(2)}, u32[]{:S(2)}) collective-permute-start(bf16[2,192,256]{2,1,0:T(8,128)(2,1)S(1)} %add_convert_fusion.10.refs_0_), channel_id=1, source_target_pairs={{0,1},{1,0},{2,3},{3,2},{4,5},{5,4},{6,7},{7,6},{8,9},{9,8},{10,11... | collective-permute-start | bytes 589832 | tf_op jit(solution)/shard_map/ppermute | solution.py:175
  648.0 13.3 %collective-permute-start.87 = (bf16[2,192,256]{2,1,0:T(8,128)(2,1)S(1)}, bf16[2,192,256]{2,1,0:T(8,128)(2,1)S(1)}, u32[]{:S(2)}, u32[]{:S(2)}) collective-permute-start(bf16[2,192,256]{2,1,0:T(8,128)(2,1)S(1)} %add_convert_fusion.8.refs_2_), channel_id=1, source_target_pairs={{0,1},{1,0},{2,3},{3,2},{4,5},{5,4},{6,7},{7,6},{8,9},{9,8},{10,11... | collective-permute-start | bytes 589832 | tf_op jit(solution)/shard_map/ppermute | solution.py:175
  661.2 14.8 %collective-permute-start.96 = (bf16[2,256,512]{2,1,0:T(8,128)(2,1)}, bf16[2,256,512]{2,1,0:T(8,128)(2,1)}, u32[]{:S(2)}, u32[]{:S(2)}) collective-permute-start(bf16[2,256,512]{2,1,0:T(8,128)(2,1)} %get-tuple-element.173), channel_id=1, source_target_pairs={{0,4},{4,0},{8,12},{12,8},{16,20},{20,16},{24,28},{28,24},{1,5},{5... | collective-permute-start | bytes 1572872 | tf_op jit(solution)/shard_map/ppermute | solution.py:164
  672.3 30.4 %collective-permute-start.97 = (bf16[4,256,512]{2,1,0:T(8,128)(2,1)}, bf16[4,256,512]{2,1,0:T(8,128)(2,1)S(1)}, u32[]{:S(2)}, u32[]{:S(2)}) collective-permute-start(bf16[4,256,512]{2,1,0:T(8,128)(2,1)} %get-tuple-element.175), channel_id=1, source_target_pairs={{0,4},{4,0},{8,12},{12,8},{16,20},{20,16},{24,28},{28,24},{1,5},{5... | collective-permute-start | bytes 3145736 | tf_op jit(solution)/shard_map/ppermute | solution.py:164
  692.7 19.4 %all-to-all-start.3 = ((bf16[8,256,256]{2,1,0:T(8,128)(2,1)}), bf16[8,256,256]{2,1,0:T(8,128)(2,1)S(1)}, u32[]{:S(2)}, u32[]{:S(2)}) async-start(bf16[8,256,256]{2,1,0:T(8,128)(2,1)} %bitcast.133), calls=%async_computation.3 | async-start | bytes 2097152 | tf_op jit(solution)/shard_map/all_to_all | solution.py:1140
  (142 other events, 1352.8 us)

commit v3 on v2

--- a/solution.py
+++ b/solution.py
@@ -187,14 +187,19 @@
         half = both(half, by_z(half, 3))
         return half, by_z(half, 1)
 
-    def reduce_groups(first, second):
+    def reduce_groups(first, second, early=None, late=None):
+        if early is not None:
+            first, second, _ = lax.optimization_barrier((tuple(first), tuple(second), early))
         ra = by_group(first[3], 1)
         rb = by_group(second[3], 2)
         ax = by_group(first[1], 1)
         by = by_group(second[2], 2)
-        ay = by_group(both(first[2], ra), 2)
-        bx = by_group(both(second[1], rb), 1)
-        return (first[0], ax, ay), (second[0], bx, by)
+        along_y, along_x = both(first[2], ra), both(second[1], rb)
+        if late is not None:
+            along_y, along_x, _ = lax.optimization_barrier((along_y, along_x, late))
+        ay = by_group(along_y, 2)
+        bx = by_group(along_x, 1)
+        return (first[0], ax, ay), (second[0], bx, by), (along_y, along_x)
 
     def gather_groups(first, second):
         ax, bx = by_group(first, 1), by_group(second, 1)
@@ -230,32 +235,66 @@
         axis=1,
     )
 
+    table = jnp.concatenate([starts, lengths, inverse, c[None]]).astype(jnp.int32)
+
     def places(part):
         packed = part * rp + jnp.arange(rp, dtype=jnp.int32)
         begun = starts[None, :] <= packed[:, None]
         first = jnp.max(jnp.where(begun, starts[None, :], 0), axis=1)
         seq = jnp.sum(begun.astype(jnp.int32), axis=1) - 1
-        at = packed - first
-        slot = jnp.sum(
-            jnp.where(seq[:, None] == jnp.arange(seqs, dtype=jnp.int32)[None, :], inverse[None, :], 0),
-            axis=1,
-        )
-        x_row = (at // per) * (seqs * per) + seq * per + at % per
-        d_row = slot * seq_len + at
-        return seq, at, first, x_row, d_row
-
-    seq, at, first, x_row, d_row = places(c)
+        return seq, packed - first, first
+
+    seq, at, first = places(c)
+
+    def slot_rows(m, j):
+        return pl.ds(pl.multiple_of(m[2 * seqs + j] * seq_len, seq_len), seq_len)
+
+    def part_rows(m, s):
+        return pl.ds(pl.multiple_of((m[3 * seqs] ^ s) * rp, rp), rp)
+
+    def block_rows(p, j):
+        return pl.ds(pl.multiple_of((p * seqs + j) * per, per), per)
+
+    def near_rows(m, j):
+        shift = m[j] & 7
+        return pl.ds(pl.multiple_of(m[j] - shift, 8), seq_len + 8), shift
+
+    def pack_body(dealt, m, all_ref, *refs):
+        outs = refs[:parts]
+        source, packed, whole = refs[parts:]
+        source[...] = all_ref[...].astype(F32)
+
+        line = lax.broadcasted_iota(jnp.int32, (seq_len + 8, ds), 0)
+
+        def one(j, carry):
+            if dealt:
+                whole[:seq_len, :] = source[slot_rows(m, j), :]
+            else:
+                for p in range(dp):
+                    whole[p * per : (p + 1) * per, :] = source[block_rows(p, j), :]
+            window, shift = near_rows(m, j)
+            moved = pltpu.roll(whole[...], shift, 0)
+            packed[window, :] = jnp.where(line < shift, packed[window, :], moved)
+            return carry
+
+        lax.fori_loop(0, seqs, one, 0)
+        for s in pieces:
+            outs[s][...] = packed[part_rows(m, s), :].astype(BF16)
+
+    def pack(value, dealt):
+        own = run(
+            functools.partial(pack_body, dealt), "pack", (1,), table, [(value, None, None)],
+            [((rp, ds), BF16, None, None)] * parts,
+            [pltpu.VMEM((n, ds), F32) for n in (rows_all, rows + seq_len + 8, seq_len + 8)],
+        )
+        return [own[0]] + [by_part(own[s], s) for s in pieces[1:]]
 
     x_send = hidden_in.reshape(seqs * per, dp, ds).transpose(1, 0, 2)
     x_all = lax.all_to_all(x_send, "dp", 0, 0, tiled=True).reshape(rows_all, ds)
+    x_pieces = pack(x_all, False)
     d_send = cotangent.reshape(held * seq_len, dp, ds).transpose(1, 0, 2)
     d_all = lax.all_to_all(d_send, "dp", 0, 0, tiled=True).reshape(rows_all, ds)
-    x_pieces = [x_all[x_row]]
-    d_pieces = [d_all[d_row]]
-    for s in pieces[1:]:
-        _, _, _, other_x, other_d = places(c ^ s)
-        x_pieces.append(by_part(x_all[other_x], s))
-        d_pieces.append(by_part(d_all[other_d], s))
+    d_pieces = pack(d_all, True)
 
     def spread(vector):
         tall = vector.reshape((groups, parts, ds) + vector.shape[1:])[g]
@@ -383,8 +422,7 @@
         flops=2 * rp * (experts + 2) * parts * ds * hw,
     )
     dh = dhidden(after(meta, qkv[8]))
-    q_sum, kv_sum = reduce_groups(qkv[0:8:2], qkv[1:8:2])
-    dh_a, dh_b = reduce_groups(dh[0:8:2], dh[1:8:2])
+    q_sum, kv_sum, sent = reduce_groups(qkv[0:8:2], qkv[1:8:2])
     stats_a = sum_groups(qkv[8])
     flat_a, cols_a = gate_columns(stats_a, low_a, high_a)
 
@@ -402,7 +440,7 @@
     ins += [(cols_a, (tile, 8), lambda i, m: (i, 0))]
     ins += [(v, (tile, HD), lambda i, m: (i, 0)) for v in (cosine, sine)]
     outs = [((rp, 2 * HD), BF16, (tile, 2 * HD), lambda i, m: (i, 0))] * 2
-    q_rot, kv_rot = run(rope_body, "rope", (rp // tile,), meta, ins, outs)
+    q_rot, kv_rot = run(rope_body, "rope", (rp // tile,), after(meta, dh[0]), ins, outs)
     halo = to_next(kv_rot[rp - seq_len :])
 
     qt = 128
@@ -447,6 +485,9 @@
         flops=8 * rp * span * HD,
     )
     gm_a, gm_b = gather_groups(gated_a, gated_b)
+    dh_a, dh_b, _ = reduce_groups(
+        dh[0:8:2], dh[1:8:2], early=sent, late=(gm_a[1], gm_b[2])
+    )
 
     chunks = 2
     zr = rp // chunks // 2
@@ -551,7 +592,7 @@
 
     up_far = up((3, 1), meta)
     up_near = up((2, 0), after(meta, up_far[0]))
-    gu_a, gu_b = reduce_groups(
+    gu_a, gu_b, _ = reduce_groups(
         (up_near[2], up_far[2], up_near[0], up_far[0]),
         (up_near[3], up_far[3], up_near[1], up_far[1]),
     )
@@ -603,7 +644,7 @@
     ag_a, ag_b = gather_groups(*late)
     dots_f = dots_f.T
 
-    dots_f = sum_z(dots_f)
+    dots_f = after(sum_z(dots_f), gg_a[3], gg_b[3])
     dots_f = jnp.stack([dots_f, by_group(dots_f, 1), by_group(dots_f, 2), by_group(dots_f, 3)])
     dots_f = jnp.take(dots_f, g ^ jnp.arange(4, dtype=jnp.int32), axis=0)
     dots_f = dots_f.transpose(1, 0, 2).reshape(8, rp)
@@ -794,7 +835,7 @@
         [pltpu.VMEM((heads, tile, 2 * HD), BF16)],
         flops=2 * rp * experts * parts * ds * hw,
     )
-    dm_a, dm_b = reduce_groups(dm[0:8:2], dm[1:8:2])
+    dm_a, dm_b, _ = reduce_groups(dm[0:8:2], dm[1:8:2])
 
     def attend_back_body(m, *refs):
         q_ref, kv_ref, halo_ref, sel_ref, cols, cos_ref, sin_ref = refs[:7]
@@ -1083,7 +1124,29 @@
             flops=2 * rp * (experts + 2) * hw * parts * ds,
         )
 
-    expertin_grad = exchange(dwin(meta)).swapaxes(1, 2)
+    tiles = ff // HD
+
+    def fold_body(m, *refs):
+        add_refs, out_ref = refs[:parts], refs[parts]
+        for j in range(2):
+            total = add_refs[0][0, j].astype(F32)
+            for ref in add_refs[1:]:
+                total = total + ref[0, j].astype(F32)
+            for t in range(tiles):
+                out_ref[0, pl.ds(2 * t + j, ds, stride=2 * tiles), :] = total[
+                    :, t * HD : (t + 1) * HD
+                ]
+
+    def fold(sums):
+        got = [sums[0]] + [by_part(sums[s], s) for s in pieces[1:]]
+        spot = lambda e, m: (e, 0, 0, 0)
+        ins = [(v, (1, 2, ds, ff), spot) for v in got]
+        outs = [((experts, 2 * tiles * ds, HD), F32, (1, 2 * tiles * ds, HD), lambda e, m: (e, 0, 0))]
+        total = run(fold_body, "fold", (experts,), meta, ins, outs)[0]
+        total = total.reshape(experts, ds, tiles, 2, HD).transpose(0, 1, 3, 2, 4)
+        return total.reshape(experts, ds, 2, ff)
+
+    expertin_grad = fold(dwin(meta))
     expertout_grad = exchange(dwout(meta))
     proj_grad = exchange(dwproj(meta))
     sums = dwqkv(meta)
@@ -1106,44 +1169,49 @@
         finish_body, "finish", (1,), meta, ins, [((parts, rp, ds), BF16, None, None)]
     )[0]
 
-    place = jnp.arange(seq_len, dtype=jnp.int32).reshape(dp, 1, per)
-    seq_ids = jnp.arange(seqs, dtype=jnp.int32).reshape(1, seqs, 1)
-    valid = place < lengths.reshape(1, seqs, 1)
-    packed = jnp.where(valid, starts.reshape(1, seqs, 1) + place, 0)
-    from_row = (((packed // rp) ^ c) * rp + packed % rp).reshape(-1)
-    cot_row = (inverse.reshape(1, seqs, 1) * seq_len + place).reshape(-1)
-    valid = valid.reshape(-1)[:, None]
-
-    found_row = jnp.where(valid, from_row[:, None], -1)
-    ut = rows_all // dp
-
-    def unpack_body(m, at_ref, other_ref, *refs):
+    def unpack_body(dealt, m, other_ref, *refs):
         v_refs, out_ref = refs[:parts], refs[parts]
-        at = at_ref[...]
-        lane = lax.broadcasted_iota(jnp.int32, (ut, rp), 1)
-        total = jnp.zeros((ut, ds), F32)
+        packed, other, total, whole = refs[parts + 1 :]
         for s in pieces:
-            hot = jnp.where(at - s * rp == lane, 1.0, 0.0).astype(BF16)
-            total += nn(hot, v_refs[s][...])
-        out_ref[...] = jnp.where(at >= 0, total, other_ref[...].astype(F32)).astype(BF16)
-
-    def unpack(value, otherwise):
+            packed[part_rows(m, s), :] = v_refs[s][...].astype(F32)
+        other[...] = other_ref[...].astype(F32)
+        line = lax.broadcasted_iota(jnp.int32, (per, ds), 0)
+
+        def one(j, carry):
+            window, shift = near_rows(m, j)
+            back = jnp.where(shift == 0, 0, seq_len + 8 - shift)
+            whole[...] = pltpu.roll(packed[window, :], back, 0)
+            for p in range(dp):
+                if dealt:
+                    spot = m[2 * seqs + j] * seq_len + p * per
+                    kept = other[pl.ds(pl.multiple_of(spot, per), per), :]
+                else:
+                    kept = other[block_rows(p, j), :]
+                value = whole[p * per : (p + 1) * per, :]
+                total[block_rows(p, j), :] = jnp.where(line < m[seqs + j] - p * per, value, kept)
+            return carry
+
+        lax.fori_loop(0, seqs, one, 0)
+        out_ref[...] = total[...].astype(BF16)
+
+    def unpack(value, otherwise, dealt):
         mine_all = [value[0]] + [by_part(value[s], s) for s in pieces[1:]]
-        ins = [(found_row, (ut, 1), lambda i, m: (i, 0))]
-        ins += [(otherwise, (ut, ds), lambda i, m: (i, 0))]
-        ins += [(v, None, None) for v in mine_all]
+        ins = [(v, None, None) for v in [otherwise] + mine_all]
         spread_rows = run(
-            unpack_body, "unpack", (dp,), meta, ins,
-            [((rows_all, ds), BF16, (ut, ds), lambda i, m: (i, 0))],
-            flops=2 * rows_all * rp * parts * ds,
+            functools.partial(unpack_body, dealt), "unpack", (1,), table, ins,
+            [((rows_all, ds), BF16, None, None)],
+            [
+                pltpu.VMEM((n, ds), F32)
+                for n in (rows + seq_len + 8, rows_all, rows_all, seq_len + 8)
+            ],
         )[0]
         landed = lax.all_to_all(
             spread_rows.reshape(dp, seqs * per, ds), "dp", 0, 0, tiled=True
         )
         return landed.transpose(1, 0, 2).reshape(seqs, per, width)
 
-    layer_out = unpack(out_rows, x_all)
-    input_grad = unpack(dinput, d_all[cot_row])
+    layer_out = unpack(out_rows, x_all, False)
+    input_grad = unpack(dinput, d_all, True)
     return (
         layer_out,
         input_grad,

time: 751 us -> 741 us (0.987)
  local copies, waits for them, and re-layouts: 92.1 us -> 81.4 us
  Pallas kernels: 230 us -> 240 us
  other arithmetic: 52.2 us -> 42.8 us
    gather x5 -> x0, local copies, waits for them, and re-layouts: 21.4 us -> none  [the longest x1 8.98 us: local(): input_grad = unpack(dinput, d_all[cot_row])]
    reshape x0 -> x1, local copies, waits for them, and re-layouts: none -> 17.6 us  [fold(): total = total.reshape(experts, ds, tiles, 2, HD).transpose(0, 1, 3, 2, 4)]
    transpose x1 -> x0, other arithmetic: 9.76 us -> none  [local(): expertin_grad = exchange(dwin(meta)).swapaxes(1, 2)]
    ppermute x57, waiting for transfers between devices: 189 us -> 179 us  [by_group(): return lax.ppermute(value, 'dp', pairs)]
    pallas_call x27 -> x30, Pallas kernels: 230 us -> 240 us  [run(): pl.pallas_call(body, name=name, grid_spec=pltpu.PrefetchScalarGridSpec(nu...]
    ppermute x25, waiting for transfers between devices: 34.2 us -> 42.4 us  [by_z(): return lax.ppermute(value, 'tensor', [(a, a ^ mask) for a in range(tp)])]
    unnamed x208 -> x246, local copies, waits for them, and re-layouts: 45.1 us -> 40.2 us
  transfers between devices with their start and end apart: 108 -> 108, of which waited for: 40 -> 46; matrix products, arithmetic and copies ran while one was open for 13% -> 10% of each run, Pallas kernels for 30% -> 30%
where the time goes in v3:
time: 741 us; the launch traced here: 734 us
  Pallas kernels  240 us (32%)
  waiting for transfers between devices  233 us (31%)
  starting transfers between devices  133 us (18%)
  local copies, waits for them, and re-layouts  81.4 us (11%)
  other arithmetic  42.8 us (6%)
    pallas_call x30, Pallas kernels, run(): pl.pallas_call(body, name=name, grid_spec=pltpu.PrefetchScalarGridSpec(nu...  240 us
    ppermute x57, waiting for transfers between devices, by_group(): return lax.ppermute(value, 'dp', pairs)  179 us
    ppermute x57, starting transfers between devices, by_group(): return lax.ppermute(value, 'dp', pairs)  66 us
    ppermute x25, waiting for transfers between devices, by_z(): return lax.ppermute(value, 'tensor', [(a, a ^ mask) for a in range(tp)])  42.4 us
    ppermute x25, starting transfers between devices, by_z(): return lax.ppermute(value, 'tensor', [(a, a ^ mask) for a in range(tp)])  41 us
    unnamed x246, local copies, waits for them, and re-layouts  40.2 us
    reshape x1, local copies, waits for them, and re-layouts, fold(): total = total.reshape(experts, ds, tiles, 2, HD).transpose(0, 1, 3, 2, 4)  17.6 us
  transfers between devices with their start and end apart: 108, of which 46 were waited for; matrix products, arithmetic and copies ran while one was open for 10% of the time, Pallas kernels for 30%

profile of v3, /device:TPU:0, one launch (start us, length us, event | category | flops | bytes accessed | tf_op | source)
XLA Modules:
  0.0 734.4 jit_solution(5190470030275034487)
XLA Ops:
  3.4 5.2 all-to-all-start
  9.7 5.9 copy.181
  23.9 3.9 all-to-all-start.1
  27.8 4.0 pack.2
  39.5 8.6 %qkv.1 = (bf16[768,256]{1,0:T(8,128)(2,1)}, bf16[768,256]{1,0:T(8,128)(2,1)}, bf16[768,256]{1,0:T(8,128)(2,1)}, bf16[768,256]{1,0:T(8,128)(2,1)}, bf16[768,256]{...) custom-call(s32[20]{0:T(128)} %stack.132.m, ...), custom_call_target="tpu_custom_call" | custom-call | flops 2415919104 | bytes 7137280 | tf_op jit(solution)/shard_map/qkv/pallas_call | solution.py:61
  57.7 4.0 pack.3
  66.2 5.5 collective-permute-done.6
  75.8 7.6 %collective-permute-done.5.a1 = bf16[768,256]{1,0:T(8,128)(2,1)S(1)} collective-permute-done((bf16[768,256]{1,0:T(8,128)(2,1)}, bf16[768,256]{1,0:T(8,128)(2,1)S(1)}, u32[]{:S(2)}, u32[]{:S(2)}) %collective-permute-start.5) | collective-permute-done | bytes 393248 | tf_op jit(solution)/shard_map/ppermute | solution.py:160
  85.4 12.0 %dhidden.1 = (bf16[192,1408]{1,0:T(8,128)(2,1)}, bf16[192,1408]{1,0:T(8,128)(2,1)}, bf16[192,1408]{1,0:T(8,128)(2,1)}, bf16[192,1408]{1,0:T(8,128)(2,1)}, bf16[1...) custom-call(s32[20]{0:T(128)} %stack.132.m, ...), custom_call_target="tpu_custom_call" | custom-call | flops 4429185024 | bytes 11714560 | tf_op jit(solution)/shard_map/dhidden/pallas_call | solution.py:61
  98.4 4.6 rope.1
  106.8 7.9 %attend.1 = (bf16[768,128]{1,0:T(8,128)(2,1)}, bf16[768,128]{1,0:T(8,128)(2,1)}, bf16[768,128]{1,0:T(8,128)(2,1)}, bf16[768,128]{1,0:T(8,128)(2,1)}) custom-call(s32[20]{0:T(128)} %stack.132.m, bf16[768,256]{1,0:T(8,128)(2,1)} %get-tuple-element.129.q_ref.refs_0_, bf16[768,256]{1,0:T(8,128)(2,1)} %get-tuple-element.130.kv_ref.refs_1_, ...), custom_call_target="tpu_custom_call" | custom-call | flops 301989888 | bytes 1753088 | tf_op jit(solution)/shard_map/attend/pallas_call | solution.py:61
  118.9 3.9 collective-permute-done.14.refs_1_
  127.4 3.3 collective-permute-done.16.refs_3_
  132.1 6.7 proj.2
  142.0 6.7 proj.3
  149.3 3.7 collective-permute-start.22
  156.1 8.5 %collective-permute-start.25 = (bf16[2,192,256]{2,1,0:T(8,128)(2,1)S(1)}, bf16[2,192,256]{2,1,0:T(8,128)(2,1)S(1)}, u32[]{:S(2)}, u32[]{:S(2)}) collective-permute-start(bf16[2,192,256]{2,1,0:T(8,128)(2,1)S(1)} %add_convert_fusion.19), channel_id=1, source_target_pairs={{0,3},{1,2},{2,1},{3,0},{4,7},{5,6},{6,5},{7,4},{8,11},{9,10},{10,... | collective-permute-start | bytes 589832 | tf_op jit(solution)/shard_map/ppermute | solution.py:175
  164.8 3.8 collective-permute-done.25
  176.2 4.4 norm.1
  180.6 10.3 %up.2 = (bf16[2,192,1408]{2,1,0:T(8,128)(2,1)}, bf16[2,192,1408]{2,1,0:T(8,128)(2,1)}, bf16[2,192,1408]{2,1,0:T(8,128)(2,1)}, bf16[2,192,1408]{2,1,0:T(8,128)(2,1)}) custom-call(s32[20]{0:T(128)} %stack.132.m, bf16[2,768,256]{2,1,0:T(8,128)(2,1)} %get-tuple-element.137.refs_0_.refs_1_, bf16[2,768,256]{2,1,0:T(8,128)(2,1)} %get-tuple-element.137.refs_0_.refs_1_, ...), custom_call_target="tpu_custom_call" | custom-call | flops 4429185024 | bytes 17481728 | tf_op jit(solution)/shard_map/up/pallas_call | solution.py:61
  195.6 19.5 %collective-permute-done.40 = f32[8,768]{1,0:T(8,128)S(1)} collective-permute-done((f32[8,768]{1,0:T(8,128)S(1)}, f32[8,768]{1,0:T(8,128)S(1)}, u32[]{:S(2)}, u32[]{:S(2)}) %collective-permute-start.40) | collective-permute-done | bytes 24608 | tf_op jit(solution)/shard_map/ppermute | solution.py:160
  216.1 10.5 %up.3 = (bf16[2,192,1408]{2,1,0:T(8,128)(2,1)}, bf16[2,192,1408]{2,1,0:T(8,128)(2,1)}, bf16[2,192,1408]{2,1,0:T(8,128)(2,1)}, bf16[2,192,1408]{2,1,0:T(8,128)(2,1)}) custom-call(s32[20]{0:T(128)} %stack.132.m, bf16[2,768,256]{2,1,0:T(8,128)(2,1)} %get-tuple-element.137.refs_0_.refs_1_, bf16[2,768,256]{2,1,0:T(8,128)(2,1)} %get-tuple-element.137.refs_0_.refs_1_, ...), custom_call_target="tpu_custom_call" | custom-call | flops 4429185024 | bytes 17481728 | tf_op jit(solution)/shard_map/up/pallas_call | solution.py:61
  237.9 49.5 %collective-permute-done.38.refs_10_ = bf16[192,1408]{1,0:T(8,128)(2,1)} collective-permute-done((bf16[192,1408]{1,0:T(8,128)(2,1)}, bf16[192,1408]{1,0:T(8,128)(2,1)}, u32[]{:S(2)}, u32[]{:S(2)}) %collective-permute-start.38) | collective-permute-done | bytes 540704 | tf_op jit(solution)/shard_map/ppermute | solution.py:160
  289.1 8.2 %mid.1 = (bf16[192,1408]{1,0:T(8,128)(2,1)}, bf16[192,1408]{1,0:T(8,128)(2,1)}, bf16[2,192,1408]{2,1,0:T(8,128)(2,1)}, bf16[2,192,1408]{2,1,0:T(8,128)(2,1)}, f32[192,8]{1,0:T(8,128)}) custom-call(s32[20]{0:T(128)} %stack.132.m, bf16[2,192,1408]{2,1,0:T(8,128)(2,1)} %get-tuple-element.140.refs_0_, bf16[2,192,1408]{2,1,0:T(8,128)(2,1)} %copy-done.21, ...), custom_call_target="tpu_custom_call" | custom-call | bytes 13006848 | tf_op jit(solution)/shard_map/mid/pallas_call | solution.py:61
  303.7 20.7 %collective-permute-done.42.refs_1_ = bf16[2,192,1408]{2,1,0:T(8,128)(2,1)S(1)} collective-permute-done((bf16[2,192,1408]{2,1,0:T(8,128)(2,1)}, bf16[2,192,1408]{2,1,0:T(8,128)(2,1)S(1)}, u32[]{:S(2)}, u32[]{:S(2)}) %collective-permute-start.42) | collective-permute-done | bytes 1081376 | tf_op jit(solution)/shard_map/ppermute | solution.py:160
  326.4 21.2 %collective-permute-done.47.refs_3_.refs_5_ = bf16[2,192,1408]{2,1,0:T(8,128)(2,1)} collective-permute-done((bf16[2,192,1408]{2,1,0:T(8,128)(2,1)}, bf16[2,192,1408]{2,1,0:T(8,128)(2,1)}, u32[]{:S(2)}, u32[]{:S(2)}) %collective-permute-start.47) | collective-permute-done | bytes 1081376 | tf_op jit(solution)/shard_map/ppermute | solution.py:160
  349.8 11.0 %dx.2 = (bf16[2,192,256]{2,1,0:T(8,128)(2,1)}, bf16[2,192,256]{2,1,0:T(8,128)(2,1)}) custom-call(s32[20]{0:T(128)} %stack.132.m, bf16[2,192,1408]{2,1,0:T(8,128)(2,1)} %get-tuple-element.166.refs_0_, bf16[2,192,1408]{2,1,0:T(8,128)(2,1)} %copy-done.18, bf16[2,192,1408]{2,1,0:T(8,128)(2,1)} %get-tuple-element.169.refs_2_.refs_4_, ...), custom_call_target="tpu_custom_call" | custom-call | flops 4429185024 | bytes 16302080 | tf_op jit(solution)/shard_map/dx/pallas_call | solution.py:61
  361.9 4.8 collective-permute-done.56
  370.7 5.4 collective-permute-done.57
  379.4 7.0 collective-permute-done.59.refs_1_.refs_3_
  389.2 3.7 collective-permute-done.60.refs_3_.refs_7_
  393.2 3.3 collective-permute-done.45.refs_2_
  405.7 10.8 %down.1 = (bf16[2,384,256]{2,1,0:T(8,128)(2,1)}, bf16[2,384,256]{2,1,0:T(8,128)(2,1)}) custom-call(s32[20]{0:T(128)} %stack.132.m, bf16[192,1408]{1,0:T(8,128)(2,1)} %get-tuple-element.167.refs_0_, bf16[192,1408]{1,0:T(8,128)(2,1)} %collective-permute-done.44.refs_1_, bf16[192,1408]{1,0:T(8,128)(2,1)} %copy-done.113, bf16[192,1408]{1,0:T(8,128)(2,1)} %copy-done.115, ...), custom_call_target="tpu_custom_call" | custom-call | flops 4429185024 | bytes 10977280 | tf_op jit(solution)/shard_map/down/pallas_call | solution.py:61
  416.9 19.3 %dwin.1 = (bf16[4,2,256,1408]{3,2,1,0:T(8,128)(2,1)}, bf16[4,2,256,1408]{3,2,1,0:T(8,128)(2,1)}) custom-call(s32[20]{0:T(128)} %stack.132.m, bf16[2,192,1408]{2,1,0:T(8,128)(2,1)} %get-tuple-element.166.refs_0_, bf16[2,192,1408]{2,1,0:T(8,128)(2,1)} %copy-done.18, bf16[2,192,1408]{2,1,0:T(8,128)(2,1)} %copy-done.17, ...), custom_call_target="tpu_custom_call" | custom-call | flops 8858370048 | bytes 20996096 | tf_op jit(solution)/shard_map/dwin/pallas_call | solution.py:61
  436.2 11.3 %dx.3 = (bf16[2,192,256]{2,1,0:T(8,128)(2,1)}, bf16[2,192,256]{2,1,0:T(8,128)(2,1)}) custom-call(s32[20]{0:T(128)} %stack.132.m, bf16[2,192,1408]{2,1,0:T(8,128)(2,1)} %copy-done.17, bf16[2,192,1408]{2,1,0:T(8,128)(2,1)} %collective-permute-done.59.refs_1_.refs_3_, bf16[2,192,1408]{2,1,0:T(8,128)(2,1)} %copy-done.19, bf16[2,192,1408]{2,1,0:T(8,128)(2,1)} %copy-done.20, ...), custom_call_target="tpu_custom_call" | custom-call | flops 4429185024 | bytes 16302080 | tf_op jit(solution)/shard_map/dx/pallas_call | solution.py:61
  450.6 3.6 collective-permute-done.61
  456.2 6.6 collective-permute-done.62
  469.3 6.6 norm_back.1
  475.9 6.0 dmix.1
  487.0 3.0 collective-permute-done.70
  503.1 14.4 %attend_back.1 = (bf16[768,256]{1,0:T(8,128)(2,1)}, f32[768,256]{1,0:T(8,128)}, f32[256,256]{1,0:T(8,128)}, f32[8,768]{1,0:T(8,128)}) custom-call(s32[20]{0:T(128)} %stack.132.m, bf16[768,256]{1,0:T(8,128)(2,1)} %get-tuple-element.129.q_ref.refs_0_, bf16[768,256]{1,0:T(8,128)(2,1)} %get-tuple-element.130.kv_ref.refs_1_, bf16[256,256]{1,0:T(8,128)(2,1)} %copy-done.44, ...), custom_call_target="tpu_custom_call" | custom-call | flops 754974720 | bytes 4792320 | tf_op jit(solution)/shard_map/attend_back/pallas_call | solution.py:61
  518.8 10.7 %dwout.1 = (bf16[4,1408,256]{2,1,0:T(8,128)(2,1)}, bf16[4,1408,256]{2,1,0:T(8,128)(2,1)}) custom-call(s32[20]{0:T(128)} %stack.132.m, bf16[192,1408]{1,0:T(8,128)(2,1)} %get-tuple-element.167.refs_0_, bf16[192,1408]{1,0:T(8,128)(2,1)} %collective-permute-done.44.refs_1_, bf16[192,1408]{1,0:T(8,128)(2,1)} %copy-done.113, bf16[192,1408]{1,0:T(8,128)(2,1)} %copy-done.115, ...), custom_call_target="tpu_custom_call" | custom-call | flops 4429185024 | bytes 10903552 | tf_op jit(solution)/shard_map/dwout/pallas_call | solution.py:61
  529.9 7.5 %dwproj.1 = (bf16[4,512,256]{2,1,0:T(8,128)(2,1)}, bf16[4,512,256]{2,1,0:T(8,128)(2,1)}) custom-call(s32[20]{0:T(128)} %stack.132.m, bf16[768,128]{1,0:T(8,128)(2,1)} %get-tuple-element.131.refs_0_, bf16[768,128]{1,0:T(8,128)(2,1)} %copy-done.28, bf16[768,128]{1,0:T(8,128)(2,1)} %copy-done.30, bf16[768,128]{1,0:T(8,128)(2,1)} %copy-done.32, ...), custom_call_target="tpu_custom_call" | custom-call | flops 1610612736 | bytes 4481024 | tf_op jit(solution)/shard_map/dwproj/pallas_call | solution.py:61
  538.2 3.8 dkv.1
  557.3 3.3 finish.1
  569.5 5.3 collective-permute-done.80.refs_6_
  575.9 3.6 collective-permute-done.79.refs_5_
  581.3 4.0 collective-permute-done.81.refs_7_
  586.1 6.4 dattn.2
  594.4 4.4 unpack.2
  598.8 3.8 all-to-all-start.2
  602.6 6.5 dattn.3
  612.3 4.6 collective-permute-done.85
  622.0 4.8 collective-permute-start.84
  627.6 3.8 collective-permute-start.87
  631.3 9.4 %dwqkv.1 = (bf16[4,256,512]{2,1,0:T(8,128)(2,1)}, bf16[4,256,512]{2,1,0:T(8,128)(2,1)}, bf16[2,256,512]{2,1,0:T(8,128)(2,1)}, bf16[2,256,512]{2,1,0:T(8,128)(2,1)}) custom-call(s32[20]{0:T(128)} %stack.132.m, bf16[768,256]{1,0:T(8,128)(2,1)} %get-tuple-element.191.refs_0_, bf16[768,256]{1,0:T(8,128)(2,1)} %copy-done.11, bf16[768,256]{1,0:T(8,128)(2,1)} %copy-done.12, ...), custom_call_target="tpu_custom_call" | custom-call | flops 2415919104 | bytes 7102464 | tf_op jit(solution)/shard_map/dwqkv/pallas_call | solution.py:61
  641.5 6.1 norm_back_first.1
  664.0 4.4 unpack.3
  668.4 3.8 all-to-all-start.3
  672.2 5.9 convert_add_fusion
  679.8 7.8 %all-to-all-done.3 = bf16[8,256,256]{2,1,0:T(8,128)(2,1)S(1)} async-done(((bf16[8,256,256]{2,1,0:T(8,128)(2,1)}), bf16[8,256,256]{2,1,0:T(8,128)(2,1)S(1)}, u32[]{:S(2)}, u32[]{:S(2)}) %all-to-all-start.3) | async-done | bytes 1048608 | tf_op jit(solution)/shard_map/all_to_all | solution.py:1208
  689.5 9.6 %fold.1 = f32[4,5632,128]{2,1,0:T(8,128)} custom-call(s32[20]{0:T(128)} %stack.132.m, bf16[4,2,256,1408]{3,2,1,0:T(8,128)(2,1)} %get-tuple-element.211.refs_0_, bf16[4,2,256,1408]{3,2,1,0:T(8,128)(2,1)} %collective-permute-done.102.refs_1_), custom_call_target="tpu_custom_call" | custom-call | bytes 23068672 | tf_op jit(solution)/shard_map/fold/pallas_call | solution.py:61
  699.1 17.6 %copy.169 = f32[4,256,11,2,128]{1,4,2,3,0:T(8,128)} copy(f32[4,256,11,2,128]{4,3,2,1,0:T(2,128)} %bitcast.111) | data formatting | bytes 23068672 | tf_op jit(solution)/shard_map/reshape | solution.py:1146
  716.7 17.5 %copy.171 = f32[4,256,2,1408]{3,2,1,0:T(2,128)} copy(f32[4,256,2,1408]{1,3,2,0:T(8,128)} %bitcast.112) | data formatting | bytes 23068672
  (562 shorter events, 210.3 us)
Async XLA Ops:
  3.4 20.6 %all-to-all-start = ((bf16[8,256,256]{2,1,0:T(8,128)(2,1)}), bf16[8,256,256]{2,1,0:T(8,128)(2,1)S(1)}, u32[]{:S(2)}, u32[]{:S(2)}) async-start(bf16[8,256,256]{2,1,0:T(8,128)(2,1)} %bitcast.110), calls=%async_computation | async-start | bytes 2097152 | tf_op jit(solution)/shard_map/all_to_all | solution.py:293
  8.6 30.1 %collective-permute-start.1 = (bf16[4,256,512]{2,1,0:T(8,128)(2,1)}, bf16[4,256,512]{2,1,0:T(8,128)(2,1)}, u32[]{:S(2)}, u32[]{:S(2)}) collective-permute-start(bf16[4,256,512]{2,1,0:T(8,128)(2,1)} %refs_9_.7), channel_id=1, source_target_pairs={{0,4},{4,0},{8,12},{12,8},{16,20},{20,16},{24,28},{28,24},{1,5},{5... | collective-permute-start | bytes 3145736 | tf_op jit(solution)/shard_map/ppermute | solution.py:164
  9.2 29.4 %collective-permute-start.2 = (bf16[2,256,512]{2,1,0:T(8,128)(2,1)}, bf16[2,256,512]{2,1,0:T(8,128)(2,1)}, u32[]{:S(2)}, u32[]{:S(2)}) collective-permute-start(bf16[2,256,512]{2,1,0:T(8,128)(2,1)} %refs_11_.3), channel_id=1, source_target_pairs={{0,4},{4,0},{8,12},{12,8},{16,20},{20,16},{24,28},{28,24},{1,5},{5... | collective-permute-start | bytes 1572872 | tf_op jit(solution)/shard_map/ppermute | solution.py:164
  9.3 74.5 %collective-permute-start.4 = (bf16[4,1408,256]{2,1,0:T(8,128)(2,1)}, bf16[4,1408,256]{2,1,0:T(8,128)(2,1)}, u32[]{:S(2)}, u32[]{:S(2)}) collective-permute-start(bf16[4,1408,256]{2,1,0:T(8,128)(2,1)} %refs_8_.1), channel_id=1, source_target_pairs={{0,4},{4,0},{8,12},{12,8},{16,20},{20,16},{24,28},{28,24},{1,5},{5... | collective-permute-start | bytes 8650760 | tf_op jit(solution)/shard_map/ppermute | solution.py:164
  15.6 165.0 %collective-permute-start.27 = (bf16[4,2,256,1408]{3,2,1,0:T(8,128)(2,1)}, bf16[4,2,256,1408]{3,2,1,0:T(8,128)(2,1)}, u32[]{:S(2)}, u32[]{:S(2)}) collective-permute-start(bf16[4,2,256,1408]{3,2,1,0:T(8,128)(2,1)} %bitcast.108.refs_2_.refs_4_), channel_id=1, source_target_pairs={{0,4},{4,0},{8,12},{12,8},{16,20},{20,16},{24,28},{28,24},{1,5},{5... | collective-permute-start | bytes 17301512 | tf_op jit(solution)/shard_map/ppermute | solution.py:164
  23.9 32.8 %all-to-all-start.1 = ((bf16[8,256,256]{2,1,0:T(8,128)(2,1)}), bf16[8,256,256]{2,1,0:T(8,128)(2,1)S(1)}, u32[]{:S(2)}, u32[]{:S(2)}) async-start(bf16[8,256,256]{2,1,0:T(8,128)(2,1)} %bitcast.109), calls=%async_computation.1 | async-start | bytes 2097152 | tf_op jit(solution)/shard_map/all_to_all | solution.py:296
  38.5 78.7 %collective-permute-start.20 = (bf16[4,512,256]{2,1,0:T(8,128)(2,1)S(1)}, bf16[4,512,256]{2,1,0:T(8,128)(2,1)S(1)}, u32[]{:S(2)}, u32[]{:S(2)}) collective-permute-start(bf16[4,512,256]{2,1,0:T(8,128)(2,1)S(1)} %copy-done.3), channel_id=1, source_target_pairs={{0,4},{4,0},{8,12},{12,8},{16,20},{20,16},{24,28},{28,24},{1,5},{5... | collective-permute-start | bytes 3145736 | tf_op jit(solution)/shard_map/ppermute | solution.py:164
  75.3 22.0 %collective-permute-start.10 = (bf16[768,256]{1,0:T(8,128)(2,1)}, bf16[768,256]{1,0:T(8,128)(2,1)S(1)}, u32[]{:S(2)}, u32[]{:S(2)}) collective-permute-start(bf16[768,256]{1,0:T(8,128)(2,1)} %get-tuple-element.128), channel_id=1, source_target_pairs={{0,16},{4,20},{8,24},{12,28},{16,0},{20,4},{24,8},{28,12},{1,17},{... | collective-permute-start | bytes 1179656 | tf_op jit(solution)/shard_map/ppermute | solution.py:160
  83.4 14.0 %collective-permute-start.7 = (bf16[768,256]{1,0:T(8,128)(2,1)}, bf16[768,256]{1,0:T(8,128)(2,1)S(1)}, u32[]{:S(2)}, u32[]{:S(2)}) collective-permute-start(bf16[768,256]{1,0:T(8,128)(2,1)} %add_convert_fusion.7), channel_id=1, source_target_pairs={{0,16},{4,20},{8,24},{12,28},{16,0},{20,4},{24,8},{28,12},{1,17},{... | collective-permute-start | bytes 1179656 | tf_op jit(solution)/shard_map/ppermute | solution.py:160
  83.7 13.7 %collective-permute-start.9 = (bf16[768,256]{1,0:T(8,128)(2,1)S(1)}, bf16[768,256]{1,0:T(8,128)(2,1)S(1)}, u32[]{:S(2)}, u32[]{:S(2)}) collective-permute-start(bf16[768,256]{1,0:T(8,128)(2,1)S(1)} %add_convert_fusion.6), channel_id=1, source_target_pairs={{0,8},{4,12},{8,0},{12,4},{16,24},{20,28},{24,16},{28,20},{1,9},{5... | collective-permute-start | bytes 1179656 | tf_op jit(solution)/shard_map/ppermute | solution.py:160
  140.3 51.1 %collective-permute-start.35 = (bf16[192,1408]{1,0:T(8,128)(2,1)}, bf16[192,1408]{1,0:T(8,128)(2,1)S(1)}, u32[]{:S(2)}, u32[]{:S(2)}) collective-permute-start(bf16[192,1408]{1,0:T(8,128)(2,1)} %get-tuple-element.157), channel_id=1, source_target_pairs={{0,8},{4,12},{8,0},{12,4},{16,24},{20,28},{24,16},{28,20},{1,9},{5... | collective-permute-start | bytes 1622024 | tf_op jit(solution)/shard_map/ppermute | solution.py:160
  149.3 15.3 %collective-permute-start.22 = (bf16[2,192,256]{2,1,0:T(8,128)(2,1)S(1)}, bf16[2,192,256]{2,1,0:T(8,128)(2,1)S(1)}, u32[]{:S(2)}, u32[]{:S(2)}) collective-permute-start(bf16[2,192,256]{2,1,0:T(8,128)(2,1)S(1)} %add_convert_fusion.21), channel_id=1, source_target_pairs={{0,3},{1,2},{2,1},{3,0},{4,7},{5,6},{6,5},{7,4},{8,11},{9,10},{10,... | collective-permute-start | bytes 589832 | tf_op jit(solution)/shard_map/ppermute | solution.py:175
  156.1 12.5 %collective-permute-start.25 = (bf16[2,192,256]{2,1,0:T(8,128)(2,1)S(1)}, bf16[2,192,256]{2,1,0:T(8,128)(2,1)S(1)}, u32[]{:S(2)}, u32[]{:S(2)}) collective-permute-start(bf16[2,192,256]{2,1,0:T(8,128)(2,1)S(1)} %add_convert_fusion.19), channel_id=1, source_target_pairs={{0,3},{1,2},{2,1},{3,0},{4,7},{5,6},{6,5},{7,4},{8,11},{9,10},{10,... | collective-permute-start | bytes 589832 | tf_op jit(solution)/shard_map/ppermute | solution.py:175
  170.6 61.6 %collective-permute-start.34 = (bf16[192,1408]{1,0:T(8,128)(2,1)}, bf16[192,1408]{1,0:T(8,128)(2,1)S(1)}, u32[]{:S(2)}, u32[]{:S(2)}) collective-permute-start(bf16[192,1408]{1,0:T(8,128)(2,1)} %get-tuple-element.155), channel_id=1, source_target_pairs={{0,8},{4,12},{8,0},{12,4},{16,24},{20,28},{24,16},{28,20},{1,9},{5... | collective-permute-start | bytes 1622024 | tf_op jit(solution)/shard_map/ppermute | solution.py:160
  172.6 21.4 %collective-permute-start.36 = (bf16[192,1408]{1,0:T(8,128)(2,1)}, bf16[192,1408]{1,0:T(8,128)(2,1)S(1)}, u32[]{:S(2)}, u32[]{:S(2)}) collective-permute-start(bf16[192,1408]{1,0:T(8,128)(2,1)} %get-tuple-element.159), channel_id=1, source_target_pairs={{0,16},{4,20},{8,24},{12,28},{16,0},{20,4},{24,8},{28,12},{1,17},{... | collective-permute-start | bytes 1622024 | tf_op jit(solution)/shard_map/ppermute | solution.py:160
  174.7 58.4 %collective-permute-start.39 = (bf16[192,1408]{1,0:T(8,128)(2,1)}, bf16[192,1408]{1,0:T(8,128)(2,1)}, u32[]{:S(2)}, u32[]{:S(2)}) collective-permute-start(bf16[192,1408]{1,0:T(8,128)(2,1)} %get-tuple-element.163), channel_id=1, source_target_pairs={{0,16},{4,20},{8,24},{12,28},{16,0},{20,4},{24,8},{28,12},{1,17},{... | collective-permute-start | bytes 1622024 | tf_op jit(solution)/shard_map/ppermute | solution.py:160
  190.9 35.7 %collective-permute-start.29 = (bf16[2,192,1408]{2,1,0:T(8,128)(2,1)}, bf16[2,192,1408]{2,1,0:T(8,128)(2,1)S(1)}, u32[]{:S(2)}, u32[]{:S(2)}) collective-permute-start(bf16[2,192,1408]{2,1,0:T(8,128)(2,1)} %get-tuple-element.138), channel_id=1, source_target_pairs={{0,8},{4,12},{8,0},{12,4},{16,24},{20,28},{24,16},{28,20},{1,9},{5... | collective-permute-start | bytes 3244040 | tf_op jit(solution)/shard_map/ppermute | solution.py:160
  192.5 22.7 %collective-permute-start.40 = (f32[8,768]{1,0:T(8,128)S(1)}, f32[8,768]{1,0:T(8,128)S(1)}, u32[]{:S(2)}, u32[]{:S(2)}) collective-permute-start(f32[8,768]{1,0:T(8,128)S(1)} %copy-done.91), channel_id=1, source_target_pairs={{0,8},{4,12},{8,0},{12,4},{16,24},{20,28},{24,16},{28,20},{1,9},{5... | collective-permute-start | bytes 73736 | tf_op jit(solution)/shard_map/ppermute | solution.py:160
  194.0 36.4 %collective-permute-start.31 = (bf16[2,192,1408]{2,1,0:T(8,128)(2,1)}, bf16[2,192,1408]{2,1,0:T(8,128)(2,1)S(1)}, u32[]{:S(2)}, u32[]{:S(2)}) collective-permute-start(bf16[2,192,1408]{2,1,0:T(8,128)(2,1)} %get-tuple-element.145), channel_id=1, source_target_pairs={{0,16},{4,20},{8,24},{12,28},{16,0},{20,4},{24,8},{28,12},{1,17},{... | collective-permute-start | bytes 3244040 | tf_op jit(solution)/shard_map/ppermute | solution.py:160
  215.1 21.2 %collective-permute-start.37 = (bf16[192,1408]{1,0:T(8,128)(2,1)}, bf16[192,1408]{1,0:T(8,128)(2,1)}, u32[]{:S(2)}, u32[]{:S(2)}) collective-permute-start(bf16[192,1408]{1,0:T(8,128)(2,1)} %add_convert_fusion.3), channel_id=1, source_target_pairs={{0,16},{4,20},{8,24},{12,28},{16,0},{20,4},{24,8},{28,12},{1,17},{... | collective-permute-start | bytes 1622024 | tf_op jit(solution)/shard_map/ppermute | solution.py:160
  230.3 57.1 %collective-permute-start.28 = (bf16[2,192,1408]{2,1,0:T(8,128)(2,1)}, bf16[2,192,1408]{2,1,0:T(8,128)(2,1)S(1)}, u32[]{:S(2)}, u32[]{:S(2)}) collective-permute-start(bf16[2,192,1408]{2,1,0:T(8,128)(2,1)} %get-tuple-element.141), channel_id=1, source_target_pairs={{0,8},{4,12},{8,0},{12,4},{16,24},{20,28},{24,16},{28,20},{1,9},{5... | collective-permute-start | bytes 3244040 | tf_op jit(solution)/shard_map/ppermute | solution.py:160
  232.2 55.3 %collective-permute-start.33 = (bf16[2,192,1408]{2,1,0:T(8,128)(2,1)}, bf16[2,192,1408]{2,1,0:T(8,128)(2,1)S(1)}, u32[]{:S(2)}, u32[]{:S(2)}) collective-permute-start(bf16[2,192,1408]{2,1,0:T(8,128)(2,1)} %get-tuple-element.146), channel_id=1, source_target_pairs={{0,16},{4,20},{8,24},{12,28},{16,0},{20,4},{24,8},{28,12},{1,17},{... | collective-permute-start | bytes 3244040 | tf_op jit(solution)/shard_map/ppermute | solution.py:160
  233.1 54.3 %collective-permute-start.30 = (bf16[2,192,1408]{2,1,0:T(8,128)(2,1)}, bf16[2,192,1408]{2,1,0:T(8,128)(2,1)S(1)}, u32[]{:S(2)}, u32[]{:S(2)}) collective-permute-start(bf16[2,192,1408]{2,1,0:T(8,128)(2,1)} %add_convert_fusion.1), channel_id=1, source_target_pairs={{0,16},{4,20},{8,24},{12,28},{16,0},{20,4},{24,8},{28,12},{1,17},{... | collective-permute-start | bytes 3244040 | tf_op jit(solution)/shard_map/ppermute | solution.py:160
  234.2 53.3 %collective-permute-start.32 = (bf16[2,192,1408]{2,1,0:T(8,128)(2,1)}, bf16[2,192,1408]{2,1,0:T(8,128)(2,1)}, u32[]{:S(2)}, u32[]{:S(2)}) collective-permute-start(bf16[2,192,1408]{2,1,0:T(8,128)(2,1)} %add_convert_fusion), channel_id=1, source_target_pairs={{0,8},{4,12},{8,0},{12,4},{16,24},{20,28},{24,16},{28,20},{1,9},{5... | collective-permute-start | bytes 3244040 | tf_op jit(solution)/shard_map/ppermute | solution.py:160
  236.3 51.1 %collective-permute-start.38 = (bf16[192,1408]{1,0:T(8,128)(2,1)}, bf16[192,1408]{1,0:T(8,128)(2,1)}, u32[]{:S(2)}, u32[]{:S(2)}) collective-permute-start(bf16[192,1408]{1,0:T(8,128)(2,1)} %add_convert_fusion.2), channel_id=1, source_target_pairs={{0,8},{4,12},{8,0},{12,4},{16,24},{20,28},{24,16},{28,20},{1,9},{5... | collective-permute-start | bytes 1622024 | tf_op jit(solution)/shard_map/ppermute | solution.py:160
  297.4 27.0 %collective-permute-start.42 = (bf16[2,192,1408]{2,1,0:T(8,128)(2,1)}, bf16[2,192,1408]{2,1,0:T(8,128)(2,1)S(1)}, u32[]{:S(2)}, u32[]{:S(2)}) collective-permute-start(bf16[2,192,1408]{2,1,0:T(8,128)(2,1)} %get-tuple-element.166.refs_0_), channel_id=1, source_target_pairs={{0,8},{4,12},{8,0},{12,4},{16,24},{20,28},{24,16},{28,20},{1,9},{5... | collective-permute-start | bytes 3244040 | tf_op jit(solution)/shard_map/ppermute | solution.py:160
  298.0 26.9 %collective-permute-start.43 = (bf16[2,192,1408]{2,1,0:T(8,128)(2,1)}, bf16[2,192,1408]{2,1,0:T(8,128)(2,1)S(1)}, u32[]{:S(2)}, u32[]{:S(2)}) collective-permute-start(bf16[2,192,1408]{2,1,0:T(8,128)(2,1)} %get-tuple-element.166.refs_0_), channel_id=1, source_target_pairs={{0,16},{4,20},{8,24},{12,28},{16,0},{20,4},{24,8},{28,12},{1,17},{... | collective-permute-start | bytes 3244040 | tf_op jit(solution)/shard_map/ppermute | solution.py:160
  299.2 48.4 %collective-permute-start.47 = (bf16[2,192,1408]{2,1,0:T(8,128)(2,1)}, bf16[2,192,1408]{2,1,0:T(8,128)(2,1)}, u32[]{:S(2)}, u32[]{:S(2)}) collective-permute-start(bf16[2,192,1408]{2,1,0:T(8,128)(2,1)} %get-tuple-element.169.refs_2_.refs_4_), channel_id=1, source_target_pairs={{0,8},{4,12},{8,0},{12,4},{16,24},{20,28},{24,16},{28,20},{1,9},{5... | collective-permute-start | bytes 3244040 | tf_op jit(solution)/shard_map/ppermute | solution.py:160
  300.7 47.0 %collective-permute-start.48 = (bf16[2,192,1408]{2,1,0:T(8,128)(2,1)}, bf16[2,192,1408]{2,1,0:T(8,128)(2,1)S(1)}, u32[]{:S(2)}, u32[]{:S(2)}) collective-permute-start(bf16[2,192,1408]{2,1,0:T(8,128)(2,1)} %get-tuple-element.169.refs_2_.refs_4_), channel_id=1, source_target_pairs={{0,16},{4,20},{8,24},{12,28},{16,0},{20,4},{24,8},{28,12},{1,17},{... | collective-permute-start | bytes 3244040 | tf_op jit(solution)/shard_map/ppermute | solution.py:160
  303.3 57.6 %collective-permute-start.64 = (f32[8,192]{0,1:T(8,128)}, f32[8,192]{0,1:T(8,128)}, u32[]{:S(2)}, u32[]{:S(2)}) collective-permute-start(f32[8,192]{0,1:T(8,128)} %bitcast.139), channel_id=1, source_target_pairs={{0,1},{1,0},{2,3},{3,2},{4,5},{5,4},{6,7},{7,6},{8,9},{9,8},{10,11... | collective-permute-start | bytes 18440 | tf_op jit(solution)/shard_map/ppermute | solution.py:175
  324.9 52.5 %collective-permute-start.44 = (bf16[192,1408]{1,0:T(8,128)(2,1)}, bf16[192,1408]{1,0:T(8,128)(2,1)}, u32[]{:S(2)}, u32[]{:S(2)}) collective-permute-start(bf16[192,1408]{1,0:T(8,128)(2,1)} %get-tuple-element.167.refs_0_), channel_id=1, source_target_pairs={{0,8},{4,12},{8,0},{12,4},{16,24},{20,28},{24,16},{28,20},{1,9},{5... | collective-permute-start | bytes 1622024 | tf_op jit(solution)/shard_map/ppermute | solution.py:160
  347.7 31.1 %collective-permute-start.50 = (bf16[192,1408]{1,0:T(8,128)(2,1)}, bf16[192,1408]{1,0:T(8,128)(2,1)}, u32[]{:S(2)}, u32[]{:S(2)}) collective-permute-start(bf16[192,1408]{1,0:T(8,128)(2,1)} %get-tuple-element.170.refs_4_), channel_id=1, source_target_pairs={{0,16},{4,20},{8,24},{12,28},{16,0},{20,4},{24,8},{28,12},{1,17},{... | collective-permute-start | bytes 1622024 | tf_op jit(solution)/shard_map/ppermute | solution.py:160
  349.0 37.4 %collective-permute-start.59 = (bf16[2,192,1408]{2,1,0:T(8,128)(2,1)S(1)}, bf16[2,192,1408]{2,1,0:T(8,128)(2,1)}, u32[]{:S(2)}, u32[]{:S(2)}) collective-permute-start(bf16[2,192,1408]{2,1,0:T(8,128)(2,1)S(1)} %collective-permute-done.42.refs_1_), channel_id=1, source_target_pairs={{0,16},{4,20},{8,24},{12,28},{16,0},{20,4},{24,8},{28,12},{1,17},{... | collective-permute-start | bytes 3244040 | tf_op jit(solution)/shard_map/ppermute | solution.py:160
  366.7 26.2 %collective-permute-start.60 = (bf16[2,192,1408]{2,1,0:T(8,128)(2,1)S(1)}, bf16[2,192,1408]{2,1,0:T(8,128)(2,1)S(1)}, u32[]{:S(2)}, u32[]{:S(2)}) collective-permute-start(bf16[2,192,1408]{2,1,0:T(8,128)(2,1)S(1)} %collective-permute-done.48.refs_2_.refs_6_), channel_id=1, source_target_pairs={{0,8},{4,12},{8,0},{12,4},{16,24},{20,28},{24,16},{28,20},{1,9},{5... | collective-permute-start | bytes 3244040 | tf_op jit(solution)/shard_map/ppermute | solution.py:160
  376.1 20.4 %collective-permute-start.45 = (bf16[192,1408]{1,0:T(8,128)(2,1)S(1)}, bf16[192,1408]{1,0:T(8,128)(2,1)S(1)}, u32[]{:S(2)}, u32[]{:S(2)}) collective-permute-start(bf16[192,1408]{1,0:T(8,128)(2,1)S(1)} %copy-done.111), channel_id=1, source_target_pairs={{0,16},{4,20},{8,24},{12,28},{16,0},{20,4},{24,8},{28,12},{1,17},{... | collective-permute-start | bytes 1622024 | tf_op jit(solution)/shard_map/ppermute | solution.py:160
  377.4 22.3 %collective-permute-start.49 = (bf16[192,1408]{1,0:T(8,128)(2,1)S(1)}, bf16[192,1408]{1,0:T(8,128)(2,1)S(1)}, u32[]{:S(2)}, u32[]{:S(2)}) collective-permute-start(bf16[192,1408]{1,0:T(8,128)(2,1)S(1)} %copy-done.112), channel_id=1, source_target_pairs={{0,8},{4,12},{8,0},{12,4},{16,24},{20,28},{24,16},{28,20},{1,9},{5... | collective-permute-start | bytes 1622024 | tf_op jit(solution)/shard_map/ppermute | solution.py:160
  378.8 23.5 %collective-permute-start.46 = (bf16[192,1408]{1,0:T(8,128)(2,1)}, bf16[192,1408]{1,0:T(8,128)(2,1)S(1)}, u32[]{:S(2)}, u32[]{:S(2)}) collective-permute-start(bf16[192,1408]{1,0:T(8,128)(2,1)} %collective-permute-done.44.refs_1_), channel_id=1, source_target_pairs={{0,16},{4,20},{8,24},{12,28},{16,0},{20,4},{24,8},{28,12},{1,17},{... | collective-permute-start | bytes 1622024 | tf_op jit(solution)/shard_map/ppermute | solution.py:160
  386.4 19.3 %collective-permute-start.51 = (bf16[192,1408]{1,0:T(8,128)(2,1)}, bf16[192,1408]{1,0:T(8,128)(2,1)}, u32[]{:S(2)}, u32[]{:S(2)}) collective-permute-start(bf16[192,1408]{1,0:T(8,128)(2,1)} %collective-permute-done.50.refs_6_), channel_id=1, source_target_pairs={{0,8},{4,12},{8,0},{12,4},{16,24},{20,28},{24,16},{28,20},{1,9},{5... | collective-permute-start | bytes 1622024 | tf_op jit(solution)/shard_map/ppermute | solution.py:160
  392.9 73.0 %collective-permute-start.58 = (bf16[2,192,256]{2,1,0:T(8,128)(2,1)S(1)}, bf16[2,192,256]{2,1,0:T(8,128)(2,1)S(1)}, u32[]{:S(2)}, u32[]{:S(2)}) collective-permute-start(bf16[2,192,256]{2,1,0:T(8,128)(2,1)S(1)} %add_convert_fusion.16.refs_0_), channel_id=1, source_target_pairs={{0,1},{1,0},{2,3},{3,2},{4,5},{5,4},{6,7},{7,6},{8,9},{9,8},{10,11... | collective-permute-start | bytes 589832 | tf_op jit(solution)/shard_map/ppermute | solution.py:175
  396.5 51.1 %collective-permute-start.68 = (f32[8,192]{0,1:T(8,128)S(1)}, f32[8,192]{0,1:T(8,128)S(1)}, u32[]{:S(2)}, u32[]{:S(2)}) collective-permute-start(f32[8,192]{0,1:T(8,128)S(1)} %add.369), channel_id=1, source_target_pairs={{0,24},{4,28},{8,16},{12,20},{16,8},{20,12},{24,0},{28,4},{1,25},{... | collective-permute-start | bytes 18440 | tf_op jit(solution)/shard_map/ppermute | solution.py:160
  399.8 49.7 %collective-permute-start.67 = (f32[8,192]{0,1:T(8,128)S(1)}, f32[8,192]{0,1:T(8,128)S(1)}, u32[]{:S(2)}, u32[]{:S(2)}) collective-permute-start(f32[8,192]{0,1:T(8,128)S(1)} %add.369), channel_id=1, source_target_pairs={{0,16},{4,20},{8,24},{12,28},{16,0},{20,4},{24,8},{28,12},{1,17},{... | collective-permute-start | bytes 18440 | tf_op jit(solution)/shard_map/ppermute | solution.py:160
  402.3 47.2 %collective-permute-start.66 = (f32[8,192]{0,1:T(8,128)S(1)}, f32[8,192]{0,1:T(8,128)S(1)}, u32[]{:S(2)}, u32[]{:S(2)}) collective-permute-start(f32[8,192]{0,1:T(8,128)S(1)} %add.369), channel_id=1, source_target_pairs={{0,8},{4,12},{8,0},{12,4},{16,24},{20,28},{24,16},{28,20},{1,9},{5... | collective-permute-start | bytes 18440 | tf_op jit(solution)/shard_map/ppermute | solution.py:160
  416.5 78.4 %collective-permute-start.52 = (bf16[2,384,256]{2,1,0:T(8,128)(2,1)}, bf16[2,384,256]{2,1,0:T(8,128)(2,1)S(1)}, u32[]{:S(2)}, u32[]{:S(2)}) collective-permute-start(bf16[2,384,256]{2,1,0:T(8,128)(2,1)} %get-tuple-element.172), channel_id=1, source_target_pairs={{0,1},{1,0},{2,3},{3,2},{4,5},{5,4},{6,7},{7,6},{8,9},{9,8},{10,11... | collective-permute-start | bytes 1179656 | tf_op jit(solution)/shard_map/ppermute | solution.py:175
  481.9 14.3 %collective-permute-start.69 = (bf16[768,128]{1,0:T(8,128)(2,1)}, bf16[768,128]{1,0:T(8,128)(2,1)S(1)}, u32[]{:S(2)}, u32[]{:S(2)}) collective-permute-start(bf16[768,128]{1,0:T(8,128)(2,1)} %get-tuple-element.182), channel_id=1, source_target_pairs={{0,8},{4,12},{8,0},{12,4},{16,24},{20,28},{24,16},{28,20},{1,9},{5... | collective-permute-start | bytes 589832 | tf_op jit(solution)/shard_map/ppermute | solution.py:160
  496.1 193.3 %collective-permute-start.102 = (bf16[4,2,256,1408]{3,2,1,0:T(8,128)(2,1)}, bf16[4,2,256,1408]{3,2,1,0:T(8,128)(2,1)}, u32[]{:S(2)}, u32[]{:S(2)}) collective-permute-start(bf16[4,2,256,1408]{3,2,1,0:T(8,128)(2,1)} %get-tuple-element.212), channel_id=1, source_target_pairs={{0,4},{4,0},{8,12},{12,8},{16,20},{20,16},{24,28},{28,24},{1,5},{5... | collective-permute-start | bytes 17301512 | tf_op jit(solution)/shard_map/ppermute | solution.py:164
  496.3 47.6 %collective-permute-start.53 = (bf16[2,384,256]{2,1,0:T(8,128)(2,1)S(1)}, bf16[2,384,256]{2,1,0:T(8,128)(2,1)S(1)}, u32[]{:S(2)}, u32[]{:S(2)}) collective-permute-start(bf16[2,384,256]{2,1,0:T(8,128)(2,1)S(1)} %add_convert_fusion.5), channel_id=1, source_target_pairs={{0,3},{1,2},{2,1},{3,0},{4,7},{5,6},{6,5},{7,4},{8,11},{9,10},{10,... | collective-permute-start | bytes 1179656 | tf_op jit(solution)/shard_map/ppermute | solution.py:175
  497.1 32.5 %collective-permute-start.100 = (f32[5,8,256]{2,1,0:T(8,128)S(1)}, f32[5,8,256]{2,1,0:T(8,128)S(1)}, u32[]{:S(2)}, u32[]{:S(2)}) collective-permute-start(f32[5,8,256]{2,1,0:T(8,128)S(1)} %add.394), channel_id=1, source_target_pairs={{0,8},{4,12},{8,0},{12,4},{16,24},{20,28},{24,16},{28,20},{1,9},{5... | collective-permute-start | bytes 122888 | tf_op jit(solution)/shard_map/ppermute | solution.py:803
  517.5 20.0 %collective-permute-start.78 = (f32[256,256]{1,0:T(8,128)}, f32[256,256]{1,0:T(8,128)S(1)}, u32[]{:S(2)}, u32[]{:S(2)}) collective-permute-start(f32[256,256]{1,0:T(8,128)} %get-tuple-element.193), channel_id=1, source_target_pairs={{4,0},{12,8},{20,16},{28,24},{5,1},{13,9},{21,17},{29,25},{6,2},{1... | collective-permute-start | bytes 786440 | tf_op jit(solution)/shard_map/ppermute | solution.py:172
  543.9 12.6 %collective-permute-start.54 = (bf16[2,384,256]{2,1,0:T(8,128)(2,1)S(1)}, bf16[2,384,256]{2,1,0:T(8,128)(2,1)S(1)}, u32[]{:S(2)}, u32[]{:S(2)}) collective-permute-start(bf16[2,384,256]{2,1,0:T(8,128)(2,1)S(1)} %add_convert_fusion.4.refs_0_), channel_id=1, source_target_pairs={{0,1},{1,0},{2,3},{3,2},{4,5},{5,4},{6,7},{7,6},{8,9},{9,8},{10,11... | collective-permute-start | bytes 1179656 | tf_op jit(solution)/shard_map/ppermute | solution.py:175
  553.8 14.8 %collective-permute-start.75 = (bf16[768,256]{1,0:T(8,128)(2,1)S(1)}, bf16[768,256]{1,0:T(8,128)(2,1)S(1)}, u32[]{:S(2)}, u32[]{:S(2)}) collective-permute-start(bf16[768,256]{1,0:T(8,128)(2,1)S(1)} %copy-done.9), channel_id=1, source_target_pairs={{0,8},{4,12},{8,0},{12,4},{16,24},{20,28},{24,16},{28,20},{1,9},{5... | collective-permute-start | bytes 1179656 | tf_op jit(solution)/shard_map/ppermute | solution.py:160
  554.8 21.0 %collective-permute-start.76 = (bf16[768,256]{1,0:T(8,128)(2,1)S(1)}, bf16[768,256]{1,0:T(8,128)(2,1)S(1)}, u32[]{:S(2)}, u32[]{:S(2)}) collective-permute-start(bf16[768,256]{1,0:T(8,128)(2,1)S(1)} %copy-done.9), channel_id=1, source_target_pairs={{0,16},{4,20},{8,24},{12,28},{16,0},{20,4},{24,8},{28,12},{1,17},{... | collective-permute-start | bytes 1179656 | tf_op jit(solution)/shard_map/ppermute | solution.py:160
  560.7 14.1 %collective-permute-start.80 = (bf16[768,256]{1,0:T(8,128)(2,1)S(1)}, bf16[768,256]{1,0:T(8,128)(2,1)S(1)}, u32[]{:S(2)}, u32[]{:S(2)}) collective-permute-start(bf16[768,256]{1,0:T(8,128)(2,1)S(1)} %copy-done.10), channel_id=1, source_target_pairs={{0,16},{4,20},{8,24},{12,28},{16,0},{20,4},{24,8},{28,12},{1,17},{... | collective-permute-start | bytes 1179656 | tf_op jit(solution)/shard_map/ppermute | solution.py:160
  567.6 12.0 %collective-permute-start.79 = (bf16[768,256]{1,0:T(8,128)(2,1)S(1)}, bf16[768,256]{1,0:T(8,128)(2,1)S(1)}, u32[]{:S(2)}, u32[]{:S(2)}) collective-permute-start(bf16[768,256]{1,0:T(8,128)(2,1)S(1)} %copy-done.10), channel_id=1, source_target_pairs={{0,8},{4,12},{8,0},{12,4},{16,24},{20,28},{24,16},{28,20},{1,9},{5... | collective-permute-start | bytes 1179656 | tf_op jit(solution)/shard_map/ppermute | solution.py:160
  568.6 12.7 %collective-permute-start.77 = (bf16[768,256]{1,0:T(8,128)(2,1)S(1)}, bf16[768,256]{1,0:T(8,128)(2,1)S(1)}, u32[]{:S(2)}, u32[]{:S(2)}) collective-permute-start(bf16[768,256]{1,0:T(8,128)(2,1)S(1)} %collective-permute-done.75.refs_1_), channel_id=1, source_target_pairs={{0,16},{4,20},{8,24},{12,28},{16,0},{20,4},{24,8},{28,12},{1,17},{... | collective-permute-start | bytes 1179656 | tf_op jit(solution)/shard_map/ppermute | solution.py:160
  575.8 17.8 %collective-permute-start.55 = (bf16[768,256]{1,0:T(8,128)(2,1)S(1)}, bf16[768,256]{1,0:T(8,128)(2,1)S(1)}, u32[]{:S(2)}, u32[]{:S(2)}) collective-permute-start(bf16[768,256]{1,0:T(8,128)(2,1)S(1)} %get-tuple-element.276), channel_id=1, source_target_pairs={{0,4},{4,0},{8,12},{12,8},{16,20},{20,16},{24,28},{28,24},{1,5},{5... | collective-permute-start | bytes 1179656 | tf_op jit(solution)/shard_map/ppermute | solution.py:164
  579.6 92.6 %collective-permute-start.103 = (bf16[4,1408,256]{2,1,0:T(8,128)(2,1)}, bf16[4,1408,256]{2,1,0:T(8,128)(2,1)}, u32[]{:S(2)}, u32[]{:S(2)}) collective-permute-start(bf16[4,1408,256]{2,1,0:T(8,128)(2,1)} %get-tuple-element.214), channel_id=1, source_target_pairs={{0,4},{4,0},{8,12},{12,8},{16,20},{20,16},{24,28},{28,24},{1,5},{5... | collective-permute-start | bytes 8650760 | tf_op jit(solution)/shard_map/ppermute | solution.py:164
  581.3 67.8 %collective-permute-start.98 = (bf16[4,512,256]{2,1,0:T(8,128)(2,1)}, bf16[4,512,256]{2,1,0:T(8,128)(2,1)}, u32[]{:S(2)}, u32[]{:S(2)}) collective-permute-start(bf16[4,512,256]{2,1,0:T(8,128)(2,1)} %get-tuple-element.209), channel_id=1, source_target_pairs={{0,4},{4,0},{8,12},{12,8},{16,20},{20,16},{24,28},{28,24},{1,5},{5... | collective-permute-start | bytes 3145736 | tf_op jit(solution)/shard_map/ppermute | solution.py:164
  592.6 18.6 %collective-permute-start.82 = (bf16[2,192,256]{2,1,0:T(8,128)(2,1)}, bf16[2,192,256]{2,1,0:T(8,128)(2,1)S(1)}, u32[]{:S(2)}, u32[]{:S(2)}) collective-permute-start(bf16[2,192,256]{2,1,0:T(8,128)(2,1)} %get-tuple-element.196), channel_id=1, source_target_pairs={{0,1},{1,0},{2,3},{3,2},{4,5},{5,4},{6,7},{7,6},{8,9},{9,8},{10,11... | collective-permute-start | bytes 589832 | tf_op jit(solution)/shard_map/ppermute | solution.py:175
  598.8 53.1 %all-to-all-start.2 = ((bf16[8,256,256]{2,1,0:T(8,128)(2,1)}), bf16[8,256,256]{2,1,0:T(8,128)(2,1)S(1)}, u32[]{:S(2)}, u32[]{:S(2)}) async-start(bf16[8,256,256]{2,1,0:T(8,128)(2,1)} %bitcast.120), calls=%async_computation.2 | async-start | bytes 2097152 | tf_op jit(solution)/shard_map/all_to_all | solution.py:1208
  622.0 18.8 %collective-permute-start.84 = (bf16[2,192,256]{2,1,0:T(8,128)(2,1)S(1)}, bf16[2,192,256]{2,1,0:T(8,128)(2,1)S(1)}, u32[]{:S(2)}, u32[]{:S(2)}) collective-permute-start(bf16[2,192,256]{2,1,0:T(8,128)(2,1)S(1)} %add_convert_fusion.10.refs_0_), channel_id=1, source_target_pairs={{0,1},{1,0},{2,3},{3,2},{4,5},{5,4},{6,7},{7,6},{8,9},{9,8},{10,11... | collective-permute-start | bytes 589832 | tf_op jit(solution)/shard_map/ppermute | solution.py:175
  627.6 13.3 %collective-permute-start.87 = (bf16[2,192,256]{2,1,0:T(8,128)(2,1)S(1)}, bf16[2,192,256]{2,1,0:T(8,128)(2,1)S(1)}, u32[]{:S(2)}, u32[]{:S(2)}) collective-permute-start(bf16[2,192,256]{2,1,0:T(8,128)(2,1)S(1)} %add_convert_fusion.8.refs_2_), channel_id=1, source_target_pairs={{0,1},{1,0},{2,3},{3,2},{4,5},{5,4},{6,7},{7,6},{8,9},{9,8},{10,11... | collective-permute-start | bytes 589832 | tf_op jit(solution)/shard_map/ppermute | solution.py:175
  640.8 14.8 %collective-permute-start.96 = (bf16[2,256,512]{2,1,0:T(8,128)(2,1)}, bf16[2,256,512]{2,1,0:T(8,128)(2,1)}, u32[]{:S(2)}, u32[]{:S(2)}) collective-permute-start(bf16[2,256,512]{2,1,0:T(8,128)(2,1)} %get-tuple-element.205), channel_id=1, source_target_pairs={{0,4},{4,0},{8,12},{12,8},{16,20},{20,16},{24,28},{28,24},{1,5},{5... | collective-permute-start | bytes 1572872 | tf_op jit(solution)/shard_map/ppermute | solution.py:164
  651.9 26.3 %collective-permute-start.97 = (bf16[4,256,512]{2,1,0:T(8,128)(2,1)}, bf16[4,256,512]{2,1,0:T(8,128)(2,1)S(1)}, u32[]{:S(2)}, u32[]{:S(2)}) collective-permute-start(bf16[4,256,512]{2,1,0:T(8,128)(2,1)} %get-tuple-element.207), channel_id=1, source_target_pairs={{0,4},{4,0},{8,12},{12,8},{16,20},{20,16},{24,28},{28,24},{1,5},{5... | collective-permute-start | bytes 3145736 | tf_op jit(solution)/shard_map/ppermute | solution.py:164
  668.4 19.2 %all-to-all-start.3 = ((bf16[8,256,256]{2,1,0:T(8,128)(2,1)}), bf16[8,256,256]{2,1,0:T(8,128)(2,1)S(1)}, u32[]{:S(2)}, u32[]{:S(2)}) async-start(bf16[8,256,256]{2,1,0:T(8,128)(2,1)} %bitcast.121), calls=%async_computation.3 | async-start | bytes 2097152 | tf_op jit(solution)/shard_map/all_to_all | solution.py:1208
  (161 other events, 1898.9 us)

commit v4 on v3

--- a/solution.py
+++ b/solution.py
@@ -119,7 +119,7 @@
 ):
     seqs = dealing.shape[0]
     seq_len = cotangent.shape[1]
-    held = cotangent.shape[0]
+    slots = cotangent.shape[0]
     per = hidden_in.shape[1]
     width = hidden_in.shape[2]
     heads = query_weight.shape[2] // HD
@@ -175,36 +175,44 @@
         return lax.ppermute(value, "tensor", [(a, a ^ mask) for a in range(tp)])
 
     def sum_groups(value):
-        value = value + by_group(value, 1)
-        return value + by_group(value, 2)
+        return (value + by_group(value, 1)) + (by_group(value, 2) + by_group(value, 3))
 
     def sum_z(value):
         value = value + by_z(value, 1)
         return value + by_z(value, 3)
 
+    def z_first(keep, send):
+        return both(keep, by_z(send, 1))
+
+    def z_second(half):
+        return both(half, by_z(half, 3))
+
+    def z_last(half):
+        return half, by_z(half, 1)
+
     def wide_sum_z(keep, send):
-        half = both(keep, by_z(send, 1))
-        half = both(half, by_z(half, 3))
-        return half, by_z(half, 1)
-
-    def reduce_groups(first, second, early=None, late=None):
-        if early is not None:
-            first, second, _ = lax.optimization_barrier((tuple(first), tuple(second), early))
+        return z_last(z_second(z_first(keep, send)))
+
+    def held(values, *others):
+        return lax.optimization_barrier((tuple(values),) + others)[0]
+
+    def reduce_groups(first, second, early=(), late=()):
+        if early:
+            first, second = held((tuple(first), tuple(second)), early)
         ra = by_group(first[3], 1)
         rb = by_group(second[3], 2)
         ax = by_group(first[1], 1)
         by = by_group(second[2], 2)
-        along_y, along_x = both(first[2], ra), both(second[1], rb)
-        if late is not None:
-            along_y, along_x, _ = lax.optimization_barrier((along_y, along_x, late))
-        ay = by_group(along_y, 2)
-        bx = by_group(along_x, 1)
-        return (first[0], ax, ay), (second[0], bx, by), (along_y, along_x)
-
-    def gather_groups(first, second):
+        along = held((both(first[2], ra), both(second[1], rb)), (ax, by), late)
+        ay = by_group(along[0], 2)
+        bx = by_group(along[1], 1)
+        return (first[0], ax, ay), (second[0], bx, by), along, (ra, rb)
+
+    def gather_groups(first, second, late=()):
         ax, bx = by_group(first, 1), by_group(second, 1)
         ay, by = by_group(first, 2), by_group(second, 2)
-        ad, bd = by_group(ax, 2), by_group(by, 1)
+        along = held((ax, by), (bx, ay), late)
+        ad, bd = by_group(along[0], 2), by_group(along[1], 1)
         return (first, ax, ay, ad), (second, bx, by, bd)
 
     def row_of(offset):
@@ -292,7 +300,7 @@
     x_send = hidden_in.reshape(seqs * per, dp, ds).transpose(1, 0, 2)
     x_all = lax.all_to_all(x_send, "dp", 0, 0, tiled=True).reshape(rows_all, ds)
     x_pieces = pack(x_all, False)
-    d_send = cotangent.reshape(held * seq_len, dp, ds).transpose(1, 0, 2)
+    d_send = cotangent.reshape(slots * seq_len, dp, ds).transpose(1, 0, 2)
     d_all = lax.all_to_all(d_send, "dp", 0, 0, tiled=True).reshape(rows_all, ds)
     d_pieces = pack(d_all, True)
 
@@ -417,13 +425,13 @@
     outs = [((rp, 2 * HD), BF16, (tile, 2 * HD), lambda i, m: (i, 0))] * 8
     outs += [((8, rp), F32, (8, tile), lambda i, m: (0, i))]
     qkv = run(
-        qkv_body, "qkv", (rp // tile,), meta, ins, outs,
+        qkv_body, "qkv", (rp // tile,), after(meta, d_pieces[0]), ins, outs,
         [pltpu.VMEM((heads, tile, 4 * HD), BF16)],
         flops=2 * rp * (experts + 2) * parts * ds * hw,
     )
     dh = dhidden(after(meta, qkv[8]))
-    q_sum, kv_sum, sent = reduce_groups(qkv[0:8:2], qkv[1:8:2])
-    stats_a = sum_groups(qkv[8])
+    q_sum, kv_sum, sent, far = reduce_groups(qkv[0:8:2], qkv[1:8:2], late=dh[0])
+    stats_a = sum_groups(after(qkv[8], far))
     flat_a, cols_a = gate_columns(stats_a, low_a, high_a)
 
     def rope_body(m, a0, a1, a2, b0, b1, b2, cols, cos_ref, sin_ref, q_ref, kv_ref):
@@ -485,10 +493,6 @@
         flops=8 * rp * span * HD,
     )
     gm_a, gm_b = gather_groups(gated_a, gated_b)
-    dh_a, dh_b, _ = reduce_groups(
-        dh[0:8:2], dh[1:8:2], early=sent, late=(gm_a[1], gm_b[2])
-    )
-
     chunks = 2
     zr = rp // chunks // 2
     hold = [((parts, zr, ds), BF16, None, None)] * 2
@@ -520,7 +524,7 @@
         for s in pieces:
             store_halves(pl.program_id(0), outs, s, acc[s].astype(BF16))
 
-    def project(k):
+    def project(k, meta):
         half = lambda i, m: (2 * k + m[7 - i], 0)
         ins = [(v, (zr, HD), half) for v in gm_a + gm_b]
         ins += [(sel, (zr, 8), half)]
@@ -531,7 +535,17 @@
             flops=4 * zr * experts * hw * parts * ds,
         )
 
-    attn_totals = [half for k in range(chunks) for half in wide_sum_z(*project(k))]
+    halves = [z_first(*project(0, meta))]
+    dh_a, dh_b = held((dh[0:8:2], dh[1:8:2]), gm_a[3], gm_b[3])
+    ra, rb = by_group(dh_a[3], 1), by_group(dh_b[3], 2)
+    for k in range(1, chunks):
+        halves.append(z_first(*project(k, after(meta, halves[-1], ra, rb))))
+    near = held((dh_a[1], dh_b[2]), halves[0])
+    ax, by = by_group(near[0], 1), by_group(near[1], 2)
+    halves = held([z_second(half) for half in halves], ax, by)
+    along = held((both(dh_a[2], ra), both(dh_b[1], rb)), halves)
+    dh_a, dh_b = (dh_a[0], ax, by_group(along[0], 2)), (dh_b[0], by_group(along[1], 1), by)
+    attn_totals = [half for v in halves for half in z_last(v)]
 
     def norm_body(m, *refs):
         t_refs = refs[: 2 * chunks]
@@ -590,9 +604,9 @@
             up_body, "up", (2,), meta, ins, outs, flops=8 * blk * experts * parts * ds * ff
         )
 
-    up_far = up((3, 1), meta)
+    up_far = up((3, 1), after(meta, stats_f, dh_a[2], dh_b[1]))
     up_near = up((2, 0), after(meta, up_far[0]))
-    gu_a, gu_b, _ = reduce_groups(
+    gu_a, gu_b, _, _ = reduce_groups(
         (up_near[2], up_far[2], up_near[0], up_far[0]),
         (up_near[3], up_far[3], up_near[1], up_far[1]),
     )
@@ -640,12 +654,13 @@
     outs += [((blk, 8), F32, (mt_rows, 8), rows_2)]
     act_a, act_b, grad_a, grad_b, dots_f = run(mid_body, "mid", (3,), meta, ins, outs)
     gg_a, gg_b = gather_groups(grad_a, grad_b)
-    late = after(act_a, gg_a[1], gg_a[2]), after(act_b, gg_b[1], gg_b[2])
-    ag_a, ag_b = gather_groups(*late)
     dots_f = dots_f.T
 
     dots_f = after(sum_z(dots_f), gg_a[3], gg_b[3])
     dots_f = jnp.stack([dots_f, by_group(dots_f, 1), by_group(dots_f, 2), by_group(dots_f, 3)])
+    act_a, act_b, _ = lax.optimization_barrier((act_a, act_b, (gg_a[3], gg_b[3])))
+    ag_a = [act_a, by_group(act_a, 1), by_group(act_a, 2)]
+    ag_b = [act_b, by_group(act_b, 1), by_group(act_b, 2)]
     dots_f = jnp.take(dots_f, g ^ jnp.arange(4, dtype=jnp.int32), axis=0)
     dots_f = dots_f.transpose(1, 0, 2).reshape(8, rp)
 
@@ -701,42 +716,83 @@
 
     dx_near = dx((0, 1), meta)
     dx_far = dx((2, 3), meta)
-    dx_totals = wide_sum_z(*dx_near) + wide_sum_z(*dx_far)
-
-    def down_body(m, *refs):
+    far_half = z_first(*dx_far)
+    dx_totals = wide_sum_z(*dx_near) + z_last(z_second(far_half))
+
+    def exchange(sums):
+        total = sums[0].astype(F32)
+        for s in pieces[1:]:
+            total = total + by_part(sums[s], s).astype(F32)
+        return total
+
+    ffn_input = (after_rows * flat_f[0][None, :, None] * gain_f).astype(BF16)
+
+    def t_left(xs, value):
+        if not wide:
+            return [tn(x, value) for x in xs]
+        total = tn(jnp.concatenate(xs, axis=1), value)
+        return [total[s * ds : (s + 1) * ds] for s in pieces]
+
+    def t_right(value, xs):
+        if not wide:
+            return [tn(value, x) for x in xs]
+        total = tn(value, jnp.concatenate(xs, axis=1))
+        return [total[:, s * ds : (s + 1) * ds] for s in pieces]
+
+    def sort_rows(m, sel_ref, x_refs, xs, ids):
+        for r in range(4):
+            src, here_r = at_row(m, 2 + r, blk), slice(r * blk, (r + 1) * blk)
+            for s in pieces:
+                xs[s, here_r, :] = x_refs[s][src, :]
+            ids[here_r, :] = sel_ref[src, :]
+
+    def dwin_body(m, *refs):
         a_refs, b_refs = refs[:4], refs[4:8]
-        w_refs = refs[8 : 8 + parts]
-        sel_refs = refs[8 + parts : 12 + parts]
-        keep_ref, send_ref, acc, xs = refs[12 + parts :]
+        sel_ref, x_ref = refs[8:10]
+        outs = refs[10 : 10 + parts]
+        xs, ids, mt = refs[10 + parts :]
         e = pl.program_id(0)
 
         @pl.when(e == 0)
         def _():
-            acc[...] = jnp.zeros_like(acc)
-
+            sort_rows(m, sel_ref, [x_ref.at[s] for s in pieces], xs, ids)
+
+        expert = e.astype(F32)
         for r in range(4):
-            ids = sel_refs[r]
-            xs[r * blk : (r + 1) * blk, :] = pick(
-                ids[:, 2:3], ids[:, 3:4], e.astype(F32), a_refs[r][...], b_refs[r][...]
+            here_r = slice(r * blk, (r + 1) * blk)
+            mt[here_r, :] = pick(
+                ids[here_r, 2:3], ids[here_r, 3:4], expert, a_refs[r][0], b_refs[r][0]
             )
-        for s, value in enumerate(nn_pieces(xs[...], [w[0] for w in w_refs])):
-            acc[s] += value
-
-        @pl.when(e == experts - 1)
-        def _():
-            keep_ref[...] = acc[:, at_row(m, 6, 2 * blk), :].astype(BF16)
-            send_ref[...] = acc[:, at_row(m, 7, 2 * blk), :].astype(BF16)
-
-    def down(meta):
-        ins = [(v, None, None) for v in ag_a + ag_b]
-        ins += [(w, (1, ff, ds), lambda e, m: (e, 0, 0)) for w in wo]
-        ins += [(sel, (blk, 8), row_of(r)) for r in range(4)]
+        for s, value in enumerate(t_left([xs[s] for s in pieces], mt[...])):
+            outs[s][0] = value.astype(BF16)
+
+    def dwin(j, meta):
+        ins = [(v, (1, blk, ff), lambda e, m: (j, 0, 0)) for v in gg_a + gg_b]
+        ins += [(sel, None, None), (ffn_input, None, None)]
+        outs = [((experts, ds, ff), BF16, (1, ds, ff), lambda e, m: (e, 0, 0))] * parts
         return run(
-            down_body, "down", (experts,), meta, ins,
-            [((parts, 2 * blk, ds), BF16, None, None)] * 2,
-            [pltpu.VMEM((parts, rp, ds), F32), pltpu.VMEM((rp, ff), BF16)],
+            dwin_body, "dwin", (experts,), meta, ins, outs,
+            [pltpu.VMEM((parts, rp, ds), BF16), pltpu.VMEM((rp, 8), F32), pltpu.VMEM((rp, ff), BF16)],
             flops=2 * rp * experts * parts * ds * ff,
         )
+
+    def fold_body(m, *refs):
+        out_ref = refs[2 * parts]
+        for j in range(2):
+            total = refs[j * parts][0].astype(F32)
+            for ref in refs[j * parts + 1 : (j + 1) * parts]:
+                total = total + ref[0].astype(F32)
+            out_ref[0, :, j, :] = total
+
+    def fold(sums, meta):
+        ins = []
+        for half in sums:
+            got = [half[0]] + [by_part(half[s], s) for s in pieces[1:]]
+            ins += [(v, (1, ds, ff), lambda e, m: (e, 0, 0)) for v in got]
+        outs = [((experts, ds, 2, ff), F32, (1, ds, 2, ff), lambda e, m: (e, 0, 0, 0))]
+        return run(fold_body, "fold", (experts,), meta, ins, outs)[0]
+
+    dwin_gate = dwin(0, after(meta, far_half))
 
     def norm_back_body(low_precision_out, m, *refs):
         t_refs = refs[:4]
@@ -789,11 +845,13 @@
         ((experts + 1, parts, ds), F32, None, None),
     ]
     dafter, dafter_low, small_f = run(
-        functools.partial(norm_back_body, True), "norm_back", (1,), meta, ins, outs
-    )
-
-    def whole_vectors(small):
-        full = jnp.zeros((experts + 1, dp, ds), F32)
+        functools.partial(norm_back_body, True), "norm_back", (1,),
+        after(meta, dwin_gate[0], ag_a[1:], ag_b[1:]), ins, outs,
+    )
+
+    def whole_vectors(*smalls):
+        small = jnp.concatenate(smalls, axis=0)
+        full = jnp.zeros((small.shape[0], dp, ds), F32)
         for s in pieces:
             full = lax.dynamic_update_slice_in_dim(
                 full, small[:, s : s + 1], g * parts + (c ^ s), axis=1
@@ -802,10 +860,8 @@
         while mask < dp:
             full = full + lax.ppermute(full, "dp", [(a, a ^ mask) for a in range(dp)])
             mask *= 2
-        full = full.reshape(experts + 1, width)
-        return full[:experts].T, full[experts]
-
-    ffnrouter_grad, ffngain_grad = whole_vectors(small_f)
+        full = full.reshape(len(smalls), experts + 1, width)
+        return [(v[:experts].T, v[experts]) for v in full]
 
     def dmix_body(m, *refs):
         d_ref = refs[0]
@@ -835,7 +891,10 @@
         [pltpu.VMEM((heads, tile, 2 * HD), BF16)],
         flops=2 * rp * experts * parts * ds * hw,
     )
-    dm_a, dm_b, _ = reduce_groups(dm[0:8:2], dm[1:8:2])
+    dwin_up = dwin(1, after(meta, dm[0]))
+    dm_a, dm_b, _, _ = reduce_groups(dm[0:8:2], dm[1:8:2], late=dwin_up[0])
+    along = held((ag_a[1], ag_b[2]), dm_a[2], dm_b[1])
+    ag_a, ag_b = ag_a + [by_group(along[0], 2)], ag_b + [by_group(along[1], 1)]
 
     def attend_back_body(m, *refs):
         q_ref, kv_ref, halo_ref, sel_ref, cols, cos_ref, sin_ref = refs[:7]
@@ -916,9 +975,89 @@
     outs = [((rp, 2 * HD), BF16, None, None), ((8, rp), F32, None, None)]
     dkv, dots_kv = run(dkv_body, "dkv", (1,), meta, ins, outs)
     third = jnp.arange(8)[:, None] == 2
-    dots_a = sum_z(sum_groups(dots_q + jnp.where(third, dots_kv, 0.0)))
+    def down_body(m, *refs):
+        a_refs, b_refs = refs[:4], refs[4:8]
+        sel_ref, d_refs = refs[8], refs[9 : 9 + parts]
+        w_refs = refs[9 + parts : 9 + 2 * parts]
+        keep_ref, send_ref = refs[9 + 2 * parts : 11 + 2 * parts]
+        outs = refs[11 + 2 * parts : 11 + 3 * parts]
+        acc, xs, ids, mt = refs[11 + 3 * parts :]
+        e = pl.program_id(0)
+
+        @pl.when(e == 0)
+        def _():
+            acc[...] = jnp.zeros_like(acc)
+            sort_rows(m, sel_ref, d_refs, xs, ids)
+
+        expert = e.astype(F32)
+        for r in range(4):
+            here_r = slice(r * blk, (r + 1) * blk)
+            mt[here_r, :] = pick(
+                ids[here_r, 2:3], ids[here_r, 3:4], expert, a_refs[r][...], b_refs[r][...]
+            )
+        for s, value in enumerate(nn_pieces(mt[...], [w[0] for w in w_refs])):
+            acc[s] += value
+        for s, value in enumerate(t_right(mt[...], [xs[s] for s in pieces])):
+            outs[s][0] = value.astype(BF16)
+
+        @pl.when(e == experts - 1)
+        def _():
+            keep_ref[...] = acc[:, at_row(m, 6, 2 * blk), :].astype(BF16)
+            send_ref[...] = acc[:, at_row(m, 7, 2 * blk), :].astype(BF16)
+
+    def down(meta):
+        spot = lambda e, m: (e, 0, 0)
+        ins = [(v, None, None) for v in ag_a + ag_b]
+        ins += [(sel, None, None)] + [(d, None, None) for d in d_pieces]
+        ins += [(w, (1, ff, ds), spot) for w in wo]
+        outs = [((parts, 2 * blk, ds), BF16, None, None)] * 2
+        outs += [((experts, ff, ds), BF16, (1, ff, ds), spot)] * parts
+        return run(
+            down_body, "down", (experts,), meta, ins, outs,
+            [
+                pltpu.VMEM((parts, rp, ds), F32),
+                pltpu.VMEM((parts, rp, ds), BF16),
+                pltpu.VMEM((rp, 8), F32),
+                pltpu.VMEM((rp, ff), BF16),
+            ],
+            flops=4 * rp * experts * parts * ds * ff,
+        )
+
+    def dwproj_body(m, *refs):
+        a_refs, b_refs = refs[:4], refs[4:8]
+        sel_ref, d_ref = refs[8:10]
+        outs = refs[10 : 10 + parts]
+        lo, hi = refs[10 + parts :]
+        e = pl.program_id(0)
+
+        @pl.when(e == 0)
+        def _():
+            for r in range(4):
+                lanes = pl.ds(pl.multiple_of(m[2 + r] * HD, HD), HD)
+                lo[:, lanes] = a_refs[r][...]
+                hi[:, lanes] = b_refs[r][...]
+
+        x = pick(sel_ref[:, 0:1], sel_ref[:, 1:2], e.astype(F32), lo[...], hi[...])
+        for s, value in enumerate(t_right(x, [d_ref[s] for s in pieces])):
+            outs[s][0] = value.astype(BF16)
+
+    def dwproj(meta):
+        ins = [(v, None, None) for v in gm_a + gm_b]
+        ins += [(sel, None, None), (dafter_low, None, None)]
+        return run(
+            dwproj_body, "dwproj", (experts,), meta, ins,
+            [((experts, hw, ds), BF16, (1, hw, ds), lambda e, m: (e, 0, 0))] * parts,
+            [pltpu.VMEM((rp, hw), BF16)] * 2,
+            flops=2 * rp * experts * hw * parts * ds,
+        )
+
+    down_halves = down(after(meta, dkv))
+    down_halves, dwout_sums = down_halves[:2], down_halves[2:]
+    da_a, da_b = gather_groups(dq, dkv, late=dwout_sums[0])
+    dwproj_sums = dwproj(after(meta, dwout_sums[0]))
+    dots_a = sum_z(sum_groups(after(dots_q, da_a[3], da_b[3]) + jnp.where(third, dots_kv, 0.0)))
     back_a = back_columns(flat_a, dots_a, low_a, high_a)
-    da_a, da_b = gather_groups(dq, dkv)
+
 
     def place_heads(m, refs, lo, hi):
         for r in range(4):
@@ -945,7 +1084,7 @@
         for s in pieces:
             store_halves(pl.program_id(0), outs, s, acc[s].astype(BF16))
 
-    def dattn(k):
+    def dattn(k, meta):
         half = lambda i, m: (2 * k + m[7 - i], 0)
         ins = [(v, (zr, 2 * HD), half) for v in da_a + da_b]
         ins += [(sel, (zr, 8), half)]
@@ -956,134 +1095,11 @@
             flops=4 * zr * (experts + 2) * hw * parts * ds,
         )
 
-    da_totals = [half for k in range(chunks) for half in wide_sum_z(*dattn(k))]
+    da_halves = [z_first(*dattn(0, after(meta, dwproj_sums[0])))]
+    for k in range(1, chunks):
+        da_halves.append(z_first(*dattn(k, after(meta, da_halves[-1]))))
     x_stack = jnp.stack(x_pieces)
-    ins = [(t, None, None) for t in da_totals]
-    ins += [(x_stack, None, None), (dafter, None, None)]
-    ins += [(gain_a, None, None), (router_a, None, None), (back_a, None, None)]
-    outs = [((parts, rp, ds), BF16, None, None), ((experts + 1, parts, ds), F32, None, None)]
-    dinput, small_a = run(
-        functools.partial(norm_back_body, False), "norm_back_first", (1,), meta, ins, outs
-    )
-    attnrouter_grad, attngain_grad = whole_vectors(small_a)
-
-    def exchange(sums):
-        total = sums[0].astype(F32)
-        for s in pieces[1:]:
-            total = total + by_part(sums[s], s).astype(F32)
-        return total
-
-    ffn_input = (after_rows * flat_f[0][None, :, None] * gain_f).astype(BF16)
     attn_input = (x_stack.astype(F32) * flat_a[0][None, :, None] * gain_a).astype(BF16)
-
-    def t_left(xs, value):
-        if not wide:
-            return [tn(x, value) for x in xs]
-        total = tn(jnp.concatenate(xs, axis=1), value)
-        return [total[s * ds : (s + 1) * ds] for s in pieces]
-
-    def t_right(value, xs):
-        if not wide:
-            return [tn(value, x) for x in xs]
-        total = tn(value, jnp.concatenate(xs, axis=1))
-        return [total[:, s * ds : (s + 1) * ds] for s in pieces]
-
-    def sort_rows(m, sel_ref, x_refs, xs, ids):
-        for r in range(4):
-            src, here_r = at_row(m, 2 + r, blk), slice(r * blk, (r + 1) * blk)
-            for s in pieces:
-                xs[s, here_r, :] = x_refs[s][src, :]
-            ids[here_r, :] = sel_ref[src, :]
-
-    def dwin_body(m, *refs):
-        a_refs, b_refs = refs[:4], refs[4:8]
-        sel_ref, x_ref = refs[8:10]
-        outs = refs[10 : 10 + parts]
-        xs, ids, mt = refs[10 + parts :]
-        j, e = pl.program_id(0), pl.program_id(1)
-
-        @pl.when((j == 0) & (e == 0))
-        def _():
-            sort_rows(m, sel_ref, [x_ref.at[s] for s in pieces], xs, ids)
-
-        expert = e.astype(F32)
-        for r in range(4):
-            here_r = slice(r * blk, (r + 1) * blk)
-            mt[here_r, :] = pick(
-                ids[here_r, 2:3], ids[here_r, 3:4], expert, a_refs[r][0], b_refs[r][0]
-            )
-        for s, value in enumerate(t_left([xs[s] for s in pieces], mt[...])):
-            outs[s][0, 0] = value.astype(BF16)
-
-    def dwin(meta):
-        spot = lambda j, e, m: (e, j, 0, 0)
-        ins = [(v, (1, blk, ff), lambda j, e, m: (j, 0, 0)) for v in gg_a + gg_b]
-        ins += [(sel, None, None), (ffn_input, None, None)]
-        outs = [((experts, 2, ds, ff), BF16, (1, 1, ds, ff), spot)] * parts
-        return run(
-            dwin_body, "dwin", (2, experts), meta, ins, outs,
-            [pltpu.VMEM((parts, rp, ds), BF16), pltpu.VMEM((rp, 8), F32), pltpu.VMEM((rp, ff), BF16)],
-            flops=4 * rp * experts * parts * ds * ff,
-        )
-
-    def dwout_body(m, *refs):
-        a_refs, b_refs = refs[:4], refs[4:8]
-        sel_ref, d_refs = refs[8], refs[9 : 9 + parts]
-        outs = refs[9 + parts : 9 + 2 * parts]
-        xs, ids, mt = refs[9 + 2 * parts :]
-        e = pl.program_id(0)
-
-        @pl.when(e == 0)
-        def _():
-            sort_rows(m, sel_ref, d_refs, xs, ids)
-
-        expert = e.astype(F32)
-        for r in range(4):
-            here_r = slice(r * blk, (r + 1) * blk)
-            mt[here_r, :] = pick(
-                ids[here_r, 2:3], ids[here_r, 3:4], expert, a_refs[r][...], b_refs[r][...]
-            )
-        for s, value in enumerate(t_right(mt[...], [xs[s] for s in pieces])):
-            outs[s][0] = value.astype(BF16)
-
-    def dwout(meta):
-        spot = lambda e, m: (e, 0, 0)
-        ins = [(v, None, None) for v in ag_a + ag_b]
-        ins += [(sel, None, None)] + [(d, None, None) for d in d_pieces]
-        outs = [((experts, ff, ds), BF16, (1, ff, ds), spot)] * parts
-        return run(
-            dwout_body, "dwout", (experts,), meta, ins, outs,
-            [pltpu.VMEM((parts, rp, ds), BF16), pltpu.VMEM((rp, 8), F32), pltpu.VMEM((rp, ff), BF16)],
-            flops=2 * rp * experts * parts * ds * ff,
-        )
-
-    def dwproj_body(m, *refs):
-        a_refs, b_refs = refs[:4], refs[4:8]
-        sel_ref, d_ref = refs[8:10]
-        outs = refs[10 : 10 + parts]
-        lo, hi = refs[10 + parts :]
-        e = pl.program_id(0)
-
-        @pl.when(e == 0)
-        def _():
-            for r in range(4):
-                lanes = pl.ds(pl.multiple_of(m[2 + r] * HD, HD), HD)
-                lo[:, lanes] = a_refs[r][...]
-                hi[:, lanes] = b_refs[r][...]
-
-        x = pick(sel_ref[:, 0:1], sel_ref[:, 1:2], e.astype(F32), lo[...], hi[...])
-        for s, value in enumerate(t_right(x, [d_ref[s] for s in pieces])):
-            outs[s][0] = value.astype(BF16)
-
-    def dwproj(meta):
-        ins = [(v, None, None) for v in gm_a + gm_b]
-        ins += [(sel, None, None), (dafter_low, None, None)]
-        return run(
-            dwproj_body, "dwproj", (experts,), meta, ins,
-            [((experts, hw, ds), BF16, (1, hw, ds), lambda e, m: (e, 0, 0))] * parts,
-            [pltpu.VMEM((rp, hw), BF16)] * 2,
-            flops=2 * rp * experts * hw * parts * ds,
-        )
 
     def dwqkv_body(m, *refs):
         a_refs, b_refs = refs[:4], refs[4:8]
@@ -1124,35 +1140,22 @@
             flops=2 * rp * (experts + 2) * hw * parts * ds,
         )
 
-    tiles = ff // HD
-
-    def fold_body(m, *refs):
-        add_refs, out_ref = refs[:parts], refs[parts]
-        for j in range(2):
-            total = add_refs[0][0, j].astype(F32)
-            for ref in add_refs[1:]:
-                total = total + ref[0, j].astype(F32)
-            for t in range(tiles):
-                out_ref[0, pl.ds(2 * t + j, ds, stride=2 * tiles), :] = total[
-                    :, t * HD : (t + 1) * HD
-                ]
-
-    def fold(sums):
-        got = [sums[0]] + [by_part(sums[s], s) for s in pieces[1:]]
-        spot = lambda e, m: (e, 0, 0, 0)
-        ins = [(v, (1, 2, ds, ff), spot) for v in got]
-        outs = [((experts, 2 * tiles * ds, HD), F32, (1, 2 * tiles * ds, HD), lambda e, m: (e, 0, 0))]
-        total = run(fold_body, "fold", (experts,), meta, ins, outs)[0]
-        total = total.reshape(experts, ds, tiles, 2, HD).transpose(0, 1, 3, 2, 4)
-        return total.reshape(experts, ds, 2, ff)
-
-    expertin_grad = fold(dwin(meta))
-    expertout_grad = exchange(dwout(meta))
-    proj_grad = exchange(dwproj(meta))
-    sums = dwqkv(meta)
-    query_grad, kv_grad = exchange(sums[:parts]), exchange(sums[parts:])
-
-    down_totals = wide_sum_z(*down(meta))
+    dwqkv_sums = dwqkv(after(meta, da_halves))
+    da_halves = held([z_second(half) for half in da_halves], dwqkv_sums[0])
+    da_totals = [half for v in da_halves for half in z_last(v)]
+    expertin_grad = fold((dwin_gate, dwin_up), after(meta, dwqkv_sums[0]))
+    ins = [(t, None, None) for t in da_totals]
+    ins += [(x_stack, None, None), (dafter, None, None)]
+    ins += [(gain_a, None, None), (router_a, None, None), (back_a, None, None)]
+    outs = [((parts, rp, ds), BF16, None, None), ((experts + 1, parts, ds), F32, None, None)]
+    dinput, small_a = run(
+        functools.partial(norm_back_body, False), "norm_back_first", (1,),
+        after(meta, expertin_grad), ins, outs,
+    )
+    expertout_grad = exchange(dwout_sums)
+    proj_grad = exchange(dwproj_sums)
+    query_grad, kv_grad = exchange(dwqkv_sums[:parts]), exchange(dwqkv_sums[parts:])
+    down_totals = wide_sum_z(*down_halves)
 
     def finish_body(m, *refs):
         t_refs, after_ref, out_ref = refs[:2], refs[2], refs[3]
@@ -1208,10 +1211,12 @@
         landed = lax.all_to_all(
             spread_rows.reshape(dp, seqs * per, ds), "dp", 0, 0, tiled=True
         )
-        return landed.transpose(1, 0, 2).reshape(seqs, per, width)
-
-    layer_out = unpack(out_rows, x_all, False)
-    input_grad = unpack(dinput, d_all, True)
+        return landed.transpose(1, 0, 2).reshape(seqs, per, width), spread_rows
+
+    layer_out, _ = unpack(out_rows, x_all, False)
+    input_grad, last_rows = unpack(dinput, d_all, True)
+    vectors = whole_vectors(after(small_a, last_rows), small_f)
+    (attnrouter_grad, attngain_grad), (ffnrouter_grad, ffngain_grad) = vectors
     return (
         layer_out,
         input_grad,

time: 741 us -> 672 us (0.907)
  local copies, waits for them, and re-layouts: 81.4 us -> 44.4 us
  waiting for transfers between devices: 233 us -> 218 us
    ppermute x57 -> x60, waiting for transfers between devices: 179 us -> 136 us  [by_group(): return lax.ppermute(value, 'dp', pairs)]
    ppermute x25, waiting for transfers between devices: 42.4 us -> 61.9 us  [by_z(): return lax.ppermute(value, 'tensor', [(a, a ^ mask) for a in range(tp)])]
    reshape x4 -> x3, local copies, waits for them, and re-layouts: 21.4 us -> 3.79 us  [the longest x2 2.62 us: unpack(): return (landed.transpose(1, 0, 2).reshape(seqs, per, width), spread_rows)]
    unnamed x246 -> x184, local copies, waits for them, and re-layouts: 40.2 us -> 23.5 us
    ppermute x57 -> x60, starting transfers between devices: 66 us -> 64.2 us  [by_group(): return lax.ppermute(value, 'dp', pairs)]
  transfers between devices with their start and end apart: 108 -> 109, of which waited for: 46 -> 49; matrix products, arithmetic and copies ran while one was open for 10% -> 10% of each run, Pallas kernels for 30% -> 31%
where the time goes in v4:
time: 672 us; the launch traced here: 667 us
  Pallas kernels  238 us (35%)
  waiting for transfers between devices  218 us (32%)
  starting transfers between devices  127 us (19%)
  local copies, waits for them, and re-layouts  44.4 us (7%)
  other arithmetic  35.8 us (5%)
    pallas_call x30, Pallas kernels, run(): pl.pallas_call(body, name=name, grid_spec=pltpu.PrefetchScalarGridSpec(nu...  238 us
    ppermute x60, waiting for transfers between devices, by_group(): return lax.ppermute(value, 'dp', pairs)  136 us
    ppermute x60, starting transfers between devices, by_group(): return lax.ppermute(value, 'dp', pairs)  64.2 us
    ppermute x25, waiting for transfers between devices, by_z(): return lax.ppermute(value, 'tensor', [(a, a ^ mask) for a in range(tp)])  61.9 us
    ppermute x25, starting transfers between devices, by_z(): return lax.ppermute(value, 'tensor', [(a, a ^ mask) for a in range(tp)])  36.6 us
    unnamed x184, local copies, waits for them, and re-layouts  23.5 us
    convert_element_type x22, other arithmetic, both(): return (a.astype(F32) + b.astype(F32)).astype(BF16)  15 us
  transfers between devices with their start and end apart: 109, of which 49 were waited for; matrix products, arithmetic and copies ran while one was open for 10% of the time, Pallas kernels for 31%

profile of v4, /device:TPU:0, one launch (start us, length us, event | category | flops | bytes accessed | tf_op | source)
XLA Modules:
  0.0 666.7 jit_solution(13832559014128605058)
XLA Ops:
  3.4 5.3 all-to-all-start
  9.8 5.9 copy.176
  18.9 5.2 all-to-all-done
  24.1 3.9 all-to-all-start.1
  30.1 4.0 pack.3
  38.2 5.1 all-to-all-done.1
  44.2 4.0 pack.2
  49.1 8.5 %qkv.1 = (bf16[768,256]{1,0:T(8,128)(2,1)}, bf16[768,256]{1,0:T(8,128)(2,1)}, bf16[768,256]{1,0:T(8,128)(2,1)}, bf16[768,256]{1,0:T(8,128)(2,1)}, bf16[768,256]{...) custom-call(s32[20]{0:T(128)} %stack.132.m, ...), custom_call_target="tpu_custom_call" | custom-call | flops 2415919104 | bytes 7137280 | tf_op jit(solution)/shard_map/qkv/pallas_call | solution.py:61
  61.4 6.2 collective-permute-done.6
  78.0 12.0 %dhidden.1 = (bf16[192,1408]{1,0:T(8,128)(2,1)}, bf16[192,1408]{1,0:T(8,128)(2,1)}, bf16[192,1408]{1,0:T(8,128)(2,1)}, bf16[192,1408]{1,0:T(8,128)(2,1)}, bf16[1...) custom-call(s32[20]{0:T(128)} %stack.132.m, ...), custom_call_target="tpu_custom_call" | custom-call | flops 4429185024 | bytes 11714560 | tf_op jit(solution)/shard_map/dhidden/pallas_call | solution.py:61
  92.2 8.1 %collective-permute-done.10.b1 = bf16[768,256]{1,0:T(8,128)(2,1)} collective-permute-done((bf16[768,256]{1,0:T(8,128)(2,1)S(1)}, bf16[768,256]{1,0:T(8,128)(2,1)}, u32[]{:S(2)}, u32[]{:S(2)}) %collective-permute-start.10) | collective-permute-done | bytes 393248 | tf_op jit(solution)/shard_map/ppermute | solution.py:160
  100.5 4.6 rope.1
  108.9 7.9 %attend.1 = (bf16[768,128]{1,0:T(8,128)(2,1)}, bf16[768,128]{1,0:T(8,128)(2,1)}, bf16[768,128]{1,0:T(8,128)(2,1)}, bf16[768,128]{1,0:T(8,128)(2,1)}) custom-call(s32[20]{0:T(128)} %stack.132.m, bf16[768,256]{1,0:T(8,128)(2,1)} %get-tuple-element.171.q_ref.refs_0_, bf16[768,256]{1,0:T(8,128)(2,1)} %get-tuple-element.172.kv_ref.refs_1_, ...), custom_call_target="tpu_custom_call" | custom-call | flops 301989888 | bytes 1753088 | tf_op jit(solution)/shard_map/attend/pallas_call | solution.py:61
  120.5 3.9 collective-permute-done.15.refs_1_
  126.4 3.3 collective-permute-done.17.refs_6_
  133.3 3.2 collective-permute-done.19.refs_3_
  138.2 6.7 %proj.2 = (bf16[2,192,256]{2,1,0:T(8,128)(2,1)}, bf16[2,192,256]{2,1,0:T(8,128)(2,1)}) custom-call(s32[20]{0:T(128)} %stack.132.m, bf16[768,128]{1,0:T(8,128)(2,1)} %get-tuple-element.173.refs_0_, bf16[768,128]{1,0:T(8,128)(2,1)} %copy-done.26, bf16[768,128]{1,0:T(8,128)(2,1)} %copy-done.27, bf16[768,128]{1,0:T(8,128)(2,1)} %copy-done.30, ...), custom_call_target="tpu_custom_call" | custom-call | flops 805306368 | bytes 4087808 | tf_op jit(solution)/shard_map/proj/pallas_call | solution.py:61
  151.8 3.7 collective-permute-start.23
  161.8 6.7 %proj.3 = (bf16[2,192,256]{2,1,0:T(8,128)(2,1)}, bf16[2,192,256]{2,1,0:T(8,128)(2,1)}) custom-call(s32[20]{0:T(128)} %stack.132.m, bf16[768,128]{1,0:T(8,128)(2,1)} %get-tuple-element.173.refs_0_, bf16[768,128]{1,0:T(8,128)(2,1)} %copy-done.26, bf16[768,128]{1,0:T(8,128)(2,1)} %copy-done.27, bf16[768,128]{1,0:T(8,128)(2,1)} %copy-done.30, ...), custom_call_target="tpu_custom_call" | custom-call | flops 805306368 | bytes 4087808 | tf_op jit(solution)/shard_map/proj/pallas_call | solution.py:61
  169.4 7.2 %collective-permute-done.26 = bf16[2,192,256]{2,1,0:T(8,128)(2,1)S(1)} collective-permute-done((bf16[2,192,256]{2,1,0:T(8,128)(2,1)}, bf16[2,192,256]{2,1,0:T(8,128)(2,1)S(1)}, u32[]{:S(2)}, u32[]{:S(2)}) %collective-permute-start.26) | collective-permute-done | bytes 196640 | tf_op jit(solution)/shard_map/ppermute | solution.py:175
  179.5 6.8 %collective-permute-done.27 = bf16[2,192,256]{2,1,0:T(8,128)(2,1)S(1)} collective-permute-done((bf16[2,192,256]{2,1,0:T(8,128)(2,1)S(1)}, bf16[2,192,256]{2,1,0:T(8,128)(2,1)S(1)}, u32[]{:S(2)}, u32[]{:S(2)}) %collective-permute-start.27) | collective-permute-done | bytes 196640 | tf_op jit(solution)/shard_map/ppermute | solution.py:175
  197.5 4.4 norm.1
  206.9 3.9 collective-permute-done.34
  211.6 10.2 %up.2 = (bf16[2,192,1408]{2,1,0:T(8,128)(2,1)}, bf16[2,192,1408]{2,1,0:T(8,128)(2,1)}, bf16[2,192,1408]{2,1,0:T(8,128)(2,1)}, bf16[2,192,1408]{2,1,0:T(8,128)(2,1)}) custom-call(s32[20]{0:T(128)} %stack.132.m, bf16[2,768,256]{2,1,0:T(8,128)(2,1)} %get-tuple-element.203.refs_0_.refs_1_, bf16[2,768,256]{2,1,0:T(8,128)(2,1)} %get-tuple-element.203.refs_0_.refs_1_, ...), custom_call_target="tpu_custom_call" | custom-call | flops 4429185024 | bytes 17481728 | tf_op jit(solution)/shard_map/up/pallas_call | solution.py:61
  223.5 10.5 %up.3 = (bf16[2,192,1408]{2,1,0:T(8,128)(2,1)}, bf16[2,192,1408]{2,1,0:T(8,128)(2,1)}, bf16[2,192,1408]{2,1,0:T(8,128)(2,1)}, bf16[2,192,1408]{2,1,0:T(8,128)(2,1)}) custom-call(s32[20]{0:T(128)} %stack.132.m, bf16[2,768,256]{2,1,0:T(8,128)(2,1)} %get-tuple-element.203.refs_0_.refs_1_, bf16[2,768,256]{2,1,0:T(8,128)(2,1)} %get-tuple-element.203.refs_0_.refs_1_, ...), custom_call_target="tpu_custom_call" | custom-call | flops 4429185024 | bytes 17481728 | tf_op jit(solution)/shard_map/up/pallas_call | solution.py:61
  236.5 10.4 %collective-permute-done.40 = bf16[2,192,1408]{2,1,0:T(8,128)(2,1)} collective-permute-done((bf16[2,192,1408]{2,1,0:T(8,128)(2,1)}, bf16[2,192,1408]{2,1,0:T(8,128)(2,1)}, u32[]{:S(2)}, u32[]{:S(2)}) %collective-permute-start.40) | collective-permute-done | bytes 1081376 | tf_op jit(solution)/shard_map/ppermute | solution.py:160
  252.0 16.7 %collective-permute-done.41.refs_5_ = bf16[2,192,1408]{2,1,0:T(8,128)(2,1)S(1)} collective-permute-done((bf16[2,192,1408]{2,1,0:T(8,128)(2,1)}, bf16[2,192,1408]{2,1,0:T(8,128)(2,1)S(1)}, u32[]{:S(2)}, u32[]{:S(2)}) %collective-permute-start.41) | collective-permute-done | bytes 1081376 | tf_op jit(solution)/shard_map/ppermute | solution.py:160
  272.1 14.4 %collective-permute-done.42.refs_2_ = bf16[2,192,1408]{2,1,0:T(8,128)(2,1)S(1)} collective-permute-done((bf16[2,192,1408]{2,1,0:T(8,128)(2,1)}, bf16[2,192,1408]{2,1,0:T(8,128)(2,1)S(1)}, u32[]{:S(2)}, u32[]{:S(2)}) %collective-permute-start.42) | collective-permute-done | bytes 1081376 | tf_op jit(solution)/shard_map/ppermute | solution.py:160
  288.5 8.2 %mid.1 = (bf16[192,1408]{1,0:T(8,128)(2,1)}, bf16[192,1408]{1,0:T(8,128)(2,1)}, bf16[2,192,1408]{2,1,0:T(8,128)(2,1)}, bf16[2,192,1408]{2,1,0:T(8,128)(2,1)}, f32[192,8]{1,0:T(8,128)}) custom-call(s32[20]{0:T(128)} %stack.132.m, bf16[2,192,1408]{2,1,0:T(8,128)(2,1)} %get-tuple-element.206.refs_0_, bf16[2,192,1408]{2,1,0:T(8,128)(2,1)} %copy-done.20, ...), custom_call_target="tpu_custom_call" | custom-call | bytes 13006848 | tf_op jit(solution)/shard_map/mid/pallas_call | solution.py:61
  301.0 18.0 %collective-permute-done.44.refs_0_.refs_2_ = bf16[2,192,1408]{2,1,0:T(8,128)(2,1)S(1)} collective-permute-done((bf16[2,192,1408]{2,1,0:T(8,128)(2,1)}, bf16[2,192,1408]{2,1,0:T(8,128)(2,1)S(1)}, u32[]{:S(2)}, u32[]{:S(2)}) %collective-permute-start.44) | collective-permute-done | bytes 1081376 | tf_op jit(solution)/shard_map/ppermute | solution.py:160
  320.3 21.9 %collective-permute-done.46.refs_2_.refs_6_ = bf16[2,192,1408]{2,1,0:T(8,128)(2,1)} collective-permute-done((bf16[2,192,1408]{2,1,0:T(8,128)(2,1)}, bf16[2,192,1408]{2,1,0:T(8,128)(2,1)}, u32[]{:S(2)}, u32[]{:S(2)}) %collective-permute-start.46) | collective-permute-done | bytes 1081376 | tf_op jit(solution)/shard_map/ppermute | solution.py:160
  345.1 11.1 %dx.3 = (bf16[2,192,256]{2,1,0:T(8,128)(2,1)}, bf16[2,192,256]{2,1,0:T(8,128)(2,1)}) custom-call(s32[20]{0:T(128)} %stack.132.m, bf16[2,192,1408]{2,1,0:T(8,128)(2,1)} %get-tuple-element.217.refs_0_, bf16[2,192,1408]{2,1,0:T(8,128)(2,1)} %copy-done.17, bf16[2,192,1408]{2,1,0:T(8,128)(2,1)} %get-tuple-element.218.refs_4_.refs_2_, ...), custom_call_target="tpu_custom_call" | custom-call | flops 4429185024 | bytes 16302080 | tf_op jit(solution)/shard_map/dx/pallas_call | solution.py:61
  357.5 6.0 collective-permute-done.55
  365.7 7.6 %collective-permute-done.56 = bf16[2,192,256]{2,1,0:T(8,128)(2,1)S(1)} collective-permute-done((bf16[2,192,256]{2,1,0:T(8,128)(2,1)S(1)}, bf16[2,192,256]{2,1,0:T(8,128)(2,1)S(1)}, u32[]{:S(2)}, u32[]{:S(2)}) %collective-permute-start.56) | collective-permute-done | bytes 196640 | tf_op jit(solution)/shard_map/ppermute | solution.py:175
  378.4 11.1 %dx.2 = (bf16[2,192,256]{2,1,0:T(8,128)(2,1)}, bf16[2,192,256]{2,1,0:T(8,128)(2,1)}) custom-call(s32[20]{0:T(128)} %stack.132.m, bf16[2,192,1408]{2,1,0:T(8,128)(2,1)} %copy-done.16, bf16[2,192,1408]{2,1,0:T(8,128)(2,1)} %collective-permute-done.48.refs_1_.refs_3_, bf16[2,192,1408]{2,1,0:T(8,128)(2,1)} %collective-permute-done.46.refs_2_.refs_6_, ...), custom_call_target="tpu_custom_call" | custom-call | flops 4429185024 | bytes 16302080 | tf_op jit(solution)/shard_map/dx/pallas_call | solution.py:61
  398.5 6.6 collective-permute-done.58
  408.5 11.4 %dwin.2 = (bf16[4,256,1408]{2,1,0:T(8,128)(2,1)}, bf16[4,256,1408]{2,1,0:T(8,128)(2,1)}) custom-call(s32[20]{0:T(128)} %stack.132.m, bf16[2,192,1408]{2,1,0:T(8,128)(2,1)} %get-tuple-element.217.refs_0_, bf16[2,192,1408]{2,1,0:T(8,128)(2,1)} %copy-done.17, bf16[2,192,1408]{2,1,0:T(8,128)(2,1)} %copy-done.16, ...), custom_call_target="tpu_custom_call" | custom-call | flops 4429185024 | bytes 15228928 | tf_op jit(solution)/shard_map/dwin/pallas_call | solution.py:61
  420.7 6.5 norm_back.1
  427.2 5.9 dmix.1
  437.3 11.3 %dwin.3 = (bf16[4,256,1408]{2,1,0:T(8,128)(2,1)}, bf16[4,256,1408]{2,1,0:T(8,128)(2,1)}) custom-call(s32[20]{0:T(128)} %stack.132.m, bf16[2,192,1408]{2,1,0:T(8,128)(2,1)} %get-tuple-element.217.refs_0_, bf16[2,192,1408]{2,1,0:T(8,128)(2,1)} %copy-done.17, bf16[2,192,1408]{2,1,0:T(8,128)(2,1)} %copy-done.16, ...), custom_call_target="tpu_custom_call" | custom-call | flops 4429185024 | bytes 15228928 | tf_op jit(solution)/shard_map/dwin/pallas_call | solution.py:61
  450.4 4.1 collective-permute-done.69.refs_9_
  457.3 14.4 %attend_back.1 = (bf16[768,256]{1,0:T(8,128)(2,1)}, f32[768,256]{1,0:T(8,128)}, f32[256,256]{1,0:T(8,128)}, f32[8,768]{1,0:T(8,128)}) custom-call(s32[20]{0:T(128)} %stack.132.m, bf16[768,256]{1,0:T(8,128)(2,1)} %get-tuple-element.171.q_ref.refs_0_, bf16[768,256]{1,0:T(8,128)(2,1)} %get-tuple-element.172.kv_ref.refs_1_, bf16[256,256]{1,0:T(8,128)(2,1)} %copy-done.45, ...), custom_call_target="tpu_custom_call" | custom-call | flops 754974720 | bytes 4792320 | tf_op jit(solution)/shard_map/attend_back/pallas_call | solution.py:61
  476.0 3.6 dkv.1
  482.7 16.4 %down.1 = (bf16[2,384,256]{2,1,0:T(8,128)(2,1)}, bf16[2,384,256]{2,1,0:T(8,128)(2,1)}, bf16[4,1408,256]{2,1,0:T(8,128)(2,1)}, bf16[4,1408,256]{2,1,0:T(8,128)(2,1)}) custom-call(s32[20]{0:T(128)} %stack.132.m, bf16[192,1408]{1,0:T(8,128)(2,1)} %get-tuple-element.228.refs_0_, bf16[192,1408]{1,0:T(8,128)(2,1)} %copy-done.82, ...), custom_call_target="tpu_custom_call" | custom-call | flops 8858370048 | bytes 17457152 | tf_op jit(solution)/shard_map/down/pallas_call | solution.py:61
  503.4 6.7 %collective-permute-done.82.refs_3_ = bf16[768,256]{1,0:T(8,128)(2,1)S(1)} collective-permute-done((bf16[768,256]{1,0:T(8,128)(2,1)S(1)}, bf16[768,256]{1,0:T(8,128)(2,1)S(1)}, u32[]{:S(2)}, u32[]{:S(2)}) %collective-permute-start.82) | collective-permute-done | bytes 393248 | tf_op jit(solution)/shard_map/ppermute | solution.py:160
  515.3 7.5 %dwproj.1 = (bf16[4,512,256]{2,1,0:T(8,128)(2,1)}, bf16[4,512,256]{2,1,0:T(8,128)(2,1)}) custom-call(s32[20]{0:T(128)} %stack.132.m, bf16[768,128]{1,0:T(8,128)(2,1)} %get-tuple-element.173.refs_0_, bf16[768,128]{1,0:T(8,128)(2,1)} %copy-done.26, bf16[768,128]{1,0:T(8,128)(2,1)} %copy-done.27, bf16[768,128]{1,0:T(8,128)(2,1)} %copy-done.30, ...), custom_call_target="tpu_custom_call" | custom-call | flops 1610612736 | bytes 4481024 | tf_op jit(solution)/shard_map/dwproj/pallas_call | solution.py:61
  529.4 6.4 dattn.2
  535.8 3.2 collective-permute-done.96
  539.0 8.8 %collective-permute-start.84 = (bf16[2,192,256]{2,1,0:T(8,128)(2,1)}, bf16[2,192,256]{2,1,0:T(8,128)(2,1)S(1)}, u32[]{:S(2)}, u32[]{:S(2)}) collective-permute-start(bf16[2,192,256]{2,1,0:T(8,128)(2,1)} %get-tuple-element.266), channel_id=1, source_target_pairs={{0,1},{1,0},{2,3},{3,2},{4,5},{5,4},{6,7},{7,6},{8,9},{9,8},{10,11... | collective-permute-start | bytes 589832 | tf_op jit(solution)/shard_map/ppermute | solution.py:175
  548.9 3.7 collective-permute-done.84
  556.0 6.4 dattn.3
  564.4 4.2 collective-permute-done.85
  570.2 9.4 %dwqkv.1 = (bf16[4,256,512]{2,1,0:T(8,128)(2,1)}, bf16[4,256,512]{2,1,0:T(8,128)(2,1)}, bf16[2,256,512]{2,1,0:T(8,128)(2,1)}, bf16[2,256,512]{2,1,0:T(8,128)(2,1)}) custom-call(s32[20]{0:T(128)} %stack.132.m, bf16[768,256]{1,0:T(8,128)(2,1)} %get-tuple-element.262.refs_0_, bf16[768,256]{1,0:T(8,128)(2,1)} %copy-done.11, bf16[768,256]{1,0:T(8,128)(2,1)} %copy-done.12, ...), custom_call_target="tpu_custom_call" | custom-call | flops 2415919104 | bytes 7102464 | tf_op jit(solution)/shard_map/dwqkv/pallas_call | solution.py:61
  583.1 4.2 collective-permute-done.89
  591.4 3.3 finish.1
  598.4 10.6 %fold.1 = f32[4,256,2,1408]{3,2,1,0:T(2,128)} custom-call(s32[20]{0:T(128)} %stack.132.m, bf16[4,256,1408]{2,1,0:T(8,128)(2,1)} %get-tuple-element.225.refs_0_, bf16[4,256,1408]{2,1,0:T(8,128)(2,1)} %copy-done.9, bf16[4,256,1408]{2,1,0:T(8,128)(2,1)} %get-tuple-element.244.refs_2_, bf16[4,256,1408]{2,1,0:T(8,128)(2,1)} %collective-permute-done.87.refs_3_), custom_call_target="tpu_custom_call" | custom-call | bytes 23068672 | tf_op jit(solution)/shard_map/fold/pallas_call | solution.py:61
  609.7 6.0 norm_back_first.1
  618.3 4.4 unpack.2
  622.7 3.6 all-to-all-start.2
  627.1 4.4 unpack.3
  638.8 3.6 collective-permute-done.99
  645.6 3.6 all-to-all-start.3
  653.6 5.9 convert_add_fusion
  659.5 5.0 all-to-all-done.3
  (492 shorter events, 196.4 us)
Async XLA Ops:
  3.4 20.7 %all-to-all-start = ((bf16[8,256,256]{2,1,0:T(8,128)(2,1)}), bf16[8,256,256]{2,1,0:T(8,128)(2,1)S(1)}, u32[]{:S(2)}, u32[]{:S(2)}) async-start(bf16[8,256,256]{2,1,0:T(8,128)(2,1)} %bitcast.106), calls=%async_computation | async-start | bytes 2097152 | tf_op jit(solution)/shard_map/all_to_all | solution.py:301
  8.7 39.6 %collective-permute-start.1 = (bf16[4,256,512]{2,1,0:T(8,128)(2,1)S(1)}, bf16[4,256,512]{2,1,0:T(8,128)(2,1)}, u32[]{:S(2)}, u32[]{:S(2)}) collective-permute-start(bf16[4,256,512]{2,1,0:T(8,128)(2,1)S(1)} %copy-done.4), channel_id=1, source_target_pairs={{0,4},{4,0},{8,12},{12,8},{16,20},{20,16},{24,28},{28,24},{1,5},{5... | collective-permute-start | bytes 3145736 | tf_op jit(solution)/shard_map/ppermute | solution.py:164
  9.3 39.0 %collective-permute-start.2 = (bf16[2,256,512]{2,1,0:T(8,128)(2,1)}, bf16[2,256,512]{2,1,0:T(8,128)(2,1)}, u32[]{:S(2)}, u32[]{:S(2)}) collective-permute-start(bf16[2,256,512]{2,1,0:T(8,128)(2,1)} %refs_11_.5), channel_id=1, source_target_pairs={{0,4},{4,0},{8,12},{12,8},{16,20},{20,16},{24,28},{28,24},{1,5},{5... | collective-permute-start | bytes 1572872 | tf_op jit(solution)/shard_map/ppermute | solution.py:164
  9.3 68.7 %collective-permute-start.4 = (bf16[4,1408,256]{2,1,0:T(8,128)(2,1)}, bf16[4,1408,256]{2,1,0:T(8,128)(2,1)}, u32[]{:S(2)}, u32[]{:S(2)}) collective-permute-start(bf16[4,1408,256]{2,1,0:T(8,128)(2,1)} %refs_11_.3), channel_id=1, source_target_pairs={{0,4},{4,0},{8,12},{12,8},{16,20},{20,16},{24,28},{28,24},{1,5},{5... | collective-permute-start | bytes 8650760 | tf_op jit(solution)/shard_map/ppermute | solution.py:164
  15.7 195.9 %collective-permute-start.37 = (bf16[4,2,256,1408]{3,2,1,0:T(8,128)(2,1)}, bf16[4,2,256,1408]{3,2,1,0:T(8,128)(2,1)}, u32[]{:S(2)}, u32[]{:S(2)}) collective-permute-start(bf16[4,2,256,1408]{3,2,1,0:T(8,128)(2,1)} %bitcast.104.refs_2_.refs_4_), channel_id=1, source_target_pairs={{0,4},{4,0},{8,12},{12,8},{16,20},{20,16},{24,28},{28,24},{1,5},{5... | collective-permute-start | bytes 17301512 | tf_op jit(solution)/shard_map/ppermute | solution.py:164
  24.1 19.2 %all-to-all-start.1 = ((bf16[8,256,256]{2,1,0:T(8,128)(2,1)}), bf16[8,256,256]{2,1,0:T(8,128)(2,1)S(1)}, u32[]{:S(2)}, u32[]{:S(2)}) async-start(bf16[8,256,256]{2,1,0:T(8,128)(2,1)} %bitcast.105), calls=%async_computation.1 | async-start | bytes 2097152 | tf_op jit(solution)/shard_map/all_to_all | solution.py:304
  34.1 14.2 %collective-permute-start = (bf16[768,256]{1,0:T(8,128)(2,1)}, bf16[768,256]{1,0:T(8,128)(2,1)S(1)}, u32[]{:S(2)}, u32[]{:S(2)}) collective-permute-start(bf16[768,256]{1,0:T(8,128)(2,1)} %get-tuple-element.154), channel_id=1, source_target_pairs={{0,4},{4,0},{8,12},{12,8},{16,20},{20,16},{24,28},{28,24},{1,5},{5... | collective-permute-start | bytes 1179656 | tf_op jit(solution)/shard_map/ppermute | solution.py:164
  72.9 60.4 %collective-permute-start.21 = (bf16[4,512,256]{2,1,0:T(8,128)(2,1)S(1)}, bf16[4,512,256]{2,1,0:T(8,128)(2,1)S(1)}, u32[]{:S(2)}, u32[]{:S(2)}) collective-permute-start(bf16[4,512,256]{2,1,0:T(8,128)(2,1)S(1)} %copy-done.3), channel_id=1, source_target_pairs={{0,4},{4,0},{8,12},{12,8},{16,20},{20,16},{24,28},{28,24},{1,5},{5... | collective-permute-start | bytes 3145736 | tf_op jit(solution)/shard_map/ppermute | solution.py:164
  74.6 15.5 %collective-permute-start.5 = (bf16[768,256]{1,0:T(8,128)(2,1)}, bf16[768,256]{1,0:T(8,128)(2,1)S(1)}, u32[]{:S(2)}, u32[]{:S(2)}) collective-permute-start(bf16[768,256]{1,0:T(8,128)(2,1)} %get-tuple-element.161), channel_id=1, source_target_pairs={{0,8},{4,12},{8,0},{12,4},{16,24},{20,28},{24,16},{28,20},{1,9},{5... | collective-permute-start | bytes 1179656 | tf_op jit(solution)/shard_map/ppermute | solution.py:160
  76.3 13.7 %collective-permute-start.8 = (bf16[768,256]{1,0:T(8,128)(2,1)}, bf16[768,256]{1,0:T(8,128)(2,1)}, u32[]{:S(2)}, u32[]{:S(2)}) collective-permute-start(bf16[768,256]{1,0:T(8,128)(2,1)} %get-tuple-element.166), channel_id=1, source_target_pairs={{0,16},{4,20},{8,24},{12,28},{16,0},{20,4},{24,8},{28,12},{1,17},{... | collective-permute-start | bytes 1179656 | tf_op jit(solution)/shard_map/ppermute | solution.py:160
  146.5 15.4 %collective-permute-start.24 = (bf16[192,1408]{1,0:T(8,128)(2,1)}, bf16[192,1408]{1,0:T(8,128)(2,1)S(1)}, u32[]{:S(2)}, u32[]{:S(2)}) collective-permute-start(bf16[192,1408]{1,0:T(8,128)(2,1)} %get-tuple-element.186), channel_id=1, source_target_pairs={{0,8},{4,12},{8,0},{12,4},{16,24},{20,28},{24,16},{28,20},{1,9},{5... | collective-permute-start | bytes 1622024 | tf_op jit(solution)/shard_map/ppermute | solution.py:160
  148.0 13.8 %collective-permute-start.25 = (bf16[192,1408]{1,0:T(8,128)(2,1)}, bf16[192,1408]{1,0:T(8,128)(2,1)S(1)}, u32[]{:S(2)}, u32[]{:S(2)}) collective-permute-start(bf16[192,1408]{1,0:T(8,128)(2,1)} %get-tuple-element.187), channel_id=1, source_target_pairs={{0,16},{4,20},{8,24},{12,28},{16,0},{20,4},{24,8},{28,12},{1,17},{... | collective-permute-start | bytes 1622024 | tf_op jit(solution)/shard_map/ppermute | solution.py:160
  155.4 31.0 %collective-permute-start.28 = (bf16[192,1408]{1,0:T(8,128)(2,1)}, bf16[192,1408]{1,0:T(8,128)(2,1)S(1)}, u32[]{:S(2)}, u32[]{:S(2)}) collective-permute-start(bf16[192,1408]{1,0:T(8,128)(2,1)} %get-tuple-element.193), channel_id=1, source_target_pairs={{0,8},{4,12},{8,0},{12,4},{16,24},{20,28},{24,16},{28,20},{1,9},{5... | collective-permute-start | bytes 1622024 | tf_op jit(solution)/shard_map/ppermute | solution.py:160
  159.4 27.0 %collective-permute-start.29 = (bf16[192,1408]{1,0:T(8,128)(2,1)}, bf16[192,1408]{1,0:T(8,128)(2,1)S(1)}, u32[]{:S(2)}, u32[]{:S(2)}) collective-permute-start(bf16[192,1408]{1,0:T(8,128)(2,1)} %get-tuple-element.194), channel_id=1, source_target_pairs={{0,16},{4,20},{8,24},{12,28},{16,0},{20,4},{24,8},{28,12},{1,17},{... | collective-permute-start | bytes 1622024 | tf_op jit(solution)/shard_map/ppermute | solution.py:160
  186.4 25.2 %collective-permute-start.35 = (bf16[192,1408]{1,0:T(8,128)(2,1)S(1)}, bf16[192,1408]{1,0:T(8,128)(2,1)S(1)}, u32[]{:S(2)}, u32[]{:S(2)}) collective-permute-start(bf16[192,1408]{1,0:T(8,128)(2,1)S(1)} %add_convert_fusion.3), channel_id=1, source_target_pairs={{0,16},{4,20},{8,24},{12,28},{16,0},{20,4},{24,8},{28,12},{1,17},{... | collective-permute-start | bytes 1622024 | tf_op jit(solution)/shard_map/ppermute | solution.py:160
  187.5 24.1 %collective-permute-start.36 = (bf16[192,1408]{1,0:T(8,128)(2,1)S(1)}, bf16[192,1408]{1,0:T(8,128)(2,1)S(1)}, u32[]{:S(2)}, u32[]{:S(2)}) collective-permute-start(bf16[192,1408]{1,0:T(8,128)(2,1)S(1)} %add_convert_fusion.2), channel_id=1, source_target_pairs={{0,8},{4,12},{8,0},{12,4},{16,24},{20,28},{24,16},{28,20},{1,9},{5... | collective-permute-start | bytes 1622024 | tf_op jit(solution)/shard_map/ppermute | solution.py:160
  221.9 25.0 %collective-permute-start.40 = (bf16[2,192,1408]{2,1,0:T(8,128)(2,1)}, bf16[2,192,1408]{2,1,0:T(8,128)(2,1)}, u32[]{:S(2)}, u32[]{:S(2)}) collective-permute-start(bf16[2,192,1408]{2,1,0:T(8,128)(2,1)} %get-tuple-element.210), channel_id=1, source_target_pairs={{0,16},{4,20},{8,24},{12,28},{16,0},{20,4},{24,8},{28,12},{1,17},{... | collective-permute-start | bytes 3244040 | tf_op jit(solution)/shard_map/ppermute | solution.py:160
  223.0 26.5 %collective-permute-start.39 = (bf16[2,192,1408]{2,1,0:T(8,128)(2,1)}, bf16[2,192,1408]{2,1,0:T(8,128)(2,1)}, u32[]{:S(2)}, u32[]{:S(2)}) collective-permute-start(bf16[2,192,1408]{2,1,0:T(8,128)(2,1)} %get-tuple-element.204), channel_id=1, source_target_pairs={{0,8},{4,12},{8,0},{12,4},{16,24},{20,28},{24,16},{28,20},{1,9},{5... | collective-permute-start | bytes 3244040 | tf_op jit(solution)/shard_map/ppermute | solution.py:160
  234.0 34.7 %collective-permute-start.41 = (bf16[2,192,1408]{2,1,0:T(8,128)(2,1)}, bf16[2,192,1408]{2,1,0:T(8,128)(2,1)S(1)}, u32[]{:S(2)}, u32[]{:S(2)}) collective-permute-start(bf16[2,192,1408]{2,1,0:T(8,128)(2,1)} %get-tuple-element.211), channel_id=1, source_target_pairs={{0,16},{4,20},{8,24},{12,28},{16,0},{20,4},{24,8},{28,12},{1,17},{... | collective-permute-start | bytes 3244040 | tf_op jit(solution)/shard_map/ppermute | solution.py:160
  235.0 33.7 %collective-permute-start.38 = (bf16[2,192,1408]{2,1,0:T(8,128)(2,1)}, bf16[2,192,1408]{2,1,0:T(8,128)(2,1)S(1)}, u32[]{:S(2)}, u32[]{:S(2)}) collective-permute-start(bf16[2,192,1408]{2,1,0:T(8,128)(2,1)} %get-tuple-element.207), channel_id=1, source_target_pairs={{0,8},{4,12},{8,0},{12,4},{16,24},{20,28},{24,16},{28,20},{1,9},{5... | collective-permute-start | bytes 3244040 | tf_op jit(solution)/shard_map/ppermute | solution.py:160
  268.8 17.8 %collective-permute-start.42 = (bf16[2,192,1408]{2,1,0:T(8,128)(2,1)}, bf16[2,192,1408]{2,1,0:T(8,128)(2,1)S(1)}, u32[]{:S(2)}, u32[]{:S(2)}) collective-permute-start(bf16[2,192,1408]{2,1,0:T(8,128)(2,1)} %add_convert_fusion.1), channel_id=1, source_target_pairs={{0,16},{4,20},{8,24},{12,28},{16,0},{20,4},{24,8},{28,12},{1,17},{... | collective-permute-start | bytes 3244040 | tf_op jit(solution)/shard_map/ppermute | solution.py:160
  270.1 18.4 %collective-permute-start.43 = (bf16[2,192,1408]{2,1,0:T(8,128)(2,1)}, bf16[2,192,1408]{2,1,0:T(8,128)(2,1)}, u32[]{:S(2)}, u32[]{:S(2)}) collective-permute-start(bf16[2,192,1408]{2,1,0:T(8,128)(2,1)} %add_convert_fusion), channel_id=1, source_target_pairs={{0,8},{4,12},{8,0},{12,4},{16,24},{20,28},{24,16},{28,20},{1,9},{5... | collective-permute-start | bytes 3244040 | tf_op jit(solution)/shard_map/ppermute | solution.py:160
  296.7 22.4 %collective-permute-start.44 = (bf16[2,192,1408]{2,1,0:T(8,128)(2,1)}, bf16[2,192,1408]{2,1,0:T(8,128)(2,1)S(1)}, u32[]{:S(2)}, u32[]{:S(2)}) collective-permute-start(bf16[2,192,1408]{2,1,0:T(8,128)(2,1)} %get-tuple-element.217.refs_0_), channel_id=1, source_target_pairs={{0,16},{4,20},{8,24},{12,28},{16,0},{20,4},{24,8},{28,12},{1,17},{... | collective-permute-start | bytes 3244040 | tf_op jit(solution)/shard_map/ppermute | solution.py:160
  297.3 23.0 %collective-permute-start.45 = (bf16[2,192,1408]{2,1,0:T(8,128)(2,1)}, bf16[2,192,1408]{2,1,0:T(8,128)(2,1)S(1)}, u32[]{:S(2)}, u32[]{:S(2)}) collective-permute-start(bf16[2,192,1408]{2,1,0:T(8,128)(2,1)} %get-tuple-element.217.refs_0_), channel_id=1, source_target_pairs={{0,8},{4,12},{8,0},{12,4},{16,24},{20,28},{24,16},{28,20},{1,9},{5... | collective-permute-start | bytes 3244040 | tf_op jit(solution)/shard_map/ppermute | solution.py:160
  297.9 44.3 %collective-permute-start.46 = (bf16[2,192,1408]{2,1,0:T(8,128)(2,1)}, bf16[2,192,1408]{2,1,0:T(8,128)(2,1)}, u32[]{:S(2)}, u32[]{:S(2)}) collective-permute-start(bf16[2,192,1408]{2,1,0:T(8,128)(2,1)} %get-tuple-element.218.refs_4_.refs_2_), channel_id=1, source_target_pairs={{0,16},{4,20},{8,24},{12,28},{16,0},{20,4},{24,8},{28,12},{1,17},{... | collective-permute-start | bytes 3244040 | tf_op jit(solution)/shard_map/ppermute | solution.py:160
  299.3 44.0 %collective-permute-start.47 = (bf16[2,192,1408]{2,1,0:T(8,128)(2,1)}, bf16[2,192,1408]{2,1,0:T(8,128)(2,1)S(1)}, u32[]{:S(2)}, u32[]{:S(2)}) collective-permute-start(bf16[2,192,1408]{2,1,0:T(8,128)(2,1)} %get-tuple-element.218.refs_4_.refs_2_), channel_id=1, source_target_pairs={{0,8},{4,12},{8,0},{12,4},{16,24},{20,28},{24,16},{28,20},{1,9},{5... | collective-permute-start | bytes 3244040 | tf_op jit(solution)/shard_map/ppermute | solution.py:160
  300.9 55.3 %collective-permute-start.60 = (f32[8,192]{0,1:T(8,128)}, f32[8,192]{0,1:T(8,128)S(1)}, u32[]{:S(2)}, u32[]{:S(2)}) collective-permute-start(f32[8,192]{0,1:T(8,128)} %bitcast.132), channel_id=1, source_target_pairs={{0,1},{1,0},{2,3},{3,2},{4,5},{5,4},{6,7},{7,6},{8,9},{9,8},{10,11... | collective-permute-start | bytes 18440 | tf_op jit(solution)/shard_map/ppermute | solution.py:175
  343.4 30.1 %collective-permute-start.48 = (bf16[2,192,1408]{2,1,0:T(8,128)(2,1)S(1)}, bf16[2,192,1408]{2,1,0:T(8,128)(2,1)}, u32[]{:S(2)}, u32[]{:S(2)}) collective-permute-start(bf16[2,192,1408]{2,1,0:T(8,128)(2,1)S(1)} %collective-permute-done.45.refs_1_), channel_id=1, source_target_pairs={{0,16},{4,20},{8,24},{12,28},{16,0},{20,4},{24,8},{28,12},{1,17},{... | collective-permute-start | bytes 3244040 | tf_op jit(solution)/shard_map/ppermute | solution.py:160
  344.4 29.0 %collective-permute-start.49 = (bf16[2,192,1408]{2,1,0:T(8,128)(2,1)}, bf16[2,192,1408]{2,1,0:T(8,128)(2,1)}, u32[]{:S(2)}, u32[]{:S(2)}) collective-permute-start(bf16[2,192,1408]{2,1,0:T(8,128)(2,1)} %collective-permute-done.46.refs_2_.refs_6_), channel_id=1, source_target_pairs={{0,8},{4,12},{8,0},{12,4},{16,24},{20,28},{24,16},{28,20},{1,9},{5... | collective-permute-start | bytes 3244040 | tf_op jit(solution)/shard_map/ppermute | solution.py:160
  373.4 46.6 %collective-permute-start.57 = (bf16[2,192,256]{2,1,0:T(8,128)(2,1)S(1)}, bf16[2,192,256]{2,1,0:T(8,128)(2,1)S(1)}, u32[]{:S(2)}, u32[]{:S(2)}) collective-permute-start(bf16[2,192,256]{2,1,0:T(8,128)(2,1)S(1)} %add_convert_fusion.15.refs_0_), channel_id=1, source_target_pairs={{0,1},{1,0},{2,3},{3,2},{4,5},{5,4},{6,7},{7,6},{8,9},{9,8},{10,11... | collective-permute-start | bytes 589832 | tf_op jit(solution)/shard_map/ppermute | solution.py:175
  373.5 16.0 %collective-permute-start.62 = (f32[8,192]{0,1:T(8,128)S(1)}, f32[8,192]{0,1:T(8,128)S(1)}, u32[]{:S(2)}, u32[]{:S(2)}) collective-permute-start(f32[8,192]{0,1:T(8,128)S(1)} %add.365), channel_id=1, source_target_pairs={{0,8},{4,12},{8,0},{12,4},{16,24},{20,28},{24,16},{28,20},{1,9},{5... | collective-permute-start | bytes 18440 | tf_op jit(solution)/shard_map/ppermute | solution.py:160
  374.8 15.7 %collective-permute-start.63 = (f32[8,192]{0,1:T(8,128)S(1)}, f32[8,192]{0,1:T(8,128)S(1)}, u32[]{:S(2)}, u32[]{:S(2)}) collective-permute-start(f32[8,192]{0,1:T(8,128)S(1)} %add.365), channel_id=1, source_target_pairs={{0,16},{4,20},{8,24},{12,28},{16,0},{20,4},{24,8},{28,12},{1,17},{... | collective-permute-start | bytes 18440 | tf_op jit(solution)/shard_map/ppermute | solution.py:160
  375.7 16.8 %collective-permute-start.64 = (f32[8,192]{0,1:T(8,128)S(1)}, f32[8,192]{0,1:T(8,128)S(1)}, u32[]{:S(2)}, u32[]{:S(2)}) collective-permute-start(f32[8,192]{0,1:T(8,128)S(1)} %add.365), channel_id=1, source_target_pairs={{0,24},{4,28},{8,16},{12,20},{16,8},{20,12},{24,0},{28,4},{1,25},{... | collective-permute-start | bytes 18440 | tf_op jit(solution)/shard_map/ppermute | solution.py:160
  377.1 29.2 %collective-permute-start.51 = (bf16[192,1408]{1,0:T(8,128)(2,1)}, bf16[192,1408]{1,0:T(8,128)(2,1)S(1)}, u32[]{:S(2)}, u32[]{:S(2)}) collective-permute-start(bf16[192,1408]{1,0:T(8,128)(2,1)} %get-tuple-element.228.refs_0_), channel_id=1, source_target_pairs={{0,8},{4,12},{8,0},{12,4},{16,24},{20,28},{24,16},{28,20},{1,9},{5... | collective-permute-start | bytes 1622024 | tf_op jit(solution)/shard_map/ppermute | solution.py:160
  389.5 30.4 %collective-permute-start.52 = (bf16[192,1408]{1,0:T(8,128)(2,1)S(1)}, bf16[192,1408]{1,0:T(8,128)(2,1)}, u32[]{:S(2)}, u32[]{:S(2)}) collective-permute-start(bf16[192,1408]{1,0:T(8,128)(2,1)S(1)} %copy-done.80), channel_id=1, source_target_pairs={{0,16},{4,20},{8,24},{12,28},{16,0},{20,4},{24,8},{28,12},{1,17},{... | collective-permute-start | bytes 1622024 | tf_op jit(solution)/shard_map/ppermute | solution.py:160
  392.6 27.4 %collective-permute-start.53 = (bf16[192,1408]{1,0:T(8,128)(2,1)S(1)}, bf16[192,1408]{1,0:T(8,128)(2,1)}, u32[]{:S(2)}, u32[]{:S(2)}) collective-permute-start(bf16[192,1408]{1,0:T(8,128)(2,1)S(1)} %copy-done.81), channel_id=1, source_target_pairs={{0,8},{4,12},{8,0},{12,4},{16,24},{20,28},{24,16},{28,20},{1,9},{5... | collective-permute-start | bytes 1622024 | tf_op jit(solution)/shard_map/ppermute | solution.py:160
  405.1 14.9 %collective-permute-start.54 = (bf16[192,1408]{1,0:T(8,128)(2,1)S(1)}, bf16[192,1408]{1,0:T(8,128)(2,1)}, u32[]{:S(2)}, u32[]{:S(2)}) collective-permute-start(bf16[192,1408]{1,0:T(8,128)(2,1)S(1)} %copy-done.81), channel_id=1, source_target_pairs={{0,16},{4,20},{8,24},{12,28},{16,0},{20,4},{24,8},{28,12},{1,17},{... | collective-permute-start | bytes 1622024 | tf_op jit(solution)/shard_map/ppermute | solution.py:160
  406.3 13.7 %collective-permute-start.59 = (bf16[2,192,256]{2,1,0:T(8,128)(2,1)S(1)}, bf16[2,192,256]{2,1,0:T(8,128)(2,1)S(1)}, u32[]{:S(2)}, u32[]{:S(2)}) collective-permute-start(bf16[2,192,256]{2,1,0:T(8,128)(2,1)S(1)} %add_convert_fusion.14.refs_2_), channel_id=1, source_target_pairs={{0,1},{1,0},{2,3},{3,2},{4,5},{5,4},{6,7},{7,6},{8,9},{9,8},{10,11... | collective-permute-start | bytes 589832 | tf_op jit(solution)/shard_map/ppermute | solution.py:175
  433.2 15.4 %collective-permute-start.67 = (bf16[768,128]{1,0:T(8,128)(2,1)}, bf16[768,128]{1,0:T(8,128)(2,1)S(1)}, u32[]{:S(2)}, u32[]{:S(2)}) collective-permute-start(bf16[768,128]{1,0:T(8,128)(2,1)} %get-tuple-element.241), channel_id=1, source_target_pairs={{0,16},{4,20},{8,24},{12,28},{16,0},{20,4},{24,8},{28,12},{1,17},{... | collective-permute-start | bytes 589832 | tf_op jit(solution)/shard_map/ppermute | solution.py:160
  434.1 14.5 %collective-permute-start.66 = (bf16[768,128]{1,0:T(8,128)(2,1)}, bf16[768,128]{1,0:T(8,128)(2,1)S(1)}, u32[]{:S(2)}, u32[]{:S(2)}) collective-permute-start(bf16[768,128]{1,0:T(8,128)(2,1)} %get-tuple-element.239), channel_id=1, source_target_pairs={{0,8},{4,12},{8,0},{12,4},{16,24},{20,28},{24,16},{28,20},{1,9},{5... | collective-permute-start | bytes 589832 | tf_op jit(solution)/shard_map/ppermute | solution.py:160
  434.8 13.9 %collective-permute-start.65 = (bf16[768,128]{1,0:T(8,128)(2,1)}, bf16[768,128]{1,0:T(8,128)(2,1)S(1)}, u32[]{:S(2)}, u32[]{:S(2)}) collective-permute-start(bf16[768,128]{1,0:T(8,128)(2,1)} %get-tuple-element.237), channel_id=1, source_target_pairs={{0,8},{4,12},{8,0},{12,4},{16,24},{20,28},{24,16},{28,20},{1,9},{5... | collective-permute-start | bytes 589832 | tf_op jit(solution)/shard_map/ppermute | solution.py:160
  436.2 12.6 %collective-permute-start.68 = (bf16[768,128]{1,0:T(8,128)(2,1)}, bf16[768,128]{1,0:T(8,128)(2,1)S(1)}, u32[]{:S(2)}, u32[]{:S(2)}) collective-permute-start(bf16[768,128]{1,0:T(8,128)(2,1)} %get-tuple-element.242), channel_id=1, source_target_pairs={{0,16},{4,20},{8,24},{12,28},{16,0},{20,4},{24,8},{28,12},{1,17},{... | collective-permute-start | bytes 589832 | tf_op jit(solution)/shard_map/ppermute | solution.py:160
  455.4 25.3 %collective-permute-start.72 = (bf16[192,1408]{1,0:T(8,128)(2,1)S(1)}, bf16[192,1408]{1,0:T(8,128)(2,1)S(1)}, u32[]{:S(2)}, u32[]{:S(2)}) collective-permute-start(bf16[192,1408]{1,0:T(8,128)(2,1)S(1)} %collective-permute-done.51.refs_1_), channel_id=1, source_target_pairs={{0,16},{4,20},{8,24},{12,28},{16,0},{20,4},{24,8},{28,12},{1,17},{... | collective-permute-start | bytes 1622024 | tf_op jit(solution)/shard_map/ppermute | solution.py:160
  456.5 25.4 %collective-permute-start.73 = (bf16[192,1408]{1,0:T(8,128)(2,1)}, bf16[192,1408]{1,0:T(8,128)(2,1)S(1)}, u32[]{:S(2)}, u32[]{:S(2)}) collective-permute-start(bf16[192,1408]{1,0:T(8,128)(2,1)} %collective-permute-done.54.refs_6_), channel_id=1, source_target_pairs={{0,8},{4,12},{8,0},{12,4},{16,24},{20,28},{24,16},{28,20},{1,9},{5... | collective-permute-start | bytes 1622024 | tf_op jit(solution)/shard_map/ppermute | solution.py:160
  473.0 26.1 %collective-permute-start.78 = (bf16[768,256]{1,0:T(8,128)(2,1)}, bf16[768,256]{1,0:T(8,128)(2,1)S(1)}, u32[]{:S(2)}, u32[]{:S(2)}) collective-permute-start(bf16[768,256]{1,0:T(8,128)(2,1)} %get-tuple-element.262.refs_0_), channel_id=1, source_target_pairs={{0,8},{4,12},{8,0},{12,4},{16,24},{20,28},{24,16},{28,20},{1,9},{5... | collective-permute-start | bytes 1179656 | tf_op jit(solution)/shard_map/ppermute | solution.py:160
  474.4 24.7 %collective-permute-start.79 = (bf16[768,256]{1,0:T(8,128)(2,1)}, bf16[768,256]{1,0:T(8,128)(2,1)S(1)}, u32[]{:S(2)}, u32[]{:S(2)}) collective-permute-start(bf16[768,256]{1,0:T(8,128)(2,1)} %get-tuple-element.262.refs_0_), channel_id=1, source_target_pairs={{0,16},{4,20},{8,24},{12,28},{16,0},{20,4},{24,8},{28,12},{1,17},{... | collective-permute-start | bytes 1179656 | tf_op jit(solution)/shard_map/ppermute | solution.py:160
  479.7 19.4 %collective-permute-start.80 = (bf16[768,256]{1,0:T(8,128)(2,1)}, bf16[768,256]{1,0:T(8,128)(2,1)}, u32[]{:S(2)}, u32[]{:S(2)}) collective-permute-start(bf16[768,256]{1,0:T(8,128)(2,1)} %get-tuple-element.252.refs_4_), channel_id=1, source_target_pairs={{0,16},{4,20},{8,24},{12,28},{16,0},{20,4},{24,8},{28,12},{1,17},{... | collective-permute-start | bytes 1179656 | tf_op jit(solution)/shard_map/ppermute | solution.py:160
  480.7 18.4 %collective-permute-start.81 = (bf16[768,256]{1,0:T(8,128)(2,1)}, bf16[768,256]{1,0:T(8,128)(2,1)S(1)}, u32[]{:S(2)}, u32[]{:S(2)}) collective-permute-start(bf16[768,256]{1,0:T(8,128)(2,1)} %get-tuple-element.252.refs_4_), channel_id=1, source_target_pairs={{0,8},{4,12},{8,0},{12,4},{16,24},{20,28},{24,16},{28,20},{1,9},{5... | collective-permute-start | bytes 1179656 | tf_op jit(solution)/shard_map/ppermute | solution.py:160
  503.3 93.5 %collective-permute-start.86 = (bf16[4,256,1408]{2,1,0:T(8,128)(2,1)}, bf16[4,256,1408]{2,1,0:T(8,128)(2,1)S(1)}, u32[]{:S(2)}, u32[]{:S(2)}) collective-permute-start(bf16[4,256,1408]{2,1,0:T(8,128)(2,1)} %get-tuple-element.273), channel_id=1, source_target_pairs={{0,4},{4,0},{8,12},{12,8},{16,20},{20,16},{24,28},{28,24},{1,5},{5... | collective-permute-start | bytes 8650760 | tf_op jit(solution)/shard_map/ppermute | solution.py:164
  503.3 20.2 %collective-permute-start.74 = (bf16[2,384,256]{2,1,0:T(8,128)(2,1)}, bf16[2,384,256]{2,1,0:T(8,128)(2,1)S(1)}, u32[]{:S(2)}, u32[]{:S(2)}) collective-permute-start(bf16[2,384,256]{2,1,0:T(8,128)(2,1)} %get-tuple-element.257), channel_id=1, source_target_pairs={{0,1},{1,0},{2,3},{3,2},{4,5},{5,4},{6,7},{7,6},{8,9},{9,8},{10,11... | collective-permute-start | bytes 1179656 | tf_op jit(solution)/shard_map/ppermute | solution.py:175
  522.8 73.9 %collective-permute-start.87 = (bf16[4,256,1408]{2,1,0:T(8,128)(2,1)}, bf16[4,256,1408]{2,1,0:T(8,128)(2,1)}, u32[]{:S(2)}, u32[]{:S(2)}) collective-permute-start(bf16[4,256,1408]{2,1,0:T(8,128)(2,1)} %get-tuple-element.274), channel_id=1, source_target_pairs={{0,4},{4,0},{8,12},{12,8},{16,20},{20,16},{24,28},{28,24},{1,5},{5... | collective-permute-start | bytes 8650760 | tf_op jit(solution)/shard_map/ppermute | solution.py:164
  522.9 130.7 %collective-permute-start.104 = (bf16[4,1408,256]{2,1,0:T(8,128)(2,1)}, bf16[4,1408,256]{2,1,0:T(8,128)(2,1)}, u32[]{:S(2)}, u32[]{:S(2)}) collective-permute-start(bf16[4,1408,256]{2,1,0:T(8,128)(2,1)} %get-tuple-element.290), channel_id=1, source_target_pairs={{0,4},{4,0},{8,12},{12,8},{16,20},{20,16},{24,28},{28,24},{1,5},{5... | collective-permute-start | bytes 8650760 | tf_op jit(solution)/shard_map/ppermute | solution.py:164
  525.4 37.0 %collective-permute-start.75 = (bf16[2,384,256]{2,1,0:T(8,128)(2,1)S(1)}, bf16[2,384,256]{2,1,0:T(8,128)(2,1)}, u32[]{:S(2)}, u32[]{:S(2)}) collective-permute-start(bf16[2,384,256]{2,1,0:T(8,128)(2,1)S(1)} %add_convert_fusion.5), channel_id=1, source_target_pairs={{0,3},{1,2},{2,1},{3,0},{4,7},{5,6},{6,5},{7,4},{8,11},{9,10},{10,... | collective-permute-start | bytes 1179656 | tf_op jit(solution)/shard_map/ppermute | solution.py:175
  539.0 13.5 %collective-permute-start.84 = (bf16[2,192,256]{2,1,0:T(8,128)(2,1)}, bf16[2,192,256]{2,1,0:T(8,128)(2,1)S(1)}, u32[]{:S(2)}, u32[]{:S(2)}) collective-permute-start(bf16[2,192,256]{2,1,0:T(8,128)(2,1)} %get-tuple-element.266), channel_id=1, source_target_pairs={{0,1},{1,0},{2,3},{3,2},{4,5},{5,4},{6,7},{7,6},{8,9},{9,8},{10,11... | collective-permute-start | bytes 589832 | tf_op jit(solution)/shard_map/ppermute | solution.py:175
  554.3 25.4 %collective-permute-start.88 = (bf16[2,192,256]{2,1,0:T(8,128)(2,1)S(1)}, bf16[2,192,256]{2,1,0:T(8,128)(2,1)}, u32[]{:S(2)}, u32[]{:S(2)}) collective-permute-start(bf16[2,192,256]{2,1,0:T(8,128)(2,1)S(1)} %add_convert_fusion.11), channel_id=1, source_target_pairs={{0,3},{1,2},{2,1},{3,0},{4,7},{5,6},{6,5},{7,4},{8,11},{9,10},{10,... | collective-permute-start | bytes 589832 | tf_op jit(solution)/shard_map/ppermute | solution.py:175
  568.6 22.7 %collective-permute-start.76 = (bf16[2,384,256]{2,1,0:T(8,128)(2,1)S(1)}, bf16[2,384,256]{2,1,0:T(8,128)(2,1)}, u32[]{:S(2)}, u32[]{:S(2)}) collective-permute-start(bf16[2,384,256]{2,1,0:T(8,128)(2,1)S(1)} %add_convert_fusion.4.refs_0_), channel_id=1, source_target_pairs={{0,1},{1,0},{2,3},{3,2},{4,5},{5,4},{6,7},{7,6},{8,9},{9,8},{10,11... | collective-permute-start | bytes 1179656 | tf_op jit(solution)/shard_map/ppermute | solution.py:175
  588.3 20.7 %collective-permute-start.90 = (bf16[2,192,256]{2,1,0:T(8,128)(2,1)S(1)}, bf16[2,192,256]{2,1,0:T(8,128)(2,1)S(1)}, u32[]{:S(2)}, u32[]{:S(2)}) collective-permute-start(bf16[2,192,256]{2,1,0:T(8,128)(2,1)S(1)} %add_convert_fusion.9.refs_0_), channel_id=1, source_target_pairs={{0,1},{1,0},{2,3},{3,2},{4,5},{5,4},{6,7},{7,6},{8,9},{9,8},{10,11... | collective-permute-start | bytes 589832 | tf_op jit(solution)/shard_map/ppermute | solution.py:175
  591.3 17.7 %collective-permute-start.91 = (bf16[2,192,256]{2,1,0:T(8,128)(2,1)S(1)}, bf16[2,192,256]{2,1,0:T(8,128)(2,1)S(1)}, u32[]{:S(2)}, u32[]{:S(2)}) collective-permute-start(bf16[2,192,256]{2,1,0:T(8,128)(2,1)S(1)} %add_convert_fusion.8.refs_2_), channel_id=1, source_target_pairs={{0,1},{1,0},{2,3},{3,2},{4,5},{5,4},{6,7},{7,6},{8,9},{9,8},{10,11... | collective-permute-start | bytes 589832 | tf_op jit(solution)/shard_map/ppermute | solution.py:175
  596.8 35.5 %collective-permute-start.103 = (bf16[4,512,256]{2,1,0:T(8,128)(2,1)}, bf16[4,512,256]{2,1,0:T(8,128)(2,1)}, u32[]{:S(2)}, u32[]{:S(2)}) collective-permute-start(bf16[4,512,256]{2,1,0:T(8,128)(2,1)} %get-tuple-element.289), channel_id=1, source_target_pairs={{0,4},{4,0},{8,12},{12,8},{16,20},{20,16},{24,28},{28,24},{1,5},{5... | collective-permute-start | bytes 3145736 | tf_op jit(solution)/shard_map/ppermute | solution.py:164
  596.8 21.5 %collective-permute-start.77 = (bf16[768,256]{1,0:T(8,128)(2,1)}, bf16[768,256]{1,0:T(8,128)(2,1)}, u32[]{:S(2)}, u32[]{:S(2)}) collective-permute-start(bf16[768,256]{1,0:T(8,128)(2,1)} %get-tuple-element.319), channel_id=1, source_target_pairs={{0,4},{4,0},{8,12},{12,8},{16,20},{20,16},{24,28},{28,24},{1,5},{5... | collective-permute-start | bytes 1179656 | tf_op jit(solution)/shard_map/ppermute | solution.py:164
  617.8 26.2 %collective-permute-start.102 = (bf16[4,256,512]{2,1,0:T(8,128)(2,1)}, bf16[4,256,512]{2,1,0:T(8,128)(2,1)S(1)}, u32[]{:S(2)}, u32[]{:S(2)}) collective-permute-start(bf16[4,256,512]{2,1,0:T(8,128)(2,1)} %get-tuple-element.288), channel_id=1, source_target_pairs={{0,4},{4,0},{8,12},{12,8},{16,20},{20,16},{24,28},{28,24},{1,5},{5... | collective-permute-start | bytes 3145736 | tf_op jit(solution)/shard_map/ppermute | solution.py:164
  618.3 18.4 %collective-permute-start.101 = (bf16[2,256,512]{2,1,0:T(8,128)(2,1)}, bf16[2,256,512]{2,1,0:T(8,128)(2,1)}, u32[]{:S(2)}, u32[]{:S(2)}) collective-permute-start(bf16[2,256,512]{2,1,0:T(8,128)(2,1)} %get-tuple-element.287), channel_id=1, source_target_pairs={{0,4},{4,0},{8,12},{12,8},{16,20},{20,16},{24,28},{28,24},{1,5},{5... | collective-permute-start | bytes 1572872 | tf_op jit(solution)/shard_map/ppermute | solution.py:164
  622.7 22.9 %all-to-all-start.2 = ((bf16[8,256,256]{2,1,0:T(8,128)(2,1)}), bf16[8,256,256]{2,1,0:T(8,128)(2,1)S(1)}, u32[]{:S(2)}, u32[]{:S(2)}) async-start(bf16[8,256,256]{2,1,0:T(8,128)(2,1)} %bitcast.114), calls=%async_computation.2 | async-start | bytes 2097152 | tf_op jit(solution)/shard_map/all_to_all | solution.py:1211
  645.6 18.9 %all-to-all-start.3 = ((bf16[8,256,256]{2,1,0:T(8,128)(2,1)}), bf16[8,256,256]{2,1,0:T(8,128)(2,1)S(1)}, u32[]{:S(2)}, u32[]{:S(2)}) async-start(bf16[8,256,256]{2,1,0:T(8,128)(2,1)} %bitcast.59), calls=%async_computation.3 | async-start | bytes 2097152 | tf_op jit(solution)/shard_map/all_to_all | solution.py:1211
  (132 other events, 1172.4 us)

commit v5 on v4

--- a/solution.py
+++ b/solution.py
@@ -146,8 +146,9 @@
     spots += [g ^ mine, g ^ theirs, g ^ (2 + mine), g ^ (2 + theirs)]
     spots += [g ^ (2 * mine), g ^ (2 * mine + 1), g ^ (2 * theirs), g ^ (2 * theirs + 1)]
     spots += [mine, theirs, 2 + mine, 2 + theirs]
+    spots += [2 * mine, 2 * mine + 1, 2 * theirs, 2 * theirs + 1]
     meta = jnp.stack(spots).astype(jnp.int32)
-    BY_CHUNK, BY_HALF, IN_ORDER = 8, 12, 16
+    BY_CHUNK, BY_HALF, IN_ORDER, IN_HALVES = 8, 12, 16, 20
 
     def after(value, *others):
         return lax.optimization_barrier((value,) + others)[0]
@@ -178,14 +179,17 @@
         return (value + by_group(value, 1)) + (by_group(value, 2) + by_group(value, 3))
 
     def sum_z(value):
-        value = value + by_z(value, 1)
-        return value + by_z(value, 3)
+        return (value + by_z(value, 1)) + (by_z(value, 2) + by_z(value, 3))
 
     def z_first(keep, send):
         return both(keep, by_z(send, 1))
 
     def z_second(half):
         return both(half, by_z(half, 3))
+
+    def z_covered(keep, send, mask, cover):
+        keep, got = held((keep, by_z(send, mask)), cover)
+        return both(keep, got)
 
     def z_last(half):
         return half, by_z(half, 1)
@@ -211,9 +215,9 @@
     def gather_groups(first, second, late=()):
         ax, bx = by_group(first, 1), by_group(second, 1)
         ay, by = by_group(first, 2), by_group(second, 2)
-        along = held((ax, by), (bx, ay), late)
+        along = held((ax, by), (bx, ay), late) if len(late) else (ax, by)
         ad, bd = by_group(along[0], 2), by_group(along[1], 1)
-        return (first, ax, ay, ad), (second, bx, by, bd)
+        return (first, ax, ay, ad), (second, bx, by, bd), along
 
     def row_of(offset):
         return lambda *a: (a[-1][2 + offset], 0)
@@ -267,10 +271,16 @@
         shift = m[j] & 7
         return pl.ds(pl.multiple_of(m[j] - shift, 8), seq_len + 8), shift
 
+    def take_rows(dealt, source, all_ref):
+        count = slots * seq_len if dealt else seqs * per
+        start = seqs * per if dealt else 0
+        for p in range(dp):
+            source[p * count : (p + 1) * count, :] = all_ref[p, start : start + count, :].astype(F32)
+
     def pack_body(dealt, m, all_ref, *refs):
         outs = refs[:parts]
         source, packed, whole = refs[parts:]
-        source[...] = all_ref[...].astype(F32)
+        take_rows(dealt, source, all_ref)
 
         line = lax.broadcasted_iota(jnp.int32, (seq_len + 8, ds), 0)
 
@@ -298,11 +308,12 @@
         return [own[0]] + [by_part(own[s], s) for s in pieces[1:]]
 
     x_send = hidden_in.reshape(seqs * per, dp, ds).transpose(1, 0, 2)
-    x_all = lax.all_to_all(x_send, "dp", 0, 0, tiled=True).reshape(rows_all, ds)
-    x_pieces = pack(x_all, False)
     d_send = cotangent.reshape(slots * seq_len, dp, ds).transpose(1, 0, 2)
-    d_all = lax.all_to_all(d_send, "dp", 0, 0, tiled=True).reshape(rows_all, ds)
-    d_pieces = pack(d_all, True)
+    arrived = lax.all_to_all(
+        jnp.concatenate([x_send, d_send], axis=1), "dp", 0, 0, tiled=True
+    )
+    x_pieces = pack(arrived, False)
+    d_pieces = pack(arrived, True)
 
     def spread(vector):
         tall = vector.reshape((groups, parts, ds) + vector.shape[1:])[g]
@@ -430,7 +441,7 @@
         flops=2 * rp * (experts + 2) * parts * ds * hw,
     )
     dh = dhidden(after(meta, qkv[8]))
-    q_sum, kv_sum, sent, far = reduce_groups(qkv[0:8:2], qkv[1:8:2], late=dh[0])
+    q_sum, kv_sum, sent, far = reduce_groups(qkv[0:8:2], qkv[1:8:2])
     stats_a = sum_groups(after(qkv[8], far))
     flat_a, cols_a = gate_columns(stats_a, low_a, high_a)
 
@@ -492,7 +503,7 @@
         [pltpu.VMEM((seq_len + rp, 2 * HD), BF16)],
         flops=8 * rp * span * HD,
     )
-    gm_a, gm_b = gather_groups(gated_a, gated_b)
+    gm_a, gm_b, _ = gather_groups(gated_a, gated_b)
     chunks = 2
     zr = rp // chunks // 2
     hold = [((parts, zr, ds), BF16, None, None)] * 2
@@ -539,11 +550,10 @@
     dh_a, dh_b = held((dh[0:8:2], dh[1:8:2]), gm_a[3], gm_b[3])
     ra, rb = by_group(dh_a[3], 1), by_group(dh_b[3], 2)
     for k in range(1, chunks):
-        halves.append(z_first(*project(k, after(meta, halves[-1], ra, rb))))
-    near = held((dh_a[1], dh_b[2]), halves[0])
-    ax, by = by_group(near[0], 1), by_group(near[1], 2)
-    halves = held([z_second(half) for half in halves], ax, by)
-    along = held((both(dh_a[2], ra), both(dh_b[1], rb)), halves)
+        halves.append(z_first(*project(k, after(meta, halves[-1]))))
+    ax, by = by_group(dh_a[1], 1), by_group(dh_b[2], 2)
+    halves = [z_second(half) for half in halves]
+    along = held((both(dh_a[2], ra), both(dh_b[1], rb)), (ax, by))
     dh_a, dh_b = (dh_a[0], ax, by_group(along[0], 2)), (dh_b[0], by_group(along[1], 1), by)
     attn_totals = [half for v in halves for half in z_last(v)]
 
@@ -573,10 +583,7 @@
         ((parts, rp, ds), BF16, None, None),
         ((8, rp), F32, None, None),
     ]
-    after_rows, u_f, stats_part = run(norm_body, "norm", (1,), meta, ins, outs)
-    stats_f = sum_groups(stats_part)
-    flat_f, cols_f = gate_columns(stats_f, low_f, high_f)
-
+    after_rows, u_f, stats_part = run(norm_body, "norm", (1,), after(meta, along), ins, outs)
     def up_body(m, *refs):
         u_refs, w_refs = refs[:2], refs[2 : 2 + parts]
         sel_refs = refs[2 + parts : 4 + parts]
@@ -604,12 +611,15 @@
             up_body, "up", (2,), meta, ins, outs, flops=8 * blk * experts * parts * ds * ff
         )
 
-    up_far = up((3, 1), after(meta, stats_f, dh_a[2], dh_b[1]))
+    up_far = up((3, 1), after(meta, dh_a[2], dh_b[1]))
     up_near = up((2, 0), after(meta, up_far[0]))
-    gu_a, gu_b, _, _ = reduce_groups(
+    gu_a, gu_b, _, far = reduce_groups(
         (up_near[2], up_far[2], up_near[0], up_far[0]),
         (up_near[3], up_far[3], up_near[1], up_far[1]),
     )
+
+    stats_f = sum_groups(after(stats_part, far))
+    flat_f, cols_f = gate_columns(stats_f, low_f, high_f)
 
     mt_rows = blk // 3
 
@@ -653,12 +663,53 @@
     outs += [((2, blk, ff), BF16, (2, mt_rows, ff), rows_3)] * 2
     outs += [((blk, 8), F32, (mt_rows, 8), rows_2)]
     act_a, act_b, grad_a, grad_b, dots_f = run(mid_body, "mid", (3,), meta, ins, outs)
-    gg_a, gg_b = gather_groups(grad_a, grad_b)
+    gg_a, gg_b, _ = gather_groups(grad_a, grad_b, late=(act_a,))
     dots_f = dots_f.T
 
+    def dx_body(m, *refs):
+        a_refs, b_refs = refs[:2], refs[2:4]
+        w_refs = refs[4 : 4 + parts]
+        sel_refs = refs[4 + parts : 6 + parts]
+        keep_ref, send_ref, acc, xs = refs[6 + parts :]
+        e = pl.program_id(0)
+        expert = e.astype(F32)
+
+        @pl.when(e == 0)
+        def _():
+            acc[...] = jnp.zeros_like(acc)
+
+        for j in range(2):
+            for k in range(2):
+                ids = sel_refs[k]
+                xs[k * blk : (k + 1) * blk, :] = pick(
+                    ids[:, 2:3], ids[:, 3:4], expert, a_refs[k][j], b_refs[k][j]
+                )
+            for s, value in enumerate(nt_pieces(xs[...], [w[0, j] for w in w_refs])):
+                acc[s] += value
+
+        @pl.when(e == experts - 1)
+        def _():
+            keep_ref[...] = acc[:, at_row(m, 6, blk), :].astype(BF16)
+            send_ref[...] = acc[:, at_row(m, 7, blk), :].astype(BF16)
+
+    def dx(pair, meta):
+        ins = [(v[r], None, None) for v in (gg_a, gg_b) for r in pair]
+        ins += [(w, (1, 2, ds, ff), lambda e, m: (e, 0, 0, 0)) for w in wi]
+        ins += [(sel, (blk, 8), row_of(r)) for r in pair]
+        return run(
+            dx_body, "dx", (experts,), meta, ins, [((parts, blk, ds), BF16, None, None)] * 2,
+            [pltpu.VMEM((parts, 2 * blk, ds), F32), pltpu.VMEM((2 * blk, ff), BF16)],
+            flops=8 * blk * experts * parts * ds * ff,
+        )
+
+    dx_near = dx((0, 1), after(meta, gg_a[2], gg_b[2]))
     dots_f = after(sum_z(dots_f), gg_a[3], gg_b[3])
     dots_f = jnp.stack([dots_f, by_group(dots_f, 1), by_group(dots_f, 2), by_group(dots_f, 3)])
-    act_a, act_b, _ = lax.optimization_barrier((act_a, act_b, (gg_a[3], gg_b[3])))
+    dx_far = dx((2, 3), meta)
+    near_half = held([z_second(z_first(*dx_near))], dx_far[0])[0]
+    far_half = z_first(*dx_far)
+
+    act_a, act_b, _ = lax.optimization_barrier((act_a, act_b, far_half))
     ag_a = [act_a, by_group(act_a, 1), by_group(act_a, 2)]
     ag_b = [act_b, by_group(act_b, 1), by_group(act_b, 2)]
     dots_f = jnp.take(dots_f, g ^ jnp.arange(4, dtype=jnp.int32), axis=0)
@@ -678,46 +729,6 @@
 
     back_f = back_columns(flat_f, dots_f, low_f, high_f)
 
-    def dx_body(m, *refs):
-        a_refs, b_refs = refs[:2], refs[2:4]
-        w_refs = refs[4 : 4 + parts]
-        sel_refs = refs[4 + parts : 6 + parts]
-        keep_ref, send_ref, acc, xs = refs[6 + parts :]
-        e = pl.program_id(0)
-        expert = e.astype(F32)
-
-        @pl.when(e == 0)
-        def _():
-            acc[...] = jnp.zeros_like(acc)
-
-        for j in range(2):
-            for k in range(2):
-                ids = sel_refs[k]
-                xs[k * blk : (k + 1) * blk, :] = pick(
-                    ids[:, 2:3], ids[:, 3:4], expert, a_refs[k][j], b_refs[k][j]
-                )
-            for s, value in enumerate(nt_pieces(xs[...], [w[0, j] for w in w_refs])):
-                acc[s] += value
-
-        @pl.when(e == experts - 1)
-        def _():
-            keep_ref[...] = acc[:, at_row(m, 6, blk), :].astype(BF16)
-            send_ref[...] = acc[:, at_row(m, 7, blk), :].astype(BF16)
-
-    def dx(pair, meta):
-        ins = [(v[r], None, None) for v in (gg_a, gg_b) for r in pair]
-        ins += [(w, (1, 2, ds, ff), lambda e, m: (e, 0, 0, 0)) for w in wi]
-        ins += [(sel, (blk, 8), row_of(r)) for r in pair]
-        return run(
-            dx_body, "dx", (experts,), meta, ins, [((parts, blk, ds), BF16, None, None)] * 2,
-            [pltpu.VMEM((parts, 2 * blk, ds), F32), pltpu.VMEM((2 * blk, ff), BF16)],
-            flops=8 * blk * experts * parts * ds * ff,
-        )
-
-    dx_near = dx((0, 1), meta)
-    dx_far = dx((2, 3), meta)
-    far_half = z_first(*dx_far)
-    dx_totals = wide_sum_z(*dx_near) + z_last(z_second(far_half))
 
     def exchange(sums):
         total = sums[0].astype(F32)
@@ -793,14 +804,15 @@
         return run(fold_body, "fold", (experts,), meta, ins, outs)[0]
 
     dwin_gate = dwin(0, after(meta, far_half))
+    dx_totals = z_last(near_half) + z_last(z_covered(far_half, far_half, 3, dwin_gate[0]))
 
     def norm_back_body(low_precision_out, m, *refs):
-        t_refs = refs[:4]
-        after_ref = refs[4]
+        sums = 4 if low_precision_out else 2
+        t_refs, after_ref, refs = refs[:sums], refs[sums], refs[sums + 1 :]
         ups = parts if low_precision_out else 1
-        up_refs = refs[5 : 5 + ups]
-        gain_ref, router_ref, back = refs[5 + ups : 8 + ups]
-        outs = refs[8 + ups :]
+        up_refs = refs[:ups]
+        gain_ref, router_ref, back = refs[ups : 3 + ups]
+        outs = refs[3 + ups :]
         small = outs[-1]
         for s in pieces:
             gain = gain_ref[s]
@@ -808,12 +820,15 @@
             gain_sum = jnp.zeros((1, ds), F32)
             router_sum = [jnp.zeros((1, ds), F32)] * experts
             for r in range(4):
-                span_r = at_row(m, (BY_CHUNK if low_precision_out else IN_ORDER) + r, blk)
+                span_r = at_row(m, (BY_CHUNK if low_precision_out else IN_HALVES) + r, blk)
                 up_value = up_refs[s][span_r, :] if low_precision_out else up_refs[0][s, span_r, :]
                 x = after_ref[s, span_r, :].astype(F32)
                 cols = back[span_r, :]
                 rms = cols[:, experts + 1 : experts + 2]
-                grad = t_refs[r][s].astype(F32)
+                if low_precision_out:
+                    grad = t_refs[r][s].astype(F32)
+                else:
+                    grad = t_refs[r // 2][s, (r % 2) * blk : (r % 2 + 1) * blk, :].astype(F32)
                 for e in range(experts):
                     grad += cols[:, e : e + 1] * router[e : e + 1]
                 normed = x * rms
@@ -831,7 +846,7 @@
                     outs[0][s, span_r, :] = total
                     outs[1][s, span_r, :] = total.astype(BF16)
                 else:
-                    outs[0][s, span_r, :] = total.astype(BF16)
+                    outs[s][span_r, :] = total.astype(BF16)
             for e in range(experts):
                 small[e, s] = router_sum[e][0]
             small[experts, s] = gain_sum[0]
@@ -973,7 +988,9 @@
 
     ins = [(v, None, None) for v in (dkv_own, dkv_in, kv_rot, cosine, sine)]
     outs = [((rp, 2 * HD), BF16, None, None), ((8, rp), F32, None, None)]
-    dkv, dots_kv = run(dkv_body, "dkv", (1,), meta, ins, outs)
+    dkv, dots_kv = run(
+        dkv_body, "dkv", (1,), after(meta, ag_a[3], ag_b[3]), ins, outs
+    )
     third = jnp.arange(8)[:, None] == 2
     def down_body(m, *refs):
         a_refs, b_refs = refs[:4], refs[4:8]
@@ -1053,12 +1070,8 @@
 
     down_halves = down(after(meta, dkv))
     down_halves, dwout_sums = down_halves[:2], down_halves[2:]
-    da_a, da_b = gather_groups(dq, dkv, late=dwout_sums[0])
-    dwproj_sums = dwproj(after(meta, dwout_sums[0]))
-    dots_a = sum_z(sum_groups(after(dots_q, da_a[3], da_b[3]) + jnp.where(third, dots_kv, 0.0)))
-    back_a = back_columns(flat_a, dots_a, low_a, high_a)
-
-
+    da_a, da_b, da_along = gather_groups(dq, dkv, late=(dwout_sums[0],))
+    dwproj_sums = dwproj(after(meta, da_along))
     def place_heads(m, refs, lo, hi):
         for r in range(4):
             lanes = pl.ds(pl.multiple_of(m[2 + r] * HD, HD), HD)
@@ -1084,20 +1097,20 @@
         for s in pieces:
             store_halves(pl.program_id(0), outs, s, acc[s].astype(BF16))
 
-    def dattn(k, meta):
-        half = lambda i, m: (2 * k + m[7 - i], 0)
-        ins = [(v, (zr, 2 * HD), half) for v in da_a + da_b]
-        ins += [(sel, (zr, 8), half)]
+    def dattn(meta):
+        half = lambda i, m: (m[7 - i], 0)
+        ins = [(v, (2 * zr, 2 * HD), half) for v in da_a + da_b]
+        ins += [(sel, (2 * zr, 8), half)]
         ins += [(w, None, None) for w in wq + wkv]
         return run(
-            dattn_body, "dattn", (2,), meta, ins, hold,
-            [pltpu.VMEM((zr, hw), BF16)] * 4,
-            flops=4 * zr * (experts + 2) * hw * parts * ds,
+            dattn_body, "dattn", (2,), meta, ins, [((parts, 2 * zr, ds), BF16, None, None)] * 2,
+            [pltpu.VMEM((2 * zr, hw), BF16)] * 4,
+            flops=8 * zr * (experts + 2) * hw * parts * ds,
         )
 
-    da_halves = [z_first(*dattn(0, after(meta, dwproj_sums[0])))]
-    for k in range(1, chunks):
-        da_halves.append(z_first(*dattn(k, after(meta, da_halves[-1]))))
+    dots_a = sum_groups(after(dots_q + jnp.where(third, dots_kv, 0.0), da_along))
+    da_halves = dattn(after(meta, dwproj_sums[0], dots_a))
+    dots_a = sum_z(dots_a)
     x_stack = jnp.stack(x_pieces)
     attn_input = (x_stack.astype(F32) * flat_a[0][None, :, None] * gain_a).astype(BF16)
 
@@ -1140,44 +1153,37 @@
             flops=2 * rp * (experts + 2) * hw * parts * ds,
         )
 
-    dwqkv_sums = dwqkv(after(meta, da_halves))
-    da_halves = held([z_second(half) for half in da_halves], dwqkv_sums[0])
-    da_totals = [half for v in da_halves for half in z_last(v)]
-    expertin_grad = fold((dwin_gate, dwin_up), after(meta, dwqkv_sums[0]))
-    ins = [(t, None, None) for t in da_totals]
-    ins += [(x_stack, None, None), (dafter, None, None)]
-    ins += [(gain_a, None, None), (router_a, None, None), (back_a, None, None)]
-    outs = [((parts, rp, ds), BF16, None, None), ((experts + 1, parts, ds), F32, None, None)]
-    dinput, small_a = run(
-        functools.partial(norm_back_body, False), "norm_back_first", (1,),
-        after(meta, expertin_grad), ins, outs,
-    )
-    expertout_grad = exchange(dwout_sums)
-    proj_grad = exchange(dwproj_sums)
-    query_grad, kv_grad = exchange(dwqkv_sums[:parts]), exchange(dwqkv_sums[parts:])
-    down_totals = wide_sum_z(*down_halves)
+    dwqkv_sums = dwqkv(after(meta, da_halves[0], dots_a))
+
+
+    da_half = z_covered(*da_halves, 1, dwqkv_sums[0])
+
+    down_half = z_covered(*down_halves, 1, dwproj_sums[0])
+    down_half = z_covered(down_half, down_half, 3, da_halves[0])
+    down_totals = z_last(down_half)
 
     def finish_body(m, *refs):
-        t_refs, after_ref, out_ref = refs[:2], refs[2], refs[3]
+        t_refs, after_ref, outs = refs[:2], refs[2], refs[3:]
         for k in range(4):
             span_k = at_row(m, BY_HALF + k, blk)
             for s in pieces:
                 total = t_refs[k // 2][s, (k % 2) * blk : (k % 2 + 1) * blk, :]
-                out_ref[s, span_k, :] = (
+                outs[s][span_k, :] = (
                     after_ref[s, span_k, :] + total.astype(F32)
                 ).astype(BF16)
 
     ins = [(t, None, None) for t in down_totals] + [(after_rows, None, None)]
     out_rows = run(
-        finish_body, "finish", (1,), meta, ins, [((parts, rp, ds), BF16, None, None)]
-    )[0]
+        finish_body, "finish", (1,), after(meta, dwqkv_sums[0]), ins,
+        [((rp, ds), BF16, None, None)] * parts,
+    )
 
     def unpack_body(dealt, m, other_ref, *refs):
         v_refs, out_ref = refs[:parts], refs[parts]
         packed, other, total, whole = refs[parts + 1 :]
         for s in pieces:
             packed[part_rows(m, s), :] = v_refs[s][...].astype(F32)
-        other[...] = other_ref[...].astype(F32)
+        take_rows(dealt, other, other_ref)
         line = lax.broadcasted_iota(jnp.int32, (per, ds), 0)
 
         def one(j, carry):
@@ -1197,7 +1203,7 @@
         lax.fori_loop(0, seqs, one, 0)
         out_ref[...] = total[...].astype(BF16)
 
-    def unpack(value, otherwise, dealt):
+    def unpack(value, otherwise, dealt, table):
         mine_all = [value[0]] + [by_part(value[s], s) for s in pieces[1:]]
         ins = [(v, None, None) for v in [otherwise] + mine_all]
         spread_rows = run(
@@ -1213,8 +1219,24 @@
         )
         return landed.transpose(1, 0, 2).reshape(seqs, per, width), spread_rows
 
-    layer_out, _ = unpack(out_rows, x_all, False)
-    input_grad, last_rows = unpack(dinput, d_all, True)
+    layer_out, layer_rows = unpack(out_rows, arrived, False, table)
+    expertin_grad = fold((dwin_gate, dwin_up), after(meta, layer_rows))
+    back_a = back_columns(flat_a, dots_a, low_a, high_a)
+    da_half = z_covered(da_half, da_half, 3, layer_rows)
+    da_totals = z_last(da_half)
+    ins = [(t, None, None) for t in da_totals]
+    ins += [(x_stack, None, None), (dafter, None, None)]
+    ins += [(gain_a, None, None), (router_a, None, None), (back_a, None, None)]
+    outs = [((rp, ds), BF16, None, None)] * parts
+    outs += [((experts + 1, parts, ds), F32, None, None)]
+    *dinput, small_a = run(
+        functools.partial(norm_back_body, False), "norm_back_first", (1,),
+        after(meta, expertin_grad), ins, outs,
+    )
+    expertout_grad = exchange(dwout_sums)
+    proj_grad = exchange(dwproj_sums)
+    query_grad, kv_grad = exchange(dwqkv_sums[:parts]), exchange(dwqkv_sums[parts:])
+    input_grad, last_rows = unpack(dinput, arrived, True, after(table, layer_out))
     vectors = whole_vectors(after(small_a, last_rows), small_f)
     (attnrouter_grad, attngain_grad), (ffnrouter_grad, ffngain_grad) = vectors
     return (

time: 672 us -> 648 us (0.964)
  waiting for transfers between devices: 218 us -> 196 us
  starting transfers between devices: 127 us -> 134 us
    ppermute x25 -> x24, waiting for transfers between devices: 61.9 us -> 29.1 us  [by_z(): return lax.ppermute(value, 'tensor', [(a, a ^ mask) for a in range(tp)])]
    all_to_all x2 -> x1, waiting for transfers between devices: 10.3 us -> 22.5 us  [local(): lax.all_to_all(jnp.concatenate([x_send, d_send], axis=1), 'dp', 0, 0, til...]
    ppermute x25 -> x24, starting transfers between devices: 36.6 us -> 45.7 us  [by_z(): return lax.ppermute(value, 'tensor', [(a, a ^ mask) for a in range(tp)])]
    convert_element_type x22 -> x20, other arithmetic: 15 us -> 9.19 us  [both(): return (a.astype(F32) + b.astype(F32)).astype(BF16)]
    pallas_call x30 -> x29, Pallas kernels: 238 us -> 234 us  [run(): pl.pallas_call(body, name=name, grid_spec=pltpu.PrefetchScalarGridSpec(nu...]
    unnamed x184 -> x196, local copies, waits for them, and re-layouts: 23.5 us -> 23.6 us
  transfers between devices with their start and end apart: 109 -> 107, of which waited for: 49 -> 38; matrix products, arithmetic and copies ran while one was open for 10% -> 8% of each run, Pallas kernels for 31% -> 32%
where the time goes in v5:
time: 648 us; the launch traced here: 637 us
  Pallas kernels  234 us (36%)
  waiting for transfers between devices  196 us (30%)
  starting transfers between devices  134 us (21%)
  local copies, waits for them, and re-layouts  38.7 us (6%)
  other arithmetic  30.7 us (5%)
    pallas_call x29, Pallas kernels, run(): pl.pallas_call(body, name=name, grid_spec=pltpu.PrefetchScalarGridSpec(nu...  234 us
    ppermute x60, waiting for transfers between devices, by_group(): return lax.ppermute(value, 'dp', pairs)  135 us
    ppermute x60, starting transfers between devices, by_group(): return lax.ppermute(value, 'dp', pairs)  67 us
    ppermute x24, starting transfers between devices, by_z(): return lax.ppermute(value, 'tensor', [(a, a ^ mask) for a in range(tp)])  45.7 us
    ppermute x24, waiting for transfers between devices, by_z(): return lax.ppermute(value, 'tensor', [(a, a ^ mask) for a in range(tp)])  29.1 us
    unnamed x196, local copies, waits for them, and re-layouts  23.6 us
    all_to_all x1, waiting for transfers between devices, local(): lax.all_to_all(jnp.concatenate([x_send, d_send], axis=1), 'dp', 0, 0, til...  22.5 us
  transfers between devices with their start and end apart: 107, of which 38 were waited for; matrix products, arithmetic and copies ran while one was open for 8% of the time, Pallas kernels for 32%

profile of v5, /device:TPU:0, one launch (start us, length us, event | category | flops | bytes accessed | tf_op | source)
XLA Modules:
  0.0 637.2 jit_solution(1867880468001579969)
XLA Ops:
  6.0 5.3 all-to-all-start
  15.4 22.5 %all-to-all-done.all_ref.other_ref = bf16[8,512,256]{2,1,0:T(8,128)(2,1)S(1)} async-done(((bf16[8,512,256]{2,1,0:T(8,128)(2,1)}), bf16[8,512,256]{2,1,0:T(8,128)(2,1)S(1)}, u32[]{:S(2)}, u32[]{:S(2)}) %all-to-all-start) | async-done | bytes 2097184 | tf_op jit(solution)/shard_map/all_to_all | solution.py:312
  39.2 4.4 pack.3
  46.7 4.4 pack.2
  51.8 8.5 %qkv.1 = (bf16[768,256]{1,0:T(8,128)(2,1)}, bf16[768,256]{1,0:T(8,128)(2,1)}, bf16[768,256]{1,0:T(8,128)(2,1)}, bf16[768,256]{1,0:T(8,128)(2,1)}, bf16[768,256]{...) custom-call(s32[24]{0:T(128)} %stack.148.m, ...), custom_call_target="tpu_custom_call" | custom-call | flops 2415919104 | bytes 7137280 | tf_op jit(solution)/shard_map/qkv/pallas_call | solution.py:61
  61.0 5.9 copy.173
  69.2 3.4 collective-permute-done.6
  75.8 3.3 collective-permute-done.7
  82.2 5.4 collective-permute-done.8.b2
  94.6 12.0 %dhidden.1 = (bf16[192,1408]{1,0:T(8,128)(2,1)}, bf16[192,1408]{1,0:T(8,128)(2,1)}, bf16[192,1408]{1,0:T(8,128)(2,1)}, bf16[192,1408]{1,0:T(8,128)(2,1)}, bf16[1...) custom-call(s32[24]{0:T(128)} %stack.148.m, ...), custom_call_target="tpu_custom_call" | custom-call | flops 4429185024 | bytes 11714560 | tf_op jit(solution)/shard_map/dhidden/pallas_call | solution.py:61
  107.4 4.6 rope.1
  115.8 7.9 %attend.1 = (bf16[768,128]{1,0:T(8,128)(2,1)}, bf16[768,128]{1,0:T(8,128)(2,1)}, bf16[768,128]{1,0:T(8,128)(2,1)}, bf16[768,128]{1,0:T(8,128)(2,1)}) custom-call(s32[24]{0:T(128)} %stack.148.m, bf16[768,256]{1,0:T(8,128)(2,1)} %get-tuple-element.180.q_ref.refs_0_, bf16[768,256]{1,0:T(8,128)(2,1)} %get-tuple-element.181.kv_ref.refs_1_, ...), custom_call_target="tpu_custom_call" | custom-call | flops 301989888 | bytes 1753088 | tf_op jit(solution)/shard_map/attend/pallas_call | solution.py:61
  127.9 3.9 collective-permute-done.15.refs_1_
  134.0 2.7 collective-permute-done.25.refs_2_
  136.8 3.3 collective-permute-done.16.refs_3_
  141.5 6.7 %proj.2 = (bf16[2,192,256]{2,1,0:T(8,128)(2,1)}, bf16[2,192,256]{2,1,0:T(8,128)(2,1)}) custom-call(s32[24]{0:T(128)} %stack.148.m, bf16[768,128]{1,0:T(8,128)(2,1)} %get-tuple-element.189.refs_0_, bf16[768,128]{1,0:T(8,128)(2,1)} %copy-done.20, bf16[768,128]{1,0:T(8,128)(2,1)} %copy-done.22, bf16[768,128]{1,0:T(8,128)(2,1)} %copy-done.24, ...), custom_call_target="tpu_custom_call" | custom-call | flops 805306368 | bytes 4087808 | tf_op jit(solution)/shard_map/proj/pallas_call | solution.py:61
  151.0 3.4 collective-permute-done.28
  155.4 6.8 %proj.3 = (bf16[2,192,256]{2,1,0:T(8,128)(2,1)}, bf16[2,192,256]{2,1,0:T(8,128)(2,1)}) custom-call(s32[24]{0:T(128)} %stack.148.m, bf16[768,128]{1,0:T(8,128)(2,1)} %get-tuple-element.189.refs_0_, bf16[768,128]{1,0:T(8,128)(2,1)} %copy-done.20, bf16[768,128]{1,0:T(8,128)(2,1)} %copy-done.22, bf16[768,128]{1,0:T(8,128)(2,1)} %copy-done.24, ...), custom_call_target="tpu_custom_call" | custom-call | flops 805306368 | bytes 4087808 | tf_op jit(solution)/shard_map/proj/pallas_call | solution.py:61
  170.7 3.7 collective-permute-start.29
  174.5 4.6 collective-permute-done.20
  181.7 6.3 collective-permute-done.22.refs_11_
  199.3 4.4 norm.1
  203.7 10.1 %up.2 = (bf16[2,192,1408]{2,1,0:T(8,128)(2,1)}, bf16[2,192,1408]{2,1,0:T(8,128)(2,1)}, bf16[2,192,1408]{2,1,0:T(8,128)(2,1)}, bf16[2,192,1408]{2,1,0:T(8,128)(2,1)}) custom-call(s32[24]{0:T(128)} %stack.148.m, bf16[2,768,256]{2,1,0:T(8,128)(2,1)} %get-tuple-element.206.refs_0_.refs_1_, bf16[2,768,256]{2,1,0:T(8,128)(2,1)} %get-tuple-element.206.refs_0_.refs_1_, ...), custom_call_target="tpu_custom_call" | custom-call | flops 4429185024 | bytes 17481728 | tf_op jit(solution)/shard_map/up/pallas_call | solution.py:61
  216.5 10.3 %up.3 = (bf16[2,192,1408]{2,1,0:T(8,128)(2,1)}, bf16[2,192,1408]{2,1,0:T(8,128)(2,1)}, bf16[2,192,1408]{2,1,0:T(8,128)(2,1)}, bf16[2,192,1408]{2,1,0:T(8,128)(2,1)}) custom-call(s32[24]{0:T(128)} %stack.148.m, bf16[2,768,256]{2,1,0:T(8,128)(2,1)} %get-tuple-element.206.refs_0_.refs_1_, bf16[2,768,256]{2,1,0:T(8,128)(2,1)} %get-tuple-element.206.refs_0_.refs_1_, ...), custom_call_target="tpu_custom_call" | custom-call | flops 4429185024 | bytes 17481728 | tf_op jit(solution)/shard_map/up/pallas_call | solution.py:61
  228.3 12.7 %collective-permute-done.37 = bf16[2,192,1408]{2,1,0:T(8,128)(2,1)} collective-permute-done((bf16[2,192,1408]{2,1,0:T(8,128)(2,1)}, bf16[2,192,1408]{2,1,0:T(8,128)(2,1)}, u32[]{:S(2)}, u32[]{:S(2)}) %collective-permute-start.37) | collective-permute-done | bytes 1081376 | tf_op jit(solution)/shard_map/ppermute | solution.py:161
  241.0 2.6 add_convert_fusion
  246.1 14.3 %collective-permute-done.35.refs_1_ = bf16[2,192,1408]{2,1,0:T(8,128)(2,1)S(1)} collective-permute-done((bf16[2,192,1408]{2,1,0:T(8,128)(2,1)}, bf16[2,192,1408]{2,1,0:T(8,128)(2,1)S(1)}, u32[]{:S(2)}, u32[]{:S(2)}) %collective-permute-start.35) | collective-permute-done | bytes 1081376 | tf_op jit(solution)/shard_map/ppermute | solution.py:161
  267.2 16.7 %collective-permute-done.43 = f32[8,768]{1,0:T(8,128)S(1)} collective-permute-done((f32[8,768]{1,0:T(8,128)S(1)}, f32[8,768]{1,0:T(8,128)S(1)}, u32[]{:S(2)}, u32[]{:S(2)}) %collective-permute-start.43) | collective-permute-done | bytes 24608 | tf_op jit(solution)/shard_map/ppermute | solution.py:161
  286.0 8.2 %mid.1 = (bf16[192,1408]{1,0:T(8,128)(2,1)}, bf16[192,1408]{1,0:T(8,128)(2,1)}, bf16[2,192,1408]{2,1,0:T(8,128)(2,1)}, bf16[2,192,1408]{2,1,0:T(8,128)(2,1)}, f32[192,8]{1,0:T(8,128)}) custom-call(s32[24]{0:T(128)} %stack.148.m, bf16[2,192,1408]{2,1,0:T(8,128)(2,1)} %get-tuple-element.209.refs_0_, bf16[2,192,1408]{2,1,0:T(8,128)(2,1)} %copy-done.12, ...), custom_call_target="tpu_custom_call" | custom-call | bytes 13006848 | tf_op jit(solution)/shard_map/mid/pallas_call | solution.py:61
  298.4 22.8 %collective-permute-done.44.refs_0_.refs_2_ = bf16[2,192,1408]{2,1,0:T(8,128)(2,1)S(1)} collective-permute-done((bf16[2,192,1408]{2,1,0:T(8,128)(2,1)}, bf16[2,192,1408]{2,1,0:T(8,128)(2,1)S(1)}, u32[]{:S(2)}, u32[]{:S(2)}) %collective-permute-start.44) | collective-permute-done | bytes 1081376 | tf_op jit(solution)/shard_map/ppermute | solution.py:161
  321.2 17.9 %collective-permute-done.46.refs_2_.refs_6_ = bf16[2,192,1408]{2,1,0:T(8,128)(2,1)S(1)} collective-permute-done((bf16[2,192,1408]{2,1,0:T(8,128)(2,1)}, bf16[2,192,1408]{2,1,0:T(8,128)(2,1)S(1)}, u32[]{:S(2)}, u32[]{:S(2)}) %collective-permute-start.46) | collective-permute-done | bytes 1081376 | tf_op jit(solution)/shard_map/ppermute | solution.py:161
  341.8 2.7 collective-permute-start.48
  345.3 11.0 %dx.3 = (bf16[2,192,256]{2,1,0:T(8,128)(2,1)}, bf16[2,192,256]{2,1,0:T(8,128)(2,1)}) custom-call(s32[24]{0:T(128)} %stack.148.m, bf16[2,192,1408]{2,1,0:T(8,128)(2,1)} %get-tuple-element.222.refs_0_, bf16[2,192,1408]{2,1,0:T(8,128)(2,1)} %collective-permute-done.45.refs_1_, bf16[2,192,1408]{2,1,0:T(8,128)(2,1)} %get-tuple-element.223.refs_4_.refs_2_, ...), custom_call_target="tpu_custom_call" | custom-call | flops 4429185024 | bytes 16302080 | tf_op jit(solution)/shard_map/dx/pallas_call | solution.py:61
  357.9 2.6 collective-permute-start.61
  363.4 5.7 collective-permute-start.56
  369.1 3.7 collective-permute-done.56
  376.5 11.1 %dx.2 = (bf16[2,192,256]{2,1,0:T(8,128)(2,1)}, bf16[2,192,256]{2,1,0:T(8,128)(2,1)}) custom-call(s32[24]{0:T(128)} %stack.148.m, bf16[2,192,1408]{2,1,0:T(8,128)(2,1)} %copy-done.9, bf16[2,192,1408]{2,1,0:T(8,128)(2,1)} %collective-permute-done.48.refs_1_.refs_3_, bf16[2,192,1408]{2,1,0:T(8,128)(2,1)} %copy-done.10, ...), custom_call_target="tpu_custom_call" | custom-call | flops 4429185024 | bytes 16302080 | tf_op jit(solution)/shard_map/dx/pallas_call | solution.py:61
  389.9 3.6 collective-permute-done.50
  394.5 3.8 collective-permute-start.58
  402.4 11.3 %dwin.2 = (bf16[4,256,1408]{2,1,0:T(8,128)(2,1)}, bf16[4,256,1408]{2,1,0:T(8,128)(2,1)}) custom-call(s32[24]{0:T(128)} %stack.148.m, bf16[2,192,1408]{2,1,0:T(8,128)(2,1)} %get-tuple-element.222.refs_0_, bf16[2,192,1408]{2,1,0:T(8,128)(2,1)} %collective-permute-done.45.refs_1_, bf16[2,192,1408]{2,1,0:T(8,128)(2,1)} %copy-done.9, ...), custom_call_target="tpu_custom_call" | custom-call | flops 4429185024 | bytes 15228928 | tf_op jit(solution)/shard_map/dwin/pallas_call | solution.py:61
  422.2 6.5 %norm_back.1 = (f32[2,768,256]{2,1,0:T(8,128)}, bf16[2,768,256]{2,1,0:T(8,128)(2,1)}, f32[5,2,256]{2,1,0:T(2,128)}) custom-call(s32[24]{0:T(128)} %stack.148.m, bf16[2,192,256]{2,1,0:T(8,128)(2,1)} %copy-done.26, bf16[2,192,256]{2,1,0:T(8,128)(2,1)} %copy-done.55, bf16[2,192,256]{2,1,0:T(8,128)(2,1)} %copy-done.27, bf16[2,192,256]{2,1,0:T(8,128)(2,1)} %copy-done.56, ...), custom_call_target="tpu_custom_call" | custom-call | bytes 5550080 | tf_op jit(solution)/shard_map/norm_back/pallas_call | solution.py:61
  428.7 6.1 dmix.1
  438.9 11.3 %dwin.3 = (bf16[4,256,1408]{2,1,0:T(8,128)(2,1)}, bf16[4,256,1408]{2,1,0:T(8,128)(2,1)}) custom-call(s32[24]{0:T(128)} %stack.148.m, bf16[2,192,1408]{2,1,0:T(8,128)(2,1)} %get-tuple-element.222.refs_0_, bf16[2,192,1408]{2,1,0:T(8,128)(2,1)} %collective-permute-done.45.refs_1_, bf16[2,192,1408]{2,1,0:T(8,128)(2,1)} %copy-done.9, ...), custom_call_target="tpu_custom_call" | custom-call | flops 4429185024 | bytes 15228928 | tf_op jit(solution)/shard_map/dwin/pallas_call | solution.py:61
  451.9 4.3 collective-permute-done.70.refs_9_
  459.4 14.6 %attend_back.1 = (bf16[768,256]{1,0:T(8,128)(2,1)}, f32[768,256]{1,0:T(8,128)}, f32[256,256]{1,0:T(8,128)}, f32[8,768]{1,0:T(8,128)}) custom-call(s32[24]{0:T(128)} %stack.148.m, bf16[768,256]{1,0:T(8,128)(2,1)} %get-tuple-element.180.q_ref.refs_0_, bf16[768,256]{1,0:T(8,128)(2,1)} %get-tuple-element.181.kv_ref.refs_1_, bf16[256,256]{1,0:T(8,128)(2,1)} %copy-done.36, ...), custom_call_target="tpu_custom_call" | custom-call | flops 754974720 | bytes 4792320 | tf_op jit(solution)/shard_map/attend_back/pallas_call | solution.py:61
  478.5 3.7 dkv.1
  484.9 16.2 %down.1 = (bf16[2,384,256]{2,1,0:T(8,128)(2,1)}, bf16[2,384,256]{2,1,0:T(8,128)(2,1)}, bf16[4,1408,256]{2,1,0:T(8,128)(2,1)}, bf16[4,1408,256]{2,1,0:T(8,128)(2,1)}) custom-call(s32[24]{0:T(128)} %stack.148.m, bf16[192,1408]{1,0:T(8,128)(2,1)} %get-tuple-element.233.refs_0_, bf16[192,1408]{1,0:T(8,128)(2,1)} %copy-done.77, bf16[192,1408]{1,0:T(8,128)(2,1)} %copy-done.76, ...), custom_call_target="tpu_custom_call" | custom-call | flops 8858370048 | bytes 17457152 | tf_op jit(solution)/shard_map/down/pallas_call | solution.py:61
  505.4 7.5 %dwproj.1 = (bf16[4,512,256]{2,1,0:T(8,128)(2,1)}, bf16[4,512,256]{2,1,0:T(8,128)(2,1)}) custom-call(s32[24]{0:T(128)} %stack.148.m, bf16[768,128]{1,0:T(8,128)(2,1)} %get-tuple-element.189.refs_0_, bf16[768,128]{1,0:T(8,128)(2,1)} %copy-done.20, bf16[768,128]{1,0:T(8,128)(2,1)} %copy-done.22, bf16[768,128]{1,0:T(8,128)(2,1)} %copy-done.24, ...), custom_call_target="tpu_custom_call" | custom-call | flops 1610612736 | bytes 4481024 | tf_op jit(solution)/shard_map/dwproj/pallas_call | solution.py:61
  517.3 7.3 %collective-permute-done.82.refs_3_ = bf16[768,256]{1,0:T(8,128)(2,1)S(1)} collective-permute-done((bf16[768,256]{1,0:T(8,128)(2,1)}, bf16[768,256]{1,0:T(8,128)(2,1)S(1)}, u32[]{:S(2)}, u32[]{:S(2)}) %collective-permute-start.82) | collective-permute-done | bytes 393248 | tf_op jit(solution)/shard_map/ppermute | solution.py:161
  524.9 3.1 collective-permute-start.85
  528.0 7.6 %dattn.1 = (bf16[2,384,256]{2,1,0:T(8,128)(2,1)}, bf16[2,384,256]{2,1,0:T(8,128)(2,1)}) custom-call(s32[24]{0:T(128)} %stack.148.m, bf16[768,256]{1,0:T(8,128)(2,1)} %get-tuple-element.259.refs_0_, bf16[768,256]{1,0:T(8,128)(2,1)} %collective-permute-done.72.refs_1_, bf16[768,256]{1,0:T(8,128)(2,1)} %collective-permute-done.78.refs_2_, ...), custom_call_target="tpu_custom_call" | custom-call | flops 2415919104 | bytes 7102464 | tf_op jit(solution)/shard_map/dattn/pallas_call | solution.py:61
  542.2 9.4 %dwqkv.1 = (bf16[4,256,512]{2,1,0:T(8,128)(2,1)}, bf16[4,256,512]{2,1,0:T(8,128)(2,1)}, bf16[2,256,512]{2,1,0:T(8,128)(2,1)}, bf16[2,256,512]{2,1,0:T(8,128)(2,1)}) custom-call(s32[24]{0:T(128)} %stack.148.m, bf16[768,256]{1,0:T(8,128)(2,1)} %get-tuple-element.259.refs_0_, bf16[768,256]{1,0:T(8,128)(2,1)} %collective-permute-done.72.refs_1_, ...), custom_call_target="tpu_custom_call" | custom-call | flops 2415919104 | bytes 7102464 | tf_op jit(solution)/shard_map/dwqkv/pallas_call | solution.py:61
  552.4 3.3 finish.1
  559.7 4.7 unpack.2
  564.4 3.8 all-to-all-start.1
  568.2 2.7 collective-permute-done.94
  571.0 7.4 %collective-permute-start.95 = (bf16[2,384,256]{2,1,0:T(8,128)(2,1)S(1)}, bf16[2,384,256]{2,1,0:T(8,128)(2,1)S(1)}, u32[]{:S(2)}, u32[]{:S(2)}) collective-permute-start(bf16[2,384,256]{2,1,0:T(8,128)(2,1)S(1)} %add_convert_fusion.4.refs_0_), channel_id=1, source_target_pairs={{0,1},{1,0},{2,3},{3,2},{4,5},{5,4},{6,7},{7,6},{8,9},{9,8},{10,11... | collective-permute-start | bytes 1179656 | tf_op jit(solution)/shard_map/ppermute | solution.py:176
  579.5 10.4 %fold.1 = f32[4,256,2,1408]{3,2,1,0:T(2,128)} custom-call(s32[24]{0:T(128)} %stack.148.m, bf16[4,256,1408]{2,1,0:T(8,128)(2,1)} %get-tuple-element.231.refs_0_, bf16[4,256,1408]{2,1,0:T(8,128)(2,1)} %collective-permute-done.91.refs_1_, bf16[4,256,1408]{2,1,0:T(8,128)(2,1)} %get-tuple-element.253.refs_2_, bf16[4,256,1408]{2,1,0:T(8,128)(2,1)} %collective-permute-done.92.refs_3_), custom_call_target="tpu_custom_call" | custom-call | bytes 23068672 | tf_op jit(solution)/shard_map/fold/pallas_call | solution.py:61
  590.6 5.8 norm_back_first.1
  600.1 4.8 unpack.3
  613.1 2.8 convert_add_fusion.2
  616.0 3.6 all-to-all-start.2
  622.1 5.9 convert_add_fusion
  627.9 6.9 %all-to-all-done.2 = bf16[8,256,256]{2,1,0:T(8,128)(2,1)S(1)} async-done(((bf16[8,256,256]{2,1,0:T(8,128)(2,1)}), bf16[8,256,256]{2,1,0:T(8,128)(2,1)S(1)}, u32[]{:S(2)}, u32[]{:S(2)}) %all-to-all-start.2) | async-done | bytes 1048608 | tf_op jit(solution)/shard_map/all_to_all | solution.py:1217
  (494 shorter events, 170.4 us)
Async XLA Ops:
  6.0 32.0 %all-to-all-start = ((bf16[8,512,256]{2,1,0:T(8,128)(2,1)}), bf16[8,512,256]{2,1,0:T(8,128)(2,1)S(1)}, u32[]{:S(2)}, u32[]{:S(2)}) async-start(bf16[8,512,256]{2,1,0:T(8,128)(2,1)} %pad_maximum_fusion), calls=%async_computation | async-start | bytes 4194304 | tf_op jit(solution)/shard_map/all_to_all | solution.py:312
  11.3 39.7 %collective-permute-start.2 = (bf16[2,256,512]{2,1,0:T(8,128)(2,1)S(1)}, bf16[2,256,512]{2,1,0:T(8,128)(2,1)}, u32[]{:S(2)}, u32[]{:S(2)}) collective-permute-start(bf16[2,256,512]{2,1,0:T(8,128)(2,1)S(1)} %copy-done.83), channel_id=1, source_target_pairs={{0,4},{4,0},{8,12},{12,8},{16,20},{20,16},{24,28},{28,24},{1,5},{5... | collective-permute-start | bytes 1572872 | tf_op jit(solution)/shard_map/ppermute | solution.py:165
  11.8 39.2 %collective-permute-start.1 = (bf16[4,256,512]{2,1,0:T(8,128)(2,1)}, bf16[4,256,512]{2,1,0:T(8,128)(2,1)}, u32[]{:S(2)}, u32[]{:S(2)}) collective-permute-start(bf16[4,256,512]{2,1,0:T(8,128)(2,1)} %refs_9_.5), channel_id=1, source_target_pairs={{0,4},{4,0},{8,12},{12,8},{16,20},{20,16},{24,28},{28,24},{1,5},{5... | collective-permute-start | bytes 3145736 | tf_op jit(solution)/shard_map/ppermute | solution.py:165
  11.9 82.7 %collective-permute-start.4 = (bf16[4,1408,256]{2,1,0:T(8,128)(2,1)}, bf16[4,1408,256]{2,1,0:T(8,128)(2,1)}, u32[]{:S(2)}, u32[]{:S(2)}) collective-permute-start(bf16[4,1408,256]{2,1,0:T(8,128)(2,1)} %refs_11_.2), channel_id=1, source_target_pairs={{0,4},{4,0},{8,12},{12,8},{16,20},{20,16},{24,28},{28,24},{1,5},{5... | collective-permute-start | bytes 8650760 | tf_op jit(solution)/shard_map/ppermute | solution.py:165
  66.9 136.9 %collective-permute-start.34 = (bf16[4,2,256,1408]{3,2,1,0:T(8,128)(2,1)}, bf16[4,2,256,1408]{3,2,1,0:T(8,128)(2,1)}, u32[]{:S(2)}, u32[]{:S(2)}) collective-permute-start(bf16[4,2,256,1408]{3,2,1,0:T(8,128)(2,1)} %bitcast.95.refs_2_.refs_4_), channel_id=1, source_target_pairs={{0,4},{4,0},{8,12},{12,8},{16,20},{20,16},{24,28},{28,24},{1,5},{5... | collective-permute-start | bytes 17301512 | tf_op jit(solution)/shard_map/ppermute | solution.py:165
  67.7 12.9 %collective-permute-start.5 = (bf16[768,256]{1,0:T(8,128)(2,1)S(1)}, bf16[768,256]{1,0:T(8,128)(2,1)S(1)}, u32[]{:S(2)}, u32[]{:S(2)}) collective-permute-start(bf16[768,256]{1,0:T(8,128)(2,1)S(1)} %copy-done.90), channel_id=1, source_target_pairs={{0,8},{4,12},{8,0},{12,4},{16,24},{20,28},{24,16},{28,20},{1,9},{5... | collective-permute-start | bytes 1179656 | tf_op jit(solution)/shard_map/ppermute | solution.py:161
  72.6 15.0 %collective-permute-start.8 = (bf16[768,256]{1,0:T(8,128)(2,1)S(1)}, bf16[768,256]{1,0:T(8,128)(2,1)S(1)}, u32[]{:S(2)}, u32[]{:S(2)}) collective-permute-start(bf16[768,256]{1,0:T(8,128)(2,1)S(1)} %copy-done.89), channel_id=1, source_target_pairs={{0,16},{4,20},{8,24},{12,28},{16,0},{20,4},{24,8},{28,12},{1,17},{... | collective-permute-start | bytes 1179656 | tf_op jit(solution)/shard_map/ppermute | solution.py:161
  89.2 37.4 %collective-permute-start.27 = (bf16[4,512,256]{2,1,0:T(8,128)(2,1)S(1)}, bf16[4,512,256]{2,1,0:T(8,128)(2,1)S(1)}, u32[]{:S(2)}, u32[]{:S(2)}) collective-permute-start(bf16[4,512,256]{2,1,0:T(8,128)(2,1)S(1)} %copy-done.2), channel_id=1, source_target_pairs={{0,4},{4,0},{8,12},{12,8},{16,20},{20,16},{24,28},{28,24},{1,5},{5... | collective-permute-start | bytes 3145736 | tf_op jit(solution)/shard_map/ppermute | solution.py:165
  91.5 15.2 %collective-permute-start.9 = (bf16[768,256]{1,0:T(8,128)(2,1)S(1)}, bf16[768,256]{1,0:T(8,128)(2,1)}, u32[]{:S(2)}, u32[]{:S(2)}) collective-permute-start(bf16[768,256]{1,0:T(8,128)(2,1)S(1)} %add_convert_fusion.9), channel_id=1, source_target_pairs={{0,16},{4,20},{8,24},{12,28},{16,0},{20,4},{24,8},{28,12},{1,17},{... | collective-permute-start | bytes 1179656 | tf_op jit(solution)/shard_map/ppermute | solution.py:161
  93.2 13.4 %collective-permute-start.10 = (bf16[768,256]{1,0:T(8,128)(2,1)S(1)}, bf16[768,256]{1,0:T(8,128)(2,1)S(1)}, u32[]{:S(2)}, u32[]{:S(2)}) collective-permute-start(bf16[768,256]{1,0:T(8,128)(2,1)S(1)} %add_convert_fusion.8), channel_id=1, source_target_pairs={{0,8},{4,12},{8,0},{12,4},{16,24},{20,28},{24,16},{28,20},{1,9},{5... | collective-permute-start | bytes 1179656 | tf_op jit(solution)/shard_map/ppermute | solution.py:161
  149.8 20.9 %collective-permute-start.19 = (bf16[192,1408]{1,0:T(8,128)(2,1)}, bf16[192,1408]{1,0:T(8,128)(2,1)S(1)}, u32[]{:S(2)}, u32[]{:S(2)}) collective-permute-start(bf16[192,1408]{1,0:T(8,128)(2,1)} %get-tuple-element.192), channel_id=1, source_target_pairs={{0,8},{4,12},{8,0},{12,4},{16,24},{20,28},{24,16},{28,20},{1,9},{5... | collective-permute-start | bytes 1622024 | tf_op jit(solution)/shard_map/ppermute | solution.py:161
  163.9 15.1 %collective-permute-start.20 = (bf16[192,1408]{1,0:T(8,128)(2,1)S(1)}, bf16[192,1408]{1,0:T(8,128)(2,1)S(1)}, u32[]{:S(2)}, u32[]{:S(2)}) collective-permute-start(bf16[192,1408]{1,0:T(8,128)(2,1)S(1)} %copy-done.80), channel_id=1, source_target_pairs={{0,16},{4,20},{8,24},{12,28},{16,0},{20,4},{24,8},{28,12},{1,17},{... | collective-permute-start | bytes 1622024 | tf_op jit(solution)/shard_map/ppermute | solution.py:161
  165.4 16.3 %collective-permute-start.21 = (bf16[192,1408]{1,0:T(8,128)(2,1)S(1)}, bf16[192,1408]{1,0:T(8,128)(2,1)S(1)}, u32[]{:S(2)}, u32[]{:S(2)}) collective-permute-start(bf16[192,1408]{1,0:T(8,128)(2,1)S(1)} %copy-done.79), channel_id=1, source_target_pairs={{0,8},{4,12},{8,0},{12,4},{16,24},{20,28},{24,16},{28,20},{1,9},{5... | collective-permute-start | bytes 1622024 | tf_op jit(solution)/shard_map/ppermute | solution.py:161
  168.2 19.7 %collective-permute-start.22 = (bf16[192,1408]{1,0:T(8,128)(2,1)S(1)}, bf16[192,1408]{1,0:T(8,128)(2,1)S(1)}, u32[]{:S(2)}, u32[]{:S(2)}) collective-permute-start(bf16[192,1408]{1,0:T(8,128)(2,1)S(1)} %copy-done.78), channel_id=1, source_target_pairs={{0,16},{4,20},{8,24},{12,28},{16,0},{20,4},{24,8},{28,12},{1,17},{... | collective-permute-start | bytes 1622024 | tf_op jit(solution)/shard_map/ppermute | solution.py:161
  170.7 20.0 %collective-permute-start.29 = (bf16[2,192,256]{2,1,0:T(8,128)(2,1)S(1)}, bf16[2,192,256]{2,1,0:T(8,128)(2,1)S(1)}, u32[]{:S(2)}, u32[]{:S(2)}) collective-permute-start(bf16[2,192,256]{2,1,0:T(8,128)(2,1)S(1)} %add_convert_fusion.19), channel_id=1, source_target_pairs={{0,3},{1,2},{2,1},{3,0},{4,7},{5,6},{6,5},{7,4},{8,11},{9,10},{10,... | collective-permute-start | bytes 589832 | tf_op jit(solution)/shard_map/ppermute | solution.py:176
  187.9 15.8 %collective-permute-start.23 = (bf16[192,1408]{1,0:T(8,128)(2,1)S(1)}, bf16[192,1408]{1,0:T(8,128)(2,1)S(1)}, u32[]{:S(2)}, u32[]{:S(2)}) collective-permute-start(bf16[192,1408]{1,0:T(8,128)(2,1)S(1)} %add_convert_fusion.3), channel_id=1, source_target_pairs={{0,16},{4,20},{8,24},{12,28},{16,0},{20,4},{24,8},{28,12},{1,17},{... | collective-permute-start | bytes 1622024 | tf_op jit(solution)/shard_map/ppermute | solution.py:161
  189.4 14.3 %collective-permute-start.24 = (bf16[192,1408]{1,0:T(8,128)(2,1)S(1)}, bf16[192,1408]{1,0:T(8,128)(2,1)S(1)}, u32[]{:S(2)}, u32[]{:S(2)}) collective-permute-start(bf16[192,1408]{1,0:T(8,128)(2,1)S(1)} %add_convert_fusion.2), channel_id=1, source_target_pairs={{0,8},{4,12},{8,0},{12,4},{16,24},{20,28},{24,16},{28,20},{1,9},{5... | collective-permute-start | bytes 1622024 | tf_op jit(solution)/shard_map/ppermute | solution.py:161
  213.9 27.1 %collective-permute-start.37 = (bf16[2,192,1408]{2,1,0:T(8,128)(2,1)}, bf16[2,192,1408]{2,1,0:T(8,128)(2,1)}, u32[]{:S(2)}, u32[]{:S(2)}) collective-permute-start(bf16[2,192,1408]{2,1,0:T(8,128)(2,1)} %get-tuple-element.213), channel_id=1, source_target_pairs={{0,16},{4,20},{8,24},{12,28},{16,0},{20,4},{24,8},{28,12},{1,17},{... | collective-permute-start | bytes 3244040 | tf_op jit(solution)/shard_map/ppermute | solution.py:161
  214.5 29.1 %collective-permute-start.36 = (bf16[2,192,1408]{2,1,0:T(8,128)(2,1)}, bf16[2,192,1408]{2,1,0:T(8,128)(2,1)}, u32[]{:S(2)}, u32[]{:S(2)}) collective-permute-start(bf16[2,192,1408]{2,1,0:T(8,128)(2,1)} %get-tuple-element.207), channel_id=1, source_target_pairs={{0,8},{4,12},{8,0},{12,4},{16,24},{20,28},{24,16},{28,20},{1,9},{5... | collective-permute-start | bytes 3244040 | tf_op jit(solution)/shard_map/ppermute | solution.py:161
  215.3 45.1 %collective-permute-start.35 = (bf16[2,192,1408]{2,1,0:T(8,128)(2,1)}, bf16[2,192,1408]{2,1,0:T(8,128)(2,1)S(1)}, u32[]{:S(2)}, u32[]{:S(2)}) collective-permute-start(bf16[2,192,1408]{2,1,0:T(8,128)(2,1)} %get-tuple-element.210), channel_id=1, source_target_pairs={{0,8},{4,12},{8,0},{12,4},{16,24},{20,28},{24,16},{28,20},{1,9},{5... | collective-permute-start | bytes 3244040 | tf_op jit(solution)/shard_map/ppermute | solution.py:161
  226.8 34.3 %collective-permute-start.38 = (bf16[2,192,1408]{2,1,0:T(8,128)(2,1)}, bf16[2,192,1408]{2,1,0:T(8,128)(2,1)S(1)}, u32[]{:S(2)}, u32[]{:S(2)}) collective-permute-start(bf16[2,192,1408]{2,1,0:T(8,128)(2,1)} %get-tuple-element.214), channel_id=1, source_target_pairs={{0,16},{4,20},{8,24},{12,28},{16,0},{20,4},{24,8},{28,12},{1,17},{... | collective-permute-start | bytes 3244040 | tf_op jit(solution)/shard_map/ppermute | solution.py:161
  261.1 23.9 %collective-permute-start.39 = (bf16[2,192,1408]{2,1,0:T(8,128)(2,1)}, bf16[2,192,1408]{2,1,0:T(8,128)(2,1)S(1)}, u32[]{:S(2)}, u32[]{:S(2)}) collective-permute-start(bf16[2,192,1408]{2,1,0:T(8,128)(2,1)} %add_convert_fusion.1), channel_id=1, source_target_pairs={{0,16},{4,20},{8,24},{12,28},{16,0},{20,4},{24,8},{28,12},{1,17},{... | collective-permute-start | bytes 3244040 | tf_op jit(solution)/shard_map/ppermute | solution.py:161
  262.9 22.1 %collective-permute-start.40 = (bf16[2,192,1408]{2,1,0:T(8,128)(2,1)}, bf16[2,192,1408]{2,1,0:T(8,128)(2,1)}, u32[]{:S(2)}, u32[]{:S(2)}) collective-permute-start(bf16[2,192,1408]{2,1,0:T(8,128)(2,1)} %add_convert_fusion), channel_id=1, source_target_pairs={{0,8},{4,12},{8,0},{12,4},{16,24},{20,28},{24,16},{28,20},{1,9},{5... | collective-permute-start | bytes 3244040 | tf_op jit(solution)/shard_map/ppermute | solution.py:161
  263.7 20.2 %collective-permute-start.43 = (f32[8,768]{1,0:T(8,128)S(1)}, f32[8,768]{1,0:T(8,128)S(1)}, u32[]{:S(2)}, u32[]{:S(2)}) collective-permute-start(f32[8,768]{1,0:T(8,128)S(1)} %copy-done.65), channel_id=1, source_target_pairs={{0,24},{4,28},{8,16},{12,20},{16,8},{20,12},{24,0},{28,4},{1,25},{... | collective-permute-start | bytes 73736 | tf_op jit(solution)/shard_map/ppermute | solution.py:161
  264.6 19.3 %collective-permute-start.42 = (f32[8,768]{1,0:T(8,128)S(1)}, f32[8,768]{1,0:T(8,128)S(1)}, u32[]{:S(2)}, u32[]{:S(2)}) collective-permute-start(f32[8,768]{1,0:T(8,128)S(1)} %copy-done.65), channel_id=1, source_target_pairs={{0,16},{4,20},{8,24},{12,28},{16,0},{20,4},{24,8},{28,12},{1,17},{... | collective-permute-start | bytes 73736 | tf_op jit(solution)/shard_map/ppermute | solution.py:161
  266.4 17.5 %collective-permute-start.41 = (f32[8,768]{1,0:T(8,128)S(1)}, f32[8,768]{1,0:T(8,128)S(1)}, u32[]{:S(2)}, u32[]{:S(2)}) collective-permute-start(f32[8,768]{1,0:T(8,128)S(1)} %copy-done.65), channel_id=1, source_target_pairs={{0,8},{4,12},{8,0},{12,4},{16,24},{20,28},{24,16},{28,20},{1,9},{5... | collective-permute-start | bytes 73736 | tf_op jit(solution)/shard_map/ppermute | solution.py:161
  294.2 27.0 %collective-permute-start.44 = (bf16[2,192,1408]{2,1,0:T(8,128)(2,1)}, bf16[2,192,1408]{2,1,0:T(8,128)(2,1)S(1)}, u32[]{:S(2)}, u32[]{:S(2)}) collective-permute-start(bf16[2,192,1408]{2,1,0:T(8,128)(2,1)} %get-tuple-element.222.refs_0_), channel_id=1, source_target_pairs={{0,16},{4,20},{8,24},{12,28},{16,0},{20,4},{24,8},{28,12},{1,17},{... | collective-permute-start | bytes 3244040 | tf_op jit(solution)/shard_map/ppermute | solution.py:161
  295.1 44.0 %collective-permute-start.46 = (bf16[2,192,1408]{2,1,0:T(8,128)(2,1)}, bf16[2,192,1408]{2,1,0:T(8,128)(2,1)S(1)}, u32[]{:S(2)}, u32[]{:S(2)}) collective-permute-start(bf16[2,192,1408]{2,1,0:T(8,128)(2,1)} %get-tuple-element.223.refs_4_.refs_2_), channel_id=1, source_target_pairs={{0,16},{4,20},{8,24},{12,28},{16,0},{20,4},{24,8},{28,12},{1,17},{... | collective-permute-start | bytes 3244040 | tf_op jit(solution)/shard_map/ppermute | solution.py:161
  296.3 42.8 %collective-permute-start.45 = (bf16[2,192,1408]{2,1,0:T(8,128)(2,1)}, bf16[2,192,1408]{2,1,0:T(8,128)(2,1)}, u32[]{:S(2)}, u32[]{:S(2)}) collective-permute-start(bf16[2,192,1408]{2,1,0:T(8,128)(2,1)} %get-tuple-element.222.refs_0_), channel_id=1, source_target_pairs={{0,8},{4,12},{8,0},{12,4},{16,24},{20,28},{24,16},{28,20},{1,9},{5... | collective-permute-start | bytes 3244040 | tf_op jit(solution)/shard_map/ppermute | solution.py:161
  297.1 43.7 %collective-permute-start.47 = (bf16[2,192,1408]{2,1,0:T(8,128)(2,1)}, bf16[2,192,1408]{2,1,0:T(8,128)(2,1)S(1)}, u32[]{:S(2)}, u32[]{:S(2)}) collective-permute-start(bf16[2,192,1408]{2,1,0:T(8,128)(2,1)} %get-tuple-element.223.refs_4_.refs_2_), channel_id=1, source_target_pairs={{0,8},{4,12},{8,0},{12,4},{16,24},{20,28},{24,16},{28,20},{1,9},{5... | collective-permute-start | bytes 3244040 | tf_op jit(solution)/shard_map/ppermute | solution.py:161
  341.8 31.1 %collective-permute-start.48 = (bf16[2,192,1408]{2,1,0:T(8,128)(2,1)}, bf16[2,192,1408]{2,1,0:T(8,128)(2,1)}, u32[]{:S(2)}, u32[]{:S(2)}) collective-permute-start(bf16[2,192,1408]{2,1,0:T(8,128)(2,1)} %collective-permute-done.45.refs_1_), channel_id=1, source_target_pairs={{0,16},{4,20},{8,24},{12,28},{16,0},{20,4},{24,8},{28,12},{1,17},{... | collective-permute-start | bytes 3244040 | tf_op jit(solution)/shard_map/ppermute | solution.py:161
  344.5 28.4 %collective-permute-start.49 = (bf16[2,192,1408]{2,1,0:T(8,128)(2,1)S(1)}, bf16[2,192,1408]{2,1,0:T(8,128)(2,1)}, u32[]{:S(2)}, u32[]{:S(2)}) collective-permute-start(bf16[2,192,1408]{2,1,0:T(8,128)(2,1)S(1)} %collective-permute-done.46.refs_2_.refs_6_), channel_id=1, source_target_pairs={{0,8},{4,12},{8,0},{12,4},{16,24},{20,28},{24,16},{28,20},{1,9},{5... | collective-permute-start | bytes 3244040 | tf_op jit(solution)/shard_map/ppermute | solution.py:161
  372.9 15.8 %collective-permute-start.65 = (f32[8,192]{0,1:T(8,128)S(1)}, f32[8,192]{0,1:T(8,128)S(1)}, u32[]{:S(2)}, u32[]{:S(2)}) collective-permute-start(f32[8,192]{0,1:T(8,128)S(1)} %add_add_fusion), channel_id=1, source_target_pairs={{0,24},{4,28},{8,16},{12,20},{16,8},{20,12},{24,0},{28,4},{1,25},{... | collective-permute-start | bytes 18440 | tf_op jit(solution)/shard_map/ppermute | solution.py:161
  373.7 15.2 %collective-permute-start.64 = (f32[8,192]{0,1:T(8,128)S(1)}, f32[8,192]{0,1:T(8,128)S(1)}, u32[]{:S(2)}, u32[]{:S(2)}) collective-permute-start(f32[8,192]{0,1:T(8,128)S(1)} %add_add_fusion), channel_id=1, source_target_pairs={{0,16},{4,20},{8,24},{12,28},{16,0},{20,4},{24,8},{28,12},{1,17},{... | collective-permute-start | bytes 18440 | tf_op jit(solution)/shard_map/ppermute | solution.py:161
  375.7 13.2 %collective-permute-start.63 = (f32[8,192]{0,1:T(8,128)S(1)}, f32[8,192]{0,1:T(8,128)S(1)}, u32[]{:S(2)}, u32[]{:S(2)}) collective-permute-start(f32[8,192]{0,1:T(8,128)S(1)} %add_add_fusion), channel_id=1, source_target_pairs={{0,8},{4,12},{8,0},{12,4},{16,24},{20,28},{24,16},{28,20},{1,9},{5... | collective-permute-start | bytes 18440 | tf_op jit(solution)/shard_map/ppermute | solution.py:161
  394.5 19.1 %collective-permute-start.58 = (bf16[2,192,256]{2,1,0:T(8,128)(2,1)S(1)}, bf16[2,192,256]{2,1,0:T(8,128)(2,1)S(1)}, u32[]{:S(2)}, u32[]{:S(2)}) collective-permute-start(bf16[2,192,256]{2,1,0:T(8,128)(2,1)S(1)} %add_convert_fusion.15), channel_id=1, source_target_pairs={{0,3},{1,2},{2,1},{3,0},{4,7},{5,6},{6,5},{7,4},{8,11},{9,10},{10,... | collective-permute-start | bytes 589832 | tf_op jit(solution)/shard_map/ppermute | solution.py:176
  398.3 15.5 %collective-permute-start.52 = (bf16[192,1408]{1,0:T(8,128)(2,1)S(1)}, bf16[192,1408]{1,0:T(8,128)(2,1)S(1)}, u32[]{:S(2)}, u32[]{:S(2)}) collective-permute-start(bf16[192,1408]{1,0:T(8,128)(2,1)S(1)} %copy-done.74), channel_id=1, source_target_pairs={{0,16},{4,20},{8,24},{12,28},{16,0},{20,4},{24,8},{28,12},{1,17},{... | collective-permute-start | bytes 1622024 | tf_op jit(solution)/shard_map/ppermute | solution.py:161
  398.3 18.6 %collective-permute-start.51 = (bf16[192,1408]{1,0:T(8,128)(2,1)S(1)}, bf16[192,1408]{1,0:T(8,128)(2,1)S(1)}, u32[]{:S(2)}, u32[]{:S(2)}) collective-permute-start(bf16[192,1408]{1,0:T(8,128)(2,1)S(1)} %copy-done.74), channel_id=1, source_target_pairs={{0,8},{4,12},{8,0},{12,4},{16,24},{20,28},{24,16},{28,20},{1,9},{5... | collective-permute-start | bytes 1622024 | tf_op jit(solution)/shard_map/ppermute | solution.py:161
  399.5 17.4 %collective-permute-start.54 = (bf16[192,1408]{1,0:T(8,128)(2,1)S(1)}, bf16[192,1408]{1,0:T(8,128)(2,1)}, u32[]{:S(2)}, u32[]{:S(2)}) collective-permute-start(bf16[192,1408]{1,0:T(8,128)(2,1)S(1)} %copy-done.75), channel_id=1, source_target_pairs={{0,16},{4,20},{8,24},{12,28},{16,0},{20,4},{24,8},{28,12},{1,17},{... | collective-permute-start | bytes 1622024 | tf_op jit(solution)/shard_map/ppermute | solution.py:161
  401.5 15.3 %collective-permute-start.53 = (bf16[192,1408]{1,0:T(8,128)(2,1)S(1)}, bf16[192,1408]{1,0:T(8,128)(2,1)}, u32[]{:S(2)}, u32[]{:S(2)}) collective-permute-start(bf16[192,1408]{1,0:T(8,128)(2,1)S(1)} %copy-done.75), channel_id=1, source_target_pairs={{0,8},{4,12},{8,0},{12,4},{16,24},{20,28},{24,16},{28,20},{1,9},{5... | collective-permute-start | bytes 1622024 | tf_op jit(solution)/shard_map/ppermute | solution.py:161
  434.8 15.6 %collective-permute-start.66 = (bf16[768,128]{1,0:T(8,128)(2,1)}, bf16[768,128]{1,0:T(8,128)(2,1)S(1)}, u32[]{:S(2)}, u32[]{:S(2)}) collective-permute-start(bf16[768,128]{1,0:T(8,128)(2,1)} %get-tuple-element.246), channel_id=1, source_target_pairs={{0,8},{4,12},{8,0},{12,4},{16,24},{20,28},{24,16},{28,20},{1,9},{5... | collective-permute-start | bytes 589832 | tf_op jit(solution)/shard_map/ppermute | solution.py:161
  436.1 14.2 %collective-permute-start.67 = (bf16[768,128]{1,0:T(8,128)(2,1)}, bf16[768,128]{1,0:T(8,128)(2,1)S(1)}, u32[]{:S(2)}, u32[]{:S(2)}) collective-permute-start(bf16[768,128]{1,0:T(8,128)(2,1)} %get-tuple-element.248), channel_id=1, source_target_pairs={{0,8},{4,12},{8,0},{12,4},{16,24},{20,28},{24,16},{28,20},{1,9},{5... | collective-permute-start | bytes 589832 | tf_op jit(solution)/shard_map/ppermute | solution.py:161
  436.9 13.4 %collective-permute-start.68 = (bf16[768,128]{1,0:T(8,128)(2,1)}, bf16[768,128]{1,0:T(8,128)(2,1)S(1)}, u32[]{:S(2)}, u32[]{:S(2)}) collective-permute-start(bf16[768,128]{1,0:T(8,128)(2,1)} %get-tuple-element.250), channel_id=1, source_target_pairs={{0,16},{4,20},{8,24},{12,28},{16,0},{20,4},{24,8},{28,12},{1,17},{... | collective-permute-start | bytes 589832 | tf_op jit(solution)/shard_map/ppermute | solution.py:161
  436.9 13.5 %collective-permute-start.69 = (bf16[768,128]{1,0:T(8,128)(2,1)}, bf16[768,128]{1,0:T(8,128)(2,1)S(1)}, u32[]{:S(2)}, u32[]{:S(2)}) collective-permute-start(bf16[768,128]{1,0:T(8,128)(2,1)} %get-tuple-element.251), channel_id=1, source_target_pairs={{0,16},{4,20},{8,24},{12,28},{16,0},{20,4},{24,8},{28,12},{1,17},{... | collective-permute-start | bytes 589832 | tf_op jit(solution)/shard_map/ppermute | solution.py:161
  456.3 21.1 %collective-permute-start.73 = (bf16[192,1408]{1,0:T(8,128)(2,1)S(1)}, bf16[192,1408]{1,0:T(8,128)(2,1)S(1)}, u32[]{:S(2)}, u32[]{:S(2)}) collective-permute-start(bf16[192,1408]{1,0:T(8,128)(2,1)S(1)} %collective-permute-done.51.refs_1_), channel_id=1, source_target_pairs={{0,16},{4,20},{8,24},{12,28},{16,0},{20,4},{24,8},{28,12},{1,17},{... | collective-permute-start | bytes 1622024 | tf_op jit(solution)/shard_map/ppermute | solution.py:161
  458.2 19.2 %collective-permute-start.74 = (bf16[192,1408]{1,0:T(8,128)(2,1)}, bf16[192,1408]{1,0:T(8,128)(2,1)S(1)}, u32[]{:S(2)}, u32[]{:S(2)}) collective-permute-start(bf16[192,1408]{1,0:T(8,128)(2,1)} %collective-permute-done.54.refs_6_), channel_id=1, source_target_pairs={{0,8},{4,12},{8,0},{12,4},{16,24},{20,28},{24,16},{28,20},{1,9},{5... | collective-permute-start | bytes 1622024 | tf_op jit(solution)/shard_map/ppermute | solution.py:161
  476.4 26.0 %collective-permute-start.78 = (bf16[768,256]{1,0:T(8,128)(2,1)S(1)}, bf16[768,256]{1,0:T(8,128)(2,1)}, u32[]{:S(2)}, u32[]{:S(2)}) collective-permute-start(bf16[768,256]{1,0:T(8,128)(2,1)S(1)} %copy-done.84), channel_id=1, source_target_pairs={{0,16},{4,20},{8,24},{12,28},{16,0},{20,4},{24,8},{28,12},{1,17},{... | collective-permute-start | bytes 1179656 | tf_op jit(solution)/shard_map/ppermute | solution.py:161
  476.6 25.9 %collective-permute-start.72 = (bf16[768,256]{1,0:T(8,128)(2,1)S(1)}, bf16[768,256]{1,0:T(8,128)(2,1)}, u32[]{:S(2)}, u32[]{:S(2)}) collective-permute-start(bf16[768,256]{1,0:T(8,128)(2,1)S(1)} %copy-done.84), channel_id=1, source_target_pairs={{0,8},{4,12},{8,0},{12,4},{16,24},{20,28},{24,16},{28,20},{1,9},{5... | collective-permute-start | bytes 1179656 | tf_op jit(solution)/shard_map/ppermute | solution.py:161
  482.1 20.8 %collective-permute-start.77 = (bf16[768,256]{1,0:T(8,128)(2,1)}, bf16[768,256]{1,0:T(8,128)(2,1)S(1)}, u32[]{:S(2)}, u32[]{:S(2)}) collective-permute-start(bf16[768,256]{1,0:T(8,128)(2,1)} %get-tuple-element.265.refs_4_), channel_id=1, source_target_pairs={{0,8},{4,12},{8,0},{12,4},{16,24},{20,28},{24,16},{28,20},{1,9},{5... | collective-permute-start | bytes 1179656 | tf_op jit(solution)/shard_map/ppermute | solution.py:161
  483.0 19.9 %collective-permute-start.76 = (bf16[768,256]{1,0:T(8,128)(2,1)}, bf16[768,256]{1,0:T(8,128)(2,1)S(1)}, u32[]{:S(2)}, u32[]{:S(2)}) collective-permute-start(bf16[768,256]{1,0:T(8,128)(2,1)} %get-tuple-element.265.refs_4_), channel_id=1, source_target_pairs={{0,16},{4,20},{8,24},{12,28},{16,0},{20,4},{24,8},{28,12},{1,17},{... | collective-permute-start | bytes 1179656 | tf_op jit(solution)/shard_map/ppermute | solution.py:161
  502.4 77.0 %collective-permute-start.91 = (bf16[4,256,1408]{2,1,0:T(8,128)(2,1)}, bf16[4,256,1408]{2,1,0:T(8,128)(2,1)}, u32[]{:S(2)}, u32[]{:S(2)}) collective-permute-start(bf16[4,256,1408]{2,1,0:T(8,128)(2,1)} %get-tuple-element.290), channel_id=1, source_target_pairs={{0,4},{4,0},{8,12},{12,8},{16,20},{20,16},{24,28},{28,24},{1,5},{5... | collective-permute-start | bytes 8650760 | tf_op jit(solution)/shard_map/ppermute | solution.py:165
  502.5 77.0 %collective-permute-start.92 = (bf16[4,256,1408]{2,1,0:T(8,128)(2,1)}, bf16[4,256,1408]{2,1,0:T(8,128)(2,1)}, u32[]{:S(2)}, u32[]{:S(2)}) collective-permute-start(bf16[4,256,1408]{2,1,0:T(8,128)(2,1)} %get-tuple-element.291), channel_id=1, source_target_pairs={{0,4},{4,0},{8,12},{12,8},{16,20},{20,16},{24,28},{28,24},{1,5},{5... | collective-permute-start | bytes 8650760 | tf_op jit(solution)/shard_map/ppermute | solution.py:165
  517.0 18.7 %collective-permute-start.88 = (bf16[2,384,256]{2,1,0:T(8,128)(2,1)S(1)}, bf16[2,384,256]{2,1,0:T(8,128)(2,1)S(1)}, u32[]{:S(2)}, u32[]{:S(2)}) collective-permute-start(bf16[2,384,256]{2,1,0:T(8,128)(2,1)S(1)} %add_convert_fusion.7), channel_id=1, source_target_pairs={{0,3},{1,2},{2,1},{3,0},{4,7},{5,6},{6,5},{7,4},{8,11},{9,10},{10,... | collective-permute-start | bytes 1179656 | tf_op jit(solution)/shard_map/ppermute | solution.py:176
  524.6 13.6 %collective-permute-start.86 = (f32[8,768]{1,0:T(8,128)S(1)}, f32[8,768]{1,0:T(8,128)S(1)}, u32[]{:S(2)}, u32[]{:S(2)}) collective-permute-start(f32[8,768]{1,0:T(8,128)S(1)} %add_add_fusion.2), channel_id=1, source_target_pairs={{0,3},{1,2},{2,1},{3,0},{4,7},{5,6},{6,5},{7,4},{8,11},{9,10},{10,... | collective-permute-start | bytes 73736 | tf_op jit(solution)/shard_map/ppermute | solution.py:176
  524.9 13.4 %collective-permute-start.85 = (f32[8,768]{1,0:T(8,128)S(1)}, f32[8,768]{1,0:T(8,128)S(1)}, u32[]{:S(2)}, u32[]{:S(2)}) collective-permute-start(f32[8,768]{1,0:T(8,128)S(1)} %add_add_fusion.2), channel_id=1, source_target_pairs={{0,2},{1,3},{2,0},{3,1},{4,6},{5,7},{6,4},{7,5},{8,10},{9,11},{10,... | collective-permute-start | bytes 73736 | tf_op jit(solution)/shard_map/ppermute | solution.py:176
  538.2 83.8 %collective-permute-start.103 = (bf16[4,1408,256]{2,1,0:T(8,128)(2,1)}, bf16[4,1408,256]{2,1,0:T(8,128)(2,1)}, u32[]{:S(2)}, u32[]{:S(2)}) collective-permute-start(bf16[4,1408,256]{2,1,0:T(8,128)(2,1)} %get-tuple-element.308), channel_id=1, source_target_pairs={{0,4},{4,0},{8,12},{12,8},{16,20},{20,16},{24,28},{28,24},{1,5},{5... | collective-permute-start | bytes 8650760 | tf_op jit(solution)/shard_map/ppermute | solution.py:165
  538.3 13.3 %collective-permute-start.89 = (bf16[2,384,256]{2,1,0:T(8,128)(2,1)S(1)}, bf16[2,384,256]{2,1,0:T(8,128)(2,1)S(1)}, u32[]{:S(2)}, u32[]{:S(2)}) collective-permute-start(bf16[2,384,256]{2,1,0:T(8,128)(2,1)S(1)} %add_convert_fusion.6.refs_0_), channel_id=1, source_target_pairs={{0,1},{1,0},{2,3},{3,2},{4,5},{5,4},{6,7},{7,6},{8,9},{9,8},{10,11... | collective-permute-start | bytes 1179656 | tf_op jit(solution)/shard_map/ppermute | solution.py:176
  539.9 18.3 %collective-permute-start.93 = (bf16[2,384,256]{2,1,0:T(8,128)(2,1)}, bf16[2,384,256]{2,1,0:T(8,128)(2,1)S(1)}, u32[]{:S(2)}, u32[]{:S(2)}) collective-permute-start(bf16[2,384,256]{2,1,0:T(8,128)(2,1)} %get-tuple-element.293), channel_id=1, source_target_pairs={{0,1},{1,0},{2,3},{3,2},{4,5},{5,4},{6,7},{7,6},{8,9},{9,8},{10,11... | collective-permute-start | bytes 1179656 | tf_op jit(solution)/shard_map/ppermute | solution.py:176
  558.4 12.6 %collective-permute-start.94 = (bf16[2,384,256]{2,1,0:T(8,128)(2,1)S(1)}, bf16[2,384,256]{2,1,0:T(8,128)(2,1)S(1)}, u32[]{:S(2)}, u32[]{:S(2)}) collective-permute-start(bf16[2,384,256]{2,1,0:T(8,128)(2,1)S(1)} %add_convert_fusion.5), channel_id=1, source_target_pairs={{0,3},{1,2},{2,1},{3,0},{4,7},{5,6},{6,5},{7,4},{8,11},{9,10},{10,... | collective-permute-start | bytes 1179656 | tf_op jit(solution)/shard_map/ppermute | solution.py:176
  564.4 33.0 %all-to-all-start.1 = ((bf16[8,256,256]{2,1,0:T(8,128)(2,1)}), bf16[8,256,256]{2,1,0:T(8,128)(2,1)S(1)}, u32[]{:S(2)}, u32[]{:S(2)}) async-start(bf16[8,256,256]{2,1,0:T(8,128)(2,1)} %bitcast.104), calls=%async_computation.1 | async-start | bytes 2097152 | tf_op jit(solution)/shard_map/all_to_all | solution.py:1217
  571.0 18.9 %collective-permute-start.95 = (bf16[2,384,256]{2,1,0:T(8,128)(2,1)S(1)}, bf16[2,384,256]{2,1,0:T(8,128)(2,1)S(1)}, u32[]{:S(2)}, u32[]{:S(2)}) collective-permute-start(bf16[2,384,256]{2,1,0:T(8,128)(2,1)S(1)} %add_convert_fusion.4.refs_0_), channel_id=1, source_target_pairs={{0,1},{1,0},{2,3},{3,2},{4,5},{5,4},{6,7},{7,6},{8,9},{9,8},{10,11... | collective-permute-start | bytes 1179656 | tf_op jit(solution)/shard_map/ppermute | solution.py:176
  596.4 12.3 %collective-permute-start.102 = (bf16[4,512,256]{2,1,0:T(8,128)(2,1)}, bf16[4,512,256]{2,1,0:T(8,128)(2,1)S(1)}, u32[]{:S(2)}, u32[]{:S(2)}) collective-permute-start(bf16[4,512,256]{2,1,0:T(8,128)(2,1)} %get-tuple-element.307), channel_id=1, source_target_pairs={{0,4},{4,0},{8,12},{12,8},{16,20},{20,16},{24,28},{28,24},{1,5},{5... | collective-permute-start | bytes 3145736 | tf_op jit(solution)/shard_map/ppermute | solution.py:165
  596.9 16.2 %collective-permute-start.101 = (bf16[4,256,512]{2,1,0:T(8,128)(2,1)}, bf16[4,256,512]{2,1,0:T(8,128)(2,1)}, u32[]{:S(2)}, u32[]{:S(2)}) collective-permute-start(bf16[4,256,512]{2,1,0:T(8,128)(2,1)} %get-tuple-element.306), channel_id=1, source_target_pairs={{0,4},{4,0},{8,12},{12,8},{16,20},{20,16},{24,28},{28,24},{1,5},{5... | collective-permute-start | bytes 3145736 | tf_op jit(solution)/shard_map/ppermute | solution.py:165
  616.0 18.9 %all-to-all-start.2 = ((bf16[8,256,256]{2,1,0:T(8,128)(2,1)}), bf16[8,256,256]{2,1,0:T(8,128)(2,1)S(1)}, u32[]{:S(2)}, u32[]{:S(2)}) async-start(bf16[8,256,256]{2,1,0:T(8,128)(2,1)} %bitcast.58), calls=%async_computation.2 | async-start | bytes 2097152 | tf_op jit(solution)/shard_map/all_to_all | solution.py:1217
  (136 other events, 1164.8 us)

commit v6 on v5

--- a/solution.py
+++ b/solution.py
@@ -271,16 +271,10 @@
         shift = m[j] & 7
         return pl.ds(pl.multiple_of(m[j] - shift, 8), seq_len + 8), shift
 
-    def take_rows(dealt, source, all_ref):
-        count = slots * seq_len if dealt else seqs * per
-        start = seqs * per if dealt else 0
-        for p in range(dp):
-            source[p * count : (p + 1) * count, :] = all_ref[p, start : start + count, :].astype(F32)
-
     def pack_body(dealt, m, all_ref, *refs):
         outs = refs[:parts]
         source, packed, whole = refs[parts:]
-        take_rows(dealt, source, all_ref)
+        source[...] = all_ref[...].astype(F32)
 
         line = lax.broadcasted_iota(jnp.int32, (seq_len + 8, ds), 0)
 
@@ -309,11 +303,10 @@
 
     x_send = hidden_in.reshape(seqs * per, dp, ds).transpose(1, 0, 2)
     d_send = cotangent.reshape(slots * seq_len, dp, ds).transpose(1, 0, 2)
-    arrived = lax.all_to_all(
-        jnp.concatenate([x_send, d_send], axis=1), "dp", 0, 0, tiled=True
-    )
-    x_pieces = pack(arrived, False)
-    d_pieces = pack(arrived, True)
+    x_all = lax.all_to_all(x_send, "dp", 0, 0, tiled=True).reshape(rows_all, ds)
+    x_pieces = pack(x_all, False)
+    d_all = lax.all_to_all(d_send, "dp", 0, 0, tiled=True).reshape(rows_all, ds)
+    d_pieces = pack(d_all, True)
 
     def spread(vector):
         tall = vector.reshape((groups, parts, ds) + vector.shape[1:])[g]
@@ -436,14 +429,14 @@
     outs = [((rp, 2 * HD), BF16, (tile, 2 * HD), lambda i, m: (i, 0))] * 8
     outs += [((8, rp), F32, (8, tile), lambda i, m: (0, i))]
     qkv = run(
-        qkv_body, "qkv", (rp // tile,), after(meta, d_pieces[0]), ins, outs,
+        qkv_body, "qkv", (rp // tile,), after(meta, in_own), ins, outs,
         [pltpu.VMEM((heads, tile, 4 * HD), BF16)],
         flops=2 * rp * (experts + 2) * parts * ds * hw,
     )
     dh = dhidden(after(meta, qkv[8]))
-    q_sum, kv_sum, sent, far = reduce_groups(qkv[0:8:2], qkv[1:8:2])
-    stats_a = sum_groups(after(qkv[8], far))
+    stats_a = sum_groups(qkv[8])
     flat_a, cols_a = gate_columns(stats_a, low_a, high_a)
+    q_sum, kv_sum, _, _ = reduce_groups(qkv[0:8:2], qkv[1:8:2], late=cols_a)
 
     def rope_body(m, a0, a1, a2, b0, b1, b2, cols, cos_ref, sin_ref, q_ref, kv_ref):
         rms = cols[:, 0:1]
@@ -546,16 +539,19 @@
             flops=4 * zr * experts * hw * parts * ds,
         )
 
-    halves = [z_first(*project(0, meta))]
+    sums = [project(0, meta)]
     dh_a, dh_b = held((dh[0:8:2], dh[1:8:2]), gm_a[3], gm_b[3])
     ra, rb = by_group(dh_a[3], 1), by_group(dh_b[3], 2)
+    halves = [z_first(*sums[0])]
     for k in range(1, chunks):
-        halves.append(z_first(*project(k, after(meta, halves[-1]))))
+        sums.append(project(k, after(meta, halves[-1])))
+        halves[-1] = z_covered(halves[-1], halves[-1], 3, sums[-1][0])
+        halves.append(z_first(*sums[-1]))
+    halves[-1] = z_second(halves[-1])
     ax, by = by_group(dh_a[1], 1), by_group(dh_b[2], 2)
-    halves = [z_second(half) for half in halves]
-    along = held((both(dh_a[2], ra), both(dh_b[1], rb)), (ax, by))
-    dh_a, dh_b = (dh_a[0], ax, by_group(along[0], 2)), (dh_b[0], by_group(along[1], 1), by)
     attn_totals = [half for v in halves for half in z_last(v)]
+    near = held((both(dh_a[2], ra), both(dh_b[1], rb)), (ax, by))
+    dh_a, dh_b = (dh_a[0], ax, by_group(near[0], 2)), (dh_b[0], by_group(near[1], 1), by)
 
     def norm_body(m, *refs):
         t_refs = refs[: 2 * chunks]
@@ -583,7 +579,7 @@
         ((parts, rp, ds), BF16, None, None),
         ((8, rp), F32, None, None),
     ]
-    after_rows, u_f, stats_part = run(norm_body, "norm", (1,), after(meta, along), ins, outs)
+    after_rows, u_f, stats_part = run(norm_body, "norm", (1,), after(meta, near), ins, outs)
     def up_body(m, *refs):
         u_refs, w_refs = refs[:2], refs[2 : 2 + parts]
         sel_refs = refs[2 + parts : 4 + parts]
@@ -663,7 +659,7 @@
     outs += [((2, blk, ff), BF16, (2, mt_rows, ff), rows_3)] * 2
     outs += [((blk, 8), F32, (mt_rows, 8), rows_2)]
     act_a, act_b, grad_a, grad_b, dots_f = run(mid_body, "mid", (3,), meta, ins, outs)
-    gg_a, gg_b, _ = gather_groups(grad_a, grad_b, late=(act_a,))
+    gg_a, gg_b, gg_along = gather_groups(grad_a, grad_b, late=(act_a,))
     dots_f = dots_f.T
 
     def dx_body(m, *refs):
@@ -706,7 +702,8 @@
     dots_f = after(sum_z(dots_f), gg_a[3], gg_b[3])
     dots_f = jnp.stack([dots_f, by_group(dots_f, 1), by_group(dots_f, 2), by_group(dots_f, 3)])
     dx_far = dx((2, 3), meta)
-    near_half = held([z_second(z_first(*dx_near))], dx_far[0])[0]
+    near_half = z_first(*dx_near)
+    near_half = z_covered(near_half, near_half, 3, dx_far[0])
     far_half = z_first(*dx_far)
 
     act_a, act_b, _ = lax.optimization_barrier((act_a, act_b, far_half))
@@ -864,20 +861,6 @@
         after(meta, dwin_gate[0], ag_a[1:], ag_b[1:]), ins, outs,
     )
 
-    def whole_vectors(*smalls):
-        small = jnp.concatenate(smalls, axis=0)
-        full = jnp.zeros((small.shape[0], dp, ds), F32)
-        for s in pieces:
-            full = lax.dynamic_update_slice_in_dim(
-                full, small[:, s : s + 1], g * parts + (c ^ s), axis=1
-            )
-        mask = 1
-        while mask < dp:
-            full = full + lax.ppermute(full, "dp", [(a, a ^ mask) for a in range(dp)])
-            mask *= 2
-        full = full.reshape(len(smalls), experts + 1, width)
-        return [(v[:experts].T, v[experts]) for v in full]
-
     def dmix_body(m, *refs):
         d_ref = refs[0]
         w_refs = refs[1 : 1 + parts]
@@ -1108,9 +1091,8 @@
             flops=8 * zr * (experts + 2) * hw * parts * ds,
         )
 
-    dots_a = sum_groups(after(dots_q + jnp.where(third, dots_kv, 0.0), da_along))
-    da_halves = dattn(after(meta, dwproj_sums[0], dots_a))
-    dots_a = sum_z(dots_a)
+    dots_a = sum_groups(after(dots_q + jnp.where(third, dots_kv, 0.0), dwproj_sums[0]))
+    da_halves = dattn(after(meta, dwproj_sums[0]))
     x_stack = jnp.stack(x_pieces)
     attn_input = (x_stack.astype(F32) * flat_a[0][None, :, None] * gain_a).astype(BF16)
 
@@ -1154,6 +1136,7 @@
         )
 
     dwqkv_sums = dwqkv(after(meta, da_halves[0], dots_a))
+    dots_a = sum_z(dots_a)
 
 
     da_half = z_covered(*da_halves, 1, dwqkv_sums[0])
@@ -1178,12 +1161,14 @@
         [((rp, ds), BF16, None, None)] * parts,
     )
 
+    count = rows_all // dp
+
     def unpack_body(dealt, m, other_ref, *refs):
-        v_refs, out_ref = refs[:parts], refs[parts]
-        packed, other, total, whole = refs[parts + 1 :]
+        v_refs, out_ref = refs[:parts], refs[-5]
+        packed, other, total, whole = refs[-4:]
         for s in pieces:
             packed[part_rows(m, s), :] = v_refs[s][...].astype(F32)
-        take_rows(dealt, other, other_ref)
+        other[...] = other_ref[...].astype(F32)
         line = lax.broadcasted_iota(jnp.int32, (per, ds), 0)
 
         def one(j, carry):
@@ -1201,26 +1186,29 @@
             return carry
 
         lax.fori_loop(0, seqs, one, 0)
-        out_ref[...] = total[...].astype(BF16)
-
-    def unpack(value, otherwise, dealt, table):
+        for p in range(dp):
+            out_ref[p, :count, :] = total[p * count : (p + 1) * count, :].astype(BF16)
+            for ref in refs[parts:-5]:
+                out_ref[p, count:, :] = ref[...]
+
+    def unpack(value, otherwise, dealt, table, extra=()):
         mine_all = [value[0]] + [by_part(value[s], s) for s in pieces[1:]]
-        ins = [(v, None, None) for v in [otherwise] + mine_all]
+        ins = [(v, None, None) for v in [otherwise] + mine_all + list(extra)]
+        tall = count + sum(v.shape[0] for v in extra)
         spread_rows = run(
             functools.partial(unpack_body, dealt), "unpack", (1,), table, ins,
-            [((rows_all, ds), BF16, None, None)],
+            [((dp, tall, ds), BF16, None, None)],
             [
                 pltpu.VMEM((n, ds), F32)
                 for n in (rows + seq_len + 8, rows_all, rows_all, seq_len + 8)
             ],
         )[0]
-        landed = lax.all_to_all(
-            spread_rows.reshape(dp, seqs * per, ds), "dp", 0, 0, tiled=True
-        )
-        return landed.transpose(1, 0, 2).reshape(seqs, per, width), spread_rows
-
-    layer_out, layer_rows = unpack(out_rows, arrived, False, table)
-    expertin_grad = fold((dwin_gate, dwin_up), after(meta, layer_rows))
+        landed = lax.all_to_all(spread_rows, "dp", 0, 0, tiled=True)
+        rows_of = landed[:, :count].transpose(1, 0, 2).reshape(seqs, per, width)
+        return rows_of, spread_rows, landed[:, count:]
+
+    layer_out, layer_rows, _ = unpack(out_rows, x_all, False, table)
+    expertin_grad = fold((dwin_gate, dwin_up), after(meta, layer_rows, dots_a))
     back_a = back_columns(flat_a, dots_a, low_a, high_a)
     da_half = z_covered(da_half, da_half, 3, layer_rows)
     da_totals = z_last(da_half)
@@ -1236,9 +1224,17 @@
     expertout_grad = exchange(dwout_sums)
     proj_grad = exchange(dwproj_sums)
     query_grad, kv_grad = exchange(dwqkv_sums[:parts]), exchange(dwqkv_sums[parts:])
-    input_grad, last_rows = unpack(dinput, arrived, True, after(table, layer_out))
-    vectors = whole_vectors(after(small_a, last_rows), small_f)
-    (attnrouter_grad, attngain_grad), (ffnrouter_grad, ffngain_grad) = vectors
+    vectors = 2 * (experts + 1)
+    small = jnp.concatenate([small_a, small_f], axis=0).reshape(vectors * parts, ds)
+    small = jnp.pad(small, ((0, -vectors * parts % 16), (0, 0))).astype(BF16)
+    input_grad, _, got = unpack(dinput, d_all, True, after(table, layer_out), [small])
+    got = got[:, : vectors * parts].astype(F32).reshape(groups, parts, vectors, parts, ds)
+    full = jnp.stack(
+        [sum(got[:, k ^ s, :, s] for s in pieces) for k in range(parts)], axis=2
+    )
+    full = full.transpose(1, 0, 2, 3).reshape(2, experts + 1, width)
+    attnrouter_grad, attngain_grad = full[0, :experts].T, full[0, experts]
+    ffnrouter_grad, ffngain_grad = full[1, :experts].T, full[1, experts]
     return (
         layer_out,
         input_grad,

time: 648 us -> 652 us (level)
  starting transfers between devices: 134 us -> 141 us
    ppermute x24, waiting for transfers between devices: 29.1 us -> 52.2 us  [by_z(): return lax.ppermute(value, 'tensor', [(a, a ^ mask) for a in range(tp)])]
    all_to_all x3 -> x4, waiting for transfers between devices: 29.5 us -> 11.7 us  [the longest x2 9.29 us: unpack(): landed = lax.all_to_all(spread_rows, 'dp', 0, 0, tiled=True)]
    ppermute x24, starting transfers between devices: 45.7 us -> 53.4 us  [by_z(): return lax.ppermute(value, 'tensor', [(a, a ^ mask) for a in range(tp)])]
    unnamed x196 -> x222, local copies, waits for them, and re-layouts: 23.6 us -> 18 us
    all_to_all x3 -> x4, starting transfers between devices: 12.7 us -> 16.6 us  [the longest x2 8.01 us: unpack(): landed = lax.all_to_all(spread_rows, 'dp', 0, 0, tiled=True)]
  transfers between devices with their start and end apart: 107 -> 105, of which waited for: 38 -> 34; matrix products, arithmetic and copies ran while one was open for 8% -> 9% of each run, Pallas kernels for 32% -> 31%
where the time goes in v6:
time: 652 us; the launch traced here: 646 us
  Pallas kernels  233 us (36%)
  waiting for transfers between devices  197 us (30%)
  starting transfers between devices  141 us (22%)
  local copies, waits for them, and re-layouts  38.1 us (6%)
  other arithmetic  33.4 us (5%)
    pallas_call x29, Pallas kernels, run(): pl.pallas_call(body, name=name, grid_spec=pltpu.PrefetchScalarGridSpec(nu...  233 us
    ppermute x60, waiting for transfers between devices, by_group(): return lax.ppermute(value, 'dp', pairs)  132 us
    ppermute x60, starting transfers between devices, by_group(): return lax.ppermute(value, 'dp', pairs)  65.2 us
    ppermute x24, starting transfers between devices, by_z(): return lax.ppermute(value, 'tensor', [(a, a ^ mask) for a in range(tp)])  53.4 us
    ppermute x24, waiting for transfers between devices, by_z(): return lax.ppermute(value, 'tensor', [(a, a ^ mask) for a in range(tp)])  52.2 us
    unnamed x222, local copies, waits for them, and re-layouts  18 us
  transfers between devices with their start and end apart: 105, of which 34 were waited for; matrix products, arithmetic and copies ran while one was open for 9% of the time, Pallas kernels for 31%

profile of v6, /device:TPU:0, one launch (start us, length us, event | category | flops | bytes accessed | tf_op | source)
XLA Modules:
  0.0 646.3 jit_solution(15501580840906497960)
XLA Ops:
  3.9 4.8 all-to-all-start
  9.4 5.9 copy.241
  24.1 3.8 all-to-all-start.1
  28.5 4.0 pack.2
  38.2 8.5 %qkv.1 = (bf16[768,256]{1,0:T(8,128)(2,1)}, bf16[768,256]{1,0:T(8,128)(2,1)}, bf16[768,256]{1,0:T(8,128)(2,1)}, bf16[768,256]{1,0:T(8,128)(2,1)}, bf16[768,256]{...) custom-call(s32[24]{0:T(128)} %stack.153.m, ...), custom_call_target="tpu_custom_call" | custom-call | flops 2415919104 | bytes 7137280 | tf_op jit(solution)/shard_map/qkv/pallas_call | solution.py:61
  52.4 4.0 pack.3
  61.9 6.9 %collective-permute-done.5.a1 = bf16[768,256]{1,0:T(8,128)(2,1)} collective-permute-done((bf16[768,256]{1,0:T(8,128)(2,1)}, bf16[768,256]{1,0:T(8,128)(2,1)}, u32[]{:S(2)}, u32[]{:S(2)}) %collective-permute-start.5) | collective-permute-done | bytes 393248 | tf_op jit(solution)/shard_map/ppermute | solution.py:161
  68.7 6.9 %collective-permute-done.6 = bf16[768,256]{1,0:T(8,128)(2,1)S(1)} collective-permute-done((bf16[768,256]{1,0:T(8,128)(2,1)}, bf16[768,256]{1,0:T(8,128)(2,1)S(1)}, u32[]{:S(2)}, u32[]{:S(2)}) %collective-permute-start.6) | collective-permute-done | bytes 393248 | tf_op jit(solution)/shard_map/ppermute | solution.py:161
  79.2 8.1 %collective-permute-done.8.b2 = bf16[768,256]{1,0:T(8,128)(2,1)S(1)} collective-permute-done((bf16[768,256]{1,0:T(8,128)(2,1)}, bf16[768,256]{1,0:T(8,128)(2,1)S(1)}, u32[]{:S(2)}, u32[]{:S(2)}) %collective-permute-start.8) | collective-permute-done | bytes 393248 | tf_op jit(solution)/shard_map/ppermute | solution.py:161
  90.6 12.0 %dhidden.1 = (bf16[192,1408]{1,0:T(8,128)(2,1)}, bf16[192,1408]{1,0:T(8,128)(2,1)}, bf16[192,1408]{1,0:T(8,128)(2,1)}, bf16[192,1408]{1,0:T(8,128)(2,1)}, bf16[1...) custom-call(s32[24]{0:T(128)} %stack.153.m, ...), custom_call_target="tpu_custom_call" | custom-call | flops 4429185024 | bytes 11714560 | tf_op jit(solution)/shard_map/dhidden/pallas_call | solution.py:61
  103.5 4.6 rope.1
  111.9 8.3 %attend.1 = (bf16[768,128]{1,0:T(8,128)(2,1)}, bf16[768,128]{1,0:T(8,128)(2,1)}, bf16[768,128]{1,0:T(8,128)(2,1)}, bf16[768,128]{1,0:T(8,128)(2,1)}) custom-call(s32[24]{0:T(128)} %stack.153.m, bf16[768,256]{1,0:T(8,128)(2,1)} %get-tuple-element.180.q_ref.refs_0_, bf16[768,256]{1,0:T(8,128)(2,1)} %get-tuple-element.181.kv_ref.refs_1_, ...), custom_call_target="tpu_custom_call" | custom-call | flops 301989888 | bytes 1753088 | tf_op jit(solution)/shard_map/attend/pallas_call | solution.py:61
  124.4 3.9 collective-permute-done.15.refs_1_
  130.4 2.8 collective-permute-done.25.refs_2_
  133.2 3.3 collective-permute-done.16.refs_3_
  137.9 6.7 %proj.2 = (bf16[2,192,256]{2,1,0:T(8,128)(2,1)}, bf16[2,192,256]{2,1,0:T(8,128)(2,1)}) custom-call(s32[24]{0:T(128)} %stack.153.m, bf16[768,128]{1,0:T(8,128)(2,1)} %get-tuple-element.189.refs_0_, bf16[768,128]{1,0:T(8,128)(2,1)} %copy-done.21, bf16[768,128]{1,0:T(8,128)(2,1)} %copy-done.23, bf16[768,128]{1,0:T(8,128)(2,1)} %copy-done.25, ...), custom_call_target="tpu_custom_call" | custom-call | flops 805306368 | bytes 4087808 | tf_op jit(solution)/shard_map/proj/pallas_call | solution.py:61
  147.5 3.3 collective-permute-done.28
  151.9 6.8 %proj.3 = (bf16[2,192,256]{2,1,0:T(8,128)(2,1)}, bf16[2,192,256]{2,1,0:T(8,128)(2,1)}) custom-call(s32[24]{0:T(128)} %stack.153.m, bf16[768,128]{1,0:T(8,128)(2,1)} %get-tuple-element.189.refs_0_, bf16[768,128]{1,0:T(8,128)(2,1)} %copy-done.21, bf16[768,128]{1,0:T(8,128)(2,1)} %copy-done.23, bf16[768,128]{1,0:T(8,128)(2,1)} %copy-done.25, ...), custom_call_target="tpu_custom_call" | custom-call | flops 805306368 | bytes 4087808 | tf_op jit(solution)/shard_map/proj/pallas_call | solution.py:61
  164.6 3.6 collective-permute-start.29
  169.2 3.0 collective-permute-done.29
  172.7 3.6 collective-permute-start.32
  176.7 7.9 %collective-permute-done.22.refs_11_ = bf16[192,1408]{1,0:T(8,128)(2,1)S(1)} collective-permute-done((bf16[192,1408]{1,0:T(8,128)(2,1)S(1)}, bf16[192,1408]{1,0:T(8,128)(2,1)S(1)}, u32[]{:S(2)}, u32[]{:S(2)}) %collective-permute-start.22) | collective-permute-done | bytes 540704 | tf_op jit(solution)/shard_map/ppermute | solution.py:161
  186.6 4.3 collective-permute-start.30
  197.4 4.4 norm.1
  201.9 10.2 %up.2 = (bf16[2,192,1408]{2,1,0:T(8,128)(2,1)}, bf16[2,192,1408]{2,1,0:T(8,128)(2,1)}, bf16[2,192,1408]{2,1,0:T(8,128)(2,1)}, bf16[2,192,1408]{2,1,0:T(8,128)(2,1)}) custom-call(s32[24]{0:T(128)} %stack.153.m, bf16[2,768,256]{2,1,0:T(8,128)(2,1)} %get-tuple-element.208.refs_0_.refs_1_, bf16[2,768,256]{2,1,0:T(8,128)(2,1)} %get-tuple-element.208.refs_0_.refs_1_, ...), custom_call_target="tpu_custom_call" | custom-call | flops 4429185024 | bytes 17481728 | tf_op jit(solution)/shard_map/up/pallas_call | solution.py:61
  216.1 10.2 %up.3 = (bf16[2,192,1408]{2,1,0:T(8,128)(2,1)}, bf16[2,192,1408]{2,1,0:T(8,128)(2,1)}, bf16[2,192,1408]{2,1,0:T(8,128)(2,1)}, bf16[2,192,1408]{2,1,0:T(8,128)(2,1)}) custom-call(s32[24]{0:T(128)} %stack.153.m, bf16[2,768,256]{2,1,0:T(8,128)(2,1)} %get-tuple-element.208.refs_0_.refs_1_, bf16[2,768,256]{2,1,0:T(8,128)(2,1)} %get-tuple-element.208.refs_0_.refs_1_, ...), custom_call_target="tpu_custom_call" | custom-call | flops 4429185024 | bytes 17481728 | tf_op jit(solution)/shard_map/up/pallas_call | solution.py:61
  226.5 12.6 %collective-permute-done.37 = bf16[2,192,1408]{2,1,0:T(8,128)(2,1)} collective-permute-done((bf16[2,192,1408]{2,1,0:T(8,128)(2,1)}, bf16[2,192,1408]{2,1,0:T(8,128)(2,1)}, u32[]{:S(2)}, u32[]{:S(2)}) %collective-permute-start.37) | collective-permute-done | bytes 1081376 | tf_op jit(solution)/shard_map/ppermute | solution.py:161
  244.3 16.3 %collective-permute-done.35.refs_1_ = bf16[2,192,1408]{2,1,0:T(8,128)(2,1)S(1)} collective-permute-done((bf16[2,192,1408]{2,1,0:T(8,128)(2,1)}, bf16[2,192,1408]{2,1,0:T(8,128)(2,1)S(1)}, u32[]{:S(2)}, u32[]{:S(2)}) %collective-permute-start.35) | collective-permute-done | bytes 1081376 | tf_op jit(solution)/shard_map/ppermute | solution.py:161
  265.0 14.2 %collective-permute-done.43 = f32[8,768]{1,0:T(8,128)S(1)} collective-permute-done((f32[8,768]{1,0:T(8,128)S(1)}, f32[8,768]{1,0:T(8,128)S(1)}, u32[]{:S(2)}, u32[]{:S(2)}) %collective-permute-start.43) | collective-permute-done | bytes 24608 | tf_op jit(solution)/shard_map/ppermute | solution.py:161
  280.6 8.3 %mid.1 = (bf16[192,1408]{1,0:T(8,128)(2,1)}, bf16[192,1408]{1,0:T(8,128)(2,1)}, bf16[2,192,1408]{2,1,0:T(8,128)(2,1)}, bf16[2,192,1408]{2,1,0:T(8,128)(2,1)}, f32[192,8]{1,0:T(8,128)}) custom-call(s32[24]{0:T(128)} %stack.153.m, bf16[2,192,1408]{2,1,0:T(8,128)(2,1)} %get-tuple-element.211.refs_0_, bf16[2,192,1408]{2,1,0:T(8,128)(2,1)} %copy-done.14, ...), custom_call_target="tpu_custom_call" | custom-call | bytes 13006848 | tf_op jit(solution)/shard_map/mid/pallas_call | solution.py:61
  293.2 22.8 %collective-permute-done.45.refs_1_ = bf16[2,192,1408]{2,1,0:T(8,128)(2,1)S(1)} collective-permute-done((bf16[2,192,1408]{2,1,0:T(8,128)(2,1)}, bf16[2,192,1408]{2,1,0:T(8,128)(2,1)S(1)}, u32[]{:S(2)}, u32[]{:S(2)}) %collective-permute-start.45) | collective-permute-done | bytes 1081376 | tf_op jit(solution)/shard_map/ppermute | solution.py:161
  316.6 18.5 %collective-permute-done.47.refs_5_.refs_3_ = bf16[2,192,1408]{2,1,0:T(8,128)(2,1)S(1)} collective-permute-done((bf16[2,192,1408]{2,1,0:T(8,128)(2,1)}, bf16[2,192,1408]{2,1,0:T(8,128)(2,1)S(1)}, u32[]{:S(2)}, u32[]{:S(2)}) %collective-permute-start.47) | collective-permute-done | bytes 1081376 | tf_op jit(solution)/shard_map/ppermute | solution.py:161
  340.9 2.8 collective-permute-start.62
  343.8 11.0 %dx.3 = (bf16[2,192,256]{2,1,0:T(8,128)(2,1)}, bf16[2,192,256]{2,1,0:T(8,128)(2,1)}) custom-call(s32[24]{0:T(128)} %stack.153.m, bf16[2,192,1408]{2,1,0:T(8,128)(2,1)} %get-tuple-element.224.refs_0_, bf16[2,192,1408]{2,1,0:T(8,128)(2,1)} %copy-done.11, bf16[2,192,1408]{2,1,0:T(8,128)(2,1)} %get-tuple-element.225.refs_4_.refs_2_, ...), custom_call_target="tpu_custom_call" | custom-call | flops 4429185024 | bytes 16302080 | tf_op jit(solution)/shard_map/dx/pallas_call | solution.py:61
  356.9 4.4 collective-permute-done.55
  367.8 11.0 %dx.2 = (bf16[2,192,256]{2,1,0:T(8,128)(2,1)}, bf16[2,192,256]{2,1,0:T(8,128)(2,1)}) custom-call(s32[24]{0:T(128)} %stack.153.m, bf16[2,192,1408]{2,1,0:T(8,128)(2,1)} %copy-done.12, bf16[2,192,1408]{2,1,0:T(8,128)(2,1)} %collective-permute-done.48.refs_1_.refs_3_, bf16[2,192,1408]{2,1,0:T(8,128)(2,1)} %collective-permute-done.46.refs_2_.refs_6_, ...), custom_call_target="tpu_custom_call" | custom-call | flops 4429185024 | bytes 16302080 | tf_op jit(solution)/shard_map/dx/pallas_call | solution.py:61
  381.6 5.3 collective-permute-done.50
  393.8 11.3 %dwin.2 = (bf16[4,256,1408]{2,1,0:T(8,128)(2,1)}, bf16[4,256,1408]{2,1,0:T(8,128)(2,1)}) custom-call(s32[24]{0:T(128)} %stack.153.m, bf16[2,192,1408]{2,1,0:T(8,128)(2,1)} %get-tuple-element.224.refs_0_, bf16[2,192,1408]{2,1,0:T(8,128)(2,1)} %copy-done.11, bf16[2,192,1408]{2,1,0:T(8,128)(2,1)} %copy-done.12, ...), custom_call_target="tpu_custom_call" | custom-call | flops 4429185024 | bytes 15228928 | tf_op jit(solution)/shard_map/dwin/pallas_call | solution.py:61
  413.6 6.5 %norm_back.1 = (f32[2,768,256]{2,1,0:T(8,128)}, bf16[2,768,256]{2,1,0:T(8,128)(2,1)}, f32[5,2,256]{2,1,0:T(2,128)}) custom-call(s32[24]{0:T(128)} %stack.153.m, bf16[2,192,256]{2,1,0:T(8,128)(2,1)} %copy-done.27, bf16[2,192,256]{2,1,0:T(8,128)(2,1)} %copy-done.55, bf16[2,192,256]{2,1,0:T(8,128)(2,1)} %copy-done.28, bf16[2,192,256]{2,1,0:T(8,128)(2,1)} %copy-done.56, ...), custom_call_target="tpu_custom_call" | custom-call | bytes 5550080 | tf_op jit(solution)/shard_map/norm_back/pallas_call | solution.py:61
  420.1 6.1 dmix.1
  430.4 11.4 %dwin.3 = (bf16[4,256,1408]{2,1,0:T(8,128)(2,1)}, bf16[4,256,1408]{2,1,0:T(8,128)(2,1)}) custom-call(s32[24]{0:T(128)} %stack.153.m, bf16[2,192,1408]{2,1,0:T(8,128)(2,1)} %get-tuple-element.224.refs_0_, bf16[2,192,1408]{2,1,0:T(8,128)(2,1)} %copy-done.11, bf16[2,192,1408]{2,1,0:T(8,128)(2,1)} %copy-done.12, ...), custom_call_target="tpu_custom_call" | custom-call | flops 4429185024 | bytes 15228928 | tf_op jit(solution)/shard_map/dwin/pallas_call | solution.py:61
  442.9 4.8 collective-permute-done.70.refs_9_
  449.8 14.4 %attend_back.1 = (bf16[768,256]{1,0:T(8,128)(2,1)}, f32[768,256]{1,0:T(8,128)}, f32[256,256]{1,0:T(8,128)}, f32[8,768]{1,0:T(8,128)}) custom-call(s32[24]{0:T(128)} %stack.153.m, bf16[768,256]{1,0:T(8,128)(2,1)} %get-tuple-element.180.q_ref.refs_0_, bf16[768,256]{1,0:T(8,128)(2,1)} %get-tuple-element.181.kv_ref.refs_1_, bf16[256,256]{1,0:T(8,128)(2,1)} %copy-done.37, ...), custom_call_target="tpu_custom_call" | custom-call | flops 754974720 | bytes 4792320 | tf_op jit(solution)/shard_map/attend_back/pallas_call | solution.py:61
  469.2 3.6 dkv.1
  475.0 16.2 %down.1 = (bf16[2,384,256]{2,1,0:T(8,128)(2,1)}, bf16[2,384,256]{2,1,0:T(8,128)(2,1)}, bf16[4,1408,256]{2,1,0:T(8,128)(2,1)}, bf16[4,1408,256]{2,1,0:T(8,128)(2,1)}) custom-call(s32[24]{0:T(128)} %stack.153.m, bf16[192,1408]{1,0:T(8,128)(2,1)} %get-tuple-element.235.refs_0_, bf16[192,1408]{1,0:T(8,128)(2,1)} %copy-done.97, bf16[192,1408]{1,0:T(8,128)(2,1)} %copy-done.96, ...), custom_call_target="tpu_custom_call" | custom-call | flops 8858370048 | bytes 17457152 | tf_op jit(solution)/shard_map/down/pallas_call | solution.py:61
  495.6 7.5 %dwproj.1 = (bf16[4,512,256]{2,1,0:T(8,128)(2,1)}, bf16[4,512,256]{2,1,0:T(8,128)(2,1)}) custom-call(s32[24]{0:T(128)} %stack.153.m, bf16[768,128]{1,0:T(8,128)(2,1)} %get-tuple-element.189.refs_0_, bf16[768,128]{1,0:T(8,128)(2,1)} %copy-done.21, bf16[768,128]{1,0:T(8,128)(2,1)} %copy-done.23, bf16[768,128]{1,0:T(8,128)(2,1)} %copy-done.25, ...), custom_call_target="tpu_custom_call" | custom-call | flops 1610612736 | bytes 4481024 | tf_op jit(solution)/shard_map/dwproj/pallas_call | solution.py:61
  503.2 2.9 collective-permute-start.85
  508.1 7.6 %dattn.1 = (bf16[2,384,256]{2,1,0:T(8,128)(2,1)}, bf16[2,384,256]{2,1,0:T(8,128)(2,1)}) custom-call(s32[24]{0:T(128)} %stack.153.m, bf16[768,256]{1,0:T(8,128)(2,1)} %get-tuple-element.262.refs_0_, bf16[768,256]{1,0:T(8,128)(2,1)} %copy-done.105, bf16[768,256]{1,0:T(8,128)(2,1)} %copy-done.104, bf16[768,256]{1,0:T(8,128)(2,1)} %collective-permute-done.79.refs_3_, ...), custom_call_target="tpu_custom_call" | custom-call | flops 2415919104 | bytes 7102464 | tf_op jit(solution)/shard_map/dattn/pallas_call | solution.py:61
  517.6 7.4 %collective-permute-start.86 = (bf16[2,384,256]{2,1,0:T(8,128)(2,1)S(1)}, bf16[2,384,256]{2,1,0:T(8,128)(2,1)S(1)}, u32[]{:S(2)}, u32[]{:S(2)}) collective-permute-start(bf16[2,384,256]{2,1,0:T(8,128)(2,1)S(1)} %add_convert_fusion.6.refs_0_), channel_id=1, source_target_pairs={{0,1},{1,0},{2,3},{3,2},{4,5},{5,4},{6,7},{7,6},{8,9},{9,8},{10,11... | collective-permute-start | bytes 1179656 | tf_op jit(solution)/shard_map/ppermute | solution.py:176
  526.3 8.6 %collective-permute-done.86.refs_1_ = bf16[2,384,256]{2,1,0:T(8,128)(2,1)S(1)} collective-permute-done((bf16[2,384,256]{2,1,0:T(8,128)(2,1)S(1)}, bf16[2,384,256]{2,1,0:T(8,128)(2,1)S(1)}, u32[]{:S(2)}, u32[]{:S(2)}) %collective-permute-start.86) | collective-permute-done | bytes 393248 | tf_op jit(solution)/shard_map/ppermute | solution.py:176
  537.2 4.4 collective-permute-done.93
  544.3 9.4 %dwqkv.1 = (bf16[4,256,512]{2,1,0:T(8,128)(2,1)}, bf16[4,256,512]{2,1,0:T(8,128)(2,1)}, bf16[2,256,512]{2,1,0:T(8,128)(2,1)}, bf16[2,256,512]{2,1,0:T(8,128)(2,1)}) custom-call(s32[24]{0:T(128)} %stack.153.m, bf16[768,256]{1,0:T(8,128)(2,1)} %get-tuple-element.262.refs_0_, bf16[768,256]{1,0:T(8,128)(2,1)} %copy-done.105, bf16[768,256]{1,0:T(8,128)(2,1)} %copy-done.104, ...), custom_call_target="tpu_custom_call" | custom-call | flops 2415919104 | bytes 7102464 | tf_op jit(solution)/shard_map/dwqkv/pallas_call | solution.py:61
  553.8 3.4 finish.1
  557.7 3.4 collective-permute-done.88
  562.8 8.4 %collective-permute-done.94 = bf16[2,384,256]{2,1,0:T(8,128)(2,1)S(1)} collective-permute-done((bf16[2,384,256]{2,1,0:T(8,128)(2,1)S(1)}, bf16[2,384,256]{2,1,0:T(8,128)(2,1)S(1)}, u32[]{:S(2)}, u32[]{:S(2)}) %collective-permute-start.94) | collective-permute-done | bytes 393248 | tf_op jit(solution)/shard_map/ppermute | solution.py:176
  572.0 4.4 unpack.2
  576.4 3.9 all-to-all-start.2
  582.7 8.3 %collective-permute-start.95 = (bf16[2,384,256]{2,1,0:T(8,128)(2,1)S(1)}, bf16[2,384,256]{2,1,0:T(8,128)(2,1)S(1)}, u32[]{:S(2)}, u32[]{:S(2)}) collective-permute-start(bf16[2,384,256]{2,1,0:T(8,128)(2,1)S(1)} %add_convert_fusion.4.refs_0_), channel_id=1, source_target_pairs={{0,1},{1,0},{2,3},{3,2},{4,5},{5,4},{6,7},{7,6},{8,9},{9,8},{10,11... | collective-permute-start | bytes 1179656 | tf_op jit(solution)/shard_map/ppermute | solution.py:176
  594.4 10.4 %fold.1 = f32[4,256,2,1408]{3,2,1,0:T(2,128)} custom-call(s32[24]{0:T(128)} %stack.153.m, bf16[4,256,1408]{2,1,0:T(8,128)(2,1)} %get-tuple-element.233.refs_0_, bf16[4,256,1408]{2,1,0:T(8,128)(2,1)} %collective-permute-done.91.refs_1_, bf16[4,256,1408]{2,1,0:T(8,128)(2,1)} %get-tuple-element.256.refs_2_, bf16[4,256,1408]{2,1,0:T(8,128)(2,1)} %collective-permute-done.92.refs_3_), custom_call_target="tpu_custom_call" | custom-call | bytes 23068672 | tf_op jit(solution)/shard_map/fold/pallas_call | solution.py:61
  605.5 5.9 norm_back_first.1
  616.8 4.5 unpack.3
  621.3 4.1 all-to-all-start.3
  627.9 4.9 convert_add_fusion
  632.8 9.3 %all-to-all-done.3 = bf16[8,288,256]{2,1,0:T(8,128)(2,1)S(1)} async-done(((bf16[8,288,256]{2,1,0:T(8,128)(2,1)}), bf16[8,288,256]{2,1,0:T(8,128)(2,1)S(1)}, u32[]{:S(2)}, u32[]{:S(2)}) %all-to-all-start.3) | async-done | bytes 1179680 | tf_op jit(solution)/shard_map/all_to_all | solution.py:1206
  (523 shorter events, 171.4 us)
Async XLA Ops:
  0.6 36.8 %collective-permute-start.2 = (bf16[2,256,512]{2,1,0:T(8,128)(2,1)}, bf16[2,256,512]{2,1,0:T(8,128)(2,1)}, u32[]{:S(2)}, u32[]{:S(2)}) collective-permute-start(bf16[2,256,512]{2,1,0:T(8,128)(2,1)} %refs_11_.3), channel_id=1, source_target_pairs={{0,4},{4,0},{8,12},{12,8},{16,20},{20,16},{24,28},{28,24},{1,5},{5... | collective-permute-start | bytes 1572872 | tf_op jit(solution)/shard_map/ppermute | solution.py:165
  3.9 20.2 %all-to-all-start = ((bf16[8,256,256]{2,1,0:T(8,128)(2,1)}), bf16[8,256,256]{2,1,0:T(8,128)(2,1)S(1)}, u32[]{:S(2)}, u32[]{:S(2)}) async-start(bf16[8,256,256]{2,1,0:T(8,128)(2,1)} %bitcast.101), calls=%async_computation | async-start | bytes 2097152 | tf_op jit(solution)/shard_map/all_to_all | solution.py:306
  8.8 28.6 %collective-permute-start.1 = (bf16[4,256,512]{2,1,0:T(8,128)(2,1)}, bf16[4,256,512]{2,1,0:T(8,128)(2,1)}, u32[]{:S(2)}, u32[]{:S(2)}) collective-permute-start(bf16[4,256,512]{2,1,0:T(8,128)(2,1)} %refs_9_.5), channel_id=1, source_target_pairs={{0,4},{4,0},{8,12},{12,8},{16,20},{20,16},{24,28},{28,24},{1,5},{5... | collective-permute-start | bytes 3145736 | tf_op jit(solution)/shard_map/ppermute | solution.py:165
  9.4 81.3 %collective-permute-start.4 = (bf16[4,1408,256]{2,1,0:T(8,128)(2,1)}, bf16[4,1408,256]{2,1,0:T(8,128)(2,1)}, u32[]{:S(2)}, u32[]{:S(2)}) collective-permute-start(bf16[4,1408,256]{2,1,0:T(8,128)(2,1)} %refs_11_.2), channel_id=1, source_target_pairs={{0,4},{4,0},{8,12},{12,8},{16,20},{20,16},{24,28},{28,24},{1,5},{5... | collective-permute-start | bytes 8650760 | tf_op jit(solution)/shard_map/ppermute | solution.py:165
  15.4 186.5 %collective-permute-start.34 = (bf16[4,2,256,1408]{3,2,1,0:T(8,128)(2,1)}, bf16[4,2,256,1408]{3,2,1,0:T(8,128)(2,1)}, u32[]{:S(2)}, u32[]{:S(2)}) collective-permute-start(bf16[4,2,256,1408]{3,2,1,0:T(8,128)(2,1)} %bitcast.99.refs_2_.refs_4_), channel_id=1, source_target_pairs={{0,4},{4,0},{8,12},{12,8},{16,20},{20,16},{24,28},{28,24},{1,5},{5... | collective-permute-start | bytes 17301512 | tf_op jit(solution)/shard_map/ppermute | solution.py:165
  24.1 27.3 %all-to-all-start.1 = ((bf16[8,256,256]{2,1,0:T(8,128)(2,1)}), bf16[8,256,256]{2,1,0:T(8,128)(2,1)S(1)}, u32[]{:S(2)}, u32[]{:S(2)}) async-start(bf16[8,256,256]{2,1,0:T(8,128)(2,1)} %bitcast.100), calls=%async_computation.1 | async-start | bytes 2097152 | tf_op jit(solution)/shard_map/all_to_all | solution.py:308
  58.1 17.6 %collective-permute-start.6 = (bf16[768,256]{1,0:T(8,128)(2,1)}, bf16[768,256]{1,0:T(8,128)(2,1)S(1)}, u32[]{:S(2)}, u32[]{:S(2)}) collective-permute-start(bf16[768,256]{1,0:T(8,128)(2,1)} %get-tuple-element.173), channel_id=1, source_target_pairs={{0,8},{4,12},{8,0},{12,4},{16,24},{20,28},{24,16},{28,20},{1,9},{5... | collective-permute-start | bytes 1179656 | tf_op jit(solution)/shard_map/ppermute | solution.py:161
  58.5 17.2 %collective-permute-start.7 = (bf16[768,256]{1,0:T(8,128)(2,1)}, bf16[768,256]{1,0:T(8,128)(2,1)S(1)}, u32[]{:S(2)}, u32[]{:S(2)}) collective-permute-start(bf16[768,256]{1,0:T(8,128)(2,1)} %get-tuple-element.175), channel_id=1, source_target_pairs={{0,16},{4,20},{8,24},{12,28},{16,0},{20,4},{24,8},{28,12},{1,17},{... | collective-permute-start | bytes 1179656 | tf_op jit(solution)/shard_map/ppermute | solution.py:161
  68.7 54.3 %collective-permute-start.27 = (bf16[4,512,256]{2,1,0:T(8,128)(2,1)S(1)}, bf16[4,512,256]{2,1,0:T(8,128)(2,1)S(1)}, u32[]{:S(2)}, u32[]{:S(2)}) collective-permute-start(bf16[4,512,256]{2,1,0:T(8,128)(2,1)S(1)} %copy-done.3), channel_id=1, source_target_pairs={{0,4},{4,0},{8,12},{12,8},{16,20},{20,16},{24,28},{28,24},{1,5},{5... | collective-permute-start | bytes 3145736 | tf_op jit(solution)/shard_map/ppermute | solution.py:165
  87.4 15.3 %collective-permute-start.12 = (bf16[768,256]{1,0:T(8,128)(2,1)}, bf16[768,256]{1,0:T(8,128)(2,1)S(1)}, u32[]{:S(2)}, u32[]{:S(2)}) collective-permute-start(bf16[768,256]{1,0:T(8,128)(2,1)} %add_convert_fusion.9), channel_id=1, source_target_pairs={{0,16},{4,20},{8,24},{12,28},{16,0},{20,4},{24,8},{28,12},{1,17},{... | collective-permute-start | bytes 1179656 | tf_op jit(solution)/shard_map/ppermute | solution.py:161
  146.2 26.6 %collective-permute-start.19 = (bf16[192,1408]{1,0:T(8,128)(2,1)}, bf16[192,1408]{1,0:T(8,128)(2,1)S(1)}, u32[]{:S(2)}, u32[]{:S(2)}) collective-permute-start(bf16[192,1408]{1,0:T(8,128)(2,1)} %get-tuple-element.192), channel_id=1, source_target_pairs={{0,8},{4,12},{8,0},{12,4},{16,24},{20,28},{24,16},{28,20},{1,9},{5... | collective-permute-start | bytes 1622024 | tf_op jit(solution)/shard_map/ppermute | solution.py:161
  160.3 16.2 %collective-permute-start.20 = (bf16[192,1408]{1,0:T(8,128)(2,1)S(1)}, bf16[192,1408]{1,0:T(8,128)(2,1)S(1)}, u32[]{:S(2)}, u32[]{:S(2)}) collective-permute-start(bf16[192,1408]{1,0:T(8,128)(2,1)S(1)} %copy-done.100), channel_id=1, source_target_pairs={{0,16},{4,20},{8,24},{12,28},{16,0},{20,4},{24,8},{28,12},{1,17},{... | collective-permute-start | bytes 1622024 | tf_op jit(solution)/shard_map/ppermute | solution.py:161
  160.9 15.8 %collective-permute-start.21 = (bf16[192,1408]{1,0:T(8,128)(2,1)S(1)}, bf16[192,1408]{1,0:T(8,128)(2,1)S(1)}, u32[]{:S(2)}, u32[]{:S(2)}) collective-permute-start(bf16[192,1408]{1,0:T(8,128)(2,1)S(1)} %copy-done.99), channel_id=1, source_target_pairs={{0,8},{4,12},{8,0},{12,4},{16,24},{20,28},{24,16},{28,20},{1,9},{5... | collective-permute-start | bytes 1622024 | tf_op jit(solution)/shard_map/ppermute | solution.py:161
  172.7 18.2 %collective-permute-start.32 = (bf16[2,192,256]{2,1,0:T(8,128)(2,1)S(1)}, bf16[2,192,256]{2,1,0:T(8,128)(2,1)S(1)}, u32[]{:S(2)}, u32[]{:S(2)}) collective-permute-start(bf16[2,192,256]{2,1,0:T(8,128)(2,1)S(1)} %add_convert_fusion.17), channel_id=1, source_target_pairs={{0,3},{1,2},{2,1},{3,0},{4,7},{5,6},{6,5},{7,4},{8,11},{9,10},{10,... | collective-permute-start | bytes 589832 | tf_op jit(solution)/shard_map/ppermute | solution.py:176
  184.6 17.2 %collective-permute-start.23 = (bf16[192,1408]{1,0:T(8,128)(2,1)S(1)}, bf16[192,1408]{1,0:T(8,128)(2,1)S(1)}, u32[]{:S(2)}, u32[]{:S(2)}) collective-permute-start(bf16[192,1408]{1,0:T(8,128)(2,1)S(1)} %add_convert_fusion.3), channel_id=1, source_target_pairs={{0,16},{4,20},{8,24},{12,28},{16,0},{20,4},{24,8},{28,12},{1,17},{... | collective-permute-start | bytes 1622024 | tf_op jit(solution)/shard_map/ppermute | solution.py:161
  185.2 16.6 %collective-permute-start.24 = (bf16[192,1408]{1,0:T(8,128)(2,1)S(1)}, bf16[192,1408]{1,0:T(8,128)(2,1)S(1)}, u32[]{:S(2)}, u32[]{:S(2)}) collective-permute-start(bf16[192,1408]{1,0:T(8,128)(2,1)S(1)} %add_convert_fusion.2), channel_id=1, source_target_pairs={{0,8},{4,12},{8,0},{12,4},{16,24},{20,28},{24,16},{28,20},{1,9},{5... | collective-permute-start | bytes 1622024 | tf_op jit(solution)/shard_map/ppermute | solution.py:161
  212.0 27.1 %collective-permute-start.37 = (bf16[2,192,1408]{2,1,0:T(8,128)(2,1)}, bf16[2,192,1408]{2,1,0:T(8,128)(2,1)}, u32[]{:S(2)}, u32[]{:S(2)}) collective-permute-start(bf16[2,192,1408]{2,1,0:T(8,128)(2,1)} %get-tuple-element.215), channel_id=1, source_target_pairs={{0,16},{4,20},{8,24},{12,28},{16,0},{20,4},{24,8},{28,12},{1,17},{... | collective-permute-start | bytes 3244040 | tf_op jit(solution)/shard_map/ppermute | solution.py:161
  214.1 27.6 %collective-permute-start.36 = (bf16[2,192,1408]{2,1,0:T(8,128)(2,1)}, bf16[2,192,1408]{2,1,0:T(8,128)(2,1)}, u32[]{:S(2)}, u32[]{:S(2)}) collective-permute-start(bf16[2,192,1408]{2,1,0:T(8,128)(2,1)} %get-tuple-element.209), channel_id=1, source_target_pairs={{0,8},{4,12},{8,0},{12,4},{16,24},{20,28},{24,16},{28,20},{1,9},{5... | collective-permute-start | bytes 3244040 | tf_op jit(solution)/shard_map/ppermute | solution.py:161
  214.8 45.8 %collective-permute-start.35 = (bf16[2,192,1408]{2,1,0:T(8,128)(2,1)}, bf16[2,192,1408]{2,1,0:T(8,128)(2,1)S(1)}, u32[]{:S(2)}, u32[]{:S(2)}) collective-permute-start(bf16[2,192,1408]{2,1,0:T(8,128)(2,1)} %get-tuple-element.212), channel_id=1, source_target_pairs={{0,8},{4,12},{8,0},{12,4},{16,24},{20,28},{24,16},{28,20},{1,9},{5... | collective-permute-start | bytes 3244040 | tf_op jit(solution)/shard_map/ppermute | solution.py:161
  226.4 34.1 %collective-permute-start.38 = (bf16[2,192,1408]{2,1,0:T(8,128)(2,1)}, bf16[2,192,1408]{2,1,0:T(8,128)(2,1)S(1)}, u32[]{:S(2)}, u32[]{:S(2)}) collective-permute-start(bf16[2,192,1408]{2,1,0:T(8,128)(2,1)} %get-tuple-element.216), channel_id=1, source_target_pairs={{0,16},{4,20},{8,24},{12,28},{16,0},{20,4},{24,8},{28,12},{1,17},{... | collective-permute-start | bytes 3244040 | tf_op jit(solution)/shard_map/ppermute | solution.py:161
  260.6 20.0 %collective-permute-start.39 = (bf16[2,192,1408]{2,1,0:T(8,128)(2,1)}, bf16[2,192,1408]{2,1,0:T(8,128)(2,1)}, u32[]{:S(2)}, u32[]{:S(2)}) collective-permute-start(bf16[2,192,1408]{2,1,0:T(8,128)(2,1)} %add_convert_fusion.1), channel_id=1, source_target_pairs={{0,16},{4,20},{8,24},{12,28},{16,0},{20,4},{24,8},{28,12},{1,17},{... | collective-permute-start | bytes 3244040 | tf_op jit(solution)/shard_map/ppermute | solution.py:161
  260.8 19.8 %collective-permute-start.40 = (bf16[2,192,1408]{2,1,0:T(8,128)(2,1)}, bf16[2,192,1408]{2,1,0:T(8,128)(2,1)}, u32[]{:S(2)}, u32[]{:S(2)}) collective-permute-start(bf16[2,192,1408]{2,1,0:T(8,128)(2,1)} %add_convert_fusion), channel_id=1, source_target_pairs={{0,8},{4,12},{8,0},{12,4},{16,24},{20,28},{24,16},{28,20},{1,9},{5... | collective-permute-start | bytes 3244040 | tf_op jit(solution)/shard_map/ppermute | solution.py:161
  261.5 17.7 %collective-permute-start.43 = (f32[8,768]{1,0:T(8,128)S(1)}, f32[8,768]{1,0:T(8,128)S(1)}, u32[]{:S(2)}, u32[]{:S(2)}) collective-permute-start(f32[8,768]{1,0:T(8,128)S(1)} %copy-done.78), channel_id=1, source_target_pairs={{0,24},{4,28},{8,16},{12,20},{16,8},{20,12},{24,0},{28,4},{1,25},{... | collective-permute-start | bytes 73736 | tf_op jit(solution)/shard_map/ppermute | solution.py:161
  264.1 15.1 %collective-permute-start.42 = (f32[8,768]{1,0:T(8,128)S(1)}, f32[8,768]{1,0:T(8,128)S(1)}, u32[]{:S(2)}, u32[]{:S(2)}) collective-permute-start(f32[8,768]{1,0:T(8,128)S(1)} %copy-done.78), channel_id=1, source_target_pairs={{0,16},{4,20},{8,24},{12,28},{16,0},{20,4},{24,8},{28,12},{1,17},{... | collective-permute-start | bytes 73736 | tf_op jit(solution)/shard_map/ppermute | solution.py:161
  264.3 15.2 %collective-permute-start.41 = (f32[8,768]{1,0:T(8,128)S(1)}, f32[8,768]{1,0:T(8,128)S(1)}, u32[]{:S(2)}, u32[]{:S(2)}) collective-permute-start(f32[8,768]{1,0:T(8,128)S(1)} %copy-done.78), channel_id=1, source_target_pairs={{0,8},{4,12},{8,0},{12,4},{16,24},{20,28},{24,16},{28,20},{1,9},{5... | collective-permute-start | bytes 73736 | tf_op jit(solution)/shard_map/ppermute | solution.py:161
  288.9 27.0 %collective-permute-start.45 = (bf16[2,192,1408]{2,1,0:T(8,128)(2,1)}, bf16[2,192,1408]{2,1,0:T(8,128)(2,1)S(1)}, u32[]{:S(2)}, u32[]{:S(2)}) collective-permute-start(bf16[2,192,1408]{2,1,0:T(8,128)(2,1)} %get-tuple-element.224.refs_0_), channel_id=1, source_target_pairs={{0,8},{4,12},{8,0},{12,4},{16,24},{20,28},{24,16},{28,20},{1,9},{5... | collective-permute-start | bytes 3244040 | tf_op jit(solution)/shard_map/ppermute | solution.py:161
  289.7 26.9 %collective-permute-start.44 = (bf16[2,192,1408]{2,1,0:T(8,128)(2,1)}, bf16[2,192,1408]{2,1,0:T(8,128)(2,1)S(1)}, u32[]{:S(2)}, u32[]{:S(2)}) collective-permute-start(bf16[2,192,1408]{2,1,0:T(8,128)(2,1)} %get-tuple-element.224.refs_0_), channel_id=1, source_target_pairs={{0,16},{4,20},{8,24},{12,28},{16,0},{20,4},{24,8},{28,12},{1,17},{... | collective-permute-start | bytes 3244040 | tf_op jit(solution)/shard_map/ppermute | solution.py:161
  290.9 44.2 %collective-permute-start.47 = (bf16[2,192,1408]{2,1,0:T(8,128)(2,1)}, bf16[2,192,1408]{2,1,0:T(8,128)(2,1)S(1)}, u32[]{:S(2)}, u32[]{:S(2)}) collective-permute-start(bf16[2,192,1408]{2,1,0:T(8,128)(2,1)} %get-tuple-element.225.refs_4_.refs_2_), channel_id=1, source_target_pairs={{0,8},{4,12},{8,0},{12,4},{16,24},{20,28},{24,16},{28,20},{1,9},{5... | collective-permute-start | bytes 3244040 | tf_op jit(solution)/shard_map/ppermute | solution.py:161
  292.2 43.9 %collective-permute-start.46 = (bf16[2,192,1408]{2,1,0:T(8,128)(2,1)}, bf16[2,192,1408]{2,1,0:T(8,128)(2,1)}, u32[]{:S(2)}, u32[]{:S(2)}) collective-permute-start(bf16[2,192,1408]{2,1,0:T(8,128)(2,1)} %get-tuple-element.225.refs_4_.refs_2_), channel_id=1, source_target_pairs={{0,16},{4,20},{8,24},{12,28},{16,0},{20,4},{24,8},{28,12},{1,17},{... | collective-permute-start | bytes 3244040 | tf_op jit(solution)/shard_map/ppermute | solution.py:161
  336.1 26.9 %collective-permute-start.48 = (bf16[2,192,1408]{2,1,0:T(8,128)(2,1)S(1)}, bf16[2,192,1408]{2,1,0:T(8,128)(2,1)}, u32[]{:S(2)}, u32[]{:S(2)}) collective-permute-start(bf16[2,192,1408]{2,1,0:T(8,128)(2,1)S(1)} %collective-permute-done.45.refs_1_), channel_id=1, source_target_pairs={{0,16},{4,20},{8,24},{12,28},{16,0},{20,4},{24,8},{28,12},{1,17},{... | collective-permute-start | bytes 3244040 | tf_op jit(solution)/shard_map/ppermute | solution.py:161
  336.9 26.1 %collective-permute-start.49 = (bf16[2,192,1408]{2,1,0:T(8,128)(2,1)}, bf16[2,192,1408]{2,1,0:T(8,128)(2,1)}, u32[]{:S(2)}, u32[]{:S(2)}) collective-permute-start(bf16[2,192,1408]{2,1,0:T(8,128)(2,1)} %collective-permute-done.46.refs_2_.refs_6_), channel_id=1, source_target_pairs={{0,8},{4,12},{8,0},{12,4},{16,24},{20,28},{24,16},{28,20},{1,9},{5... | collective-permute-start | bytes 3244040 | tf_op jit(solution)/shard_map/ppermute | solution.py:161
  340.2 14.6 %collective-permute-start.61 = (f32[8,192]{0,1:T(8,128)S(1)}, f32[8,192]{0,1:T(8,128)S(1)}, u32[]{:S(2)}, u32[]{:S(2)}) collective-permute-start(f32[8,192]{0,1:T(8,128)S(1)} %bitcast.127), channel_id=1, source_target_pairs={{0,2},{1,3},{2,0},{3,1},{4,6},{5,7},{6,4},{7,5},{8,10},{9,11},{10,... | collective-permute-start | bytes 18440 | tf_op jit(solution)/shard_map/ppermute | solution.py:176
  340.9 15.9 %collective-permute-start.62 = (f32[8,192]{0,1:T(8,128)S(1)}, f32[8,192]{0,1:T(8,128)S(1)}, u32[]{:S(2)}, u32[]{:S(2)}) collective-permute-start(f32[8,192]{0,1:T(8,128)S(1)} %bitcast.128), channel_id=1, source_target_pairs={{0,3},{1,2},{2,1},{3,0},{4,7},{5,6},{6,5},{7,4},{8,11},{9,10},{10,... | collective-permute-start | bytes 18440 | tf_op jit(solution)/shard_map/ppermute | solution.py:176
  362.3 16.5 %collective-permute-start.56 = (bf16[2,192,256]{2,1,0:T(8,128)(2,1)S(1)}, bf16[2,192,256]{2,1,0:T(8,128)(2,1)S(1)}, u32[]{:S(2)}, u32[]{:S(2)}) collective-permute-start(bf16[2,192,256]{2,1,0:T(8,128)(2,1)S(1)} %add_convert_fusion.14), channel_id=1, source_target_pairs={{0,3},{1,2},{2,1},{3,0},{4,7},{5,6},{6,5},{7,4},{8,11},{9,10},{10,... | collective-permute-start | bytes 589832 | tf_op jit(solution)/shard_map/ppermute | solution.py:176
  363.1 17.4 %collective-permute-start.65 = (f32[8,192]{0,1:T(8,128)S(1)}, f32[8,192]{0,1:T(8,128)S(1)}, u32[]{:S(2)}, u32[]{:S(2)}) collective-permute-start(f32[8,192]{0,1:T(8,128)S(1)} %add_add_fusion), channel_id=1, source_target_pairs={{0,24},{4,28},{8,16},{12,20},{16,8},{20,12},{24,0},{28,4},{1,25},{... | collective-permute-start | bytes 18440 | tf_op jit(solution)/shard_map/ppermute | solution.py:161
  364.2 16.3 %collective-permute-start.64 = (f32[8,192]{0,1:T(8,128)S(1)}, f32[8,192]{0,1:T(8,128)S(1)}, u32[]{:S(2)}, u32[]{:S(2)}) collective-permute-start(f32[8,192]{0,1:T(8,128)S(1)} %add_add_fusion), channel_id=1, source_target_pairs={{0,16},{4,20},{8,24},{12,28},{16,0},{20,4},{24,8},{28,12},{1,17},{... | collective-permute-start | bytes 18440 | tf_op jit(solution)/shard_map/ppermute | solution.py:161
  366.7 13.9 %collective-permute-start.63 = (f32[8,192]{0,1:T(8,128)S(1)}, f32[8,192]{0,1:T(8,128)S(1)}, u32[]{:S(2)}, u32[]{:S(2)}) collective-permute-start(f32[8,192]{0,1:T(8,128)S(1)} %add_add_fusion), channel_id=1, source_target_pairs={{0,8},{4,12},{8,0},{12,4},{16,24},{20,28},{24,16},{28,20},{1,9},{5... | collective-permute-start | bytes 18440 | tf_op jit(solution)/shard_map/ppermute | solution.py:161
  387.8 17.3 %collective-permute-start.58 = (bf16[2,192,256]{2,1,0:T(8,128)(2,1)S(1)}, bf16[2,192,256]{2,1,0:T(8,128)(2,1)S(1)}, u32[]{:S(2)}, u32[]{:S(2)}) collective-permute-start(bf16[2,192,256]{2,1,0:T(8,128)(2,1)S(1)} %add_convert_fusion.15), channel_id=1, source_target_pairs={{0,3},{1,2},{2,1},{3,0},{4,7},{5,6},{6,5},{7,4},{8,11},{9,10},{10,... | collective-permute-start | bytes 589832 | tf_op jit(solution)/shard_map/ppermute | solution.py:176
  389.8 16.0 %collective-permute-start.52 = (bf16[192,1408]{1,0:T(8,128)(2,1)S(1)}, bf16[192,1408]{1,0:T(8,128)(2,1)S(1)}, u32[]{:S(2)}, u32[]{:S(2)}) collective-permute-start(bf16[192,1408]{1,0:T(8,128)(2,1)S(1)} %copy-done.94), channel_id=1, source_target_pairs={{0,16},{4,20},{8,24},{12,28},{16,0},{20,4},{24,8},{28,12},{1,17},{... | collective-permute-start | bytes 1622024 | tf_op jit(solution)/shard_map/ppermute | solution.py:161
  390.6 17.7 %collective-permute-start.51 = (bf16[192,1408]{1,0:T(8,128)(2,1)S(1)}, bf16[192,1408]{1,0:T(8,128)(2,1)S(1)}, u32[]{:S(2)}, u32[]{:S(2)}) collective-permute-start(bf16[192,1408]{1,0:T(8,128)(2,1)S(1)} %copy-done.94), channel_id=1, source_target_pairs={{0,8},{4,12},{8,0},{12,4},{16,24},{20,28},{24,16},{28,20},{1,9},{5... | collective-permute-start | bytes 1622024 | tf_op jit(solution)/shard_map/ppermute | solution.py:161
  390.6 17.7 %collective-permute-start.54 = (bf16[192,1408]{1,0:T(8,128)(2,1)S(1)}, bf16[192,1408]{1,0:T(8,128)(2,1)}, u32[]{:S(2)}, u32[]{:S(2)}) collective-permute-start(bf16[192,1408]{1,0:T(8,128)(2,1)S(1)} %copy-done.95), channel_id=1, source_target_pairs={{0,16},{4,20},{8,24},{12,28},{16,0},{20,4},{24,8},{28,12},{1,17},{... | collective-permute-start | bytes 1622024 | tf_op jit(solution)/shard_map/ppermute | solution.py:161
  391.8 16.5 %collective-permute-start.53 = (bf16[192,1408]{1,0:T(8,128)(2,1)S(1)}, bf16[192,1408]{1,0:T(8,128)(2,1)}, u32[]{:S(2)}, u32[]{:S(2)}) collective-permute-start(bf16[192,1408]{1,0:T(8,128)(2,1)S(1)} %copy-done.95), channel_id=1, source_target_pairs={{0,8},{4,12},{8,0},{12,4},{16,24},{20,28},{24,16},{28,20},{1,9},{5... | collective-permute-start | bytes 1622024 | tf_op jit(solution)/shard_map/ppermute | solution.py:161
  426.3 15.6 %collective-permute-start.66 = (bf16[768,128]{1,0:T(8,128)(2,1)}, bf16[768,128]{1,0:T(8,128)(2,1)S(1)}, u32[]{:S(2)}, u32[]{:S(2)}) collective-permute-start(bf16[768,128]{1,0:T(8,128)(2,1)} %get-tuple-element.249), channel_id=1, source_target_pairs={{0,8},{4,12},{8,0},{12,4},{16,24},{20,28},{24,16},{28,20},{1,9},{5... | collective-permute-start | bytes 589832 | tf_op jit(solution)/shard_map/ppermute | solution.py:161
  426.4 15.4 %collective-permute-start.67 = (bf16[768,128]{1,0:T(8,128)(2,1)}, bf16[768,128]{1,0:T(8,128)(2,1)S(1)}, u32[]{:S(2)}, u32[]{:S(2)}) collective-permute-start(bf16[768,128]{1,0:T(8,128)(2,1)} %get-tuple-element.251), channel_id=1, source_target_pairs={{0,8},{4,12},{8,0},{12,4},{16,24},{20,28},{24,16},{28,20},{1,9},{5... | collective-permute-start | bytes 589832 | tf_op jit(solution)/shard_map/ppermute | solution.py:161
  448.5 19.9 %collective-permute-start.73 = (bf16[192,1408]{1,0:T(8,128)(2,1)S(1)}, bf16[192,1408]{1,0:T(8,128)(2,1)S(1)}, u32[]{:S(2)}, u32[]{:S(2)}) collective-permute-start(bf16[192,1408]{1,0:T(8,128)(2,1)S(1)} %collective-permute-done.51.refs_1_), channel_id=1, source_target_pairs={{0,16},{4,20},{8,24},{12,28},{16,0},{20,4},{24,8},{28,12},{1,17},{... | collective-permute-start | bytes 1622024 | tf_op jit(solution)/shard_map/ppermute | solution.py:161
  449.7 18.7 %collective-permute-start.74 = (bf16[192,1408]{1,0:T(8,128)(2,1)}, bf16[192,1408]{1,0:T(8,128)(2,1)S(1)}, u32[]{:S(2)}, u32[]{:S(2)}) collective-permute-start(bf16[192,1408]{1,0:T(8,128)(2,1)} %collective-permute-done.54.refs_6_), channel_id=1, source_target_pairs={{0,8},{4,12},{8,0},{12,4},{16,24},{20,28},{24,16},{28,20},{1,9},{5... | collective-permute-start | bytes 1622024 | tf_op jit(solution)/shard_map/ppermute | solution.py:161
  465.5 27.5 %collective-permute-start.78 = (bf16[768,256]{1,0:T(8,128)(2,1)}, bf16[768,256]{1,0:T(8,128)(2,1)S(1)}, u32[]{:S(2)}, u32[]{:S(2)}) collective-permute-start(bf16[768,256]{1,0:T(8,128)(2,1)} %get-tuple-element.262.refs_0_), channel_id=1, source_target_pairs={{0,16},{4,20},{8,24},{12,28},{16,0},{20,4},{24,8},{28,12},{1,17},{... | collective-permute-start | bytes 1179656 | tf_op jit(solution)/shard_map/ppermute | solution.py:161
  466.4 26.7 %collective-permute-start.72 = (bf16[768,256]{1,0:T(8,128)(2,1)}, bf16[768,256]{1,0:T(8,128)(2,1)S(1)}, u32[]{:S(2)}, u32[]{:S(2)}) collective-permute-start(bf16[768,256]{1,0:T(8,128)(2,1)} %get-tuple-element.262.refs_0_), channel_id=1, source_target_pairs={{0,8},{4,12},{8,0},{12,4},{16,24},{20,28},{24,16},{28,20},{1,9},{5... | collective-permute-start | bytes 1179656 | tf_op jit(solution)/shard_map/ppermute | solution.py:161
  472.8 20.8 %collective-permute-start.77 = (bf16[768,256]{1,0:T(8,128)(2,1)}, bf16[768,256]{1,0:T(8,128)(2,1)S(1)}, u32[]{:S(2)}, u32[]{:S(2)}) collective-permute-start(bf16[768,256]{1,0:T(8,128)(2,1)} %get-tuple-element.268.refs_4_), channel_id=1, source_target_pairs={{0,8},{4,12},{8,0},{12,4},{16,24},{20,28},{24,16},{28,20},{1,9},{5... | collective-permute-start | bytes 1179656 | tf_op jit(solution)/shard_map/ppermute | solution.py:161
  474.2 19.5 %collective-permute-start.76 = (bf16[768,256]{1,0:T(8,128)(2,1)}, bf16[768,256]{1,0:T(8,128)(2,1)S(1)}, u32[]{:S(2)}, u32[]{:S(2)}) collective-permute-start(bf16[768,256]{1,0:T(8,128)(2,1)} %get-tuple-element.268.refs_4_), channel_id=1, source_target_pairs={{0,16},{4,20},{8,24},{12,28},{16,0},{20,4},{24,8},{28,12},{1,17},{... | collective-permute-start | bytes 1179656 | tf_op jit(solution)/shard_map/ppermute | solution.py:161
  493.1 89.6 %collective-permute-start.91 = (bf16[4,256,1408]{2,1,0:T(8,128)(2,1)}, bf16[4,256,1408]{2,1,0:T(8,128)(2,1)}, u32[]{:S(2)}, u32[]{:S(2)}) collective-permute-start(bf16[4,256,1408]{2,1,0:T(8,128)(2,1)} %get-tuple-element.293), channel_id=1, source_target_pairs={{0,4},{4,0},{8,12},{12,8},{16,20},{20,16},{24,28},{28,24},{1,5},{5... | collective-permute-start | bytes 8650760 | tf_op jit(solution)/shard_map/ppermute | solution.py:165
  493.1 101.3 %collective-permute-start.92 = (bf16[4,256,1408]{2,1,0:T(8,128)(2,1)}, bf16[4,256,1408]{2,1,0:T(8,128)(2,1)}, u32[]{:S(2)}, u32[]{:S(2)}) collective-permute-start(bf16[4,256,1408]{2,1,0:T(8,128)(2,1)} %get-tuple-element.294), channel_id=1, source_target_pairs={{0,4},{4,0},{8,12},{12,8},{16,20},{20,16},{24,28},{28,24},{1,5},{5... | collective-permute-start | bytes 8650760 | tf_op jit(solution)/shard_map/ppermute | solution.py:165
  507.9 17.0 %collective-permute-start.82 = (f32[8,768]{1,0:T(8,128)S(1)}, f32[8,768]{1,0:T(8,128)S(1)}, u32[]{:S(2)}, u32[]{:S(2)}) collective-permute-start(f32[8,768]{1,0:T(8,128)S(1)} %select_add_fusion), channel_id=1, source_target_pairs={{0,16},{4,20},{8,24},{12,28},{16,0},{20,4},{24,8},{28,12},{1,17},{... | collective-permute-start | bytes 73736 | tf_op jit(solution)/shard_map/ppermute | solution.py:161
  517.6 17.3 %collective-permute-start.86 = (bf16[2,384,256]{2,1,0:T(8,128)(2,1)S(1)}, bf16[2,384,256]{2,1,0:T(8,128)(2,1)S(1)}, u32[]{:S(2)}, u32[]{:S(2)}) collective-permute-start(bf16[2,384,256]{2,1,0:T(8,128)(2,1)S(1)} %add_convert_fusion.6.refs_0_), channel_id=1, source_target_pairs={{0,1},{1,0},{2,3},{3,2},{4,5},{5,4},{6,7},{7,6},{8,9},{9,8},{10,11... | collective-permute-start | bytes 1179656 | tf_op jit(solution)/shard_map/ppermute | solution.py:176
  525.0 16.7 %collective-permute-start.93 = (bf16[2,384,256]{2,1,0:T(8,128)(2,1)}, bf16[2,384,256]{2,1,0:T(8,128)(2,1)S(1)}, u32[]{:S(2)}, u32[]{:S(2)}) collective-permute-start(bf16[2,384,256]{2,1,0:T(8,128)(2,1)} %get-tuple-element.296), channel_id=1, source_target_pairs={{0,1},{1,0},{2,3},{3,2},{4,5},{5,4},{6,7},{7,6},{8,9},{9,8},{10,11... | collective-permute-start | bytes 1179656 | tf_op jit(solution)/shard_map/ppermute | solution.py:176
  526.2 100.8 %collective-permute-start.100 = (bf16[4,1408,256]{2,1,0:T(8,128)(2,1)}, bf16[4,1408,256]{2,1,0:T(8,128)(2,1)}, u32[]{:S(2)}, u32[]{:S(2)}) collective-permute-start(bf16[4,1408,256]{2,1,0:T(8,128)(2,1)} %get-tuple-element.310), channel_id=1, source_target_pairs={{0,4},{4,0},{8,12},{12,8},{16,20},{20,16},{24,28},{28,24},{1,5},{5... | collective-permute-start | bytes 8650760 | tf_op jit(solution)/shard_map/ppermute | solution.py:165
  534.9 22.3 %collective-permute-start.90 = (f32[8,768]{1,0:T(8,128)S(1)}, f32[8,768]{1,0:T(8,128)S(1)}, u32[]{:S(2)}, u32[]{:S(2)}) collective-permute-start(f32[8,768]{1,0:T(8,128)S(1)} %add_add_fusion.2), channel_id=1, source_target_pairs={{0,3},{1,2},{2,1},{3,0},{4,7},{5,6},{6,5},{7,4},{8,11},{9,10},{10,... | collective-permute-start | bytes 73736 | tf_op jit(solution)/shard_map/ppermute | solution.py:176
  541.6 15.9 %collective-permute-start.89 = (f32[8,768]{1,0:T(8,128)S(1)}, f32[8,768]{1,0:T(8,128)S(1)}, u32[]{:S(2)}, u32[]{:S(2)}) collective-permute-start(f32[8,768]{1,0:T(8,128)S(1)} %add_add_fusion.2), channel_id=1, source_target_pairs={{0,2},{1,3},{2,0},{3,1},{4,6},{5,7},{6,4},{7,5},{8,10},{9,11},{10,... | collective-permute-start | bytes 73736 | tf_op jit(solution)/shard_map/ppermute | solution.py:176
  562.7 17.7 %collective-permute-start.97 = (bf16[2,256,512]{2,1,0:T(8,128)(2,1)S(1)}, bf16[2,256,512]{2,1,0:T(8,128)(2,1)S(1)}, u32[]{:S(2)}, u32[]{:S(2)}) collective-permute-start(bf16[2,256,512]{2,1,0:T(8,128)(2,1)S(1)} %copy-done.103), channel_id=1, source_target_pairs={{0,4},{4,0},{8,12},{12,8},{16,20},{20,16},{24,28},{28,24},{1,5},{5... | collective-permute-start | bytes 1572872 | tf_op jit(solution)/shard_map/ppermute | solution.py:165
  571.9 39.5 %collective-permute-start.99 = (bf16[4,512,256]{2,1,0:T(8,128)(2,1)}, bf16[4,512,256]{2,1,0:T(8,128)(2,1)}, u32[]{:S(2)}, u32[]{:S(2)}) collective-permute-start(bf16[4,512,256]{2,1,0:T(8,128)(2,1)} %get-tuple-element.309), channel_id=1, source_target_pairs={{0,4},{4,0},{8,12},{12,8},{16,20},{20,16},{24,28},{28,24},{1,5},{5... | collective-permute-start | bytes 3145736 | tf_op jit(solution)/shard_map/ppermute | solution.py:165
  576.4 38.5 %all-to-all-start.2 = ((bf16[8,256,256]{2,1,0:T(8,128)(2,1)}), bf16[8,256,256]{2,1,0:T(8,128)(2,1)S(1)}, u32[]{:S(2)}, u32[]{:S(2)}) async-start(bf16[8,256,256]{2,1,0:T(8,128)(2,1)} %unpack.2), calls=%async_computation.2 | async-start | bytes 2097152 | tf_op jit(solution)/shard_map/all_to_all | solution.py:1206
  581.1 44.2 %collective-permute-start.98 = (bf16[4,256,512]{2,1,0:T(8,128)(2,1)}, bf16[4,256,512]{2,1,0:T(8,128)(2,1)S(1)}, u32[]{:S(2)}, u32[]{:S(2)}) collective-permute-start(bf16[4,256,512]{2,1,0:T(8,128)(2,1)} %get-tuple-element.308), channel_id=1, source_target_pairs={{0,4},{4,0},{8,12},{12,8},{16,20},{20,16},{24,28},{28,24},{1,5},{5... | collective-permute-start | bytes 3145736 | tf_op jit(solution)/shard_map/ppermute | solution.py:165
  582.7 22.1 %collective-permute-start.95 = (bf16[2,384,256]{2,1,0:T(8,128)(2,1)S(1)}, bf16[2,384,256]{2,1,0:T(8,128)(2,1)S(1)}, u32[]{:S(2)}, u32[]{:S(2)}) collective-permute-start(bf16[2,384,256]{2,1,0:T(8,128)(2,1)S(1)} %add_convert_fusion.4.refs_0_), channel_id=1, source_target_pairs={{0,1},{1,0},{2,3},{3,2},{4,5},{5,4},{6,7},{7,6},{8,9},{9,8},{10,11... | collective-permute-start | bytes 1179656 | tf_op jit(solution)/shard_map/ppermute | solution.py:176
  621.3 20.9 %all-to-all-start.3 = ((bf16[8,288,256]{2,1,0:T(8,128)(2,1)}), bf16[8,288,256]{2,1,0:T(8,128)(2,1)S(1)}, u32[]{:S(2)}, u32[]{:S(2)}) async-start(bf16[8,288,256]{2,1,0:T(8,128)(2,1)} %unpack.3), calls=%async_computation.3 | async-start | bytes 2359296 | tf_op jit(solution)/shard_map/all_to_all | solution.py:1206
  (150 other events, 1827.1 us)

commit v7 on v6

--- a/solution.py
+++ b/solution.py
@@ -176,10 +176,12 @@
         return lax.ppermute(value, "tensor", [(a, a ^ mask) for a in range(tp)])
 
     def sum_groups(value):
-        return (value + by_group(value, 1)) + (by_group(value, 2) + by_group(value, 3))
+        value = value + by_group(value, 1)
+        return value + by_group(value, 2)
 
     def sum_z(value):
-        return (value + by_z(value, 1)) + (by_z(value, 2) + by_z(value, 3))
+        value = value + by_z(value, 1)
+        return value + by_z(value, 3)
 
     def z_first(keep, send):
         return both(keep, by_z(send, 1))
@@ -293,7 +295,7 @@
         for s in pieces:
             outs[s][...] = packed[part_rows(m, s), :].astype(BF16)
 
-    def pack(value, dealt):
+    def pack(value, dealt, table):
         own = run(
             functools.partial(pack_body, dealt), "pack", (1,), table, [(value, None, None)],
             [((rp, ds), BF16, None, None)] * parts,
@@ -304,10 +306,7 @@
     x_send = hidden_in.reshape(seqs * per, dp, ds).transpose(1, 0, 2)
     d_send = cotangent.reshape(slots * seq_len, dp, ds).transpose(1, 0, 2)
     x_all = lax.all_to_all(x_send, "dp", 0, 0, tiled=True).reshape(rows_all, ds)
-    x_pieces = pack(x_all, False)
-    d_all = lax.all_to_all(d_send, "dp", 0, 0, tiled=True).reshape(rows_all, ds)
-    d_pieces = pack(d_all, True)
-
+    x_pieces = pack(x_all, False, table)
     def spread(vector):
         tall = vector.reshape((groups, parts, ds) + vector.shape[1:])[g]
         return jnp.stack([tall[c ^ s] for s in pieces])
@@ -353,39 +352,6 @@
         zero = jnp.zeros_like(rms)
         flat = jnp.stack([rms, low_gate, high_gate, gap, zero, zero, zero, zero])
         return flat, flat.T
-
-    def rows_pair(refs):
-        return jnp.concatenate([ref[...] for ref in refs], axis=0)
-
-    def dhidden_body(m, *refs):
-        d_refs = refs[: 2 * parts]
-        w_refs, sel_refs = refs[2 * parts : 3 * parts], refs[3 * parts : 3 * parts + 2]
-        outs = refs[3 * parts + 2 :]
-        ids = rows_pair(sel_refs)
-        rows_of = [rows_pair(d_refs[2 * s : 2 * s + 2]) for s in pieces]
-        products = []
-        for e in range(experts):
-            products.append(sum(nt(rows_of[s], w_refs[s][e]) for s in pieces))
-        low, high = two_slots(ids[:, 2:3], ids[:, 3:4], products)
-        low, high = low.astype(BF16), high.astype(BF16)
-        for step, pair in enumerate(((3, 1), (2, 0))):
-
-            @pl.when(pl.program_id(0) == step)
-            def _():
-                for k, r in enumerate(pair):
-                    outs[2 * r][...] = low[k * blk : (k + 1) * blk]
-                    outs[2 * r + 1][...] = high[k * blk : (k + 1) * blk]
-
-    def dhidden(meta):
-        spots = [lambda i, m: (m[5 - i], 0), lambda i, m: (m[3 - i], 0)]
-        ins = [(d, (blk, ds), spot) for d in d_pieces for spot in spots]
-        ins += [(w, None, None) for w in wo]
-        ins += [(sel, (blk, 8), spot) for spot in spots]
-        outs = [((blk, ff), BF16, None, None)] * 8
-        return run(
-            dhidden_body, "dhidden", (2,), meta, ins, outs,
-            flops=2 * rp * experts * parts * ds * ff,
-        )
 
     tile = 256
 
@@ -429,14 +395,51 @@
     outs = [((rp, 2 * HD), BF16, (tile, 2 * HD), lambda i, m: (i, 0))] * 8
     outs += [((8, rp), F32, (8, tile), lambda i, m: (0, i))]
     qkv = run(
-        qkv_body, "qkv", (rp // tile,), after(meta, in_own), ins, outs,
+        qkv_body, "qkv", (rp // tile,), after(meta, wo[1:], wi[1:], wp[1:]), ins, outs,
         [pltpu.VMEM((heads, tile, 4 * HD), BF16)],
         flops=2 * rp * (experts + 2) * parts * ds * hw,
     )
-    dh = dhidden(after(meta, qkv[8]))
     stats_a = sum_groups(qkv[8])
     flat_a, cols_a = gate_columns(stats_a, low_a, high_a)
-    q_sum, kv_sum, _, _ = reduce_groups(qkv[0:8:2], qkv[1:8:2], late=cols_a)
+    q_sum, kv_sum, _, far = reduce_groups(qkv[0:8:2], qkv[1:8:2], late=cols_a)
+
+    d_all = lax.all_to_all(d_send, "dp", 0, 0, tiled=True).reshape(rows_all, ds)
+    d_pieces = pack(d_all, True, after(table, far[0]))
+
+    def rows_pair(refs):
+        return jnp.concatenate([ref[...] for ref in refs], axis=0)
+
+    def dhidden_body(m, *refs):
+        d_refs = refs[: 2 * parts]
+        w_refs, sel_refs = refs[2 * parts : 3 * parts], refs[3 * parts : 3 * parts + 2]
+        outs = refs[3 * parts + 2 :]
+        ids = rows_pair(sel_refs)
+        rows_of = [rows_pair(d_refs[2 * s : 2 * s + 2]) for s in pieces]
+        products = []
+        for e in range(experts):
+            products.append(sum(nt(rows_of[s], w_refs[s][e]) for s in pieces))
+        low, high = two_slots(ids[:, 2:3], ids[:, 3:4], products)
+        low, high = low.astype(BF16), high.astype(BF16)
+        for step, pair in enumerate(((3, 1), (2, 0))):
+
+            @pl.when(pl.program_id(0) == step)
+            def _():
+                for k, r in enumerate(pair):
+                    outs[2 * r][...] = low[k * blk : (k + 1) * blk]
+                    outs[2 * r + 1][...] = high[k * blk : (k + 1) * blk]
+
+    def dhidden(meta):
+        spots = [lambda i, m: (m[5 - i], 0), lambda i, m: (m[3 - i], 0)]
+        ins = [(d, (blk, ds), spot) for d in d_pieces for spot in spots]
+        ins += [(w, None, None) for w in wo]
+        ins += [(sel, (blk, 8), spot) for spot in spots]
+        outs = [((blk, ff), BF16, None, None)] * 8
+        return run(
+            dhidden_body, "dhidden", (2,), meta, ins, outs,
+            flops=2 * rp * experts * parts * ds * ff,
+        )
+
+    dh = dhidden(meta)
 
     def rope_body(m, a0, a1, a2, b0, b1, b2, cols, cos_ref, sin_ref, q_ref, kv_ref):
         rms = cols[:, 0:1]
@@ -497,8 +500,7 @@
         flops=8 * rp * span * HD,
     )
     gm_a, gm_b, _ = gather_groups(gated_a, gated_b)
-    chunks = 2
-    zr = rp // chunks // 2
+    zr = rp // 2
     hold = [((parts, zr, ds), BF16, None, None)] * 2
 
     def store_halves(i, refs, s, value):
@@ -528,8 +530,8 @@
         for s in pieces:
             store_halves(pl.program_id(0), outs, s, acc[s].astype(BF16))
 
-    def project(k, meta):
-        half = lambda i, m: (2 * k + m[7 - i], 0)
+    def project(meta):
+        half = lambda i, m: (m[7 - i], 0)
         ins = [(v, (zr, HD), half) for v in gm_a + gm_b]
         ins += [(sel, (zr, 8), half)]
         ins += [(w, None, None) for w in wp]
@@ -539,25 +541,20 @@
             flops=4 * zr * experts * hw * parts * ds,
         )
 
-    sums = [project(0, meta)]
+    proj_halves = project(meta)
     dh_a, dh_b = held((dh[0:8:2], dh[1:8:2]), gm_a[3], gm_b[3])
     ra, rb = by_group(dh_a[3], 1), by_group(dh_b[3], 2)
-    halves = [z_first(*sums[0])]
-    for k in range(1, chunks):
-        sums.append(project(k, after(meta, halves[-1])))
-        halves[-1] = z_covered(halves[-1], halves[-1], 3, sums[-1][0])
-        halves.append(z_first(*sums[-1]))
-    halves[-1] = z_second(halves[-1])
     ax, by = by_group(dh_a[1], 1), by_group(dh_b[2], 2)
-    attn_totals = [half for v in halves for half in z_last(v)]
-    near = held((both(dh_a[2], ra), both(dh_b[1], rb)), (ax, by))
+    half = z_second(z_first(*proj_halves))
+    near = held((both(dh_a[2], ra), both(dh_b[1], rb)), (ax, by), half)
     dh_a, dh_b = (dh_a[0], ax, by_group(near[0], 2)), (dh_b[0], by_group(near[1], 1), by)
+    attn_totals = list(z_last(half))
 
     def norm_body(m, *refs):
-        t_refs = refs[: 2 * chunks]
-        x_refs = refs[2 * chunks : 2 * chunks + parts]
-        gain_ref, router_ref, after_ref, u_ref, stats_ref = refs[2 * chunks + parts :]
-        for k in range(2 * chunks):
+        t_refs = refs[: 2]
+        x_refs = refs[2 : 2 + parts]
+        gain_ref, router_ref, after_ref, u_ref, stats_ref = refs[2 + parts :]
+        for k in range(2):
             span_k = at_row(m, IN_ORDER + k, zr)
             for s in pieces:
                 after_ref[s, span_k, :] = x_refs[s][span_k, :].astype(F32) + t_refs[k][s].astype(F32)
@@ -579,7 +576,7 @@
         ((parts, rp, ds), BF16, None, None),
         ((8, rp), F32, None, None),
     ]
-    after_rows, u_f, stats_part = run(norm_body, "norm", (1,), after(meta, near), ins, outs)
+    after_rows, u_f, stats_part = run(norm_body, "norm", (1,), meta, ins, outs)
     def up_body(m, *refs):
         u_refs, w_refs = refs[:2], refs[2 : 2 + parts]
         sel_refs = refs[2 + parts : 4 + parts]
@@ -699,9 +696,10 @@
         )
 
     dx_near = dx((0, 1), after(meta, gg_a[2], gg_b[2]))
-    dots_f = after(sum_z(dots_f), gg_a[3], gg_b[3])
-    dots_f = jnp.stack([dots_f, by_group(dots_f, 1), by_group(dots_f, 2), by_group(dots_f, 3)])
     dx_far = dx((2, 3), meta)
+    dots_f = sum_z(dots_f)
+    dots_f = jnp.stack([dots_f, held([by_group(dots_f, 1)], dx_near[0])[0]])
+    dots_f = jnp.concatenate([dots_f, held([by_group(dots_f, 2)], dx_far[0])[0]])
     near_half = z_first(*dx_near)
     near_half = z_covered(near_half, near_half, 3, dx_far[0])
     far_half = z_first(*dx_far)
@@ -728,10 +726,10 @@
 
 
     def exchange(sums):
-        total = sums[0].astype(F32)
-        for s in pieces[1:]:
-            total = total + by_part(sums[s], s).astype(F32)
-        return total
+        return [sums[0]] + [by_part(sums[s], s) for s in pieces[1:]]
+
+    def add_up(got):
+        return sum(v.astype(F32) for v in got)
 
     ffn_input = (after_rows * flat_f[0][None, :, None] * gain_f).astype(BF16)
 
@@ -793,10 +791,7 @@
             out_ref[0, :, j, :] = total
 
     def fold(sums, meta):
-        ins = []
-        for half in sums:
-            got = [half[0]] + [by_part(half[s], s) for s in pieces[1:]]
-            ins += [(v, (1, ds, ff), lambda e, m: (e, 0, 0)) for v in got]
+        ins = [(v, (1, ds, ff), lambda e, m: (e, 0, 0)) for half in sums for v in half]
         outs = [((experts, ds, 2, ff), F32, (1, ds, 2, ff), lambda e, m: (e, 0, 0, 0))]
         return run(fold_body, "fold", (experts,), meta, ins, outs)[0]
 
@@ -971,6 +966,7 @@
 
     ins = [(v, None, None) for v in (dkv_own, dkv_in, kv_rot, cosine, sine)]
     outs = [((rp, 2 * HD), BF16, None, None), ((8, rp), F32, None, None)]
+    got_in = [exchange(dwin_gate), exchange(held(dwin_up, dm_a[2], dm_b[1]))]
     dkv, dots_kv = run(
         dkv_body, "dkv", (1,), after(meta, ag_a[3], ag_b[3]), ins, outs
     )
@@ -1054,7 +1050,7 @@
     down_halves = down(after(meta, dkv))
     down_halves, dwout_sums = down_halves[:2], down_halves[2:]
     da_a, da_b, da_along = gather_groups(dq, dkv, late=(dwout_sums[0],))
-    dwproj_sums = dwproj(after(meta, da_along))
+    dwproj_sums = dwproj(after(meta, da_along, got_in))
     def place_heads(m, refs, lo, hi):
         for r in range(4):
             lanes = pl.ds(pl.multiple_of(m[2 + r] * HD, HD), HD)
@@ -1082,17 +1078,20 @@
 
     def dattn(meta):
         half = lambda i, m: (m[7 - i], 0)
-        ins = [(v, (2 * zr, 2 * HD), half) for v in da_a + da_b]
-        ins += [(sel, (2 * zr, 8), half)]
+        ins = [(v, (zr, 2 * HD), half) for v in da_a + da_b]
+        ins += [(sel, (zr, 8), half)]
         ins += [(w, None, None) for w in wq + wkv]
         return run(
-            dattn_body, "dattn", (2,), meta, ins, [((parts, 2 * zr, ds), BF16, None, None)] * 2,
-            [pltpu.VMEM((2 * zr, hw), BF16)] * 4,
-            flops=8 * zr * (experts + 2) * hw * parts * ds,
+            dattn_body, "dattn", (2,), meta, ins, [((parts, zr, ds), BF16, None, None)] * 2,
+            [pltpu.VMEM((zr, hw), BF16)] * 4,
+            flops=4 * zr * (experts + 2) * hw * parts * ds,
         )
 
-    dots_a = sum_groups(after(dots_q + jnp.where(third, dots_kv, 0.0), dwproj_sums[0]))
+    dots_a = dots_q + jnp.where(third, dots_kv, 0.0)
+    dots_a = sum_groups(after(dots_a, dwproj_sums[0]))
+    got_out = exchange(dwout_sums)
     da_halves = dattn(after(meta, dwproj_sums[0]))
+    got_proj = exchange(dwproj_sums)
     x_stack = jnp.stack(x_pieces)
     attn_input = (x_stack.astype(F32) * flat_a[0][None, :, None] * gain_a).astype(BF16)
 
@@ -1135,8 +1134,7 @@
             flops=2 * rp * (experts + 2) * hw * parts * ds,
         )
 
-    dwqkv_sums = dwqkv(after(meta, da_halves[0], dots_a))
-    dots_a = sum_z(dots_a)
+    dwqkv_sums = dwqkv(after(meta, da_halves[0]))
 
 
     da_half = z_covered(*da_halves, 1, dwqkv_sums[0])
@@ -1157,7 +1155,7 @@
 
     ins = [(t, None, None) for t in down_totals] + [(after_rows, None, None)]
     out_rows = run(
-        finish_body, "finish", (1,), after(meta, dwqkv_sums[0]), ins,
+        finish_body, "finish", (1,), after(meta, dwqkv_sums[0], dots_a), ins,
         [((rp, ds), BF16, None, None)] * parts,
     )
 
@@ -1208,10 +1206,12 @@
         return rows_of, spread_rows, landed[:, count:]
 
     layer_out, layer_rows, _ = unpack(out_rows, x_all, False, table)
-    expertin_grad = fold((dwin_gate, dwin_up), after(meta, layer_rows, dots_a))
+    got_q, got_kv = exchange(dwqkv_sums[:parts]), exchange(dwqkv_sums[parts:])
+    expertin_grad = fold(got_in, after(meta, layer_rows))
+    da_half = z_covered(da_half, da_half, 3, (expertin_grad, layer_out))
+    da_totals = z_last(da_half)
+    dots_a = sum_z(after(dots_a, da_half))
     back_a = back_columns(flat_a, dots_a, low_a, high_a)
-    da_half = z_covered(da_half, da_half, 3, layer_rows)
-    da_totals = z_last(da_half)
     ins = [(t, None, None) for t in da_totals]
     ins += [(x_stack, None, None), (dafter, None, None)]
     ins += [(gain_a, None, None), (router_a, None, None), (back_a, None, None)]
@@ -1219,11 +1219,10 @@
     outs += [((experts + 1, parts, ds), F32, None, None)]
     *dinput, small_a = run(
         functools.partial(norm_back_body, False), "norm_back_first", (1,),
-        after(meta, expertin_grad), ins, outs,
-    )
-    expertout_grad = exchange(dwout_sums)
-    proj_grad = exchange(dwproj_sums)
-    query_grad, kv_grad = exchange(dwqkv_sums[:parts]), exchange(dwqkv_sums[parts:])
+        meta, ins, outs,
+    )
+    expertout_grad, proj_grad = add_up(got_out), add_up(got_proj)
+    query_grad, kv_grad = add_up(got_q), add_up(got_kv)
     vectors = 2 * (experts + 1)
     small = jnp.concatenate([small_a, small_f], axis=0).reshape(vectors * parts, ds)
     small = jnp.pad(small, ((0, -vectors * parts % 16), (0, 0))).astype(BF16)

time: 652 us -> 621 us (0.952)
  starting transfers between devices: 141 us -> 118 us
    ppermute x24 -> x19, starting transfers between devices: 53.4 us -> 34.6 us  [by_z(): return lax.ppermute(value, 'tensor', [(a, a ^ mask) for a in range(tp)])]
    all_to_all x1, waiting for transfers between devices: 2.45 us -> 10.8 us  [local(): x_all = lax.all_to_all(x_send, 'dp', 0, 0, tiled=True).reshape(rows_all, ds)]
    ppermute x24 -> x19, waiting for transfers between devices: 52.2 us -> 45.6 us  [by_z(): return lax.ppermute(value, 'tensor', [(a, a ^ mask) for a in range(tp)])]
    ppermute x60 -> x56, waiting for transfers between devices: 132 us -> 126 us  [by_group(): return lax.ppermute(value, 'dp', pairs)]
    ppermute x60 -> x56, starting transfers between devices: 65.2 us -> 61.2 us  [by_group(): return lax.ppermute(value, 'dp', pairs)]
    pallas_call x29 -> x28, Pallas kernels: 233 us -> 229 us  [run(): pl.pallas_call(body, name=name, grid_spec=pltpu.PrefetchScalarGridSpec(nu...]
    unnamed x222 -> x220, local copies, waits for them, and re-layouts: 18 us -> 17.9 us
  transfers between devices with their start and end apart: 105 -> 96, of which waited for: 34 -> 40; matrix products, arithmetic and copies ran while one was open for 9% -> 8% of each run, Pallas kernels for 31% -> 28%
where the time goes in v7:
time: 621 us; the launch traced here: 616 us
  Pallas kernels  229 us (37%)
  waiting for transfers between devices  195 us (31%)
  starting transfers between devices  118 us (19%)
  local copies, waits for them, and re-layouts  37.4 us (6%)
  other arithmetic  32 us (5%)
    pallas_call x28, Pallas kernels, run(): pl.pallas_call(body, name=name, grid_spec=pltpu.PrefetchScalarGridSpec(nu...  229 us
    ppermute x56, waiting for transfers between devices, by_group(): return lax.ppermute(value, 'dp', pairs)  126 us
    ppermute x56, starting transfers between devices, by_group(): return lax.ppermute(value, 'dp', pairs)  61.2 us
    ppermute x19, waiting for transfers between devices, by_z(): return lax.ppermute(value, 'tensor', [(a, a ^ mask) for a in range(tp)])  45.6 us
    ppermute x19, starting transfers between devices, by_z(): return lax.ppermute(value, 'tensor', [(a, a ^ mask) for a in range(tp)])  34.6 us
    unnamed x220, local copies, waits for them, and re-layouts  17.9 us
  transfers between devices with their start and end apart: 96, of which 40 were waited for; matrix products, arithmetic and copies ran while one was open for 8% of the time, Pallas kernels for 28%

profile of v7, /device:TPU:0, one launch (start us, length us, event | category | flops | bytes accessed | tf_op | source)
XLA Modules:
  0.0 615.8 jit_solution(3726214054670068346)
XLA Ops:
  0.7 6.1 copy.230
  9.3 5.0 all-to-all-start
  18.8 10.8 %all-to-all-done = bf16[8,256,256]{2,1,0:T(8,128)(2,1)S(1)} async-done(((bf16[8,256,256]{2,1,0:T(8,128)(2,1)}), bf16[8,256,256]{2,1,0:T(8,128)(2,1)S(1)}, u32[]{:S(2)}, u32[]{:S(2)}) %all-to-all-start) | async-done | bytes 1048608 | tf_op jit(solution)/shard_map/all_to_all | solution.py:308
  29.6 3.8 all-to-all-start.1
  33.4 4.0 pack.2
  42.3 8.5 %qkv.1 = (bf16[768,256]{1,0:T(8,128)(2,1)}, bf16[768,256]{1,0:T(8,128)(2,1)}, bf16[768,256]{1,0:T(8,128)(2,1)}, bf16[768,256]{1,0:T(8,128)(2,1)}, bf16[768,256]{...) custom-call(s32[24]{0:T(128)} %stack.147.m, ...), custom_call_target="tpu_custom_call" | custom-call | flops 2415919104 | bytes 7137280 | tf_op jit(solution)/shard_map/qkv/pallas_call | solution.py:61
  64.3 6.8 %collective-permute-done.6 = bf16[768,256]{1,0:T(8,128)(2,1)S(1)} collective-permute-done((bf16[768,256]{1,0:T(8,128)(2,1)}, bf16[768,256]{1,0:T(8,128)(2,1)S(1)}, u32[]{:S(2)}, u32[]{:S(2)}) %collective-permute-start.6) | collective-permute-done | bytes 393248 | tf_op jit(solution)/shard_map/ppermute | solution.py:161
  72.0 4.0 pack.3
  81.1 12.0 %dhidden.1 = (bf16[192,1408]{1,0:T(8,128)(2,1)}, bf16[192,1408]{1,0:T(8,128)(2,1)}, bf16[192,1408]{1,0:T(8,128)(2,1)}, bf16[192,1408]{1,0:T(8,128)(2,1)}, bf16[1...) custom-call(s32[24]{0:T(128)} %stack.147.m, ...), custom_call_target="tpu_custom_call" | custom-call | flops 4429185024 | bytes 11714560 | tf_op jit(solution)/shard_map/dhidden/pallas_call | solution.py:61
  94.0 4.6 rope.1
  102.5 7.9 %attend.1 = (bf16[768,128]{1,0:T(8,128)(2,1)}, bf16[768,128]{1,0:T(8,128)(2,1)}, bf16[768,128]{1,0:T(8,128)(2,1)}, bf16[768,128]{1,0:T(8,128)(2,1)}) custom-call(s32[24]{0:T(128)} %stack.147.m, bf16[768,256]{1,0:T(8,128)(2,1)} %get-tuple-element.177.q_ref.refs_0_, bf16[768,256]{1,0:T(8,128)(2,1)} %get-tuple-element.178.kv_ref.refs_1_, ...), custom_call_target="tpu_custom_call" | custom-call | flops 301989888 | bytes 1753088 | tf_op jit(solution)/shard_map/attend/pallas_call | solution.py:61
  114.6 3.8 collective-permute-done.16.refs_1_
  120.6 2.7 collective-permute-done.24.refs_2_
  123.3 3.3 collective-permute-done.17.refs_3_
  127.3 9.9 %proj.1 = (bf16[2,384,256]{2,1,0:T(8,128)(2,1)}, bf16[2,384,256]{2,1,0:T(8,128)(2,1)}) custom-call(s32[24]{0:T(128)} %stack.147.m, bf16[768,128]{1,0:T(8,128)(2,1)} %get-tuple-element.186.refs_0_, bf16[768,128]{1,0:T(8,128)(2,1)} %copy-done.102, bf16[768,128]{1,0:T(8,128)(2,1)} %copy-done.104, bf16[768,128]{1,0:T(8,128)(2,1)} %copy-done.106, ...), custom_call_target="tpu_custom_call" | custom-call | flops 1610612736 | bytes 4481024 | tf_op jit(solution)/shard_map/proj/pallas_call | solution.py:61
  142.9 4.9 collective-permute-done.26
  148.9 3.7 collective-permute-start.27
  155.1 5.3 collective-permute-done.27
  160.5 3.8 collective-permute-done.22.refs_7_
  166.8 3.9 collective-permute-start.30
  172.0 7.0 %collective-permute-done.30.refs_1_ = bf16[2,384,256]{2,1,0:T(8,128)(2,1)S(1)} collective-permute-done((bf16[2,384,256]{2,1,0:T(8,128)(2,1)S(1)}, bf16[2,384,256]{2,1,0:T(8,128)(2,1)S(1)}, u32[]{:S(2)}, u32[]{:S(2)}) %collective-permute-start.30) | collective-permute-done | bytes 393248 | tf_op jit(solution)/shard_map/ppermute | solution.py:176
  179.7 4.4 norm.1
  184.1 10.1 %up.2 = (bf16[2,192,1408]{2,1,0:T(8,128)(2,1)}, bf16[2,192,1408]{2,1,0:T(8,128)(2,1)}, bf16[2,192,1408]{2,1,0:T(8,128)(2,1)}, bf16[2,192,1408]{2,1,0:T(8,128)(2,1)}) custom-call(s32[24]{0:T(128)} %stack.147.m, bf16[2,768,256]{2,1,0:T(8,128)(2,1)} %get-tuple-element.199.refs_0_.refs_1_, bf16[2,768,256]{2,1,0:T(8,128)(2,1)} %get-tuple-element.199.refs_0_.refs_1_, ...), custom_call_target="tpu_custom_call" | custom-call | flops 4429185024 | bytes 17481728 | tf_op jit(solution)/shard_map/up/pallas_call | solution.py:61
  196.0 10.3 %up.3 = (bf16[2,192,1408]{2,1,0:T(8,128)(2,1)}, bf16[2,192,1408]{2,1,0:T(8,128)(2,1)}, bf16[2,192,1408]{2,1,0:T(8,128)(2,1)}, bf16[2,192,1408]{2,1,0:T(8,128)(2,1)}) custom-call(s32[24]{0:T(128)} %stack.147.m, bf16[2,768,256]{2,1,0:T(8,128)(2,1)} %get-tuple-element.199.refs_0_.refs_1_, bf16[2,768,256]{2,1,0:T(8,128)(2,1)} %get-tuple-element.199.refs_0_.refs_1_, ...), custom_call_target="tpu_custom_call" | custom-call | flops 4429185024 | bytes 17481728 | tf_op jit(solution)/shard_map/up/pallas_call | solution.py:61
  208.7 12.6 %collective-permute-done.33 = bf16[2,192,1408]{2,1,0:T(8,128)(2,1)} collective-permute-done((bf16[2,192,1408]{2,1,0:T(8,128)(2,1)}, bf16[2,192,1408]{2,1,0:T(8,128)(2,1)}, u32[]{:S(2)}, u32[]{:S(2)}) %collective-permute-start.33) | collective-permute-done | bytes 1081376 | tf_op jit(solution)/shard_map/ppermute | solution.py:161
  221.3 2.6 add_convert_fusion
  224.0 2.5 add_convert_fusion.1
  226.5 15.3 %collective-permute-done.34.refs_5_ = bf16[2,192,1408]{2,1,0:T(8,128)(2,1)S(1)} collective-permute-done((bf16[2,192,1408]{2,1,0:T(8,128)(2,1)}, bf16[2,192,1408]{2,1,0:T(8,128)(2,1)S(1)}, u32[]{:S(2)}, u32[]{:S(2)}) %collective-permute-start.34) | collective-permute-done | bytes 1081376 | tf_op jit(solution)/shard_map/ppermute | solution.py:161
  245.6 21.4 %collective-permute-done.37 = f32[8,768]{1,0:T(8,128)S(1)} collective-permute-done((f32[8,768]{1,0:T(8,128)S(1)}, f32[8,768]{1,0:T(8,128)S(1)}, u32[]{:S(2)}, u32[]{:S(2)}) %collective-permute-start.37) | collective-permute-done | bytes 24608 | tf_op jit(solution)/shard_map/ppermute | solution.py:161
  267.6 3.2 collective-permute-done.38
  273.4 8.2 %mid.1 = (bf16[192,1408]{1,0:T(8,128)(2,1)}, bf16[192,1408]{1,0:T(8,128)(2,1)}, bf16[2,192,1408]{2,1,0:T(8,128)(2,1)}, bf16[2,192,1408]{2,1,0:T(8,128)(2,1)}, f32[192,8]{1,0:T(8,128)}) custom-call(s32[24]{0:T(128)} %stack.147.m, bf16[2,192,1408]{2,1,0:T(8,128)(2,1)} %get-tuple-element.202.refs_0_, bf16[2,192,1408]{2,1,0:T(8,128)(2,1)} %copy-done.14, ...), custom_call_target="tpu_custom_call" | custom-call | bytes 13006848 | tf_op jit(solution)/shard_map/mid/pallas_call | solution.py:61
  287.6 3.9 collective-permute-done.55
  292.4 16.2 %collective-permute-done.39.refs_0_.refs_2_ = bf16[2,192,1408]{2,1,0:T(8,128)(2,1)S(1)} collective-permute-done((bf16[2,192,1408]{2,1,0:T(8,128)(2,1)}, bf16[2,192,1408]{2,1,0:T(8,128)(2,1)S(1)}, u32[]{:S(2)}, u32[]{:S(2)}) %collective-permute-start.39) | collective-permute-done | bytes 1081376 | tf_op jit(solution)/shard_map/ppermute | solution.py:161
  308.7 19.3 %collective-permute-done.41.refs_2_.refs_6_ = bf16[2,192,1408]{2,1,0:T(8,128)(2,1)S(1)} collective-permute-done((bf16[2,192,1408]{2,1,0:T(8,128)(2,1)}, bf16[2,192,1408]{2,1,0:T(8,128)(2,1)S(1)}, u32[]{:S(2)}, u32[]{:S(2)}) %collective-permute-start.41) | collective-permute-done | bytes 1081376 | tf_op jit(solution)/shard_map/ppermute | solution.py:161
  334.3 11.0 %dx.3 = (bf16[2,192,256]{2,1,0:T(8,128)(2,1)}, bf16[2,192,256]{2,1,0:T(8,128)(2,1)}) custom-call(s32[24]{0:T(128)} %stack.147.m, bf16[2,192,1408]{2,1,0:T(8,128)(2,1)} %get-tuple-element.215.refs_0_, bf16[2,192,1408]{2,1,0:T(8,128)(2,1)} %collective-permute-done.40.refs_1_, bf16[2,192,1408]{2,1,0:T(8,128)(2,1)} %get-tuple-element.216.refs_4_.refs_2_, ...), custom_call_target="tpu_custom_call" | custom-call | flops 4429185024 | bytes 16302080 | tf_op jit(solution)/shard_map/dx/pallas_call | solution.py:61
  348.4 4.6 collective-permute-done.57
  354.2 11.1 %dx.2 = (bf16[2,192,256]{2,1,0:T(8,128)(2,1)}, bf16[2,192,256]{2,1,0:T(8,128)(2,1)}) custom-call(s32[24]{0:T(128)} %stack.147.m, bf16[2,192,1408]{2,1,0:T(8,128)(2,1)} %copy-done.10, bf16[2,192,1408]{2,1,0:T(8,128)(2,1)} %collective-permute-done.43.refs_1_.refs_3_, bf16[2,192,1408]{2,1,0:T(8,128)(2,1)} %copy-done.11, ...), custom_call_target="tpu_custom_call" | custom-call | flops 4429185024 | bytes 16302080 | tf_op jit(solution)/shard_map/dx/pallas_call | solution.py:61
  367.3 6.1 collective-permute-done.45
  374.4 3.8 collective-permute-start.53
  382.3 11.3 %dwin.2 = (bf16[4,256,1408]{2,1,0:T(8,128)(2,1)}, bf16[4,256,1408]{2,1,0:T(8,128)(2,1)}) custom-call(s32[24]{0:T(128)} %stack.147.m, bf16[2,192,1408]{2,1,0:T(8,128)(2,1)} %get-tuple-element.215.refs_0_, bf16[2,192,1408]{2,1,0:T(8,128)(2,1)} %collective-permute-done.40.refs_1_, bf16[2,192,1408]{2,1,0:T(8,128)(2,1)} %copy-done.10, ...), custom_call_target="tpu_custom_call" | custom-call | flops 4429185024 | bytes 15228928 | tf_op jit(solution)/shard_map/dwin/pallas_call | solution.py:61
  396.8 2.5 collective-permute-done.52.refs_1_
  402.1 6.5 %norm_back.1 = (f32[2,768,256]{2,1,0:T(8,128)}, bf16[2,768,256]{2,1,0:T(8,128)(2,1)}, f32[5,2,256]{2,1,0:T(2,128)}) custom-call(s32[24]{0:T(128)} %stack.147.m, bf16[2,192,256]{2,1,0:T(8,128)(2,1)} %copy-done.22, bf16[2,192,256]{2,1,0:T(8,128)(2,1)} %copy-done.51, bf16[2,192,256]{2,1,0:T(8,128)(2,1)} %copy-done.23, bf16[2,192,256]{2,1,0:T(8,128)(2,1)} %copy-done.52, ...), custom_call_target="tpu_custom_call" | custom-call | bytes 5550080 | tf_op jit(solution)/shard_map/norm_back/pallas_call | solution.py:61
  408.6 6.1 dmix.1
  418.9 11.3 %dwin.3 = (bf16[4,256,1408]{2,1,0:T(8,128)(2,1)}, bf16[4,256,1408]{2,1,0:T(8,128)(2,1)}) custom-call(s32[24]{0:T(128)} %stack.147.m, bf16[2,192,1408]{2,1,0:T(8,128)(2,1)} %get-tuple-element.215.refs_0_, bf16[2,192,1408]{2,1,0:T(8,128)(2,1)} %collective-permute-done.40.refs_1_, bf16[2,192,1408]{2,1,0:T(8,128)(2,1)} %copy-done.10, ...), custom_call_target="tpu_custom_call" | custom-call | flops 4429185024 | bytes 15228928 | tf_op jit(solution)/shard_map/dwin/pallas_call | solution.py:61
  432.3 3.8 collective-permute-done.63.refs_9_
  438.4 14.4 %attend_back.1 = (bf16[768,256]{1,0:T(8,128)(2,1)}, f32[768,256]{1,0:T(8,128)}, f32[256,256]{1,0:T(8,128)}, f32[8,768]{1,0:T(8,128)}) custom-call(s32[24]{0:T(128)} %stack.147.m, bf16[768,256]{1,0:T(8,128)(2,1)} %get-tuple-element.177.q_ref.refs_0_, bf16[768,256]{1,0:T(8,128)(2,1)} %get-tuple-element.178.kv_ref.refs_1_, bf16[256,256]{1,0:T(8,128)(2,1)} %copy-done.30, ...), custom_call_target="tpu_custom_call" | custom-call | flops 754974720 | bytes 4792320 | tf_op jit(solution)/shard_map/attend_back/pallas_call | solution.py:61
  459.0 3.6 dkv.1
  465.9 16.2 %down.1 = (bf16[2,384,256]{2,1,0:T(8,128)(2,1)}, bf16[2,384,256]{2,1,0:T(8,128)(2,1)}, bf16[4,1408,256]{2,1,0:T(8,128)(2,1)}, bf16[4,1408,256]{2,1,0:T(8,128)(2,1)}) custom-call(s32[24]{0:T(128)} %stack.147.m, bf16[192,1408]{1,0:T(8,128)(2,1)} %get-tuple-element.226.refs_0_, bf16[192,1408]{1,0:T(8,128)(2,1)} %copy-done.95, bf16[192,1408]{1,0:T(8,128)(2,1)} %copy-done.96, ...), custom_call_target="tpu_custom_call" | custom-call | flops 8858370048 | bytes 17457152 | tf_op jit(solution)/shard_map/down/pallas_call | solution.py:61
  484.2 7.8 %dwproj.1 = (bf16[4,512,256]{2,1,0:T(8,128)(2,1)}, bf16[4,512,256]{2,1,0:T(8,128)(2,1)}) custom-call(s32[24]{0:T(128)} %stack.147.m, bf16[768,128]{1,0:T(8,128)(2,1)} %get-tuple-element.186.refs_0_, bf16[768,128]{1,0:T(8,128)(2,1)} %copy-done.102, bf16[768,128]{1,0:T(8,128)(2,1)} %copy-done.104, bf16[768,128]{1,0:T(8,128)(2,1)} %copy-done.106, ...), custom_call_target="tpu_custom_call" | custom-call | flops 1610612736 | bytes 4481024 | tf_op jit(solution)/shard_map/dwproj/pallas_call | solution.py:61
  494.4 7.6 %dattn.1 = (bf16[2,384,256]{2,1,0:T(8,128)(2,1)}, bf16[2,384,256]{2,1,0:T(8,128)(2,1)}) custom-call(s32[24]{0:T(128)} %stack.147.m, bf16[768,256]{1,0:T(8,128)(2,1)} %get-tuple-element.254.refs_0_, bf16[768,256]{1,0:T(8,128)(2,1)} %copy-done.101, bf16[768,256]{1,0:T(8,128)(2,1)} %collective-permute-done.71.refs_2_, ...), custom_call_target="tpu_custom_call" | custom-call | flops 2415919104 | bytes 7102464 | tf_op jit(solution)/shard_map/dattn/pallas_call | solution.py:61
  503.6 8.3 %collective-permute-start.80 = (bf16[2,384,256]{2,1,0:T(8,128)(2,1)S(1)}, bf16[2,384,256]{2,1,0:T(8,128)(2,1)S(1)}, u32[]{:S(2)}, u32[]{:S(2)}) collective-permute-start(bf16[2,384,256]{2,1,0:T(8,128)(2,1)S(1)} %add_convert_fusion.6.refs_0_), channel_id=1, source_target_pairs={{0,1},{1,0},{2,3},{3,2},{4,5},{5,4},{6,7},{7,6},{8,9},{9,8},{10,11... | collective-permute-start | bytes 1179656 | tf_op jit(solution)/shard_map/ppermute | solution.py:176
  514.2 9.5 %dwqkv.1 = (bf16[4,256,512]{2,1,0:T(8,128)(2,1)}, bf16[4,256,512]{2,1,0:T(8,128)(2,1)}, bf16[2,256,512]{2,1,0:T(8,128)(2,1)}, bf16[2,256,512]{2,1,0:T(8,128)(2,1)}) custom-call(s32[24]{0:T(128)} %stack.147.m, bf16[768,256]{1,0:T(8,128)(2,1)} %get-tuple-element.254.refs_0_, bf16[768,256]{1,0:T(8,128)(2,1)} %copy-done.101, ...), custom_call_target="tpu_custom_call" | custom-call | flops 2415919104 | bytes 7102464 | tf_op jit(solution)/shard_map/dwqkv/pallas_call | solution.py:61
  524.5 3.4 finish.1
  530.5 4.4 unpack.2
  534.9 3.9 all-to-all-start.2
  540.9 10.4 %fold.1 = f32[4,256,2,1408]{3,2,1,0:T(2,128)} custom-call(s32[24]{0:T(128)} %stack.147.m, bf16[4,256,1408]{2,1,0:T(8,128)(2,1)} %get-tuple-element.224.refs_0_, bf16[4,256,1408]{2,1,0:T(8,128)(2,1)} %copy-done.6, bf16[4,256,1408]{2,1,0:T(8,128)(2,1)} %get-tuple-element.267.refs_2_, bf16[4,256,1408]{2,1,0:T(8,128)(2,1)} %collective-permute-done.73.refs_3_), custom_call_target="tpu_custom_call" | custom-call | bytes 23068672 | tf_op jit(solution)/shard_map/fold/pallas_call | solution.py:61
  551.3 2.9 all-to-all-done.2
  557.2 3.6 collective-permute-start.85
  569.5 7.1 %collective-permute-done.84.refs_1_ = bf16[2,384,256]{2,1,0:T(8,128)(2,1)S(1)} collective-permute-done((bf16[2,384,256]{2,1,0:T(8,128)(2,1)S(1)}, bf16[2,384,256]{2,1,0:T(8,128)(2,1)S(1)}, u32[]{:S(2)}, u32[]{:S(2)}) %collective-permute-start.84) | collective-permute-done | bytes 393248 | tf_op jit(solution)/shard_map/ppermute | solution.py:176
  577.4 5.9 norm_back_first.1
  586.5 4.5 unpack.3
  590.9 3.9 all-to-all-start.3
  594.8 5.9 convert_add_fusion
  603.9 7.6 %all-to-all-done.3 = bf16[8,288,256]{2,1,0:T(8,128)(2,1)S(1)} async-done(((bf16[8,288,256]{2,1,0:T(8,128)(2,1)}), bf16[8,288,256]{2,1,0:T(8,128)(2,1)S(1)}, u32[]{:S(2)}, u32[]{:S(2)}) %all-to-all-start.3) | async-done | bytes 1179680 | tf_op jit(solution)/shard_map/all_to_all | solution.py:1204
  (504 shorter events, 152.3 us)
Async XLA Ops:
  6.7 34.8 %collective-permute-start.1 = (bf16[4,2,256,1408]{3,2,1,0:T(8,128)(2,1)}, bf16[4,2,256,1408]{3,2,1,0:T(8,128)(2,1)}, u32[]{:S(2)}, u32[]{:S(2)}) collective-permute-start(bf16[4,2,256,1408]{3,2,1,0:T(8,128)(2,1)} %bitcast.97.refs_2_.refs_4_), channel_id=1, source_target_pairs={{0,4},{4,0},{8,12},{12,8},{16,20},{20,16},{24,28},{28,24},{1,5},{5... | collective-permute-start | bytes 17301512 | tf_op jit(solution)/shard_map/ppermute | solution.py:165
  7.2 34.3 %collective-permute-start = (bf16[4,1408,256]{2,1,0:T(8,128)(2,1)}, bf16[4,1408,256]{2,1,0:T(8,128)(2,1)}, u32[]{:S(2)}, u32[]{:S(2)}) collective-permute-start(bf16[4,1408,256]{2,1,0:T(8,128)(2,1)} %refs_11_.2), channel_id=1, source_target_pairs={{0,4},{4,0},{8,12},{12,8},{16,20},{20,16},{24,28},{28,24},{1,5},{5... | collective-permute-start | bytes 8650760 | tf_op jit(solution)/shard_map/ppermute | solution.py:165
  7.2 30.2 %collective-permute-start.2 = (bf16[4,512,256]{2,1,0:T(8,128)(2,1)S(1)}, bf16[4,512,256]{2,1,0:T(8,128)(2,1)}, u32[]{:S(2)}, u32[]{:S(2)}) collective-permute-start(bf16[4,512,256]{2,1,0:T(8,128)(2,1)S(1)} %copy-done.92), channel_id=1, source_target_pairs={{0,4},{4,0},{8,12},{12,8},{16,20},{20,16},{24,28},{28,24},{1,5},{5... | collective-permute-start | bytes 3145736 | tf_op jit(solution)/shard_map/ppermute | solution.py:165
  9.3 20.3 %all-to-all-start = ((bf16[8,256,256]{2,1,0:T(8,128)(2,1)}), bf16[8,256,256]{2,1,0:T(8,128)(2,1)S(1)}, u32[]{:S(2)}, u32[]{:S(2)}) async-start(bf16[8,256,256]{2,1,0:T(8,128)(2,1)} %bitcast.99), calls=%async_computation | async-start | bytes 2097152 | tf_op jit(solution)/shard_map/all_to_all | solution.py:308
  14.2 27.3 %collective-permute-start.4 = (bf16[4,256,512]{2,1,0:T(8,128)(2,1)}, bf16[4,256,512]{2,1,0:T(8,128)(2,1)}, u32[]{:S(2)}, u32[]{:S(2)}) collective-permute-start(bf16[4,256,512]{2,1,0:T(8,128)(2,1)} %refs_9_.3), channel_id=1, source_target_pairs={{0,4},{4,0},{8,12},{12,8},{16,20},{20,16},{24,28},{28,24},{1,5},{5... | collective-permute-start | bytes 3145736 | tf_op jit(solution)/shard_map/ppermute | solution.py:165
  14.7 26.8 %collective-permute-start.5 = (bf16[2,256,512]{2,1,0:T(8,128)(2,1)}, bf16[2,256,512]{2,1,0:T(8,128)(2,1)}, u32[]{:S(2)}, u32[]{:S(2)}) collective-permute-start(bf16[2,256,512]{2,1,0:T(8,128)(2,1)} %refs_11_.3), channel_id=1, source_target_pairs={{0,4},{4,0},{8,12},{12,8},{16,20},{20,16},{24,28},{28,24},{1,5},{5... | collective-permute-start | bytes 1572872 | tf_op jit(solution)/shard_map/ppermute | solution.py:165
  29.6 41.4 %all-to-all-start.1 = ((bf16[8,256,256]{2,1,0:T(8,128)(2,1)}), bf16[8,256,256]{2,1,0:T(8,128)(2,1)S(1)}, u32[]{:S(2)}, u32[]{:S(2)}) async-start(bf16[8,256,256]{2,1,0:T(8,128)(2,1)} %bitcast.98), calls=%async_computation.1 | async-start | bytes 2097152 | tf_op jit(solution)/shard_map/all_to_all | solution.py:406
  58.5 17.7 %collective-permute-start.9 = (bf16[768,256]{1,0:T(8,128)(2,1)}, bf16[768,256]{1,0:T(8,128)(2,1)S(1)}, u32[]{:S(2)}, u32[]{:S(2)}) collective-permute-start(bf16[768,256]{1,0:T(8,128)(2,1)} %get-tuple-element.171), channel_id=1, source_target_pairs={{0,16},{4,20},{8,24},{12,28},{16,0},{20,4},{24,8},{28,12},{1,17},{... | collective-permute-start | bytes 1179656 | tf_op jit(solution)/shard_map/ppermute | solution.py:161
  58.9 12.2 %collective-permute-start.6 = (bf16[768,256]{1,0:T(8,128)(2,1)}, bf16[768,256]{1,0:T(8,128)(2,1)S(1)}, u32[]{:S(2)}, u32[]{:S(2)}) collective-permute-start(bf16[768,256]{1,0:T(8,128)(2,1)} %get-tuple-element.161), channel_id=1, source_target_pairs={{0,8},{4,12},{8,0},{12,4},{16,24},{20,28},{24,16},{28,20},{1,9},{5... | collective-permute-start | bytes 1179656 | tf_op jit(solution)/shard_map/ppermute | solution.py:161
  60.5 16.6 %collective-permute-start.10 = (bf16[768,256]{1,0:T(8,128)(2,1)}, bf16[768,256]{1,0:T(8,128)(2,1)S(1)}, u32[]{:S(2)}, u32[]{:S(2)}) collective-permute-start(bf16[768,256]{1,0:T(8,128)(2,1)} %get-tuple-element.172), channel_id=1, source_target_pairs={{0,16},{4,20},{8,24},{12,28},{16,0},{20,4},{24,8},{28,12},{1,17},{... | collective-permute-start | bytes 1179656 | tf_op jit(solution)/shard_map/ppermute | solution.py:161
  62.0 15.1 %collective-permute-start.8 = (bf16[768,256]{1,0:T(8,128)(2,1)}, bf16[768,256]{1,0:T(8,128)(2,1)S(1)}, u32[]{:S(2)}, u32[]{:S(2)}) collective-permute-start(bf16[768,256]{1,0:T(8,128)(2,1)} %get-tuple-element.168), channel_id=1, source_target_pairs={{0,8},{4,12},{8,0},{12,4},{16,24},{20,28},{24,16},{28,20},{1,9},{5... | collective-permute-start | bytes 1179656 | tf_op jit(solution)/shard_map/ppermute | solution.py:161
  77.1 16.0 %collective-permute-start.13 = (bf16[768,256]{1,0:T(8,128)(2,1)S(1)}, bf16[768,256]{1,0:T(8,128)(2,1)S(1)}, u32[]{:S(2)}, u32[]{:S(2)}) collective-permute-start(bf16[768,256]{1,0:T(8,128)(2,1)S(1)} %add_convert_fusion.11), channel_id=1, source_target_pairs={{0,16},{4,20},{8,24},{12,28},{16,0},{20,4},{24,8},{28,12},{1,17},{... | collective-permute-start | bytes 1179656 | tf_op jit(solution)/shard_map/ppermute | solution.py:161
  78.9 14.3 %collective-permute-start.14 = (bf16[768,256]{1,0:T(8,128)(2,1)S(1)}, bf16[768,256]{1,0:T(8,128)(2,1)S(1)}, u32[]{:S(2)}, u32[]{:S(2)}) collective-permute-start(bf16[768,256]{1,0:T(8,128)(2,1)S(1)} %add_convert_fusion.10), channel_id=1, source_target_pairs={{0,8},{4,12},{8,0},{12,4},{16,24},{20,28},{24,16},{28,20},{1,9},{5... | collective-permute-start | bytes 1179656 | tf_op jit(solution)/shard_map/ppermute | solution.py:161
  138.8 15.1 %collective-permute-start.21 = (bf16[192,1408]{1,0:T(8,128)(2,1)S(1)}, bf16[192,1408]{1,0:T(8,128)(2,1)S(1)}, u32[]{:S(2)}, u32[]{:S(2)}) collective-permute-start(bf16[192,1408]{1,0:T(8,128)(2,1)S(1)} %copy-done.100), channel_id=1, source_target_pairs={{0,16},{4,20},{8,24},{12,28},{16,0},{20,4},{24,8},{28,12},{1,17},{... | collective-permute-start | bytes 1622024 | tf_op jit(solution)/shard_map/ppermute | solution.py:161
  139.8 15.1 %collective-permute-start.20 = (bf16[192,1408]{1,0:T(8,128)(2,1)S(1)}, bf16[192,1408]{1,0:T(8,128)(2,1)S(1)}, u32[]{:S(2)}, u32[]{:S(2)}) collective-permute-start(bf16[192,1408]{1,0:T(8,128)(2,1)S(1)} %copy-done.99), channel_id=1, source_target_pairs={{0,8},{4,12},{8,0},{12,4},{16,24},{20,28},{24,16},{28,20},{1,9},{5... | collective-permute-start | bytes 1622024 | tf_op jit(solution)/shard_map/ppermute | solution.py:161
  140.8 23.5 %collective-permute-start.22 = (bf16[192,1408]{1,0:T(8,128)(2,1)S(1)}, bf16[192,1408]{1,0:T(8,128)(2,1)S(1)}, u32[]{:S(2)}, u32[]{:S(2)}) collective-permute-start(bf16[192,1408]{1,0:T(8,128)(2,1)S(1)} %copy-done.98), channel_id=1, source_target_pairs={{0,8},{4,12},{8,0},{12,4},{16,24},{20,28},{24,16},{28,20},{1,9},{5... | collective-permute-start | bytes 1622024 | tf_op jit(solution)/shard_map/ppermute | solution.py:161
  141.9 22.5 %collective-permute-start.23 = (bf16[192,1408]{1,0:T(8,128)(2,1)S(1)}, bf16[192,1408]{1,0:T(8,128)(2,1)S(1)}, u32[]{:S(2)}, u32[]{:S(2)}) collective-permute-start(bf16[192,1408]{1,0:T(8,128)(2,1)S(1)} %copy-done.97), channel_id=1, source_target_pairs={{0,16},{4,20},{8,24},{12,28},{16,0},{20,4},{24,8},{28,12},{1,17},{... | collective-permute-start | bytes 1622024 | tf_op jit(solution)/shard_map/ppermute | solution.py:161
  164.4 19.7 %collective-permute-start.28 = (bf16[192,1408]{1,0:T(8,128)(2,1)S(1)}, bf16[192,1408]{1,0:T(8,128)(2,1)S(1)}, u32[]{:S(2)}, u32[]{:S(2)}) collective-permute-start(bf16[192,1408]{1,0:T(8,128)(2,1)S(1)} %add_convert_fusion.3), channel_id=1, source_target_pairs={{0,16},{4,20},{8,24},{12,28},{16,0},{20,4},{24,8},{28,12},{1,17},{... | collective-permute-start | bytes 1622024 | tf_op jit(solution)/shard_map/ppermute | solution.py:161
  165.5 18.6 %collective-permute-start.29 = (bf16[192,1408]{1,0:T(8,128)(2,1)S(1)}, bf16[192,1408]{1,0:T(8,128)(2,1)S(1)}, u32[]{:S(2)}, u32[]{:S(2)}) collective-permute-start(bf16[192,1408]{1,0:T(8,128)(2,1)S(1)} %add_convert_fusion.2), channel_id=1, source_target_pairs={{0,8},{4,12},{8,0},{12,4},{16,24},{20,28},{24,16},{28,20},{1,9},{5... | collective-permute-start | bytes 1622024 | tf_op jit(solution)/shard_map/ppermute | solution.py:161
  166.8 12.1 %collective-permute-start.30 = (bf16[2,384,256]{2,1,0:T(8,128)(2,1)S(1)}, bf16[2,384,256]{2,1,0:T(8,128)(2,1)S(1)}, u32[]{:S(2)}, u32[]{:S(2)}) collective-permute-start(bf16[2,384,256]{2,1,0:T(8,128)(2,1)S(1)} %add_convert_fusion.8.refs_0_), channel_id=1, source_target_pairs={{0,1},{1,0},{2,3},{3,2},{4,5},{5,4},{6,7},{7,6},{8,9},{9,8},{10,11... | collective-permute-start | bytes 1179656 | tf_op jit(solution)/shard_map/ppermute | solution.py:176
  194.2 27.1 %collective-permute-start.33 = (bf16[2,192,1408]{2,1,0:T(8,128)(2,1)}, bf16[2,192,1408]{2,1,0:T(8,128)(2,1)}, u32[]{:S(2)}, u32[]{:S(2)}) collective-permute-start(bf16[2,192,1408]{2,1,0:T(8,128)(2,1)} %get-tuple-element.206), channel_id=1, source_target_pairs={{0,16},{4,20},{8,24},{12,28},{16,0},{20,4},{24,8},{28,12},{1,17},{... | collective-permute-start | bytes 3244040 | tf_op jit(solution)/shard_map/ppermute | solution.py:161
  195.3 28.7 %collective-permute-start.32 = (bf16[2,192,1408]{2,1,0:T(8,128)(2,1)}, bf16[2,192,1408]{2,1,0:T(8,128)(2,1)}, u32[]{:S(2)}, u32[]{:S(2)}) collective-permute-start(bf16[2,192,1408]{2,1,0:T(8,128)(2,1)} %get-tuple-element.200), channel_id=1, source_target_pairs={{0,8},{4,12},{8,0},{12,4},{16,24},{20,28},{24,16},{28,20},{1,9},{5... | collective-permute-start | bytes 3244040 | tf_op jit(solution)/shard_map/ppermute | solution.py:161
  206.3 35.5 %collective-permute-start.34 = (bf16[2,192,1408]{2,1,0:T(8,128)(2,1)}, bf16[2,192,1408]{2,1,0:T(8,128)(2,1)S(1)}, u32[]{:S(2)}, u32[]{:S(2)}) collective-permute-start(bf16[2,192,1408]{2,1,0:T(8,128)(2,1)} %get-tuple-element.207), channel_id=1, source_target_pairs={{0,16},{4,20},{8,24},{12,28},{16,0},{20,4},{24,8},{28,12},{1,17},{... | collective-permute-start | bytes 3244040 | tf_op jit(solution)/shard_map/ppermute | solution.py:161
  207.4 34.8 %collective-permute-start.31 = (bf16[2,192,1408]{2,1,0:T(8,128)(2,1)}, bf16[2,192,1408]{2,1,0:T(8,128)(2,1)S(1)}, u32[]{:S(2)}, u32[]{:S(2)}) collective-permute-start(bf16[2,192,1408]{2,1,0:T(8,128)(2,1)} %get-tuple-element.203), channel_id=1, source_target_pairs={{0,8},{4,12},{8,0},{12,4},{16,24},{20,28},{24,16},{28,20},{1,9},{5... | collective-permute-start | bytes 3244040 | tf_op jit(solution)/shard_map/ppermute | solution.py:161
  242.2 30.3 %collective-permute-start.35 = (bf16[2,192,1408]{2,1,0:T(8,128)(2,1)}, bf16[2,192,1408]{2,1,0:T(8,128)(2,1)S(1)}, u32[]{:S(2)}, u32[]{:S(2)}) collective-permute-start(bf16[2,192,1408]{2,1,0:T(8,128)(2,1)} %add_convert_fusion.1), channel_id=1, source_target_pairs={{0,16},{4,20},{8,24},{12,28},{16,0},{20,4},{24,8},{28,12},{1,17},{... | collective-permute-start | bytes 3244040 | tf_op jit(solution)/shard_map/ppermute | solution.py:161
  243.5 28.9 %collective-permute-start.36 = (bf16[2,192,1408]{2,1,0:T(8,128)(2,1)}, bf16[2,192,1408]{2,1,0:T(8,128)(2,1)}, u32[]{:S(2)}, u32[]{:S(2)}) collective-permute-start(bf16[2,192,1408]{2,1,0:T(8,128)(2,1)} %add_convert_fusion), channel_id=1, source_target_pairs={{0,8},{4,12},{8,0},{12,4},{16,24},{20,28},{24,16},{28,20},{1,9},{5... | collective-permute-start | bytes 3244040 | tf_op jit(solution)/shard_map/ppermute | solution.py:161
  244.0 23.0 %collective-permute-start.37 = (f32[8,768]{1,0:T(8,128)S(1)}, f32[8,768]{1,0:T(8,128)S(1)}, u32[]{:S(2)}, u32[]{:S(2)}) collective-permute-start(f32[8,768]{1,0:T(8,128)S(1)} %copy-done.78), channel_id=1, source_target_pairs={{0,8},{4,12},{8,0},{12,4},{16,24},{20,28},{24,16},{28,20},{1,9},{5... | collective-permute-start | bytes 73736 | tf_op jit(solution)/shard_map/ppermute | solution.py:161
  281.7 27.0 %collective-permute-start.39 = (bf16[2,192,1408]{2,1,0:T(8,128)(2,1)}, bf16[2,192,1408]{2,1,0:T(8,128)(2,1)S(1)}, u32[]{:S(2)}, u32[]{:S(2)}) collective-permute-start(bf16[2,192,1408]{2,1,0:T(8,128)(2,1)} %get-tuple-element.215.refs_0_), channel_id=1, source_target_pairs={{0,16},{4,20},{8,24},{12,28},{16,0},{20,4},{24,8},{28,12},{1,17},{... | collective-permute-start | bytes 3244040 | tf_op jit(solution)/shard_map/ppermute | solution.py:161
  282.4 45.7 %collective-permute-start.41 = (bf16[2,192,1408]{2,1,0:T(8,128)(2,1)}, bf16[2,192,1408]{2,1,0:T(8,128)(2,1)S(1)}, u32[]{:S(2)}, u32[]{:S(2)}) collective-permute-start(bf16[2,192,1408]{2,1,0:T(8,128)(2,1)} %get-tuple-element.216.refs_4_.refs_2_), channel_id=1, source_target_pairs={{0,16},{4,20},{8,24},{12,28},{16,0},{20,4},{24,8},{28,12},{1,17},{... | collective-permute-start | bytes 3244040 | tf_op jit(solution)/shard_map/ppermute | solution.py:161
  283.8 44.3 %collective-permute-start.40 = (bf16[2,192,1408]{2,1,0:T(8,128)(2,1)}, bf16[2,192,1408]{2,1,0:T(8,128)(2,1)}, u32[]{:S(2)}, u32[]{:S(2)}) collective-permute-start(bf16[2,192,1408]{2,1,0:T(8,128)(2,1)} %get-tuple-element.215.refs_0_), channel_id=1, source_target_pairs={{0,8},{4,12},{8,0},{12,4},{16,24},{20,28},{24,16},{28,20},{1,9},{5... | collective-permute-start | bytes 3244040 | tf_op jit(solution)/shard_map/ppermute | solution.py:161
  284.0 46.4 %collective-permute-start.42 = (bf16[2,192,1408]{2,1,0:T(8,128)(2,1)}, bf16[2,192,1408]{2,1,0:T(8,128)(2,1)S(1)}, u32[]{:S(2)}, u32[]{:S(2)}) collective-permute-start(bf16[2,192,1408]{2,1,0:T(8,128)(2,1)} %get-tuple-element.216.refs_4_.refs_2_), channel_id=1, source_target_pairs={{0,8},{4,12},{8,0},{12,4},{16,24},{20,28},{24,16},{28,20},{1,9},{5... | collective-permute-start | bytes 3244040 | tf_op jit(solution)/shard_map/ppermute | solution.py:161
  292.4 40.2 %collective-permute-start.56 = (f32[8,192]{0,1:T(8,128)S(1)}, f32[8,192]{0,1:T(8,128)S(1)}, u32[]{:S(2)}, u32[]{:S(2)}) collective-permute-start(f32[8,192]{0,1:T(8,128)S(1)} %bitcast_add_fusion), channel_id=1, source_target_pairs={{0,3},{1,2},{2,1},{3,0},{4,7},{5,6},{6,5},{7,4},{8,11},{9,10},{10,... | collective-permute-start | bytes 18440 | tf_op jit(solution)/shard_map/ppermute | solution.py:176
  330.5 23.7 %collective-permute-start.43 = (bf16[2,192,1408]{2,1,0:T(8,128)(2,1)}, bf16[2,192,1408]{2,1,0:T(8,128)(2,1)}, u32[]{:S(2)}, u32[]{:S(2)}) collective-permute-start(bf16[2,192,1408]{2,1,0:T(8,128)(2,1)} %collective-permute-done.40.refs_1_), channel_id=1, source_target_pairs={{0,16},{4,20},{8,24},{12,28},{16,0},{20,4},{24,8},{28,12},{1,17},{... | collective-permute-start | bytes 3244040 | tf_op jit(solution)/shard_map/ppermute | solution.py:161
  331.0 23.2 %collective-permute-start.44 = (bf16[2,192,1408]{2,1,0:T(8,128)(2,1)S(1)}, bf16[2,192,1408]{2,1,0:T(8,128)(2,1)}, u32[]{:S(2)}, u32[]{:S(2)}) collective-permute-start(bf16[2,192,1408]{2,1,0:T(8,128)(2,1)S(1)} %collective-permute-done.41.refs_2_.refs_6_), channel_id=1, source_target_pairs={{0,8},{4,12},{8,0},{12,4},{16,24},{20,28},{24,16},{28,20},{1,9},{5... | collective-permute-start | bytes 3244040 | tf_op jit(solution)/shard_map/ppermute | solution.py:161
  332.6 20.4 %collective-permute-start.57 = (f32[8,192]{0,1:T(8,128)S(1)}, f32[8,192]{0,1:T(8,128)S(1)}, u32[]{:S(2)}, u32[]{:S(2)}) collective-permute-start(f32[8,192]{0,1:T(8,128)S(1)} %add.349), channel_id=1, source_target_pairs={{0,8},{4,12},{8,0},{12,4},{16,24},{20,28},{24,16},{28,20},{1,9},{5... | collective-permute-start | bytes 18440 | tf_op jit(solution)/shard_map/ppermute | solution.py:161
  353.1 12.2 %collective-permute-start.58 = (f32[2,8,192]{2,1,0:T(8,128)S(1)}, f32[2,8,192]{2,1,0:T(8,128)S(1)}, u32[]{:S(2)}, u32[]{:S(2)}) collective-permute-start(f32[2,8,192]{2,1,0:T(8,128)S(1)} %pad_maximum_fusion.4), channel_id=1, source_target_pairs={{0,16},{4,20},{8,24},{12,28},{16,0},{20,4},{24,8},{28,12},{1,17},{... | collective-permute-start | bytes 36872 | tf_op jit(solution)/shard_map/ppermute | solution.py:161
  354.1 13.1 %collective-permute-start.51 = (bf16[2,192,256]{2,1,0:T(8,128)(2,1)S(1)}, bf16[2,192,256]{2,1,0:T(8,128)(2,1)S(1)}, u32[]{:S(2)}, u32[]{:S(2)}) collective-permute-start(bf16[2,192,256]{2,1,0:T(8,128)(2,1)S(1)} %add_convert_fusion.16), channel_id=1, source_target_pairs={{0,3},{1,2},{2,1},{3,0},{4,7},{5,6},{6,5},{7,4},{8,11},{9,10},{10,... | collective-permute-start | bytes 589832 | tf_op jit(solution)/shard_map/ppermute | solution.py:176
  374.4 19.2 %collective-permute-start.53 = (bf16[2,192,256]{2,1,0:T(8,128)(2,1)S(1)}, bf16[2,192,256]{2,1,0:T(8,128)(2,1)S(1)}, u32[]{:S(2)}, u32[]{:S(2)}) collective-permute-start(bf16[2,192,256]{2,1,0:T(8,128)(2,1)S(1)} %add_convert_fusion.17), channel_id=1, source_target_pairs={{0,3},{1,2},{2,1},{3,0},{4,7},{5,6},{6,5},{7,4},{8,11},{9,10},{10,... | collective-permute-start | bytes 589832 | tf_op jit(solution)/shard_map/ppermute | solution.py:176
  378.2 15.5 %collective-permute-start.46 = (bf16[192,1408]{1,0:T(8,128)(2,1)S(1)}, bf16[192,1408]{1,0:T(8,128)(2,1)S(1)}, u32[]{:S(2)}, u32[]{:S(2)}) collective-permute-start(bf16[192,1408]{1,0:T(8,128)(2,1)S(1)} %copy-done.93), channel_id=1, source_target_pairs={{0,8},{4,12},{8,0},{12,4},{16,24},{20,28},{24,16},{28,20},{1,9},{5... | collective-permute-start | bytes 1622024 | tf_op jit(solution)/shard_map/ppermute | solution.py:161
  378.4 18.4 %collective-permute-start.47 = (bf16[192,1408]{1,0:T(8,128)(2,1)S(1)}, bf16[192,1408]{1,0:T(8,128)(2,1)S(1)}, u32[]{:S(2)}, u32[]{:S(2)}) collective-permute-start(bf16[192,1408]{1,0:T(8,128)(2,1)S(1)} %copy-done.93), channel_id=1, source_target_pairs={{0,16},{4,20},{8,24},{12,28},{16,0},{20,4},{24,8},{28,12},{1,17},{... | collective-permute-start | bytes 1622024 | tf_op jit(solution)/shard_map/ppermute | solution.py:161
  380.1 16.7 %collective-permute-start.48 = (bf16[192,1408]{1,0:T(8,128)(2,1)S(1)}, bf16[192,1408]{1,0:T(8,128)(2,1)}, u32[]{:S(2)}, u32[]{:S(2)}) collective-permute-start(bf16[192,1408]{1,0:T(8,128)(2,1)S(1)} %copy-done.94), channel_id=1, source_target_pairs={{0,8},{4,12},{8,0},{12,4},{16,24},{20,28},{24,16},{28,20},{1,9},{5... | collective-permute-start | bytes 1622024 | tf_op jit(solution)/shard_map/ppermute | solution.py:161
  381.9 14.9 %collective-permute-start.49 = (bf16[192,1408]{1,0:T(8,128)(2,1)S(1)}, bf16[192,1408]{1,0:T(8,128)(2,1)}, u32[]{:S(2)}, u32[]{:S(2)}) collective-permute-start(bf16[192,1408]{1,0:T(8,128)(2,1)S(1)} %copy-done.94), channel_id=1, source_target_pairs={{0,16},{4,20},{8,24},{12,28},{16,0},{20,4},{24,8},{28,12},{1,17},{... | collective-permute-start | bytes 1622024 | tf_op jit(solution)/shard_map/ppermute | solution.py:161
  414.7 15.5 %collective-permute-start.61 = (bf16[768,128]{1,0:T(8,128)(2,1)}, bf16[768,128]{1,0:T(8,128)(2,1)S(1)}, u32[]{:S(2)}, u32[]{:S(2)}) collective-permute-start(bf16[768,128]{1,0:T(8,128)(2,1)} %get-tuple-element.245), channel_id=1, source_target_pairs={{0,16},{4,20},{8,24},{12,28},{16,0},{20,4},{24,8},{28,12},{1,17},{... | collective-permute-start | bytes 589832 | tf_op jit(solution)/shard_map/ppermute | solution.py:161
  416.4 13.8 %collective-permute-start.60 = (bf16[768,128]{1,0:T(8,128)(2,1)}, bf16[768,128]{1,0:T(8,128)(2,1)S(1)}, u32[]{:S(2)}, u32[]{:S(2)}) collective-permute-start(bf16[768,128]{1,0:T(8,128)(2,1)} %get-tuple-element.243), channel_id=1, source_target_pairs={{0,8},{4,12},{8,0},{12,4},{16,24},{20,28},{24,16},{28,20},{1,9},{5... | collective-permute-start | bytes 589832 | tf_op jit(solution)/shard_map/ppermute | solution.py:161
  416.7 13.7 %collective-permute-start.59 = (bf16[768,128]{1,0:T(8,128)(2,1)}, bf16[768,128]{1,0:T(8,128)(2,1)S(1)}, u32[]{:S(2)}, u32[]{:S(2)}) collective-permute-start(bf16[768,128]{1,0:T(8,128)(2,1)} %get-tuple-element.241), channel_id=1, source_target_pairs={{0,8},{4,12},{8,0},{12,4},{16,24},{20,28},{24,16},{28,20},{1,9},{5... | collective-permute-start | bytes 589832 | tf_op jit(solution)/shard_map/ppermute | solution.py:161
  418.5 11.9 %collective-permute-start.62 = (bf16[768,128]{1,0:T(8,128)(2,1)}, bf16[768,128]{1,0:T(8,128)(2,1)S(1)}, u32[]{:S(2)}, u32[]{:S(2)}) collective-permute-start(bf16[768,128]{1,0:T(8,128)(2,1)} %get-tuple-element.246), channel_id=1, source_target_pairs={{0,16},{4,20},{8,24},{12,28},{16,0},{20,4},{24,8},{28,12},{1,17},{... | collective-permute-start | bytes 589832 | tf_op jit(solution)/shard_map/ppermute | solution.py:161
  432.3 51.9 %collective-permute-start.72 = (bf16[4,256,1408]{2,1,0:T(8,128)(2,1)}, bf16[4,256,1408]{2,1,0:T(8,128)(2,1)S(1)}, u32[]{:S(2)}, u32[]{:S(2)}) collective-permute-start(bf16[4,256,1408]{2,1,0:T(8,128)(2,1)} %get-tuple-element.265), channel_id=1, source_target_pairs={{0,4},{4,0},{8,12},{12,8},{16,20},{20,16},{24,28},{28,24},{1,5},{5... | collective-permute-start | bytes 8650760 | tf_op jit(solution)/shard_map/ppermute | solution.py:165
  437.8 46.5 %collective-permute-start.73 = (bf16[4,256,1408]{2,1,0:T(8,128)(2,1)}, bf16[4,256,1408]{2,1,0:T(8,128)(2,1)}, u32[]{:S(2)}, u32[]{:S(2)}) collective-permute-start(bf16[4,256,1408]{2,1,0:T(8,128)(2,1)} %get-tuple-element.268), channel_id=1, source_target_pairs={{0,4},{4,0},{8,12},{12,8},{16,20},{20,16},{24,28},{28,24},{1,5},{5... | collective-permute-start | bytes 8650760 | tf_op jit(solution)/shard_map/ppermute | solution.py:165
  437.8 16.9 %collective-permute-start.66 = (bf16[192,1408]{1,0:T(8,128)(2,1)}, bf16[192,1408]{1,0:T(8,128)(2,1)}, u32[]{:S(2)}, u32[]{:S(2)}) collective-permute-start(bf16[192,1408]{1,0:T(8,128)(2,1)} %copy-done.95), channel_id=1, source_target_pairs={{0,16},{4,20},{8,24},{12,28},{16,0},{20,4},{24,8},{28,12},{1,17},{... | collective-permute-start | bytes 1622024 | tf_op jit(solution)/shard_map/ppermute | solution.py:161
  438.2 17.8 %collective-permute-start.67 = (bf16[192,1408]{1,0:T(8,128)(2,1)}, bf16[192,1408]{1,0:T(8,128)(2,1)}, u32[]{:S(2)}, u32[]{:S(2)}) collective-permute-start(bf16[192,1408]{1,0:T(8,128)(2,1)} %collective-permute-done.49.refs_6_), channel_id=1, source_target_pairs={{0,8},{4,12},{8,0},{12,4},{16,24},{20,28},{24,16},{28,20},{1,9},{5... | collective-permute-start | bytes 1622024 | tf_op jit(solution)/shard_map/ppermute | solution.py:161
  456.0 26.0 %collective-permute-start.71 = (bf16[768,256]{1,0:T(8,128)(2,1)}, bf16[768,256]{1,0:T(8,128)(2,1)}, u32[]{:S(2)}, u32[]{:S(2)}) collective-permute-start(bf16[768,256]{1,0:T(8,128)(2,1)} %get-tuple-element.254.refs_0_), channel_id=1, source_target_pairs={{0,16},{4,20},{8,24},{12,28},{16,0},{20,4},{24,8},{28,12},{1,17},{... | collective-permute-start | bytes 1179656 | tf_op jit(solution)/shard_map/ppermute | solution.py:161
  462.6 19.6 %collective-permute-start.69 = (bf16[768,256]{1,0:T(8,128)(2,1)}, bf16[768,256]{1,0:T(8,128)(2,1)}, u32[]{:S(2)}, u32[]{:S(2)}) collective-permute-start(bf16[768,256]{1,0:T(8,128)(2,1)} %get-tuple-element.260.refs_4_), channel_id=1, source_target_pairs={{0,16},{4,20},{8,24},{12,28},{16,0},{20,4},{24,8},{28,12},{1,17},{... | collective-permute-start | bytes 1179656 | tf_op jit(solution)/shard_map/ppermute | solution.py:161
  464.3 17.9 %collective-permute-start.70 = (bf16[768,256]{1,0:T(8,128)(2,1)}, bf16[768,256]{1,0:T(8,128)(2,1)}, u32[]{:S(2)}, u32[]{:S(2)}) collective-permute-start(bf16[768,256]{1,0:T(8,128)(2,1)} %get-tuple-element.260.refs_4_), channel_id=1, source_target_pairs={{0,8},{4,12},{8,0},{12,4},{16,24},{20,28},{24,16},{28,20},{1,9},{5... | collective-permute-start | bytes 1179656 | tf_op jit(solution)/shard_map/ppermute | solution.py:161
  482.2 12.1 %collective-permute-start.74 = (bf16[768,256]{1,0:T(8,128)(2,1)}, bf16[768,256]{1,0:T(8,128)(2,1)}, u32[]{:S(2)}, u32[]{:S(2)}) collective-permute-start(bf16[768,256]{1,0:T(8,128)(2,1)} %copy-done.101), channel_id=1, source_target_pairs={{0,16},{4,20},{8,24},{12,28},{16,0},{20,4},{24,8},{28,12},{1,17},{... | collective-permute-start | bytes 1179656 | tf_op jit(solution)/shard_map/ppermute | solution.py:161
  492.8 20.2 %collective-permute-start.76 = (f32[8,768]{1,0:T(8,128)S(1)}, f32[8,768]{1,0:T(8,128)S(1)}, u32[]{:S(2)}, u32[]{:S(2)}) collective-permute-start(f32[8,768]{1,0:T(8,128)S(1)} %select_add_fusion), channel_id=1, source_target_pairs={{0,8},{4,12},{8,0},{12,4},{16,24},{20,28},{24,16},{28,20},{1,9},{5... | collective-permute-start | bytes 73736 | tf_op jit(solution)/shard_map/ppermute | solution.py:161
  503.6 20.1 %collective-permute-start.80 = (bf16[2,384,256]{2,1,0:T(8,128)(2,1)S(1)}, bf16[2,384,256]{2,1,0:T(8,128)(2,1)S(1)}, u32[]{:S(2)}, u32[]{:S(2)}) collective-permute-start(bf16[2,384,256]{2,1,0:T(8,128)(2,1)S(1)} %add_convert_fusion.6.refs_0_), channel_id=1, source_target_pairs={{0,1},{1,0},{2,3},{3,2},{4,5},{5,4},{6,7},{7,6},{8,9},{9,8},{10,11... | collective-permute-start | bytes 1179656 | tf_op jit(solution)/shard_map/ppermute | solution.py:176
  527.8 67.0 %collective-permute-start.91 = (bf16[4,1408,256]{2,1,0:T(8,128)(2,1)}, bf16[4,1408,256]{2,1,0:T(8,128)(2,1)}, u32[]{:S(2)}, u32[]{:S(2)}) collective-permute-start(bf16[4,1408,256]{2,1,0:T(8,128)(2,1)} %get-tuple-element.304), channel_id=1, source_target_pairs={{0,4},{4,0},{8,12},{12,8},{16,20},{20,16},{24,28},{28,24},{1,5},{5... | collective-permute-start | bytes 8650760 | tf_op jit(solution)/shard_map/ppermute | solution.py:165
  534.9 19.3 %all-to-all-start.2 = ((bf16[8,256,256]{2,1,0:T(8,128)(2,1)}), bf16[8,256,256]{2,1,0:T(8,128)(2,1)S(1)}, u32[]{:S(2)}, u32[]{:S(2)}) async-start(bf16[8,256,256]{2,1,0:T(8,128)(2,1)} %unpack.2), calls=%async_computation.2 | async-start | bytes 2097152 | tf_op jit(solution)/shard_map/all_to_all | solution.py:1204
  539.7 16.4 %collective-permute-start.83 = (bf16[2,384,256]{2,1,0:T(8,128)(2,1)S(1)}, bf16[2,384,256]{2,1,0:T(8,128)(2,1)}, u32[]{:S(2)}, u32[]{:S(2)}) collective-permute-start(bf16[2,384,256]{2,1,0:T(8,128)(2,1)S(1)} %add_convert_fusion.5), channel_id=1, source_target_pairs={{0,3},{1,2},{2,1},{3,0},{4,7},{5,6},{6,5},{7,4},{8,11},{9,10},{10,... | collective-permute-start | bytes 1179656 | tf_op jit(solution)/shard_map/ppermute | solution.py:176
  564.8 19.1 %collective-permute-start.88 = (bf16[2,256,512]{2,1,0:T(8,128)(2,1)}, bf16[2,256,512]{2,1,0:T(8,128)(2,1)S(1)}, u32[]{:S(2)}, u32[]{:S(2)}) collective-permute-start(bf16[2,256,512]{2,1,0:T(8,128)(2,1)} %get-tuple-element.301), channel_id=1, source_target_pairs={{0,4},{4,0},{8,12},{12,8},{16,20},{20,16},{24,28},{28,24},{1,5},{5... | collective-permute-start | bytes 1572872 | tf_op jit(solution)/shard_map/ppermute | solution.py:165
  564.8 11.8 %collective-permute-start.84 = (bf16[2,384,256]{2,1,0:T(8,128)(2,1)S(1)}, bf16[2,384,256]{2,1,0:T(8,128)(2,1)S(1)}, u32[]{:S(2)}, u32[]{:S(2)}) collective-permute-start(bf16[2,384,256]{2,1,0:T(8,128)(2,1)S(1)} %add_convert_fusion.4.refs_0_), channel_id=1, source_target_pairs={{0,1},{1,0},{2,3},{3,2},{4,5},{5,4},{6,7},{7,6},{8,9},{9,8},{10,11... | collective-permute-start | bytes 1179656 | tf_op jit(solution)/shard_map/ppermute | solution.py:176
  583.3 17.5 %collective-permute-start.90 = (bf16[4,512,256]{2,1,0:T(8,128)(2,1)}, bf16[4,512,256]{2,1,0:T(8,128)(2,1)S(1)}, u32[]{:S(2)}, u32[]{:S(2)}) collective-permute-start(bf16[4,512,256]{2,1,0:T(8,128)(2,1)} %get-tuple-element.303), channel_id=1, source_target_pairs={{0,4},{4,0},{8,12},{12,8},{16,20},{20,16},{24,28},{28,24},{1,5},{5... | collective-permute-start | bytes 3145736 | tf_op jit(solution)/shard_map/ppermute | solution.py:165
  583.8 18.5 %collective-permute-start.89 = (bf16[4,256,512]{2,1,0:T(8,128)(2,1)}, bf16[4,256,512]{2,1,0:T(8,128)(2,1)S(1)}, u32[]{:S(2)}, u32[]{:S(2)}) collective-permute-start(bf16[4,256,512]{2,1,0:T(8,128)(2,1)} %get-tuple-element.302), channel_id=1, source_target_pairs={{0,4},{4,0},{8,12},{12,8},{16,20},{20,16},{24,28},{28,24},{1,5},{5... | collective-permute-start | bytes 3145736 | tf_op jit(solution)/shard_map/ppermute | solution.py:165
  590.9 20.7 %all-to-all-start.3 = ((bf16[8,288,256]{2,1,0:T(8,128)(2,1)}), bf16[8,288,256]{2,1,0:T(8,128)(2,1)S(1)}, u32[]{:S(2)}, u32[]{:S(2)}) async-start(bf16[8,288,256]{2,1,0:T(8,128)(2,1)} %unpack.3), calls=%async_computation.3 | async-start | bytes 2359296 | tf_op jit(solution)/shard_map/all_to_all | solution.py:1204
  (140 other events, 2029.8 us)

commit v8 on v7

--- a/solution.py
+++ b/solution.py
@@ -395,11 +395,11 @@
     outs = [((rp, 2 * HD), BF16, (tile, 2 * HD), lambda i, m: (i, 0))] * 8
     outs += [((8, rp), F32, (8, tile), lambda i, m: (0, i))]
     qkv = run(
-        qkv_body, "qkv", (rp // tile,), after(meta, wo[1:], wi[1:], wp[1:]), ins, outs,
+        qkv_body, "qkv", (rp // tile,), after(meta, wo[1:], wp[1:]), ins, outs,
         [pltpu.VMEM((heads, tile, 4 * HD), BF16)],
         flops=2 * rp * (experts + 2) * parts * ds * hw,
     )
-    stats_a = sum_groups(qkv[8])
+    stats_a = sum_groups(after(qkv[8], wi[1:]))
     flat_a, cols_a = gate_columns(stats_a, low_a, high_a)
     q_sum, kv_sum, _, far = reduce_groups(qkv[0:8:2], qkv[1:8:2], late=cols_a)
 
@@ -1140,8 +1140,6 @@
     da_half = z_covered(*da_halves, 1, dwqkv_sums[0])
 
     down_half = z_covered(*down_halves, 1, dwproj_sums[0])
-    down_half = z_covered(down_half, down_half, 3, da_halves[0])
-    down_totals = z_last(down_half)
 
     def finish_body(m, *refs):
         t_refs, after_ref, outs = refs[:2], refs[2], refs[3:]
@@ -1153,9 +1151,13 @@
                     after_ref[s, span_k, :] + total.astype(F32)
                 ).astype(BF16)
 
+    got_q, got_kv = exchange(dwqkv_sums[:parts]), exchange(dwqkv_sums[parts:])
+    dots_a = sum_z(dots_a)
+    back_a = back_columns(flat_a, dots_a, low_a, high_a)
+    down_totals = z_last(z_covered(down_half, down_half, 3, da_half))
     ins = [(t, None, None) for t in down_totals] + [(after_rows, None, None)]
     out_rows = run(
-        finish_body, "finish", (1,), after(meta, dwqkv_sums[0], dots_a), ins,
+        finish_body, "finish", (1,), after(meta, dots_a), ins,
         [((rp, ds), BF16, None, None)] * parts,
     )
 
@@ -1205,13 +1207,10 @@
         rows_of = landed[:, :count].transpose(1, 0, 2).reshape(seqs, per, width)
         return rows_of, spread_rows, landed[:, count:]
 
+    da_half = z_covered(da_half, da_half, 3, out_rows[0])
+    expertin_grad = fold(got_in, after(meta, da_half))
     layer_out, layer_rows, _ = unpack(out_rows, x_all, False, table)
-    got_q, got_kv = exchange(dwqkv_sums[:parts]), exchange(dwqkv_sums[parts:])
-    expertin_grad = fold(got_in, after(meta, layer_rows))
-    da_half = z_covered(da_half, da_half, 3, (expertin_grad, layer_out))
     da_totals = z_last(da_half)
-    dots_a = sum_z(after(dots_a, da_half))
-    back_a = back_columns(flat_a, dots_a, low_a, high_a)
     ins = [(t, None, None) for t in da_totals]
     ins += [(x_stack, None, None), (dafter, None, None)]
     ins += [(gain_a, None, None), (router_a, None, None), (back_a, None, None)]
@@ -1219,7 +1218,7 @@
     outs += [((experts + 1, parts, ds), F32, None, None)]
     *dinput, small_a = run(
         functools.partial(norm_back_body, False), "norm_back_first", (1,),
-        meta, ins, outs,
+        after(meta, expertin_grad), ins, outs,
     )
     expertout_grad, proj_grad = add_up(got_out), add_up(got_proj)
     query_grad, kv_grad = add_up(got_q), add_up(got_kv)

time: 621 us -> 628 us (1.011)
    unnamed x220 -> x222, local copies, waits for them, and re-layouts: 17.9 us -> 17.8 us
where the time goes in v8:
time: 628 us; the launch traced here: 622 us
  Pallas kernels  229 us (36%)
  waiting for transfers between devices  201 us (32%)
  starting transfers between devices  118 us (19%)
  local copies, waits for them, and re-layouts  37.2 us (6%)
  other arithmetic  32.7 us (5%)
    pallas_call x28, Pallas kernels, run(): pl.pallas_call(body, name=name, grid_spec=pltpu.PrefetchScalarGridSpec(nu...  229 us
    ppermute x56, waiting for transfers between devices, by_group(): return lax.ppermute(value, 'dp', pairs)  131 us
    ppermute x56, starting transfers between devices, by_group(): return lax.ppermute(value, 'dp', pairs)  61.5 us
    ppermute x19, waiting for transfers between devices, by_z(): return lax.ppermute(value, 'tensor', [(a, a ^ mask) for a in range(tp)])  51.7 us
    ppermute x19, starting transfers between devices, by_z(): return lax.ppermute(value, 'tensor', [(a, a ^ mask) for a in range(tp)])  34.4 us
    unnamed x222, local copies, waits for them, and re-layouts  17.8 us
    add x4, other arithmetic, add_up(): return sum((v.astype(F32) for v in got))  12.6 us
  transfers between devices with their start and end apart: 96, of which 40 were waited for; matrix products, arithmetic and copies ran while one was open for 8% of the time, Pallas kernels for 28%

profile of v8, /device:TPU:0, one launch (start us, length us, event | category | flops | bytes accessed | tf_op | source)
XLA Modules:
  0.0 622.4 jit_solution(15602247379365014408)
XLA Ops:
  0.7 6.1 copy.230
  9.3 5.0 all-to-all-start
  18.9 10.7 %all-to-all-done = bf16[8,256,256]{2,1,0:T(8,128)(2,1)S(1)} async-done(((bf16[8,256,256]{2,1,0:T(8,128)(2,1)}), bf16[8,256,256]{2,1,0:T(8,128)(2,1)S(1)}, u32[]{:S(2)}, u32[]{:S(2)}) %all-to-all-start) | async-done | bytes 1048608 | tf_op jit(solution)/shard_map/all_to_all | solution.py:308
  29.6 3.8 all-to-all-start.1
  33.4 4.0 pack.2
  42.2 8.4 %qkv.1 = (bf16[768,256]{1,0:T(8,128)(2,1)}, bf16[768,256]{1,0:T(8,128)(2,1)}, bf16[768,256]{1,0:T(8,128)(2,1)}, bf16[768,256]{1,0:T(8,128)(2,1)}, bf16[768,256]{...) custom-call(s32[24]{0:T(128)} %stack.147.m, ...), custom_call_target="tpu_custom_call" | custom-call | flops 2415919104 | bytes 7137280 | tf_op jit(solution)/shard_map/qkv/pallas_call | solution.py:61
  57.5 5.5 collective-permute-done.5
  63.9 4.1 pack.3
  81.5 12.0 %dhidden.1 = (bf16[192,1408]{1,0:T(8,128)(2,1)}, bf16[192,1408]{1,0:T(8,128)(2,1)}, bf16[192,1408]{1,0:T(8,128)(2,1)}, bf16[192,1408]{1,0:T(8,128)(2,1)}, bf16[1...) custom-call(s32[24]{0:T(128)} %stack.147.m, ...), custom_call_target="tpu_custom_call" | custom-call | flops 4429185024 | bytes 11714560 | tf_op jit(solution)/shard_map/dhidden/pallas_call | solution.py:61
  94.4 4.6 rope.1
  102.8 7.9 %attend.1 = (bf16[768,128]{1,0:T(8,128)(2,1)}, bf16[768,128]{1,0:T(8,128)(2,1)}, bf16[768,128]{1,0:T(8,128)(2,1)}, bf16[768,128]{1,0:T(8,128)(2,1)}) custom-call(s32[24]{0:T(128)} %stack.147.m, bf16[768,256]{1,0:T(8,128)(2,1)} %get-tuple-element.179.q_ref.refs_0_, bf16[768,256]{1,0:T(8,128)(2,1)} %get-tuple-element.180.kv_ref.refs_1_, ...), custom_call_target="tpu_custom_call" | custom-call | flops 301989888 | bytes 1753088 | tf_op jit(solution)/shard_map/attend/pallas_call | solution.py:61
  115.0 3.8 collective-permute-done.16.refs_1_
  120.9 2.7 collective-permute-done.24.refs_2_
  123.7 3.3 collective-permute-done.17.refs_3_
  127.7 9.9 %proj.1 = (bf16[2,384,256]{2,1,0:T(8,128)(2,1)}, bf16[2,384,256]{2,1,0:T(8,128)(2,1)}) custom-call(s32[24]{0:T(128)} %stack.147.m, bf16[768,128]{1,0:T(8,128)(2,1)} %get-tuple-element.188.refs_0_, bf16[768,128]{1,0:T(8,128)(2,1)} %copy-done.103, bf16[768,128]{1,0:T(8,128)(2,1)} %copy-done.105, bf16[768,128]{1,0:T(8,128)(2,1)} %copy-done.107, ...), custom_call_target="tpu_custom_call" | custom-call | flops 1610612736 | bytes 4481024 | tf_op jit(solution)/shard_map/proj/pallas_call | solution.py:61
  143.2 4.9 collective-permute-done.26
  149.2 3.7 collective-permute-start.27
  154.8 6.0 collective-permute-done.27
  160.9 3.2 collective-permute-done.22.refs_7_
  167.2 3.9 collective-permute-start.30
  172.3 6.9 %collective-permute-done.30.refs_1_ = bf16[2,384,256]{2,1,0:T(8,128)(2,1)S(1)} collective-permute-done((bf16[2,384,256]{2,1,0:T(8,128)(2,1)S(1)}, bf16[2,384,256]{2,1,0:T(8,128)(2,1)S(1)}, u32[]{:S(2)}, u32[]{:S(2)}) %collective-permute-start.30) | collective-permute-done | bytes 393248 | tf_op jit(solution)/shard_map/ppermute | solution.py:176
  179.9 4.4 norm.1
  184.3 10.2 %up.2 = (bf16[2,192,1408]{2,1,0:T(8,128)(2,1)}, bf16[2,192,1408]{2,1,0:T(8,128)(2,1)}, bf16[2,192,1408]{2,1,0:T(8,128)(2,1)}, bf16[2,192,1408]{2,1,0:T(8,128)(2,1)}) custom-call(s32[24]{0:T(128)} %stack.147.m, bf16[2,768,256]{2,1,0:T(8,128)(2,1)} %get-tuple-element.201.refs_0_.refs_1_, bf16[2,768,256]{2,1,0:T(8,128)(2,1)} %get-tuple-element.201.refs_0_.refs_1_, ...), custom_call_target="tpu_custom_call" | custom-call | flops 4429185024 | bytes 17481728 | tf_op jit(solution)/shard_map/up/pallas_call | solution.py:61
  196.4 10.3 %up.3 = (bf16[2,192,1408]{2,1,0:T(8,128)(2,1)}, bf16[2,192,1408]{2,1,0:T(8,128)(2,1)}, bf16[2,192,1408]{2,1,0:T(8,128)(2,1)}, bf16[2,192,1408]{2,1,0:T(8,128)(2,1)}) custom-call(s32[24]{0:T(128)} %stack.147.m, bf16[2,768,256]{2,1,0:T(8,128)(2,1)} %get-tuple-element.201.refs_0_.refs_1_, bf16[2,768,256]{2,1,0:T(8,128)(2,1)} %get-tuple-element.201.refs_0_.refs_1_, ...), custom_call_target="tpu_custom_call" | custom-call | flops 4429185024 | bytes 17481728 | tf_op jit(solution)/shard_map/up/pallas_call | solution.py:61
  209.0 12.7 %collective-permute-done.33 = bf16[2,192,1408]{2,1,0:T(8,128)(2,1)} collective-permute-done((bf16[2,192,1408]{2,1,0:T(8,128)(2,1)}, bf16[2,192,1408]{2,1,0:T(8,128)(2,1)}, u32[]{:S(2)}, u32[]{:S(2)}) %collective-permute-start.33) | collective-permute-done | bytes 1081376 | tf_op jit(solution)/shard_map/ppermute | solution.py:161
  226.8 15.3 %collective-permute-done.34.refs_5_ = bf16[2,192,1408]{2,1,0:T(8,128)(2,1)S(1)} collective-permute-done((bf16[2,192,1408]{2,1,0:T(8,128)(2,1)}, bf16[2,192,1408]{2,1,0:T(8,128)(2,1)S(1)}, u32[]{:S(2)}, u32[]{:S(2)}) %collective-permute-start.34) | collective-permute-done | bytes 1081376 | tf_op jit(solution)/shard_map/ppermute | solution.py:161
  245.9 21.4 %collective-permute-done.37 = f32[8,768]{1,0:T(8,128)S(1)} collective-permute-done((f32[8,768]{1,0:T(8,128)S(1)}, f32[8,768]{1,0:T(8,128)S(1)}, u32[]{:S(2)}, u32[]{:S(2)}) %collective-permute-start.37) | collective-permute-done | bytes 24608 | tf_op jit(solution)/shard_map/ppermute | solution.py:161
  267.8 3.2 collective-permute-done.38
  273.7 8.2 %mid.1 = (bf16[192,1408]{1,0:T(8,128)(2,1)}, bf16[192,1408]{1,0:T(8,128)(2,1)}, bf16[2,192,1408]{2,1,0:T(8,128)(2,1)}, bf16[2,192,1408]{2,1,0:T(8,128)(2,1)}, f32[192,8]{1,0:T(8,128)}) custom-call(s32[24]{0:T(128)} %stack.147.m, bf16[2,192,1408]{2,1,0:T(8,128)(2,1)} %get-tuple-element.204.refs_0_, bf16[2,192,1408]{2,1,0:T(8,128)(2,1)} %copy-done.14, ...), custom_call_target="tpu_custom_call" | custom-call | bytes 13006848 | tf_op jit(solution)/shard_map/mid/pallas_call | solution.py:61
  287.9 3.9 collective-permute-done.55
  292.7 16.2 %collective-permute-done.39.refs_0_.refs_2_ = bf16[2,192,1408]{2,1,0:T(8,128)(2,1)S(1)} collective-permute-done((bf16[2,192,1408]{2,1,0:T(8,128)(2,1)}, bf16[2,192,1408]{2,1,0:T(8,128)(2,1)S(1)}, u32[]{:S(2)}, u32[]{:S(2)}) %collective-permute-start.39) | collective-permute-done | bytes 1081376 | tf_op jit(solution)/shard_map/ppermute | solution.py:161
  309.0 19.3 %collective-permute-done.41.refs_2_.refs_6_ = bf16[2,192,1408]{2,1,0:T(8,128)(2,1)S(1)} collective-permute-done((bf16[2,192,1408]{2,1,0:T(8,128)(2,1)}, bf16[2,192,1408]{2,1,0:T(8,128)(2,1)S(1)}, u32[]{:S(2)}, u32[]{:S(2)}) %collective-permute-start.41) | collective-permute-done | bytes 1081376 | tf_op jit(solution)/shard_map/ppermute | solution.py:161
  334.6 11.0 %dx.3 = (bf16[2,192,256]{2,1,0:T(8,128)(2,1)}, bf16[2,192,256]{2,1,0:T(8,128)(2,1)}) custom-call(s32[24]{0:T(128)} %stack.147.m, bf16[2,192,1408]{2,1,0:T(8,128)(2,1)} %get-tuple-element.217.refs_0_, bf16[2,192,1408]{2,1,0:T(8,128)(2,1)} %collective-permute-done.40.refs_1_, bf16[2,192,1408]{2,1,0:T(8,128)(2,1)} %get-tuple-element.218.refs_4_.refs_2_, ...), custom_call_target="tpu_custom_call" | custom-call | flops 4429185024 | bytes 16302080 | tf_op jit(solution)/shard_map/dx/pallas_call | solution.py:61
  348.7 4.6 collective-permute-done.57
  354.4 11.1 %dx.2 = (bf16[2,192,256]{2,1,0:T(8,128)(2,1)}, bf16[2,192,256]{2,1,0:T(8,128)(2,1)}) custom-call(s32[24]{0:T(128)} %stack.147.m, bf16[2,192,1408]{2,1,0:T(8,128)(2,1)} %copy-done.10, bf16[2,192,1408]{2,1,0:T(8,128)(2,1)} %collective-permute-done.43.refs_1_.refs_3_, bf16[2,192,1408]{2,1,0:T(8,128)(2,1)} %copy-done.11, ...), custom_call_target="tpu_custom_call" | custom-call | flops 4429185024 | bytes 16302080 | tf_op jit(solution)/shard_map/dx/pallas_call | solution.py:61
  367.6 6.0 collective-permute-done.45
  374.6 3.8 collective-permute-start.53
  382.5 11.3 %dwin.2 = (bf16[4,256,1408]{2,1,0:T(8,128)(2,1)}, bf16[4,256,1408]{2,1,0:T(8,128)(2,1)}) custom-call(s32[24]{0:T(128)} %stack.147.m, bf16[2,192,1408]{2,1,0:T(8,128)(2,1)} %get-tuple-element.217.refs_0_, bf16[2,192,1408]{2,1,0:T(8,128)(2,1)} %collective-permute-done.40.refs_1_, bf16[2,192,1408]{2,1,0:T(8,128)(2,1)} %copy-done.10, ...), custom_call_target="tpu_custom_call" | custom-call | flops 4429185024 | bytes 15228928 | tf_op jit(solution)/shard_map/dwin/pallas_call | solution.py:61
  402.3 6.5 %norm_back.1 = (f32[2,768,256]{2,1,0:T(8,128)}, bf16[2,768,256]{2,1,0:T(8,128)(2,1)}, f32[5,2,256]{2,1,0:T(2,128)}) custom-call(s32[24]{0:T(128)} %stack.147.m, bf16[2,192,256]{2,1,0:T(8,128)(2,1)} %copy-done.22, bf16[2,192,256]{2,1,0:T(8,128)(2,1)} %copy-done.51, bf16[2,192,256]{2,1,0:T(8,128)(2,1)} %copy-done.23, bf16[2,192,256]{2,1,0:T(8,128)(2,1)} %copy-done.52, ...), custom_call_target="tpu_custom_call" | custom-call | bytes 5550080 | tf_op jit(solution)/shard_map/norm_back/pallas_call | solution.py:61
  408.8 6.1 dmix.1
  419.1 11.3 %dwin.3 = (bf16[4,256,1408]{2,1,0:T(8,128)(2,1)}, bf16[4,256,1408]{2,1,0:T(8,128)(2,1)}) custom-call(s32[24]{0:T(128)} %stack.147.m, bf16[2,192,1408]{2,1,0:T(8,128)(2,1)} %get-tuple-element.217.refs_0_, bf16[2,192,1408]{2,1,0:T(8,128)(2,1)} %collective-permute-done.40.refs_1_, bf16[2,192,1408]{2,1,0:T(8,128)(2,1)} %copy-done.10, ...), custom_call_target="tpu_custom_call" | custom-call | flops 4429185024 | bytes 15228928 | tf_op jit(solution)/shard_map/dwin/pallas_call | solution.py:61
  433.1 3.2 collective-permute-done.63.refs_9_
  439.2 14.4 %attend_back.1 = (bf16[768,256]{1,0:T(8,128)(2,1)}, f32[768,256]{1,0:T(8,128)}, f32[256,256]{1,0:T(8,128)}, f32[8,768]{1,0:T(8,128)}) custom-call(s32[24]{0:T(128)} %stack.147.m, bf16[768,256]{1,0:T(8,128)(2,1)} %get-tuple-element.179.q_ref.refs_0_, bf16[768,256]{1,0:T(8,128)(2,1)} %get-tuple-element.180.kv_ref.refs_1_, bf16[256,256]{1,0:T(8,128)(2,1)} %copy-done.30, ...), custom_call_target="tpu_custom_call" | custom-call | flops 754974720 | bytes 4792320 | tf_op jit(solution)/shard_map/attend_back/pallas_call | solution.py:61
  459.3 3.6 dkv.1
  466.1 16.1 %down.1 = (bf16[2,384,256]{2,1,0:T(8,128)(2,1)}, bf16[2,384,256]{2,1,0:T(8,128)(2,1)}, bf16[4,1408,256]{2,1,0:T(8,128)(2,1)}, bf16[4,1408,256]{2,1,0:T(8,128)(2,1)}) custom-call(s32[24]{0:T(128)} %stack.147.m, bf16[192,1408]{1,0:T(8,128)(2,1)} %get-tuple-element.228.refs_0_, bf16[192,1408]{1,0:T(8,128)(2,1)} %copy-done.96, bf16[192,1408]{1,0:T(8,128)(2,1)} %copy-done.97, ...), custom_call_target="tpu_custom_call" | custom-call | flops 8858370048 | bytes 17457152 | tf_op jit(solution)/shard_map/down/pallas_call | solution.py:61
  486.1 7.7 %dwproj.1 = (bf16[4,512,256]{2,1,0:T(8,128)(2,1)}, bf16[4,512,256]{2,1,0:T(8,128)(2,1)}) custom-call(s32[24]{0:T(128)} %stack.147.m, bf16[768,128]{1,0:T(8,128)(2,1)} %get-tuple-element.188.refs_0_, bf16[768,128]{1,0:T(8,128)(2,1)} %copy-done.103, bf16[768,128]{1,0:T(8,128)(2,1)} %copy-done.105, bf16[768,128]{1,0:T(8,128)(2,1)} %copy-done.107, ...), custom_call_target="tpu_custom_call" | custom-call | flops 1610612736 | bytes 4481024 | tf_op jit(solution)/shard_map/dwproj/pallas_call | solution.py:61
  494.0 7.6 %dattn.1 = (bf16[2,384,256]{2,1,0:T(8,128)(2,1)}, bf16[2,384,256]{2,1,0:T(8,128)(2,1)}) custom-call(s32[24]{0:T(128)} %stack.147.m, bf16[768,256]{1,0:T(8,128)(2,1)} %get-tuple-element.263.refs_0_, bf16[768,256]{1,0:T(8,128)(2,1)} %copy-done.102, bf16[768,256]{1,0:T(8,128)(2,1)} %collective-permute-done.71.refs_2_, ...), custom_call_target="tpu_custom_call" | custom-call | flops 2415919104 | bytes 7102464 | tf_op jit(solution)/shard_map/dattn/pallas_call | solution.py:61
  504.0 9.4 %dwqkv.1 = (bf16[4,256,512]{2,1,0:T(8,128)(2,1)}, bf16[4,256,512]{2,1,0:T(8,128)(2,1)}, bf16[2,256,512]{2,1,0:T(8,128)(2,1)}, bf16[2,256,512]{2,1,0:T(8,128)(2,1)}) custom-call(s32[24]{0:T(128)} %stack.147.m, bf16[768,256]{1,0:T(8,128)(2,1)} %get-tuple-element.263.refs_0_, bf16[768,256]{1,0:T(8,128)(2,1)} %copy-done.102, ...), custom_call_target="tpu_custom_call" | custom-call | flops 2415919104 | bytes 7102464 | tf_op jit(solution)/shard_map/dwqkv/pallas_call | solution.py:61
  513.4 8.4 %collective-permute-done.82 = bf16[2,384,256]{2,1,0:T(8,128)(2,1)S(1)} collective-permute-done((bf16[2,384,256]{2,1,0:T(8,128)(2,1)}, bf16[2,384,256]{2,1,0:T(8,128)(2,1)S(1)}, u32[]{:S(2)}, u32[]{:S(2)}) %collective-permute-start.82) | collective-permute-done | bytes 393248 | tf_op jit(solution)/shard_map/ppermute | solution.py:176
  528.0 3.4 collective-permute-done.75
  531.8 3.4 collective-permute-done.76
  538.1 2.8 collective-permute-done.77
  543.5 3.3 finish.1
  546.9 4.7 collective-permute-done.85
  552.3 4.4 unpack.2
  556.7 3.9 all-to-all-start.2
  560.8 7.7 %collective-permute-start.86 = (bf16[2,384,256]{2,1,0:T(8,128)(2,1)S(1)}, bf16[2,384,256]{2,1,0:T(8,128)(2,1)S(1)}, u32[]{:S(2)}, u32[]{:S(2)}) collective-permute-start(bf16[2,384,256]{2,1,0:T(8,128)(2,1)S(1)} %add_convert_fusion.4.refs_0_), channel_id=1, source_target_pairs={{0,1},{1,0},{2,3},{3,2},{4,5},{5,4},{6,7},{7,6},{8,9},{9,8},{10,11... | collective-permute-start | bytes 1179656 | tf_op jit(solution)/shard_map/ppermute | solution.py:176
  569.5 10.4 %fold.1 = f32[4,256,2,1408]{3,2,1,0:T(2,128)} custom-call(s32[24]{0:T(128)} %stack.147.m, bf16[4,256,1408]{2,1,0:T(8,128)(2,1)} %get-tuple-element.226.refs_0_, bf16[4,256,1408]{2,1,0:T(8,128)(2,1)} %copy-done.6, bf16[4,256,1408]{2,1,0:T(8,128)(2,1)} %get-tuple-element.271.refs_2_, bf16[4,256,1408]{2,1,0:T(8,128)(2,1)} %collective-permute-done.73.refs_3_), custom_call_target="tpu_custom_call" | custom-call | bytes 23068672 | tf_op jit(solution)/shard_map/fold/pallas_call | solution.py:61
  580.7 5.9 norm_back_first.1
  592.9 4.5 unpack.3
  597.3 4.1 all-to-all-start.3
  601.5 5.9 convert_add_fusion
  607.4 2.8 convert_add_fusion.1
  611.9 6.3 %all-to-all-done.3 = bf16[8,288,256]{2,1,0:T(8,128)(2,1)S(1)} async-done(((bf16[8,288,256]{2,1,0:T(8,128)(2,1)}), bf16[8,288,256]{2,1,0:T(8,128)(2,1)S(1)}, u32[]{:S(2)}, u32[]{:S(2)}) %all-to-all-start.3) | async-done | bytes 1179680 | tf_op jit(solution)/shard_map/all_to_all | solution.py:1206
  (506 shorter events, 158.3 us)
Async XLA Ops:
  6.7 61.3 %collective-permute-start.10 = (bf16[4,2,256,1408]{3,2,1,0:T(8,128)(2,1)}, bf16[4,2,256,1408]{3,2,1,0:T(8,128)(2,1)}, u32[]{:S(2)}, u32[]{:S(2)}) collective-permute-start(bf16[4,2,256,1408]{3,2,1,0:T(8,128)(2,1)} %bitcast.97.refs_2_.refs_4_), channel_id=1, source_target_pairs={{0,4},{4,0},{8,12},{12,8},{16,20},{20,16},{24,28},{28,24},{1,5},{5... | collective-permute-start | bytes 17301512 | tf_op jit(solution)/shard_map/ppermute | solution.py:165
  7.2 34.3 %collective-permute-start = (bf16[4,1408,256]{2,1,0:T(8,128)(2,1)}, bf16[4,1408,256]{2,1,0:T(8,128)(2,1)}, u32[]{:S(2)}, u32[]{:S(2)}) collective-permute-start(bf16[4,1408,256]{2,1,0:T(8,128)(2,1)} %refs_11_.2), channel_id=1, source_target_pairs={{0,4},{4,0},{8,12},{12,8},{16,20},{20,16},{24,28},{28,24},{1,5},{5... | collective-permute-start | bytes 8650760 | tf_op jit(solution)/shard_map/ppermute | solution.py:165
  7.2 30.2 %collective-permute-start.1 = (bf16[4,512,256]{2,1,0:T(8,128)(2,1)S(1)}, bf16[4,512,256]{2,1,0:T(8,128)(2,1)}, u32[]{:S(2)}, u32[]{:S(2)}) collective-permute-start(bf16[4,512,256]{2,1,0:T(8,128)(2,1)S(1)} %copy-done.93), channel_id=1, source_target_pairs={{0,4},{4,0},{8,12},{12,8},{16,20},{20,16},{24,28},{28,24},{1,5},{5... | collective-permute-start | bytes 3145736 | tf_op jit(solution)/shard_map/ppermute | solution.py:165
  9.3 20.3 %all-to-all-start = ((bf16[8,256,256]{2,1,0:T(8,128)(2,1)}), bf16[8,256,256]{2,1,0:T(8,128)(2,1)S(1)}, u32[]{:S(2)}, u32[]{:S(2)}) async-start(bf16[8,256,256]{2,1,0:T(8,128)(2,1)} %bitcast.99), calls=%async_computation | async-start | bytes 2097152 | tf_op jit(solution)/shard_map/all_to_all | solution.py:308
  14.2 27.2 %collective-permute-start.3 = (bf16[4,256,512]{2,1,0:T(8,128)(2,1)}, bf16[4,256,512]{2,1,0:T(8,128)(2,1)}, u32[]{:S(2)}, u32[]{:S(2)}) collective-permute-start(bf16[4,256,512]{2,1,0:T(8,128)(2,1)} %refs_9_.3), channel_id=1, source_target_pairs={{0,4},{4,0},{8,12},{12,8},{16,20},{20,16},{24,28},{28,24},{1,5},{5... | collective-permute-start | bytes 3145736 | tf_op jit(solution)/shard_map/ppermute | solution.py:165
  14.7 26.7 %collective-permute-start.4 = (bf16[2,256,512]{2,1,0:T(8,128)(2,1)}, bf16[2,256,512]{2,1,0:T(8,128)(2,1)}, u32[]{:S(2)}, u32[]{:S(2)}) collective-permute-start(bf16[2,256,512]{2,1,0:T(8,128)(2,1)} %refs_11_.3), channel_id=1, source_target_pairs={{0,4},{4,0},{8,12},{12,8},{16,20},{20,16},{24,28},{28,24},{1,5},{5... | collective-permute-start | bytes 1572872 | tf_op jit(solution)/shard_map/ppermute | solution.py:165
  29.6 33.4 %all-to-all-start.1 = ((bf16[8,256,256]{2,1,0:T(8,128)(2,1)}), bf16[8,256,256]{2,1,0:T(8,128)(2,1)S(1)}, u32[]{:S(2)}, u32[]{:S(2)}) async-start(bf16[8,256,256]{2,1,0:T(8,128)(2,1)} %bitcast.98), calls=%async_computation.1 | async-start | bytes 2097152 | tf_op jit(solution)/shard_map/all_to_all | solution.py:406
  50.7 12.3 %collective-permute-start.5 = (bf16[768,256]{1,0:T(8,128)(2,1)}, bf16[768,256]{1,0:T(8,128)(2,1)S(1)}, u32[]{:S(2)}, u32[]{:S(2)}) collective-permute-start(bf16[768,256]{1,0:T(8,128)(2,1)} %get-tuple-element.162), channel_id=1, source_target_pairs={{0,8},{4,12},{8,0},{12,4},{16,24},{20,28},{24,16},{28,20},{1,9},{5... | collective-permute-start | bytes 1179656 | tf_op jit(solution)/shard_map/ppermute | solution.py:161
  52.4 21.2 %collective-permute-start.8 = (bf16[768,256]{1,0:T(8,128)(2,1)}, bf16[768,256]{1,0:T(8,128)(2,1)S(1)}, u32[]{:S(2)}, u32[]{:S(2)}) collective-permute-start(bf16[768,256]{1,0:T(8,128)(2,1)} %get-tuple-element.172), channel_id=1, source_target_pairs={{0,16},{4,20},{8,24},{12,28},{16,0},{20,4},{24,8},{28,12},{1,17},{... | collective-permute-start | bytes 1179656 | tf_op jit(solution)/shard_map/ppermute | solution.py:161
  56.6 20.9 %collective-permute-start.7 = (bf16[768,256]{1,0:T(8,128)(2,1)}, bf16[768,256]{1,0:T(8,128)(2,1)S(1)}, u32[]{:S(2)}, u32[]{:S(2)}) collective-permute-start(bf16[768,256]{1,0:T(8,128)(2,1)} %get-tuple-element.169), channel_id=1, source_target_pairs={{0,8},{4,12},{8,0},{12,4},{16,24},{20,28},{24,16},{28,20},{1,9},{5... | collective-permute-start | bytes 1179656 | tf_op jit(solution)/shard_map/ppermute | solution.py:161
  57.1 20.4 %collective-permute-start.9 = (bf16[768,256]{1,0:T(8,128)(2,1)}, bf16[768,256]{1,0:T(8,128)(2,1)S(1)}, u32[]{:S(2)}, u32[]{:S(2)}) collective-permute-start(bf16[768,256]{1,0:T(8,128)(2,1)} %get-tuple-element.173), channel_id=1, source_target_pairs={{0,16},{4,20},{8,24},{12,28},{16,0},{20,4},{24,8},{28,12},{1,17},{... | collective-permute-start | bytes 1179656 | tf_op jit(solution)/shard_map/ppermute | solution.py:161
  68.0 12.7 %collective-permute-start.6 = (bf16[768,256]{1,0:T(8,128)(2,1)}, bf16[768,256]{1,0:T(8,128)(2,1)S(1)}, u32[]{:S(2)}, u32[]{:S(2)}) collective-permute-start(bf16[768,256]{1,0:T(8,128)(2,1)} %get-tuple-element.165), channel_id=1, source_target_pairs={{0,4},{4,0},{8,12},{12,8},{16,20},{20,16},{24,28},{28,24},{1,5},{5... | collective-permute-start | bytes 1179656 | tf_op jit(solution)/shard_map/ppermute | solution.py:165
  77.5 16.0 %collective-permute-start.13 = (bf16[768,256]{1,0:T(8,128)(2,1)S(1)}, bf16[768,256]{1,0:T(8,128)(2,1)S(1)}, u32[]{:S(2)}, u32[]{:S(2)}) collective-permute-start(bf16[768,256]{1,0:T(8,128)(2,1)S(1)} %add_convert_fusion.11), channel_id=1, source_target_pairs={{0,16},{4,20},{8,24},{12,28},{16,0},{20,4},{24,8},{28,12},{1,17},{... | collective-permute-start | bytes 1179656 | tf_op jit(solution)/shard_map/ppermute | solution.py:161
  79.2 14.3 %collective-permute-start.14 = (bf16[768,256]{1,0:T(8,128)(2,1)S(1)}, bf16[768,256]{1,0:T(8,128)(2,1)S(1)}, u32[]{:S(2)}, u32[]{:S(2)}) collective-permute-start(bf16[768,256]{1,0:T(8,128)(2,1)S(1)} %add_convert_fusion.10), channel_id=1, source_target_pairs={{0,8},{4,12},{8,0},{12,4},{16,24},{20,28},{24,16},{28,20},{1,9},{5... | collective-permute-start | bytes 1179656 | tf_op jit(solution)/shard_map/ppermute | solution.py:161
  139.2 15.1 %collective-permute-start.21 = (bf16[192,1408]{1,0:T(8,128)(2,1)S(1)}, bf16[192,1408]{1,0:T(8,128)(2,1)S(1)}, u32[]{:S(2)}, u32[]{:S(2)}) collective-permute-start(bf16[192,1408]{1,0:T(8,128)(2,1)S(1)} %copy-done.101), channel_id=1, source_target_pairs={{0,16},{4,20},{8,24},{12,28},{16,0},{20,4},{24,8},{28,12},{1,17},{... | collective-permute-start | bytes 1622024 | tf_op jit(solution)/shard_map/ppermute | solution.py:161
  139.5 15.1 %collective-permute-start.20 = (bf16[192,1408]{1,0:T(8,128)(2,1)S(1)}, bf16[192,1408]{1,0:T(8,128)(2,1)S(1)}, u32[]{:S(2)}, u32[]{:S(2)}) collective-permute-start(bf16[192,1408]{1,0:T(8,128)(2,1)S(1)} %copy-done.100), channel_id=1, source_target_pairs={{0,8},{4,12},{8,0},{12,4},{16,24},{20,28},{24,16},{28,20},{1,9},{5... | collective-permute-start | bytes 1622024 | tf_op jit(solution)/shard_map/ppermute | solution.py:161
  141.2 22.9 %collective-permute-start.22 = (bf16[192,1408]{1,0:T(8,128)(2,1)S(1)}, bf16[192,1408]{1,0:T(8,128)(2,1)S(1)}, u32[]{:S(2)}, u32[]{:S(2)}) collective-permute-start(bf16[192,1408]{1,0:T(8,128)(2,1)S(1)} %copy-done.99), channel_id=1, source_target_pairs={{0,8},{4,12},{8,0},{12,4},{16,24},{20,28},{24,16},{28,20},{1,9},{5... | collective-permute-start | bytes 1622024 | tf_op jit(solution)/shard_map/ppermute | solution.py:161
  141.5 22.5 %collective-permute-start.23 = (bf16[192,1408]{1,0:T(8,128)(2,1)S(1)}, bf16[192,1408]{1,0:T(8,128)(2,1)S(1)}, u32[]{:S(2)}, u32[]{:S(2)}) collective-permute-start(bf16[192,1408]{1,0:T(8,128)(2,1)S(1)} %copy-done.98), channel_id=1, source_target_pairs={{0,16},{4,20},{8,24},{12,28},{16,0},{20,4},{24,8},{28,12},{1,17},{... | collective-permute-start | bytes 1622024 | tf_op jit(solution)/shard_map/ppermute | solution.py:161
  164.1 20.3 %collective-permute-start.28 = (bf16[192,1408]{1,0:T(8,128)(2,1)S(1)}, bf16[192,1408]{1,0:T(8,128)(2,1)S(1)}, u32[]{:S(2)}, u32[]{:S(2)}) collective-permute-start(bf16[192,1408]{1,0:T(8,128)(2,1)S(1)} %add_convert_fusion.3), channel_id=1, source_target_pairs={{0,16},{4,20},{8,24},{12,28},{16,0},{20,4},{24,8},{28,12},{1,17},{... | collective-permute-start | bytes 1622024 | tf_op jit(solution)/shard_map/ppermute | solution.py:161
  165.8 18.5 %collective-permute-start.29 = (bf16[192,1408]{1,0:T(8,128)(2,1)S(1)}, bf16[192,1408]{1,0:T(8,128)(2,1)S(1)}, u32[]{:S(2)}, u32[]{:S(2)}) collective-permute-start(bf16[192,1408]{1,0:T(8,128)(2,1)S(1)} %add_convert_fusion.2), channel_id=1, source_target_pairs={{0,8},{4,12},{8,0},{12,4},{16,24},{20,28},{24,16},{28,20},{1,9},{5... | collective-permute-start | bytes 1622024 | tf_op jit(solution)/shard_map/ppermute | solution.py:161
  167.2 12.0 %collective-permute-start.30 = (bf16[2,384,256]{2,1,0:T(8,128)(2,1)S(1)}, bf16[2,384,256]{2,1,0:T(8,128)(2,1)S(1)}, u32[]{:S(2)}, u32[]{:S(2)}) collective-permute-start(bf16[2,384,256]{2,1,0:T(8,128)(2,1)S(1)} %add_convert_fusion.8.refs_0_), channel_id=1, source_target_pairs={{0,1},{1,0},{2,3},{3,2},{4,5},{5,4},{6,7},{7,6},{8,9},{9,8},{10,11... | collective-permute-start | bytes 1179656 | tf_op jit(solution)/shard_map/ppermute | solution.py:176
  194.6 27.1 %collective-permute-start.33 = (bf16[2,192,1408]{2,1,0:T(8,128)(2,1)}, bf16[2,192,1408]{2,1,0:T(8,128)(2,1)}, u32[]{:S(2)}, u32[]{:S(2)}) collective-permute-start(bf16[2,192,1408]{2,1,0:T(8,128)(2,1)} %get-tuple-element.208), channel_id=1, source_target_pairs={{0,16},{4,20},{8,24},{12,28},{16,0},{20,4},{24,8},{28,12},{1,17},{... | collective-permute-start | bytes 3244040 | tf_op jit(solution)/shard_map/ppermute | solution.py:161
  195.6 28.7 %collective-permute-start.32 = (bf16[2,192,1408]{2,1,0:T(8,128)(2,1)}, bf16[2,192,1408]{2,1,0:T(8,128)(2,1)}, u32[]{:S(2)}, u32[]{:S(2)}) collective-permute-start(bf16[2,192,1408]{2,1,0:T(8,128)(2,1)} %get-tuple-element.202), channel_id=1, source_target_pairs={{0,8},{4,12},{8,0},{12,4},{16,24},{20,28},{24,16},{28,20},{1,9},{5... | collective-permute-start | bytes 3244040 | tf_op jit(solution)/shard_map/ppermute | solution.py:161
  206.6 35.4 %collective-permute-start.34 = (bf16[2,192,1408]{2,1,0:T(8,128)(2,1)}, bf16[2,192,1408]{2,1,0:T(8,128)(2,1)S(1)}, u32[]{:S(2)}, u32[]{:S(2)}) collective-permute-start(bf16[2,192,1408]{2,1,0:T(8,128)(2,1)} %get-tuple-element.209), channel_id=1, source_target_pairs={{0,16},{4,20},{8,24},{12,28},{16,0},{20,4},{24,8},{28,12},{1,17},{... | collective-permute-start | bytes 3244040 | tf_op jit(solution)/shard_map/ppermute | solution.py:161
  207.7 34.8 %collective-permute-start.31 = (bf16[2,192,1408]{2,1,0:T(8,128)(2,1)}, bf16[2,192,1408]{2,1,0:T(8,128)(2,1)S(1)}, u32[]{:S(2)}, u32[]{:S(2)}) collective-permute-start(bf16[2,192,1408]{2,1,0:T(8,128)(2,1)} %get-tuple-element.205), channel_id=1, source_target_pairs={{0,8},{4,12},{8,0},{12,4},{16,24},{20,28},{24,16},{28,20},{1,9},{5... | collective-permute-start | bytes 3244040 | tf_op jit(solution)/shard_map/ppermute | solution.py:161
  242.5 30.2 %collective-permute-start.35 = (bf16[2,192,1408]{2,1,0:T(8,128)(2,1)}, bf16[2,192,1408]{2,1,0:T(8,128)(2,1)S(1)}, u32[]{:S(2)}, u32[]{:S(2)}) collective-permute-start(bf16[2,192,1408]{2,1,0:T(8,128)(2,1)} %add_convert_fusion.1), channel_id=1, source_target_pairs={{0,16},{4,20},{8,24},{12,28},{16,0},{20,4},{24,8},{28,12},{1,17},{... | collective-permute-start | bytes 3244040 | tf_op jit(solution)/shard_map/ppermute | solution.py:161
  243.8 28.9 %collective-permute-start.36 = (bf16[2,192,1408]{2,1,0:T(8,128)(2,1)}, bf16[2,192,1408]{2,1,0:T(8,128)(2,1)}, u32[]{:S(2)}, u32[]{:S(2)}) collective-permute-start(bf16[2,192,1408]{2,1,0:T(8,128)(2,1)} %add_convert_fusion), channel_id=1, source_target_pairs={{0,8},{4,12},{8,0},{12,4},{16,24},{20,28},{24,16},{28,20},{1,9},{5... | collective-permute-start | bytes 3244040 | tf_op jit(solution)/shard_map/ppermute | solution.py:161
  244.6 22.6 %collective-permute-start.37 = (f32[8,768]{1,0:T(8,128)S(1)}, f32[8,768]{1,0:T(8,128)S(1)}, u32[]{:S(2)}, u32[]{:S(2)}) collective-permute-start(f32[8,768]{1,0:T(8,128)S(1)} %copy-done.78), channel_id=1, source_target_pairs={{0,8},{4,12},{8,0},{12,4},{16,24},{20,28},{24,16},{28,20},{1,9},{5... | collective-permute-start | bytes 73736 | tf_op jit(solution)/shard_map/ppermute | solution.py:161
  282.0 27.0 %collective-permute-start.39 = (bf16[2,192,1408]{2,1,0:T(8,128)(2,1)}, bf16[2,192,1408]{2,1,0:T(8,128)(2,1)S(1)}, u32[]{:S(2)}, u32[]{:S(2)}) collective-permute-start(bf16[2,192,1408]{2,1,0:T(8,128)(2,1)} %get-tuple-element.217.refs_0_), channel_id=1, source_target_pairs={{0,16},{4,20},{8,24},{12,28},{16,0},{20,4},{24,8},{28,12},{1,17},{... | collective-permute-start | bytes 3244040 | tf_op jit(solution)/shard_map/ppermute | solution.py:161
  282.6 45.7 %collective-permute-start.41 = (bf16[2,192,1408]{2,1,0:T(8,128)(2,1)}, bf16[2,192,1408]{2,1,0:T(8,128)(2,1)S(1)}, u32[]{:S(2)}, u32[]{:S(2)}) collective-permute-start(bf16[2,192,1408]{2,1,0:T(8,128)(2,1)} %get-tuple-element.218.refs_4_.refs_2_), channel_id=1, source_target_pairs={{0,16},{4,20},{8,24},{12,28},{16,0},{20,4},{24,8},{28,12},{1,17},{... | collective-permute-start | bytes 3244040 | tf_op jit(solution)/shard_map/ppermute | solution.py:161
  284.0 44.3 %collective-permute-start.40 = (bf16[2,192,1408]{2,1,0:T(8,128)(2,1)}, bf16[2,192,1408]{2,1,0:T(8,128)(2,1)}, u32[]{:S(2)}, u32[]{:S(2)}) collective-permute-start(bf16[2,192,1408]{2,1,0:T(8,128)(2,1)} %get-tuple-element.217.refs_0_), channel_id=1, source_target_pairs={{0,8},{4,12},{8,0},{12,4},{16,24},{20,28},{24,16},{28,20},{1,9},{5... | collective-permute-start | bytes 3244040 | tf_op jit(solution)/shard_map/ppermute | solution.py:161
  284.8 45.9 %collective-permute-start.42 = (bf16[2,192,1408]{2,1,0:T(8,128)(2,1)}, bf16[2,192,1408]{2,1,0:T(8,128)(2,1)S(1)}, u32[]{:S(2)}, u32[]{:S(2)}) collective-permute-start(bf16[2,192,1408]{2,1,0:T(8,128)(2,1)} %get-tuple-element.218.refs_4_.refs_2_), channel_id=1, source_target_pairs={{0,8},{4,12},{8,0},{12,4},{16,24},{20,28},{24,16},{28,20},{1,9},{5... | collective-permute-start | bytes 3244040 | tf_op jit(solution)/shard_map/ppermute | solution.py:161
  292.6 40.6 %collective-permute-start.56 = (f32[8,192]{0,1:T(8,128)S(1)}, f32[8,192]{0,1:T(8,128)S(1)}, u32[]{:S(2)}, u32[]{:S(2)}) collective-permute-start(f32[8,192]{0,1:T(8,128)S(1)} %bitcast_add_fusion), channel_id=1, source_target_pairs={{0,3},{1,2},{2,1},{3,0},{4,7},{5,6},{6,5},{7,4},{8,11},{9,10},{10,... | collective-permute-start | bytes 18440 | tf_op jit(solution)/shard_map/ppermute | solution.py:176
  330.8 23.6 %collective-permute-start.43 = (bf16[2,192,1408]{2,1,0:T(8,128)(2,1)}, bf16[2,192,1408]{2,1,0:T(8,128)(2,1)}, u32[]{:S(2)}, u32[]{:S(2)}) collective-permute-start(bf16[2,192,1408]{2,1,0:T(8,128)(2,1)} %collective-permute-done.40.refs_1_), channel_id=1, source_target_pairs={{0,16},{4,20},{8,24},{12,28},{16,0},{20,4},{24,8},{28,12},{1,17},{... | collective-permute-start | bytes 3244040 | tf_op jit(solution)/shard_map/ppermute | solution.py:161
  331.3 23.1 %collective-permute-start.44 = (bf16[2,192,1408]{2,1,0:T(8,128)(2,1)S(1)}, bf16[2,192,1408]{2,1,0:T(8,128)(2,1)}, u32[]{:S(2)}, u32[]{:S(2)}) collective-permute-start(bf16[2,192,1408]{2,1,0:T(8,128)(2,1)S(1)} %collective-permute-done.41.refs_2_.refs_6_), channel_id=1, source_target_pairs={{0,8},{4,12},{8,0},{12,4},{16,24},{20,28},{24,16},{28,20},{1,9},{5... | collective-permute-start | bytes 3244040 | tf_op jit(solution)/shard_map/ppermute | solution.py:161
  333.3 20.0 %collective-permute-start.57 = (f32[8,192]{0,1:T(8,128)S(1)}, f32[8,192]{0,1:T(8,128)S(1)}, u32[]{:S(2)}, u32[]{:S(2)}) collective-permute-start(f32[8,192]{0,1:T(8,128)S(1)} %add.349), channel_id=1, source_target_pairs={{0,8},{4,12},{8,0},{12,4},{16,24},{20,28},{24,16},{28,20},{1,9},{5... | collective-permute-start | bytes 18440 | tf_op jit(solution)/shard_map/ppermute | solution.py:161
  353.4 12.2 %collective-permute-start.58 = (f32[2,8,192]{2,1,0:T(8,128)S(1)}, f32[2,8,192]{2,1,0:T(8,128)S(1)}, u32[]{:S(2)}, u32[]{:S(2)}) collective-permute-start(f32[2,8,192]{2,1,0:T(8,128)S(1)} %pad_maximum_fusion.4), channel_id=1, source_target_pairs={{0,16},{4,20},{8,24},{12,28},{16,0},{20,4},{24,8},{28,12},{1,17},{... | collective-permute-start | bytes 36872 | tf_op jit(solution)/shard_map/ppermute | solution.py:161
  354.3 13.1 %collective-permute-start.51 = (bf16[2,192,256]{2,1,0:T(8,128)(2,1)S(1)}, bf16[2,192,256]{2,1,0:T(8,128)(2,1)S(1)}, u32[]{:S(2)}, u32[]{:S(2)}) collective-permute-start(bf16[2,192,256]{2,1,0:T(8,128)(2,1)S(1)} %add_convert_fusion.16), channel_id=1, source_target_pairs={{0,3},{1,2},{2,1},{3,0},{4,7},{5,6},{6,5},{7,4},{8,11},{9,10},{10,... | collective-permute-start | bytes 589832 | tf_op jit(solution)/shard_map/ppermute | solution.py:176
  374.6 19.1 %collective-permute-start.53 = (bf16[2,192,256]{2,1,0:T(8,128)(2,1)S(1)}, bf16[2,192,256]{2,1,0:T(8,128)(2,1)S(1)}, u32[]{:S(2)}, u32[]{:S(2)}) collective-permute-start(bf16[2,192,256]{2,1,0:T(8,128)(2,1)S(1)} %add_convert_fusion.17), channel_id=1, source_target_pairs={{0,3},{1,2},{2,1},{3,0},{4,7},{5,6},{6,5},{7,4},{8,11},{9,10},{10,... | collective-permute-start | bytes 589832 | tf_op jit(solution)/shard_map/ppermute | solution.py:176
  378.5 15.5 %collective-permute-start.46 = (bf16[192,1408]{1,0:T(8,128)(2,1)S(1)}, bf16[192,1408]{1,0:T(8,128)(2,1)S(1)}, u32[]{:S(2)}, u32[]{:S(2)}) collective-permute-start(bf16[192,1408]{1,0:T(8,128)(2,1)S(1)} %copy-done.94), channel_id=1, source_target_pairs={{0,8},{4,12},{8,0},{12,4},{16,24},{20,28},{24,16},{28,20},{1,9},{5... | collective-permute-start | bytes 1622024 | tf_op jit(solution)/shard_map/ppermute | solution.py:161
  379.3 17.7 %collective-permute-start.47 = (bf16[192,1408]{1,0:T(8,128)(2,1)S(1)}, bf16[192,1408]{1,0:T(8,128)(2,1)S(1)}, u32[]{:S(2)}, u32[]{:S(2)}) collective-permute-start(bf16[192,1408]{1,0:T(8,128)(2,1)S(1)} %copy-done.94), channel_id=1, source_target_pairs={{0,16},{4,20},{8,24},{12,28},{16,0},{20,4},{24,8},{28,12},{1,17},{... | collective-permute-start | bytes 1622024 | tf_op jit(solution)/shard_map/ppermute | solution.py:161
  380.9 16.1 %collective-permute-start.48 = (bf16[192,1408]{1,0:T(8,128)(2,1)S(1)}, bf16[192,1408]{1,0:T(8,128)(2,1)}, u32[]{:S(2)}, u32[]{:S(2)}) collective-permute-start(bf16[192,1408]{1,0:T(8,128)(2,1)S(1)} %copy-done.95), channel_id=1, source_target_pairs={{0,8},{4,12},{8,0},{12,4},{16,24},{20,28},{24,16},{28,20},{1,9},{5... | collective-permute-start | bytes 1622024 | tf_op jit(solution)/shard_map/ppermute | solution.py:161
  382.1 14.9 %collective-permute-start.49 = (bf16[192,1408]{1,0:T(8,128)(2,1)S(1)}, bf16[192,1408]{1,0:T(8,128)(2,1)}, u32[]{:S(2)}, u32[]{:S(2)}) collective-permute-start(bf16[192,1408]{1,0:T(8,128)(2,1)S(1)} %copy-done.95), channel_id=1, source_target_pairs={{0,16},{4,20},{8,24},{12,28},{16,0},{20,4},{24,8},{28,12},{1,17},{... | collective-permute-start | bytes 1622024 | tf_op jit(solution)/shard_map/ppermute | solution.py:161
  415.0 15.5 %collective-permute-start.61 = (bf16[768,128]{1,0:T(8,128)(2,1)}, bf16[768,128]{1,0:T(8,128)(2,1)S(1)}, u32[]{:S(2)}, u32[]{:S(2)}) collective-permute-start(bf16[768,128]{1,0:T(8,128)(2,1)} %get-tuple-element.247), channel_id=1, source_target_pairs={{0,16},{4,20},{8,24},{12,28},{16,0},{20,4},{24,8},{28,12},{1,17},{... | collective-permute-start | bytes 589832 | tf_op jit(solution)/shard_map/ppermute | solution.py:161
  416.6 13.8 %collective-permute-start.60 = (bf16[768,128]{1,0:T(8,128)(2,1)}, bf16[768,128]{1,0:T(8,128)(2,1)S(1)}, u32[]{:S(2)}, u32[]{:S(2)}) collective-permute-start(bf16[768,128]{1,0:T(8,128)(2,1)} %get-tuple-element.245), channel_id=1, source_target_pairs={{0,8},{4,12},{8,0},{12,4},{16,24},{20,28},{24,16},{28,20},{1,9},{5... | collective-permute-start | bytes 589832 | tf_op jit(solution)/shard_map/ppermute | solution.py:161
  417.5 13.1 %collective-permute-start.59 = (bf16[768,128]{1,0:T(8,128)(2,1)}, bf16[768,128]{1,0:T(8,128)(2,1)S(1)}, u32[]{:S(2)}, u32[]{:S(2)}) collective-permute-start(bf16[768,128]{1,0:T(8,128)(2,1)} %get-tuple-element.243), channel_id=1, source_target_pairs={{0,8},{4,12},{8,0},{12,4},{16,24},{20,28},{24,16},{28,20},{1,9},{5... | collective-permute-start | bytes 589832 | tf_op jit(solution)/shard_map/ppermute | solution.py:161
  433.1 53.0 %collective-permute-start.72 = (bf16[4,256,1408]{2,1,0:T(8,128)(2,1)}, bf16[4,256,1408]{2,1,0:T(8,128)(2,1)S(1)}, u32[]{:S(2)}, u32[]{:S(2)}) collective-permute-start(bf16[4,256,1408]{2,1,0:T(8,128)(2,1)} %get-tuple-element.269), channel_id=1, source_target_pairs={{0,4},{4,0},{8,12},{12,8},{16,20},{20,16},{24,28},{28,24},{1,5},{5... | collective-permute-start | bytes 8650760 | tf_op jit(solution)/shard_map/ppermute | solution.py:165
  437.9 48.2 %collective-permute-start.73 = (bf16[4,256,1408]{2,1,0:T(8,128)(2,1)}, bf16[4,256,1408]{2,1,0:T(8,128)(2,1)}, u32[]{:S(2)}, u32[]{:S(2)}) collective-permute-start(bf16[4,256,1408]{2,1,0:T(8,128)(2,1)} %get-tuple-element.272), channel_id=1, source_target_pairs={{0,4},{4,0},{8,12},{12,8},{16,20},{20,16},{24,28},{28,24},{1,5},{5... | collective-permute-start | bytes 8650760 | tf_op jit(solution)/shard_map/ppermute | solution.py:165
  438.0 17.0 %collective-permute-start.65 = (bf16[192,1408]{1,0:T(8,128)(2,1)}, bf16[192,1408]{1,0:T(8,128)(2,1)}, u32[]{:S(2)}, u32[]{:S(2)}) collective-permute-start(bf16[192,1408]{1,0:T(8,128)(2,1)} %copy-done.96), channel_id=1, source_target_pairs={{0,16},{4,20},{8,24},{12,28},{16,0},{20,4},{24,8},{28,12},{1,17},{... | collective-permute-start | bytes 1622024 | tf_op jit(solution)/shard_map/ppermute | solution.py:161
  438.4 17.9 %collective-permute-start.66 = (bf16[192,1408]{1,0:T(8,128)(2,1)}, bf16[192,1408]{1,0:T(8,128)(2,1)}, u32[]{:S(2)}, u32[]{:S(2)}) collective-permute-start(bf16[192,1408]{1,0:T(8,128)(2,1)} %collective-permute-done.49.refs_6_), channel_id=1, source_target_pairs={{0,8},{4,12},{8,0},{12,4},{16,24},{20,28},{24,16},{28,20},{1,9},{5... | collective-permute-start | bytes 1622024 | tf_op jit(solution)/shard_map/ppermute | solution.py:161
  456.2 26.0 %collective-permute-start.71 = (bf16[768,256]{1,0:T(8,128)(2,1)}, bf16[768,256]{1,0:T(8,128)(2,1)}, u32[]{:S(2)}, u32[]{:S(2)}) collective-permute-start(bf16[768,256]{1,0:T(8,128)(2,1)} %get-tuple-element.263.refs_0_), channel_id=1, source_target_pairs={{0,16},{4,20},{8,24},{12,28},{16,0},{20,4},{24,8},{28,12},{1,17},{... | collective-permute-start | bytes 1179656 | tf_op jit(solution)/shard_map/ppermute | solution.py:161
  462.9 19.5 %collective-permute-start.69 = (bf16[768,256]{1,0:T(8,128)(2,1)}, bf16[768,256]{1,0:T(8,128)(2,1)}, u32[]{:S(2)}, u32[]{:S(2)}) collective-permute-start(bf16[768,256]{1,0:T(8,128)(2,1)} %get-tuple-element.264.refs_4_), channel_id=1, source_target_pairs={{0,16},{4,20},{8,24},{12,28},{16,0},{20,4},{24,8},{28,12},{1,17},{... | collective-permute-start | bytes 1179656 | tf_op jit(solution)/shard_map/ppermute | solution.py:161
  464.9 17.5 %collective-permute-start.70 = (bf16[768,256]{1,0:T(8,128)(2,1)}, bf16[768,256]{1,0:T(8,128)(2,1)}, u32[]{:S(2)}, u32[]{:S(2)}) collective-permute-start(bf16[768,256]{1,0:T(8,128)(2,1)} %get-tuple-element.264.refs_4_), channel_id=1, source_target_pairs={{0,8},{4,12},{8,0},{12,4},{16,24},{20,28},{24,16},{28,20},{1,9},{5... | collective-permute-start | bytes 1179656 | tf_op jit(solution)/shard_map/ppermute | solution.py:161
  482.3 21.3 %collective-permute-start.78 = (bf16[2,384,256]{2,1,0:T(8,128)(2,1)}, bf16[2,384,256]{2,1,0:T(8,128)(2,1)S(1)}, u32[]{:S(2)}, u32[]{:S(2)}) collective-permute-start(bf16[2,384,256]{2,1,0:T(8,128)(2,1)} %get-tuple-element.278), channel_id=1, source_target_pairs={{0,1},{1,0},{2,3},{3,2},{4,5},{5,4},{6,7},{7,6},{8,9},{9,8},{10,11... | collective-permute-start | bytes 1179656 | tf_op jit(solution)/shard_map/ppermute | solution.py:176
  486.1 115.4 %collective-permute-start.91 = (bf16[4,1408,256]{2,1,0:T(8,128)(2,1)}, bf16[4,1408,256]{2,1,0:T(8,128)(2,1)}, u32[]{:S(2)}, u32[]{:S(2)}) collective-permute-start(bf16[4,1408,256]{2,1,0:T(8,128)(2,1)} %get-tuple-element.306), channel_id=1, source_target_pairs={{0,4},{4,0},{8,12},{12,8},{16,20},{20,16},{24,28},{28,24},{1,5},{5... | collective-permute-start | bytes 8650760 | tf_op jit(solution)/shard_map/ppermute | solution.py:165
  501.6 20.1 %collective-permute-start.82 = (bf16[2,384,256]{2,1,0:T(8,128)(2,1)}, bf16[2,384,256]{2,1,0:T(8,128)(2,1)S(1)}, u32[]{:S(2)}, u32[]{:S(2)}) collective-permute-start(bf16[2,384,256]{2,1,0:T(8,128)(2,1)} %get-tuple-element.283), channel_id=1, source_target_pairs={{0,1},{1,0},{2,3},{3,2},{4,5},{5,4},{6,7},{7,6},{8,9},{9,8},{10,11... | collective-permute-start | bytes 1179656 | tf_op jit(solution)/shard_map/ppermute | solution.py:176
  503.7 18.2 %collective-permute-start.79 = (bf16[2,384,256]{2,1,0:T(8,128)(2,1)S(1)}, bf16[2,384,256]{2,1,0:T(8,128)(2,1)S(1)}, u32[]{:S(2)}, u32[]{:S(2)}) collective-permute-start(bf16[2,384,256]{2,1,0:T(8,128)(2,1)S(1)} %add_convert_fusion.7), channel_id=1, source_target_pairs={{0,3},{1,2},{2,1},{3,0},{4,7},{5,6},{6,5},{7,4},{8,11},{9,10},{10,... | collective-permute-start | bytes 1179656 | tf_op jit(solution)/shard_map/ppermute | solution.py:176
  522.0 20.7 %collective-permute-start.83 = (bf16[2,384,256]{2,1,0:T(8,128)(2,1)S(1)}, bf16[2,384,256]{2,1,0:T(8,128)(2,1)S(1)}, u32[]{:S(2)}, u32[]{:S(2)}) collective-permute-start(bf16[2,384,256]{2,1,0:T(8,128)(2,1)S(1)} %add_convert_fusion.5.refs_0_), channel_id=1, source_target_pairs={{0,1},{1,0},{2,3},{3,2},{4,5},{5,4},{6,7},{7,6},{8,9},{9,8},{10,11... | collective-permute-start | bytes 1179656 | tf_op jit(solution)/shard_map/ppermute | solution.py:176
  538.1 49.3 %collective-permute-start.88 = (bf16[2,256,512]{2,1,0:T(8,128)(2,1)}, bf16[2,256,512]{2,1,0:T(8,128)(2,1)}, u32[]{:S(2)}, u32[]{:S(2)}) collective-permute-start(bf16[2,256,512]{2,1,0:T(8,128)(2,1)} %get-tuple-element.303), channel_id=1, source_target_pairs={{0,4},{4,0},{8,12},{12,8},{16,20},{20,16},{24,28},{28,24},{1,5},{5... | collective-permute-start | bytes 1572872 | tf_op jit(solution)/shard_map/ppermute | solution.py:165
  556.7 33.5 %all-to-all-start.2 = ((bf16[8,256,256]{2,1,0:T(8,128)(2,1)}), bf16[8,256,256]{2,1,0:T(8,128)(2,1)S(1)}, u32[]{:S(2)}, u32[]{:S(2)}) async-start(bf16[8,256,256]{2,1,0:T(8,128)(2,1)} %unpack.2), calls=%async_computation.2 | async-start | bytes 2097152 | tf_op jit(solution)/shard_map/all_to_all | solution.py:1206
  560.8 19.1 %collective-permute-start.86 = (bf16[2,384,256]{2,1,0:T(8,128)(2,1)S(1)}, bf16[2,384,256]{2,1,0:T(8,128)(2,1)S(1)}, u32[]{:S(2)}, u32[]{:S(2)}) collective-permute-start(bf16[2,384,256]{2,1,0:T(8,128)(2,1)S(1)} %add_convert_fusion.4.refs_0_), channel_id=1, source_target_pairs={{0,1},{1,0},{2,3},{3,2},{4,5},{5,4},{6,7},{7,6},{8,9},{9,8},{10,11... | collective-permute-start | bytes 1179656 | tf_op jit(solution)/shard_map/ppermute | solution.py:176
  586.8 20.6 %collective-permute-start.90 = (bf16[4,512,256]{2,1,0:T(8,128)(2,1)}, bf16[4,512,256]{2,1,0:T(8,128)(2,1)}, u32[]{:S(2)}, u32[]{:S(2)}) collective-permute-start(bf16[4,512,256]{2,1,0:T(8,128)(2,1)} %get-tuple-element.305), channel_id=1, source_target_pairs={{0,4},{4,0},{8,12},{12,8},{16,20},{20,16},{24,28},{28,24},{1,5},{5... | collective-permute-start | bytes 3145736 | tf_op jit(solution)/shard_map/ppermute | solution.py:165
  587.2 23.1 %collective-permute-start.89 = (bf16[4,256,512]{2,1,0:T(8,128)(2,1)}, bf16[4,256,512]{2,1,0:T(8,128)(2,1)S(1)}, u32[]{:S(2)}, u32[]{:S(2)}) collective-permute-start(bf16[4,256,512]{2,1,0:T(8,128)(2,1)} %get-tuple-element.304), channel_id=1, source_target_pairs={{0,4},{4,0},{8,12},{12,8},{16,20},{20,16},{24,28},{28,24},{1,5},{5... | collective-permute-start | bytes 3145736 | tf_op jit(solution)/shard_map/ppermute | solution.py:165
  597.3 20.9 %all-to-all-start.3 = ((bf16[8,288,256]{2,1,0:T(8,128)(2,1)}), bf16[8,288,256]{2,1,0:T(8,128)(2,1)S(1)}, u32[]{:S(2)}, u32[]{:S(2)}) async-start(bf16[8,288,256]{2,1,0:T(8,128)(2,1)} %unpack.3), calls=%async_computation.3 | async-start | bytes 2359296 | tf_op jit(solution)/shard_map/all_to_all | solution.py:1206
  (141 other events, 2044.0 us)

commit v9 on v8

--- a/solution.py
+++ b/solution.py
@@ -317,7 +317,7 @@
     router_a = jnp.pad(spread(attn_router).transpose(0, 2, 1), pad)
     router_f = jnp.pad(spread(ffn_router).transpose(0, 2, 1), pad)
 
-    in_own = expert_in.swapaxes(1, 2)
+    in_own = after(expert_in, x_send).swapaxes(1, 2)
     wq = [query_weight] + [by_part(query_weight, s) for s in pieces[1:]]
     wkv = [kv_weight] + [by_part(kv_weight, s) for s in pieces[1:]]
     wp = [proj_weight] + [by_part(proj_weight, s) for s in pieces[1:]]
@@ -1088,7 +1088,8 @@
         )
 
     dots_a = dots_q + jnp.where(third, dots_kv, 0.0)
-    dots_a = sum_groups(after(dots_a, dwproj_sums[0]))
+    dots_a = after(dots_a, dwproj_sums[0])
+    dots_a = (dots_a + by_group(dots_a, 1)) + (by_group(dots_a, 2) + by_group(dots_a, 3))
     got_out = exchange(dwout_sums)
     da_halves = dattn(after(meta, dwproj_sums[0]))
     got_proj = exchange(dwproj_sums)
@@ -1134,7 +1135,7 @@
             flops=2 * rp * (experts + 2) * hw * parts * ds,
         )
 
-    dwqkv_sums = dwqkv(after(meta, da_halves[0]))
+    dwqkv_sums = dwqkv(after(meta, da_halves[0], dots_a))
 
 
     da_half = z_covered(*da_halves, 1, dwqkv_sums[0])
@@ -1152,7 +1153,7 @@
                 ).astype(BF16)
 
     got_q, got_kv = exchange(dwqkv_sums[:parts]), exchange(dwqkv_sums[parts:])
-    dots_a = sum_z(dots_a)
+    dots_a = (dots_a + by_z(dots_a, 1)) + (by_z(dots_a, 2) + by_z(dots_a, 3))
     back_a = back_columns(flat_a, dots_a, low_a, high_a)
     down_totals = z_last(z_covered(down_half, down_half, 3, da_half))
     ins = [(t, None, None) for t in down_totals] + [(after_rows, None, None)]
@@ -1203,14 +1204,18 @@
                 for n in (rows + seq_len + 8, rows_all, rows_all, seq_len + 8)
             ],
         )[0]
+        return spread_rows
+
+    def land(spread_rows):
         landed = lax.all_to_all(spread_rows, "dp", 0, 0, tiled=True)
         rows_of = landed[:, :count].transpose(1, 0, 2).reshape(seqs, per, width)
-        return rows_of, spread_rows, landed[:, count:]
+        return rows_of, landed[:, count:]
 
     da_half = z_covered(da_half, da_half, 3, out_rows[0])
-    expertin_grad = fold(got_in, after(meta, da_half))
-    layer_out, layer_rows, _ = unpack(out_rows, x_all, False, table)
+    layer_rows = unpack(out_rows, x_all, False, table)
+    expertin_grad = fold(got_in, after(meta, da_half, layer_rows))
     da_totals = z_last(da_half)
+    layer_out, _ = land(after(layer_rows, expertin_grad, da_totals[1]))
     ins = [(t, None, None) for t in da_totals]
     ins += [(x_stack, None, None), (dafter, None, None)]
     ins += [(gain_a, None, None), (router_a, None, None), (back_a, None, None)]
@@ -1225,7 +1230,7 @@
     vectors = 2 * (experts + 1)
     small = jnp.concatenate([small_a, small_f], axis=0).reshape(vectors * parts, ds)
     small = jnp.pad(small, ((0, -vectors * parts % 16), (0, 0))).astype(BF16)
-    input_grad, _, got = unpack(dinput, d_all, True, after(table, layer_out), [small])
+    input_grad, got = land(unpack(dinput, d_all, True, table, [small]))
     got = got[:, : vectors * parts].astype(F32).reshape(groups, parts, vectors, parts, ds)
     full = jnp.stack(
         [sum(got[:, k ^ s, :, s] for s in pieces) for k in range(parts)], axis=2

time: 628 us -> 621 us (0.989)
  waiting for transfers between devices: 201 us -> 193 us
    ppermute x56 -> x57, waiting for transfers between devices: 131 us -> 125 us  [by_group(): return lax.ppermute(value, 'dp', pairs)]
    unnamed x222 -> x219, local copies, waits for them, and re-layouts: 17.8 us -> 12.2 us
    ppermute x56 -> x57, starting transfers between devices: 61.5 us -> 63.6 us  [by_group(): return lax.ppermute(value, 'dp', pairs)]
    ppermute x19 -> x20, starting transfers between devices: 34.4 us -> 32.9 us  [by_z(): return lax.ppermute(value, 'tensor', [(a, a ^ mask) for a in range(tp)])]
    ppermute x19 -> x20, waiting for transfers between devices: 51.7 us -> 52.2 us  [by_z(): return lax.ppermute(value, 'tensor', [(a, a ^ mask) for a in range(tp)])]
  transfers between devices with their start and end apart: 96 -> 98, of which waited for: 40 -> 38; matrix products, arithmetic and copies ran while one was open for 8% -> 8% of each run, Pallas kernels for 28% -> 29%
where the time goes in v9:
time: 621 us; the launch traced here: 616 us
  Pallas kernels  229 us (37%)
  waiting for transfers between devices  193 us (31%)
  starting transfers between devices  119 us (19%)
  local copies, waits for them, and re-layouts  37.7 us (6%)
  other arithmetic  33.5 us (5%)
    pallas_call x28, Pallas kernels, run(): pl.pallas_call(body, name=name, grid_spec=pltpu.PrefetchScalarGridSpec(nu...  229 us
    ppermute x57, waiting for transfers between devices, by_group(): return lax.ppermute(value, 'dp', pairs)  125 us
    ppermute x57, starting transfers between devices, by_group(): return lax.ppermute(value, 'dp', pairs)  63.6 us
    ppermute x20, waiting for transfers between devices, by_z(): return lax.ppermute(value, 'tensor', [(a, a ^ mask) for a in range(tp)])  52.2 us
    ppermute x20, starting transfers between devices, by_z(): return lax.ppermute(value, 'tensor', [(a, a ^ mask) for a in range(tp)])  32.9 us
    add x4, other arithmetic, add_up(): return sum((v.astype(F32) for v in got))  12.6 us
  transfers between devices with their start and end apart: 98, of which 38 were waited for; matrix products, arithmetic and copies ran while one was open for 8% of the time, Pallas kernels for 29%

profile of v9, /device:TPU:0, one launch (start us, length us, event | category | flops | bytes accessed | tf_op | source)
XLA Modules:
  0.0 615.7 jit_solution(2175442348308476769)
XLA Ops:
  3.4 6.0 copy.230
  10.0 5.1 all-to-all-start
  20.3 10.2 %all-to-all-done = bf16[8,256,256]{2,1,0:T(8,128)(2,1)S(1)} async-done(((bf16[8,256,256]{2,1,0:T(8,128)(2,1)}), bf16[8,256,256]{2,1,0:T(8,128)(2,1)S(1)}, u32[]{:S(2)}, u32[]{:S(2)}) %all-to-all-start) | async-done | bytes 1048608 | tf_op jit(solution)/shard_map/all_to_all | solution.py:308
  30.6 3.8 all-to-all-start.1
  34.4 4.0 pack.2
  43.2 8.5 %qkv.1 = (bf16[768,256]{1,0:T(8,128)(2,1)}, bf16[768,256]{1,0:T(8,128)(2,1)}, bf16[768,256]{1,0:T(8,128)(2,1)}, bf16[768,256]{1,0:T(8,128)(2,1)}, bf16[768,256]{...) custom-call(s32[24]{0:T(128)} %stack.147.m, ...), custom_call_target="tpu_custom_call" | custom-call | flops 2415919104 | bytes 7137280 | tf_op jit(solution)/shard_map/qkv/pallas_call | solution.py:61
  58.5 5.5 collective-permute-done.5
  65.0 4.1 pack.3
  82.5 12.0 %dhidden.1 = (bf16[192,1408]{1,0:T(8,128)(2,1)}, bf16[192,1408]{1,0:T(8,128)(2,1)}, bf16[192,1408]{1,0:T(8,128)(2,1)}, bf16[192,1408]{1,0:T(8,128)(2,1)}, bf16[1...) custom-call(s32[24]{0:T(128)} %stack.147.m, ...), custom_call_target="tpu_custom_call" | custom-call | flops 4429185024 | bytes 11714560 | tf_op jit(solution)/shard_map/dhidden/pallas_call | solution.py:61
  95.5 4.6 rope.1
  103.9 8.0 %attend.1 = (bf16[768,128]{1,0:T(8,128)(2,1)}, bf16[768,128]{1,0:T(8,128)(2,1)}, bf16[768,128]{1,0:T(8,128)(2,1)}, bf16[768,128]{1,0:T(8,128)(2,1)}) custom-call(s32[24]{0:T(128)} %stack.147.m, bf16[768,256]{1,0:T(8,128)(2,1)} %get-tuple-element.181.q_ref.refs_0_, bf16[768,256]{1,0:T(8,128)(2,1)} %get-tuple-element.182.kv_ref.refs_1_, ...), custom_call_target="tpu_custom_call" | custom-call | flops 301989888 | bytes 1753088 | tf_op jit(solution)/shard_map/attend/pallas_call | solution.py:61
  116.0 3.8 collective-permute-done.16.refs_1_
  122.0 2.7 collective-permute-done.24.refs_2_
  124.7 3.3 collective-permute-done.17.refs_3_
  128.7 9.9 %proj.1 = (bf16[2,384,256]{2,1,0:T(8,128)(2,1)}, bf16[2,384,256]{2,1,0:T(8,128)(2,1)}) custom-call(s32[24]{0:T(128)} %stack.147.m, bf16[768,128]{1,0:T(8,128)(2,1)} %get-tuple-element.190.refs_0_, bf16[768,128]{1,0:T(8,128)(2,1)} %copy-done.102, bf16[768,128]{1,0:T(8,128)(2,1)} %copy-done.104, bf16[768,128]{1,0:T(8,128)(2,1)} %copy-done.106, ...), custom_call_target="tpu_custom_call" | custom-call | flops 1610612736 | bytes 4481024 | tf_op jit(solution)/shard_map/proj/pallas_call | solution.py:61
  144.3 4.9 collective-permute-done.26
  150.3 3.7 collective-permute-start.27
  155.9 6.0 collective-permute-done.27
  161.9 3.2 collective-permute-done.22.refs_7_
  168.2 3.9 collective-permute-start.30
  173.4 6.9 %collective-permute-done.30.refs_1_ = bf16[2,384,256]{2,1,0:T(8,128)(2,1)S(1)} collective-permute-done((bf16[2,384,256]{2,1,0:T(8,128)(2,1)S(1)}, bf16[2,384,256]{2,1,0:T(8,128)(2,1)S(1)}, u32[]{:S(2)}, u32[]{:S(2)}) %collective-permute-start.30) | collective-permute-done | bytes 393248 | tf_op jit(solution)/shard_map/ppermute | solution.py:176
  181.0 4.4 norm.1
  185.4 10.2 %up.2 = (bf16[2,192,1408]{2,1,0:T(8,128)(2,1)}, bf16[2,192,1408]{2,1,0:T(8,128)(2,1)}, bf16[2,192,1408]{2,1,0:T(8,128)(2,1)}, bf16[2,192,1408]{2,1,0:T(8,128)(2,1)}) custom-call(s32[24]{0:T(128)} %stack.147.m, bf16[2,768,256]{2,1,0:T(8,128)(2,1)} %get-tuple-element.203.refs_0_.refs_1_, bf16[2,768,256]{2,1,0:T(8,128)(2,1)} %get-tuple-element.203.refs_0_.refs_1_, ...), custom_call_target="tpu_custom_call" | custom-call | flops 4429185024 | bytes 17481728 | tf_op jit(solution)/shard_map/up/pallas_call | solution.py:61
  197.4 10.3 %up.3 = (bf16[2,192,1408]{2,1,0:T(8,128)(2,1)}, bf16[2,192,1408]{2,1,0:T(8,128)(2,1)}, bf16[2,192,1408]{2,1,0:T(8,128)(2,1)}, bf16[2,192,1408]{2,1,0:T(8,128)(2,1)}) custom-call(s32[24]{0:T(128)} %stack.147.m, bf16[2,768,256]{2,1,0:T(8,128)(2,1)} %get-tuple-element.203.refs_0_.refs_1_, bf16[2,768,256]{2,1,0:T(8,128)(2,1)} %get-tuple-element.203.refs_0_.refs_1_, ...), custom_call_target="tpu_custom_call" | custom-call | flops 4429185024 | bytes 17481728 | tf_op jit(solution)/shard_map/up/pallas_call | solution.py:61
  210.1 12.7 %collective-permute-done.33 = bf16[2,192,1408]{2,1,0:T(8,128)(2,1)} collective-permute-done((bf16[2,192,1408]{2,1,0:T(8,128)(2,1)}, bf16[2,192,1408]{2,1,0:T(8,128)(2,1)}, u32[]{:S(2)}, u32[]{:S(2)}) %collective-permute-start.33) | collective-permute-done | bytes 1081376 | tf_op jit(solution)/shard_map/ppermute | solution.py:161
  222.7 2.6 add_convert_fusion
  225.4 2.5 add_convert_fusion.1
  227.9 15.3 %collective-permute-done.34.refs_5_ = bf16[2,192,1408]{2,1,0:T(8,128)(2,1)S(1)} collective-permute-done((bf16[2,192,1408]{2,1,0:T(8,128)(2,1)}, bf16[2,192,1408]{2,1,0:T(8,128)(2,1)S(1)}, u32[]{:S(2)}, u32[]{:S(2)}) %collective-permute-start.34) | collective-permute-done | bytes 1081376 | tf_op jit(solution)/shard_map/ppermute | solution.py:161
  246.9 21.4 %collective-permute-done.37 = f32[8,768]{1,0:T(8,128)S(1)} collective-permute-done((f32[8,768]{1,0:T(8,128)S(1)}, f32[8,768]{1,0:T(8,128)S(1)}, u32[]{:S(2)}, u32[]{:S(2)}) %collective-permute-start.37) | collective-permute-done | bytes 24608 | tf_op jit(solution)/shard_map/ppermute | solution.py:161
  268.9 3.2 collective-permute-done.38
  274.8 8.2 %mid.1 = (bf16[192,1408]{1,0:T(8,128)(2,1)}, bf16[192,1408]{1,0:T(8,128)(2,1)}, bf16[2,192,1408]{2,1,0:T(8,128)(2,1)}, bf16[2,192,1408]{2,1,0:T(8,128)(2,1)}, f32[192,8]{1,0:T(8,128)}) custom-call(s32[24]{0:T(128)} %stack.147.m, bf16[2,192,1408]{2,1,0:T(8,128)(2,1)} %get-tuple-element.206.refs_0_, bf16[2,192,1408]{2,1,0:T(8,128)(2,1)} %copy-done.14, ...), custom_call_target="tpu_custom_call" | custom-call | bytes 13006848 | tf_op jit(solution)/shard_map/mid/pallas_call | solution.py:61
  288.9 3.9 collective-permute-done.55
  293.8 16.2 %collective-permute-done.39.refs_0_.refs_2_ = bf16[2,192,1408]{2,1,0:T(8,128)(2,1)S(1)} collective-permute-done((bf16[2,192,1408]{2,1,0:T(8,128)(2,1)}, bf16[2,192,1408]{2,1,0:T(8,128)(2,1)S(1)}, u32[]{:S(2)}, u32[]{:S(2)}) %collective-permute-start.39) | collective-permute-done | bytes 1081376 | tf_op jit(solution)/shard_map/ppermute | solution.py:161
  310.0 19.3 %collective-permute-done.41.refs_2_.refs_6_ = bf16[2,192,1408]{2,1,0:T(8,128)(2,1)S(1)} collective-permute-done((bf16[2,192,1408]{2,1,0:T(8,128)(2,1)}, bf16[2,192,1408]{2,1,0:T(8,128)(2,1)S(1)}, u32[]{:S(2)}, u32[]{:S(2)}) %collective-permute-start.41) | collective-permute-done | bytes 1081376 | tf_op jit(solution)/shard_map/ppermute | solution.py:161
  329.4 2.4 collective-permute-done.42.refs_5_.refs_3_
  335.7 11.0 %dx.3 = (bf16[2,192,256]{2,1,0:T(8,128)(2,1)}, bf16[2,192,256]{2,1,0:T(8,128)(2,1)}) custom-call(s32[24]{0:T(128)} %stack.147.m, bf16[2,192,1408]{2,1,0:T(8,128)(2,1)} %get-tuple-element.219.refs_0_, bf16[2,192,1408]{2,1,0:T(8,128)(2,1)} %collective-permute-done.40.refs_1_, bf16[2,192,1408]{2,1,0:T(8,128)(2,1)} %get-tuple-element.220.refs_4_.refs_2_, ...), custom_call_target="tpu_custom_call" | custom-call | flops 4429185024 | bytes 16302080 | tf_op jit(solution)/shard_map/dx/pallas_call | solution.py:61
  349.8 4.6 collective-permute-done.57
  355.5 11.1 %dx.2 = (bf16[2,192,256]{2,1,0:T(8,128)(2,1)}, bf16[2,192,256]{2,1,0:T(8,128)(2,1)}) custom-call(s32[24]{0:T(128)} %stack.147.m, bf16[2,192,1408]{2,1,0:T(8,128)(2,1)} %copy-done.10, bf16[2,192,1408]{2,1,0:T(8,128)(2,1)} %collective-permute-done.43.refs_1_.refs_3_, bf16[2,192,1408]{2,1,0:T(8,128)(2,1)} %copy-done.11, ...), custom_call_target="tpu_custom_call" | custom-call | flops 4429185024 | bytes 16302080 | tf_op jit(solution)/shard_map/dx/pallas_call | solution.py:61
  368.7 6.0 collective-permute-done.45
  375.7 3.8 collective-permute-start.53
  383.5 11.3 %dwin.2 = (bf16[4,256,1408]{2,1,0:T(8,128)(2,1)}, bf16[4,256,1408]{2,1,0:T(8,128)(2,1)}) custom-call(s32[24]{0:T(128)} %stack.147.m, bf16[2,192,1408]{2,1,0:T(8,128)(2,1)} %get-tuple-element.219.refs_0_, bf16[2,192,1408]{2,1,0:T(8,128)(2,1)} %collective-permute-done.40.refs_1_, bf16[2,192,1408]{2,1,0:T(8,128)(2,1)} %copy-done.10, ...), custom_call_target="tpu_custom_call" | custom-call | flops 4429185024 | bytes 15228928 | tf_op jit(solution)/shard_map/dwin/pallas_call | solution.py:61
  398.1 2.5 collective-permute-done.52.refs_1_
  403.3 6.5 %norm_back.1 = (f32[2,768,256]{2,1,0:T(8,128)}, bf16[2,768,256]{2,1,0:T(8,128)(2,1)}, f32[5,2,256]{2,1,0:T(2,128)}) custom-call(s32[24]{0:T(128)} %stack.147.m, bf16[2,192,256]{2,1,0:T(8,128)(2,1)} %copy-done.21, bf16[2,192,256]{2,1,0:T(8,128)(2,1)} %copy-done.50, bf16[2,192,256]{2,1,0:T(8,128)(2,1)} %copy-done.22, bf16[2,192,256]{2,1,0:T(8,128)(2,1)} %copy-done.51, ...), custom_call_target="tpu_custom_call" | custom-call | bytes 5550080 | tf_op jit(solution)/shard_map/norm_back/pallas_call | solution.py:61
  409.9 6.1 dmix.1
  420.1 11.3 %dwin.3 = (bf16[4,256,1408]{2,1,0:T(8,128)(2,1)}, bf16[4,256,1408]{2,1,0:T(8,128)(2,1)}) custom-call(s32[24]{0:T(128)} %stack.147.m, bf16[2,192,1408]{2,1,0:T(8,128)(2,1)} %get-tuple-element.219.refs_0_, bf16[2,192,1408]{2,1,0:T(8,128)(2,1)} %collective-permute-done.40.refs_1_, bf16[2,192,1408]{2,1,0:T(8,128)(2,1)} %copy-done.10, ...), custom_call_target="tpu_custom_call" | custom-call | flops 4429185024 | bytes 15228928 | tf_op jit(solution)/shard_map/dwin/pallas_call | solution.py:61
  434.1 3.3 collective-permute-done.63.refs_9_
  440.2 14.4 %attend_back.1 = (bf16[768,256]{1,0:T(8,128)(2,1)}, f32[768,256]{1,0:T(8,128)}, f32[256,256]{1,0:T(8,128)}, f32[8,768]{1,0:T(8,128)}) custom-call(s32[24]{0:T(128)} %stack.147.m, bf16[768,256]{1,0:T(8,128)(2,1)} %get-tuple-element.181.q_ref.refs_0_, bf16[768,256]{1,0:T(8,128)(2,1)} %get-tuple-element.182.kv_ref.refs_1_, bf16[256,256]{1,0:T(8,128)(2,1)} %copy-done.29, ...), custom_call_target="tpu_custom_call" | custom-call | flops 754974720 | bytes 4792320 | tf_op jit(solution)/shard_map/attend_back/pallas_call | solution.py:61
  460.3 3.6 dkv.1
  467.3 16.2 %down.1 = (bf16[2,384,256]{2,1,0:T(8,128)(2,1)}, bf16[2,384,256]{2,1,0:T(8,128)(2,1)}, bf16[4,1408,256]{2,1,0:T(8,128)(2,1)}, bf16[4,1408,256]{2,1,0:T(8,128)(2,1)}) custom-call(s32[24]{0:T(128)} %stack.147.m, bf16[192,1408]{1,0:T(8,128)(2,1)} %get-tuple-element.230.refs_0_, bf16[192,1408]{1,0:T(8,128)(2,1)} %copy-done.94, bf16[192,1408]{1,0:T(8,128)(2,1)} %copy-done.95, ...), custom_call_target="tpu_custom_call" | custom-call | flops 8858370048 | bytes 17457152 | tf_op jit(solution)/shard_map/down/pallas_call | solution.py:61
  487.4 7.7 %dwproj.1 = (bf16[4,512,256]{2,1,0:T(8,128)(2,1)}, bf16[4,512,256]{2,1,0:T(8,128)(2,1)}) custom-call(s32[24]{0:T(128)} %stack.147.m, bf16[768,128]{1,0:T(8,128)(2,1)} %get-tuple-element.190.refs_0_, bf16[768,128]{1,0:T(8,128)(2,1)} %copy-done.102, bf16[768,128]{1,0:T(8,128)(2,1)} %copy-done.104, bf16[768,128]{1,0:T(8,128)(2,1)} %copy-done.106, ...), custom_call_target="tpu_custom_call" | custom-call | flops 1610612736 | bytes 4481024 | tf_op jit(solution)/shard_map/dwproj/pallas_call | solution.py:61
  498.7 7.6 %dattn.1 = (bf16[2,384,256]{2,1,0:T(8,128)(2,1)}, bf16[2,384,256]{2,1,0:T(8,128)(2,1)}) custom-call(s32[24]{0:T(128)} %stack.147.m, bf16[768,256]{1,0:T(8,128)(2,1)} %get-tuple-element.265.refs_0_, bf16[768,256]{1,0:T(8,128)(2,1)} %collective-permute-done.68.refs_1_, bf16[768,256]{1,0:T(8,128)(2,1)} %copy-done.101, ...), custom_call_target="tpu_custom_call" | custom-call | flops 2415919104 | bytes 7102464 | tf_op jit(solution)/shard_map/dattn/pallas_call | solution.py:61
  508.6 9.6 %dwqkv.1 = (bf16[4,256,512]{2,1,0:T(8,128)(2,1)}, bf16[4,256,512]{2,1,0:T(8,128)(2,1)}, bf16[2,256,512]{2,1,0:T(8,128)(2,1)}, bf16[2,256,512]{2,1,0:T(8,128)(2,1)}) custom-call(s32[24]{0:T(128)} %stack.147.m, bf16[768,256]{1,0:T(8,128)(2,1)} %get-tuple-element.265.refs_0_, bf16[768,256]{1,0:T(8,128)(2,1)} %collective-permute-done.68.refs_1_, ...), custom_call_target="tpu_custom_call" | custom-call | flops 2415919104 | bytes 7102464 | tf_op jit(solution)/shard_map/dwqkv/pallas_call | solution.py:61
  518.2 7.5 %collective-permute-done.84 = bf16[2,384,256]{2,1,0:T(8,128)(2,1)S(1)} collective-permute-done((bf16[2,384,256]{2,1,0:T(8,128)(2,1)}, bf16[2,384,256]{2,1,0:T(8,128)(2,1)S(1)}, u32[]{:S(2)}, u32[]{:S(2)}) %collective-permute-start.84) | collective-permute-done | bytes 393248 | tf_op jit(solution)/shard_map/ppermute | solution.py:176
  532.0 10.6 %collective-permute-done.77 = f32[8,768]{1,0:T(8,128)S(1)} collective-permute-done((f32[8,768]{1,0:T(8,128)S(1)}, f32[8,768]{1,0:T(8,128)S(1)}, u32[]{:S(2)}, u32[]{:S(2)}) %collective-permute-start.77) | collective-permute-done | bytes 24608 | tf_op jit(solution)/shard_map/ppermute | solution.py:176
  542.6 5.9 collective-permute-start.79
  551.1 3.3 finish.1
  557.2 4.4 unpack.2
  561.6 10.4 %fold.1 = f32[4,256,2,1408]{3,2,1,0:T(2,128)} custom-call(s32[24]{0:T(128)} %stack.147.m, bf16[4,256,1408]{2,1,0:T(8,128)(2,1)} %get-tuple-element.228.refs_0_, bf16[4,256,1408]{2,1,0:T(8,128)(2,1)} %copy-done.6, bf16[4,256,1408]{2,1,0:T(8,128)(2,1)} %get-tuple-element.273.refs_2_, bf16[4,256,1408]{2,1,0:T(8,128)(2,1)} %collective-permute-done.73.refs_3_), custom_call_target="tpu_custom_call" | custom-call | bytes 23068672 | tf_op jit(solution)/shard_map/fold/pallas_call | solution.py:61
  572.0 3.8 all-to-all-start.2
  576.9 5.9 norm_back_first.1
  586.1 4.5 unpack.3
  591.2 3.6 all-to-all-start.3
  594.8 5.9 convert_add_fusion
  603.0 2.8 convert_add_fusion.1
  (506 shorter events, 155.3 us)
Async XLA Ops:
  9.4 59.6 %collective-permute-start.10 = (bf16[4,2,256,1408]{3,2,1,0:T(8,128)(2,1)}, bf16[4,2,256,1408]{3,2,1,0:T(8,128)(2,1)}, u32[]{:S(2)}, u32[]{:S(2)}) collective-permute-start(bf16[4,2,256,1408]{3,2,1,0:T(8,128)(2,1)} %bitcast.97.refs_2_.refs_4_), channel_id=1, source_target_pairs={{0,4},{4,0},{8,12},{12,8},{16,20},{20,16},{24,28},{28,24},{1,5},{5... | collective-permute-start | bytes 17301512 | tf_op jit(solution)/shard_map/ppermute | solution.py:165
  10.0 32.5 %collective-permute-start = (bf16[4,1408,256]{2,1,0:T(8,128)(2,1)}, bf16[4,1408,256]{2,1,0:T(8,128)(2,1)}, u32[]{:S(2)}, u32[]{:S(2)}) collective-permute-start(bf16[4,1408,256]{2,1,0:T(8,128)(2,1)} %refs_11_.2), channel_id=1, source_target_pairs={{0,4},{4,0},{8,12},{12,8},{16,20},{20,16},{24,28},{28,24},{1,5},{5... | collective-permute-start | bytes 8650760 | tf_op jit(solution)/shard_map/ppermute | solution.py:165
  10.0 20.5 %all-to-all-start = ((bf16[8,256,256]{2,1,0:T(8,128)(2,1)}), bf16[8,256,256]{2,1,0:T(8,128)(2,1)S(1)}, u32[]{:S(2)}, u32[]{:S(2)}) async-start(bf16[8,256,256]{2,1,0:T(8,128)(2,1)} %bitcast.99), calls=%async_computation | async-start | bytes 2097152 | tf_op jit(solution)/shard_map/all_to_all | solution.py:308
  15.2 23.2 %collective-permute-start.1 = (bf16[4,512,256]{2,1,0:T(8,128)(2,1)S(1)}, bf16[4,512,256]{2,1,0:T(8,128)(2,1)}, u32[]{:S(2)}, u32[]{:S(2)}) collective-permute-start(bf16[4,512,256]{2,1,0:T(8,128)(2,1)S(1)} %copy-done.91), channel_id=1, source_target_pairs={{0,4},{4,0},{8,12},{12,8},{16,20},{20,16},{24,28},{28,24},{1,5},{5... | collective-permute-start | bytes 3145736 | tf_op jit(solution)/shard_map/ppermute | solution.py:165
  15.7 26.8 %collective-permute-start.3 = (bf16[4,256,512]{2,1,0:T(8,128)(2,1)}, bf16[4,256,512]{2,1,0:T(8,128)(2,1)}, u32[]{:S(2)}, u32[]{:S(2)}) collective-permute-start(bf16[4,256,512]{2,1,0:T(8,128)(2,1)} %refs_9_.3), channel_id=1, source_target_pairs={{0,4},{4,0},{8,12},{12,8},{16,20},{20,16},{24,28},{28,24},{1,5},{5... | collective-permute-start | bytes 3145736 | tf_op jit(solution)/shard_map/ppermute | solution.py:165
  15.8 26.7 %collective-permute-start.4 = (bf16[2,256,512]{2,1,0:T(8,128)(2,1)}, bf16[2,256,512]{2,1,0:T(8,128)(2,1)}, u32[]{:S(2)}, u32[]{:S(2)}) collective-permute-start(bf16[2,256,512]{2,1,0:T(8,128)(2,1)} %refs_11_.3), channel_id=1, source_target_pairs={{0,4},{4,0},{8,12},{12,8},{16,20},{20,16},{24,28},{28,24},{1,5},{5... | collective-permute-start | bytes 1572872 | tf_op jit(solution)/shard_map/ppermute | solution.py:165
  30.6 33.4 %all-to-all-start.1 = ((bf16[8,256,256]{2,1,0:T(8,128)(2,1)}), bf16[8,256,256]{2,1,0:T(8,128)(2,1)S(1)}, u32[]{:S(2)}, u32[]{:S(2)}) async-start(bf16[8,256,256]{2,1,0:T(8,128)(2,1)} %bitcast.98), calls=%async_computation.1 | async-start | bytes 2097152 | tf_op jit(solution)/shard_map/all_to_all | solution.py:406
  53.4 21.2 %collective-permute-start.8 = (bf16[768,256]{1,0:T(8,128)(2,1)}, bf16[768,256]{1,0:T(8,128)(2,1)S(1)}, u32[]{:S(2)}, u32[]{:S(2)}) collective-permute-start(bf16[768,256]{1,0:T(8,128)(2,1)} %get-tuple-element.173), channel_id=1, source_target_pairs={{0,16},{4,20},{8,24},{12,28},{16,0},{20,4},{24,8},{28,12},{1,17},{... | collective-permute-start | bytes 1179656 | tf_op jit(solution)/shard_map/ppermute | solution.py:161
  57.6 20.9 %collective-permute-start.7 = (bf16[768,256]{1,0:T(8,128)(2,1)}, bf16[768,256]{1,0:T(8,128)(2,1)S(1)}, u32[]{:S(2)}, u32[]{:S(2)}) collective-permute-start(bf16[768,256]{1,0:T(8,128)(2,1)} %get-tuple-element.170), channel_id=1, source_target_pairs={{0,8},{4,12},{8,0},{12,4},{16,24},{20,28},{24,16},{28,20},{1,9},{5... | collective-permute-start | bytes 1179656 | tf_op jit(solution)/shard_map/ppermute | solution.py:161
  58.1 20.3 %collective-permute-start.9 = (bf16[768,256]{1,0:T(8,128)(2,1)}, bf16[768,256]{1,0:T(8,128)(2,1)S(1)}, u32[]{:S(2)}, u32[]{:S(2)}) collective-permute-start(bf16[768,256]{1,0:T(8,128)(2,1)} %get-tuple-element.174), channel_id=1, source_target_pairs={{0,16},{4,20},{8,24},{12,28},{16,0},{20,4},{24,8},{28,12},{1,17},{... | collective-permute-start | bytes 1179656 | tf_op jit(solution)/shard_map/ppermute | solution.py:161
  78.5 16.0 %collective-permute-start.13 = (bf16[768,256]{1,0:T(8,128)(2,1)S(1)}, bf16[768,256]{1,0:T(8,128)(2,1)S(1)}, u32[]{:S(2)}, u32[]{:S(2)}) collective-permute-start(bf16[768,256]{1,0:T(8,128)(2,1)S(1)} %add_convert_fusion.11), channel_id=1, source_target_pairs={{0,16},{4,20},{8,24},{12,28},{16,0},{20,4},{24,8},{28,12},{1,17},{... | collective-permute-start | bytes 1179656 | tf_op jit(solution)/shard_map/ppermute | solution.py:161
  80.3 14.3 %collective-permute-start.14 = (bf16[768,256]{1,0:T(8,128)(2,1)S(1)}, bf16[768,256]{1,0:T(8,128)(2,1)S(1)}, u32[]{:S(2)}, u32[]{:S(2)}) collective-permute-start(bf16[768,256]{1,0:T(8,128)(2,1)S(1)} %add_convert_fusion.10), channel_id=1, source_target_pairs={{0,8},{4,12},{8,0},{12,4},{16,24},{20,28},{24,16},{28,20},{1,9},{5... | collective-permute-start | bytes 1179656 | tf_op jit(solution)/shard_map/ppermute | solution.py:161
  140.2 15.1 %collective-permute-start.21 = (bf16[192,1408]{1,0:T(8,128)(2,1)S(1)}, bf16[192,1408]{1,0:T(8,128)(2,1)S(1)}, u32[]{:S(2)}, u32[]{:S(2)}) collective-permute-start(bf16[192,1408]{1,0:T(8,128)(2,1)S(1)} %copy-done.100), channel_id=1, source_target_pairs={{0,16},{4,20},{8,24},{12,28},{16,0},{20,4},{24,8},{28,12},{1,17},{... | collective-permute-start | bytes 1622024 | tf_op jit(solution)/shard_map/ppermute | solution.py:161
  140.6 15.1 %collective-permute-start.20 = (bf16[192,1408]{1,0:T(8,128)(2,1)S(1)}, bf16[192,1408]{1,0:T(8,128)(2,1)S(1)}, u32[]{:S(2)}, u32[]{:S(2)}) collective-permute-start(bf16[192,1408]{1,0:T(8,128)(2,1)S(1)} %copy-done.99), channel_id=1, source_target_pairs={{0,8},{4,12},{8,0},{12,4},{16,24},{20,28},{24,16},{28,20},{1,9},{5... | collective-permute-start | bytes 1622024 | tf_op jit(solution)/shard_map/ppermute | solution.py:161
  142.2 22.9 %collective-permute-start.22 = (bf16[192,1408]{1,0:T(8,128)(2,1)S(1)}, bf16[192,1408]{1,0:T(8,128)(2,1)S(1)}, u32[]{:S(2)}, u32[]{:S(2)}) collective-permute-start(bf16[192,1408]{1,0:T(8,128)(2,1)S(1)} %copy-done.98), channel_id=1, source_target_pairs={{0,8},{4,12},{8,0},{12,4},{16,24},{20,28},{24,16},{28,20},{1,9},{5... | collective-permute-start | bytes 1622024 | tf_op jit(solution)/shard_map/ppermute | solution.py:161
  142.6 22.5 %collective-permute-start.23 = (bf16[192,1408]{1,0:T(8,128)(2,1)S(1)}, bf16[192,1408]{1,0:T(8,128)(2,1)S(1)}, u32[]{:S(2)}, u32[]{:S(2)}) collective-permute-start(bf16[192,1408]{1,0:T(8,128)(2,1)S(1)} %copy-done.97), channel_id=1, source_target_pairs={{0,16},{4,20},{8,24},{12,28},{16,0},{20,4},{24,8},{28,12},{1,17},{... | collective-permute-start | bytes 1622024 | tf_op jit(solution)/shard_map/ppermute | solution.py:161
  165.1 20.3 %collective-permute-start.28 = (bf16[192,1408]{1,0:T(8,128)(2,1)S(1)}, bf16[192,1408]{1,0:T(8,128)(2,1)S(1)}, u32[]{:S(2)}, u32[]{:S(2)}) collective-permute-start(bf16[192,1408]{1,0:T(8,128)(2,1)S(1)} %add_convert_fusion.3), channel_id=1, source_target_pairs={{0,16},{4,20},{8,24},{12,28},{16,0},{20,4},{24,8},{28,12},{1,17},{... | collective-permute-start | bytes 1622024 | tf_op jit(solution)/shard_map/ppermute | solution.py:161
  166.9 18.6 %collective-permute-start.29 = (bf16[192,1408]{1,0:T(8,128)(2,1)S(1)}, bf16[192,1408]{1,0:T(8,128)(2,1)S(1)}, u32[]{:S(2)}, u32[]{:S(2)}) collective-permute-start(bf16[192,1408]{1,0:T(8,128)(2,1)S(1)} %add_convert_fusion.2), channel_id=1, source_target_pairs={{0,8},{4,12},{8,0},{12,4},{16,24},{20,28},{24,16},{28,20},{1,9},{5... | collective-permute-start | bytes 1622024 | tf_op jit(solution)/shard_map/ppermute | solution.py:161
  195.6 27.1 %collective-permute-start.33 = (bf16[2,192,1408]{2,1,0:T(8,128)(2,1)}, bf16[2,192,1408]{2,1,0:T(8,128)(2,1)}, u32[]{:S(2)}, u32[]{:S(2)}) collective-permute-start(bf16[2,192,1408]{2,1,0:T(8,128)(2,1)} %get-tuple-element.210), channel_id=1, source_target_pairs={{0,16},{4,20},{8,24},{12,28},{16,0},{20,4},{24,8},{28,12},{1,17},{... | collective-permute-start | bytes 3244040 | tf_op jit(solution)/shard_map/ppermute | solution.py:161
  196.7 28.7 %collective-permute-start.32 = (bf16[2,192,1408]{2,1,0:T(8,128)(2,1)}, bf16[2,192,1408]{2,1,0:T(8,128)(2,1)}, u32[]{:S(2)}, u32[]{:S(2)}) collective-permute-start(bf16[2,192,1408]{2,1,0:T(8,128)(2,1)} %get-tuple-element.204), channel_id=1, source_target_pairs={{0,8},{4,12},{8,0},{12,4},{16,24},{20,28},{24,16},{28,20},{1,9},{5... | collective-permute-start | bytes 3244040 | tf_op jit(solution)/shard_map/ppermute | solution.py:161
  207.7 35.5 %collective-permute-start.34 = (bf16[2,192,1408]{2,1,0:T(8,128)(2,1)}, bf16[2,192,1408]{2,1,0:T(8,128)(2,1)S(1)}, u32[]{:S(2)}, u32[]{:S(2)}) collective-permute-start(bf16[2,192,1408]{2,1,0:T(8,128)(2,1)} %get-tuple-element.211), channel_id=1, source_target_pairs={{0,16},{4,20},{8,24},{12,28},{16,0},{20,4},{24,8},{28,12},{1,17},{... | collective-permute-start | bytes 3244040 | tf_op jit(solution)/shard_map/ppermute | solution.py:161
  208.8 34.8 %collective-permute-start.31 = (bf16[2,192,1408]{2,1,0:T(8,128)(2,1)}, bf16[2,192,1408]{2,1,0:T(8,128)(2,1)S(1)}, u32[]{:S(2)}, u32[]{:S(2)}) collective-permute-start(bf16[2,192,1408]{2,1,0:T(8,128)(2,1)} %get-tuple-element.207), channel_id=1, source_target_pairs={{0,8},{4,12},{8,0},{12,4},{16,24},{20,28},{24,16},{28,20},{1,9},{5... | collective-permute-start | bytes 3244040 | tf_op jit(solution)/shard_map/ppermute | solution.py:161
  243.6 30.3 %collective-permute-start.35 = (bf16[2,192,1408]{2,1,0:T(8,128)(2,1)}, bf16[2,192,1408]{2,1,0:T(8,128)(2,1)S(1)}, u32[]{:S(2)}, u32[]{:S(2)}) collective-permute-start(bf16[2,192,1408]{2,1,0:T(8,128)(2,1)} %add_convert_fusion.1), channel_id=1, source_target_pairs={{0,16},{4,20},{8,24},{12,28},{16,0},{20,4},{24,8},{28,12},{1,17},{... | collective-permute-start | bytes 3244040 | tf_op jit(solution)/shard_map/ppermute | solution.py:161
  244.9 28.9 %collective-permute-start.36 = (bf16[2,192,1408]{2,1,0:T(8,128)(2,1)}, bf16[2,192,1408]{2,1,0:T(8,128)(2,1)}, u32[]{:S(2)}, u32[]{:S(2)}) collective-permute-start(bf16[2,192,1408]{2,1,0:T(8,128)(2,1)} %add_convert_fusion), channel_id=1, source_target_pairs={{0,8},{4,12},{8,0},{12,4},{16,24},{20,28},{24,16},{28,20},{1,9},{5... | collective-permute-start | bytes 3244040 | tf_op jit(solution)/shard_map/ppermute | solution.py:161
  245.7 22.6 %collective-permute-start.37 = (f32[8,768]{1,0:T(8,128)S(1)}, f32[8,768]{1,0:T(8,128)S(1)}, u32[]{:S(2)}, u32[]{:S(2)}) collective-permute-start(f32[8,768]{1,0:T(8,128)S(1)} %copy-done.76), channel_id=1, source_target_pairs={{0,8},{4,12},{8,0},{12,4},{16,24},{20,28},{24,16},{28,20},{1,9},{5... | collective-permute-start | bytes 73736 | tf_op jit(solution)/shard_map/ppermute | solution.py:161
  283.0 27.0 %collective-permute-start.39 = (bf16[2,192,1408]{2,1,0:T(8,128)(2,1)}, bf16[2,192,1408]{2,1,0:T(8,128)(2,1)S(1)}, u32[]{:S(2)}, u32[]{:S(2)}) collective-permute-start(bf16[2,192,1408]{2,1,0:T(8,128)(2,1)} %get-tuple-element.219.refs_0_), channel_id=1, source_target_pairs={{0,16},{4,20},{8,24},{12,28},{16,0},{20,4},{24,8},{28,12},{1,17},{... | collective-permute-start | bytes 3244040 | tf_op jit(solution)/shard_map/ppermute | solution.py:161
  283.7 45.7 %collective-permute-start.41 = (bf16[2,192,1408]{2,1,0:T(8,128)(2,1)}, bf16[2,192,1408]{2,1,0:T(8,128)(2,1)S(1)}, u32[]{:S(2)}, u32[]{:S(2)}) collective-permute-start(bf16[2,192,1408]{2,1,0:T(8,128)(2,1)} %get-tuple-element.220.refs_4_.refs_2_), channel_id=1, source_target_pairs={{0,16},{4,20},{8,24},{12,28},{16,0},{20,4},{24,8},{28,12},{1,17},{... | collective-permute-start | bytes 3244040 | tf_op jit(solution)/shard_map/ppermute | solution.py:161
  285.1 44.3 %collective-permute-start.40 = (bf16[2,192,1408]{2,1,0:T(8,128)(2,1)}, bf16[2,192,1408]{2,1,0:T(8,128)(2,1)}, u32[]{:S(2)}, u32[]{:S(2)}) collective-permute-start(bf16[2,192,1408]{2,1,0:T(8,128)(2,1)} %get-tuple-element.219.refs_0_), channel_id=1, source_target_pairs={{0,8},{4,12},{8,0},{12,4},{16,24},{20,28},{24,16},{28,20},{1,9},{5... | collective-permute-start | bytes 3244040 | tf_op jit(solution)/shard_map/ppermute | solution.py:161
  285.8 45.9 %collective-permute-start.42 = (bf16[2,192,1408]{2,1,0:T(8,128)(2,1)}, bf16[2,192,1408]{2,1,0:T(8,128)(2,1)S(1)}, u32[]{:S(2)}, u32[]{:S(2)}) collective-permute-start(bf16[2,192,1408]{2,1,0:T(8,128)(2,1)} %get-tuple-element.220.refs_4_.refs_2_), channel_id=1, source_target_pairs={{0,8},{4,12},{8,0},{12,4},{16,24},{20,28},{24,16},{28,20},{1,9},{5... | collective-permute-start | bytes 3244040 | tf_op jit(solution)/shard_map/ppermute | solution.py:161
  293.7 40.6 %collective-permute-start.56 = (f32[8,192]{0,1:T(8,128)S(1)}, f32[8,192]{0,1:T(8,128)S(1)}, u32[]{:S(2)}, u32[]{:S(2)}) collective-permute-start(f32[8,192]{0,1:T(8,128)S(1)} %bitcast_add_fusion), channel_id=1, source_target_pairs={{0,3},{1,2},{2,1},{3,0},{4,7},{5,6},{6,5},{7,4},{8,11},{9,10},{10,... | collective-permute-start | bytes 18440 | tf_op jit(solution)/shard_map/ppermute | solution.py:176
  331.8 23.7 %collective-permute-start.43 = (bf16[2,192,1408]{2,1,0:T(8,128)(2,1)}, bf16[2,192,1408]{2,1,0:T(8,128)(2,1)}, u32[]{:S(2)}, u32[]{:S(2)}) collective-permute-start(bf16[2,192,1408]{2,1,0:T(8,128)(2,1)} %collective-permute-done.40.refs_1_), channel_id=1, source_target_pairs={{0,16},{4,20},{8,24},{12,28},{16,0},{20,4},{24,8},{28,12},{1,17},{... | collective-permute-start | bytes 3244040 | tf_op jit(solution)/shard_map/ppermute | solution.py:161
  332.4 23.1 %collective-permute-start.44 = (bf16[2,192,1408]{2,1,0:T(8,128)(2,1)S(1)}, bf16[2,192,1408]{2,1,0:T(8,128)(2,1)}, u32[]{:S(2)}, u32[]{:S(2)}) collective-permute-start(bf16[2,192,1408]{2,1,0:T(8,128)(2,1)S(1)} %collective-permute-done.41.refs_2_.refs_6_), channel_id=1, source_target_pairs={{0,8},{4,12},{8,0},{12,4},{16,24},{20,28},{24,16},{28,20},{1,9},{5... | collective-permute-start | bytes 3244040 | tf_op jit(solution)/shard_map/ppermute | solution.py:161
  334.3 20.0 %collective-permute-start.57 = (f32[8,192]{0,1:T(8,128)S(1)}, f32[8,192]{0,1:T(8,128)S(1)}, u32[]{:S(2)}, u32[]{:S(2)}) collective-permute-start(f32[8,192]{0,1:T(8,128)S(1)} %add.355), channel_id=1, source_target_pairs={{0,8},{4,12},{8,0},{12,4},{16,24},{20,28},{24,16},{28,20},{1,9},{5... | collective-permute-start | bytes 18440 | tf_op jit(solution)/shard_map/ppermute | solution.py:161
  355.4 13.1 %collective-permute-start.51 = (bf16[2,192,256]{2,1,0:T(8,128)(2,1)S(1)}, bf16[2,192,256]{2,1,0:T(8,128)(2,1)S(1)}, u32[]{:S(2)}, u32[]{:S(2)}) collective-permute-start(bf16[2,192,256]{2,1,0:T(8,128)(2,1)S(1)} %add_convert_fusion.16), channel_id=1, source_target_pairs={{0,3},{1,2},{2,1},{3,0},{4,7},{5,6},{6,5},{7,4},{8,11},{9,10},{10,... | collective-permute-start | bytes 589832 | tf_op jit(solution)/shard_map/ppermute | solution.py:176
  375.7 19.1 %collective-permute-start.53 = (bf16[2,192,256]{2,1,0:T(8,128)(2,1)S(1)}, bf16[2,192,256]{2,1,0:T(8,128)(2,1)S(1)}, u32[]{:S(2)}, u32[]{:S(2)}) collective-permute-start(bf16[2,192,256]{2,1,0:T(8,128)(2,1)S(1)} %add_convert_fusion.17), channel_id=1, source_target_pairs={{0,3},{1,2},{2,1},{3,0},{4,7},{5,6},{6,5},{7,4},{8,11},{9,10},{10,... | collective-permute-start | bytes 589832 | tf_op jit(solution)/shard_map/ppermute | solution.py:176
  379.5 15.5 %collective-permute-start.46 = (bf16[192,1408]{1,0:T(8,128)(2,1)S(1)}, bf16[192,1408]{1,0:T(8,128)(2,1)S(1)}, u32[]{:S(2)}, u32[]{:S(2)}) collective-permute-start(bf16[192,1408]{1,0:T(8,128)(2,1)S(1)} %copy-done.92), channel_id=1, source_target_pairs={{0,8},{4,12},{8,0},{12,4},{16,24},{20,28},{24,16},{28,20},{1,9},{5... | collective-permute-start | bytes 1622024 | tf_op jit(solution)/shard_map/ppermute | solution.py:161
  380.2 17.8 %collective-permute-start.47 = (bf16[192,1408]{1,0:T(8,128)(2,1)S(1)}, bf16[192,1408]{1,0:T(8,128)(2,1)S(1)}, u32[]{:S(2)}, u32[]{:S(2)}) collective-permute-start(bf16[192,1408]{1,0:T(8,128)(2,1)S(1)} %copy-done.92), channel_id=1, source_target_pairs={{0,16},{4,20},{8,24},{12,28},{16,0},{20,4},{24,8},{28,12},{1,17},{... | collective-permute-start | bytes 1622024 | tf_op jit(solution)/shard_map/ppermute | solution.py:161
  381.8 16.2 %collective-permute-start.48 = (bf16[192,1408]{1,0:T(8,128)(2,1)S(1)}, bf16[192,1408]{1,0:T(8,128)(2,1)S(1)}, u32[]{:S(2)}, u32[]{:S(2)}) collective-permute-start(bf16[192,1408]{1,0:T(8,128)(2,1)S(1)} %copy-done.93), channel_id=1, source_target_pairs={{0,8},{4,12},{8,0},{12,4},{16,24},{20,28},{24,16},{28,20},{1,9},{5... | collective-permute-start | bytes 1622024 | tf_op jit(solution)/shard_map/ppermute | solution.py:161
  383.1 14.9 %collective-permute-start.49 = (bf16[192,1408]{1,0:T(8,128)(2,1)S(1)}, bf16[192,1408]{1,0:T(8,128)(2,1)}, u32[]{:S(2)}, u32[]{:S(2)}) collective-permute-start(bf16[192,1408]{1,0:T(8,128)(2,1)S(1)} %copy-done.93), channel_id=1, source_target_pairs={{0,16},{4,20},{8,24},{12,28},{16,0},{20,4},{24,8},{28,12},{1,17},{... | collective-permute-start | bytes 1622024 | tf_op jit(solution)/shard_map/ppermute | solution.py:161
  416.0 15.5 %collective-permute-start.61 = (bf16[768,128]{1,0:T(8,128)(2,1)}, bf16[768,128]{1,0:T(8,128)(2,1)S(1)}, u32[]{:S(2)}, u32[]{:S(2)}) collective-permute-start(bf16[768,128]{1,0:T(8,128)(2,1)} %get-tuple-element.249), channel_id=1, source_target_pairs={{0,16},{4,20},{8,24},{12,28},{16,0},{20,4},{24,8},{28,12},{1,17},{... | collective-permute-start | bytes 589832 | tf_op jit(solution)/shard_map/ppermute | solution.py:161
  417.7 13.9 %collective-permute-start.60 = (bf16[768,128]{1,0:T(8,128)(2,1)}, bf16[768,128]{1,0:T(8,128)(2,1)S(1)}, u32[]{:S(2)}, u32[]{:S(2)}) collective-permute-start(bf16[768,128]{1,0:T(8,128)(2,1)} %get-tuple-element.247), channel_id=1, source_target_pairs={{0,8},{4,12},{8,0},{12,4},{16,24},{20,28},{24,16},{28,20},{1,9},{5... | collective-permute-start | bytes 589832 | tf_op jit(solution)/shard_map/ppermute | solution.py:161
  418.4 13.2 %collective-permute-start.59 = (bf16[768,128]{1,0:T(8,128)(2,1)}, bf16[768,128]{1,0:T(8,128)(2,1)S(1)}, u32[]{:S(2)}, u32[]{:S(2)}) collective-permute-start(bf16[768,128]{1,0:T(8,128)(2,1)} %get-tuple-element.245), channel_id=1, source_target_pairs={{0,8},{4,12},{8,0},{12,4},{16,24},{20,28},{24,16},{28,20},{1,9},{5... | collective-permute-start | bytes 589832 | tf_op jit(solution)/shard_map/ppermute | solution.py:161
  434.1 53.2 %collective-permute-start.72 = (bf16[4,256,1408]{2,1,0:T(8,128)(2,1)}, bf16[4,256,1408]{2,1,0:T(8,128)(2,1)S(1)}, u32[]{:S(2)}, u32[]{:S(2)}) collective-permute-start(bf16[4,256,1408]{2,1,0:T(8,128)(2,1)} %get-tuple-element.271), channel_id=1, source_target_pairs={{0,4},{4,0},{8,12},{12,8},{16,20},{20,16},{24,28},{28,24},{1,5},{5... | collective-permute-start | bytes 8650760 | tf_op jit(solution)/shard_map/ppermute | solution.py:165
  439.0 48.4 %collective-permute-start.73 = (bf16[4,256,1408]{2,1,0:T(8,128)(2,1)}, bf16[4,256,1408]{2,1,0:T(8,128)(2,1)}, u32[]{:S(2)}, u32[]{:S(2)}) collective-permute-start(bf16[4,256,1408]{2,1,0:T(8,128)(2,1)} %get-tuple-element.274), channel_id=1, source_target_pairs={{0,4},{4,0},{8,12},{12,8},{16,20},{20,16},{24,28},{28,24},{1,5},{5... | collective-permute-start | bytes 8650760 | tf_op jit(solution)/shard_map/ppermute | solution.py:165
  439.0 17.0 %collective-permute-start.65 = (bf16[192,1408]{1,0:T(8,128)(2,1)}, bf16[192,1408]{1,0:T(8,128)(2,1)}, u32[]{:S(2)}, u32[]{:S(2)}) collective-permute-start(bf16[192,1408]{1,0:T(8,128)(2,1)} %copy-done.94), channel_id=1, source_target_pairs={{0,16},{4,20},{8,24},{12,28},{16,0},{20,4},{24,8},{28,12},{1,17},{... | collective-permute-start | bytes 1622024 | tf_op jit(solution)/shard_map/ppermute | solution.py:161
  439.4 17.9 %collective-permute-start.66 = (bf16[192,1408]{1,0:T(8,128)(2,1)}, bf16[192,1408]{1,0:T(8,128)(2,1)}, u32[]{:S(2)}, u32[]{:S(2)}) collective-permute-start(bf16[192,1408]{1,0:T(8,128)(2,1)} %collective-permute-done.49.refs_6_), channel_id=1, source_target_pairs={{0,8},{4,12},{8,0},{12,4},{16,24},{20,28},{24,16},{28,20},{1,9},{5... | collective-permute-start | bytes 1622024 | tf_op jit(solution)/shard_map/ppermute | solution.py:161
  457.3 26.1 %collective-permute-start.71 = (bf16[768,256]{1,0:T(8,128)(2,1)}, bf16[768,256]{1,0:T(8,128)(2,1)S(1)}, u32[]{:S(2)}, u32[]{:S(2)}) collective-permute-start(bf16[768,256]{1,0:T(8,128)(2,1)} %get-tuple-element.265.refs_0_), channel_id=1, source_target_pairs={{0,16},{4,20},{8,24},{12,28},{16,0},{20,4},{24,8},{28,12},{1,17},{... | collective-permute-start | bytes 1179656 | tf_op jit(solution)/shard_map/ppermute | solution.py:161
  464.0 19.5 %collective-permute-start.69 = (bf16[768,256]{1,0:T(8,128)(2,1)}, bf16[768,256]{1,0:T(8,128)(2,1)}, u32[]{:S(2)}, u32[]{:S(2)}) collective-permute-start(bf16[768,256]{1,0:T(8,128)(2,1)} %get-tuple-element.266.refs_4_), channel_id=1, source_target_pairs={{0,16},{4,20},{8,24},{12,28},{16,0},{20,4},{24,8},{28,12},{1,17},{... | collective-permute-start | bytes 1179656 | tf_op jit(solution)/shard_map/ppermute | solution.py:161
  466.0 17.5 %collective-permute-start.70 = (bf16[768,256]{1,0:T(8,128)(2,1)}, bf16[768,256]{1,0:T(8,128)(2,1)}, u32[]{:S(2)}, u32[]{:S(2)}) collective-permute-start(bf16[768,256]{1,0:T(8,128)(2,1)} %get-tuple-element.266.refs_4_), channel_id=1, source_target_pairs={{0,8},{4,12},{8,0},{12,4},{16,24},{20,28},{24,16},{28,20},{1,9},{5... | collective-permute-start | bytes 1179656 | tf_op jit(solution)/shard_map/ppermute | solution.py:161
  487.2 19.1 %collective-permute-start.80 = (bf16[2,384,256]{2,1,0:T(8,128)(2,1)}, bf16[2,384,256]{2,1,0:T(8,128)(2,1)S(1)}, u32[]{:S(2)}, u32[]{:S(2)}) collective-permute-start(bf16[2,384,256]{2,1,0:T(8,128)(2,1)} %get-tuple-element.280), channel_id=1, source_target_pairs={{0,1},{1,0},{2,3},{3,2},{4,5},{5,4},{6,7},{7,6},{8,9},{9,8},{10,11... | collective-permute-start | bytes 1179656 | tf_op jit(solution)/shard_map/ppermute | solution.py:176
  487.3 107.5 %collective-permute-start.93 = (bf16[4,1408,256]{2,1,0:T(8,128)(2,1)}, bf16[4,1408,256]{2,1,0:T(8,128)(2,1)}, u32[]{:S(2)}, u32[]{:S(2)}) collective-permute-start(bf16[4,1408,256]{2,1,0:T(8,128)(2,1)} %get-tuple-element.308), channel_id=1, source_target_pairs={{0,4},{4,0},{8,12},{12,8},{16,20},{20,16},{24,28},{28,24},{1,5},{5... | collective-permute-start | bytes 8650760 | tf_op jit(solution)/shard_map/ppermute | solution.py:165
  495.1 13.3 %collective-permute-start.74 = (f32[8,768]{1,0:T(8,128)S(1)}, f32[8,768]{1,0:T(8,128)S(1)}, u32[]{:S(2)}, u32[]{:S(2)}) collective-permute-start(f32[8,768]{1,0:T(8,128)S(1)} %select_add_fusion), channel_id=1, source_target_pairs={{0,8},{4,12},{8,0},{12,4},{16,24},{20,28},{24,16},{28,20},{1,9},{5... | collective-permute-start | bytes 73736 | tf_op jit(solution)/shard_map/ppermute | solution.py:161
  506.3 19.4 %collective-permute-start.84 = (bf16[2,384,256]{2,1,0:T(8,128)(2,1)}, bf16[2,384,256]{2,1,0:T(8,128)(2,1)S(1)}, u32[]{:S(2)}, u32[]{:S(2)}) collective-permute-start(bf16[2,384,256]{2,1,0:T(8,128)(2,1)} %get-tuple-element.285), channel_id=1, source_target_pairs={{0,1},{1,0},{2,3},{3,2},{4,5},{5,4},{6,7},{7,6},{8,9},{9,8},{10,11... | collective-permute-start | bytes 1179656 | tf_op jit(solution)/shard_map/ppermute | solution.py:176
  508.4 17.4 %collective-permute-start.81 = (bf16[2,384,256]{2,1,0:T(8,128)(2,1)S(1)}, bf16[2,384,256]{2,1,0:T(8,128)(2,1)S(1)}, u32[]{:S(2)}, u32[]{:S(2)}) collective-permute-start(bf16[2,384,256]{2,1,0:T(8,128)(2,1)S(1)} %add_convert_fusion.7), channel_id=1, source_target_pairs={{0,3},{1,2},{2,1},{3,0},{4,7},{5,6},{6,5},{7,4},{8,11},{9,10},{10,... | collective-permute-start | bytes 1179656 | tf_op jit(solution)/shard_map/ppermute | solution.py:176
  525.9 24.4 %collective-permute-start.85 = (bf16[2,384,256]{2,1,0:T(8,128)(2,1)S(1)}, bf16[2,384,256]{2,1,0:T(8,128)(2,1)S(1)}, u32[]{:S(2)}, u32[]{:S(2)}) collective-permute-start(bf16[2,384,256]{2,1,0:T(8,128)(2,1)S(1)} %add_convert_fusion.5.refs_0_), channel_id=1, source_target_pairs={{0,1},{1,0},{2,3},{3,2},{4,5},{5,4},{6,7},{7,6},{8,9},{9,8},{10,11... | collective-permute-start | bytes 1179656 | tf_op jit(solution)/shard_map/ppermute | solution.py:176
  527.6 26.9 %collective-permute-start.87 = (bf16[2,384,256]{2,1,0:T(8,128)(2,1)S(1)}, bf16[2,384,256]{2,1,0:T(8,128)(2,1)S(1)}, u32[]{:S(2)}, u32[]{:S(2)}) collective-permute-start(bf16[2,384,256]{2,1,0:T(8,128)(2,1)S(1)} %add_convert_fusion.6), channel_id=1, source_target_pairs={{0,3},{1,2},{2,1},{3,0},{4,7},{5,6},{6,5},{7,4},{8,11},{9,10},{10,... | collective-permute-start | bytes 1179656 | tf_op jit(solution)/shard_map/ppermute | solution.py:176
  529.6 13.0 %collective-permute-start.77 = (f32[8,768]{1,0:T(8,128)S(1)}, f32[8,768]{1,0:T(8,128)S(1)}, u32[]{:S(2)}, u32[]{:S(2)}) collective-permute-start(f32[8,768]{1,0:T(8,128)S(1)} %add_add_fusion.1), channel_id=1, source_target_pairs={{0,1},{1,0},{2,3},{3,2},{4,5},{5,4},{6,7},{7,6},{8,9},{9,8},{10,11... | collective-permute-start | bytes 73736 | tf_op jit(solution)/shard_map/ppermute | solution.py:176
  530.7 17.8 %collective-permute-start.78 = (f32[8,768]{1,0:T(8,128)S(1)}, f32[8,768]{1,0:T(8,128)S(1)}, u32[]{:S(2)}, u32[]{:S(2)}) collective-permute-start(f32[8,768]{1,0:T(8,128)S(1)} %add_add_fusion.1), channel_id=1, source_target_pairs={{0,2},{1,3},{2,0},{3,1},{4,6},{5,7},{6,4},{7,5},{8,10},{9,11},{10,... | collective-permute-start | bytes 73736 | tf_op jit(solution)/shard_map/ppermute | solution.py:176
  554.6 17.4 %collective-permute-start.88 = (bf16[2,384,256]{2,1,0:T(8,128)(2,1)S(1)}, bf16[2,384,256]{2,1,0:T(8,128)(2,1)S(1)}, u32[]{:S(2)}, u32[]{:S(2)}) collective-permute-start(bf16[2,384,256]{2,1,0:T(8,128)(2,1)S(1)} %add_convert_fusion.4.refs_0_), channel_id=1, source_target_pairs={{0,1},{1,0},{2,3},{3,2},{4,5},{5,4},{6,7},{7,6},{8,9},{9,8},{10,11... | collective-permute-start | bytes 1179656 | tf_op jit(solution)/shard_map/ppermute | solution.py:176
  572.0 19.1 %all-to-all-start.2 = ((bf16[8,256,256]{2,1,0:T(8,128)(2,1)}), bf16[8,256,256]{2,1,0:T(8,128)(2,1)S(1)}, u32[]{:S(2)}, u32[]{:S(2)}) async-start(bf16[8,256,256]{2,1,0:T(8,128)(2,1)} %unpack.2), calls=%async_computation.2 | async-start | bytes 2097152 | tf_op jit(solution)/shard_map/all_to_all | solution.py:1210
  583.3 19.7 %collective-permute-start.92 = (bf16[4,512,256]{2,1,0:T(8,128)(2,1)}, bf16[4,512,256]{2,1,0:T(8,128)(2,1)}, u32[]{:S(2)}, u32[]{:S(2)}) collective-permute-start(bf16[4,512,256]{2,1,0:T(8,128)(2,1)} %get-tuple-element.307), channel_id=1, source_target_pairs={{0,4},{4,0},{8,12},{12,8},{16,20},{20,16},{24,28},{28,24},{1,5},{5... | collective-permute-start | bytes 3145736 | tf_op jit(solution)/shard_map/ppermute | solution.py:165
  583.4 22.4 %collective-permute-start.91 = (bf16[4,256,512]{2,1,0:T(8,128)(2,1)}, bf16[4,256,512]{2,1,0:T(8,128)(2,1)S(1)}, u32[]{:S(2)}, u32[]{:S(2)}) collective-permute-start(bf16[4,256,512]{2,1,0:T(8,128)(2,1)} %get-tuple-element.306), channel_id=1, source_target_pairs={{0,4},{4,0},{8,12},{12,8},{16,20},{20,16},{24,28},{28,24},{1,5},{5... | collective-permute-start | bytes 3145736 | tf_op jit(solution)/shard_map/ppermute | solution.py:165
  583.9 16.8 %collective-permute-start.90 = (bf16[2,256,512]{2,1,0:T(8,128)(2,1)}, bf16[2,256,512]{2,1,0:T(8,128)(2,1)}, u32[]{:S(2)}, u32[]{:S(2)}) collective-permute-start(bf16[2,256,512]{2,1,0:T(8,128)(2,1)} %get-tuple-element.305), channel_id=1, source_target_pairs={{0,4},{4,0},{8,12},{12,8},{16,20},{20,16},{24,28},{28,24},{1,5},{5... | collective-permute-start | bytes 1572872 | tf_op jit(solution)/shard_map/ppermute | solution.py:165
  591.2 20.3 %all-to-all-start.3 = ((bf16[8,288,256]{2,1,0:T(8,128)(2,1)}), bf16[8,288,256]{2,1,0:T(8,128)(2,1)S(1)}, u32[]{:S(2)}, u32[]{:S(2)}) async-start(bf16[8,288,256]{2,1,0:T(8,128)(2,1)} %unpack.3), calls=%async_computation.3 | async-start | bytes 2359296 | tf_op jit(solution)/shard_map/all_to_all | solution.py:1210
  (142 other events, 2043.7 us)

commit v10 on v9

--- a/solution.py
+++ b/solution.py
@@ -1153,12 +1153,10 @@
                 ).astype(BF16)
 
     got_q, got_kv = exchange(dwqkv_sums[:parts]), exchange(dwqkv_sums[parts:])
-    dots_a = (dots_a + by_z(dots_a, 1)) + (by_z(dots_a, 2) + by_z(dots_a, 3))
-    back_a = back_columns(flat_a, dots_a, low_a, high_a)
     down_totals = z_last(z_covered(down_half, down_half, 3, da_half))
     ins = [(t, None, None) for t in down_totals] + [(after_rows, None, None)]
     out_rows = run(
-        finish_body, "finish", (1,), after(meta, dots_a), ins,
+        finish_body, "finish", (1,), meta, ins,
         [((rp, ds), BF16, None, None)] * parts,
     )
 
@@ -1213,6 +1211,9 @@
 
     da_half = z_covered(da_half, da_half, 3, out_rows[0])
     layer_rows = unpack(out_rows, x_all, False, table)
+    dots_a = after(dots_a, out_rows[0])
+    dots_a = (dots_a + by_z(dots_a, 1)) + (by_z(dots_a, 2) + by_z(dots_a, 3))
+    back_a = back_columns(flat_a, dots_a, low_a, high_a)
     expertin_grad = fold(got_in, after(meta, da_half, layer_rows))
     da_totals = z_last(da_half)
     layer_out, _ = land(after(layer_rows, expertin_grad, da_totals[1]))

time: 621 us -> 623 us (level)
  transfers between devices with their start and end apart: 98 -> 98, of which waited for: 38 -> 38; matrix products, arithmetic and copies ran while one was open for 8% -> 8% of each run, Pallas kernels for 29% -> 28%
where the time goes in v10:
time: 623 us; the launch traced here: 618 us
  Pallas kernels  229 us (37%)
  waiting for transfers between devices  191 us (31%)
  starting transfers between devices  123 us (20%)
  local copies, waits for them, and re-layouts  37.7 us (6%)
  other arithmetic  33.5 us (5%)
    pallas_call x28, Pallas kernels, run(): pl.pallas_call(body, name=name, grid_spec=pltpu.PrefetchScalarGridSpec(nu...  229 us
    ppermute x57, waiting for transfers between devices, by_group(): return lax.ppermute(value, 'dp', pairs)  125 us
    ppermute x57, starting transfers between devices, by_group(): return lax.ppermute(value, 'dp', pairs)  63.6 us
    ppermute x20, waiting for transfers between devices, by_z(): return lax.ppermute(value, 'tensor', [(a, a ^ mask) for a in range(tp)])  51.3 us
    ppermute x20, starting transfers between devices, by_z(): return lax.ppermute(value, 'tensor', [(a, a ^ mask) for a in range(tp)])  36.8 us
    add x4, other arithmetic, add_up(): return sum((v.astype(F32) for v in got))  12.6 us
  transfers between devices with their start and end apart: 98, of which 38 were waited for; matrix products, arithmetic and copies ran while one was open for 8% of the time, Pallas kernels for 28%

profile of v10, /device:TPU:0, one launch (start us, length us, event | category | flops | bytes accessed | tf_op | source)
XLA Modules:
  0.0 617.9 jit_solution(7423176683576965657)
XLA Ops:
  3.4 6.0 copy.230
  10.0 5.1 all-to-all-start
  20.3 10.2 %all-to-all-done = bf16[8,256,256]{2,1,0:T(8,128)(2,1)S(1)} async-done(((bf16[8,256,256]{2,1,0:T(8,128)(2,1)}), bf16[8,256,256]{2,1,0:T(8,128)(2,1)S(1)}, u32[]{:S(2)}, u32[]{:S(2)}) %all-to-all-start) | async-done | bytes 1048608 | tf_op jit(solution)/shard_map/all_to_all | solution.py:308
  30.6 3.8 all-to-all-start.1
  34.4 4.0 pack.2
  43.3 8.5 %qkv.1 = (bf16[768,256]{1,0:T(8,128)(2,1)}, bf16[768,256]{1,0:T(8,128)(2,1)}, bf16[768,256]{1,0:T(8,128)(2,1)}, bf16[768,256]{1,0:T(8,128)(2,1)}, bf16[768,256]{...) custom-call(s32[24]{0:T(128)} %stack.147.m, ...), custom_call_target="tpu_custom_call" | custom-call | flops 2415919104 | bytes 7137280 | tf_op jit(solution)/shard_map/qkv/pallas_call | solution.py:61
  58.5 5.5 collective-permute-done.5
  65.0 4.1 pack.3
  82.5 12.0 %dhidden.1 = (bf16[192,1408]{1,0:T(8,128)(2,1)}, bf16[192,1408]{1,0:T(8,128)(2,1)}, bf16[192,1408]{1,0:T(8,128)(2,1)}, bf16[192,1408]{1,0:T(8,128)(2,1)}, bf16[1...) custom-call(s32[24]{0:T(128)} %stack.147.m, ...), custom_call_target="tpu_custom_call" | custom-call | flops 4429185024 | bytes 11714560 | tf_op jit(solution)/shard_map/dhidden/pallas_call | solution.py:61
  95.5 4.6 rope.1
  103.9 8.0 %attend.1 = (bf16[768,128]{1,0:T(8,128)(2,1)}, bf16[768,128]{1,0:T(8,128)(2,1)}, bf16[768,128]{1,0:T(8,128)(2,1)}, bf16[768,128]{1,0:T(8,128)(2,1)}) custom-call(s32[24]{0:T(128)} %stack.147.m, bf16[768,256]{1,0:T(8,128)(2,1)} %get-tuple-element.188.q_ref.refs_0_, bf16[768,256]{1,0:T(8,128)(2,1)} %get-tuple-element.189.kv_ref.refs_1_, ...), custom_call_target="tpu_custom_call" | custom-call | flops 301989888 | bytes 1753088 | tf_op jit(solution)/shard_map/attend/pallas_call | solution.py:61
  116.0 3.8 collective-permute-done.16.refs_1_
  122.0 2.7 collective-permute-done.24.refs_2_
  124.7 3.3 collective-permute-done.17.refs_3_
  128.7 9.9 %proj.1 = (bf16[2,384,256]{2,1,0:T(8,128)(2,1)}, bf16[2,384,256]{2,1,0:T(8,128)(2,1)}) custom-call(s32[24]{0:T(128)} %stack.147.m, bf16[768,128]{1,0:T(8,128)(2,1)} %get-tuple-element.190.refs_0_, bf16[768,128]{1,0:T(8,128)(2,1)} %copy-done.102, bf16[768,128]{1,0:T(8,128)(2,1)} %copy-done.104, bf16[768,128]{1,0:T(8,128)(2,1)} %copy-done.106, ...), custom_call_target="tpu_custom_call" | custom-call | flops 1610612736 | bytes 4481024 | tf_op jit(solution)/shard_map/proj/pallas_call | solution.py:61
  144.3 4.9 collective-permute-done.26
  150.3 3.7 collective-permute-start.27
  155.9 6.0 collective-permute-done.27
  162.0 3.2 collective-permute-done.22.refs_7_
  168.3 3.9 collective-permute-start.30
  173.4 6.9 %collective-permute-done.30.refs_1_ = bf16[2,384,256]{2,1,0:T(8,128)(2,1)S(1)} collective-permute-done((bf16[2,384,256]{2,1,0:T(8,128)(2,1)S(1)}, bf16[2,384,256]{2,1,0:T(8,128)(2,1)S(1)}, u32[]{:S(2)}, u32[]{:S(2)}) %collective-permute-start.30) | collective-permute-done | bytes 393248 | tf_op jit(solution)/shard_map/ppermute | solution.py:176
  181.1 4.4 norm.1
  185.5 10.2 %up.2 = (bf16[2,192,1408]{2,1,0:T(8,128)(2,1)}, bf16[2,192,1408]{2,1,0:T(8,128)(2,1)}, bf16[2,192,1408]{2,1,0:T(8,128)(2,1)}, bf16[2,192,1408]{2,1,0:T(8,128)(2,1)}) custom-call(s32[24]{0:T(128)} %stack.147.m, bf16[2,768,256]{2,1,0:T(8,128)(2,1)} %get-tuple-element.203.refs_0_.refs_1_, bf16[2,768,256]{2,1,0:T(8,128)(2,1)} %get-tuple-element.203.refs_0_.refs_1_, ...), custom_call_target="tpu_custom_call" | custom-call | flops 4429185024 | bytes 17481728 | tf_op jit(solution)/shard_map/up/pallas_call | solution.py:61
  197.4 10.3 %up.3 = (bf16[2,192,1408]{2,1,0:T(8,128)(2,1)}, bf16[2,192,1408]{2,1,0:T(8,128)(2,1)}, bf16[2,192,1408]{2,1,0:T(8,128)(2,1)}, bf16[2,192,1408]{2,1,0:T(8,128)(2,1)}) custom-call(s32[24]{0:T(128)} %stack.147.m, bf16[2,768,256]{2,1,0:T(8,128)(2,1)} %get-tuple-element.203.refs_0_.refs_1_, bf16[2,768,256]{2,1,0:T(8,128)(2,1)} %get-tuple-element.203.refs_0_.refs_1_, ...), custom_call_target="tpu_custom_call" | custom-call | flops 4429185024 | bytes 17481728 | tf_op jit(solution)/shard_map/up/pallas_call | solution.py:61
  210.1 12.7 %collective-permute-done.33 = bf16[2,192,1408]{2,1,0:T(8,128)(2,1)} collective-permute-done((bf16[2,192,1408]{2,1,0:T(8,128)(2,1)}, bf16[2,192,1408]{2,1,0:T(8,128)(2,1)}, u32[]{:S(2)}, u32[]{:S(2)}) %collective-permute-start.33) | collective-permute-done | bytes 1081376 | tf_op jit(solution)/shard_map/ppermute | solution.py:161
  222.8 2.6 add_convert_fusion
  225.4 2.5 add_convert_fusion.1
  227.9 15.3 %collective-permute-done.34.refs_5_ = bf16[2,192,1408]{2,1,0:T(8,128)(2,1)S(1)} collective-permute-done((bf16[2,192,1408]{2,1,0:T(8,128)(2,1)}, bf16[2,192,1408]{2,1,0:T(8,128)(2,1)S(1)}, u32[]{:S(2)}, u32[]{:S(2)}) %collective-permute-start.34) | collective-permute-done | bytes 1081376 | tf_op jit(solution)/shard_map/ppermute | solution.py:161
  247.0 21.4 %collective-permute-done.37 = f32[8,768]{1,0:T(8,128)S(1)} collective-permute-done((f32[8,768]{1,0:T(8,128)S(1)}, f32[8,768]{1,0:T(8,128)S(1)}, u32[]{:S(2)}, u32[]{:S(2)}) %collective-permute-start.37) | collective-permute-done | bytes 24608 | tf_op jit(solution)/shard_map/ppermute | solution.py:161
  269.0 3.2 collective-permute-done.38
  274.8 8.2 %mid.1 = (bf16[192,1408]{1,0:T(8,128)(2,1)}, bf16[192,1408]{1,0:T(8,128)(2,1)}, bf16[2,192,1408]{2,1,0:T(8,128)(2,1)}, bf16[2,192,1408]{2,1,0:T(8,128)(2,1)}, f32[192,8]{1,0:T(8,128)}) custom-call(s32[24]{0:T(128)} %stack.147.m, bf16[2,192,1408]{2,1,0:T(8,128)(2,1)} %get-tuple-element.206.refs_0_, bf16[2,192,1408]{2,1,0:T(8,128)(2,1)} %copy-done.14, ...), custom_call_target="tpu_custom_call" | custom-call | bytes 13006848 | tf_op jit(solution)/shard_map/mid/pallas_call | solution.py:61
  288.9 3.9 collective-permute-done.55
  293.8 16.3 %collective-permute-done.39.refs_0_.refs_2_ = bf16[2,192,1408]{2,1,0:T(8,128)(2,1)S(1)} collective-permute-done((bf16[2,192,1408]{2,1,0:T(8,128)(2,1)}, bf16[2,192,1408]{2,1,0:T(8,128)(2,1)S(1)}, u32[]{:S(2)}, u32[]{:S(2)}) %collective-permute-start.39) | collective-permute-done | bytes 1081376 | tf_op jit(solution)/shard_map/ppermute | solution.py:161
  310.0 19.3 %collective-permute-done.41.refs_2_.refs_6_ = bf16[2,192,1408]{2,1,0:T(8,128)(2,1)S(1)} collective-permute-done((bf16[2,192,1408]{2,1,0:T(8,128)(2,1)}, bf16[2,192,1408]{2,1,0:T(8,128)(2,1)S(1)}, u32[]{:S(2)}, u32[]{:S(2)}) %collective-permute-start.41) | collective-permute-done | bytes 1081376 | tf_op jit(solution)/shard_map/ppermute | solution.py:161
  335.7 11.0 %dx.3 = (bf16[2,192,256]{2,1,0:T(8,128)(2,1)}, bf16[2,192,256]{2,1,0:T(8,128)(2,1)}) custom-call(s32[24]{0:T(128)} %stack.147.m, bf16[2,192,1408]{2,1,0:T(8,128)(2,1)} %get-tuple-element.221.refs_0_, bf16[2,192,1408]{2,1,0:T(8,128)(2,1)} %collective-permute-done.40.refs_1_, bf16[2,192,1408]{2,1,0:T(8,128)(2,1)} %get-tuple-element.222.refs_4_.refs_2_, ...), custom_call_target="tpu_custom_call" | custom-call | flops 4429185024 | bytes 16302080 | tf_op jit(solution)/shard_map/dx/pallas_call | solution.py:61
  349.8 4.6 collective-permute-done.57
  355.5 11.1 %dx.2 = (bf16[2,192,256]{2,1,0:T(8,128)(2,1)}, bf16[2,192,256]{2,1,0:T(8,128)(2,1)}) custom-call(s32[24]{0:T(128)} %stack.147.m, bf16[2,192,1408]{2,1,0:T(8,128)(2,1)} %copy-done.10, bf16[2,192,1408]{2,1,0:T(8,128)(2,1)} %collective-permute-done.43.refs_1_.refs_3_, bf16[2,192,1408]{2,1,0:T(8,128)(2,1)} %copy-done.11, ...), custom_call_target="tpu_custom_call" | custom-call | flops 4429185024 | bytes 16302080 | tf_op jit(solution)/shard_map/dx/pallas_call | solution.py:61
  368.7 6.0 collective-permute-done.45
  375.7 3.8 collective-permute-start.53
  383.6 11.3 %dwin.2 = (bf16[4,256,1408]{2,1,0:T(8,128)(2,1)}, bf16[4,256,1408]{2,1,0:T(8,128)(2,1)}) custom-call(s32[24]{0:T(128)} %stack.147.m, bf16[2,192,1408]{2,1,0:T(8,128)(2,1)} %get-tuple-element.221.refs_0_, bf16[2,192,1408]{2,1,0:T(8,128)(2,1)} %collective-permute-done.40.refs_1_, bf16[2,192,1408]{2,1,0:T(8,128)(2,1)} %copy-done.10, ...), custom_call_target="tpu_custom_call" | custom-call | flops 4429185024 | bytes 15228928 | tf_op jit(solution)/shard_map/dwin/pallas_call | solution.py:61
  403.4 6.5 %norm_back.1 = (f32[2,768,256]{2,1,0:T(8,128)}, bf16[2,768,256]{2,1,0:T(8,128)(2,1)}, f32[5,2,256]{2,1,0:T(2,128)}) custom-call(s32[24]{0:T(128)} %stack.147.m, bf16[2,192,256]{2,1,0:T(8,128)(2,1)} %copy-done.21, bf16[2,192,256]{2,1,0:T(8,128)(2,1)} %copy-done.50, bf16[2,192,256]{2,1,0:T(8,128)(2,1)} %copy-done.22, bf16[2,192,256]{2,1,0:T(8,128)(2,1)} %copy-done.51, ...), custom_call_target="tpu_custom_call" | custom-call | bytes 5550080 | tf_op jit(solution)/shard_map/norm_back/pallas_call | solution.py:61
  409.9 6.1 dmix.1
  420.2 11.3 %dwin.3 = (bf16[4,256,1408]{2,1,0:T(8,128)(2,1)}, bf16[4,256,1408]{2,1,0:T(8,128)(2,1)}) custom-call(s32[24]{0:T(128)} %stack.147.m, bf16[2,192,1408]{2,1,0:T(8,128)(2,1)} %get-tuple-element.221.refs_0_, bf16[2,192,1408]{2,1,0:T(8,128)(2,1)} %collective-permute-done.40.refs_1_, bf16[2,192,1408]{2,1,0:T(8,128)(2,1)} %copy-done.10, ...), custom_call_target="tpu_custom_call" | custom-call | flops 4429185024 | bytes 15228928 | tf_op jit(solution)/shard_map/dwin/pallas_call | solution.py:61
  434.1 3.3 collective-permute-done.63.refs_9_
  440.2 14.4 %attend_back.1 = (bf16[768,256]{1,0:T(8,128)(2,1)}, f32[768,256]{1,0:T(8,128)}, f32[256,256]{1,0:T(8,128)}, f32[8,768]{1,0:T(8,128)}) custom-call(s32[24]{0:T(128)} %stack.147.m, bf16[768,256]{1,0:T(8,128)(2,1)} %get-tuple-element.188.q_ref.refs_0_, bf16[768,256]{1,0:T(8,128)(2,1)} %get-tuple-element.189.kv_ref.refs_1_, bf16[256,256]{1,0:T(8,128)(2,1)} %copy-done.29, ...), custom_call_target="tpu_custom_call" | custom-call | flops 754974720 | bytes 4792320 | tf_op jit(solution)/shard_map/attend_back/pallas_call | solution.py:61
  460.4 3.6 dkv.1
  467.3 16.2 %down.1 = (bf16[2,384,256]{2,1,0:T(8,128)(2,1)}, bf16[2,384,256]{2,1,0:T(8,128)(2,1)}, bf16[4,1408,256]{2,1,0:T(8,128)(2,1)}, bf16[4,1408,256]{2,1,0:T(8,128)(2,1)}) custom-call(s32[24]{0:T(128)} %stack.147.m, bf16[192,1408]{1,0:T(8,128)(2,1)} %get-tuple-element.227.refs_0_, bf16[192,1408]{1,0:T(8,128)(2,1)} %copy-done.94, bf16[192,1408]{1,0:T(8,128)(2,1)} %copy-done.95, ...), custom_call_target="tpu_custom_call" | custom-call | flops 8858370048 | bytes 17457152 | tf_op jit(solution)/shard_map/down/pallas_call | solution.py:61
  487.4 7.7 %dwproj.1 = (bf16[4,512,256]{2,1,0:T(8,128)(2,1)}, bf16[4,512,256]{2,1,0:T(8,128)(2,1)}) custom-call(s32[24]{0:T(128)} %stack.147.m, bf16[768,128]{1,0:T(8,128)(2,1)} %get-tuple-element.190.refs_0_, bf16[768,128]{1,0:T(8,128)(2,1)} %copy-done.102, bf16[768,128]{1,0:T(8,128)(2,1)} %copy-done.104, bf16[768,128]{1,0:T(8,128)(2,1)} %copy-done.106, ...), custom_call_target="tpu_custom_call" | custom-call | flops 1610612736 | bytes 4481024 | tf_op jit(solution)/shard_map/dwproj/pallas_call | solution.py:61
  498.7 7.6 %dattn.1 = (bf16[2,384,256]{2,1,0:T(8,128)(2,1)}, bf16[2,384,256]{2,1,0:T(8,128)(2,1)}) custom-call(s32[24]{0:T(128)} %stack.147.m, bf16[768,256]{1,0:T(8,128)(2,1)} %get-tuple-element.267.refs_0_, bf16[768,256]{1,0:T(8,128)(2,1)} %collective-permute-done.69.refs_1_, bf16[768,256]{1,0:T(8,128)(2,1)} %copy-done.101, ...), custom_call_target="tpu_custom_call" | custom-call | flops 2415919104 | bytes 7102464 | tf_op jit(solution)/shard_map/dattn/pallas_call | solution.py:61
  508.7 9.6 %dwqkv.1 = (bf16[4,256,512]{2,1,0:T(8,128)(2,1)}, bf16[4,256,512]{2,1,0:T(8,128)(2,1)}, bf16[2,256,512]{2,1,0:T(8,128)(2,1)}, bf16[2,256,512]{2,1,0:T(8,128)(2,1)}) custom-call(s32[24]{0:T(128)} %stack.147.m, bf16[768,256]{1,0:T(8,128)(2,1)} %get-tuple-element.267.refs_0_, bf16[768,256]{1,0:T(8,128)(2,1)} %collective-permute-done.69.refs_1_, ...), custom_call_target="tpu_custom_call" | custom-call | flops 2415919104 | bytes 7102464 | tf_op jit(solution)/shard_map/dwqkv/pallas_call | solution.py:61
  518.3 7.4 %collective-permute-done.78 = bf16[2,384,256]{2,1,0:T(8,128)(2,1)S(1)} collective-permute-done((bf16[2,384,256]{2,1,0:T(8,128)(2,1)}, bf16[2,384,256]{2,1,0:T(8,128)(2,1)S(1)}, u32[]{:S(2)}, u32[]{:S(2)}) %collective-permute-start.78) | collective-permute-done | bytes 393248 | tf_op jit(solution)/shard_map/ppermute | solution.py:176
  530.6 6.5 %collective-permute-done.82.refs_1_ = bf16[2,384,256]{2,1,0:T(8,128)(2,1)S(1)} collective-permute-done((bf16[2,384,256]{2,1,0:T(8,128)(2,1)S(1)}, bf16[2,384,256]{2,1,0:T(8,128)(2,1)S(1)}, u32[]{:S(2)}, u32[]{:S(2)}) %collective-permute-start.82) | collective-permute-done | bytes 393248 | tf_op jit(solution)/shard_map/ppermute | solution.py:176
  537.9 3.3 finish.1
  541.2 2.5 collective-permute-start.86
  543.7 9.0 %collective-permute-start.87 = (f32[8,768]{1,0:T(8,128)S(1)}, f32[8,768]{1,0:T(8,128)S(1)}, u32[]{:S(2)}, u32[]{:S(2)}) collective-permute-start(f32[8,768]{1,0:T(8,128)S(1)} %add_add_fusion.1), channel_id=1, source_target_pairs={{0,2},{1,3},{2,0},{3,1},{4,6},{5,7},{6,4},{7,5},{8,10},{9,11},{10,... | collective-permute-start | bytes 73736 | tf_op jit(solution)/shard_map/ppermute | solution.py:176
  554.5 4.1 collective-permute-done.88
  559.4 4.4 unpack.2
  563.8 10.4 %fold.1 = f32[4,256,2,1408]{3,2,1,0:T(2,128)} custom-call(s32[24]{0:T(128)} %stack.147.m, bf16[4,256,1408]{2,1,0:T(8,128)(2,1)} %get-tuple-element.231.refs_0_, bf16[4,256,1408]{2,1,0:T(8,128)(2,1)} %copy-done.6, bf16[4,256,1408]{2,1,0:T(8,128)(2,1)} %get-tuple-element.273.refs_2_, bf16[4,256,1408]{2,1,0:T(8,128)(2,1)} %collective-permute-done.74.refs_3_), custom_call_target="tpu_custom_call" | custom-call | bytes 23068672 | tf_op jit(solution)/shard_map/fold/pallas_call | solution.py:61
  574.2 3.8 all-to-all-start.2
  579.1 5.9 norm_back_first.1
  588.3 4.5 unpack.3
  593.4 3.6 all-to-all-start.3
  597.0 5.9 convert_add_fusion
  605.2 2.8 convert_add_fusion.1
  (506 shorter events, 156.8 us)
Async XLA Ops:
  9.4 59.6 %collective-permute-start.10 = (bf16[4,2,256,1408]{3,2,1,0:T(8,128)(2,1)}, bf16[4,2,256,1408]{3,2,1,0:T(8,128)(2,1)}, u32[]{:S(2)}, u32[]{:S(2)}) collective-permute-start(bf16[4,2,256,1408]{3,2,1,0:T(8,128)(2,1)} %bitcast.97.refs_2_.refs_4_), channel_id=1, source_target_pairs={{0,4},{4,0},{8,12},{12,8},{16,20},{20,16},{24,28},{28,24},{1,5},{5... | collective-permute-start | bytes 17301512 | tf_op jit(solution)/shard_map/ppermute | solution.py:165
  10.0 32.5 %collective-permute-start = (bf16[4,1408,256]{2,1,0:T(8,128)(2,1)}, bf16[4,1408,256]{2,1,0:T(8,128)(2,1)}, u32[]{:S(2)}, u32[]{:S(2)}) collective-permute-start(bf16[4,1408,256]{2,1,0:T(8,128)(2,1)} %refs_11_.2), channel_id=1, source_target_pairs={{0,4},{4,0},{8,12},{12,8},{16,20},{20,16},{24,28},{28,24},{1,5},{5... | collective-permute-start | bytes 8650760 | tf_op jit(solution)/shard_map/ppermute | solution.py:165
  10.0 20.5 %all-to-all-start = ((bf16[8,256,256]{2,1,0:T(8,128)(2,1)}), bf16[8,256,256]{2,1,0:T(8,128)(2,1)S(1)}, u32[]{:S(2)}, u32[]{:S(2)}) async-start(bf16[8,256,256]{2,1,0:T(8,128)(2,1)} %bitcast.99), calls=%async_computation | async-start | bytes 2097152 | tf_op jit(solution)/shard_map/all_to_all | solution.py:308
  15.2 23.2 %collective-permute-start.1 = (bf16[4,512,256]{2,1,0:T(8,128)(2,1)S(1)}, bf16[4,512,256]{2,1,0:T(8,128)(2,1)}, u32[]{:S(2)}, u32[]{:S(2)}) collective-permute-start(bf16[4,512,256]{2,1,0:T(8,128)(2,1)S(1)} %copy-done.91), channel_id=1, source_target_pairs={{0,4},{4,0},{8,12},{12,8},{16,20},{20,16},{24,28},{28,24},{1,5},{5... | collective-permute-start | bytes 3145736 | tf_op jit(solution)/shard_map/ppermute | solution.py:165
  15.7 26.8 %collective-permute-start.3 = (bf16[4,256,512]{2,1,0:T(8,128)(2,1)}, bf16[4,256,512]{2,1,0:T(8,128)(2,1)}, u32[]{:S(2)}, u32[]{:S(2)}) collective-permute-start(bf16[4,256,512]{2,1,0:T(8,128)(2,1)} %refs_9_.3), channel_id=1, source_target_pairs={{0,4},{4,0},{8,12},{12,8},{16,20},{20,16},{24,28},{28,24},{1,5},{5... | collective-permute-start | bytes 3145736 | tf_op jit(solution)/shard_map/ppermute | solution.py:165
  15.8 26.7 %collective-permute-start.4 = (bf16[2,256,512]{2,1,0:T(8,128)(2,1)}, bf16[2,256,512]{2,1,0:T(8,128)(2,1)}, u32[]{:S(2)}, u32[]{:S(2)}) collective-permute-start(bf16[2,256,512]{2,1,0:T(8,128)(2,1)} %refs_11_.3), channel_id=1, source_target_pairs={{0,4},{4,0},{8,12},{12,8},{16,20},{20,16},{24,28},{28,24},{1,5},{5... | collective-permute-start | bytes 1572872 | tf_op jit(solution)/shard_map/ppermute | solution.py:165
  30.6 33.4 %all-to-all-start.1 = ((bf16[8,256,256]{2,1,0:T(8,128)(2,1)}), bf16[8,256,256]{2,1,0:T(8,128)(2,1)S(1)}, u32[]{:S(2)}, u32[]{:S(2)}) async-start(bf16[8,256,256]{2,1,0:T(8,128)(2,1)} %bitcast.98), calls=%async_computation.1 | async-start | bytes 2097152 | tf_op jit(solution)/shard_map/all_to_all | solution.py:406
  51.7 12.3 %collective-permute-start.5 = (bf16[768,256]{1,0:T(8,128)(2,1)}, bf16[768,256]{1,0:T(8,128)(2,1)S(1)}, u32[]{:S(2)}, u32[]{:S(2)}) collective-permute-start(bf16[768,256]{1,0:T(8,128)(2,1)} %get-tuple-element.163), channel_id=1, source_target_pairs={{0,8},{4,12},{8,0},{12,4},{16,24},{20,28},{24,16},{28,20},{1,9},{5... | collective-permute-start | bytes 1179656 | tf_op jit(solution)/shard_map/ppermute | solution.py:161
  53.4 21.2 %collective-permute-start.8 = (bf16[768,256]{1,0:T(8,128)(2,1)}, bf16[768,256]{1,0:T(8,128)(2,1)S(1)}, u32[]{:S(2)}, u32[]{:S(2)}) collective-permute-start(bf16[768,256]{1,0:T(8,128)(2,1)} %get-tuple-element.180), channel_id=1, source_target_pairs={{0,16},{4,20},{8,24},{12,28},{16,0},{20,4},{24,8},{28,12},{1,17},{... | collective-permute-start | bytes 1179656 | tf_op jit(solution)/shard_map/ppermute | solution.py:161
  57.6 20.9 %collective-permute-start.7 = (bf16[768,256]{1,0:T(8,128)(2,1)}, bf16[768,256]{1,0:T(8,128)(2,1)S(1)}, u32[]{:S(2)}, u32[]{:S(2)}) collective-permute-start(bf16[768,256]{1,0:T(8,128)(2,1)} %get-tuple-element.177), channel_id=1, source_target_pairs={{0,8},{4,12},{8,0},{12,4},{16,24},{20,28},{24,16},{28,20},{1,9},{5... | collective-permute-start | bytes 1179656 | tf_op jit(solution)/shard_map/ppermute | solution.py:161
  58.2 20.4 %collective-permute-start.9 = (bf16[768,256]{1,0:T(8,128)(2,1)}, bf16[768,256]{1,0:T(8,128)(2,1)S(1)}, u32[]{:S(2)}, u32[]{:S(2)}) collective-permute-start(bf16[768,256]{1,0:T(8,128)(2,1)} %get-tuple-element.181), channel_id=1, source_target_pairs={{0,16},{4,20},{8,24},{12,28},{16,0},{20,4},{24,8},{28,12},{1,17},{... | collective-permute-start | bytes 1179656 | tf_op jit(solution)/shard_map/ppermute | solution.py:161
  69.0 12.7 %collective-permute-start.6 = (bf16[768,256]{1,0:T(8,128)(2,1)}, bf16[768,256]{1,0:T(8,128)(2,1)S(1)}, u32[]{:S(2)}, u32[]{:S(2)}) collective-permute-start(bf16[768,256]{1,0:T(8,128)(2,1)} %get-tuple-element.166), channel_id=1, source_target_pairs={{0,4},{4,0},{8,12},{12,8},{16,20},{20,16},{24,28},{28,24},{1,5},{5... | collective-permute-start | bytes 1179656 | tf_op jit(solution)/shard_map/ppermute | solution.py:165
  78.5 16.0 %collective-permute-start.13 = (bf16[768,256]{1,0:T(8,128)(2,1)S(1)}, bf16[768,256]{1,0:T(8,128)(2,1)S(1)}, u32[]{:S(2)}, u32[]{:S(2)}) collective-permute-start(bf16[768,256]{1,0:T(8,128)(2,1)S(1)} %add_convert_fusion.11), channel_id=1, source_target_pairs={{0,16},{4,20},{8,24},{12,28},{16,0},{20,4},{24,8},{28,12},{1,17},{... | collective-permute-start | bytes 1179656 | tf_op jit(solution)/shard_map/ppermute | solution.py:161
  80.3 14.3 %collective-permute-start.14 = (bf16[768,256]{1,0:T(8,128)(2,1)S(1)}, bf16[768,256]{1,0:T(8,128)(2,1)S(1)}, u32[]{:S(2)}, u32[]{:S(2)}) collective-permute-start(bf16[768,256]{1,0:T(8,128)(2,1)S(1)} %add_convert_fusion.10), channel_id=1, source_target_pairs={{0,8},{4,12},{8,0},{12,4},{16,24},{20,28},{24,16},{28,20},{1,9},{5... | collective-permute-start | bytes 1179656 | tf_op jit(solution)/shard_map/ppermute | solution.py:161
  140.3 15.1 %collective-permute-start.21 = (bf16[192,1408]{1,0:T(8,128)(2,1)S(1)}, bf16[192,1408]{1,0:T(8,128)(2,1)S(1)}, u32[]{:S(2)}, u32[]{:S(2)}) collective-permute-start(bf16[192,1408]{1,0:T(8,128)(2,1)S(1)} %copy-done.100), channel_id=1, source_target_pairs={{0,16},{4,20},{8,24},{12,28},{16,0},{20,4},{24,8},{28,12},{1,17},{... | collective-permute-start | bytes 1622024 | tf_op jit(solution)/shard_map/ppermute | solution.py:161
  140.6 15.1 %collective-permute-start.20 = (bf16[192,1408]{1,0:T(8,128)(2,1)S(1)}, bf16[192,1408]{1,0:T(8,128)(2,1)S(1)}, u32[]{:S(2)}, u32[]{:S(2)}) collective-permute-start(bf16[192,1408]{1,0:T(8,128)(2,1)S(1)} %copy-done.99), channel_id=1, source_target_pairs={{0,8},{4,12},{8,0},{12,4},{16,24},{20,28},{24,16},{28,20},{1,9},{5... | collective-permute-start | bytes 1622024 | tf_op jit(solution)/shard_map/ppermute | solution.py:161
  142.3 22.9 %collective-permute-start.22 = (bf16[192,1408]{1,0:T(8,128)(2,1)S(1)}, bf16[192,1408]{1,0:T(8,128)(2,1)S(1)}, u32[]{:S(2)}, u32[]{:S(2)}) collective-permute-start(bf16[192,1408]{1,0:T(8,128)(2,1)S(1)} %copy-done.98), channel_id=1, source_target_pairs={{0,8},{4,12},{8,0},{12,4},{16,24},{20,28},{24,16},{28,20},{1,9},{5... | collective-permute-start | bytes 1622024 | tf_op jit(solution)/shard_map/ppermute | solution.py:161
  142.7 22.5 %collective-permute-start.23 = (bf16[192,1408]{1,0:T(8,128)(2,1)S(1)}, bf16[192,1408]{1,0:T(8,128)(2,1)S(1)}, u32[]{:S(2)}, u32[]{:S(2)}) collective-permute-start(bf16[192,1408]{1,0:T(8,128)(2,1)S(1)} %copy-done.97), channel_id=1, source_target_pairs={{0,16},{4,20},{8,24},{12,28},{16,0},{20,4},{24,8},{28,12},{1,17},{... | collective-permute-start | bytes 1622024 | tf_op jit(solution)/shard_map/ppermute | solution.py:161
  165.2 20.3 %collective-permute-start.28 = (bf16[192,1408]{1,0:T(8,128)(2,1)S(1)}, bf16[192,1408]{1,0:T(8,128)(2,1)S(1)}, u32[]{:S(2)}, u32[]{:S(2)}) collective-permute-start(bf16[192,1408]{1,0:T(8,128)(2,1)S(1)} %add_convert_fusion.3), channel_id=1, source_target_pairs={{0,16},{4,20},{8,24},{12,28},{16,0},{20,4},{24,8},{28,12},{1,17},{... | collective-permute-start | bytes 1622024 | tf_op jit(solution)/shard_map/ppermute | solution.py:161
  166.9 18.6 %collective-permute-start.29 = (bf16[192,1408]{1,0:T(8,128)(2,1)S(1)}, bf16[192,1408]{1,0:T(8,128)(2,1)S(1)}, u32[]{:S(2)}, u32[]{:S(2)}) collective-permute-start(bf16[192,1408]{1,0:T(8,128)(2,1)S(1)} %add_convert_fusion.2), channel_id=1, source_target_pairs={{0,8},{4,12},{8,0},{12,4},{16,24},{20,28},{24,16},{28,20},{1,9},{5... | collective-permute-start | bytes 1622024 | tf_op jit(solution)/shard_map/ppermute | solution.py:161
  195.7 27.1 %collective-permute-start.33 = (bf16[2,192,1408]{2,1,0:T(8,128)(2,1)}, bf16[2,192,1408]{2,1,0:T(8,128)(2,1)}, u32[]{:S(2)}, u32[]{:S(2)}) collective-permute-start(bf16[2,192,1408]{2,1,0:T(8,128)(2,1)} %get-tuple-element.210), channel_id=1, source_target_pairs={{0,16},{4,20},{8,24},{12,28},{16,0},{20,4},{24,8},{28,12},{1,17},{... | collective-permute-start | bytes 3244040 | tf_op jit(solution)/shard_map/ppermute | solution.py:161
  196.7 28.7 %collective-permute-start.32 = (bf16[2,192,1408]{2,1,0:T(8,128)(2,1)}, bf16[2,192,1408]{2,1,0:T(8,128)(2,1)}, u32[]{:S(2)}, u32[]{:S(2)}) collective-permute-start(bf16[2,192,1408]{2,1,0:T(8,128)(2,1)} %get-tuple-element.204), channel_id=1, source_target_pairs={{0,8},{4,12},{8,0},{12,4},{16,24},{20,28},{24,16},{28,20},{1,9},{5... | collective-permute-start | bytes 3244040 | tf_op jit(solution)/shard_map/ppermute | solution.py:161
  207.7 35.5 %collective-permute-start.34 = (bf16[2,192,1408]{2,1,0:T(8,128)(2,1)}, bf16[2,192,1408]{2,1,0:T(8,128)(2,1)S(1)}, u32[]{:S(2)}, u32[]{:S(2)}) collective-permute-start(bf16[2,192,1408]{2,1,0:T(8,128)(2,1)} %get-tuple-element.211), channel_id=1, source_target_pairs={{0,16},{4,20},{8,24},{12,28},{16,0},{20,4},{24,8},{28,12},{1,17},{... | collective-permute-start | bytes 3244040 | tf_op jit(solution)/shard_map/ppermute | solution.py:161
  208.8 34.8 %collective-permute-start.31 = (bf16[2,192,1408]{2,1,0:T(8,128)(2,1)}, bf16[2,192,1408]{2,1,0:T(8,128)(2,1)S(1)}, u32[]{:S(2)}, u32[]{:S(2)}) collective-permute-start(bf16[2,192,1408]{2,1,0:T(8,128)(2,1)} %get-tuple-element.207), channel_id=1, source_target_pairs={{0,8},{4,12},{8,0},{12,4},{16,24},{20,28},{24,16},{28,20},{1,9},{5... | collective-permute-start | bytes 3244040 | tf_op jit(solution)/shard_map/ppermute | solution.py:161
  243.6 30.2 %collective-permute-start.35 = (bf16[2,192,1408]{2,1,0:T(8,128)(2,1)}, bf16[2,192,1408]{2,1,0:T(8,128)(2,1)S(1)}, u32[]{:S(2)}, u32[]{:S(2)}) collective-permute-start(bf16[2,192,1408]{2,1,0:T(8,128)(2,1)} %add_convert_fusion.1), channel_id=1, source_target_pairs={{0,16},{4,20},{8,24},{12,28},{16,0},{20,4},{24,8},{28,12},{1,17},{... | collective-permute-start | bytes 3244040 | tf_op jit(solution)/shard_map/ppermute | solution.py:161
  244.9 28.9 %collective-permute-start.36 = (bf16[2,192,1408]{2,1,0:T(8,128)(2,1)}, bf16[2,192,1408]{2,1,0:T(8,128)(2,1)}, u32[]{:S(2)}, u32[]{:S(2)}) collective-permute-start(bf16[2,192,1408]{2,1,0:T(8,128)(2,1)} %add_convert_fusion), channel_id=1, source_target_pairs={{0,8},{4,12},{8,0},{12,4},{16,24},{20,28},{24,16},{28,20},{1,9},{5... | collective-permute-start | bytes 3244040 | tf_op jit(solution)/shard_map/ppermute | solution.py:161
  245.7 22.6 %collective-permute-start.37 = (f32[8,768]{1,0:T(8,128)S(1)}, f32[8,768]{1,0:T(8,128)S(1)}, u32[]{:S(2)}, u32[]{:S(2)}) collective-permute-start(f32[8,768]{1,0:T(8,128)S(1)} %copy-done.76), channel_id=1, source_target_pairs={{0,8},{4,12},{8,0},{12,4},{16,24},{20,28},{24,16},{28,20},{1,9},{5... | collective-permute-start | bytes 73736 | tf_op jit(solution)/shard_map/ppermute | solution.py:161
  283.0 27.0 %collective-permute-start.39 = (bf16[2,192,1408]{2,1,0:T(8,128)(2,1)}, bf16[2,192,1408]{2,1,0:T(8,128)(2,1)S(1)}, u32[]{:S(2)}, u32[]{:S(2)}) collective-permute-start(bf16[2,192,1408]{2,1,0:T(8,128)(2,1)} %get-tuple-element.221.refs_0_), channel_id=1, source_target_pairs={{0,16},{4,20},{8,24},{12,28},{16,0},{20,4},{24,8},{28,12},{1,17},{... | collective-permute-start | bytes 3244040 | tf_op jit(solution)/shard_map/ppermute | solution.py:161
  283.7 45.7 %collective-permute-start.41 = (bf16[2,192,1408]{2,1,0:T(8,128)(2,1)}, bf16[2,192,1408]{2,1,0:T(8,128)(2,1)S(1)}, u32[]{:S(2)}, u32[]{:S(2)}) collective-permute-start(bf16[2,192,1408]{2,1,0:T(8,128)(2,1)} %get-tuple-element.222.refs_4_.refs_2_), channel_id=1, source_target_pairs={{0,16},{4,20},{8,24},{12,28},{16,0},{20,4},{24,8},{28,12},{1,17},{... | collective-permute-start | bytes 3244040 | tf_op jit(solution)/shard_map/ppermute | solution.py:161
  285.1 44.3 %collective-permute-start.40 = (bf16[2,192,1408]{2,1,0:T(8,128)(2,1)}, bf16[2,192,1408]{2,1,0:T(8,128)(2,1)}, u32[]{:S(2)}, u32[]{:S(2)}) collective-permute-start(bf16[2,192,1408]{2,1,0:T(8,128)(2,1)} %get-tuple-element.221.refs_0_), channel_id=1, source_target_pairs={{0,8},{4,12},{8,0},{12,4},{16,24},{20,28},{24,16},{28,20},{1,9},{5... | collective-permute-start | bytes 3244040 | tf_op jit(solution)/shard_map/ppermute | solution.py:161
  285.9 46.0 %collective-permute-start.42 = (bf16[2,192,1408]{2,1,0:T(8,128)(2,1)}, bf16[2,192,1408]{2,1,0:T(8,128)(2,1)S(1)}, u32[]{:S(2)}, u32[]{:S(2)}) collective-permute-start(bf16[2,192,1408]{2,1,0:T(8,128)(2,1)} %get-tuple-element.222.refs_4_.refs_2_), channel_id=1, source_target_pairs={{0,8},{4,12},{8,0},{12,4},{16,24},{20,28},{24,16},{28,20},{1,9},{5... | collective-permute-start | bytes 3244040 | tf_op jit(solution)/shard_map/ppermute | solution.py:161
  293.7 40.6 %collective-permute-start.56 = (f32[8,192]{0,1:T(8,128)S(1)}, f32[8,192]{0,1:T(8,128)S(1)}, u32[]{:S(2)}, u32[]{:S(2)}) collective-permute-start(f32[8,192]{0,1:T(8,128)S(1)} %bitcast_add_fusion), channel_id=1, source_target_pairs={{0,3},{1,2},{2,1},{3,0},{4,7},{5,6},{6,5},{7,4},{8,11},{9,10},{10,... | collective-permute-start | bytes 18440 | tf_op jit(solution)/shard_map/ppermute | solution.py:176
  331.8 23.7 %collective-permute-start.43 = (bf16[2,192,1408]{2,1,0:T(8,128)(2,1)}, bf16[2,192,1408]{2,1,0:T(8,128)(2,1)}, u32[]{:S(2)}, u32[]{:S(2)}) collective-permute-start(bf16[2,192,1408]{2,1,0:T(8,128)(2,1)} %collective-permute-done.40.refs_1_), channel_id=1, source_target_pairs={{0,16},{4,20},{8,24},{12,28},{16,0},{20,4},{24,8},{28,12},{1,17},{... | collective-permute-start | bytes 3244040 | tf_op jit(solution)/shard_map/ppermute | solution.py:161
  332.4 23.1 %collective-permute-start.44 = (bf16[2,192,1408]{2,1,0:T(8,128)(2,1)S(1)}, bf16[2,192,1408]{2,1,0:T(8,128)(2,1)}, u32[]{:S(2)}, u32[]{:S(2)}) collective-permute-start(bf16[2,192,1408]{2,1,0:T(8,128)(2,1)S(1)} %collective-permute-done.41.refs_2_.refs_6_), channel_id=1, source_target_pairs={{0,8},{4,12},{8,0},{12,4},{16,24},{20,28},{24,16},{28,20},{1,9},{5... | collective-permute-start | bytes 3244040 | tf_op jit(solution)/shard_map/ppermute | solution.py:161
  334.3 20.0 %collective-permute-start.57 = (f32[8,192]{0,1:T(8,128)S(1)}, f32[8,192]{0,1:T(8,128)S(1)}, u32[]{:S(2)}, u32[]{:S(2)}) collective-permute-start(f32[8,192]{0,1:T(8,128)S(1)} %add.355), channel_id=1, source_target_pairs={{0,8},{4,12},{8,0},{12,4},{16,24},{20,28},{24,16},{28,20},{1,9},{5... | collective-permute-start | bytes 18440 | tf_op jit(solution)/shard_map/ppermute | solution.py:161
  355.4 13.2 %collective-permute-start.51 = (bf16[2,192,256]{2,1,0:T(8,128)(2,1)S(1)}, bf16[2,192,256]{2,1,0:T(8,128)(2,1)S(1)}, u32[]{:S(2)}, u32[]{:S(2)}) collective-permute-start(bf16[2,192,256]{2,1,0:T(8,128)(2,1)S(1)} %add_convert_fusion.16), channel_id=1, source_target_pairs={{0,3},{1,2},{2,1},{3,0},{4,7},{5,6},{6,5},{7,4},{8,11},{9,10},{10,... | collective-permute-start | bytes 589832 | tf_op jit(solution)/shard_map/ppermute | solution.py:176
  375.7 19.1 %collective-permute-start.53 = (bf16[2,192,256]{2,1,0:T(8,128)(2,1)S(1)}, bf16[2,192,256]{2,1,0:T(8,128)(2,1)S(1)}, u32[]{:S(2)}, u32[]{:S(2)}) collective-permute-start(bf16[2,192,256]{2,1,0:T(8,128)(2,1)S(1)} %add_convert_fusion.17), channel_id=1, source_target_pairs={{0,3},{1,2},{2,1},{3,0},{4,7},{5,6},{6,5},{7,4},{8,11},{9,10},{10,... | collective-permute-start | bytes 589832 | tf_op jit(solution)/shard_map/ppermute | solution.py:176
  379.5 15.5 %collective-permute-start.46 = (bf16[192,1408]{1,0:T(8,128)(2,1)S(1)}, bf16[192,1408]{1,0:T(8,128)(2,1)S(1)}, u32[]{:S(2)}, u32[]{:S(2)}) collective-permute-start(bf16[192,1408]{1,0:T(8,128)(2,1)S(1)} %copy-done.92), channel_id=1, source_target_pairs={{0,8},{4,12},{8,0},{12,4},{16,24},{20,28},{24,16},{28,20},{1,9},{5... | collective-permute-start | bytes 1622024 | tf_op jit(solution)/shard_map/ppermute | solution.py:161
  380.2 17.8 %collective-permute-start.48 = (bf16[192,1408]{1,0:T(8,128)(2,1)S(1)}, bf16[192,1408]{1,0:T(8,128)(2,1)S(1)}, u32[]{:S(2)}, u32[]{:S(2)}) collective-permute-start(bf16[192,1408]{1,0:T(8,128)(2,1)S(1)} %copy-done.92), channel_id=1, source_target_pairs={{0,16},{4,20},{8,24},{12,28},{16,0},{20,4},{24,8},{28,12},{1,17},{... | collective-permute-start | bytes 1622024 | tf_op jit(solution)/shard_map/ppermute | solution.py:161
  381.9 16.2 %collective-permute-start.47 = (bf16[192,1408]{1,0:T(8,128)(2,1)S(1)}, bf16[192,1408]{1,0:T(8,128)(2,1)S(1)}, u32[]{:S(2)}, u32[]{:S(2)}) collective-permute-start(bf16[192,1408]{1,0:T(8,128)(2,1)S(1)} %copy-done.93), channel_id=1, source_target_pairs={{0,16},{4,20},{8,24},{12,28},{16,0},{20,4},{24,8},{28,12},{1,17},{... | collective-permute-start | bytes 1622024 | tf_op jit(solution)/shard_map/ppermute | solution.py:161
  382.3 15.8 %collective-permute-start.49 = (bf16[192,1408]{1,0:T(8,128)(2,1)S(1)}, bf16[192,1408]{1,0:T(8,128)(2,1)}, u32[]{:S(2)}, u32[]{:S(2)}) collective-permute-start(bf16[192,1408]{1,0:T(8,128)(2,1)S(1)} %copy-done.93), channel_id=1, source_target_pairs={{0,8},{4,12},{8,0},{12,4},{16,24},{20,28},{24,16},{28,20},{1,9},{5... | collective-permute-start | bytes 1622024 | tf_op jit(solution)/shard_map/ppermute | solution.py:161
  416.0 15.5 %collective-permute-start.60 = (bf16[768,128]{1,0:T(8,128)(2,1)}, bf16[768,128]{1,0:T(8,128)(2,1)S(1)}, u32[]{:S(2)}, u32[]{:S(2)}) collective-permute-start(bf16[768,128]{1,0:T(8,128)(2,1)} %get-tuple-element.247), channel_id=1, source_target_pairs={{0,16},{4,20},{8,24},{12,28},{16,0},{20,4},{24,8},{28,12},{1,17},{... | collective-permute-start | bytes 589832 | tf_op jit(solution)/shard_map/ppermute | solution.py:161
  417.7 13.9 %collective-permute-start.59 = (bf16[768,128]{1,0:T(8,128)(2,1)}, bf16[768,128]{1,0:T(8,128)(2,1)S(1)}, u32[]{:S(2)}, u32[]{:S(2)}) collective-permute-start(bf16[768,128]{1,0:T(8,128)(2,1)} %get-tuple-element.245), channel_id=1, source_target_pairs={{0,8},{4,12},{8,0},{12,4},{16,24},{20,28},{24,16},{28,20},{1,9},{5... | collective-permute-start | bytes 589832 | tf_op jit(solution)/shard_map/ppermute | solution.py:161
  418.5 13.2 %collective-permute-start.61 = (bf16[768,128]{1,0:T(8,128)(2,1)}, bf16[768,128]{1,0:T(8,128)(2,1)S(1)}, u32[]{:S(2)}, u32[]{:S(2)}) collective-permute-start(bf16[768,128]{1,0:T(8,128)(2,1)} %get-tuple-element.248), channel_id=1, source_target_pairs={{0,8},{4,12},{8,0},{12,4},{16,24},{20,28},{24,16},{28,20},{1,9},{5... | collective-permute-start | bytes 589832 | tf_op jit(solution)/shard_map/ppermute | solution.py:161
  434.1 53.2 %collective-permute-start.73 = (bf16[4,256,1408]{2,1,0:T(8,128)(2,1)}, bf16[4,256,1408]{2,1,0:T(8,128)(2,1)S(1)}, u32[]{:S(2)}, u32[]{:S(2)}) collective-permute-start(bf16[4,256,1408]{2,1,0:T(8,128)(2,1)} %get-tuple-element.271), channel_id=1, source_target_pairs={{0,4},{4,0},{8,12},{12,8},{16,20},{20,16},{24,28},{28,24},{1,5},{5... | collective-permute-start | bytes 8650760 | tf_op jit(solution)/shard_map/ppermute | solution.py:165
  439.1 48.4 %collective-permute-start.74 = (bf16[4,256,1408]{2,1,0:T(8,128)(2,1)}, bf16[4,256,1408]{2,1,0:T(8,128)(2,1)}, u32[]{:S(2)}, u32[]{:S(2)}) collective-permute-start(bf16[4,256,1408]{2,1,0:T(8,128)(2,1)} %get-tuple-element.274), channel_id=1, source_target_pairs={{0,4},{4,0},{8,12},{12,8},{16,20},{20,16},{24,28},{28,24},{1,5},{5... | collective-permute-start | bytes 8650760 | tf_op jit(solution)/shard_map/ppermute | solution.py:165
  439.1 17.0 %collective-permute-start.65 = (bf16[192,1408]{1,0:T(8,128)(2,1)}, bf16[192,1408]{1,0:T(8,128)(2,1)}, u32[]{:S(2)}, u32[]{:S(2)}) collective-permute-start(bf16[192,1408]{1,0:T(8,128)(2,1)} %copy-done.94), channel_id=1, source_target_pairs={{0,16},{4,20},{8,24},{12,28},{16,0},{20,4},{24,8},{28,12},{1,17},{... | collective-permute-start | bytes 1622024 | tf_op jit(solution)/shard_map/ppermute | solution.py:161
  439.5 17.9 %collective-permute-start.66 = (bf16[192,1408]{1,0:T(8,128)(2,1)}, bf16[192,1408]{1,0:T(8,128)(2,1)}, u32[]{:S(2)}, u32[]{:S(2)}) collective-permute-start(bf16[192,1408]{1,0:T(8,128)(2,1)} %copy-done.96), channel_id=1, source_target_pairs={{0,8},{4,12},{8,0},{12,4},{16,24},{20,28},{24,16},{28,20},{1,9},{5... | collective-permute-start | bytes 1622024 | tf_op jit(solution)/shard_map/ppermute | solution.py:161
  457.3 26.1 %collective-permute-start.72 = (bf16[768,256]{1,0:T(8,128)(2,1)}, bf16[768,256]{1,0:T(8,128)(2,1)S(1)}, u32[]{:S(2)}, u32[]{:S(2)}) collective-permute-start(bf16[768,256]{1,0:T(8,128)(2,1)} %get-tuple-element.267.refs_0_), channel_id=1, source_target_pairs={{0,16},{4,20},{8,24},{12,28},{16,0},{20,4},{24,8},{28,12},{1,17},{... | collective-permute-start | bytes 1179656 | tf_op jit(solution)/shard_map/ppermute | solution.py:161
  464.0 19.5 %collective-permute-start.70 = (bf16[768,256]{1,0:T(8,128)(2,1)}, bf16[768,256]{1,0:T(8,128)(2,1)}, u32[]{:S(2)}, u32[]{:S(2)}) collective-permute-start(bf16[768,256]{1,0:T(8,128)(2,1)} %get-tuple-element.263.refs_4_), channel_id=1, source_target_pairs={{0,16},{4,20},{8,24},{12,28},{16,0},{20,4},{24,8},{28,12},{1,17},{... | collective-permute-start | bytes 1179656 | tf_op jit(solution)/shard_map/ppermute | solution.py:161
  466.0 17.5 %collective-permute-start.71 = (bf16[768,256]{1,0:T(8,128)(2,1)}, bf16[768,256]{1,0:T(8,128)(2,1)}, u32[]{:S(2)}, u32[]{:S(2)}) collective-permute-start(bf16[768,256]{1,0:T(8,128)(2,1)} %get-tuple-element.263.refs_4_), channel_id=1, source_target_pairs={{0,8},{4,12},{8,0},{12,4},{16,24},{20,28},{24,16},{28,20},{1,9},{5... | collective-permute-start | bytes 1179656 | tf_op jit(solution)/shard_map/ppermute | solution.py:161
  483.5 13.0 %collective-permute-start.76 = (bf16[768,256]{1,0:T(8,128)(2,1)}, bf16[768,256]{1,0:T(8,128)(2,1)}, u32[]{:S(2)}, u32[]{:S(2)}) collective-permute-start(bf16[768,256]{1,0:T(8,128)(2,1)} %collective-permute-done.69.refs_1_), channel_id=1, source_target_pairs={{0,16},{4,20},{8,24},{12,28},{16,0},{20,4},{24,8},{28,12},{1,17},{... | collective-permute-start | bytes 1179656 | tf_op jit(solution)/shard_map/ppermute | solution.py:161
  487.2 19.1 %collective-permute-start.68 = (bf16[2,384,256]{2,1,0:T(8,128)(2,1)}, bf16[2,384,256]{2,1,0:T(8,128)(2,1)S(1)}, u32[]{:S(2)}, u32[]{:S(2)}) collective-permute-start(bf16[2,384,256]{2,1,0:T(8,128)(2,1)} %get-tuple-element.266), channel_id=1, source_target_pairs={{0,1},{1,0},{2,3},{3,2},{4,5},{5,4},{6,7},{7,6},{8,9},{9,8},{10,11... | collective-permute-start | bytes 1179656 | tf_op jit(solution)/shard_map/ppermute | solution.py:176
  487.3 109.6 %collective-permute-start.93 = (bf16[4,1408,256]{2,1,0:T(8,128)(2,1)}, bf16[4,1408,256]{2,1,0:T(8,128)(2,1)}, u32[]{:S(2)}, u32[]{:S(2)}) collective-permute-start(bf16[4,1408,256]{2,1,0:T(8,128)(2,1)} %get-tuple-element.308), channel_id=1, source_target_pairs={{0,4},{4,0},{8,12},{12,8},{16,20},{20,16},{24,28},{28,24},{1,5},{5... | collective-permute-start | bytes 8650760 | tf_op jit(solution)/shard_map/ppermute | solution.py:165
  495.1 13.3 %collective-permute-start.79 = (f32[8,768]{1,0:T(8,128)S(1)}, f32[8,768]{1,0:T(8,128)S(1)}, u32[]{:S(2)}, u32[]{:S(2)}) collective-permute-start(f32[8,768]{1,0:T(8,128)S(1)} %select_add_fusion), channel_id=1, source_target_pairs={{0,8},{4,12},{8,0},{12,4},{16,24},{20,28},{24,16},{28,20},{1,9},{5... | collective-permute-start | bytes 73736 | tf_op jit(solution)/shard_map/ppermute | solution.py:161
  506.3 19.4 %collective-permute-start.78 = (bf16[2,384,256]{2,1,0:T(8,128)(2,1)}, bf16[2,384,256]{2,1,0:T(8,128)(2,1)S(1)}, u32[]{:S(2)}, u32[]{:S(2)}) collective-permute-start(bf16[2,384,256]{2,1,0:T(8,128)(2,1)} %get-tuple-element.281), channel_id=1, source_target_pairs={{0,1},{1,0},{2,3},{3,2},{4,5},{5,4},{6,7},{7,6},{8,9},{9,8},{10,11... | collective-permute-start | bytes 1179656 | tf_op jit(solution)/shard_map/ppermute | solution.py:176
  508.4 17.4 %collective-permute-start.75 = (bf16[2,384,256]{2,1,0:T(8,128)(2,1)S(1)}, bf16[2,384,256]{2,1,0:T(8,128)(2,1)S(1)}, u32[]{:S(2)}, u32[]{:S(2)}) collective-permute-start(bf16[2,384,256]{2,1,0:T(8,128)(2,1)S(1)} %add_convert_fusion.7), channel_id=1, source_target_pairs={{0,3},{1,2},{2,1},{3,0},{4,7},{5,6},{6,5},{7,4},{8,11},{9,10},{10,... | collective-permute-start | bytes 1179656 | tf_op jit(solution)/shard_map/ppermute | solution.py:176
  527.6 25.1 %collective-permute-start.84 = (bf16[2,384,256]{2,1,0:T(8,128)(2,1)S(1)}, bf16[2,384,256]{2,1,0:T(8,128)(2,1)S(1)}, u32[]{:S(2)}, u32[]{:S(2)}) collective-permute-start(bf16[2,384,256]{2,1,0:T(8,128)(2,1)S(1)} %add_convert_fusion.6), channel_id=1, source_target_pairs={{0,3},{1,2},{2,1},{3,0},{4,7},{5,6},{6,5},{7,4},{8,11},{9,10},{10,... | collective-permute-start | bytes 1179656 | tf_op jit(solution)/shard_map/ppermute | solution.py:176
  552.8 21.4 %collective-permute-start.85 = (bf16[2,384,256]{2,1,0:T(8,128)(2,1)S(1)}, bf16[2,384,256]{2,1,0:T(8,128)(2,1)S(1)}, u32[]{:S(2)}, u32[]{:S(2)}) collective-permute-start(bf16[2,384,256]{2,1,0:T(8,128)(2,1)S(1)} %add_convert_fusion.4.refs_0_), channel_id=1, source_target_pairs={{0,1},{1,0},{2,3},{3,2},{4,5},{5,4},{6,7},{7,6},{8,9},{9,8},{10,11... | collective-permute-start | bytes 1179656 | tf_op jit(solution)/shard_map/ppermute | solution.py:176
  574.2 19.1 %all-to-all-start.2 = ((bf16[8,256,256]{2,1,0:T(8,128)(2,1)}), bf16[8,256,256]{2,1,0:T(8,128)(2,1)S(1)}, u32[]{:S(2)}, u32[]{:S(2)}) async-start(bf16[8,256,256]{2,1,0:T(8,128)(2,1)} %unpack.2), calls=%async_computation.2 | async-start | bytes 2097152 | tf_op jit(solution)/shard_map/all_to_all | solution.py:1208
  585.5 19.7 %collective-permute-start.92 = (bf16[4,512,256]{2,1,0:T(8,128)(2,1)}, bf16[4,512,256]{2,1,0:T(8,128)(2,1)}, u32[]{:S(2)}, u32[]{:S(2)}) collective-permute-start(bf16[4,512,256]{2,1,0:T(8,128)(2,1)} %get-tuple-element.307), channel_id=1, source_target_pairs={{0,4},{4,0},{8,12},{12,8},{16,20},{20,16},{24,28},{28,24},{1,5},{5... | collective-permute-start | bytes 3145736 | tf_op jit(solution)/shard_map/ppermute | solution.py:165
  585.6 22.4 %collective-permute-start.91 = (bf16[4,256,512]{2,1,0:T(8,128)(2,1)}, bf16[4,256,512]{2,1,0:T(8,128)(2,1)S(1)}, u32[]{:S(2)}, u32[]{:S(2)}) collective-permute-start(bf16[4,256,512]{2,1,0:T(8,128)(2,1)} %get-tuple-element.306), channel_id=1, source_target_pairs={{0,4},{4,0},{8,12},{12,8},{16,20},{20,16},{24,28},{28,24},{1,5},{5... | collective-permute-start | bytes 3145736 | tf_op jit(solution)/shard_map/ppermute | solution.py:165
  586.1 16.8 %collective-permute-start.90 = (bf16[2,256,512]{2,1,0:T(8,128)(2,1)}, bf16[2,256,512]{2,1,0:T(8,128)(2,1)}, u32[]{:S(2)}, u32[]{:S(2)}) collective-permute-start(bf16[2,256,512]{2,1,0:T(8,128)(2,1)} %get-tuple-element.305), channel_id=1, source_target_pairs={{0,4},{4,0},{8,12},{12,8},{16,20},{20,16},{24,28},{28,24},{1,5},{5... | collective-permute-start | bytes 1572872 | tf_op jit(solution)/shard_map/ppermute | solution.py:165
  593.4 20.3 %all-to-all-start.3 = ((bf16[8,288,256]{2,1,0:T(8,128)(2,1)}), bf16[8,288,256]{2,1,0:T(8,128)(2,1)S(1)}, u32[]{:S(2)}, u32[]{:S(2)}) async-start(bf16[8,288,256]{2,1,0:T(8,128)(2,1)} %unpack.3), calls=%async_computation.3 | async-start | bytes 2359296 | tf_op jit(solution)/shard_map/all_to_all | solution.py:1208
  (142 other events, 2096.1 us)
